TPU v7x, 32 devices: a whole 2x2x4 slice. The times are simulated.
32 devices in a mesh: sp: 4 (over y, core), ep: 8 (over z, x).
Axes of the slice: x: 2, y: 2, z: 4, core: 2. Of those that a mesh axis runs over, the one named last changes fastest.
Arguments:
- tokens: bfloat16 [8, 1024, 2048], P('ep', 'sp'), may hold values from -6 to 6
- doc_lengths: int32 [8, 8], P('ep'), may hold values from 1 to 512, 1024 in all within a row
- routes: int32 [8, 1024, 8], P('ep', 'sp'), may hold values from 0 to 15, all different within a row
- attn_gain: bfloat16 [2048], P('ep'), may hold values from 0.25 to 1.75
- w_query: bfloat16 [2048, 2048], P('ep'), may hold values from -0.125 to 0.125
- w_key: bfloat16 [2048, 2048], P('ep'), may hold values from -0.125 to 0.125
- w_value: bfloat16 [2048, 2048], P('ep'), may hold values from -0.125 to 0.125
- q_gain: bfloat16 [2048], P('ep'), may hold values from 0.25 to 1.75
- k_gain: bfloat16 [2048], P('ep'), may hold values from 0.25 to 1.75
- w_out: bfloat16 [2048, 2048], P('ep'), may hold values from -1 to 1
- ffn_gain: bfloat16 [2048], P('ep'), may hold values from 0.25 to 1.75
- w_router: bfloat16 [2048, 16], P('ep'), may hold values from -0.0625 to 0.0625
- w_gate: bfloat16 [16, 2048, 1024], P('ep'), may hold values from -0.125 to 0.125
- w_up: bfloat16 [16, 2048, 1024], P('ep'), may hold values from -0.125 to 0.125
- w_down: bfloat16 [16, 1024, 2048], P('ep'), may hold values from -0.5 to 0.5
- cotangent: bfloat16 [8, 1024, 2048], P('ep', 'sp'), may hold values from -6 to 6
Outputs:
- output: bfloat16 [8, 1024, 2048], P('ep', 'sp')
- input_grad: float32 [8, 1024, 2048], P('ep', 'sp')
- grad_attn_gain: float32 [2048], P('ep')
- grad_query: float32 [2048, 2048], P('ep')
- grad_key: float32 [2048, 2048], P('ep')
- grad_value: float32 [2048, 2048], P('ep')
- grad_q_gain: float32 [2048], P('ep')
- grad_k_gain: float32 [2048], P('ep')
- grad_out: float32 [2048, 2048], P('ep')
- grad_ffn_gain: float32 [2048], P('ep')
- grad_router: float32 [2048, 16], P('ep')
- grad_gate: float32 [16, 2048, 1024], P('ep', 'sp')
- grad_up: float32 [16, 2048, 1024], P('ep', 'sp')
- grad_down: float32 [16, 1024, 2048], P('ep', 'sp')
Inputs may be any that keep to these rules, and one draw needn't show every extreme that they name: `doc_lengths`: in each sequence the 8 lengths sum to 1024, and the longest is exactly 512. `routes`: each token names 8 different experts; every expert is named by some token.
All inputs are finite; a program needn't handle non-finite values.
Results may differ from a plain program's by a relative error of at most 0.02.
Values may be sent and summed in bfloat16 or wider, within the bound.
No kernel may reach another device: no remote copies, remote signals or barrier semaphores. Data moves between devices by JAX's collectives and lax.ppermute only.
A program may use at most 384 MiB of HBM per device.

v0:
```python
import jax
import jax.numpy as jnp
from jax import lax
from jax.sharding import PartitionSpec as P

HEAD_DIM = 128


EPS = 1e-05
THETA = 10000.0
NEG_FILL = -1e30


def product(left, right):
    return jnp.dot(left, right, preferred_element_type=jnp.float32)


def product_left(left, right):
    return lax.dot_general(
        left, right, (((0,), (0,)), ((), ())), preferred_element_type=jnp.float32
    )


def product_right(left, right):
    return lax.dot_general(
        left, right, (((1,), (1,)), ((), ())), preferred_element_type=jnp.float32
    )


def rms_scale(values_in, gain_vec):
    return (
        values_in
        * lax.rsqrt(jnp.mean(values_in * values_in, axis=-1, keepdims=True) + EPS)
        * gain_vec
    )


def rotate_table(positions):
    half_dim = HEAD_DIM // 2
    frequency = THETA ** (-(2.0 * jnp.arange(half_dim, dtype=jnp.float32)) / HEAD_DIM)
    angles = positions.astype(jnp.float32)[:, None] * frequency[None, :]
    cosine_table = jnp.concatenate([jnp.cos(angles), jnp.cos(angles)], axis=1)
    sine_table = jnp.concatenate([jnp.sin(angles), jnp.sin(angles)], axis=1)
    return (cosine_table[:, None, :], sine_table[:, None, :])


def rotary(values_in, cosine_table, sine_table):
    row_count = values_in.shape[0]
    half_dim = HEAD_DIM // 2
    shaped = values_in.reshape(row_count, -1, HEAD_DIM)
    turned = jnp.concatenate([-shaped[..., half_dim:], shaped[..., :half_dim]], axis=-1)
    return (shaped * cosine_table + turned * sine_table).reshape(row_count, -1)


def doc_starts(lengths, places):
    doc_ends = jnp.cumsum(lengths)
    return jnp.sum(jnp.where(doc_ends[None, :] <= places[:, None], lengths[None, :], 0), axis=1)


def block_mask(places, row_ids, row_starts):
    return (places[None, :] <= row_ids[:, None]) & (places[None, :] >= row_starts[:, None])


def attention_forward(q_heads, k_heads, v_heads, starts):
    row_count, local_width = q_heads.shape
    head_count = local_width // HEAD_DIM
    block_rows = min(512, row_count)
    block_count = row_count // block_rows
    key_rows = k_heads.reshape(row_count, head_count, HEAD_DIM)
    value_rows = v_heads.reshape(row_count, head_count, HEAD_DIM)
    places = jnp.arange(row_count, dtype=jnp.int32)
    score_scale = HEAD_DIM ** (-0.5)

    def one_block(block_index):
        first_row = block_index * block_rows
        query_rows = lax.dynamic_slice_in_dim(q_heads, first_row, block_rows, 0).reshape(
            block_rows, head_count, HEAD_DIM
        )
        row_ids = first_row + jnp.arange(block_rows, dtype=jnp.int32)
        row_starts = lax.dynamic_slice_in_dim(starts, first_row, block_rows, 0)
        scores = (
            jnp.einsum("qhd,khd->hqk", query_rows, key_rows, preferred_element_type=jnp.float32)
            * score_scale
        )
        scores = jnp.where(block_mask(places, row_ids, row_starts)[None], scores, NEG_FILL)
        row_max = jnp.max(scores, axis=-1, keepdims=True)
        exp_scores = jnp.exp(scores - row_max)
        row_total = jnp.sum(exp_scores, axis=-1, keepdims=True)
        probs_low = (exp_scores / row_total).astype(jnp.bfloat16)
        mixed_rows = jnp.einsum(
            "hqk,khd->qhd", probs_low, value_rows, preferred_element_type=jnp.float32
        )
        return (mixed_rows.reshape(block_rows, local_width), (row_max + jnp.log(row_total))[..., 0])

    mixed_rows, log_total = lax.map(one_block, jnp.arange(block_count, dtype=jnp.int32))
    return (mixed_rows.reshape(row_count, local_width), log_total)


def attention_backward(q_heads, k_heads, v_heads, d_heads, starts, log_total):
    row_count, local_width = q_heads.shape
    head_count = local_width // HEAD_DIM
    block_rows = min(512, row_count)
    block_count = row_count // block_rows
    key_rows = k_heads.reshape(row_count, head_count, HEAD_DIM)
    value_rows = v_heads.reshape(row_count, head_count, HEAD_DIM)
    places = jnp.arange(row_count, dtype=jnp.int32)
    score_scale = HEAD_DIM ** (-0.5)

    def one_block(carry, block_index):
        d_keys, d_values = carry
        first_row = block_index * block_rows
        query_rows = lax.dynamic_slice_in_dim(q_heads, first_row, block_rows, 0).reshape(
            block_rows, head_count, HEAD_DIM
        )
        grad_rows = lax.dynamic_slice_in_dim(d_heads, first_row, block_rows, 0).reshape(
            block_rows, head_count, HEAD_DIM
        )
        row_ids = first_row + jnp.arange(block_rows, dtype=jnp.int32)
        row_starts = lax.dynamic_slice_in_dim(starts, first_row, block_rows, 0)
        scores = (
            jnp.einsum("qhd,khd->hqk", query_rows, key_rows, preferred_element_type=jnp.float32)
            * score_scale
        )
        scores = jnp.where(block_mask(places, row_ids, row_starts)[None], scores, NEG_FILL)
        probs_full = jnp.exp(scores - log_total[block_index][..., None])
        probs_low = probs_full.astype(jnp.bfloat16)
        d_probs = jnp.einsum(
            "qhd,khd->hqk", grad_rows, value_rows, preferred_element_type=jnp.float32
        )
        row_delta = jnp.sum(probs_full * d_probs, axis=-1, keepdims=True)
        d_scores = (probs_full * (d_probs - row_delta) * score_scale).astype(jnp.bfloat16)
        d_query = jnp.einsum("hqk,khd->qhd", d_scores, key_rows, preferred_element_type=jnp.float32)
        d_keys = d_keys + jnp.einsum(
            "hqk,qhd->khd", d_scores, query_rows, preferred_element_type=jnp.float32
        )
        d_values = d_values + jnp.einsum(
            "hqk,qhd->khd", probs_low, grad_rows, preferred_element_type=jnp.float32
        )
        return ((d_keys, d_values), d_query.reshape(block_rows, local_width))

    zero_rows = jnp.zeros((row_count, head_count, HEAD_DIM), jnp.float32)
    (d_keys, d_values), d_query = lax.scan(
        one_block, (zero_rows, zero_rows), jnp.arange(block_count, dtype=jnp.int32)
    )
    return (
        d_query.reshape(row_count, local_width),
        d_keys.reshape(row_count, local_width),
        d_values.reshape(row_count, local_width),
    )


def body(
    tokens,
    doc_lengths,
    routes,
    attn_gain,
    w_query,
    w_key,
    w_value,
    q_gain,
    k_gain,
    w_out,
    ffn_gain,
    w_router,
    w_gate,
    w_up,
    w_down,
    cotangent,
):
    n_sp = lax.axis_size("sp")
    n_ep = lax.axis_size("ep")
    sp_index = lax.axis_index("sp")
    x_rows = tokens[0].astype(jnp.float32)
    tok_dev, model_width = x_rows.shape
    row_count = tok_dev * n_sp
    (
        full_query,
        full_key,
        full_value,
        full_out,
        full_router,
        gain_attn,
        gain_query,
        gain_key,
        gain_ffn,
    ) = (
        lax.all_gather(w_query, "ep", axis=0, tiled=True),
        lax.all_gather(w_key, "ep", axis=0, tiled=True),
        lax.all_gather(w_value, "ep", axis=0, tiled=True),
        lax.all_gather(w_out, "ep", axis=0, tiled=True),
        lax.all_gather(w_router, "ep", axis=0, tiled=True),
        lax.all_gather(attn_gain, "ep", axis=0, tiled=True),
        lax.all_gather(q_gain, "ep", axis=0, tiled=True),
        lax.all_gather(k_gain, "ep", axis=0, tiled=True),
        lax.all_gather(ffn_gain, "ep", axis=0, tiled=True),
    )
    gain_attn = gain_attn.astype(jnp.float32)
    gain_query = gain_query.astype(jnp.float32)
    gain_key = gain_key.astype(jnp.float32)
    gain_ffn = gain_ffn.astype(jnp.float32)
    all_places = jnp.arange(row_count, dtype=jnp.int32)
    starts = doc_starts(doc_lengths[0], all_places)
    my_places = sp_index * tok_dev + jnp.arange(tok_dev, dtype=jnp.int32)
    my_starts = lax.dynamic_slice_in_dim(starts, sp_index * tok_dev, tok_dev, 0)
    cosine_table, sine_table = rotate_table(my_places - my_starts)

    def prep_rows(raw_rows, gain_vec):
        return rotary(rms_scale(raw_rows, gain_vec), cosine_table, sine_table)

    h_low = rms_scale(x_rows, gain_attn).astype(jnp.bfloat16)
    q_raw = product(h_low, full_query)
    k_raw = product(h_low, full_key)
    v_low = product(h_low, full_value).astype(jnp.bfloat16)
    q_rot = prep_rows(q_raw, gain_query).astype(jnp.bfloat16)
    k_rot = prep_rows(k_raw, gain_key).astype(jnp.bfloat16)
    q_heads, k_heads, v_heads = (
        lax.all_to_all(q_rot, "sp", split_axis=1, concat_axis=0, tiled=True),
        lax.all_to_all(k_rot, "sp", split_axis=1, concat_axis=0, tiled=True),
        lax.all_to_all(v_low, "sp", split_axis=1, concat_axis=0, tiled=True),
    )
    mixed_heads, log_total = attention_forward(q_heads, k_heads, v_heads, starts)
    attn_tok = lax.all_to_all(
        mixed_heads.astype(jnp.bfloat16), "sp", split_axis=0, concat_axis=1, tiled=True
    )
    stream_one = x_rows + product(attn_tok, full_out)
    h2_low = rms_scale(stream_one, gain_ffn).astype(jnp.bfloat16)
    logits = product(h2_low, full_router)
    route_rows = routes[0]
    top_count = route_rows.shape[1]
    expert_count = full_router.shape[1]
    chosen_mask = route_rows[:, :, None] == jnp.arange(expert_count, dtype=jnp.int32)[None, None, :]
    chosen = jnp.sum(jnp.where(chosen_mask, logits[:, None, :], 0.0), axis=2)
    gate_probs = jax.nn.softmax(chosen, axis=-1)
    capacity = 9 * tok_dev * top_count // (8 * expert_count)
    pair_count = tok_dev * top_count
    local_experts = w_gate.shape[0]
    flat_routes = route_rows.reshape(pair_count)
    onehot = chosen_mask.reshape(pair_count, expert_count).astype(jnp.int32)
    earlier = jnp.cumsum(onehot, axis=0) - onehot
    slot_index = jnp.sum(earlier * onehot, axis=1)
    pair_place = jnp.where(
        slot_index < capacity, flat_routes * capacity + slot_index, expert_count * capacity
    )
    pair_ids = jnp.arange(pair_count, dtype=jnp.int32)
    source = (
        jnp.full((expert_count * capacity,), tok_dev, jnp.int32)
        .at[pair_place]
        .set(pair_ids // top_count, mode="drop")
    )
    owner_pair = (
        jnp.full((expert_count * capacity,), pair_count, jnp.int32)
        .at[pair_place]
        .set(pair_ids, mode="drop")
    )
    zero_row = jnp.zeros((1, model_width), jnp.bfloat16)
    padded = jnp.concatenate([h2_low, zero_row], axis=0)
    send_rows = padded[source].reshape(n_ep, local_experts, capacity, model_width)
    expert_rows = lax.all_to_all(send_rows, "ep", split_axis=0, concat_axis=2, tiled=True)[0]
    gate_pre = jnp.einsum("erd,edf->erf", expert_rows, w_gate, preferred_element_type=jnp.float32)
    up_pre = jnp.einsum("erd,edf->erf", expert_rows, w_up, preferred_element_type=jnp.float32)
    act_low = (jax.nn.silu(gate_pre) * up_pre).astype(jnp.bfloat16)
    expert_out = jnp.einsum(
        "erf,efd->erd", act_low, w_down, preferred_element_type=jnp.float32
    ).astype(jnp.bfloat16)
    returned = lax.all_to_all(expert_out[None], "ep", split_axis=2, concat_axis=0, tiled=True)
    back_padded = jnp.concatenate(
        [returned.reshape(expert_count * capacity, model_width), zero_row], axis=0
    )
    per_pair = back_padded[pair_place].reshape(tok_dev, top_count, model_width).astype(jnp.float32)
    expert_mix = jnp.sum(gate_probs[:, :, None] * per_pair, axis=1)
    output = (stream_one + expert_mix).astype(jnp.bfloat16)
    d_out = cotangent[0].astype(jnp.float32)
    d_gates = jnp.sum(per_pair * d_out[:, None, :], axis=2)
    d_pair_out = (
        (gate_probs[:, :, None] * d_out[:, None, :])
        .astype(jnp.bfloat16)
        .reshape(pair_count, model_width)
    )
    d_padded = jnp.concatenate([d_pair_out, zero_row], axis=0)
    d_send = d_padded[owner_pair].reshape(n_ep, local_experts, capacity, model_width)
    d_expert_out = lax.all_to_all(d_send, "ep", split_axis=0, concat_axis=2, tiled=True)[0]
    d_act = jnp.einsum("erd,efd->erf", d_expert_out, w_down, preferred_element_type=jnp.float32)
    sigma_gate = jax.nn.sigmoid(gate_pre)
    d_gate_low = (d_act * up_pre * sigma_gate * (1.0 + gate_pre * (1.0 - sigma_gate))).astype(
        jnp.bfloat16
    )
    d_up_low = (d_act * gate_pre * sigma_gate).astype(jnp.bfloat16)
    grad_down_full = jnp.einsum(
        "erf,erd->efd", act_low, d_expert_out, preferred_element_type=jnp.float32
    )
    grad_gate_full = jnp.einsum(
        "erd,erf->edf", expert_rows, d_gate_low, preferred_element_type=jnp.float32
    )
    grad_up_full = jnp.einsum(
        "erd,erf->edf", expert_rows, d_up_low, preferred_element_type=jnp.float32
    )
    d_rows_in = (
        jnp.einsum("erf,edf->erd", d_gate_low, w_gate, preferred_element_type=jnp.float32)
        + jnp.einsum("erf,edf->erd", d_up_low, w_up, preferred_element_type=jnp.float32)
    ).astype(jnp.bfloat16)
    d_back = lax.all_to_all(d_rows_in[None], "ep", split_axis=2, concat_axis=0, tiled=True)
    grad_gate, grad_up, grad_down = (
        lax.psum_scatter(
            grad_gate_full.astype(jnp.bfloat16), "sp", scatter_dimension=1, tiled=True
        ).astype(jnp.float32),
        lax.psum_scatter(
            grad_up_full.astype(jnp.bfloat16), "sp", scatter_dimension=1, tiled=True
        ).astype(jnp.float32),
        lax.psum_scatter(
            grad_down_full.astype(jnp.bfloat16), "sp", scatter_dimension=1, tiled=True
        ).astype(jnp.float32),
    )
    d_back_padded = jnp.concatenate(
        [d_back.reshape(expert_count * capacity, model_width), zero_row], axis=0
    )
    d_h2 = jnp.sum(
        d_back_padded[pair_place].reshape(tok_dev, top_count, model_width).astype(jnp.float32),
        axis=1,
    )
    d_chosen = gate_probs * (d_gates - jnp.sum(gate_probs * d_gates, axis=1, keepdims=True))
    d_logits = jnp.sum(jnp.where(chosen_mask, d_chosen[:, :, None], 0.0), axis=1).astype(
        jnp.bfloat16
    )
    grad_router_full = product_left(h2_low, d_logits)
    d_h2 = d_h2 + product_right(d_logits, full_router)
    pull_ffn = jax.vjp(rms_scale, stream_one, gain_ffn)[1]
    d_stream_norm, grad_ffn_full = pull_ffn(d_h2)
    d_stream_one = d_out + d_stream_norm
    d_branch = d_stream_one.astype(jnp.bfloat16)
    grad_out_full = product_left(attn_tok, d_branch)
    d_attn = product_right(d_branch, full_out).astype(jnp.bfloat16)
    d_heads = lax.all_to_all(d_attn, "sp", split_axis=1, concat_axis=0, tiled=True)
    d_q_heads, d_k_heads, d_v_heads = attention_backward(
        q_heads, k_heads, v_heads, d_heads, starts, log_total
    )
    d_q_rot, d_k_rot, d_v_low = (
        lax.all_to_all(
            d_q_heads.astype(jnp.bfloat16), "sp", split_axis=0, concat_axis=1, tiled=True
        ),
        lax.all_to_all(
            d_k_heads.astype(jnp.bfloat16), "sp", split_axis=0, concat_axis=1, tiled=True
        ),
        lax.all_to_all(
            d_v_heads.astype(jnp.bfloat16), "sp", split_axis=0, concat_axis=1, tiled=True
        ),
    )
    pull_query = jax.vjp(prep_rows, q_raw, gain_query)[1]
    d_q_raw, grad_qgain_full = pull_query(d_q_rot.astype(jnp.float32))
    pull_key = jax.vjp(prep_rows, k_raw, gain_key)[1]
    d_k_raw, grad_kgain_full = pull_key(d_k_rot.astype(jnp.float32))
    d_q_low = d_q_raw.astype(jnp.bfloat16)
    d_k_low = d_k_raw.astype(jnp.bfloat16)
    grad_query_full = product_left(h_low, d_q_low)
    grad_key_full = product_left(h_low, d_k_low)
    grad_value_full = product_left(h_low, d_v_low)
    d_h = (
        product_right(d_q_low, full_query)
        + product_right(d_k_low, full_key)
        + product_right(d_v_low, full_value)
    )
    pull_attn = jax.vjp(rms_scale, x_rows, gain_attn)[1]
    d_x_norm, grad_again_full = pull_attn(d_h)
    input_grad = d_stream_one + d_x_norm
    (
        shard_attn,
        shard_query,
        shard_key,
        shard_value,
        shard_qgain,
        shard_kgain,
        shard_out,
        shard_ffn,
        shard_router,
    ) = (
        lax.psum_scatter(
            grad_again_full.astype(jnp.bfloat16), "ep", scatter_dimension=0, tiled=True
        ).astype(jnp.float32),
        lax.psum_scatter(
            grad_query_full.astype(jnp.bfloat16), "ep", scatter_dimension=0, tiled=True
        ).astype(jnp.float32),
        lax.psum_scatter(
            grad_key_full.astype(jnp.bfloat16), "ep", scatter_dimension=0, tiled=True
        ).astype(jnp.float32),
        lax.psum_scatter(
            grad_value_full.astype(jnp.bfloat16), "ep", scatter_dimension=0, tiled=True
        ).astype(jnp.float32),
        lax.psum_scatter(
            grad_qgain_full.astype(jnp.bfloat16), "ep", scatter_dimension=0, tiled=True
        ).astype(jnp.float32),
        lax.psum_scatter(
            grad_kgain_full.astype(jnp.bfloat16), "ep", scatter_dimension=0, tiled=True
        ).astype(jnp.float32),
        lax.psum_scatter(
            grad_out_full.astype(jnp.bfloat16), "ep", scatter_dimension=0, tiled=True
        ).astype(jnp.float32),
        lax.psum_scatter(
            grad_ffn_full.astype(jnp.bfloat16), "ep", scatter_dimension=0, tiled=True
        ).astype(jnp.float32),
        lax.psum_scatter(
            grad_router_full.astype(jnp.bfloat16), "ep", scatter_dimension=0, tiled=True
        ).astype(jnp.float32),
    )
    summed = (
        lax.psum(shard_attn.astype(jnp.bfloat16), "sp").astype(jnp.float32),
        lax.psum(shard_query.astype(jnp.bfloat16), "sp").astype(jnp.float32),
        lax.psum(shard_key.astype(jnp.bfloat16), "sp").astype(jnp.float32),
        lax.psum(shard_value.astype(jnp.bfloat16), "sp").astype(jnp.float32),
        lax.psum(shard_qgain.astype(jnp.bfloat16), "sp").astype(jnp.float32),
        lax.psum(shard_kgain.astype(jnp.bfloat16), "sp").astype(jnp.float32),
        lax.psum(shard_out.astype(jnp.bfloat16), "sp").astype(jnp.float32),
        lax.psum(shard_ffn.astype(jnp.bfloat16), "sp").astype(jnp.float32),
        lax.psum(shard_router.astype(jnp.bfloat16), "sp").astype(jnp.float32),
    )
    return (
        output[None],
        input_grad[None],
        summed[0],
        summed[1],
        summed[2],
        summed[3],
        summed[4],
        summed[5],
        summed[6],
        summed[7],
        summed[8],
        grad_gate,
        grad_up,
        grad_down,
    )


def solution(mesh):
    in_specs = (
        P("ep", "sp", None),
        P("ep", None),
        P("ep", "sp", None),
        P("ep"),
        P("ep", None),
        P("ep", None),
        P("ep", None),
        P("ep"),
        P("ep"),
        P("ep", None),
        P("ep"),
        P("ep", None),
        P("ep", None, None),
        P("ep", None, None),
        P("ep", None, None),
        P("ep", "sp", None),
    )
    out_specs = (
        P("ep", "sp", None),
        P("ep", "sp", None),
        P("ep"),
        P("ep", None),
        P("ep", None),
        P("ep", None),
        P("ep"),
        P("ep"),
        P("ep", None),
        P("ep"),
        P("ep", None),
        P("ep", "sp", None),
        P("ep", "sp", None),
        P("ep", "sp", None),
    )
    return jax.shard_map(body, mesh=mesh, in_specs=in_specs, out_specs=out_specs, check_vma=False)
```

profile of v0, /device:TPU:0, one launch (start us, length us, event | category | flops | bytes accessed | tf_op | source)
XLA Modules:
  0.0 2417.8 jit_solution(8730332078892718520)
XLA Ops:
  10.6 22.4 all-gather.2
  33.0 16.5 all-gather.1
  49.6 18.3 all-gather
  71.1 66.9 %all-gather.13.cloned.1.call-done = bf16[2048,2048]{1,0:T(8,128)(2,1)} async-done(((bf16[256,2048]{1,0:T(8,128)(2,1)}), bf16[2048,2048]{1,0:T(8,128)(2,1)}) %all-gather.13.cloned.1.call-update) | async-done | bytes 8388624 | tf_op jit(solution)/shard_map/all_gather | solution.py:189
  149.1 114.2 %all-gather.11.cloned.1.call-done = bf16[2048,2048]{1,0:T(8,128)(2,1)} async-done(((bf16[256,2048]{1,0:T(8,128)(2,1)}), bf16[2048,2048]{1,0:T(8,128)(2,1)}) %all-gather.11.cloned.1.call-update) | async-done | bytes 8388624 | tf_op jit(solution)/shard_map/all_gather | solution.py:188
  272.5 116.0 %all-gather.9.cloned.1.call-done = bf16[2048,2048]{1,0:T(8,128)(2,1)} async-done(((bf16[256,2048]{1,0:T(8,128)(2,1)}), bf16[2048,2048]{1,0:T(8,128)(2,1)}) %all-gather.9.cloned.1.call-update) | async-done | bytes 8388624 | tf_op jit(solution)/shard_map/all_gather | solution.py:187
  457.7 23.7 while.30
  484.9 18.0 all-gather.3
  521.2 9.9 gather_fusion
  544.7 217.3 %all_gather.35 = bf16[2048,16]{0,1:T(8,128)(2,1)S(1)} all-gather(bf16[256,16]{0,1:T(8,128)(2,1)S(1)} %copy-done.81), channel_id=1, replica_groups=mesh['sp'=4,'ep'=8] {'ep'}, dimensions={0}, use_global_device_ids=true | all-gather | bytes 73728 | tf_op jit(solution)/shard_map/all_gather | solution.py:191
  778.3 22.8 gather_fusion.2
  815.5 191.2 %all-to-all-done.6 = bf16[8,2,144,2048]{3,2,1,0:T(8,128)(2,1)} async-done(((bf16[8,2,144,2048]{3,2,1,0:T(8,128)(2,1)}), bf16[8,2,144,2048]{3,2,1,0:T(8,128)(2,1)}, u32[]{:S(2)}, u32[]{:S(2)}) %all-to-all-start.6) | async-done | bytes 9437216 | tf_op jit(solution)/shard_map/all_to_all | solution.py:281
  1006.7 9.4 copy.231
  1016.0 17.4 fusion.122
  1033.4 14.5 fusion.121
  1047.9 22.8 multiply_convert_fusion.1
  1070.7 17.9 convolution_convert_fusion.5
  1088.6 14.2 fusion.63
  1102.9 27.9 %copy.228 = bf16[1,2,1152,2048]{3,1,0,2:T(2,128)(2,1)} copy(bf16[1,2,1152,2048]{3,2,1,0:T(8,128)(2,1)S(1)} %fusion.63) | data formatting | bytes 18874368 | tf_op jit(solution)/shard_map/broadcast_in_dim | solution.py:265
  1135.9 17.6 convolution_convert_fusion.6
  1153.6 18.5 fusion.123
  1172.1 22.2 fusion.64
  1194.4 18.3 copy.232
  1212.7 127.6 %all-to-all-done.5 = bf16[1,2,1152,2048]{3,1,0,2:T(2,128)(2,1)} async-done(((bf16[1,2,1152,2048]{3,1,0,2:T(2,128)(2,1)}), bf16[1,2,1152,2048]{3,1,0,2:T(2,128)(2,1)}, u32[]{:S(2)}, u32[]{:S(2)}) %all-to-all-start.5) | async-done | bytes 9437216 | tf_op jit(solution)/shard_map/all_to_all | solution.py:265
  1345.4 17.0 convolution_convert_fusion.7
  1363.1 13.7 copy.229
  1376.8 10.1 concatenate.29
  1386.9 22.1 gather_fusion.1
  1409.0 9.6 fusion.61
  1418.7 131.3 %all-to-all-done.7 = bf16[1,2,1152,2048]{3,1,0,2:T(2,128)(2,1)} async-done(((bf16[1,2,1152,2048]{3,1,0,2:T(2,128)(2,1)}), bf16[1,2,1152,2048]{3,1,0,2:T(2,128)(2,1)}, u32[]{:S(2)}, u32[]{:S(2)}) %all-to-all-start.7) | async-done | bytes 9437216 | tf_op jit(solution)/shard_map/all_to_all | solution.py:301
  1550.0 11.7 copy.233
  1561.7 9.3 concatenate.31
  1571.0 21.4 gather_fusion.3
  1592.6 11.4 convert_reduce_fusion
  1630.6 12.7 all-to-all-done.8
  1644.4 134.9 %while.31 = (s32[]{:T(128)}, f32[1024,4,128]{0,2,1:T(8,128)}, f32[1024,4,128]{0,2,1:T(8,128)}, bf16[2,512,512]{2,1,0:T(8,128)(2,1)}, s32[2]{0:T(128)S(1)}, /*ind...) while((s32[]{:T(128)}, f32[1024,4,128]{0,2,1:T(8,128)}, ...), condition=%wide.region_26.27_spmd.clone.clone, body=%wide.region_24.26_spmd.clone.clone.sunk | while | flops 2742557184 | bytes 132696456 | solution.py:142
  1663.0 22.6 fusion.216
  1685.6 24.1 bitcast_add_fusion.4
  1729.8 22.6 fusion.216
  1752.3 24.7 %bitcast_add_fusion.4 = f32[1024,4,128]{0,2,1:T(8,128)} fusion(f32[1024,4,128]{0,2,1:T(8,128)} %get-tuple-element.619, bf16[512,4,128]{0,2,1:T(8,128)(2,1)S(1)} %bitcast.277, f32[4,512,1024]{2,1,0:T(8,128)} %fusion.213, f32[4,512,1024]{2,1,0:T(8,128)} %copy-done, f32[4,512]{1,0:T(4,128)S(1)} %dynamic-slice_bitcast_fusion.2, ...), kind=kOutput, calls=%fused_computation.47.clone.1 | convolution fusion | flops 560991232 | bytes 22028288 | tf_op jit(solution)/shard_map/while/body/eval_jaxpr/hqk,qhd->khd/dot_general | solution.py:133
  1782.8 16.9 all_to_all.182
  1832.0 10.9 all-to-all-done.10
  1896.4 57.4 %reduce-scatter.13.cloned.1.call-done = bf16[256,2048]{1,0:T(8,128)(2,1)} async-done(((bf16[2048,2048]{1,0:T(8,128)(2,1)}), bf16[256,2048]{1,0:T(8,128)(2,1)}) %reduce-scatter.13.cloned.1.call-update) | async-done | bytes 1048592 | tf_op jit(solution)/shard_map/reduce_scatter | solution.py:384
  1953.8 152.0 %reduce-scatter.11.cloned.1.call-done = bf16[256,2048]{1,0:T(8,128)(2,1)} async-done(((bf16[2048,2048]{1,0:T(8,128)(2,1)}), bf16[256,2048]{1,0:T(8,128)(2,1)}) %reduce-scatter.11.cloned.1.call-update) | async-done | bytes 1048592 | tf_op jit(solution)/shard_map/reduce_scatter | solution.py:381
  2105.8 151.7 %reduce-scatter.9.cloned.1.call-done = bf16[256,2048]{1,0:T(8,128)(2,1)} async-done(((bf16[2048,2048]{1,0:T(8,128)(2,1)}), bf16[256,2048]{1,0:T(8,128)(2,1)}) %reduce-scatter.9.cloned.1.call-update) | async-done | bytes 1048592 | tf_op jit(solution)/shard_map/reduce_scatter | solution.py:378
  2271.6 35.2 %all-reduce.12 = (bf16[2048]{0:T(1024)(128)(2,1)S(1)}, bf16[2048]{0:T(1024)(128)(2,1)S(1)}, bf16[2048]{0:T(1024)(128)(2,1)S(1)}, bf16[2048]{0:T(1024)(128)(2,1)S(1)}) all-reduce(bf16[2048]{0:T(1024)(128)(2,1)S(1)} %get-tuple-element.354, bf16[2048]{0:T(1024)(128)(2,1)S(1)} %get-tuple-element.352, ...), channel_id=2, replica_groups=mesh['sp'=4,'ep'=8] {'ep'}, use_global_device_ids=true, to_apply=%region_31.32.clone | all-reduce | flops 8192 | bytes 32768
  2314.1 10.1 all-reduce.13
  2330.6 71.4 %all-reduce.17.cloned.1.call-done = (bf16[256,2048]{1,0:T(8,128)(2,1)}, bf16[256,2048]{1,0:T(8,128)(2,1)}, bf16[256,2048]{1,0:T(8,128)(2,1)}, bf16[256,2048]{1,0:T(8,128)(2,1)}) async-done(((bf16[256,2048]{1,0:T(8,128)(2,1)}, bf16[256,2048]{1,0:T(8,128)(2,1)}, bf16[256,2048]{1,0:T(8,128)(2,1)}, bf16[256,2048]{1,0:T(8,128)(2,1)}), (bf16[256,2048]{1,0:T(8,128)(2,1)}, bf16[256,2048]{1,0:T(8,128)(2,1)}, ...) | async-done | bytes 4194320 | tf_op jit(solution)/shard_map/psum | solution.py:405
  (444 shorter events, 382.5 us)
Async XLA Ops:
  7.2 130.8 %all-gather.13.cloned.1.call-start = ((), (), s32[]{:S(2)}) async-start(), calls=%async_computation.22 | async-start | bytes 9437184 | tf_op jit(solution)/shard_map/all_gather | solution.py:189
  8.0 255.3 %all-gather.11.cloned.1.call-start = ((), (), s32[]{:S(2)}) async-start(), calls=%async_computation.21 | async-start | bytes 9437184 | tf_op jit(solution)/shard_map/all_gather | solution.py:188
  8.7 379.8 %all-gather.9.cloned.1.call-start = ((), (), s32[]{:S(2)}) async-start(), calls=%async_computation.20 | async-start | bytes 9437184 | tf_op jit(solution)/shard_map/all_gather | solution.py:187
  9.4 504.2 %all-gather.15.cloned.1.call-start = ((), (), s32[]{:S(2)}) async-start(), calls=%async_computation.23 | async-start | bytes 9437184 | tf_op jit(solution)/shard_map/all_gather | solution.py:190
  10.5 133.2 %copy-start.77 = (f32[256]{0:T(256)}, f32[256]{0:T(256)S(1)}, u32[]{:S(2)}) copy-start(f32[256]{0:T(256)S(1)} %fusion.74) | copy-start | bytes 3076
  33.0 377.0 %copy-start.51 = (f32[8,1,256]{2,1,0:T(1,128)}, f32[8,1,256]{2,1,0:T(1,128)S(1)}, u32[]{:S(2)}) copy-start(f32[8,1,256]{2,1,0:T(1,128)S(1)} %convert_element_type.347) | copy-start | bytes 24580
  49.5 360.4 %copy-start.49 = (f32[8,1,256]{2,1,0:T(1,128)}, f32[8,1,256]{2,1,0:T(1,128)S(1)}, u32[]{:S(2)}) copy-start(f32[8,1,256]{2,1,0:T(1,128)S(1)} %convert_element_type.346) | copy-start | bytes 24580
  67.9 320.6 %copy-start.43 = (f32[8,1,256]{2,1,0:T(1,128)}, f32[8,1,256]{2,1,0:T(1,128)S(1)}, u32[]{:S(2)}) copy-start(f32[8,1,256]{2,1,0:T(1,128)S(1)} %convert_element_type.345) | copy-start | bytes 24580
  68.4 333.4 %copy-start.34 = (f32[256,128]{0,1:T(8,128)}, f32[256,128]{0,1:T(8,128)S(1)}, u32[]{:S(2)}) copy-start(f32[256,128]{0,1:T(8,128)S(1)} %get-tuple-element.443) | copy-start | bytes 393220
  71.1 317.5 %copy-start.63 = (f32[256]{0:T(256)}, f32[256]{0:T(256)S(1)}, u32[]{:S(2)}) copy-start(f32[256]{0:T(256)S(1)} %fusion.105) | copy-start | bytes 3076
  144.9 271.4 %all-to-all-start.2 = ((bf16[256,4,512]{2,0,1:T(8,128)(2,1)}), bf16[256,4,512]{2,0,1:T(8,128)(2,1)}, u32[]{:S(2)}, u32[]{:S(2)}) async-start(bf16[256,4,512]{2,0,1:T(8,128)(2,1)} %bitcast.226), calls=%async_computation.2 | async-start | bytes 2097152 | tf_op jit(solution)/shard_map/all_to_all | solution.py:219
  269.2 140.8 %copy-start.70 = (f32[256]{0:T(256)}, f32[256]{0:T(256)S(1)}, u32[]{:S(2)}) copy-start(f32[256]{0:T(256)S(1)} %fusion.107) | copy-start | bytes 3076
  416.2 18.0 all-to-all-start
  434.2 19.0 all-to-all-start.1
  481.4 38.1 %copy-start.53 = (s32[1024]{0:T(1024)}, s32[1024]{0:T(1024)S(1)}, u32[]{:S(2)}) copy-start(s32[1024]{0:T(1024)S(1)} %get-tuple-element.726) | copy-start | bytes 12292
  481.4 38.1 %copy-start.59 = (f32[2,4,512]{2,1,0:T(4,128)}, f32[2,4,512]{2,1,0:T(4,128)S(1)}, u32[]{:S(2)}) copy-start(f32[2,4,512]{2,1,0:T(4,128)S(1)} %get-tuple-element.610) | copy-start | bytes 49156
  481.4 29.6 %all-to-all-start.3 = ((bf16[4,256,512]{2,1,0:T(8,128)(2,1)}), bf16[4,256,512]{2,1,0:T(8,128)(2,1)S(1)}, u32[]{:S(2)}, u32[]{:S(2)}) async-start(bf16[4,256,512]{2,1,0:T(8,128)(2,1)} %bitcast.308), calls=%async_computation.3 | async-start | bytes 2097152 | tf_op jit(solution)/shard_map/all_to_all | solution.py:222
  521.1 242.4 %copy-start.16 = (bf16[256,2048]{1,0:T(8,128)(2,1)}, bf16[256,2048]{1,0:T(8,128)(2,1)S(1)}, u32[]{:S(2)}) copy-start(bf16[256,2048]{1,0:T(8,128)(2,1)S(1)} %multiply_convert_fusion.4) | copy-start | bytes 3145732
  531.1 270.0 %all-to-all-start.4 = ((bf16[8,2,144,2048]{3,2,1,0:T(8,128)(2,1)}), bf16[8,2,144,2048]{3,2,1,0:T(8,128)(2,1)}, u32[]{:S(2)}, u32[]{:S(2)}) async-start(bf16[8,2,144,2048]{3,2,1,0:T(8,128)(2,1)} %bitcast.281), calls=%async_computation.4 | async-start | bytes 18874368 | tf_op jit(solution)/shard_map/all_to_all | solution.py:258
  801.1 205.5 %all-to-all-start.6 = ((bf16[8,2,144,2048]{3,2,1,0:T(8,128)(2,1)}), bf16[8,2,144,2048]{3,2,1,0:T(8,128)(2,1)}, u32[]{:S(2)}, u32[]{:S(2)}) async-start(bf16[8,2,144,2048]{3,2,1,0:T(8,128)(2,1)} %bitcast.282), calls=%async_computation.6 | async-start | bytes 18874368 | tf_op jit(solution)/shard_map/all_to_all | solution.py:281
  806.2 1070.4 %reduce-scatter.23.cloned.1.call-start = ((), (), s32[]{:S(2)}) async-start(), calls=%async_computation.31 | async-start | bytes 10485760 | tf_op jit(solution)/shard_map/reduce_scatter | solution.py:309
  1006.7 26.8 %slice-start = ((s8[9437184]{0:T(1024)(128)(4,1)}), s8[1048576]{0:T(1024)(128)(4,1)S(1)}, s32[]{:S(2)}) async-start(s8[9437184]{0:T(1024)(128)(4,1)} %bitcast.294), calls=%async_computation.33 | async-start | bytes 2097152
  1130.8 209.4 %all-to-all-start.5 = ((bf16[1,2,1152,2048]{3,1,0,2:T(2,128)(2,1)}), bf16[1,2,1152,2048]{3,1,0,2:T(2,128)(2,1)}, u32[]{:S(2)}, u32[]{:S(2)}) async-start(bf16[1,2,1152,2048]{3,1,0,2:T(2,128)(2,1)} %copy.228), calls=%async_computation.5 | async-start | bytes 18874368 | tf_op jit(solution)/shard_map/all_to_all | solution.py:265
  1135.9 744.9 %reduce-scatter.21.cloned.1.call-start = ((), (), s32[]{:S(2)}) async-start(), calls=%async_computation.30 | async-start | bytes 10485760 | tf_op jit(solution)/shard_map/reduce_scatter | solution.py:306
  1340.2 209.7 %all-to-all-start.7 = ((bf16[1,2,1152,2048]{3,1,0,2:T(2,128)(2,1)}), bf16[1,2,1152,2048]{3,1,0,2:T(2,128)(2,1)}, u32[]{:S(2)}, u32[]{:S(2)}) async-start(bf16[1,2,1152,2048]{3,1,0,2:T(2,128)(2,1)} %copy.232), calls=%async_computation.7 | async-start | bytes 18874368 | tf_op jit(solution)/shard_map/all_to_all | solution.py:301
  1345.3 539.6 %reduce-scatter.19.cloned.1.call-start = ((), (), s32[]{:S(2)}) async-start(), calls=%async_computation.29 | async-start | bytes 10485760 | tf_op jit(solution)/shard_map/reduce_scatter | solution.py:303
  1362.4 533.9 %reduce-scatter.15.cloned.1.call-start = ((), (), s32[]{:S(2)}) async-start(), calls=%async_computation.27 | async-start | bytes 9437184 | tf_op jit(solution)/shard_map/reduce_scatter | solution.py:393
  1386.9 22.1 copy-start.13
  1386.9 22.1 copy-start.39
  1571.0 21.5 copy-start.48
  1571.0 21.5 copy-start.67
  1571.0 21.5 copy-start.76
  1571.0 21.5 copy-start.58
  1624.4 20.0 copy-start.54
  1624.4 20.0 copy-start.60
  1624.4 18.9 all-to-all-start.8
  1628.8 325.0 %reduce-scatter.13.cloned.1.call-start = ((), (), s32[]{:S(2)}) async-start(), calls=%async_computation.26 | async-start | bytes 9437184 | tf_op jit(solution)/shard_map/reduce_scatter | solution.py:384
  1781.0 19.2 copy-start.2
  1781.0 19.2 copy-start.44
  1806.1 18.0 all-to-all-start.9
  1824.1 18.8 all-to-all-start.10
  1828.3 277.5 %reduce-scatter.11.cloned.1.call-start = ((), (), s32[]{:S(2)}) async-start(), calls=%async_computation.25 | async-start | bytes 9437184 | tf_op jit(solution)/shard_map/reduce_scatter | solution.py:381
  1860.9 396.6 %reduce-scatter.9.cloned.1.call-start = ((), (), s32[]{:S(2)}) async-start(), calls=%async_computation.24 | async-start | bytes 9437184 | tf_op jit(solution)/shard_map/reduce_scatter | solution.py:378
  1873.8 440.3 %reduce-scatter.17.cloned.1.call-start = ((), (), s32[]{:S(2)}) async-start(), calls=%async_computation.28 | async-start | bytes 73728 | tf_op jit(solution)/shard_map/reduce_scatter | solution.py:399
  1876.6 525.5 %all-reduce.17.cloned.1.call-start = ((), (), s32[]{:S(2)}) async-start(), calls=%async_computation.32 | async-start | bytes 8388608 | tf_op jit(solution)/shard_map/psum | solution.py:405
  1896.3 361.1 %copy-start.26 = (bf16[256,2048]{1,0:T(8,128)(2,1)S(1)}, bf16[256,2048]{1,0:T(8,128)(2,1)}, u32[]{:S(2)}) copy-start(bf16[256,2048]{1,0:T(8,128)(2,1)} %copy-done.25) | copy-start | bytes 3145732
  2264.0 63.1 %copy-start.78 = (f32[256]{0:T(256)S(1)}, f32[256]{0:T(256)}, u32[]{:S(2)}) copy-start(f32[256]{0:T(256)} %copy-done.77) | copy-start | bytes 3076
  2264.0 63.1 %copy-start.11 = (f32[256,2048]{1,0:T(8,128)S(1)}, f32[256,2048]{1,0:T(8,128)}, u32[]{:S(2)}) copy-start(f32[256,2048]{1,0:T(8,128)} %copy-done.9) | copy-start | bytes 6291460
  (76 other events, 413.7 us)
Sparse Core Ops, SparseCore 0:
  10.2 127.7 all-gather.12
  140.1 123.0 all-gather.10
  265.4 123.1 all-gather.8
  390.5 123.1 all-gather.14
  1088.8 70.7 reduce-scatter.22
  1162.1 71.7 reduce-scatter.20
  1362.5 72.9 reduce-scatter.18
  1616.1 148.3 reduce-scatter.14
  1806.2 147.5 reduce-scatter.12
  1957.7 148.0 reduce-scatter.10
  2109.4 148.0 reduce-scatter.8
  2261.3 52.7 reduce-scatter.16
  2316.8 85.1 all-reduce.16
where the time goes:
time: 2430 us; the launch traced here: 2420 us
  waiting for transfers between devices  1240 us (51%)
  matrix products  362 us (15%)
  blocking collectives  355 us (15%)
  local copies, waits for them, and re-layouts  288 us (12%)
  other arithmetic  99.4 us (4%)
  starting transfers between devices  49.4 us (2%)
    all_gather x1, blocking collectives, body(): lax.all_gather(w_router, 'ep', axis=0, tiled=True)  217 us
    all_to_all x1, waiting for transfers between devices, body(): lax.all_to_all(d_send, 'ep', split_axis=0, concat_axis=2, tiled=True)[0]  191 us
    reduce_scatter x1, waiting for transfers between devices, body(): lax.psum_scatter(grad_key_full.astype(jnp.bfloat16), 'ep', scatter_dimens...  152 us
    reduce_scatter x1, waiting for transfers between devices, body(): lax.psum_scatter(grad_query_full.astype(jnp.bfloat16), 'ep', scatter_dime...  152 us
    all_to_all x1, waiting for transfers between devices, body(): lax.all_to_all(d_rows_in[None], 'ep', split_axis=2, concat_axis=0, tiled=...  131 us
    all_to_all x1, waiting for transfers between devices, body(): lax.all_to_all(expert_out[None], 'ep', split_axis=2, concat_axis=0, tiled...  128 us
    all_gather x1, waiting for transfers between devices, body(): lax.all_gather(w_query, 'ep', axis=0, tiled=True)  116 us
    all_gather x1, waiting for transfers between devices, body(): lax.all_gather(w_key, 'ep', axis=0, tiled=True)  114 us
  transfers between devices with their start and end apart: 24, of which 17 were waited for; matrix products, arithmetic and copies ran while one was open for 26% of the time, Pallas kernels for 0%

commit v1 on v0

v1 whole, which is shorter than its diff:
```python
import functools

import jax
import jax.numpy as jnp
from jax import lax
from jax.experimental import pallas as pl
from jax.experimental.pallas import tpu as pltpu
from jax.sharding import PartitionSpec as P

HEAD_DIM = 128
EPS = 1e-05
THETA = 10000.0
NEG_FILL = -1e30
F32 = jnp.float32
BF16 = jnp.bfloat16
MIB = 1 << 20


def product(left, right):
    return jnp.dot(left, right, preferred_element_type=F32)


def product_left(left, right):
    return lax.dot_general(left, right, (((0,), (0,)), ((), ())), preferred_element_type=F32)


def product_right(left, right):
    return lax.dot_general(left, right, (((1,), (1,)), ((), ())), preferred_element_type=F32)


def row_sums(values_in):
    ones = jnp.ones((8, values_in.shape[1]), F32)
    return lax.dot_general(
        ones, values_in, (((1,), (1,)), ((), ())),
        preferred_element_type=F32, precision=lax.Precision.HIGHEST,
    )


def call(kernel, out_shape, args, flops, name, scratch=(), scalars=(), grid=(1,), in_specs=None,
         out_specs=None, aliases=None, vmem=60):
    single = not isinstance(out_shape, (list, tuple))
    shapes = [out_shape] if single else list(out_shape)
    count = len(grid)

    def fixed(shape):
        rank = len(shape)
        return pl.BlockSpec(tuple(shape), lambda *ids: (0,) * rank)

    in_specs = in_specs or [None] * len(args)
    out_specs = out_specs or [None] * len(shapes)
    in_specs = [s if s is not None else fixed(a.shape) for s, a in zip(in_specs, args)]
    out_specs = [s if s is not None else fixed(o.shape) for s, o in zip(out_specs, shapes)]
    moved = sum(a.size * a.dtype.itemsize for a in args)
    moved += sum(o.size * o.dtype.itemsize for o in shapes)
    result = pl.pallas_call(
        kernel,
        grid_spec=pltpu.PrefetchScalarGridSpec(
            num_scalar_prefetch=len(scalars), grid=grid, in_specs=in_specs, out_specs=out_specs,
            scratch_shapes=list(scratch),
        ),
        out_shape=shapes,
        input_output_aliases={k + len(scalars): v for k, v in (aliases or {}).items()},
        compiler_params=pltpu.CompilerParams(
            vmem_limit_bytes=vmem * MIB, dimension_semantics=("arbitrary",) * count
        ),
        cost_estimate=pl.CostEstimate(flops=int(flops), bytes_accessed=int(moved), transcendentals=0),
        name=name,
    )(*scalars, *args)
    return result[0] if single else result


def like(shape, dtype):
    return jax.ShapeDtypeStruct(tuple(shape), dtype)


MIDDLE = [(2, 4), (3, 5), (4, 2), (5, 3)]
OUTWARD = [(2, 0), (3, 1), (4, 6), (5, 7)]
INWARD = [(0, 2), (1, 3), (6, 4), (7, 5)]


def shift(value, pairs):
    return lax.ppermute(value, "ep", pairs)


def swap(value, bits):
    return shift(value, [(i, i ^ bits) for i in range(8)])


def swap_sp(value, bits):
    return lax.ppermute(value, "sp", [(i, i ^ bits) for i in range(4)])


def piece_blocks(n_ep, ep_index):
    ids = jnp.arange(n_ep, dtype=jnp.int32)
    return jnp.bitwise_xor(ids, ep_index) if n_ep == 8 else ids


def gather_line(value, n_ep):
    if n_ep != 8:
        return gather_turn(value, n_ep)
    near = swap(value, 2)
    inner_a = shift(value, MIDDLE)
    inner_b = shift(near, MIDDLE)
    third = inner_b + shift(inner_a, OUTWARD)
    fourth = inner_a + shift(inner_b, OUTWARD)
    pieces = []
    for own in (value, near, third, fourth):
        pieces += [own, swap(own, 1)]
    return pieces


def gather_turn(value, n_ep):
    if n_ep != 8:
        whole = lax.all_gather(value, "ep", axis=0, tiled=False)
        return [whole[i] for i in range(n_ep)]
    pieces = []
    for own in (value, swap(value, 2), swap(value, 4), swap(value, 6)):
        pieces += [own, swap(own, 1)]
    return pieces


def plus(left, right):
    return (left.astype(F32) + right.astype(F32)).astype(left.dtype)


def scatter_line(pieces, n_ep):
    if n_ep != 8:
        return scatter_turn(pieces, n_ep)
    own, near, third, fourth = (plus(pieces[2 * i], swap(pieces[2 * i + 1], 1)) for i in range(4))
    third_in, fourth_in = shift(fourth, INWARD), shift(third, INWARD)
    third, fourth = plus(third, third_in), plus(fourth, fourth_in)
    near = plus(near, shift(third, MIDDLE))
    return own.astype(F32) + shift(fourth, MIDDLE).astype(F32) + swap(near, 2).astype(F32)


def scatter_turn(pieces, n_ep):
    if n_ep != 8:
        stacked = jnp.stack(pieces)
        return lax.psum_scatter(stacked, "ep", scatter_dimension=0, tiled=False).astype(F32)
    sums = [plus(pieces[2 * i], swap(pieces[2 * i + 1], 1)) for i in range(4)]
    total = sums[0].astype(F32)
    for i in range(1, 4):
        total = total + swap(sums[i], 2 * i).astype(F32)
    return total


def gather_sp(value):
    over = swap_sp(value, 2)
    return [value, swap_sp(value, 1), over, swap_sp(over, 1)]


def sum_sp(value):
    value = value + swap_sp(value, 1)
    return value + swap_sp(value, 2)


def block_at(ids, position, size):
    if size % HEAD_DIM:
        return pl.ds(position * size, size)
    return pl.ds(pl.multiple_of(ids[position] * size, size), size)


def qk_kernel(count, ids, h_ref, *refs):
    pieces, (q_ref, k_ref, squares_ref, w_ref) = refs[:count], refs[count:]
    shard = pieces[0].shape[0]

    @pl.when(pl.program_id(0) == 0)
    def _():
        for k in range(count):
            w_ref[block_at(ids, k, shard), :] = pieces[k][...]

    width = q_ref.shape[1]
    for at, ref in enumerate((q_ref, k_ref)):
        part = product(h_ref[...], w_ref[:, at * width : (at + 1) * width])
        ref[...] = part
        squares_ref[8 * at : 8 * at + 8, :] = row_sums(part * part)


def qk_project(ids, h_all, pieces):
    total, depth = h_all.shape
    shard, both = pieces[0].shape
    width = both // 2
    rows = min(256, total)
    block = pl.BlockSpec((rows, width), lambda i, ids: (i, 0))
    return call(
        functools.partial(qk_kernel, len(pieces)),
        [like((total, width), F32)] * 2 + [like((16, total), F32), like((depth, both), BF16)],
        [h_all, *pieces],
        2 * total * depth * both,
        "qk_project",
        scalars=(ids,),
        grid=(total // rows,),
        in_specs=[pl.BlockSpec((rows, depth), lambda i, ids: (i, 0))] + [None] * len(pieces),
        out_specs=[block, block, pl.BlockSpec((16, rows), lambda i, ids: (0, i)), None],
    )


def v_kernel(count, ids, h_ref, *refs):
    pieces, (v_ref, w_ref, out_ref) = refs[:count], refs[count:]
    shard = pieces[0].shape[0]
    width = v_ref.shape[1]

    @pl.when(pl.program_id(0) == 0)
    def _():
        for k in range(count):
            rows = block_at(ids, k, shard)
            w_ref[rows, :] = pieces[k][:, :width]
            out_ref[rows, :] = pieces[k][:, width:]

    v_ref[...] = product(h_ref[...], w_ref[...]).astype(BF16)


def v_project(ids, h_all, pieces):
    total, depth = h_all.shape
    width = pieces[0].shape[1] // 2
    rows = min(256, total)
    return call(
        functools.partial(v_kernel, len(pieces)),
        [like((total, width), BF16), like((depth, width), BF16), like((depth, width), BF16)],
        [h_all, *pieces],
        2 * total * depth * width,
        "v_project",
        scalars=(ids,),
        grid=(total // rows,),
        in_specs=[pl.BlockSpec((rows, depth), lambda i, ids: (i, 0))] + [None] * len(pieces),
        out_specs=[pl.BlockSpec((rows, width), lambda i, ids: (i, 0)), None, None],
    )


def out_kernel(n_ep, ids, attn_ref, x_ref, gain_ref, *refs):
    weights, (one_ref, low_ref) = refs[:-2], refs[-2:]
    width = weights[0].shape[1]
    for j, weight in enumerate(weights):
        cols = block_at(ids, n_ep + j, width)
        one_ref[:, cols] = x_ref[:, cols].astype(F32) + product(attn_ref[...], weight[...])
    one = one_ref[...]
    scale = lax.rsqrt(jnp.mean(one * one, axis=1, keepdims=True) + EPS)
    low_ref[...] = (one * scale * gain_ref[...]).astype(BF16)


def out_project(ids, n_ep, attn_tok, tokens, gain, weights):
    return call(
        functools.partial(out_kernel, n_ep),
        [like(tokens.shape, F32), like(tokens.shape, BF16)],
        [attn_tok, tokens, gain, *weights],
        2 * tokens.size * attn_tok.shape[1],
        "out_project",
        scalars=(ids,),
    )


def out_back_kernel(n_ep, ids, d_ref, *refs):
    weights, d_attn_ref = refs[:-1], refs[-1]
    width = weights[0].shape[1]
    total = None
    for j, weight in enumerate(weights):
        part = product_right(d_ref[:, block_at(ids, n_ep + j, width)], weight[...])
        total = part if total is None else total + part
    d_attn_ref[...] = total.astype(BF16)


def out_back(ids, n_ep, d_z, weights):
    return call(
        functools.partial(out_back_kernel, n_ep),
        like((d_z.shape[0], weights[0].shape[0]), BF16),
        [d_z, *weights],
        2 * d_z.size * weights[0].shape[0],
        "out_back",
        scalars=(ids,),
    )


def grad_pieces_kernel(count, ids, left_ref, right_ref, *pieces):
    shard = pieces[0].shape[0]
    for k in range(count):
        pieces[k][...] = product_left(
            left_ref[:, block_at(ids, k, shard)], right_ref[...]
        ).astype(BF16)


def grad_pieces(ids, count, left, right, name):
    shard = left.shape[1] // count
    return call(
        functools.partial(grad_pieces_kernel, count),
        [like((shard, right.shape[1]), BF16)] * count,
        [left, right],
        2 * left.size * right.shape[1],
        name,
        scalars=(ids,),
    )


def qkv_back_kernel(
    count, width_all, ids, h_ref, dqn_ref, dkn_ref, dv_ref, qr_ref, kr_ref, scale_ref, sums_ref,
    tiny_ref, *refs
):
    pieces, d_ref = refs[:count], refs[count]
    width = dv_ref.shape[1]
    scales = jnp.transpose(scale_ref[...])
    means = jnp.transpose(sums_ref[...]) * (1.0 / width_all)
    for at, (d_normed, raw) in enumerate(((dqn_ref, qr_ref), (dkn_ref, kr_ref))):
        scale, mean = scales[:, 8 * at : 8 * at + 1], means[:, 8 * at : 8 * at + 1]
        d_ref[:, at * width : (at + 1) * width] = (
            scale * (d_normed[...] - raw[...] * scale * mean)
        ).astype(BF16)
    d_ref[:, 2 * width :] = dv_ref[...]
    shard = h_ref.shape[1] // count
    per_row = 3 * width // shard
    for k in range(count):
        block = block_at(ids, k, shard)
        pieces[k][:shard, :] = product_left(h_ref[:, block], d_ref[...]).astype(BF16)
        pieces[k][shard:, :] = jnp.zeros_like(pieces[k][shard:, :])
        for at in range(tiny_ref.shape[0]):
            row, col = shard + at // per_row, (at % per_row) * shard
            pieces[k][row : row + 1, col : col + shard] = tiny_ref[at : at + 1, block].astype(BF16)


def qkv_back(ids, count, h_all, d_qn, d_kn, d_v, q_raw, k_raw, scales, sums, tiny):
    total, depth = h_all.shape
    width = d_v.shape[1]
    shard = depth // count
    extra = -(-tiny.shape[0] // (3 * width // shard))
    extra = -(-extra // 16) * 16
    return call(
        functools.partial(qkv_back_kernel, count, depth),
        [like((shard + extra, 3 * width), BF16)] * count + [like((total, 3 * width), BF16)],
        [h_all, d_qn, d_kn, d_v, q_raw, k_raw, scales, sums, tiny],
        2 * h_all.size * 3 * width,
        "qkv_back",
        scalars=(ids,),
    )


def d_h_kernel(d_ref, qk_ref, v_ref, out_ref):
    both = qk_ref.shape[1]
    out_ref[...] = (
        product_right(d_ref[:, :both], qk_ref[...]) + product_right(d_ref[:, both:], v_ref[...])
    ).astype(BF16)


def d_h_rows(d_qkv, w_qk, w_v):
    total, wide = d_qkv.shape
    depth = w_qk.shape[0]
    rows = min(256, total)
    return call(
        d_h_kernel,
        like((total, depth), BF16),
        [d_qkv, w_qk, w_v],
        2 * d_qkv.size * depth,
        "d_h",
        grid=(total // rows,),
        in_specs=[pl.BlockSpec((rows, wide), lambda i: (i, 0)), None, None],
        out_specs=[pl.BlockSpec((rows, depth), lambda i: (i, 0))],
    )


def finish_kernel(n_ep, ids, wq_ref, wk_ref, wv_ref, gain_ref, *refs):
    parts, (gq_ref, gk_ref, gv_ref, tiny_ref, attn_ref) = refs[:-5], refs[-5:]
    shard = wq_ref.shape[0]
    width = parts[0].shape[1] // 3
    dots = jnp.zeros((shard, 1), F32)
    tiny = jnp.zeros(tiny_ref.shape, F32)
    for j, part in enumerate(parts):
        cols = block_at(ids, n_ep + j, width)
        for at, (grad, weight) in enumerate(((gq_ref, wq_ref), (gk_ref, wk_ref), (gv_ref, wv_ref))):
            value = part[:shard, at * width : (at + 1) * width].astype(F32)
            grad[:, cols] = value
            dots += jnp.sum(value * weight[:, cols].astype(F32), axis=1, keepdims=True)
        tiny += part[shard:, :].astype(F32)
    tiny_ref[...] = tiny
    attn_ref[...] = dots / gain_ref[...]


def finish(ids, n_ep, w_query, w_key, w_value, gain, parts):
    shard, depth = w_query.shape
    extra = parts[0].shape[0] - shard
    return call(
        functools.partial(finish_kernel, n_ep),
        [like((shard, depth), F32)] * 3 + [like((extra, parts[0].shape[1]), F32), like((shard, 1), F32)],
        [w_query, w_key, w_value, gain, *parts],
        shard * depth * 6,
        "finish",
        scalars=(ids,),
    )


def turn(values_in):
    return pltpu.roll(values_in, HEAD_DIM // 2, 1)


def masked_probs(q_ref, k_ref, start_ref, block, rows):
    first, last = block * rows, (block + 1) * rows
    scores = product_right(q_ref[first:last, :], k_ref[0:last, :]) * (HEAD_DIM ** (-0.5))
    row_ids = first + lax.broadcasted_iota(jnp.int32, scores.shape, 0)
    places = lax.broadcasted_iota(jnp.int32, scores.shape, 1)
    allowed = (places <= row_ids) & (places >= start_ref[first:last, :])
    scores = jnp.where(allowed, scores, NEG_FILL)
    top = jnp.max(scores, axis=1, keepdims=True)
    weights = jnp.exp(scores - top)
    return weights * (1.0 / jnp.sum(weights, axis=1, keepdims=True))


def attend_kernel(
    rows, qr_ref, kr_ref, v_ref, scale_ref, gq_ref, gk_ref, cos_ref, sin_ref, start_ref,
    q_ref, k_ref, out_ref,
):
    scales = jnp.transpose(scale_ref[...])
    for at, (raw, gain, low) in enumerate(((qr_ref, gq_ref, q_ref), (kr_ref, gk_ref, k_ref))):
        normed = raw[...] * scales[:, 8 * at : 8 * at + 1] * gain[...]
        low[...] = (normed * cos_ref[...] + turn(normed) * sin_ref[...]).astype(BF16)
    for block in range(q_ref.shape[0] // rows):
        probs = masked_probs(q_ref, k_ref, start_ref, block, rows)
        last = (block + 1) * rows
        out_ref[block * rows : last, :] = product(
            probs.astype(BF16), v_ref[0:last, :]
        ).astype(BF16)


def head_spec(rows):
    return pl.BlockSpec((rows, HEAD_DIM), lambda h: (0, h))


def attend(q_raw, k_raw, v_low, scales, q_gain, k_gain, cosine, sine, starts):
    total, width = v_low.shape
    heads = width // HEAD_DIM
    head, gain = head_spec(total), head_spec(1)
    return call(
        functools.partial(attend_kernel, min(256, total)),
        [like((total, width), BF16)] * 3,
        [q_raw, k_raw, v_low, scales, q_gain, k_gain, cosine, sine, starts],
        3 * heads * total * total * HEAD_DIM,
        "attend",
        grid=(heads,),
        in_specs=[head, head, head, None, gain, gain, None, None, None],
        out_specs=[head, head, head],
    )


def attend_back_kernel(
    rows, q_ref, k_ref, v_ref, do_ref, qr_ref, kr_ref, scale_ref, gq_ref, gk_ref,
    cos_ref, sin_ref, start_ref,
    dq_ref, dk_ref, dv_ref, sums_ref, dgq_ref, dgk_ref, q_acc, k_acc, v_acc,
):
    k_acc[...] = jnp.zeros_like(k_acc)
    v_acc[...] = jnp.zeros_like(v_acc)
    for block in range(q_ref.shape[0] // rows):
        first, last = block * rows, (block + 1) * rows
        probs = masked_probs(q_ref, k_ref, start_ref, block, rows)
        d_rows = do_ref[first:last, :]
        d_probs = product_right(d_rows, v_ref[0:last, :])
        delta = jnp.sum(probs * d_probs, axis=1, keepdims=True)
        d_scores = (probs * (d_probs - delta) * (HEAD_DIM ** (-0.5))).astype(BF16)
        q_acc[first:last, :] = product(d_scores, k_ref[0:last, :])
        k_acc[0:last, :] += product_left(d_scores, q_ref[first:last, :])
        v_acc[0:last, :] += product_left(probs.astype(BF16), d_rows)
    dv_ref[...] = v_acc[...].astype(BF16)

    @pl.when(pl.program_id(0) == 0)
    def _():
        sums_ref[...] = jnp.zeros_like(sums_ref)

    scales = jnp.transpose(scale_ref[...])
    for at, (acc, raw, gain, d_ref, dg_ref) in enumerate(
        ((q_acc, qr_ref, gq_ref, dq_ref, dgq_ref), (k_acc, kr_ref, gk_ref, dk_ref, dgk_ref))
    ):
        turned = acc[...].astype(BF16).astype(F32)
        back = turned * cos_ref[...] + turn(turned * sin_ref[...])
        normed = raw[...] * scales[:, 8 * at : 8 * at + 1]
        both = back * normed
        dg_ref[...] = jnp.sum(both, axis=0, keepdims=True)
        d_ref[...] = back * gain[...]
        sums_ref[8 * at : 8 * at + 8, :] += row_sums(both * gain[...])


def attend_back(
    q_rot, k_rot, v_low, d_heads, q_raw, k_raw, scales, q_gain, k_gain, cosine, sine, starts
):
    total, width = v_low.shape
    heads = width // HEAD_DIM
    head, gain = head_spec(total), head_spec(1)
    wide, thin = like((total, width), F32), like((1, width), F32)
    return call(
        functools.partial(attend_back_kernel, min(256, total)),
        [wide, wide, like((total, width), BF16), like((16, total), F32), thin, thin],
        [q_rot, k_rot, v_low, d_heads, q_raw, k_raw, scales, q_gain, k_gain, cosine, sine, starts],
        7 * heads * total * total * HEAD_DIM,
        "attend_back",
        scratch=[pltpu.VMEM((total, HEAD_DIM), F32)] * 3,
        grid=(heads,),
        in_specs=[head] * 6 + [None, gain, gain, None, None, None],
        out_specs=[head, head, head, None, gain, gain],
    )


def chooser(places_ref, at, cap):
    row = places_ref[at : at + 1, :]
    slots = lax.broadcasted_iota(jnp.int32, (cap, row.shape[1]), 0)
    return slots == row


def dispatch_kernel(
    pieces_here, local, cap, gated, mine, *refs
):
    pieces, refs = refs[:pieces_here], refs[pieces_here:]
    places_ref, refs = refs[0], refs[1:]
    if gated:
        (picked_ref, router_ref), refs = refs[:2], refs[2:]
        rows_ref, gate_ref, all_ref = refs[-3:]
    else:
        rows_ref = refs[-1]
    for p in range(pieces_here):
        if gated:
            logits = product_right(router_ref[...], pieces[p][...])
            experts = logits.shape[0]
            picked = picked_ref[p * experts : (p + 1) * experts, :] > 0
            logits = jnp.where(picked, logits, NEG_FILL)
            weights = jnp.exp(logits - jnp.max(logits, axis=0, keepdims=True))
            weights = jnp.where(picked, weights, 0.0)
            gates = weights / jnp.sum(weights, axis=0, keepdims=True)
            all_ref[p * experts : (p + 1) * experts, :] = gates
        for e in range(local):
            chosen = chooser(places_ref, p * local + e, cap)
            rows_ref[e, p * cap : (p + 1) * cap, :] = product(
                chosen.astype(BF16), pieces[p][...]
            ).astype(BF16)
            if gated:
                row = all_ref[pl.ds(p * experts + mine[0] * local + e, 1), :]
                gate_ref[e, p * cap : (p + 1) * cap, :] = jnp.sum(
                    jnp.where(chosen, row, 0.0), axis=1, keepdims=True
                )


def dispatch(mine, pieces, places, picked, router, local, cap, group, at, rows, gates):
    gated = router is not None
    here = len(pieces)
    width = pieces[0].shape[1]
    args = [*pieces, places]
    shapes = [like((local, group * cap, width), BF16)]
    spec = pl.BlockSpec((local, here * cap, width), lambda i, mine: (0, at, 0))
    out_specs = [spec]
    if gated:
        args += [picked, router]
        shapes += [like((local, group * cap, 1), F32), like((picked.shape[0], places.shape[1]), F32)]
        out_specs += [pl.BlockSpec((local, here * cap, 1), lambda i, mine: (0, at, 0)), None]
    in_specs = [None] * len(args)
    aliases = {}
    if rows is not None:
        aliases[len(args)] = 0
        args.append(rows)
        in_specs.append(pl.BlockSpec(memory_space=pl.ANY))
        if gated:
            aliases[len(args)] = 1
            args.append(gates)
            in_specs.append(pl.BlockSpec(memory_space=pl.ANY))
    return call(
        functools.partial(dispatch_kernel, here, local, cap, gated),
        shapes,
        args,
        2 * here * local * cap * places.shape[1] * width,
        "dispatch",
        scalars=(mine,),
        in_specs=in_specs,
        out_specs=out_specs,
        aliases=aliases,
    )


def expert_kernel(
    x_ref, d_ref, gate_ref, wg_ref, wu_ref, wd_ref,
    act_ref, dg_ref, du_ref, dots_ref, mix_ref, back_ref, mix_acc, back_acc,
):
    step = pl.program_id(1)
    last = pl.num_programs(1) - 1
    x_rows, d_rows, gate = x_ref[0], d_ref[0], gate_ref[0]
    pre = product(x_rows, wg_ref[0])
    up = product(x_rows, wu_ref[0])
    pulled = product_right(d_rows, wd_ref[0])
    sigma = jax.nn.sigmoid(pre)
    silu = pre * sigma
    act = silu * up
    dots = jnp.sum(act * pulled, axis=1, keepdims=True)
    act_low = (act * gate).astype(BF16)
    act_ref[0] = act_low
    d_act = pulled * gate
    du_low = (d_act * silu).astype(BF16)
    dg_low = (d_act * up * sigma * (1.0 + pre * (1.0 - sigma))).astype(BF16)
    dg_ref[0] = dg_low
    du_ref[0] = du_low
    mix = product(act_low, wd_ref[0])
    back = product_right(dg_low, wg_ref[0]) + product_right(du_low, wu_ref[0])

    @pl.when(step == 0)
    def _():
        dots_ref[0] = dots
        mix_acc[...] = mix
        back_acc[...] = back

    @pl.when((step > 0) & (step < last))
    def _():
        dots_ref[0] += dots
        mix_acc[...] += mix
        back_acc[...] += back

    @pl.when(step == last)
    def _():
        dots_ref[0] += dots
        mix_ref[0] = (mix_acc[...] + mix).astype(BF16)
        back_ref[0] = (back_acc[...] + back).astype(BF16)


def experts(rows, d_rows, gates, w_gate, w_up, w_down):
    local, count, width = rows.shape
    hidden = w_gate.shape[2]
    part = hidden // 2
    wide = pl.BlockSpec((1, count, width), lambda e, f: (e, 0, 0))
    column = pl.BlockSpec((1, count, 1), lambda e, f: (e, 0, 0))
    thin = pl.BlockSpec((1, count, part), lambda e, f: (e, 0, f))
    into = pl.BlockSpec((1, width, part), lambda e, f: (e, 0, f))
    outof = pl.BlockSpec((1, part, width), lambda e, f: (e, f, 0))
    return call(
        expert_kernel,
        [like((local, count, hidden), BF16)] * 3
        + [like((local, count, 1), F32)]
        + [like((local, count, width), BF16)] * 2,
        [rows, d_rows, gates, w_gate, w_up, w_down],
        12 * rows.size * hidden,
        "experts",
        scratch=[pltpu.VMEM((count, width), F32)] * 2,
        grid=(local, 2),
        in_specs=[wide, wide, column, into, into, outof],
        out_specs=[thin, thin, thin, column, wide, wide],
    )


def combine_kernel(here, local, cap, dotted, places_ref, rows_ref, *refs):
    pieces = refs[int(dotted) : int(dotted) + here]
    for p in range(here):
        chosen = [chooser(places_ref, p * local + e, cap) for e in range(local)]
        total = None
        for e in range(local):
            part = product_left(chosen[e].astype(BF16), rows_ref[e, p * cap : (p + 1) * cap, :])
            total = part if total is None else total + part
            if dotted:
                refs[-1][p * local + e : p * local + e + 1, :] = jnp.sum(
                    jnp.where(chosen[e], refs[0][e, p * cap : (p + 1) * cap, :], 0.0),
                    axis=0, keepdims=True,
                )
        pieces[p][...] = total.astype(BF16)


def combine(places, rows, here, local, cap, at, dots=None):
    width = rows.shape[2]
    tokens = places.shape[1]
    dotted = dots is not None
    args = [places, rows] + ([dots] if dotted else [])
    in_specs = [None, pl.BlockSpec((local, here * cap, width), lambda i: (0, at, 0))]
    if dotted:
        in_specs.append(pl.BlockSpec((local, here * cap, 1), lambda i: (0, at, 0)))
    shapes = [like((tokens, width), BF16)] * here
    if dotted:
        shapes.append(like(places.shape, F32))
    return call(
        functools.partial(combine_kernel, here, local, cap, dotted),
        shapes,
        args,
        2 * here * local * cap * tokens * width,
        "combine",
        in_specs=in_specs,
    )


def weight_grad_kernel(groups, *refs):
    lefts, rights = refs[:groups], refs[groups : 2 * groups]
    total = None
    for left, right in zip(lefts, rights):
        part = product_left(left[0], right[0])
        total = part if total is None else total + part
    refs[-1][0] = total.astype(BF16)


def weight_grad(lefts, rights):
    local, count, tall = lefts[0].shape
    wide = rights[0].shape[2]
    part = min(512, tall)
    left = pl.BlockSpec((1, count, part), lambda e, i: (e, 0, i))
    right = pl.BlockSpec((1, count, wide), lambda e, i: (e, 0, 0))
    return call(
        functools.partial(weight_grad_kernel, len(lefts)),
        like((local, tall, wide), BF16),
        [*lefts, *rights],
        2 * len(lefts) * lefts[0].size * wide,
        "weight_grad",
        grid=(local, tall // part),
        in_specs=[left] * len(lefts) + [right] * len(lefts),
        out_specs=[pl.BlockSpec((1, part, wide), lambda e, i: (e, i, 0))],
    )


def tie(*values):
    return lax.optimization_barrier(values)


def body(
    tokens, doc_lengths, routes, attn_gain, w_query, w_key, w_value, q_gain, k_gain, w_out,
    ffn_gain, w_router, w_gate, w_up, w_down, cotangent,
):
    n_sp = lax.axis_size("sp")
    n_ep = lax.axis_size("ep")
    sp_index = lax.axis_index("sp")
    ep_index = lax.axis_index("ep")
    tok_dev, width = tokens.shape[1:]
    total = tok_dev * n_sp
    shard = width // n_ep
    head_width = width // n_sp
    top_count = routes.shape[2]
    local = w_gate.shape[0]
    expert_count = local * n_ep
    capacity = 9 * tok_dev * top_count // (8 * expert_count)
    cap = -(-capacity // 16) * 16
    group = 4
    blocks = piece_blocks(n_ep, ep_index)
    partners = jnp.bitwise_xor(jnp.arange(n_sp, dtype=jnp.int32), sp_index)
    ids = jnp.concatenate([blocks, partners]).astype(jnp.int32)
    mine = ep_index.astype(jnp.int32).reshape(1)

    def own_columns(value):
        return lax.dynamic_slice_in_dim(value, sp_index * head_width, head_width, 1)

    def by_block(value):
        order = jnp.bitwise_xor(jnp.arange(n_ep, dtype=jnp.int32), ep_index) if n_ep == 8 else blocks
        return jnp.stack(
            [lax.dynamic_index_in_dim(value, order[i], 0, keepdims=False) for i in range(n_ep)]
        )

    qk_pieces = gather_line(
        jnp.concatenate([own_columns(w_query), own_columns(w_key)], axis=1), n_ep
    )

    expert_ids = jnp.arange(expert_count, dtype=jnp.int32)
    picked = jnp.any(routes[0][:, :, None] == expert_ids[None, None, :], axis=1)
    small = jnp.concatenate(
        [
            jnp.stack([attn_gain, q_gain, k_gain, ffn_gain]),
            jnp.zeros((12, shard), BF16),
            w_router.T,
        ],
        axis=0,
    )
    picked_low = picked.T.astype(BF16)
    if shard == tok_dev:
        both = jnp.stack(gather_turn(jnp.concatenate([small, picked_low], axis=0), n_ep))
        small_all, picked_all = both[:, : 16 + expert_count], both[:, 16 + expert_count :]
    else:
        small_all = jnp.stack(gather_turn(small, n_ep))
        picked_all = jnp.stack(gather_turn(picked_low, n_ep))
    small_rows = jnp.swapaxes(by_block(small_all), 0, 1).reshape(16 + expert_count, width)
    gains = small_rows[:4].astype(F32)
    full_router = small_rows[16:]

    x_rows = tokens[0].astype(F32)
    x_scale = lax.rsqrt(jnp.mean(x_rows * x_rows, axis=-1, keepdims=True) + EPS)
    h_low = (x_rows * x_scale * gains[0][None, :]).astype(BF16)
    h_all = lax.all_gather(h_low, "sp", axis=0, tiled=True)

    upper = (
        jnp.arange(tok_dev, dtype=jnp.int32)[:, None] < jnp.arange(tok_dev, dtype=jnp.int32)[None, :]
    ).astype(BF16)
    picked_mine = lax.dynamic_slice_in_dim(picked_all, ep_index * local, local, 1)
    picked_mine = picked_mine.reshape(n_ep * local, tok_dev)
    earlier = product(picked_mine, upper).astype(jnp.int32)
    places = jnp.where((picked_mine > 0) & (earlier < capacity), earlier, -1)
    picked_flat = picked_all.reshape(n_ep * expert_count, tok_dev).astype(F32)

    positions = jnp.arange(total, dtype=jnp.int32)
    lengths = doc_lengths[0]
    doc_ends = jnp.cumsum(lengths)
    starts = jnp.sum(
        jnp.where(doc_ends[None, :] <= positions[:, None], lengths[None, :], 0), axis=1
    )
    half = HEAD_DIM // 2
    frequency = THETA ** (-(2.0 * jnp.arange(half, dtype=F32)) / HEAD_DIM)
    angles = (positions - starts).astype(F32)[:, None] * frequency[None, :]
    cosine = jnp.concatenate([jnp.cos(angles), jnp.cos(angles)], axis=1)
    sine = jnp.concatenate([-jnp.sin(angles), jnp.sin(angles)], axis=1)
    starts = starts[:, None].astype(jnp.int32)

    vo_own = jnp.concatenate([own_columns(w_value), own_columns(w_out)], axis=1)
    *qk_pieces, vo_own = tie(*qk_pieces, vo_own)
    vo_pieces = gather_turn(vo_own, n_ep)
    *vo_pieces, cot_own = tie(*vo_pieces, cotangent[0])
    cot_pieces = gather_turn(cot_own, n_ep)

    q_raw, k_raw, squares, w_qk = qk_project(ids, h_all, qk_pieces)
    scales = lax.rsqrt(sum_sp(squares) / width + EPS)
    v_low, w_v, w_o = v_project(ids, h_all, vo_pieces)
    w_o_parts = gather_sp(w_o)
    gain_q, gain_k = own_columns(gains)[1:2], own_columns(gains)[2:3]
    q_rot, k_rot, mixed = attend(
        q_raw, k_raw, v_low, scales, gain_q, gain_k, cosine, sine, starts
    )
    attn_tok = lax.all_to_all(mixed, "sp", split_axis=0, concat_axis=1, tiled=True)
    x_one, h2_low = out_project(ids, n_ep, attn_tok, tokens[0], gains[3:4], w_o_parts)
    attn_all = lax.all_gather(attn_tok, "sp", axis=0, tiled=True)

    def pair_places(p):
        return places[p * local : (p + 2) * local]

    h2_pieces = gather_line(h2_low, n_ep)
    groups = []
    home_gates = None
    for g in range(0, n_ep, group):
        rows = gates = d_rows = None
        for at, p in enumerate(range(g, g + group, 2)):
            (d_rows,) = dispatch(
                mine, cot_pieces[p : p + 2], pair_places(p), None, None, local, cap, group, at,
                d_rows, None,
            )
        for at, p in enumerate(range(g, g + group, 2)):
            rows, gates, piece_gates = dispatch(
                mine, h2_pieces[p : p + 2], pair_places(p),
                picked_flat[p * expert_count : (p + 2) * expert_count], full_router, local, cap,
                group, at, rows, gates,
            )
            if p == 0:
                home_gates = piece_gates
        groups.append((rows, d_rows, experts(rows, d_rows, gates, w_gate, w_up, w_down)))

    d_pieces, d_gates = [], []
    for g, (_, _, made) in enumerate(groups):
        for at in range(group // 2):
            p = g * group + 2 * at
            *two, dots = combine(pair_places(p), made[5], 2, local, cap, at, made[3])
            d_pieces += two
            d_gates.append(dots)
    d_h2 = scatter_line(d_pieces, n_ep)
    d_gates = by_block(jnp.concatenate(d_gates, axis=0).reshape(n_ep, local, tok_dev))
    d_gates = lax.all_to_all(d_gates, "ep", split_axis=0, concat_axis=0, tiled=True)
    d_gates = d_gates.reshape(expert_count, tok_dev)

    acts = [made[0] for _, _, made in groups]
    d_gate_rows = [made[1] for _, _, made in groups]
    d_up_rows = [made[2] for _, _, made in groups]
    ins = [rows for rows, _, _ in groups]
    outs = [d_rows for _, d_rows, _ in groups]
    grad_down = weight_grad(acts, outs)
    grad_gate = weight_grad(ins, d_gate_rows)
    grad_up = weight_grad(ins, d_up_rows)
    d_h2, grad_down, grad_gate, grad_up = tie(d_h2, grad_down, grad_gate, grad_up)

    def over_sp(value):
        return lax.psum_scatter(value, "sp", scatter_dimension=1, tiled=True).astype(F32)

    grad_down, grad_gate, grad_up = over_sp(grad_down), over_sp(grad_gate), over_sp(grad_up)

    if n_ep == 8:
        gates_here = home_gates[:expert_count]
    else:
        logits = product_right(full_router, h2_low)
        logits = jnp.where(picked.T, logits, NEG_FILL)
        gates_here = jax.nn.softmax(logits, axis=0)
    d_logits = gates_here * (d_gates - jnp.sum(gates_here * d_gates, axis=0, keepdims=True))
    d_logits = jnp.where(picked.T, d_logits, 0.0).astype(BF16)
    grad_router = product(d_logits, h2_low)
    d_h2 = d_h2 + product_left(d_logits, full_router)
    one_scale = lax.rsqrt(jnp.mean(x_one * x_one, axis=-1, keepdims=True) + EPS)
    one_normed = x_one * one_scale
    grad_ffn = jnp.sum(d_h2 * one_normed, axis=0)
    d_normed = d_h2 * gains[3][None, :]
    d_one = cotangent[0].astype(F32) + one_scale * (
        d_normed - one_normed * jnp.mean(d_normed * one_normed, axis=-1, keepdims=True)
    )
    d_z = d_one.astype(BF16)
    d_attn = out_back(ids, n_ep, d_z, w_o_parts)
    d_heads = lax.all_to_all(d_attn, "sp", split_axis=1, concat_axis=0, tiled=True)
    d_z_cols = lax.all_to_all(d_z, "sp", split_axis=1, concat_axis=0, tiled=True)
    out_grads = grad_pieces(ids, n_ep, attn_all, d_z_cols, "out_grads")

    mix_pieces = []
    for g, (_, _, made) in enumerate(groups):
        for at in range(group // 2):
            mix_pieces += combine(pair_places(g * group + 2 * at), made[4], 2, local, cap, at)
    if shard == tok_dev:
        sent = [jnp.concatenate(two, axis=1) for two in zip(mix_pieces, out_grads)]
        got = scatter_turn(sent, n_ep)
        mix, grad_out = got[:, :width], got[:, width:].astype(BF16)
    else:
        mix = scatter_turn(mix_pieces, n_ep)
        grad_out = scatter_turn(out_grads, n_ep).astype(BF16)
    output = (x_one + mix).astype(BF16)

    d_qn, d_kn, d_v, sums, grad_qg, grad_kg = attend_back(
        q_rot, k_rot, v_low, d_heads, q_raw, k_raw, scales, gain_q, gain_k, cosine, sine, starts
    )

    def placed(value):
        return lax.dynamic_update_slice_in_dim(
            jnp.zeros((1, width), F32), value, sp_index * head_width, 1
        )

    tiny = jnp.concatenate(
        [placed(grad_qg), placed(grad_kg), grad_ffn[None], grad_router], axis=0
    )
    *qkv_pieces, d_qkv = qkv_back(
        ids, n_ep, h_all, d_qn, d_kn, d_v, q_raw, k_raw, scales, sum_sp(sums), tiny
    )
    grad_qkv = scatter_line(qkv_pieces, n_ep).astype(BF16)

    d_h = d_h_rows(d_qkv, w_qk, w_v).reshape(n_sp, tok_dev, width)
    parts = [
        lax.dynamic_index_in_dim(d_h, partners[j], 0, keepdims=False) for j in range(4)
    ]
    kept = plus(parts[0], swap_sp(parts[1], 1))
    sent = plus(parts[2], swap_sp(parts[3], 1))
    d_h = kept.astype(F32) + swap_sp(sent, 2).astype(F32)
    x_normed = x_rows * x_scale
    d_normed = d_h * gains[0][None, :]
    input_grad = d_one + x_scale * (
        d_normed - x_normed * jnp.mean(d_normed * x_normed, axis=-1, keepdims=True)
    )

    g_query, g_key, g_value, tiny, g_attn = finish(
        ids, n_ep, w_query, w_key, w_value, attn_gain.astype(F32)[:, None], gather_sp(grad_qkv)
    )
    out_parts = gather_sp(grad_out)
    g_out = jnp.concatenate(
        [
            lax.dynamic_index_in_dim(jnp.stack(out_parts), partners[j], 0, keepdims=False)
            for j in range(4)
        ],
        axis=1,
    ).astype(F32)
    per_row = 3 * head_width // shard

    def vector(at):
        col = (at % per_row) * shard
        return tiny[at // per_row, col : col + shard]

    g_router = jnp.stack([vector(3 + i) for i in range(expert_count)], axis=1)
    return (
        output[None], input_grad[None], g_attn[:, 0], g_query, g_key, g_value, vector(0), vector(1),
        g_out, vector(2), g_router, grad_gate, grad_up, grad_down,
    )


def solution(mesh):
    seq = P("ep", "sp", None)
    vec = P("ep")
    mat = P("ep", None)
    expert = P("ep", None, None)
    in_specs = (
        seq, mat, seq, vec, mat, mat, mat, vec, vec, mat, vec, mat, expert, expert, expert, seq,
    )
    out_specs = (
        seq, seq, vec, mat, mat, mat, vec, vec, mat, vec, mat, seq, seq, seq,
    )
    return jax.shard_map(body, mesh=mesh, in_specs=in_specs, out_specs=out_specs, check_vma=False)
```

time: 2430 us -> 1270 us (0.52)
  waiting for transfers between devices: 1240 us -> 575 us
  matrix products: 362 us -> 4.19 us
  blocking collectives: 355 us -> 18.5 us
  Pallas kernels: 0 us -> 327 us
  local copies, waits for them, and re-layouts: 288 us -> 33.2 us
  starting transfers between devices: 49.4 us -> 185 us
    ppermute x0 -> x80, waiting for transfers between devices: none -> 567 us  [the longest x64 524 us: shift(): return lax.ppermute(value, 'ep', pairs)]
    all_to_all x10 -> x2, waiting for transfers between devices: 486 us -> 6.5 us  [the longest x1 6.5 us: body(): lax.all_to_all(d_gates, 'ep', split_axis=0, concat_axis=0, tiled=True)]
    reduce_scatter x8 -> x3, waiting for transfers between devices: 368 us -> 0.01 us  [over_sp(): lax.psum_scatter(value, 'sp', scatter_dimension=1, tiled=True).astype(F32)]
    dot_general x33 -> x2, matrix products: 338 us -> 1.63 us  [product(): return jnp.dot(left, right, preferred_element_type=F32)]
    pallas_call x0 -> x31, Pallas kernels: none -> 327 us  [call(): pl.pallas_call(kernel, grid_spec=pltpu.PrefetchScalarGridSpec(num_scalar_...]
    all_gather x4 -> x2, waiting for transfers between devices: 299 us -> 0.02 us  [the longest x1 0.02 us: body(): attn_all = lax.all_gather(attn_tok, 'sp', axis=0, tiled=True)]
    all_gather x5 -> x0, blocking collectives: 292 us -> none  [the longest x1 217 us: body(): lax.all_gather(w_router, 'ep', axis=0, tiled=True)]
    ppermute x0 -> x80, starting transfers between devices: none -> 174 us  [the longest x64 165 us: shift(): return lax.ppermute(value, 'ep', pairs)]
  transfers between devices with their start and end apart: 24 -> 88, of which waited for: 17 -> 39; matrix products, arithmetic and copies ran while one was open for 26% -> 8% of each run, Pallas kernels for 0% -> 25%
where the time goes in v1:
time: 1270 us; the launch traced here: 1260 us
  waiting for transfers between devices  575 us (45%)
  Pallas kernels  327 us (26%)
  starting transfers between devices  185 us (15%)
  other arithmetic  78.8 us (6%)
  between operations  38.6 us (3%)
  local copies, waits for them, and re-layouts  33.2 us (3%)
  blocking collectives  18.5 us (1%)
    ppermute x64, waiting for transfers between devices, shift(): return lax.ppermute(value, 'ep', pairs)  524 us
    pallas_call x31, Pallas kernels, call(): pl.pallas_call(kernel, grid_spec=pltpu.PrefetchScalarGridSpec(num_scalar_...  327 us
    ppermute x64, starting transfers between devices, shift(): return lax.ppermute(value, 'ep', pairs)  165 us
    ppermute x16, waiting for transfers between devices, swap_sp(): return lax.ppermute(value, 'sp', [(i, i ^ bits) for i in range(4)])  42.1 us
  transfers between devices with their start and end apart: 88, of which 39 were waited for; matrix products, arithmetic and copies ran while one was open for 8% of the time, Pallas kernels for 25%

profile of v1, /device:TPU:0, one launch (start us, length us, event | category | flops | bytes accessed | tf_op | source)
XLA Modules:
  0.0 1260.1 jit_solution(2467635472087006491)
XLA Ops:
  48.0 9.5 collective-permute-done.8.refs_2_
  63.2 9.7 collective-permute-done.12
  73.7 10.7 collective-permute-done.14
  87.3 11.2 collective-permute-done.13.refs_5_
  98.5 6.3 collective-permute-done.15.refs_7_
  104.8 15.4 %collective-permute-start.17 = (bf16[256,1024]{1,0:T(8,128)(2,1)S(1)}, bf16[256,1024]{1,0:T(8,128)(2,1)S(1)}, u32[]{:S(2)}, u32[]{:S(2)}) collective-permute-start(bf16[256,1024]{1,0:T(8,128)(2,1)S(1)} %pad_maximum_fusion.6.refs_0_), channel_id=1, source_target_pairs={{0,2},{1,3},{2,0},{3,1},{4,6},{5,7},{6,4},{7,5},{8,10},{9,11},{10,... | collective-permute-start | bytes 1572872 | tf_op jit(solution)/shard_map/ppermute | solution.py:82
  123.4 14.8 %collective-permute-done.17.refs_2_ = bf16[256,1024]{1,0:T(8,128)(2,1)S(1)} collective-permute-done((bf16[256,1024]{1,0:T(8,128)(2,1)S(1)}, bf16[256,1024]{1,0:T(8,128)(2,1)S(1)}, u32[]{:S(2)}, u32[]{:S(2)}) %collective-permute-start.17) | collective-permute-done | bytes 524320 | tf_op jit(solution)/shard_map/ppermute | solution.py:82
  138.8 19.7 %collective-permute-done.19.refs_4_ = bf16[256,1024]{1,0:T(8,128)(2,1)S(1)} collective-permute-done((bf16[256,1024]{1,0:T(8,128)(2,1)S(1)}, bf16[256,1024]{1,0:T(8,128)(2,1)S(1)}, u32[]{:S(2)}, u32[]{:S(2)}) %collective-permute-start.19) | collective-permute-done | bytes 524320 | tf_op jit(solution)/shard_map/ppermute | solution.py:82
  161.2 6.5 collective-permute-done.20.refs_5_
  167.7 5.6 collective-permute-done.22.refs_7_
  174.2 8.4 v_project.1
  184.5 33.2 %collective-permute-done.26.refs_2_ = bf16[2048,512]{1,0:T(8,128)(2,1)S(1)} collective-permute-done((bf16[2048,512]{1,0:T(8,128)(2,1)}, bf16[2048,512]{1,0:T(8,128)(2,1)S(1)}, u32[]{:S(2)}, u32[]{:S(2)}) %collective-permute-start.26) | collective-permute-done | bytes 2097184 | tf_op jit(solution)/shard_map/ppermute | solution.py:90
  219.7 15.1 %qk_project.1 = (f32[1024,512]{1,0:T(8,128)}, f32[1024,512]{1,0:T(8,128)}, f32[16,1024]{1,0:T(8,128)}, bf16[2048,1024]{1,0:T(8,128)(2,1)}) custom-call(s32[12]{0:T(128)} %pad_add_fusion.ids, bf16[1024,2048]{1,0:T(8,128)(2,1)} %all-gather.3.cloned.1.call-done.h_ref, bf16[256,1024]{1,0:T(8,128)(2,1)} %copy-done.48, bf16[256,1024]{1,0:T(8,128)(2,1)} %copy-done.75, ...), custom_call_target="tpu_custom_call" | custom-call | flops 4294967296 | bytes 16842752 | tf_op jit(solution)/shard_map/qk_project/pallas_call | solution.py:55
  242.7 17.2 %attend.1 = (bf16[1024,512]{1,0:T(8,128)(2,1)}, bf16[1024,512]{1,0:T(8,128)(2,1)}, bf16[1024,512]{1,0:T(8,128)(2,1)}) custom-call(f32[1024,512]{1,0:T(8,128)} %get-tuple-element.125.qr_ref, f32[1024,512]{1,0:T(8,128)} %get-tuple-element.126.kr_ref, bf16[1024,512]{1,0:T(8,128)(2,1)} %get-tuple-element.136.v_ref, f32[16,1024]{1,0:T(8,128)} %add_rsqrt_fusion.scale_ref, ...), custom_call_target="tpu_custom_call" | custom-call | flops 1610612736 | bytes 9510912 | tf_op jit(solution)/shard_map/attend/pallas_call | solution.py:55
  259.9 18.5 %all_to_all.62 = bf16[4,256,512]{2,1,0:T(8,128)(2,1)S(1)} all-to-all(bf16[4,256,512]{2,1,0:T(8,128)(2,1)} %bitcast.172), channel_id=1, replica_groups=mesh['sp'=4,'ep'=8] {'sp'}, dimensions={0} | all-to-all | bytes 2097152 | tf_op jit(solution)/shard_map/all_to_all | solution.py:801
  279.5 8.9 out_project.1
  288.4 14.9 %collective-permute-start.28 = (bf16[256,2048]{1,0:T(8,128)(2,1)}, bf16[256,2048]{1,0:T(8,128)(2,1)S(1)}, u32[]{:S(2)}, u32[]{:S(2)}) collective-permute-start(bf16[256,2048]{1,0:T(8,128)(2,1)} %get-tuple-element.141.refs_0_), channel_id=1, source_target_pairs={{0,2},{1,3},{2,0},{3,1},{4,6},{5,7},{6,4},{7,5},{8,10},{9,11},{10,... | collective-permute-start | bytes 3145736 | tf_op jit(solution)/shard_map/ppermute | solution.py:82
  304.1 22.3 %collective-permute-done.28.refs_0_ = bf16[256,2048]{1,0:T(8,128)(2,1)S(1)} collective-permute-done((bf16[256,2048]{1,0:T(8,128)(2,1)}, bf16[256,2048]{1,0:T(8,128)(2,1)S(1)}, u32[]{:S(2)}, u32[]{:S(2)}) %collective-permute-start.28) | collective-permute-done | bytes 1048608 | tf_op jit(solution)/shard_map/ppermute | solution.py:82
  335.1 86.6 %collective-permute-done.43.refs_0_ = bf16[256,2048]{1,0:T(8,128)(2,1)} collective-permute-done((bf16[256,2048]{1,0:T(8,128)(2,1)S(1)}, bf16[256,2048]{1,0:T(8,128)(2,1)}, u32[]{:S(2)}, u32[]{:S(2)}) %collective-permute-start.43) | collective-permute-done | bytes 1048608 | tf_op jit(solution)/shard_map/ppermute | solution.py:82
  427.4 15.6 %collective-permute-done.37 = bf16[256,2048]{1,0:T(8,128)(2,1)} collective-permute-done((bf16[256,2048]{1,0:T(8,128)(2,1)}, bf16[256,2048]{1,0:T(8,128)(2,1)}, u32[]{:S(2)}, u32[]{:S(2)}) %collective-permute-start.37) | collective-permute-done | bytes 1048608 | tf_op jit(solution)/shard_map/ppermute | solution.py:82
  457.1 13.6 %collective-permute-done.42.refs_1_ = bf16[256,2048]{1,0:T(8,128)(2,1)} collective-permute-done((bf16[256,2048]{1,0:T(8,128)(2,1)}, bf16[256,2048]{1,0:T(8,128)(2,1)}, u32[]{:S(2)}, u32[]{:S(2)}) %collective-permute-start.42) | collective-permute-done | bytes 1048608 | tf_op jit(solution)/shard_map/ppermute | solution.py:82
  474.5 18.7 %collective-permute-done.40.refs_1_ = bf16[256,2048]{1,0:T(8,128)(2,1)} collective-permute-done((bf16[256,2048]{1,0:T(8,128)(2,1)}, bf16[256,2048]{1,0:T(8,128)(2,1)}, u32[]{:S(2)}, u32[]{:S(2)}) %collective-permute-start.40) | collective-permute-done | bytes 1048608 | tf_op jit(solution)/shard_map/ppermute | solution.py:82
  497.6 14.8 %collective-permute-done.38.refs_1_ = bf16[256,2048]{1,0:T(8,128)(2,1)} collective-permute-done((bf16[256,2048]{1,0:T(8,128)(2,1)S(1)}, bf16[256,2048]{1,0:T(8,128)(2,1)}, u32[]{:S(2)}, u32[]{:S(2)}) %collective-permute-start.38) | collective-permute-done | bytes 1048608 | tf_op jit(solution)/shard_map/ppermute | solution.py:82
  516.8 42.5 %experts.3 = (bf16[2,576,1024]{2,1,0:T(8,128)(2,1)}, bf16[2,576,1024]{2,1,0:T(8,128)(2,1)}, bf16[2,576,1024]{2,1,0:T(8,128)(2,1)}, f32[2,576,1]{2,1,0:T(8,128)},...) custom-call(bf16[2,576,2048]{2,1,0:T(8,128)(2,1)} %get-tuple-element.155.x_ref.refs_1_, ...), custom_call_target="tpu_custom_call" | custom-call | flops 28991029248 | bytes 51127296 | tf_op jit(solution)/shard_map/experts/pallas_call | solution.py:55
  572.0 17.7 %collective-permute-done.46 = bf16[256,2048]{1,0:T(8,128)(2,1)S(1)} collective-permute-done((bf16[256,2048]{1,0:T(8,128)(2,1)}, bf16[256,2048]{1,0:T(8,128)(2,1)S(1)}, u32[]{:S(2)}, u32[]{:S(2)}) %collective-permute-start.46) | collective-permute-done | bytes 1048608 | tf_op jit(solution)/shard_map/ppermute | solution.py:82
  592.5 19.7 %collective-permute-done.33.refs_1_ = bf16[256,2048]{1,0:T(8,128)(2,1)} collective-permute-done((bf16[256,2048]{1,0:T(8,128)(2,1)S(1)}, bf16[256,2048]{1,0:T(8,128)(2,1)}, u32[]{:S(2)}, u32[]{:S(2)}) %collective-permute-start.33) | collective-permute-done | bytes 1048608 | tf_op jit(solution)/shard_map/ppermute | solution.py:82
  618.9 15.8 %collective-permute-done.32.refs_1_ = bf16[256,2048]{1,0:T(8,128)(2,1)} collective-permute-done((bf16[256,2048]{1,0:T(8,128)(2,1)}, bf16[256,2048]{1,0:T(8,128)(2,1)}, u32[]{:S(2)}, u32[]{:S(2)}) %collective-permute-start.32) | collective-permute-done | bytes 1048608 | tf_op jit(solution)/shard_map/ppermute | solution.py:82
  638.4 18.7 %collective-permute-done.30.refs_1_ = bf16[256,2048]{1,0:T(8,128)(2,1)} collective-permute-done((bf16[256,2048]{1,0:T(8,128)(2,1)}, bf16[256,2048]{1,0:T(8,128)(2,1)}, u32[]{:S(2)}, u32[]{:S(2)}) %collective-permute-start.30) | collective-permute-done | bytes 1048608 | tf_op jit(solution)/shard_map/ppermute | solution.py:82
  661.6 18.0 %collective-permute-done.29.refs_1_ = bf16[256,2048]{1,0:T(8,128)(2,1)} collective-permute-done((bf16[256,2048]{1,0:T(8,128)(2,1)S(1)}, bf16[256,2048]{1,0:T(8,128)(2,1)}, u32[]{:S(2)}, u32[]{:S(2)}) %collective-permute-start.29) | collective-permute-done | bytes 1048608 | tf_op jit(solution)/shard_map/ppermute | solution.py:82
  684.2 13.7 %collective-permute-done.45 = bf16[256,2048]{1,0:T(8,128)(2,1)} collective-permute-done((bf16[256,2048]{1,0:T(8,128)(2,1)}, bf16[256,2048]{1,0:T(8,128)(2,1)}, u32[]{:S(2)}, u32[]{:S(2)}) %collective-permute-start.45) | collective-permute-done | bytes 1048608 | tf_op jit(solution)/shard_map/ppermute | solution.py:82
  706.9 42.3 %experts.2 = (bf16[2,576,1024]{2,1,0:T(8,128)(2,1)}, bf16[2,576,1024]{2,1,0:T(8,128)(2,1)}, bf16[2,576,1024]{2,1,0:T(8,128)(2,1)}, f32[2,576,1]{2,1,0:T(8,128)},...) custom-call(bf16[2,576,2048]{2,1,0:T(8,128)(2,1)} %get-tuple-element.144.x_ref.refs_0_, ...), custom_call_target="tpu_custom_call" | custom-call | flops 28991029248 | bytes 51127296 | tf_op jit(solution)/shard_map/experts/pallas_call | solution.py:55
  762.6 18.0 %weight_grad.3 = bf16[2,1024,2048]{2,1,0:T(8,128)(2,1)} custom-call(bf16[2,576,1024]{2,1,0:T(8,128)(2,1)} %get-tuple-element.165.refs_0_, bf16[2,576,1024]{2,1,0:T(8,128)(2,1)} %get-tuple-element.166.refs_1_, bf16[2,576,2048]{2,1,0:T(8,128)(2,1)} %dispatch.11.d_ref.refs_2_, bf16[2,576,2048]{2,1,0:T(8,128)(2,1)} %dispatch.15.d_ref.refs_3_), custom_call_target="tpu_custom_call" | custom-call | flops 9663676416 | bytes 22544384 | tf_op jit(solution)/shard_map/weight_grad/pallas_call | solution.py:55
  786.2 18.3 %weight_grad.4 = bf16[2,2048,1024]{2,1,0:T(8,128)(2,1)} custom-call(bf16[2,576,2048]{2,1,0:T(8,128)(2,1)} %get-tuple-element.144.x_ref.refs_0_, bf16[2,576,2048]{2,1,0:T(8,128)(2,1)} %get-tuple-element.155.x_ref.refs_1_, bf16[2,576,1024]{2,1,0:T(8,128)(2,1)} %get-tuple-element.167.refs_2_, bf16[2,576,1024]{2,1,0:T(8,128)(2,1)} %get-tuple-element.168.refs_3_), custom_call_target="tpu_custom_call" | custom-call | flops 9663676416 | bytes 22544384 | tf_op jit(solution)/shard_map/weight_grad/pallas_call | solution.py:55
  804.5 18.3 %weight_grad.5 = bf16[2,2048,1024]{2,1,0:T(8,128)(2,1)} custom-call(bf16[2,576,2048]{2,1,0:T(8,128)(2,1)} %get-tuple-element.144.x_ref.refs_0_, bf16[2,576,2048]{2,1,0:T(8,128)(2,1)} %get-tuple-element.155.x_ref.refs_1_, bf16[2,576,1024]{2,1,0:T(8,128)(2,1)} %get-tuple-element.169.refs_2_, bf16[2,576,1024]{2,1,0:T(8,128)(2,1)} %get-tuple-element.170.refs_3_), custom_call_target="tpu_custom_call" | custom-call | flops 9663676416 | bytes 22544384 | tf_op jit(solution)/shard_map/weight_grad/pallas_call | solution.py:55
  836.3 6.5 all-to-all-done.1
  848.0 7.8 out_back.1
  892.3 23.2 %attend_back.1 = (f32[1024,512]{1,0:T(8,128)}, f32[1024,512]{1,0:T(8,128)}, bf16[1024,512]{1,0:T(8,128)(2,1)}, f32[16,1024]{1,0:T(8,128)}, f32[1,512]{1,0:T(1,128)}, /*index=5*/f32[1,512]{1,0:T(1,128)}) custom-call(bf16[1024,512]{1,0:T(8,128)(2,1)} %get-tuple-element.193.q_ref, bf16[1024,512]{1,0:T(8,128)(2,1)} %get-tuple-element.194.k_ref, ...), custom_call_target="tpu_custom_call" | custom-call | flops 3758096384 | bytes 14823424 | tf_op jit(solution)/shard_map/attend_back/pallas_call | solution.py:55
  923.3 16.7 %qkv_back.1 = (bf16[272,1536]{1,0:T(8,128)(2,1)}, bf16[272,1536]{1,0:T(8,128)(2,1)}, bf16[272,1536]{1,0:T(8,128)(2,1)}, bf16[272,1536]{1,0:T(8,128)(2,1)}, bf16[...) custom-call(s32[12]{0:T(128)} %pad_add_fusion.ids, ...), custom_call_target="tpu_custom_call" | custom-call | flops 6442450944 | bytes 23748608 | tf_op jit(solution)/shard_map/qkv_back/pallas_call | solution.py:55
  941.1 6.5 out_grads.1
  955.1 6.8 collective-permute-done.67
  965.9 11.6 d_h.1
  979.5 54.4 %collective-permute-done.66 = bf16[272,1536]{1,0:T(8,128)(2,1)} collective-permute-done((bf16[272,1536]{1,0:T(8,128)(2,1)}, bf16[272,1536]{1,0:T(8,128)(2,1)}, u32[]{:S(2)}, u32[]{:S(2)}) %collective-permute-start.66) | collective-permute-done | bytes 835616 | tf_op jit(solution)/shard_map/ppermute | solution.py:82
  1041.5 13.0 %collective-permute-done.71 = bf16[272,1536]{1,0:T(8,128)(2,1)S(1)} collective-permute-done((bf16[272,1536]{1,0:T(8,128)(2,1)S(1)}, bf16[272,1536]{1,0:T(8,128)(2,1)S(1)}, u32[]{:S(2)}, u32[]{:S(2)}) %collective-permute-start.71) | collective-permute-done | bytes 835616 | tf_op jit(solution)/shard_map/ppermute | solution.py:82
  1063.3 20.2 %collective-permute-done.70 = bf16[272,1536]{1,0:T(8,128)(2,1)S(1)} collective-permute-done((bf16[272,1536]{1,0:T(8,128)(2,1)S(1)}, bf16[272,1536]{1,0:T(8,128)(2,1)S(1)}, u32[]{:S(2)}, u32[]{:S(2)}) %collective-permute-start.70) | collective-permute-done | bytes 835616 | tf_op jit(solution)/shard_map/ppermute | solution.py:82
  1090.9 7.5 collective-permute-done.65
  1103.9 54.9 %collective-permute-start.55 = (bf16[256,2560]{1,0:T(8,128)(2,1)}, bf16[256,2560]{1,0:T(8,128)(2,1)}, u32[]{:S(2)}, u32[]{:S(2)}) collective-permute-start(bf16[256,2560]{1,0:T(8,128)(2,1)} %add_convert_fusion.2), channel_id=1, source_target_pairs={{0,2},{1,3},{2,0},{3,1},{4,6},{5,7},{6,4},{7,5},{8,10},{9,11},{10,... | collective-permute-start | bytes 3932168 | tf_op jit(solution)/shard_map/ppermute | solution.py:82
  1166.3 48.9 %collective-permute-done.57 = bf16[256,2560]{1,0:T(8,128)(2,1)} collective-permute-done((bf16[256,2560]{1,0:T(8,128)(2,1)}, bf16[256,2560]{1,0:T(8,128)(2,1)}, u32[]{:S(2)}, u32[]{:S(2)}) %collective-permute-start.57) | collective-permute-done | bytes 1310752 | tf_op jit(solution)/shard_map/ppermute | solution.py:82
  1229.7 7.0 finish.1
  (452 shorter events, 296.3 us)
Async XLA Ops:
  7.2 166.9 %all-gather.3.cloned.1.call-start = ((), (), s32[]{:S(2)}) async-start(), calls=%async_computation.7 | async-start | bytes 5242880 | tf_op jit(solution)/shard_map/all_gather | solution.py:763
  45.3 894.8 %all-gather.5.cloned.1.call-start = ((), (), s32[]{:S(2)}) async-start(), calls=%async_computation.8 | async-start | bytes 5242880 | tf_op jit(solution)/shard_map/all_gather | solution.py:803
  104.8 33.4 %collective-permute-start.17 = (bf16[256,1024]{1,0:T(8,128)(2,1)S(1)}, bf16[256,1024]{1,0:T(8,128)(2,1)S(1)}, u32[]{:S(2)}, u32[]{:S(2)}) collective-permute-start(bf16[256,1024]{1,0:T(8,128)(2,1)S(1)} %pad_maximum_fusion.6.refs_0_), channel_id=1, source_target_pairs={{0,2},{1,3},{2,0},{3,1},{4,6},{5,7},{6,4},{7,5},{8,10},{9,11},{10,... | collective-permute-start | bytes 1572872 | tf_op jit(solution)/shard_map/ppermute | solution.py:82
  120.3 38.2 %collective-permute-start.19 = (bf16[256,1024]{1,0:T(8,128)(2,1)S(1)}, bf16[256,1024]{1,0:T(8,128)(2,1)S(1)}, u32[]{:S(2)}, u32[]{:S(2)}) collective-permute-start(bf16[256,1024]{1,0:T(8,128)(2,1)S(1)} %pad_maximum_fusion.6.refs_0_), channel_id=1, source_target_pairs={{0,4},{1,5},{2,6},{3,7},{4,0},{5,1},{6,2},{7,3},{8,12},{9,13},{10,... | collective-permute-start | bytes 1572872 | tf_op jit(solution)/shard_map/ppermute | solution.py:82
  121.5 37.5 %collective-permute-start.21 = (bf16[256,1024]{1,0:T(8,128)(2,1)S(1)}, bf16[256,1024]{1,0:T(8,128)(2,1)S(1)}, u32[]{:S(2)}, u32[]{:S(2)}) collective-permute-start(bf16[256,1024]{1,0:T(8,128)(2,1)S(1)} %pad_maximum_fusion.6.refs_0_), channel_id=1, source_target_pairs={{0,6},{1,7},{2,4},{3,5},{4,2},{5,3},{6,0},{7,1},{8,14},{9,15},{10,... | collective-permute-start | bytes 1572872 | tf_op jit(solution)/shard_map/ppermute | solution.py:82
  122.9 38.2 %collective-permute-start.16 = (bf16[256,1024]{1,0:T(8,128)(2,1)S(1)}, bf16[256,1024]{1,0:T(8,128)(2,1)S(1)}, u32[]{:S(2)}, u32[]{:S(2)}) collective-permute-start(bf16[256,1024]{1,0:T(8,128)(2,1)S(1)} %pad_maximum_fusion.6.refs_0_), channel_id=1, source_target_pairs={{0,1},{1,0},{2,3},{3,2},{4,5},{5,4},{6,7},{7,6},{8,9},{9,8},{10,11... | collective-permute-start | bytes 1572872 | tf_op jit(solution)/shard_map/ppermute | solution.py:82
  182.6 35.2 %collective-permute-start.26 = (bf16[2048,512]{1,0:T(8,128)(2,1)}, bf16[2048,512]{1,0:T(8,128)(2,1)S(1)}, u32[]{:S(2)}, u32[]{:S(2)}) collective-permute-start(bf16[2048,512]{1,0:T(8,128)(2,1)} %get-tuple-element.139.refs_0_), channel_id=1, source_target_pairs={{0,16},{8,24},{16,0},{24,8},{1,17},{9,25},{17,1},{25,9},{2,18},{10... | collective-permute-start | bytes 6291464 | tf_op jit(solution)/shard_map/ppermute | solution.py:90
  184.4 95.1 %collective-permute-start.25 = (bf16[2048,512]{1,0:T(8,128)(2,1)}, bf16[2048,512]{1,0:T(8,128)(2,1)}, u32[]{:S(2)}, u32[]{:S(2)}) collective-permute-start(bf16[2048,512]{1,0:T(8,128)(2,1)} %get-tuple-element.139.refs_0_), channel_id=1, source_target_pairs={{0,8},{8,0},{16,24},{24,16},{1,9},{9,1},{17,25},{25,17},{2,10},{10... | collective-permute-start | bytes 6291464 | tf_op jit(solution)/shard_map/ppermute | solution.py:90
  217.7 61.8 %collective-permute-start.27 = (bf16[2048,512]{1,0:T(8,128)(2,1)S(1)}, bf16[2048,512]{1,0:T(8,128)(2,1)}, u32[]{:S(2)}, u32[]{:S(2)}) collective-permute-start(bf16[2048,512]{1,0:T(8,128)(2,1)S(1)} %collective-permute-done.26.refs_2_), channel_id=1, source_target_pairs={{0,8},{8,0},{16,24},{24,16},{1,9},{9,1},{17,25},{25,17},{2,10},{10... | collective-permute-start | bytes 6291464 | tf_op jit(solution)/shard_map/ppermute | solution.py:90
  288.4 38.0 %collective-permute-start.28 = (bf16[256,2048]{1,0:T(8,128)(2,1)}, bf16[256,2048]{1,0:T(8,128)(2,1)S(1)}, u32[]{:S(2)}, u32[]{:S(2)}) collective-permute-start(bf16[256,2048]{1,0:T(8,128)(2,1)} %get-tuple-element.141.refs_0_), channel_id=1, source_target_pairs={{0,2},{1,3},{2,0},{3,1},{4,6},{5,7},{6,4},{7,5},{8,10},{9,11},{10,... | collective-permute-start | bytes 3145736 | tf_op jit(solution)/shard_map/ppermute | solution.py:82
  328.0 93.8 %collective-permute-start.43 = (bf16[256,2048]{1,0:T(8,128)(2,1)S(1)}, bf16[256,2048]{1,0:T(8,128)(2,1)}, u32[]{:S(2)}, u32[]{:S(2)}) collective-permute-start(bf16[256,2048]{1,0:T(8,128)(2,1)S(1)} %bitcast.159), channel_id=1, source_target_pairs={{0,4},{1,5},{2,6},{3,7},{4,0},{5,1},{6,2},{7,3},{8,12},{9,13},{10,... | collective-permute-start | bytes 3145736 | tf_op jit(solution)/shard_map/ppermute | solution.py:82
  331.6 90.8 %collective-permute-start.41 = (bf16[256,2048]{1,0:T(8,128)(2,1)S(1)}, bf16[256,2048]{1,0:T(8,128)(2,1)}, u32[]{:S(2)}, u32[]{:S(2)}) collective-permute-start(bf16[256,2048]{1,0:T(8,128)(2,1)S(1)} %bitcast.160), channel_id=1, source_target_pairs={{0,6},{1,7},{2,4},{3,5},{4,2},{5,3},{6,0},{7,1},{8,14},{9,15},{10,... | collective-permute-start | bytes 3145736 | tf_op jit(solution)/shard_map/ppermute | solution.py:82
  332.5 91.4 %collective-permute-start.39 = (bf16[256,2048]{1,0:T(8,128)(2,1)S(1)}, bf16[256,2048]{1,0:T(8,128)(2,1)}, u32[]{:S(2)}, u32[]{:S(2)}) collective-permute-start(bf16[256,2048]{1,0:T(8,128)(2,1)S(1)} %collective-permute-done.35), channel_id=1, source_target_pairs={{2,0},{3,1},{4,6},{5,7},{10,8},{11,9},{12,14},{13,15},{18,16},{19,... | collective-permute-start | bytes 3145736 | tf_op jit(solution)/shard_map/ppermute | solution.py:82
  333.8 109.2 %collective-permute-start.37 = (bf16[256,2048]{1,0:T(8,128)(2,1)}, bf16[256,2048]{1,0:T(8,128)(2,1)}, u32[]{:S(2)}, u32[]{:S(2)}) collective-permute-start(bf16[256,2048]{1,0:T(8,128)(2,1)} %collective-permute-done.36), channel_id=1, source_target_pairs={{2,0},{3,1},{4,6},{5,7},{10,8},{11,9},{12,14},{13,15},{18,16},{19,... | collective-permute-start | bytes 3145736 | tf_op jit(solution)/shard_map/ppermute | solution.py:82
  421.8 31.5 %collective-permute-start.44 = (bf16[256,2048]{1,0:T(8,128)(2,1)}, bf16[256,2048]{1,0:T(8,128)(2,1)}, u32[]{:S(2)}, u32[]{:S(2)}) collective-permute-start(bf16[256,2048]{1,0:T(8,128)(2,1)} %collective-permute-done.43.refs_0_), channel_id=1, source_target_pairs={{0,1},{1,0},{2,3},{3,2},{4,5},{5,4},{6,7},{7,6},{8,9},{9,8},{10,11... | collective-permute-start | bytes 3145736 | tf_op jit(solution)/shard_map/ppermute | solution.py:82
  422.4 48.3 %collective-permute-start.42 = (bf16[256,2048]{1,0:T(8,128)(2,1)}, bf16[256,2048]{1,0:T(8,128)(2,1)}, u32[]{:S(2)}, u32[]{:S(2)}) collective-permute-start(bf16[256,2048]{1,0:T(8,128)(2,1)} %collective-permute-done.41.refs_0_), channel_id=1, source_target_pairs={{0,1},{1,0},{2,3},{3,2},{4,5},{5,4},{6,7},{7,6},{8,9},{9,8},{10,11... | collective-permute-start | bytes 3145736 | tf_op jit(solution)/shard_map/ppermute | solution.py:82
  426.8 66.3 %collective-permute-start.40 = (bf16[256,2048]{1,0:T(8,128)(2,1)}, bf16[256,2048]{1,0:T(8,128)(2,1)}, u32[]{:S(2)}, u32[]{:S(2)}) collective-permute-start(bf16[256,2048]{1,0:T(8,128)(2,1)} %add.233.refs_0_), channel_id=1, source_target_pairs={{0,1},{1,0},{2,3},{3,2},{4,5},{5,4},{6,7},{7,6},{8,9},{9,8},{10,11... | collective-permute-start | bytes 3145736 | tf_op jit(solution)/shard_map/ppermute | solution.py:82
  445.0 67.4 %collective-permute-start.38 = (bf16[256,2048]{1,0:T(8,128)(2,1)S(1)}, bf16[256,2048]{1,0:T(8,128)(2,1)}, u32[]{:S(2)}, u32[]{:S(2)}) collective-permute-start(bf16[256,2048]{1,0:T(8,128)(2,1)S(1)} %add.232.refs_0_), channel_id=1, source_target_pairs={{0,1},{1,0},{2,3},{3,2},{4,5},{5,4},{6,7},{7,6},{8,9},{9,8},{10,11... | collective-permute-start | bytes 3145736 | tf_op jit(solution)/shard_map/ppermute | solution.py:82
  447.7 117.6 %collective-permute-start.31 = (bf16[256,2048]{1,0:T(8,128)(2,1)S(1)}, bf16[256,2048]{1,0:T(8,128)(2,1)}, u32[]{:S(2)}, u32[]{:S(2)}) collective-permute-start(bf16[256,2048]{1,0:T(8,128)(2,1)S(1)} %bitcast.161), channel_id=1, source_target_pairs={{0,2},{1,3},{2,0},{3,1},{4,6},{5,7},{6,4},{7,5},{8,10},{9,11},{10,... | collective-permute-start | bytes 3145736 | tf_op jit(solution)/shard_map/ppermute | solution.py:82
  563.9 48.3 %collective-permute-start.33 = (bf16[256,2048]{1,0:T(8,128)(2,1)S(1)}, bf16[256,2048]{1,0:T(8,128)(2,1)}, u32[]{:S(2)}, u32[]{:S(2)}) collective-permute-start(bf16[256,2048]{1,0:T(8,128)(2,1)S(1)} %bitcast.162), channel_id=1, source_target_pairs={{0,1},{1,0},{2,3},{3,2},{4,5},{5,4},{6,7},{7,6},{8,9},{9,8},{10,11... | collective-permute-start | bytes 3145736 | tf_op jit(solution)/shard_map/ppermute | solution.py:82
  565.3 69.3 %collective-permute-start.32 = (bf16[256,2048]{1,0:T(8,128)(2,1)}, bf16[256,2048]{1,0:T(8,128)(2,1)}, u32[]{:S(2)}, u32[]{:S(2)}) collective-permute-start(bf16[256,2048]{1,0:T(8,128)(2,1)} %collective-permute-done.31.refs_0_), channel_id=1, source_target_pairs={{0,1},{1,0},{2,3},{3,2},{4,5},{5,4},{6,7},{7,6},{8,9},{9,8},{10,11... | collective-permute-start | bytes 3145736 | tf_op jit(solution)/shard_map/ppermute | solution.py:82
  565.9 91.2 %collective-permute-start.30 = (bf16[256,2048]{1,0:T(8,128)(2,1)}, bf16[256,2048]{1,0:T(8,128)(2,1)}, u32[]{:S(2)}, u32[]{:S(2)}) collective-permute-start(bf16[256,2048]{1,0:T(8,128)(2,1)} %get-tuple-element.141.refs_0_), channel_id=1, source_target_pairs={{0,1},{1,0},{2,3},{3,2},{4,5},{5,4},{6,7},{7,6},{8,9},{9,8},{10,11... | collective-permute-start | bytes 3145736 | tf_op jit(solution)/shard_map/ppermute | solution.py:82
  567.4 112.2 %collective-permute-start.29 = (bf16[256,2048]{1,0:T(8,128)(2,1)S(1)}, bf16[256,2048]{1,0:T(8,128)(2,1)}, u32[]{:S(2)}, u32[]{:S(2)}) collective-permute-start(bf16[256,2048]{1,0:T(8,128)(2,1)S(1)} %collective-permute-done.28.refs_0_), channel_id=1, source_target_pairs={{0,1},{1,0},{2,3},{3,2},{4,5},{5,4},{6,7},{7,6},{8,9},{9,8},{10,11... | collective-permute-start | bytes 3145736 | tf_op jit(solution)/shard_map/ppermute | solution.py:82
  589.6 108.3 %collective-permute-start.45 = (bf16[256,2048]{1,0:T(8,128)(2,1)}, bf16[256,2048]{1,0:T(8,128)(2,1)}, u32[]{:S(2)}, u32[]{:S(2)}) collective-permute-start(bf16[256,2048]{1,0:T(8,128)(2,1)} %get-tuple-element.160), channel_id=1, source_target_pairs={{0,1},{1,0},{2,3},{3,2},{4,5},{5,4},{6,7},{7,6},{8,9},{9,8},{10,11... | collective-permute-start | bytes 3145736 | tf_op jit(solution)/shard_map/ppermute | solution.py:82
  612.2 85.7 %collective-permute-start.47 = (bf16[256,2048]{1,0:T(8,128)(2,1)S(1)}, bf16[256,2048]{1,0:T(8,128)(2,1)S(1)}, u32[]{:S(2)}, u32[]{:S(2)}) collective-permute-start(bf16[256,2048]{1,0:T(8,128)(2,1)S(1)} %add_convert_fusion.8), channel_id=1, source_target_pairs={{0,2},{1,3},{6,4},{7,5},{8,10},{9,11},{14,12},{15,13},{16,18},{17,... | collective-permute-start | bytes 3145736 | tf_op jit(solution)/shard_map/ppermute | solution.py:82
  638.4 602.7 %reduce-scatter.4.cloned.1.call-start = ((), (), s32[]{:S(2)}) async-start(), calls=%async_computation.9 | async-start | bytes 10485760 | tf_op jit(solution)/shard_map/reduce_scatter | solution.py:851
  702.2 51.5 %collective-permute-start.50 = (bf16[256,2048]{1,0:T(8,128)(2,1)}, bf16[256,2048]{1,0:T(8,128)(2,1)}, u32[]{:S(2)}, u32[]{:S(2)}) collective-permute-start(bf16[256,2048]{1,0:T(8,128)(2,1)} %get-tuple-element.227), channel_id=1, source_target_pairs={{0,2},{1,3},{6,4},{7,5},{8,10},{9,11},{14,12},{15,13},{16,18},{17,... | collective-permute-start | bytes 3145736 | tf_op jit(solution)/shard_map/ppermute | solution.py:82
  761.1 61.7 %collective-permute-start.34 = (bf16[256,2048]{1,0:T(8,128)(2,1)}, bf16[256,2048]{1,0:T(8,128)(2,1)}, u32[]{:S(2)}, u32[]{:S(2)}) collective-permute-start(bf16[256,2048]{1,0:T(8,128)(2,1)} %get-tuple-element.152), channel_id=1, source_target_pairs={{0,1},{1,0},{2,3},{3,2},{4,5},{5,4},{6,7},{7,6},{8,9},{9,8},{10,11... | collective-permute-start | bytes 3145736 | tf_op jit(solution)/shard_map/ppermute | solution.py:82
  780.6 42.2 %collective-permute-start.48 = (bf16[256,2048]{1,0:T(8,128)(2,1)S(1)}, bf16[256,2048]{1,0:T(8,128)(2,1)}, u32[]{:S(2)}, u32[]{:S(2)}) collective-permute-start(bf16[256,2048]{1,0:T(8,128)(2,1)S(1)} %get-tuple-element.226), channel_id=1, source_target_pairs={{2,4},{3,5},{4,2},{5,3},{10,12},{11,13},{12,10},{13,11},{18,20},{1... | collective-permute-start | bytes 3145736 | tf_op jit(solution)/shard_map/ppermute | solution.py:82
  785.4 37.5 %collective-permute-start.52 = (bf16[256,2048]{1,0:T(8,128)(2,1)}, bf16[256,2048]{1,0:T(8,128)(2,1)S(1)}, u32[]{:S(2)}, u32[]{:S(2)}) collective-permute-start(bf16[256,2048]{1,0:T(8,128)(2,1)} %add_convert_fusion.4), channel_id=1, source_target_pairs={{0,2},{1,3},{2,0},{3,1},{4,6},{5,7},{6,4},{7,5},{8,10},{9,11},{10,... | collective-permute-start | bytes 3145736 | tf_op jit(solution)/shard_map/ppermute | solution.py:82
  826.4 418.8 %reduce-scatter.6.cloned.1.call-start = ((), (), s32[]{:S(2)}) async-start(), calls=%async_computation.10 | async-start | bytes 10485760 | tf_op jit(solution)/shard_map/reduce_scatter | solution.py:851
  827.0 422.2 %reduce-scatter.8.cloned.1.call-start = ((), (), s32[]{:S(2)}) async-start(), calls=%async_computation.11 | async-start | bytes 10485760 | tf_op jit(solution)/shard_map/reduce_scatter | solution.py:851
  858.2 30.6 %all-to-all-start.3 = ((bf16[256,4,512]{2,0,1:T(8,128)(2,1)}), bf16[256,4,512]{2,0,1:T(8,128)(2,1)}, u32[]{:S(2)}, u32[]{:S(2)}) async-start(bf16[256,4,512]{2,0,1:T(8,128)(2,1)} %bitcast.148), calls=%async_computation.3 | async-start | bytes 2097152 | tf_op jit(solution)/shard_map/all_to_all | solution.py:874
  888.7 51.3 %all-to-all-start.2 = ((bf16[256,4,512]{2,0,1:T(8,128)(2,1)}), bf16[256,4,512]{2,0,1:T(8,128)(2,1)S(1)}, u32[]{:S(2)}, u32[]{:S(2)}) async-start(bf16[256,4,512]{2,0,1:T(8,128)(2,1)} %bitcast.163), calls=%async_computation.2 | async-start | bytes 2097152 | tf_op jit(solution)/shard_map/all_to_all | solution.py:875
  949.8 106.7 %collective-permute-start.58 = (bf16[256,2560]{1,0:T(8,128)(2,1)}, bf16[256,2560]{1,0:T(8,128)(2,1)}, u32[]{:S(2)}, u32[]{:S(2)}) collective-permute-start(bf16[256,2560]{1,0:T(8,128)(2,1)} %pad_maximum_fusion.3), channel_id=1, source_target_pairs={{0,1},{1,0},{2,3},{3,2},{4,5},{5,4},{6,7},{7,6},{8,9},{9,8},{10,11... | collective-permute-start | bytes 3932168 | tf_op jit(solution)/shard_map/ppermute | solution.py:82
  953.1 107.0 %collective-permute-start.56 = (bf16[256,2560]{1,0:T(8,128)(2,1)}, bf16[256,2560]{1,0:T(8,128)(2,1)}, u32[]{:S(2)}, u32[]{:S(2)}) collective-permute-start(bf16[256,2560]{1,0:T(8,128)(2,1)} %pad_maximum_fusion.2), channel_id=1, source_target_pairs={{0,1},{1,0},{2,3},{3,2},{4,5},{5,4},{6,7},{7,6},{8,9},{9,8},{10,11... | collective-permute-start | bytes 3932168 | tf_op jit(solution)/shard_map/ppermute | solution.py:82
  953.1 80.8 %collective-permute-start.66 = (bf16[272,1536]{1,0:T(8,128)(2,1)}, bf16[272,1536]{1,0:T(8,128)(2,1)}, u32[]{:S(2)}, u32[]{:S(2)}) collective-permute-start(bf16[272,1536]{1,0:T(8,128)(2,1)} %get-tuple-element.207), channel_id=1, source_target_pairs={{0,1},{1,0},{2,3},{3,2},{4,5},{5,4},{6,7},{7,6},{8,9},{9,8},{10,11... | collective-permute-start | bytes 2506760 | tf_op jit(solution)/shard_map/ppermute | solution.py:82
  963.3 70.9 %collective-permute-start.68 = (bf16[272,1536]{1,0:T(8,128)(2,1)S(1)}, bf16[272,1536]{1,0:T(8,128)(2,1)}, u32[]{:S(2)}, u32[]{:S(2)}) collective-permute-start(bf16[272,1536]{1,0:T(8,128)(2,1)S(1)} %add_convert_fusion.16), channel_id=1, source_target_pairs={{0,2},{1,3},{6,4},{7,5},{8,10},{9,11},{14,12},{15,13},{16,18},{17,... | collective-permute-start | bytes 2506760 | tf_op jit(solution)/shard_map/ppermute | solution.py:82
  979.3 60.3 %collective-permute-start.63 = (bf16[256,2048]{1,0:T(8,128)(2,1)S(1)}, bf16[256,2048]{1,0:T(8,128)(2,1)S(1)}, u32[]{:S(2)}, u32[]{:S(2)}) collective-permute-start(bf16[256,2048]{1,0:T(8,128)(2,1)S(1)} %get-tuple-element.229), channel_id=1, source_target_pairs={{0,8},{8,0},{16,24},{24,16},{1,9},{9,1},{17,25},{25,17},{2,10},{10... | collective-permute-start | bytes 3145736 | tf_op jit(solution)/shard_map/ppermute | solution.py:90
  1033.9 53.2 %collective-permute-start.54 = (bf16[256,2560]{1,0:T(8,128)(2,1)S(1)}, bf16[256,2560]{1,0:T(8,128)(2,1)S(1)}, u32[]{:S(2)}, u32[]{:S(2)}) collective-permute-start(bf16[256,2560]{1,0:T(8,128)(2,1)S(1)} %pad_maximum_fusion.1), channel_id=1, source_target_pairs={{0,1},{1,0},{2,3},{3,2},{4,5},{5,4},{6,7},{7,6},{8,9},{9,8},{10,11... | collective-permute-start | bytes 3932168 | tf_op jit(solution)/shard_map/ppermute | solution.py:82
  1039.6 59.5 %collective-permute-start.62 = (bf16[256,2048]{1,0:T(8,128)(2,1)S(1)}, bf16[256,2048]{1,0:T(8,128)(2,1)}, u32[]{:S(2)}, u32[]{:S(2)}) collective-permute-start(bf16[256,2048]{1,0:T(8,128)(2,1)S(1)} %get-tuple-element.228), channel_id=1, source_target_pairs={{0,8},{8,0},{16,24},{24,16},{1,9},{9,1},{17,25},{25,17},{2,10},{10... | collective-permute-start | bytes 3145736 | tf_op jit(solution)/shard_map/ppermute | solution.py:90
  1060.2 38.2 %collective-permute-start.65 = (bf16[272,1536]{1,0:T(8,128)(2,1)S(1)}, bf16[272,1536]{1,0:T(8,128)(2,1)S(1)}, u32[]{:S(2)}, u32[]{:S(2)}) collective-permute-start(bf16[272,1536]{1,0:T(8,128)(2,1)S(1)} %copy-done.72), channel_id=1, source_target_pairs={{0,1},{1,0},{2,3},{3,2},{4,5},{5,4},{6,7},{7,6},{8,9},{9,8},{10,11... | collective-permute-start | bytes 2506760 | tf_op jit(solution)/shard_map/ppermute | solution.py:82
  1087.1 77.4 %collective-permute-start.73 = (bf16[272,1536]{1,0:T(8,128)(2,1)}, bf16[272,1536]{1,0:T(8,128)(2,1)}, u32[]{:S(2)}, u32[]{:S(2)}) collective-permute-start(bf16[272,1536]{1,0:T(8,128)(2,1)} %add_convert_fusion.12), channel_id=1, source_target_pairs={{0,2},{1,3},{2,0},{3,1},{4,6},{5,7},{6,4},{7,5},{8,10},{9,11},{10,... | collective-permute-start | bytes 2506760 | tf_op jit(solution)/shard_map/ppermute | solution.py:82
  1098.4 67.8 %collective-permute-start.53 = (bf16[256,2560]{1,0:T(8,128)(2,1)}, bf16[256,2560]{1,0:T(8,128)(2,1)}, u32[]{:S(2)}, u32[]{:S(2)}) collective-permute-start(bf16[256,2560]{1,0:T(8,128)(2,1)} %pad_maximum_fusion), channel_id=1, source_target_pairs={{0,1},{1,0},{2,3},{3,2},{4,5},{5,4},{6,7},{7,6},{8,9},{9,8},{10,11... | collective-permute-start | bytes 3932168 | tf_op jit(solution)/shard_map/ppermute | solution.py:82
  1099.1 67.2 %collective-permute-start.59 = (bf16[256,2560]{1,0:T(8,128)(2,1)}, bf16[256,2560]{1,0:T(8,128)(2,1)}, u32[]{:S(2)}, u32[]{:S(2)}) collective-permute-start(bf16[256,2560]{1,0:T(8,128)(2,1)} %add_convert_fusion), channel_id=1, source_target_pairs={{0,6},{1,7},{2,4},{3,5},{4,2},{5,3},{6,0},{7,1},{8,14},{9,15},{10,... | collective-permute-start | bytes 3932168 | tf_op jit(solution)/shard_map/ppermute | solution.py:82
  1102.8 112.4 %collective-permute-start.57 = (bf16[256,2560]{1,0:T(8,128)(2,1)}, bf16[256,2560]{1,0:T(8,128)(2,1)}, u32[]{:S(2)}, u32[]{:S(2)}) collective-permute-start(bf16[256,2560]{1,0:T(8,128)(2,1)} %add_convert_fusion.1), channel_id=1, source_target_pairs={{0,4},{1,5},{2,6},{3,7},{4,0},{5,1},{6,2},{7,3},{8,12},{9,13},{10,... | collective-permute-start | bytes 3932168 | tf_op jit(solution)/shard_map/ppermute | solution.py:82
  1103.9 111.3 %collective-permute-start.55 = (bf16[256,2560]{1,0:T(8,128)(2,1)}, bf16[256,2560]{1,0:T(8,128)(2,1)}, u32[]{:S(2)}, u32[]{:S(2)}) collective-permute-start(bf16[256,2560]{1,0:T(8,128)(2,1)} %add_convert_fusion.2), channel_id=1, source_target_pairs={{0,2},{1,3},{2,0},{3,1},{4,6},{5,7},{6,4},{7,5},{8,10},{9,11},{10,... | collective-permute-start | bytes 3932168 | tf_op jit(solution)/shard_map/ppermute | solution.py:82
  1166.2 59.4 %collective-permute-start.75 = (bf16[272,1536]{1,0:T(8,128)(2,1)S(1)}, bf16[272,1536]{1,0:T(8,128)(2,1)S(1)}, u32[]{:S(2)}, u32[]{:S(2)}) collective-permute-start(bf16[272,1536]{1,0:T(8,128)(2,1)S(1)} %add_convert_fusion.11.refs_0_), channel_id=1, source_target_pairs={{0,16},{8,24},{16,0},{24,8},{1,17},{9,25},{17,1},{25,9},{2,18},{10... | collective-permute-start | bytes 2506760 | tf_op jit(solution)/shard_map/ppermute | solution.py:90
  (120 other events, 2753.0 us)
Sparse Core Ops, SparseCore 0:
  45.4 34.7 all-gather.2
  638.5 31.5 all-gather.4
  826.5 90.8 reduce-scatter.3
  920.0 72.6 reduce-scatter.5
  995.1 71.7 reduce-scatter.7

commit v2 on v1

--- a/solution.py
+++ b/solution.py
@@ -14,6 +14,7 @@
 F32 = jnp.float32
 BF16 = jnp.bfloat16
 MIB = 1 << 20
+COVER = 20
 
 
 def product(left, right):
@@ -29,15 +30,12 @@
 
 
 def row_sums(values_in):
-    ones = jnp.ones((8, values_in.shape[1]), F32)
-    return lax.dot_general(
-        ones, values_in, (((1,), (1,)), ((), ())),
-        preferred_element_type=F32, precision=lax.Precision.HIGHEST,
-    )
+    sums = jnp.sum(values_in, axis=1, keepdims=True)
+    return jnp.transpose(jnp.broadcast_to(sums, (sums.shape[0], HEAD_DIM)))[:8]
 
 
 def call(kernel, out_shape, args, flops, name, scratch=(), scalars=(), grid=(1,), in_specs=None,
-         out_specs=None, aliases=None, vmem=60):
+         out_specs=None, aliases=None, vmem=60, after=()):
     single = not isinstance(out_shape, (list, tuple))
     shapes = [out_shape] if single else list(out_shape)
     count = len(grid)
@@ -50,7 +48,16 @@
     out_specs = out_specs or [None] * len(shapes)
     in_specs = [s if s is not None else fixed(a.shape) for s, a in zip(in_specs, args)]
     out_specs = [s if s is not None else fixed(o.shape) for s, o in zip(out_specs, shapes)]
-    moved = sum(a.size * a.dtype.itemsize for a in args)
+    waited = len(after)
+    args = [*args, *after]
+    in_specs = in_specs + [pl.BlockSpec(memory_space=pl.ANY)] * waited
+    if waited:
+        inner, first = kernel, len(scalars) + len(args) - waited
+
+        def kernel(*refs):
+            inner(*refs[:first], *refs[first + waited :])
+
+    moved = sum(a.size * a.dtype.itemsize for a in args[: len(args) - waited])
     moved += sum(o.size * o.dtype.itemsize for o in shapes)
     result = pl.pallas_call(
         kernel,
@@ -63,7 +70,7 @@
         compiler_params=pltpu.CompilerParams(
             vmem_limit_bytes=vmem * MIB, dimension_semantics=("arbitrary",) * count
         ),
-        cost_estimate=pl.CostEstimate(flops=int(flops), bytes_accessed=int(moved), transcendentals=0),
+        cost_estimate=pl.CostEstimate(flops=int(COVER * flops), bytes_accessed=int(moved), transcendentals=0),
         name=name,
     )(*scalars, *args)
     return result[0] if single else result
@@ -78,6 +85,10 @@
 INWARD = [(0, 2), (1, 3), (6, 4), (7, 5)]
 
 
+def tie(*values):
+    return lax.optimization_barrier(values)
+
+
 def shift(value, pairs):
     return lax.ppermute(value, "ep", pairs)
 
@@ -95,7 +106,7 @@
     return jnp.bitwise_xor(ids, ep_index) if n_ep == 8 else ids
 
 
-def gather_line(value, n_ep):
+def gather_line(value, n_ep, gate=()):
     if n_ep != 8:
         return gather_turn(value, n_ep)
     near = swap(value, 2)
@@ -103,8 +114,11 @@
     inner_b = shift(near, MIDDLE)
     third = inner_b + shift(inner_a, OUTWARD)
     fourth = inner_a + shift(inner_b, OUTWARD)
-    pieces = []
-    for own in (value, near, third, fourth):
+    crossed = value
+    if gate:
+        crossed = tie(value, *gate)[0]
+    pieces = [value, swap(crossed, 1)]
+    for own in (near, third, fourth):
         pieces += [own, swap(own, 1)]
     return pieces
 
@@ -123,25 +137,30 @@
     return (left.astype(F32) + right.astype(F32)).astype(left.dtype)
 
 
-def scatter_line(pieces, n_ep):
-    if n_ep != 8:
-        return scatter_turn(pieces, n_ep)
-    own, near, third, fourth = (plus(pieces[2 * i], swap(pieces[2 * i + 1], 1)) for i in range(4))
+def crossed_sums(pieces):
+    return [plus(pieces[i], swap(pieces[i + 1], 1)) for i in range(0, len(pieces), 2)]
+
+
+def scatter_line(own, near, third, fourth):
     third_in, fourth_in = shift(fourth, INWARD), shift(third, INWARD)
     third, fourth = plus(third, third_in), plus(fourth, fourth_in)
     near = plus(near, shift(third, MIDDLE))
-    return own.astype(F32) + shift(fourth, MIDDLE).astype(F32) + swap(near, 2).astype(F32)
+    total = own.astype(F32) + shift(fourth, MIDDLE).astype(F32) + swap(near, 2).astype(F32)
+    return total, [third, fourth]
+
+
+def turned_sum(sums):
+    total = sums[0].astype(F32)
+    for i in range(1, 4):
+        total = total + swap(sums[i], 2 * i).astype(F32)
+    return total
 
 
 def scatter_turn(pieces, n_ep):
     if n_ep != 8:
         stacked = jnp.stack(pieces)
         return lax.psum_scatter(stacked, "ep", scatter_dimension=0, tiled=False).astype(F32)
-    sums = [plus(pieces[2 * i], swap(pieces[2 * i + 1], 1)) for i in range(4)]
-    total = sums[0].astype(F32)
-    for i in range(1, 4):
-        total = total + swap(sums[i], 2 * i).astype(F32)
-    return total
+    return turned_sum(crossed_sums(pieces))
 
 
 def gather_sp(value):
@@ -210,7 +229,7 @@
     v_ref[...] = product(h_ref[...], w_ref[...]).astype(BF16)
 
 
-def v_project(ids, h_all, pieces):
+def v_project(ids, h_all, pieces, after):
     total, depth = h_all.shape
     width = pieces[0].shape[1] // 2
     rows = min(256, total)
@@ -220,6 +239,7 @@
         [h_all, *pieces],
         2 * total * depth * width,
         "v_project",
+        after=after,
         scalars=(ids,),
         grid=(total // rows,),
         in_specs=[pl.BlockSpec((rows, depth), lambda i, ids: (i, 0))] + [None] * len(pieces),
@@ -238,13 +258,14 @@
     low_ref[...] = (one * scale * gain_ref[...]).astype(BF16)
 
 
-def out_project(ids, n_ep, attn_tok, tokens, gain, weights):
+def out_project(ids, n_ep, attn_tok, tokens, gain, weights, after):
     return call(
         functools.partial(out_kernel, n_ep),
         [like(tokens.shape, F32), like(tokens.shape, BF16)],
         [attn_tok, tokens, gain, *weights],
         2 * tokens.size * attn_tok.shape[1],
         "out_project",
+        after=after,
         scalars=(ids,),
     )
 
@@ -259,43 +280,46 @@
     d_attn_ref[...] = total.astype(BF16)
 
 
-def out_back(ids, n_ep, d_z, weights):
+def out_back(ids, n_ep, d_z, weights, after):
     return call(
         functools.partial(out_back_kernel, n_ep),
         like((d_z.shape[0], weights[0].shape[0]), BF16),
         [d_z, *weights],
         2 * d_z.size * weights[0].shape[0],
         "out_back",
+        after=after,
         scalars=(ids,),
     )
 
 
-def grad_pieces_kernel(count, ids, left_ref, right_ref, *pieces):
+def vo_grads_kernel(count, ids, h_ref, dv_ref, attn_ref, dz_ref, *pieces):
     shard = pieces[0].shape[0]
+    width = dv_ref.shape[1]
     for k in range(count):
-        pieces[k][...] = product_left(
-            left_ref[:, block_at(ids, k, shard)], right_ref[...]
-        ).astype(BF16)
-
-
-def grad_pieces(ids, count, left, right, name):
-    shard = left.shape[1] // count
-    return call(
-        functools.partial(grad_pieces_kernel, count),
-        [like((shard, right.shape[1]), BF16)] * count,
-        [left, right],
-        2 * left.size * right.shape[1],
-        name,
+        block = block_at(ids, k, shard)
+        pieces[k][:, :width] = product_left(h_ref[:, block], dv_ref[...]).astype(BF16)
+        pieces[k][:, width:] = product_left(attn_ref[:, block], dz_ref[...]).astype(BF16)
+
+
+def vo_grads(ids, count, h_all, d_v, attn_all, d_z_cols):
+    shard = h_all.shape[1] // count
+    width = d_v.shape[1]
+    return call(
+        functools.partial(vo_grads_kernel, count),
+        [like((shard, 2 * width), BF16)] * count,
+        [h_all, d_v, attn_all, d_z_cols],
+        4 * h_all.size * width,
+        "vo_grads",
         scalars=(ids,),
     )
 
 
-def qkv_back_kernel(
-    count, width_all, ids, h_ref, dqn_ref, dkn_ref, dv_ref, qr_ref, kr_ref, scale_ref, sums_ref,
+def qk_back_kernel(
+    count, width_all, ids, h_ref, dqn_ref, dkn_ref, qr_ref, kr_ref, scale_ref, sums_ref,
     tiny_ref, *refs
 ):
     pieces, d_ref = refs[:count], refs[count]
-    width = dv_ref.shape[1]
+    width = dqn_ref.shape[1]
     scales = jnp.transpose(scale_ref[...])
     means = jnp.transpose(sums_ref[...]) * (1.0 / width_all)
     for at, (d_normed, raw) in enumerate(((dqn_ref, qr_ref), (dkn_ref, kr_ref))):
@@ -303,9 +327,8 @@
         d_ref[:, at * width : (at + 1) * width] = (
             scale * (d_normed[...] - raw[...] * scale * mean)
         ).astype(BF16)
-    d_ref[:, 2 * width :] = dv_ref[...]
     shard = h_ref.shape[1] // count
-    per_row = 3 * width // shard
+    per_row = 2 * width // shard
     for k in range(count):
         block = block_at(ids, k, shard)
         pieces[k][:shard, :] = product_left(h_ref[:, block], d_ref[...]).astype(BF16)
@@ -315,69 +338,75 @@
             pieces[k][row : row + 1, col : col + shard] = tiny_ref[at : at + 1, block].astype(BF16)
 
 
-def qkv_back(ids, count, h_all, d_qn, d_kn, d_v, q_raw, k_raw, scales, sums, tiny):
+def qk_back(ids, count, h_all, d_qn, d_kn, q_raw, k_raw, scales, sums, tiny, after):
     total, depth = h_all.shape
-    width = d_v.shape[1]
+    width = d_qn.shape[1]
     shard = depth // count
-    extra = -(-tiny.shape[0] // (3 * width // shard))
+    extra = -(-tiny.shape[0] // (2 * width // shard))
     extra = -(-extra // 16) * 16
     return call(
-        functools.partial(qkv_back_kernel, count, depth),
-        [like((shard + extra, 3 * width), BF16)] * count + [like((total, 3 * width), BF16)],
-        [h_all, d_qn, d_kn, d_v, q_raw, k_raw, scales, sums, tiny],
-        2 * h_all.size * 3 * width,
-        "qkv_back",
+        functools.partial(qk_back_kernel, count, depth),
+        [like((shard + extra, 2 * width), BF16)] * count + [like((total, 2 * width), BF16)],
+        [h_all, d_qn, d_kn, q_raw, k_raw, scales, sums, tiny],
+        2 * h_all.size * 2 * width,
+        "qk_back",
         scalars=(ids,),
-    )
-
-
-def d_h_kernel(d_ref, qk_ref, v_ref, out_ref):
-    both = qk_ref.shape[1]
+        after=after,
+    )
+
+
+def d_h_kernel(d_ref, dv_ref, qk_ref, v_ref, out_ref):
     out_ref[...] = (
-        product_right(d_ref[:, :both], qk_ref[...]) + product_right(d_ref[:, both:], v_ref[...])
+        product_right(d_ref[...], qk_ref[...]) + product_right(dv_ref[...], v_ref[...])
     ).astype(BF16)
 
 
-def d_h_rows(d_qkv, w_qk, w_v):
-    total, wide = d_qkv.shape
+def d_h_rows(d_qk, d_v, w_qk, w_v):
+    total, wide = d_qk.shape
     depth = w_qk.shape[0]
     rows = min(256, total)
     return call(
         d_h_kernel,
         like((total, depth), BF16),
-        [d_qkv, w_qk, w_v],
-        2 * d_qkv.size * depth,
+        [d_qk, d_v, w_qk, w_v],
+        3 * d_qk.size * depth,
         "d_h",
         grid=(total // rows,),
-        in_specs=[pl.BlockSpec((rows, wide), lambda i: (i, 0)), None, None],
+        in_specs=[
+            pl.BlockSpec((rows, wide), lambda i: (i, 0)),
+            pl.BlockSpec((rows, d_v.shape[1]), lambda i: (i, 0)), None, None,
+        ],
         out_specs=[pl.BlockSpec((rows, depth), lambda i: (i, 0))],
     )
 
 
-def finish_kernel(n_ep, ids, wq_ref, wk_ref, wv_ref, gain_ref, *refs):
-    parts, (gq_ref, gk_ref, gv_ref, tiny_ref, attn_ref) = refs[:-5], refs[-5:]
+def finish_kernel(n_ep, n_sp, ids, wq_ref, wk_ref, wv_ref, gain_ref, *refs):
+    firsts, seconds = refs[:n_sp], refs[n_sp : 2 * n_sp]
+    gq_ref, gk_ref, gv_ref, go_ref, tiny_ref, attn_ref = refs[2 * n_sp :]
     shard = wq_ref.shape[0]
-    width = parts[0].shape[1] // 3
+    width = firsts[0].shape[1] // 2
     dots = jnp.zeros((shard, 1), F32)
     tiny = jnp.zeros(tiny_ref.shape, F32)
-    for j, part in enumerate(parts):
+    for j in range(n_sp):
         cols = block_at(ids, n_ep + j, width)
-        for at, (grad, weight) in enumerate(((gq_ref, wq_ref), (gk_ref, wk_ref), (gv_ref, wv_ref))):
-            value = part[:shard, at * width : (at + 1) * width].astype(F32)
+        for at, grad, weight in ((0, gq_ref, wq_ref), (1, gk_ref, wk_ref), (2, gv_ref, wv_ref)):
+            part = firsts[j][:shard, at * width : (at + 1) * width] if at < 2 else seconds[j][:, :width]
+            value = part.astype(F32)
             grad[:, cols] = value
             dots += jnp.sum(value * weight[:, cols].astype(F32), axis=1, keepdims=True)
-        tiny += part[shard:, :].astype(F32)
+        go_ref[:, cols] = seconds[j][:, width:].astype(F32)
+        tiny += firsts[j][shard:, :].astype(F32)
     tiny_ref[...] = tiny
     attn_ref[...] = dots / gain_ref[...]
 
 
-def finish(ids, n_ep, w_query, w_key, w_value, gain, parts):
+def finish(ids, n_ep, w_query, w_key, w_value, gain, firsts, seconds):
     shard, depth = w_query.shape
-    extra = parts[0].shape[0] - shard
-    return call(
-        functools.partial(finish_kernel, n_ep),
-        [like((shard, depth), F32)] * 3 + [like((extra, parts[0].shape[1]), F32), like((shard, 1), F32)],
-        [w_query, w_key, w_value, gain, *parts],
+    extra = firsts[0].shape[0] - shard
+    return call(
+        functools.partial(finish_kernel, n_ep, len(firsts)),
+        [like((shard, depth), F32)] * 4 + [like((extra, firsts[0].shape[1]), F32), like((shard, 1), F32)],
+        [w_query, w_key, w_value, gain, *firsts, *seconds],
         shard * depth * 6,
         "finish",
         scalars=(ids,),
@@ -530,7 +559,7 @@
                 )
 
 
-def dispatch(mine, pieces, places, picked, router, local, cap, group, at, rows, gates):
+def dispatch(mine, pieces, places, picked, router, local, cap, group, at, rows, gates, after=()):
     gated = router is not None
     here = len(pieces)
     width = pieces[0].shape[1]
@@ -562,6 +591,7 @@
         in_specs=in_specs,
         out_specs=out_specs,
         aliases=aliases,
+        after=after,
     )
 
 
@@ -608,7 +638,7 @@
         back_ref[0] = (back_acc[...] + back).astype(BF16)
 
 
-def experts(rows, d_rows, gates, w_gate, w_up, w_down):
+def experts(rows, d_rows, gates, w_gate, w_up, w_down, after=()):
     local, count, width = rows.shape
     hidden = w_gate.shape[2]
     part = hidden // 2
@@ -625,6 +655,7 @@
         [rows, d_rows, gates, w_gate, w_up, w_down],
         12 * rows.size * hidden,
         "experts",
+        after=after,
         scratch=[pltpu.VMEM((count, width), F32)] * 2,
         grid=(local, 2),
         in_specs=[wide, wide, column, into, into, outof],
@@ -648,7 +679,7 @@
         pieces[p][...] = total.astype(BF16)
 
 
-def combine(places, rows, here, local, cap, at, dots=None):
+def combine(places, rows, here, local, cap, at, dots=None, after=()):
     width = rows.shape[2]
     tokens = places.shape[1]
     dotted = dots is not None
@@ -665,6 +696,7 @@
         args,
         2 * here * local * cap * tokens * width,
         "combine",
+        after=after,
         in_specs=in_specs,
     )
 
@@ -678,7 +710,7 @@
     refs[-1][0] = total.astype(BF16)
 
 
-def weight_grad(lefts, rights):
+def weight_grad(lefts, rights, after=()):
     local, count, tall = lefts[0].shape
     wide = rights[0].shape[2]
     part = min(512, tall)
@@ -690,14 +722,11 @@
         [*lefts, *rights],
         2 * len(lefts) * lefts[0].size * wide,
         "weight_grad",
+        after=after,
         grid=(local, tall // part),
         in_specs=[left] * len(lefts) + [right] * len(lefts),
         out_specs=[pl.BlockSpec((1, part, wide), lambda e, i: (e, i, 0))],
     )
-
-
-def tie(*values):
-    return lax.optimization_barrier(values)
 
 
 def body(
@@ -732,7 +761,7 @@
             [lax.dynamic_index_in_dim(value, order[i], 0, keepdims=False) for i in range(n_ep)]
         )
 
-    qk_pieces = gather_line(
+    qk_pieces = gather_turn(
         jnp.concatenate([own_columns(w_query), own_columns(w_key)], axis=1), n_ep
     )
 
@@ -785,72 +814,102 @@
     starts = starts[:, None].astype(jnp.int32)
 
     vo_own = jnp.concatenate([own_columns(w_value), own_columns(w_out)], axis=1)
-    *qk_pieces, vo_own = tie(*qk_pieces, vo_own)
+    qk_pieces[-1], vo_own = tie(qk_pieces[-1], vo_own)
     vo_pieces = gather_turn(vo_own, n_ep)
-    *vo_pieces, cot_own = tie(*vo_pieces, cotangent[0])
+    vo_pieces[-1], cot_own = tie(vo_pieces[-1], cotangent[0])
     cot_pieces = gather_turn(cot_own, n_ep)
 
     q_raw, k_raw, squares, w_qk = qk_project(ids, h_all, qk_pieces)
     scales = lax.rsqrt(sum_sp(squares) / width + EPS)
-    v_low, w_v, w_o = v_project(ids, h_all, vo_pieces)
+    v_low, w_v, w_o = v_project(ids, h_all, vo_pieces, [q_raw])
     w_o_parts = gather_sp(w_o)
     gain_q, gain_k = own_columns(gains)[1:2], own_columns(gains)[2:3]
     q_rot, k_rot, mixed = attend(
         q_raw, k_raw, v_low, scales, gain_q, gain_k, cosine, sine, starts
     )
-    attn_tok = lax.all_to_all(mixed, "sp", split_axis=0, concat_axis=1, tiled=True)
-    x_one, h2_low = out_project(ids, n_ep, attn_tok, tokens[0], gains[3:4], w_o_parts)
-    attn_all = lax.all_gather(attn_tok, "sp", axis=0, tiled=True)
 
     def pair_places(p):
         return places[p * local : (p + 2) * local]
 
-    h2_pieces = gather_line(h2_low, n_ep)
-    groups = []
-    home_gates = None
-    for g in range(0, n_ep, group):
-        rows = gates = d_rows = None
+    def cot_rows(g, after):
+        d_rows = None
         for at, p in enumerate(range(g, g + group, 2)):
             (d_rows,) = dispatch(
                 mine, cot_pieces[p : p + 2], pair_places(p), None, None, local, cap, group, at,
-                d_rows, None,
+                d_rows, None, after,
             )
+        return d_rows
+
+    attn_tok = lax.all_to_all(mixed, "sp", split_axis=0, concat_axis=1, tiled=True)
+    near_rows = cot_rows(0, [mixed])
+    x_one, h2_low = out_project(
+        ids, n_ep, attn_tok, tokens[0], gains[3:4], w_o_parts, [near_rows]
+    )
+    attn_all = lax.all_gather(attn_tok, "sp", axis=0, tiled=True)
+
+    h2_pieces = gather_line(h2_low, n_ep, cot_pieces[-1:])
+    cots = [near_rows] + [cot_rows(g, [x_one]) for g in range(group, n_ep, group)]
+    groups, d_pieces, d_gates, d_sums = [], [], [], []
+    home_gates = None
+
+    def rows_of(g, after):
+        rows = gates = first_gates = None
         for at, p in enumerate(range(g, g + group, 2)):
             rows, gates, piece_gates = dispatch(
                 mine, h2_pieces[p : p + 2], pair_places(p),
                 picked_flat[p * expert_count : (p + 2) * expert_count], full_router, local, cap,
-                group, at, rows, gates,
+                group, at, rows, gates, after,
             )
-            if p == 0:
-                home_gates = piece_gates
-        groups.append((rows, d_rows, experts(rows, d_rows, gates, w_gate, w_up, w_down)))
-
-    d_pieces, d_gates = [], []
-    for g, (_, _, made) in enumerate(groups):
+            first_gates = piece_gates if first_gates is None else first_gates
+        return rows, gates, first_gates
+
+    rows, gates, home_gates = rows_of(0, [])
+    for g in range(0, n_ep, group):
+        d_rows = cots[g // group]
+        made = experts(rows, d_rows, gates, w_gate, w_up, w_down, d_pieces[-group:] + cots)
+        groups.append((rows, d_rows, made))
+        following = []
+        if g + group < n_ep:
+            rows, gates, _ = rows_of(g + group, [made[5]])
+            following = [rows]
+        sums_before = list(d_sums)
         for at in range(group // 2):
-            p = g * group + 2 * at
-            *two, dots = combine(pair_places(p), made[5], 2, local, cap, at, made[3])
+            *two, dots = combine(
+                pair_places(g + 2 * at), made[5], 2, local, cap, at, made[3],
+                sums_before + following,
+            )
             d_pieces += two
             d_gates.append(dots)
-    d_h2 = scatter_line(d_pieces, n_ep)
-    d_gates = by_block(jnp.concatenate(d_gates, axis=0).reshape(n_ep, local, tok_dev))
-    d_gates = lax.all_to_all(d_gates, "ep", split_axis=0, concat_axis=0, tiled=True)
-    d_gates = d_gates.reshape(expert_count, tok_dev)
+        if n_ep == 8:
+            d_sums += crossed_sums(d_pieces[-group:])
 
     acts = [made[0] for _, _, made in groups]
     d_gate_rows = [made[1] for _, _, made in groups]
     d_up_rows = [made[2] for _, _, made in groups]
     ins = [rows for rows, _, _ in groups]
     outs = [d_rows for _, d_rows, _ in groups]
+    if n_ep == 8:
+        d_h2, inside = scatter_line(*d_sums)
+    else:
+        d_h2, inside = scatter_turn(d_pieces, n_ep), []
     grad_down = weight_grad(acts, outs)
     grad_gate = weight_grad(ins, d_gate_rows)
-    grad_up = weight_grad(ins, d_up_rows)
-    d_h2, grad_down, grad_gate, grad_up = tie(d_h2, grad_down, grad_gate, grad_up)
+    grad_up = weight_grad(ins, d_up_rows, [*d_sums, grad_down, grad_gate])
 
     def over_sp(value):
         return lax.psum_scatter(value, "sp", scatter_dimension=1, tiled=True).astype(F32)
 
-    grad_down, grad_gate, grad_up = over_sp(grad_down), over_sp(grad_gate), over_sp(grad_up)
+    d_gates = by_block(jnp.concatenate(d_gates, axis=0).reshape(n_ep, local, tok_dev))
+    d_gates = lax.all_to_all(d_gates, "ep", split_axis=0, concat_axis=0, tiled=True)
+    d_gates = d_gates.reshape(expert_count, tok_dev)
+
+    mix_pieces = []
+    for g, (_, _, made) in enumerate(groups):
+        for at in range(group // 2):
+            mix_pieces += combine(
+                pair_places(g * group + 2 * at), made[4], 2, local, cap, at, None,
+                [grad_up, *inside],
+            )
 
     if n_ep == 8:
         gates_here = home_gates[:expert_count]
@@ -870,27 +929,25 @@
         d_normed - one_normed * jnp.mean(d_normed * one_normed, axis=-1, keepdims=True)
     )
     d_z = d_one.astype(BF16)
-    d_attn = out_back(ids, n_ep, d_z, w_o_parts)
+    d_attn = out_back(ids, n_ep, d_z, w_o_parts, [grad_up, grad_gate, grad_down, *mix_pieces])
     d_heads = lax.all_to_all(d_attn, "sp", split_axis=1, concat_axis=0, tiled=True)
     d_z_cols = lax.all_to_all(d_z, "sp", split_axis=1, concat_axis=0, tiled=True)
-    out_grads = grad_pieces(ids, n_ep, attn_all, d_z_cols, "out_grads")
-
-    mix_pieces = []
-    for g, (_, _, made) in enumerate(groups):
-        for at in range(group // 2):
-            mix_pieces += combine(pair_places(g * group + 2 * at), made[4], 2, local, cap, at)
-    if shard == tok_dev:
-        sent = [jnp.concatenate(two, axis=1) for two in zip(mix_pieces, out_grads)]
-        got = scatter_turn(sent, n_ep)
-        mix, grad_out = got[:, :width], got[:, width:].astype(BF16)
+    if n_ep == 8:
+        mix_sums = crossed_sums(mix_pieces)
+        mix_sums[0], mix_sums[1], d_heads = tie(mix_sums[0], mix_sums[1], d_heads)
+    grad_down, grad_gate, grad_up = over_sp(grad_down), over_sp(grad_gate), over_sp(grad_up)
+
+    d_qn, d_kn, d_v, sums, grad_qg, grad_kg = attend_back(
+        q_rot, k_rot, v_low, d_heads, q_raw, k_raw, scales, gain_q, gain_k, cosine, sine, starts
+    )
+    if n_ep == 8:
+        mix_sums[2], mix_sums[3], d_v = tie(mix_sums[2], mix_sums[3], d_v)
+        mix = turned_sum(mix_sums)
     else:
         mix = scatter_turn(mix_pieces, n_ep)
-        grad_out = scatter_turn(out_grads, n_ep).astype(BF16)
     output = (x_one + mix).astype(BF16)
-
-    d_qn, d_kn, d_v, sums, grad_qg, grad_kg = attend_back(
-        q_rot, k_rot, v_low, d_heads, q_raw, k_raw, scales, gain_q, gain_k, cosine, sine, starts
-    )
+    vo_pieces = vo_grads(ids, n_ep, h_all, d_v, attn_all, d_z_cols)
+    grad_vo = scatter_turn(vo_pieces, n_ep).astype(BF16)
 
     def placed(value):
         return lax.dynamic_update_slice_in_dim(
@@ -900,12 +957,12 @@
     tiny = jnp.concatenate(
         [placed(grad_qg), placed(grad_kg), grad_ffn[None], grad_router], axis=0
     )
-    *qkv_pieces, d_qkv = qkv_back(
-        ids, n_ep, h_all, d_qn, d_kn, d_v, q_raw, k_raw, scales, sum_sp(sums), tiny
-    )
-    grad_qkv = scatter_line(qkv_pieces, n_ep).astype(BF16)
-
-    d_h = d_h_rows(d_qkv, w_qk, w_v).reshape(n_sp, tok_dev, width)
+    *qk_pieces, d_qk = qk_back(
+        ids, n_ep, h_all, d_qn, d_kn, q_raw, k_raw, scales, sum_sp(sums), tiny, vo_pieces[-1:]
+    )
+    grad_qk = scatter_turn(qk_pieces, n_ep).astype(BF16)
+
+    d_h = d_h_rows(d_qk, d_v, w_qk, w_v).reshape(n_sp, tok_dev, width)
     parts = [
         lax.dynamic_index_in_dim(d_h, partners[j], 0, keepdims=False) for j in range(4)
     ]
@@ -918,18 +975,11 @@
         d_normed - x_normed * jnp.mean(d_normed * x_normed, axis=-1, keepdims=True)
     )
 
-    g_query, g_key, g_value, tiny, g_attn = finish(
-        ids, n_ep, w_query, w_key, w_value, attn_gain.astype(F32)[:, None], gather_sp(grad_qkv)
-    )
-    out_parts = gather_sp(grad_out)
-    g_out = jnp.concatenate(
-        [
-            lax.dynamic_index_in_dim(jnp.stack(out_parts), partners[j], 0, keepdims=False)
-            for j in range(4)
-        ],
-        axis=1,
-    ).astype(F32)
-    per_row = 3 * head_width // shard
+    g_query, g_key, g_value, g_out, tiny, g_attn = finish(
+        ids, n_ep, w_query, w_key, w_value, attn_gain.astype(F32)[:, None],
+        gather_sp(grad_qk), gather_sp(grad_vo),
+    )
+    per_row = 2 * head_width // shard
 
     def vector(at):
         col = (at % per_row) * shard

time: 1270 us -> 1070 us (0.84)
  waiting for transfers between devices: 575 us -> 469 us
  starting transfers between devices: 185 us -> 110 us
  blocking collectives: 18.5 us -> 0 us
    ppermute x64 -> x67, waiting for transfers between devices: 524 us -> 431 us  [shift(): return lax.ppermute(value, 'ep', pairs)]
    ppermute x64 -> x67, starting transfers between devices: 165 us -> 85.9 us  [shift(): return lax.ppermute(value, 'ep', pairs)]
    all_to_all x1 -> x0, blocking collectives: 18.5 us -> none  [body(): lax.all_to_all(mixed, 'sp', split_axis=0, concat_axis=1, tiled=True)]
    ppermute x16, waiting for transfers between devices: 42.1 us -> 26.8 us  [swap_sp(): return lax.ppermute(value, 'sp', [(i, i ^ bits) for i in range(4)])]
    convert_element_type x12 -> x17, other arithmetic: 23.1 us -> 32.3 us  [plus(): return (left.astype(F32) + right.astype(F32)).astype(left.dtype)]
  transfers between devices with their start and end apart: 88 -> 92, of which waited for: 39 -> 32; matrix products, arithmetic and copies ran while one was open for 8% -> 9% of each run, Pallas kernels for 25% -> 31%
where the time goes in v2:
time: 1070 us; the launch traced here: 1060 us
  waiting for transfers between devices  469 us (44%)
  Pallas kernels  326 us (30%)
  starting transfers between devices  110 us (10%)
  other arithmetic  75 us (7%)
  between operations  38.5 us (4%)
  local copies, waits for them, and re-layouts  36.7 us (3%)
    ppermute x67, waiting for transfers between devices, shift(): return lax.ppermute(value, 'ep', pairs)  431 us
    pallas_call x31, Pallas kernels, call(): pl.pallas_call(kernel, grid_spec=pltpu.PrefetchScalarGridSpec(num_scalar_...  326 us
    ppermute x67, starting transfers between devices, shift(): return lax.ppermute(value, 'ep', pairs)  85.9 us
    convert_element_type x17, other arithmetic, plus(): return (left.astype(F32) + right.astype(F32)).astype(left.dtype)  32.3 us
    ppermute x16, waiting for transfers between devices, swap_sp(): return lax.ppermute(value, 'sp', [(i, i ^ bits) for i in range(4)])  26.8 us
  transfers between devices with their start and end apart: 92, of which 32 were waited for; matrix products, arithmetic and copies ran while one was open for 9% of the time, Pallas kernels for 31%

profile of v2, /device:TPU:0, one launch (start us, length us, event | category | flops | bytes accessed | tf_op | source)
XLA Modules:
  0.0 1059.9 jit_solution(4282460312703031575)
XLA Ops:
  51.5 11.6 %collective-permute-done.12.refs_6_ = bf16[256,1024]{1,0:T(8,128)(2,1)S(1)} collective-permute-done((bf16[256,1024]{1,0:T(8,128)(2,1)S(1)}, bf16[256,1024]{1,0:T(8,128)(2,1)S(1)}, u32[]{:S(2)}, u32[]{:S(2)}) %collective-permute-start.12) | collective-permute-done | bytes 524320 | tf_op jit(solution)/shard_map/ppermute | solution.py:93
  65.2 7.1 collective-permute-done.13.refs_7_
  87.2 17.2 %collective-permute-done.10.refs_4_ = bf16[256,1024]{1,0:T(8,128)(2,1)} collective-permute-done((bf16[256,1024]{1,0:T(8,128)(2,1)S(1)}, bf16[256,1024]{1,0:T(8,128)(2,1)}, u32[]{:S(2)}, u32[]{:S(2)}) %collective-permute-start.10) | collective-permute-done | bytes 524320 | tf_op jit(solution)/shard_map/ppermute | solution.py:93
  107.0 30.3 %collective-permute-done.20.refs_9_ = bf16[256,1024]{1,0:T(8,128)(2,1)} collective-permute-done((bf16[256,1024]{1,0:T(8,128)(2,1)S(1)}, bf16[256,1024]{1,0:T(8,128)(2,1)}, u32[]{:S(2)}, u32[]{:S(2)}) %collective-permute-start.20) | collective-permute-done | bytes 524320 | tf_op jit(solution)/shard_map/ppermute | solution.py:93
  137.3 7.1 collective-permute-start.15
  148.8 11.0 %qk_project.1 = (f32[1024,512]{1,0:T(8,128)}, f32[1024,512]{1,0:T(8,128)}, f32[16,1024]{1,0:T(8,128)}, bf16[2048,1024]{1,0:T(8,128)(2,1)}) custom-call(s32[12]{0:T(128)} %pad_add_fusion.ids.refs_0_, bf16[1024,2048]{1,0:T(8,128)(2,1)} %all-gather.3.cloned.1.call-done.h_ref.refs_1_, bf16[256,1024]{1,0:T(8,128)(2,1)} %copy-done.39, ...), custom_call_target="tpu_custom_call" | custom-call | flops 85899345920 | bytes 16842752 | tf_op jit(solution)/shard_map/qk_project/pallas_call | solution.py:62
  159.8 6.0 collective-permute-done.15.refs_4_
  172.9 10.2 collective-permute-done.16.refs_5_
  183.6 10.5 collective-permute-done.26.refs_1_
  194.7 17.1 %collective-permute-done.31.refs_1_ = bf16[256,2048]{1,0:T(8,128)(2,1)S(1)} collective-permute-done((bf16[256,2048]{1,0:T(8,128)(2,1)S(1)}, bf16[256,2048]{1,0:T(8,128)(2,1)S(1)}, u32[]{:S(2)}, u32[]{:S(2)}) %collective-permute-start.31) | collective-permute-done | bytes 1048608 | tf_op jit(solution)/shard_map/ppermute | solution.py:93
  212.3 36.4 %collective-permute-done.34.refs_1_ = bf16[256,2048]{1,0:T(8,128)(2,1)} collective-permute-done((bf16[256,2048]{1,0:T(8,128)(2,1)S(1)}, bf16[256,2048]{1,0:T(8,128)(2,1)}, u32[]{:S(2)}, u32[]{:S(2)}) %collective-permute-start.34) | collective-permute-done | bytes 1048608 | tf_op jit(solution)/shard_map/ppermute | solution.py:93
  251.6 8.4 v_project.1
  261.3 17.2 %attend.1 = (bf16[1024,512]{1,0:T(8,128)(2,1)}, bf16[1024,512]{1,0:T(8,128)(2,1)}, bf16[1024,512]{1,0:T(8,128)(2,1)}) custom-call(f32[1024,512]{1,0:T(8,128)} %get-tuple-element.108.refs_10_.qr_ref.refs_4_, f32[1024,512]{1,0:T(8,128)} %get-tuple-element.109.kr_ref.refs_5_, bf16[1024,512]{1,0:T(8,128)(2,1)} %get-tuple-element.112.v_ref, ...), custom_call_target="tpu_custom_call" | custom-call | flops 32212254720 | bytes 9510912 | tf_op jit(solution)/shard_map/attend/pallas_call | solution.py:62
  282.7 23.4 %collective-permute-done.24.refs_6_.refs_4_ = bf16[2048,512]{1,0:T(8,128)(2,1)} collective-permute-done((bf16[2048,512]{1,0:T(8,128)(2,1)}, bf16[2048,512]{1,0:T(8,128)(2,1)}, u32[]{:S(2)}, u32[]{:S(2)}) %collective-permute-start.24) | collective-permute-done | bytes 2097184 | tf_op jit(solution)/shard_map/ppermute | solution.py:101
  314.9 9.0 out_project.1
  336.0 13.8 %collective-permute-done.29.refs_0_ = bf16[256,2048]{1,0:T(8,128)(2,1)} collective-permute-done((bf16[256,2048]{1,0:T(8,128)(2,1)}, bf16[256,2048]{1,0:T(8,128)(2,1)}, u32[]{:S(2)}, u32[]{:S(2)}) %collective-permute-start.29) | collective-permute-done | bytes 1048608 | tf_op jit(solution)/shard_map/ppermute | solution.py:93
  354.2 4.4 dispatch.10
  358.7 20.7 %collective-permute-done.40 = bf16[256,2048]{1,0:T(8,128)(2,1)S(1)} collective-permute-done((bf16[256,2048]{1,0:T(8,128)(2,1)S(1)}, bf16[256,2048]{1,0:T(8,128)(2,1)S(1)}, u32[]{:S(2)}, u32[]{:S(2)}) %collective-permute-start.40) | collective-permute-done | bytes 1048608 | tf_op jit(solution)/shard_map/ppermute | solution.py:93
  385.3 4.5 dispatch.11
  389.8 42.6 %experts.2 = (bf16[2,576,1024]{2,1,0:T(8,128)(2,1)}, bf16[2,576,1024]{2,1,0:T(8,128)(2,1)}, bf16[2,576,1024]{2,1,0:T(8,128)(2,1)}, f32[2,576,1]{2,1,0:T(8,128)},...) custom-call(bf16[2,576,2048]{2,1,0:T(8,128)(2,1)} %get-tuple-element.122.refs_0_, ...), custom_call_target="tpu_custom_call" | custom-call | flops 579820584960 | bytes 51127296 | tf_op jit(solution)/shard_map/experts/pallas_call | solution.py:62
  435.6 4.4 dispatch.14
  440.0 17.5 %collective-permute-done.39.refs_2_ = bf16[256,2048]{1,0:T(8,128)(2,1)S(1)} collective-permute-done((bf16[256,2048]{1,0:T(8,128)(2,1)S(1)}, bf16[256,2048]{1,0:T(8,128)(2,1)S(1)}, u32[]{:S(2)}, u32[]{:S(2)}) %collective-permute-start.39) | collective-permute-done | bytes 1048608 | tf_op jit(solution)/shard_map/ppermute | solution.py:93
  458.6 4.5 dispatch.15
  473.0 42.4 %experts.3 = (bf16[2,576,1024]{2,1,0:T(8,128)(2,1)}, bf16[2,576,1024]{2,1,0:T(8,128)(2,1)}, bf16[2,576,1024]{2,1,0:T(8,128)(2,1)}, f32[2,576,1]{2,1,0:T(8,128)},...) custom-call(bf16[2,576,2048]{2,1,0:T(8,128)(2,1)} %get-tuple-element.128.refs_3_.refs_0_.refs_1_, ...), custom_call_target="tpu_custom_call" | custom-call | flops 579820584960 | bytes 51127296 | tf_op jit(solution)/shard_map/experts/pallas_call | solution.py:62
  515.4 18.7 %weight_grad.4.refs_9_.refs_7_ = bf16[2,2048,1024]{2,1,0:T(8,128)(2,1)} custom-call(bf16[2,576,2048]{2,1,0:T(8,128)(2,1)} %get-tuple-element.122.refs_0_, bf16[2,576,2048]{2,1,0:T(8,128)(2,1)} %get-tuple-element.128.refs_3_.refs_0_.refs_1_, bf16[2,576,1024]{2,1,0:T(8,128)(2,1)} %get-tuple-element.145.refs_2_, bf16[2,576,1024]{2,1,0:T(8,128)(2,1)} %get-tuple-element.146.refs_3_), custom_call_target="tpu_custom_call" | custom-call | flops 193273528320 | bytes 22544384 | tf_op jit(solution)/shard_map/weight_grad/pallas_call | solution.py:62
  546.1 4.8 combine.11
  556.7 5.6 all-to-all-start.1
  562.3 8.7 collective-permute-done.44
  572.4 6.8 collective-permute-start.47
  579.2 18.0 %weight_grad.3.refs_8_ = bf16[2,1024,2048]{2,1,0:T(8,128)(2,1)} custom-call(bf16[2,576,1024]{2,1,0:T(8,128)(2,1)} %get-tuple-element.143.refs_0_, bf16[2,576,1024]{2,1,0:T(8,128)(2,1)} %get-tuple-element.144.refs_1_, bf16[2,576,2048]{2,1,0:T(8,128)(2,1)} %dispatch.9.refs_8_.refs_1_.refs_6_.refs_10_.refs_2_, ...), custom_call_target="tpu_custom_call" | custom-call | flops 193273528320 | bytes 22544384 | tf_op jit(solution)/shard_map/weight_grad/pallas_call | solution.py:62
  606.9 18.7 %weight_grad.5.refs_2_.refs_6_ = bf16[2,2048,1024]{2,1,0:T(8,128)(2,1)} custom-call(bf16[2,576,2048]{2,1,0:T(8,128)(2,1)} %get-tuple-element.122.refs_0_, bf16[2,576,2048]{2,1,0:T(8,128)(2,1)} %get-tuple-element.128.refs_3_.refs_0_.refs_1_, bf16[2,576,1024]{2,1,0:T(8,128)(2,1)} %get-tuple-element.129.refs_2_, ...), custom_call_target="tpu_custom_call" | custom-call | flops 193273528320 | bytes 22544384 | tf_op jit(solution)/shard_map/weight_grad/pallas_call | solution.py:62
  652.1 12.7 %collective-permute-done.48 = bf16[256,2048]{1,0:T(8,128)(2,1)} collective-permute-done((bf16[256,2048]{1,0:T(8,128)(2,1)}, bf16[256,2048]{1,0:T(8,128)(2,1)}, u32[]{:S(2)}, u32[]{:S(2)}) %collective-permute-start.48) | collective-permute-done | bytes 1048608 | tf_op jit(solution)/shard_map/ppermute | solution.py:93
  667.6 19.5 %collective-permute-done.49 = bf16[256,2048]{1,0:T(8,128)(2,1)S(1)} collective-permute-done((bf16[256,2048]{1,0:T(8,128)(2,1)}, bf16[256,2048]{1,0:T(8,128)(2,1)S(1)}, u32[]{:S(2)}, u32[]{:S(2)}) %collective-permute-start.49) | collective-permute-done | bytes 1048608 | tf_op jit(solution)/shard_map/ppermute | solution.py:93
  693.5 9.1 out_back.1
  711.0 11.9 %collective-permute-done.55 = bf16[256,2048]{1,0:T(8,128)(2,1)} collective-permute-done((bf16[256,2048]{1,0:T(8,128)(2,1)}, bf16[256,2048]{1,0:T(8,128)(2,1)}, u32[]{:S(2)}, u32[]{:S(2)}) %collective-permute-start.55) | collective-permute-done | bytes 1048608 | tf_op jit(solution)/shard_map/ppermute | solution.py:93
  726.6 8.9 all-to-all-done.2
  739.0 23.2 %attend_back.1 = (f32[1024,512]{1,0:T(8,128)}, f32[1024,512]{1,0:T(8,128)}, bf16[1024,512]{1,0:T(8,128)(2,1)}, f32[16,1024]{1,0:T(8,128)}, f32[1,512]{1,0:T(1,128)}, /*index=5*/f32[1,512]{1,0:T(1,128)}) custom-call(bf16[1024,512]{1,0:T(8,128)(2,1)} %get-tuple-element.163.q_ref, bf16[1024,512]{1,0:T(8,128)(2,1)} %get-tuple-element.164.k_ref, ...), custom_call_target="tpu_custom_call" | custom-call | flops 75161927680 | bytes 14823424 | tf_op jit(solution)/shard_map/attend_back/pallas_call | solution.py:62
  766.0 10.2 vo_grads.1
  785.3 12.4 %qk_back.1 = (bf16[272,1024]{1,0:T(8,128)(2,1)}, bf16[272,1024]{1,0:T(8,128)(2,1)}, bf16[272,1024]{1,0:T(8,128)(2,1)}, bf16[272,1024]{1,0:T(8,128)(2,1)}, bf16[2...) custom-call(s32[12]{0:T(128)} %pad_add_fusion.ids.refs_0_, ...), custom_call_target="tpu_custom_call" | custom-call | flops 85899345920 | bytes 19423232 | tf_op jit(solution)/shard_map/qk_back/pallas_call | solution.py:62
  797.7 11.7 %d_h.1 = bf16[1024,2048]{1,0:T(8,128)(2,1)} custom-call(bf16[1024,1024]{1,0:T(8,128)(2,1)} %get-tuple-element.176.d_ref, bf16[1024,512]{1,0:T(8,128)(2,1)} %get-tuple-element.174.dv_ref, bf16[2048,1024]{1,0:T(8,128)(2,1)} %get-tuple-element.177.qk_ref, bf16[2048,512]{1,0:T(8,128)(2,1)} %get-tuple-element.178.v_ref), custom_call_target="tpu_custom_call" | custom-call | flops 128849018880 | bytes 13631488 | tf_op jit(solution)/shard_map/d_h/pallas_call | solution.py:62
  820.2 16.7 %collective-permute-done.68 = bf16[272,1024]{1,0:T(8,128)(2,1)S(1)} collective-permute-done((bf16[272,1024]{1,0:T(8,128)(2,1)S(1)}, bf16[272,1024]{1,0:T(8,128)(2,1)S(1)}, u32[]{:S(2)}, u32[]{:S(2)}) %collective-permute-start.68) | collective-permute-done | bytes 557088 | tf_op jit(solution)/shard_map/ppermute | solution.py:93
  841.0 7.9 collective-permute-done.66
  850.3 10.5 collective-permute-done.64
  862.7 8.7 collective-permute-done.63
  872.9 34.1 %collective-permute-done.77 = bf16[256,1024]{1,0:T(8,128)(2,1)S(1)} collective-permute-done((bf16[256,1024]{1,0:T(8,128)(2,1)S(1)}, bf16[256,1024]{1,0:T(8,128)(2,1)S(1)}, u32[]{:S(2)}, u32[]{:S(2)}) %collective-permute-start.77) | collective-permute-done | bytes 524320 | tf_op jit(solution)/shard_map/ppermute | solution.py:93
  917.5 58.2 %collective-permute-done.67 = bf16[272,1024]{1,0:T(8,128)(2,1)} collective-permute-done((bf16[272,1024]{1,0:T(8,128)(2,1)}, bf16[272,1024]{1,0:T(8,128)(2,1)}, u32[]{:S(2)}, u32[]{:S(2)}) %collective-permute-start.67) | collective-permute-done | bytes 557088 | tf_op jit(solution)/shard_map/ppermute | solution.py:93
  983.6 38.6 %collective-permute-done.56 = bf16[256,2048]{1,0:T(8,128)(2,1)S(1)} collective-permute-done((bf16[256,2048]{1,0:T(8,128)(2,1)}, bf16[256,2048]{1,0:T(8,128)(2,1)S(1)}, u32[]{:S(2)}, u32[]{:S(2)}) %collective-permute-start.56) | collective-permute-done | bytes 1048608 | tf_op jit(solution)/shard_map/ppermute | solution.py:93
  1028.4 8.0 finish.1
  (461 shorter events, 260.8 us)
Async XLA Ops:
  7.2 141.6 %all-gather.3.cloned.1.call-start = ((), (), s32[]{:S(2)}) async-start(), calls=%async_computation.7 | async-start | bytes 5242880 | tf_op jit(solution)/shard_map/all_gather | solution.py:792
  50.1 94.3 %collective-permute-start.7 = (bf16[256,1024]{1,0:T(8,128)(2,1)S(1)}, bf16[256,1024]{1,0:T(8,128)(2,1)}, u32[]{:S(2)}, u32[]{:S(2)}) collective-permute-start(bf16[256,1024]{1,0:T(8,128)(2,1)S(1)} %pad_maximum_fusion.refs_0_), channel_id=1, source_target_pairs={{0,1},{1,0},{2,3},{3,2},{4,5},{5,4},{6,7},{7,6},{8,9},{9,8},{10,11... | collective-permute-start | bytes 1572872 | tf_op jit(solution)/shard_map/ppermute | solution.py:93
  50.6 53.8 %collective-permute-start.10 = (bf16[256,1024]{1,0:T(8,128)(2,1)S(1)}, bf16[256,1024]{1,0:T(8,128)(2,1)}, u32[]{:S(2)}, u32[]{:S(2)}) collective-permute-start(bf16[256,1024]{1,0:T(8,128)(2,1)S(1)} %pad_maximum_fusion.refs_0_), channel_id=1, source_target_pairs={{0,4},{1,5},{2,6},{3,7},{4,0},{5,1},{6,2},{7,3},{8,12},{9,13},{10,... | collective-permute-start | bytes 1572872 | tf_op jit(solution)/shard_map/ppermute | solution.py:93
  86.7 57.7 %collective-permute-start.9 = (bf16[256,1024]{1,0:T(8,128)(2,1)}, bf16[256,1024]{1,0:T(8,128)(2,1)}, u32[]{:S(2)}, u32[]{:S(2)}) collective-permute-start(bf16[256,1024]{1,0:T(8,128)(2,1)} %collective-permute-done.8.refs_2_), channel_id=1, source_target_pairs={{0,1},{1,0},{2,3},{3,2},{4,5},{5,4},{6,7},{7,6},{8,9},{9,8},{10,11... | collective-permute-start | bytes 1572872 | tf_op jit(solution)/shard_map/ppermute | solution.py:93
  104.4 42.0 %collective-permute-start.11 = (bf16[256,1024]{1,0:T(8,128)(2,1)}, bf16[256,1024]{1,0:T(8,128)(2,1)}, u32[]{:S(2)}, u32[]{:S(2)}) collective-permute-start(bf16[256,1024]{1,0:T(8,128)(2,1)} %collective-permute-done.10.refs_4_), channel_id=1, source_target_pairs={{0,1},{1,0},{2,3},{3,2},{4,5},{5,4},{6,7},{7,6},{8,9},{9,8},{10,11... | collective-permute-start | bytes 1572872 | tf_op jit(solution)/shard_map/ppermute | solution.py:93
  104.9 43.9 %collective-permute-start.14 = (bf16[256,1024]{1,0:T(8,128)(2,1)S(1)}, bf16[256,1024]{1,0:T(8,128)(2,1)}, u32[]{:S(2)}, u32[]{:S(2)}) collective-permute-start(bf16[256,1024]{1,0:T(8,128)(2,1)S(1)} %pad_maximum_fusion.1.refs_2_), channel_id=1, source_target_pairs={{0,1},{1,0},{2,3},{3,2},{4,5},{5,4},{6,7},{7,6},{8,9},{9,8},{10,11... | collective-permute-start | bytes 1572872 | tf_op jit(solution)/shard_map/ppermute | solution.py:93
  144.4 49.7 %collective-permute-start.26 = (bf16[256,2048]{1,0:T(8,128)(2,1)S(1)}, bf16[256,2048]{1,0:T(8,128)(2,1)}, u32[]{:S(2)}, u32[]{:S(2)}) collective-permute-start(bf16[256,2048]{1,0:T(8,128)(2,1)S(1)} %bitcast.146), channel_id=1, source_target_pairs={{0,2},{1,3},{2,0},{3,1},{4,6},{5,7},{6,4},{7,5},{8,10},{9,11},{10,... | collective-permute-start | bytes 3145736 | tf_op jit(solution)/shard_map/ppermute | solution.py:93
  146.3 65.5 %collective-permute-start.31 = (bf16[256,2048]{1,0:T(8,128)(2,1)S(1)}, bf16[256,2048]{1,0:T(8,128)(2,1)S(1)}, u32[]{:S(2)}, u32[]{:S(2)}) collective-permute-start(bf16[256,2048]{1,0:T(8,128)(2,1)S(1)} %bitcast.147), channel_id=1, source_target_pairs={{0,6},{1,7},{2,4},{3,5},{4,2},{5,3},{6,0},{7,1},{8,14},{9,15},{10,... | collective-permute-start | bytes 3145736 | tf_op jit(solution)/shard_map/ppermute | solution.py:93
  148.8 100.0 %collective-permute-start.34 = (bf16[256,2048]{1,0:T(8,128)(2,1)S(1)}, bf16[256,2048]{1,0:T(8,128)(2,1)}, u32[]{:S(2)}, u32[]{:S(2)}) collective-permute-start(bf16[256,2048]{1,0:T(8,128)(2,1)S(1)} %bitcast.148), channel_id=1, source_target_pairs={{0,4},{1,5},{2,6},{3,7},{4,0},{5,1},{6,2},{7,3},{8,12},{9,13},{10,... | collective-permute-start | bytes 3145736 | tf_op jit(solution)/shard_map/ppermute | solution.py:93
  168.6 80.7 %collective-permute-start.18 = (bf16[256,1024]{1,0:T(8,128)(2,1)S(1)}, bf16[256,1024]{1,0:T(8,128)(2,1)S(1)}, u32[]{:S(2)}, u32[]{:S(2)}) collective-permute-start(bf16[256,1024]{1,0:T(8,128)(2,1)S(1)} %collective-permute-done.17.refs_6_), channel_id=1, source_target_pairs={{0,1},{1,0},{2,3},{3,2},{4,5},{5,4},{6,7},{7,6},{8,9},{9,8},{10,11... | collective-permute-start | bytes 1572872 | tf_op jit(solution)/shard_map/ppermute | solution.py:93
  183.1 99.1 %collective-permute-start.28 = (bf16[256,2048]{1,0:T(8,128)(2,1)S(1)}, bf16[256,2048]{1,0:T(8,128)(2,1)}, u32[]{:S(2)}, u32[]{:S(2)}) collective-permute-start(bf16[256,2048]{1,0:T(8,128)(2,1)S(1)} %bitcast.149), channel_id=1, source_target_pairs={{0,1},{1,0},{2,3},{3,2},{4,5},{5,4},{6,7},{7,6},{8,9},{9,8},{10,11... | collective-permute-start | bytes 3145736 | tf_op jit(solution)/shard_map/ppermute | solution.py:93
  194.2 115.8 %collective-permute-start.27 = (bf16[256,2048]{1,0:T(8,128)(2,1)}, bf16[256,2048]{1,0:T(8,128)(2,1)}, u32[]{:S(2)}, u32[]{:S(2)}) collective-permute-start(bf16[256,2048]{1,0:T(8,128)(2,1)} %collective-permute-done.26.refs_1_), channel_id=1, source_target_pairs={{0,1},{1,0},{2,3},{3,2},{4,5},{5,4},{6,7},{7,6},{8,9},{9,8},{10,11... | collective-permute-start | bytes 3145736 | tf_op jit(solution)/shard_map/ppermute | solution.py:93
  211.8 112.8 %collective-permute-start.32 = (bf16[256,2048]{1,0:T(8,128)(2,1)S(1)}, bf16[256,2048]{1,0:T(8,128)(2,1)}, u32[]{:S(2)}, u32[]{:S(2)}) collective-permute-start(bf16[256,2048]{1,0:T(8,128)(2,1)S(1)} %collective-permute-done.31.refs_1_), channel_id=1, source_target_pairs={{0,1},{1,0},{2,3},{3,2},{4,5},{5,4},{6,7},{7,6},{8,9},{9,8},{10,11... | collective-permute-start | bytes 3145736 | tf_op jit(solution)/shard_map/ppermute | solution.py:93
  248.7 79.7 %collective-permute-start.35 = (bf16[256,2048]{1,0:T(8,128)(2,1)}, bf16[256,2048]{1,0:T(8,128)(2,1)}, u32[]{:S(2)}, u32[]{:S(2)}) collective-permute-start(bf16[256,2048]{1,0:T(8,128)(2,1)} %collective-permute-done.34.refs_1_), channel_id=1, source_target_pairs={{0,1},{1,0},{2,3},{3,2},{4,5},{5,4},{6,7},{7,6},{8,9},{9,8},{10,11... | collective-permute-start | bytes 3145736 | tf_op jit(solution)/shard_map/ppermute | solution.py:93
  260.0 46.1 %collective-permute-start.24 = (bf16[2048,512]{1,0:T(8,128)(2,1)}, bf16[2048,512]{1,0:T(8,128)(2,1)}, u32[]{:S(2)}, u32[]{:S(2)}) collective-permute-start(bf16[2048,512]{1,0:T(8,128)(2,1)} %get-tuple-element.115.refs_4_.refs_2_), channel_id=1, source_target_pairs={{0,16},{8,24},{16,0},{24,8},{1,17},{9,25},{17,1},{25,9},{2,18},{10... | collective-permute-start | bytes 6291464 | tf_op jit(solution)/shard_map/ppermute | solution.py:101
  282.0 480.8 %all-gather.5.cloned.1.call-start = ((), (), s32[]{:S(2)}) async-start(), calls=%async_computation.8 | async-start | bytes 5242880 | tf_op jit(solution)/shard_map/all_gather | solution.py:848
  314.8 725.8 %reduce-scatter.4.cloned.1.call-start = ((), (), s32[]{:S(2)}) async-start(), calls=%async_computation.9 | async-start | bytes 10485760 | tf_op jit(solution)/shard_map/reduce_scatter | solution.py:900
  382.1 53.5 %collective-permute-start.41 = (bf16[256,2048]{1,0:T(8,128)(2,1)}, bf16[256,2048]{1,0:T(8,128)(2,1)}, u32[]{:S(2)}, u32[]{:S(2)}) collective-permute-start(bf16[256,2048]{1,0:T(8,128)(2,1)} %add.233.refs_1_), channel_id=1, source_target_pairs={{0,1},{1,0},{2,3},{3,2},{4,5},{5,4},{6,7},{7,6},{8,9},{9,8},{10,11... | collective-permute-start | bytes 3145736 | tf_op jit(solution)/shard_map/ppermute | solution.py:93
  382.7 49.8 %collective-permute-start.38 = (bf16[256,2048]{1,0:T(8,128)(2,1)}, bf16[256,2048]{1,0:T(8,128)(2,1)}, u32[]{:S(2)}, u32[]{:S(2)}) collective-permute-start(bf16[256,2048]{1,0:T(8,128)(2,1)} %collective-permute-done.37), channel_id=1, source_target_pairs={{2,0},{3,1},{4,6},{5,7},{10,8},{11,9},{12,14},{13,15},{18,16},{19,... | collective-permute-start | bytes 3145736 | tf_op jit(solution)/shard_map/ppermute | solution.py:93
  471.0 63.1 %collective-permute-start.42 = (bf16[256,2048]{1,0:T(8,128)(2,1)}, bf16[256,2048]{1,0:T(8,128)(2,1)}, u32[]{:S(2)}, u32[]{:S(2)}) collective-permute-start(bf16[256,2048]{1,0:T(8,128)(2,1)} %get-tuple-element.133.refs_7_), channel_id=1, source_target_pairs={{0,1},{1,0},{2,3},{3,2},{4,5},{5,4},{6,7},{7,6},{8,9},{9,8},{10,11... | collective-permute-start | bytes 3145736 | tf_op jit(solution)/shard_map/ppermute | solution.py:93
  472.5 65.4 %collective-permute-start.43 = (bf16[256,2048]{1,0:T(8,128)(2,1)}, bf16[256,2048]{1,0:T(8,128)(2,1)}, u32[]{:S(2)}, u32[]{:S(2)}) collective-permute-start(bf16[256,2048]{1,0:T(8,128)(2,1)} %get-tuple-element.135.refs_9_), channel_id=1, source_target_pairs={{0,1},{1,0},{2,3},{3,2},{4,5},{5,4},{6,7},{7,6},{8,9},{9,8},{10,11... | collective-permute-start | bytes 3145736 | tf_op jit(solution)/shard_map/ppermute | solution.py:93
  550.9 48.6 %collective-permute-start.45 = (bf16[256,2048]{1,0:T(8,128)(2,1)}, bf16[256,2048]{1,0:T(8,128)(2,1)}, u32[]{:S(2)}, u32[]{:S(2)}) collective-permute-start(bf16[256,2048]{1,0:T(8,128)(2,1)} %get-tuple-element.142), channel_id=1, source_target_pairs={{0,1},{1,0},{2,3},{3,2},{4,5},{5,4},{6,7},{7,6},{8,9},{9,8},{10,11... | collective-permute-start | bytes 3145736 | tf_op jit(solution)/shard_map/ppermute | solution.py:93
  556.7 40.6 %all-to-all-start.1 = ((f32[8,2,256]{2,1,0:T(2,128)}), f32[8,2,256]{2,1,0:T(2,128)}, u32[]{:S(2)}, u32[]{:S(2)}) async-start(f32[8,2,256]{2,1,0:T(2,128)} %constant_dynamic-update-slice_fusion.16), calls=%async_computation.1 | async-start | bytes 32768 | tf_op jit(solution)/shard_map/all_to_all | solution.py:903
  562.3 482.4 %reduce-scatter.8.cloned.1.call-start = ((), (), s32[]{:S(2)}) async-start(), calls=%async_computation.11 | async-start | bytes 10485760 | tf_op jit(solution)/shard_map/reduce_scatter | solution.py:900
  597.3 451.6 %reduce-scatter.6.cloned.1.call-start = ((), (), s32[]{:S(2)}) async-start(), calls=%async_computation.10 | async-start | bytes 10485760 | tf_op jit(solution)/shard_map/reduce_scatter | solution.py:900
  605.3 83.3 %collective-permute-start.50 = (bf16[256,2048]{1,0:T(8,128)(2,1)}, bf16[256,2048]{1,0:T(8,128)(2,1)}, u32[]{:S(2)}, u32[]{:S(2)}) collective-permute-start(bf16[256,2048]{1,0:T(8,128)(2,1)} %get-tuple-element.203.refs_4_), channel_id=1, source_target_pairs={{2,4},{3,5},{4,2},{5,3},{10,12},{11,13},{12,10},{13,11},{18,20},{1... | collective-permute-start | bytes 3145736 | tf_op jit(solution)/shard_map/ppermute | solution.py:93
  648.1 39.1 %collective-permute-start.49 = (bf16[256,2048]{1,0:T(8,128)(2,1)}, bf16[256,2048]{1,0:T(8,128)(2,1)S(1)}, u32[]{:S(2)}, u32[]{:S(2)}) collective-permute-start(bf16[256,2048]{1,0:T(8,128)(2,1)} %get-tuple-element.150.refs_12_), channel_id=1, source_target_pairs={{0,1},{1,0},{2,3},{3,2},{4,5},{5,4},{6,7},{7,6},{8,9},{9,8},{10,11... | collective-permute-start | bytes 3145736 | tf_op jit(solution)/shard_map/ppermute | solution.py:93
  648.5 61.2 %collective-permute-start.54 = (bf16[256,2048]{1,0:T(8,128)(2,1)}, bf16[256,2048]{1,0:T(8,128)(2,1)S(1)}, u32[]{:S(2)}, u32[]{:S(2)}) collective-permute-start(bf16[256,2048]{1,0:T(8,128)(2,1)} %get-tuple-element.158.refs_14_), channel_id=1, source_target_pairs={{0,1},{1,0},{2,3},{3,2},{4,5},{5,4},{6,7},{7,6},{8,9},{9,8},{10,11... | collective-permute-start | bytes 3145736 | tf_op jit(solution)/shard_map/ppermute | solution.py:93
  650.1 72.8 %collective-permute-start.55 = (bf16[256,2048]{1,0:T(8,128)(2,1)}, bf16[256,2048]{1,0:T(8,128)(2,1)}, u32[]{:S(2)}, u32[]{:S(2)}) collective-permute-start(bf16[256,2048]{1,0:T(8,128)(2,1)} %get-tuple-element.160.refs_16_), channel_id=1, source_target_pairs={{0,1},{1,0},{2,3},{3,2},{4,5},{5,4},{6,7},{7,6},{8,9},{9,8},{10,11... | collective-permute-start | bytes 3145736 | tf_op jit(solution)/shard_map/ppermute | solution.py:93
  776.2 36.1 %collective-permute-start.78 = (bf16[256,1024]{1,0:T(8,128)(2,1)}, bf16[256,1024]{1,0:T(8,128)(2,1)}, u32[]{:S(2)}, u32[]{:S(2)}) collective-permute-start(bf16[256,1024]{1,0:T(8,128)(2,1)} %get-tuple-element.175.refs_9_), channel_id=1, source_target_pairs={{0,1},{1,0},{2,3},{3,2},{4,5},{5,4},{6,7},{7,6},{8,9},{9,8},{10,11... | collective-permute-start | bytes 1572872 | tf_op jit(solution)/shard_map/ppermute | solution.py:93
  777.9 37.5 %collective-permute-start.76 = (bf16[256,1024]{1,0:T(8,128)(2,1)}, bf16[256,1024]{1,0:T(8,128)(2,1)}, u32[]{:S(2)}, u32[]{:S(2)}) collective-permute-start(bf16[256,1024]{1,0:T(8,128)(2,1)} %get-tuple-element.192), channel_id=1, source_target_pairs={{0,1},{1,0},{2,3},{3,2},{4,5},{5,4},{6,7},{7,6},{8,9},{9,8},{10,11... | collective-permute-start | bytes 1572872 | tf_op jit(solution)/shard_map/ppermute | solution.py:93
  778.2 38.9 %collective-permute-start.74 = (bf16[256,1024]{1,0:T(8,128)(2,1)}, bf16[256,1024]{1,0:T(8,128)(2,1)}, u32[]{:S(2)}, u32[]{:S(2)}) collective-permute-start(bf16[256,1024]{1,0:T(8,128)(2,1)} %get-tuple-element.190), channel_id=1, source_target_pairs={{0,1},{1,0},{2,3},{3,2},{4,5},{5,4},{6,7},{7,6},{8,9},{9,8},{10,11... | collective-permute-start | bytes 1572872 | tf_op jit(solution)/shard_map/ppermute | solution.py:93
  779.9 59.7 %collective-permute-start.73 = (bf16[256,1024]{1,0:T(8,128)(2,1)}, bf16[256,1024]{1,0:T(8,128)(2,1)}, u32[]{:S(2)}, u32[]{:S(2)}) collective-permute-start(bf16[256,1024]{1,0:T(8,128)(2,1)} %get-tuple-element.188), channel_id=1, source_target_pairs={{0,1},{1,0},{2,3},{3,2},{4,5},{5,4},{6,7},{7,6},{8,9},{9,8},{10,11... | collective-permute-start | bytes 1572872 | tf_op jit(solution)/shard_map/ppermute | solution.py:93
  812.3 94.6 %collective-permute-start.61 = (bf16[256,2048]{1,0:T(8,128)(2,1)S(1)}, bf16[256,2048]{1,0:T(8,128)(2,1)S(1)}, u32[]{:S(2)}, u32[]{:S(2)}) collective-permute-start(bf16[256,2048]{1,0:T(8,128)(2,1)S(1)} %get-tuple-element.206), channel_id=1, source_target_pairs={{0,8},{8,0},{16,24},{24,16},{1,9},{9,1},{17,25},{25,17},{2,10},{10... | collective-permute-start | bytes 3145736 | tf_op jit(solution)/shard_map/ppermute | solution.py:101
  817.2 43.6 %collective-permute-start.64 = (bf16[272,1024]{1,0:T(8,128)(2,1)S(1)}, bf16[272,1024]{1,0:T(8,128)(2,1)S(1)}, u32[]{:S(2)}, u32[]{:S(2)}) collective-permute-start(bf16[272,1024]{1,0:T(8,128)(2,1)S(1)} %copy-done.75), channel_id=1, source_target_pairs={{0,1},{1,0},{2,3},{3,2},{4,5},{5,4},{6,7},{7,6},{8,9},{9,8},{10,11... | collective-permute-start | bytes 1671176 | tf_op jit(solution)/shard_map/ppermute | solution.py:93
  848.8 58.1 %collective-permute-start.77 = (bf16[256,1024]{1,0:T(8,128)(2,1)S(1)}, bf16[256,1024]{1,0:T(8,128)(2,1)S(1)}, u32[]{:S(2)}, u32[]{:S(2)}) collective-permute-start(bf16[256,1024]{1,0:T(8,128)(2,1)S(1)} %add_convert_fusion.19), channel_id=1, source_target_pairs={{0,4},{1,5},{2,6},{3,7},{4,0},{5,1},{6,2},{7,3},{8,12},{9,13},{10,... | collective-permute-start | bytes 1572872 | tf_op jit(solution)/shard_map/ppermute | solution.py:93
  860.8 49.7 %collective-permute-start.75 = (bf16[256,1024]{1,0:T(8,128)(2,1)S(1)}, bf16[256,1024]{1,0:T(8,128)(2,1)S(1)}, u32[]{:S(2)}, u32[]{:S(2)}) collective-permute-start(bf16[256,1024]{1,0:T(8,128)(2,1)S(1)} %add_convert_fusion.20), channel_id=1, source_target_pairs={{0,2},{1,3},{2,0},{3,1},{4,6},{5,7},{6,4},{7,5},{8,10},{9,11},{10,... | collective-permute-start | bytes 1572872 | tf_op jit(solution)/shard_map/ppermute | solution.py:93
  871.4 106.8 %collective-permute-start.60 = (bf16[256,2048]{1,0:T(8,128)(2,1)}, bf16[256,2048]{1,0:T(8,128)(2,1)S(1)}, u32[]{:S(2)}, u32[]{:S(2)}) collective-permute-start(bf16[256,2048]{1,0:T(8,128)(2,1)} %get-tuple-element.205), channel_id=1, source_target_pairs={{0,8},{8,0},{16,24},{24,16},{1,9},{9,1},{17,25},{25,17},{2,10},{10... | collective-permute-start | bytes 3145736 | tf_op jit(solution)/shard_map/ppermute | solution.py:101
  871.4 42.4 %collective-permute-start.69 = (bf16[272,1024]{1,0:T(8,128)(2,1)}, bf16[272,1024]{1,0:T(8,128)(2,1)}, u32[]{:S(2)}, u32[]{:S(2)}) collective-permute-start(bf16[272,1024]{1,0:T(8,128)(2,1)} %add_convert_fusion.13), channel_id=1, source_target_pairs={{0,6},{1,7},{2,4},{3,5},{4,2},{5,3},{6,0},{7,1},{8,14},{9,15},{10,... | collective-permute-start | bytes 1671176 | tf_op jit(solution)/shard_map/ppermute | solution.py:93
  906.9 68.8 %collective-permute-start.67 = (bf16[272,1024]{1,0:T(8,128)(2,1)}, bf16[272,1024]{1,0:T(8,128)(2,1)}, u32[]{:S(2)}, u32[]{:S(2)}) collective-permute-start(bf16[272,1024]{1,0:T(8,128)(2,1)} %add_convert_fusion.14), channel_id=1, source_target_pairs={{0,4},{1,5},{2,6},{3,7},{4,0},{5,1},{6,2},{7,3},{8,12},{9,13},{10,... | collective-permute-start | bytes 1671176 | tf_op jit(solution)/shard_map/ppermute | solution.py:93
  907.7 68.0 %collective-permute-start.65 = (bf16[272,1024]{1,0:T(8,128)(2,1)}, bf16[272,1024]{1,0:T(8,128)(2,1)}, u32[]{:S(2)}, u32[]{:S(2)}) collective-permute-start(bf16[272,1024]{1,0:T(8,128)(2,1)} %add_convert_fusion.15), channel_id=1, source_target_pairs={{0,2},{1,3},{2,0},{3,1},{4,6},{5,7},{6,4},{7,5},{8,10},{9,11},{10,... | collective-permute-start | bytes 1671176 | tf_op jit(solution)/shard_map/ppermute | solution.py:93
  910.4 70.9 %collective-permute-start.62 = (bf16[256,2048]{1,0:T(8,128)(2,1)}, bf16[256,2048]{1,0:T(8,128)(2,1)S(1)}, u32[]{:S(2)}, u32[]{:S(2)}) collective-permute-start(bf16[256,2048]{1,0:T(8,128)(2,1)} %fusion.10), channel_id=1, source_target_pairs={{0,16},{8,24},{16,0},{24,8},{1,17},{9,25},{17,1},{25,9},{2,18},{10... | collective-permute-start | bytes 3145736 | tf_op jit(solution)/shard_map/ppermute | solution.py:101
  913.8 69.7 %collective-permute-start.57 = (bf16[256,2048]{1,0:T(8,128)(2,1)}, bf16[256,2048]{1,0:T(8,128)(2,1)S(1)}, u32[]{:S(2)}, u32[]{:S(2)}) collective-permute-start(bf16[256,2048]{1,0:T(8,128)(2,1)} %add_convert_fusion.1), channel_id=1, source_target_pairs={{0,6},{1,7},{2,4},{3,5},{4,2},{5,3},{6,0},{7,1},{8,14},{9,15},{10,... | collective-permute-start | bytes 3145736 | tf_op jit(solution)/shard_map/ppermute | solution.py:93
  975.7 46.5 %collective-permute-start.56 = (bf16[256,2048]{1,0:T(8,128)(2,1)}, bf16[256,2048]{1,0:T(8,128)(2,1)S(1)}, u32[]{:S(2)}, u32[]{:S(2)}) collective-permute-start(bf16[256,2048]{1,0:T(8,128)(2,1)} %add_convert_fusion.2), channel_id=1, source_target_pairs={{0,4},{1,5},{2,6},{3,7},{4,0},{5,1},{6,2},{7,3},{8,12},{9,13},{10,... | collective-permute-start | bytes 3145736 | tf_op jit(solution)/shard_map/ppermute | solution.py:93
  975.7 47.1 %collective-permute-start.53 = (bf16[256,2048]{1,0:T(8,128)(2,1)}, bf16[256,2048]{1,0:T(8,128)(2,1)S(1)}, u32[]{:S(2)}, u32[]{:S(2)}) collective-permute-start(bf16[256,2048]{1,0:T(8,128)(2,1)} %add_convert_fusion.4), channel_id=1, source_target_pairs={{0,2},{1,3},{2,0},{3,1},{4,6},{5,7},{6,4},{7,5},{8,10},{9,11},{10,... | collective-permute-start | bytes 3145736 | tf_op jit(solution)/shard_map/ppermute | solution.py:93
  978.2 44.5 %collective-permute-start.71 = (bf16[272,1024]{1,0:T(8,128)(2,1)S(1)}, bf16[272,1024]{1,0:T(8,128)(2,1)S(1)}, u32[]{:S(2)}, u32[]{:S(2)}) collective-permute-start(bf16[272,1024]{1,0:T(8,128)(2,1)S(1)} %add_convert_fusion.12.refs_0_), channel_id=1, source_target_pairs={{0,16},{8,24},{16,0},{24,8},{1,17},{9,25},{17,1},{25,9},{2,18},{10... | collective-permute-start | bytes 1671176 | tf_op jit(solution)/shard_map/ppermute | solution.py:101
  981.4 40.8 %collective-permute-start.81 = (bf16[256,1024]{1,0:T(8,128)(2,1)S(1)}, bf16[256,1024]{1,0:T(8,128)(2,1)S(1)}, u32[]{:S(2)}, u32[]{:S(2)}) collective-permute-start(bf16[256,1024]{1,0:T(8,128)(2,1)S(1)} %add_convert_fusion.17.refs_4_), channel_id=1, source_target_pairs={{0,16},{8,24},{16,0},{24,8},{1,17},{9,25},{17,1},{25,9},{2,18},{10... | collective-permute-start | bytes 1572872 | tf_op jit(solution)/shard_map/ppermute | solution.py:101
  983.5 43.1 %collective-permute-start.80 = (bf16[256,1024]{1,0:T(8,128)(2,1)S(1)}, bf16[256,1024]{1,0:T(8,128)(2,1)S(1)}, u32[]{:S(2)}, u32[]{:S(2)}) collective-permute-start(bf16[256,1024]{1,0:T(8,128)(2,1)S(1)} %add_convert_fusion.17.refs_4_), channel_id=1, source_target_pairs={{0,8},{8,0},{16,24},{24,16},{1,9},{9,1},{17,25},{25,17},{2,10},{10... | collective-permute-start | bytes 1572872 | tf_op jit(solution)/shard_map/ppermute | solution.py:101
  (129 other events, 2596.0 us)
Sparse Core Ops, SparseCore 0:
  45.3 34.7 all-gather.2
  315.0 32.6 all-gather.4
  534.2 71.7 reduce-scatter.3
  608.6 71.7 reduce-scatter.7
  682.8 94.1 reduce-scatter.5

commit v3 on v2

--- a/solution.py
+++ b/solution.py
@@ -80,21 +80,12 @@
     return jax.ShapeDtypeStruct(tuple(shape), dtype)
 
 
-MIDDLE = [(2, 4), (3, 5), (4, 2), (5, 3)]
-OUTWARD = [(2, 0), (3, 1), (4, 6), (5, 7)]
-INWARD = [(0, 2), (1, 3), (6, 4), (7, 5)]
-
-
 def tie(*values):
     return lax.optimization_barrier(values)
 
 
-def shift(value, pairs):
-    return lax.ppermute(value, "ep", pairs)
-
-
 def swap(value, bits):
-    return shift(value, [(i, i ^ bits) for i in range(8)])
+    return lax.ppermute(value, "ep", [(i, i ^ bits) for i in range(8)])
 
 
 def swap_sp(value, bits):
@@ -106,31 +97,25 @@
     return jnp.bitwise_xor(ids, ep_index) if n_ep == 8 else ids
 
 
-def gather_line(value, n_ep, gate=()):
-    if n_ep != 8:
-        return gather_turn(value, n_ep)
-    near = swap(value, 2)
-    inner_a = shift(value, MIDDLE)
-    inner_b = shift(near, MIDDLE)
-    third = inner_b + shift(inner_a, OUTWARD)
-    fourth = inner_a + shift(inner_b, OUTWARD)
-    crossed = value
-    if gate:
-        crossed = tie(value, *gate)[0]
-    pieces = [value, swap(crossed, 1)]
-    for own in (near, third, fourth):
+def along_z(value):
+    far = swap(value, 4)
+    return [value, swap(value, 2), far, swap(far, 2)]
+
+
+def across_x(blocks):
+    pieces = []
+    for own in blocks:
         pieces += [own, swap(own, 1)]
     return pieces
 
 
-def gather_turn(value, n_ep):
-    if n_ep != 8:
-        whole = lax.all_gather(value, "ep", axis=0, tiled=False)
-        return [whole[i] for i in range(n_ep)]
-    pieces = []
-    for own in (value, swap(value, 2), swap(value, 4), swap(value, 6)):
-        pieces += [own, swap(own, 1)]
-    return pieces
+def gather_whole(value):
+    whole = lax.all_gather(value, "ep", axis=0, tiled=False)
+    return [whole[i] for i in range(whole.shape[0])]
+
+
+def gather(value, n_ep):
+    return across_x(along_z(value)) if n_ep == 8 else gather_whole(value)
 
 
 def plus(left, right):
@@ -141,26 +126,16 @@
     return [plus(pieces[i], swap(pieces[i + 1], 1)) for i in range(0, len(pieces), 2)]
 
 
-def scatter_line(own, near, third, fourth):
-    third_in, fourth_in = shift(fourth, INWARD), shift(third, INWARD)
-    third, fourth = plus(third, third_in), plus(fourth, fourth_in)
-    near = plus(near, shift(third, MIDDLE))
-    total = own.astype(F32) + shift(fourth, MIDDLE).astype(F32) + swap(near, 2).astype(F32)
-    return total, [third, fourth]
-
-
-def turned_sum(sums):
-    total = sums[0].astype(F32)
-    for i in range(1, 4):
-        total = total + swap(sums[i], 2 * i).astype(F32)
-    return total
-
-
-def scatter_turn(pieces, n_ep):
+def scatter_z(own, near, far, farther):
+    far = plus(far, swap(farther, 2))
+    return own.astype(F32) + swap(near, 2).astype(F32) + swap(far, 4).astype(F32), far
+
+
+def scatter(pieces, n_ep):
     if n_ep != 8:
         stacked = jnp.stack(pieces)
         return lax.psum_scatter(stacked, "ep", scatter_dimension=0, tiled=False).astype(F32)
-    return turned_sum(crossed_sums(pieces))
+    return scatter_z(*crossed_sums(pieces))[0]
 
 
 def gather_sp(value):
@@ -361,7 +336,7 @@
     ).astype(BF16)
 
 
-def d_h_rows(d_qk, d_v, w_qk, w_v):
+def d_h_rows(d_qk, d_v, w_qk, w_v, after):
     total, wide = d_qk.shape
     depth = w_qk.shape[0]
     rows = min(256, total)
@@ -371,6 +346,7 @@
         [d_qk, d_v, w_qk, w_v],
         3 * d_qk.size * depth,
         "d_h",
+        after=after,
         grid=(total // rows,),
         in_specs=[
             pl.BlockSpec((rows, wide), lambda i: (i, 0)),
@@ -392,15 +368,15 @@
         for at, grad, weight in ((0, gq_ref, wq_ref), (1, gk_ref, wk_ref), (2, gv_ref, wv_ref)):
             part = firsts[j][:shard, at * width : (at + 1) * width] if at < 2 else seconds[j][:, :width]
             value = part.astype(F32)
-            grad[:, cols] = value
+            grad[:, cols] = value * gain_ref[...]
             dots += jnp.sum(value * weight[:, cols].astype(F32), axis=1, keepdims=True)
         go_ref[:, cols] = seconds[j][:, width:].astype(F32)
         tiny += firsts[j][shard:, :].astype(F32)
     tiny_ref[...] = tiny
-    attn_ref[...] = dots / gain_ref[...]
-
-
-def finish(ids, n_ep, w_query, w_key, w_value, gain, firsts, seconds):
+    attn_ref[...] = dots
+
+
+def finish(ids, n_ep, w_query, w_key, w_value, gain, firsts, seconds, after):
     shard, depth = w_query.shape
     extra = firsts[0].shape[0] - shard
     return call(
@@ -409,6 +385,7 @@
         [w_query, w_key, w_value, gain, *firsts, *seconds],
         shard * depth * 6,
         "finish",
+        after=after,
         scalars=(ids,),
     )
 
@@ -761,35 +738,54 @@
             [lax.dynamic_index_in_dim(value, order[i], 0, keepdims=False) for i in range(n_ep)]
         )
 
-    qk_pieces = gather_turn(
-        jnp.concatenate([own_columns(w_query), own_columns(w_key)], axis=1), n_ep
-    )
+    row_gain = attn_gain.astype(F32)[:, None]
+
+    def scaled(value):
+        return (own_columns(value).astype(F32) * row_gain).astype(BF16)
+
+    qk_own = jnp.concatenate([scaled(w_query), scaled(w_key)], axis=1)
+    vo_own = jnp.concatenate([scaled(w_value), own_columns(w_out)], axis=1)
+    cot_own = cotangent[0]
+    x_rows = tokens[0].astype(F32)
+    x_scale = lax.rsqrt(jnp.mean(x_rows * x_rows, axis=-1, keepdims=True) + EPS)
+    x_normed = x_rows * x_scale
+    h_all = lax.all_gather(x_normed.astype(BF16), "sp", axis=0, tiled=True)
 
     expert_ids = jnp.arange(expert_count, dtype=jnp.int32)
     picked = jnp.any(routes[0][:, :, None] == expert_ids[None, None, :], axis=1)
     small = jnp.concatenate(
         [
-            jnp.stack([attn_gain, q_gain, k_gain, ffn_gain]),
-            jnp.zeros((12, shard), BF16),
+            jnp.stack([q_gain, k_gain, ffn_gain]),
+            jnp.zeros((13, shard), BF16),
             w_router.T,
         ],
         axis=0,
     )
     picked_low = picked.T.astype(BF16)
+    if n_ep == 8:
+        qk_blocks = along_z(qk_own)
+        qk_blocks[2], vo_own, small = tie(qk_blocks[2], vo_own, small)
+        vo_blocks = along_z(vo_own)
+        vo_blocks[2], cot_own = tie(vo_blocks[2], cot_own)
+        cot_blocks = along_z(cot_own)
+        qk_pieces = across_x(qk_blocks)
+        qk_pieces[7], vo_blocks[0], vo_blocks[1] = tie(qk_pieces[7], vo_blocks[0], vo_blocks[1])
+        vo_pieces = across_x(vo_blocks)
+        vo_pieces[7], cot_blocks[0], cot_blocks[1] = tie(vo_pieces[7], cot_blocks[0], cot_blocks[1])
+        cot_pieces = across_x(cot_blocks)
+    else:
+        qk_pieces, vo_pieces, cot_pieces = (
+            gather_whole(value) for value in (qk_own, vo_own, cot_own)
+        )
     if shard == tok_dev:
-        both = jnp.stack(gather_turn(jnp.concatenate([small, picked_low], axis=0), n_ep))
+        both = jnp.stack(gather(jnp.concatenate([small, picked_low], axis=0), n_ep))
         small_all, picked_all = both[:, : 16 + expert_count], both[:, 16 + expert_count :]
     else:
-        small_all = jnp.stack(gather_turn(small, n_ep))
-        picked_all = jnp.stack(gather_turn(picked_low, n_ep))
+        small_all = jnp.stack(gather(small, n_ep))
+        picked_all = jnp.stack(gather(picked_low, n_ep))
     small_rows = jnp.swapaxes(by_block(small_all), 0, 1).reshape(16 + expert_count, width)
-    gains = small_rows[:4].astype(F32)
+    gains = small_rows[:3].astype(F32)
     full_router = small_rows[16:]
-
-    x_rows = tokens[0].astype(F32)
-    x_scale = lax.rsqrt(jnp.mean(x_rows * x_rows, axis=-1, keepdims=True) + EPS)
-    h_low = (x_rows * x_scale * gains[0][None, :]).astype(BF16)
-    h_all = lax.all_gather(h_low, "sp", axis=0, tiled=True)
 
     upper = (
         jnp.arange(tok_dev, dtype=jnp.int32)[:, None] < jnp.arange(tok_dev, dtype=jnp.int32)[None, :]
@@ -813,17 +809,11 @@
     sine = jnp.concatenate([-jnp.sin(angles), jnp.sin(angles)], axis=1)
     starts = starts[:, None].astype(jnp.int32)
 
-    vo_own = jnp.concatenate([own_columns(w_value), own_columns(w_out)], axis=1)
-    qk_pieces[-1], vo_own = tie(qk_pieces[-1], vo_own)
-    vo_pieces = gather_turn(vo_own, n_ep)
-    vo_pieces[-1], cot_own = tie(vo_pieces[-1], cotangent[0])
-    cot_pieces = gather_turn(cot_own, n_ep)
-
     q_raw, k_raw, squares, w_qk = qk_project(ids, h_all, qk_pieces)
     scales = lax.rsqrt(sum_sp(squares) / width + EPS)
     v_low, w_v, w_o = v_project(ids, h_all, vo_pieces, [q_raw])
     w_o_parts = gather_sp(w_o)
-    gain_q, gain_k = own_columns(gains)[1:2], own_columns(gains)[2:3]
+    gain_q, gain_k = own_columns(gains)[0:1], own_columns(gains)[1:2]
     q_rot, k_rot, mixed = attend(
         q_raw, k_raw, v_low, scales, gain_q, gain_k, cosine, sine, starts
     )
@@ -843,11 +833,11 @@
     attn_tok = lax.all_to_all(mixed, "sp", split_axis=0, concat_axis=1, tiled=True)
     near_rows = cot_rows(0, [mixed])
     x_one, h2_low = out_project(
-        ids, n_ep, attn_tok, tokens[0], gains[3:4], w_o_parts, [near_rows]
+        ids, n_ep, attn_tok, tokens[0], gains[2:3], w_o_parts, [near_rows]
     )
     attn_all = lax.all_gather(attn_tok, "sp", axis=0, tiled=True)
 
-    h2_pieces = gather_line(h2_low, n_ep, cot_pieces[-1:])
+    h2_pieces = gather(h2_low, n_ep)
     cots = [near_rows] + [cot_rows(g, [x_one]) for g in range(group, n_ep, group)]
     groups, d_pieces, d_gates, d_sums = [], [], [], []
     home_gates = None
@@ -889,10 +879,11 @@
     ins = [rows for rows, _, _ in groups]
     outs = [d_rows for _, d_rows, _ in groups]
     if n_ep == 8:
-        d_h2, inside = scatter_line(*d_sums)
+        d_h2, inside = scatter_z(*d_sums)
+        inside = [inside]
     else:
-        d_h2, inside = scatter_turn(d_pieces, n_ep), []
-    grad_down = weight_grad(acts, outs)
+        d_h2, inside = scatter(d_pieces, n_ep), []
+    grad_down = weight_grad(acts, outs, d_pieces)
     grad_gate = weight_grad(ins, d_gate_rows)
     grad_up = weight_grad(ins, d_up_rows, [*d_sums, grad_down, grad_gate])
 
@@ -924,7 +915,7 @@
     one_scale = lax.rsqrt(jnp.mean(x_one * x_one, axis=-1, keepdims=True) + EPS)
     one_normed = x_one * one_scale
     grad_ffn = jnp.sum(d_h2 * one_normed, axis=0)
-    d_normed = d_h2 * gains[3][None, :]
+    d_normed = d_h2 * gains[2][None, :]
     d_one = cotangent[0].astype(F32) + one_scale * (
         d_normed - one_normed * jnp.mean(d_normed * one_normed, axis=-1, keepdims=True)
     )
@@ -934,20 +925,20 @@
     d_z_cols = lax.all_to_all(d_z, "sp", split_axis=1, concat_axis=0, tiled=True)
     if n_ep == 8:
         mix_sums = crossed_sums(mix_pieces)
-        mix_sums[0], mix_sums[1], d_heads = tie(mix_sums[0], mix_sums[1], d_heads)
+        mix_sums[3], d_heads = tie(mix_sums[3], d_heads)
     grad_down, grad_gate, grad_up = over_sp(grad_down), over_sp(grad_gate), over_sp(grad_up)
 
     d_qn, d_kn, d_v, sums, grad_qg, grad_kg = attend_back(
         q_rot, k_rot, v_low, d_heads, q_raw, k_raw, scales, gain_q, gain_k, cosine, sine, starts
     )
     if n_ep == 8:
-        mix_sums[2], mix_sums[3], d_v = tie(mix_sums[2], mix_sums[3], d_v)
-        mix = turned_sum(mix_sums)
+        mix_sums[2], mix_sums[1], d_v = tie(mix_sums[2], mix_sums[1], d_v)
+        mix = scatter_z(*mix_sums)[0]
     else:
-        mix = scatter_turn(mix_pieces, n_ep)
+        mix = scatter(mix_pieces, n_ep)
     output = (x_one + mix).astype(BF16)
     vo_pieces = vo_grads(ids, n_ep, h_all, d_v, attn_all, d_z_cols)
-    grad_vo = scatter_turn(vo_pieces, n_ep).astype(BF16)
+    grad_vo = scatter(vo_pieces, n_ep).astype(BF16)
 
     def placed(value):
         return lax.dynamic_update_slice_in_dim(
@@ -960,24 +951,22 @@
     *qk_pieces, d_qk = qk_back(
         ids, n_ep, h_all, d_qn, d_kn, q_raw, k_raw, scales, sum_sp(sums), tiny, vo_pieces[-1:]
     )
-    grad_qk = scatter_turn(qk_pieces, n_ep).astype(BF16)
-
-    d_h = d_h_rows(d_qk, d_v, w_qk, w_v).reshape(n_sp, tok_dev, width)
+    grad_qk = scatter(qk_pieces, n_ep).astype(BF16)
+
+    d_h = d_h_rows(d_qk, d_v, w_qk, w_v, [output]).reshape(n_sp, tok_dev, width)
     parts = [
         lax.dynamic_index_in_dim(d_h, partners[j], 0, keepdims=False) for j in range(4)
     ]
     kept = plus(parts[0], swap_sp(parts[1], 1))
     sent = plus(parts[2], swap_sp(parts[3], 1))
     d_h = kept.astype(F32) + swap_sp(sent, 2).astype(F32)
-    x_normed = x_rows * x_scale
-    d_normed = d_h * gains[0][None, :]
     input_grad = d_one + x_scale * (
-        d_normed - x_normed * jnp.mean(d_normed * x_normed, axis=-1, keepdims=True)
+        d_h - x_normed * jnp.mean(d_h * x_normed, axis=-1, keepdims=True)
     )
 
     g_query, g_key, g_value, g_out, tiny, g_attn = finish(
-        ids, n_ep, w_query, w_key, w_value, attn_gain.astype(F32)[:, None],
-        gather_sp(grad_qk), gather_sp(grad_vo),
+        ids, n_ep, w_query, w_key, w_value, row_gain,
+        gather_sp(grad_qk), gather_sp(grad_vo), [grad_down, grad_gate, grad_up, input_grad],
     )
     per_row = 2 * head_width // shard
 

time: 1070 us -> 918 us (0.86)
  waiting for transfers between devices: 469 us -> 340 us
  starting transfers between devices: 110 us -> 91.9 us
    ppermute x67 -> x63, waiting for transfers between devices: 431 us -> 317 us  [swap(): return lax.ppermute(value, 'ep', [(i, i ^ bits) for i in range(8)])]
    ppermute x67 -> x63, starting transfers between devices: 85.9 us -> 68.4 us  [swap(): return lax.ppermute(value, 'ep', [(i, i ^ bits) for i in range(8)])]
    convert_element_type x17 -> x15, other arithmetic: 32.3 us -> 32.7 us  [plus(): return (left.astype(F32) + right.astype(F32)).astype(left.dtype)]
  transfers between devices with their start and end apart: 92 -> 88, of which waited for: 32 -> 39; matrix products, arithmetic and copies ran while one was open for 9% -> 11% of each run, Pallas kernels for 31% -> 35%
where the time goes in v3:
time: 918 us; the launch traced here: 907 us
  waiting for transfers between devices  340 us (37%)
  Pallas kernels  326 us (36%)
  starting transfers between devices  91.9 us (10%)
  other arithmetic  78.7 us (9%)
  between operations  38.6 us (4%)
  local copies, waits for them, and re-layouts  27.8 us (3%)
    pallas_call x31, Pallas kernels, call(): pl.pallas_call(kernel, grid_spec=pltpu.PrefetchScalarGridSpec(num_scalar_...  326 us
    ppermute x63, waiting for transfers between devices, swap(): return lax.ppermute(value, 'ep', [(i, i ^ bits) for i in range(8)])  317 us
    ppermute x63, starting transfers between devices, swap(): return lax.ppermute(value, 'ep', [(i, i ^ bits) for i in range(8)])  68.4 us
    convert_element_type x15, other arithmetic, plus(): return (left.astype(F32) + right.astype(F32)).astype(left.dtype)  32.7 us
    ppermute x16, waiting for transfers between devices, swap_sp(): return lax.ppermute(value, 'sp', [(i, i ^ bits) for i in range(4)])  22.4 us
  transfers between devices with their start and end apart: 88, of which 39 were waited for; matrix products, arithmetic and copies ran while one was open for 11% of the time, Pallas kernels for 35%

profile of v3, /device:TPU:0, one launch (start us, length us, event | category | flops | bytes accessed | tf_op | source)
XLA Modules:
  0.0 907.1 jit_solution(7517054454174331628)
XLA Ops:
  50.3 16.2 %collective-permute-done.18 = bf16[48,256]{1,0:T(8,128)(2,1)S(1)} collective-permute-done((bf16[48,256]{1,0:T(8,128)(2,1)S(1)}, bf16[48,256]{1,0:T(8,128)(2,1)S(1)}, u32[]{:S(2)}, u32[]{:S(2)}) %collective-permute-start.18) | collective-permute-done | bytes 24608 | tf_op jit(solution)/shard_map/ppermute | solution.py:88
  79.1 5.5 collective-permute-done.5.refs_6_
  89.3 10.3 %collective-permute-done.6.refs_7_ = bf16[256,1024]{1,0:T(8,128)(2,1)S(1)} collective-permute-done((bf16[256,1024]{1,0:T(8,128)(2,1)}, bf16[256,1024]{1,0:T(8,128)(2,1)S(1)}, u32[]{:S(2)}, u32[]{:S(2)}) %collective-permute-start.6) | collective-permute-done | bytes 524320 | tf_op jit(solution)/shard_map/ppermute | solution.py:88
  100.5 5.2 collective-permute-done.12.refs_8_
  111.0 22.3 %collective-permute-done.2.refs_3_ = bf16[256,1024]{1,0:T(8,128)(2,1)S(1)} collective-permute-done((bf16[256,1024]{1,0:T(8,128)(2,1)}, bf16[256,1024]{1,0:T(8,128)(2,1)S(1)}, u32[]{:S(2)}, u32[]{:S(2)}) %collective-permute-start.2) | collective-permute-done | bytes 524320 | tf_op jit(solution)/shard_map/ppermute | solution.py:88
  135.4 9.2 %collective-permute-done.13.refs_9_ = bf16[256,1024]{1,0:T(8,128)(2,1)S(1)} collective-permute-done((bf16[256,1024]{1,0:T(8,128)(2,1)S(1)}, bf16[256,1024]{1,0:T(8,128)(2,1)S(1)}, u32[]{:S(2)}, u32[]{:S(2)}) %collective-permute-start.13) | collective-permute-done | bytes 524320 | tf_op jit(solution)/shard_map/ppermute | solution.py:88
  146.9 11.0 %qk_project.1 = (f32[1024,512]{1,0:T(8,128)}, f32[1024,512]{1,0:T(8,128)}, f32[16,1024]{1,0:T(8,128)}, bf16[2048,1024]{1,0:T(8,128)(2,1)}) custom-call(s32[12]{0:T(128)} %pad_add_fusion.ids.refs_0_, bf16[1024,2048]{1,0:T(8,128)(2,1)} %all-gather.3.cloned.1.call-done.h_ref.refs_1_, bf16[256,1024]{1,0:T(8,128)(2,1)} %pad_maximum_fusion.refs_0_, ...), custom_call_target="tpu_custom_call" | custom-call | flops 85899345920 | bytes 16842752 | tf_op jit(solution)/shard_map/qk_project/pallas_call | solution.py:62
  162.4 4.8 collective-permute-done.8.refs_3_
  169.2 9.2 %collective-permute-done.9.refs_5_ = bf16[256,1024]{1,0:T(8,128)(2,1)} collective-permute-done((bf16[256,1024]{1,0:T(8,128)(2,1)S(1)}, bf16[256,1024]{1,0:T(8,128)(2,1)}, u32[]{:S(2)}, u32[]{:S(2)}) %collective-permute-start.9) | collective-permute-done | bytes 524320 | tf_op jit(solution)/shard_map/ppermute | solution.py:88
  179.9 8.4 v_project.1
  189.5 17.2 %attend.1 = (bf16[1024,512]{1,0:T(8,128)(2,1)}, bf16[1024,512]{1,0:T(8,128)(2,1)}, bf16[1024,512]{1,0:T(8,128)(2,1)}) custom-call(f32[1024,512]{1,0:T(8,128)} %get-tuple-element.115.refs_10_.qr_ref.refs_4_, f32[1024,512]{1,0:T(8,128)} %get-tuple-element.116.kr_ref.refs_5_, bf16[1024,512]{1,0:T(8,128)(2,1)} %get-tuple-element.122.v_ref, ...), custom_call_target="tpu_custom_call" | custom-call | flops 32212254720 | bytes 9510912 | tf_op jit(solution)/shard_map/attend/pallas_call | solution.py:62
  210.5 12.9 %collective-permute-done.28.refs_2_ = bf16[256,2048]{1,0:T(8,128)(2,1)} collective-permute-done((bf16[256,2048]{1,0:T(8,128)(2,1)S(1)}, bf16[256,2048]{1,0:T(8,128)(2,1)}, u32[]{:S(2)}, u32[]{:S(2)}) %collective-permute-start.28) | collective-permute-done | bytes 1048608 | tf_op jit(solution)/shard_map/ppermute | solution.py:88
  223.4 6.5 collective-permute-done.25.refs_6_.refs_4_
  238.6 8.8 out_project.1
  257.6 10.6 %collective-permute-done.34.refs_2_ = bf16[256,2048]{1,0:T(8,128)(2,1)} collective-permute-done((bf16[256,2048]{1,0:T(8,128)(2,1)}, bf16[256,2048]{1,0:T(8,128)(2,1)}, u32[]{:S(2)}, u32[]{:S(2)}) %collective-permute-start.34) | collective-permute-done | bytes 1048608 | tf_op jit(solution)/shard_map/ppermute | solution.py:88
  272.0 24.6 %collective-permute-done.36.refs_1_ = bf16[256,2048]{1,0:T(8,128)(2,1)} collective-permute-done((bf16[256,2048]{1,0:T(8,128)(2,1)}, bf16[256,2048]{1,0:T(8,128)(2,1)}, u32[]{:S(2)}, u32[]{:S(2)}) %collective-permute-start.36) | collective-permute-done | bytes 1048608 | tf_op jit(solution)/shard_map/ppermute | solution.py:88
  298.7 4.5 dispatch.10
  303.2 41.0 %collective-permute-done.30.refs_1_ = bf16[256,2048]{1,0:T(8,128)(2,1)S(1)} collective-permute-done((bf16[256,2048]{1,0:T(8,128)(2,1)S(1)}, bf16[256,2048]{1,0:T(8,128)(2,1)S(1)}, u32[]{:S(2)}, u32[]{:S(2)}) %collective-permute-start.30) | collective-permute-done | bytes 1048608 | tf_op jit(solution)/shard_map/ppermute | solution.py:88
  345.1 4.5 dispatch.11
  349.6 42.8 %experts.2 = (bf16[2,576,1024]{2,1,0:T(8,128)(2,1)}, bf16[2,576,1024]{2,1,0:T(8,128)(2,1)}, bf16[2,576,1024]{2,1,0:T(8,128)(2,1)}, f32[2,576,1]{2,1,0:T(8,128)},...) custom-call(bf16[2,576,2048]{2,1,0:T(8,128)(2,1)} %get-tuple-element.133.refs_0_, ...), custom_call_target="tpu_custom_call" | custom-call | flops 579820584960 | bytes 51127296 | tf_op jit(solution)/shard_map/experts/pallas_call | solution.py:62
  394.1 4.5 dispatch.14
  398.6 18.1 %collective-permute-done.38.refs_2_ = bf16[256,2048]{1,0:T(8,128)(2,1)S(1)} collective-permute-done((bf16[256,2048]{1,0:T(8,128)(2,1)}, bf16[256,2048]{1,0:T(8,128)(2,1)S(1)}, u32[]{:S(2)}, u32[]{:S(2)}) %collective-permute-start.38) | collective-permute-done | bytes 1048608 | tf_op jit(solution)/shard_map/ppermute | solution.py:88
  417.8 4.5 dispatch.15
  432.3 42.5 %experts.3 = (bf16[2,576,1024]{2,1,0:T(8,128)(2,1)}, bf16[2,576,1024]{2,1,0:T(8,128)(2,1)}, bf16[2,576,1024]{2,1,0:T(8,128)(2,1)}, f32[2,576,1]{2,1,0:T(8,128)},...) custom-call(bf16[2,576,2048]{2,1,0:T(8,128)(2,1)} %get-tuple-element.139.refs_3_.refs_0_.refs_1_, ...), custom_call_target="tpu_custom_call" | custom-call | flops 579820584960 | bytes 51127296 | tf_op jit(solution)/shard_map/experts/pallas_call | solution.py:62
  474.7 18.3 %weight_grad.4.refs_9_.refs_7_ = bf16[2,2048,1024]{2,1,0:T(8,128)(2,1)} custom-call(bf16[2,576,2048]{2,1,0:T(8,128)(2,1)} %get-tuple-element.133.refs_0_, bf16[2,576,2048]{2,1,0:T(8,128)(2,1)} %get-tuple-element.139.refs_3_.refs_0_.refs_1_, bf16[2,576,1024]{2,1,0:T(8,128)(2,1)} %get-tuple-element.156.refs_2_, bf16[2,576,1024]{2,1,0:T(8,128)(2,1)} %get-tuple-element.157.refs_3_), custom_call_target="tpu_custom_call" | custom-call | flops 193273528320 | bytes 22544384 | tf_op jit(solution)/shard_map/weight_grad/pallas_call | solution.py:62
  499.5 4.6 combine.11
  521.7 8.9 collective-permute-done.43
  533.6 18.7 %weight_grad.3.refs_8_ = bf16[2,1024,2048]{2,1,0:T(8,128)(2,1)} custom-call(bf16[2,576,1024]{2,1,0:T(8,128)(2,1)} %get-tuple-element.154.refs_0_, bf16[2,576,1024]{2,1,0:T(8,128)(2,1)} %get-tuple-element.155.refs_1_, bf16[2,576,2048]{2,1,0:T(8,128)(2,1)} %dispatch.9.refs_8_.refs_1_.refs_6_.refs_10_.refs_2_, ...), custom_call_target="tpu_custom_call" | custom-call | flops 193273528320 | bytes 22544384 | tf_op jit(solution)/shard_map/weight_grad/pallas_call | solution.py:62
  560.2 18.3 %weight_grad.5.refs_2_.refs_6_ = bf16[2,2048,1024]{2,1,0:T(8,128)(2,1)} custom-call(bf16[2,576,2048]{2,1,0:T(8,128)(2,1)} %get-tuple-element.133.refs_0_, bf16[2,576,2048]{2,1,0:T(8,128)(2,1)} %get-tuple-element.139.refs_3_.refs_0_.refs_1_, bf16[2,576,1024]{2,1,0:T(8,128)(2,1)} %get-tuple-element.140.refs_2_, ...), custom_call_target="tpu_custom_call" | custom-call | flops 193273528320 | bytes 22544384 | tf_op jit(solution)/shard_map/weight_grad/pallas_call | solution.py:62
  578.5 4.5 combine.15
  599.0 5.2 collective-permute-done.50
  609.2 7.7 out_back.1
  625.8 10.1 %collective-permute-done.46 = bf16[256,2048]{1,0:T(8,128)(2,1)} collective-permute-done((bf16[256,2048]{1,0:T(8,128)(2,1)}, bf16[256,2048]{1,0:T(8,128)(2,1)}, u32[]{:S(2)}, u32[]{:S(2)}) %collective-permute-start.46) | collective-permute-done | bytes 1048608 | tf_op jit(solution)/shard_map/ppermute | solution.py:88
  639.6 18.8 %collective-permute-done.47 = bf16[256,2048]{1,0:T(8,128)(2,1)} collective-permute-done((bf16[256,2048]{1,0:T(8,128)(2,1)}, bf16[256,2048]{1,0:T(8,128)(2,1)}, u32[]{:S(2)}, u32[]{:S(2)}) %collective-permute-start.47) | collective-permute-done | bytes 1048608 | tf_op jit(solution)/shard_map/ppermute | solution.py:88
  665.3 23.0 %attend_back.1 = (f32[1024,512]{1,0:T(8,128)}, f32[1024,512]{1,0:T(8,128)}, bf16[1024,512]{1,0:T(8,128)(2,1)}, f32[16,1024]{1,0:T(8,128)}, f32[1,512]{1,0:T(1,128)}, /*index=5*/f32[1,512]{1,0:T(1,128)}) custom-call(bf16[1024,512]{1,0:T(8,128)(2,1)} %get-tuple-element.165.q_ref, bf16[1024,512]{1,0:T(8,128)(2,1)} %get-tuple-element.166.k_ref, ...), custom_call_target="tpu_custom_call" | custom-call | flops 75161927680 | bytes 14823424 | tf_op jit(solution)/shard_map/attend_back/pallas_call | solution.py:62
  690.7 10.2 %vo_grads.1 = (bf16[256,1024]{1,0:T(8,128)(2,1)}, bf16[256,1024]{1,0:T(8,128)(2,1)}, bf16[256,1024]{1,0:T(8,128)(2,1)}, bf16[256,1024]{1,0:T(8,128)(2,1)}, bf16[...) custom-call(s32[12]{0:T(128)} %pad_add_fusion.ids.refs_0_, ...), custom_call_target="tpu_custom_call" | custom-call | flops 85899345920 | bytes 14680064 | tf_op jit(solution)/shard_map/vo_grads/pallas_call | solution.py:62
  711.0 12.5 %qk_back.1 = (bf16[272,1024]{1,0:T(8,128)(2,1)}, bf16[272,1024]{1,0:T(8,128)(2,1)}, bf16[272,1024]{1,0:T(8,128)(2,1)}, bf16[272,1024]{1,0:T(8,128)(2,1)}, bf16[2...) custom-call(s32[12]{0:T(128)} %pad_add_fusion.ids.refs_0_, ...), custom_call_target="tpu_custom_call" | custom-call | flops 85899345920 | bytes 19423232 | tf_op jit(solution)/shard_map/qk_back/pallas_call | solution.py:62
  734.5 4.9 collective-permute-done.63
  744.6 13.3 %collective-permute-done.53 = bf16[256,2048]{1,0:T(8,128)(2,1)} collective-permute-done((bf16[256,2048]{1,0:T(8,128)(2,1)}, bf16[256,2048]{1,0:T(8,128)(2,1)}, u32[]{:S(2)}, u32[]{:S(2)}) %collective-permute-start.53) | collective-permute-done | bytes 1048608 | tf_op jit(solution)/shard_map/ppermute | solution.py:88
  761.5 11.9 %d_h.1 = bf16[1024,2048]{1,0:T(8,128)(2,1)} custom-call(bf16[1024,1024]{1,0:T(8,128)(2,1)} %get-tuple-element.186.refs_0_, bf16[1024,512]{1,0:T(8,128)(2,1)} %get-tuple-element.184.dv_ref.refs_1_, bf16[2048,1024]{1,0:T(8,128)(2,1)} %get-tuple-element.187.refs_2_, bf16[2048,512]{1,0:T(8,128)(2,1)} %get-tuple-element.188.refs_3_, ...), custom_call_target="tpu_custom_call" | custom-call | flops 128849018880 | bytes 13631488 | tf_op jit(solution)/shard_map/d_h/pallas_call | solution.py:62
  777.9 6.1 collective-permute-done.60
  791.1 13.8 %collective-permute-done.74 = bf16[256,1024]{1,0:T(8,128)(2,1)S(1)} collective-permute-done((bf16[256,1024]{1,0:T(8,128)(2,1)S(1)}, bf16[256,1024]{1,0:T(8,128)(2,1)S(1)}, u32[]{:S(2)}, u32[]{:S(2)}) %collective-permute-start.74) | collective-permute-done | bytes 524320 | tf_op jit(solution)/shard_map/ppermute | solution.py:88
  806.2 4.9 collective-permute-done.59
  818.1 13.3 %collective-permute-done.65 = bf16[272,1024]{1,0:T(8,128)(2,1)S(1)} collective-permute-done((bf16[272,1024]{1,0:T(8,128)(2,1)S(1)}, bf16[272,1024]{1,0:T(8,128)(2,1)S(1)}, u32[]{:S(2)}, u32[]{:S(2)}) %collective-permute-start.65) | collective-permute-done | bytes 557088 | tf_op jit(solution)/shard_map/ppermute | solution.py:88
  837.9 10.4 %collective-permute-done.75 = bf16[256,1024]{1,0:T(8,128)(2,1)S(1)} collective-permute-done((bf16[256,1024]{1,0:T(8,128)(2,1)S(1)}, bf16[256,1024]{1,0:T(8,128)(2,1)S(1)}, u32[]{:S(2)}, u32[]{:S(2)}) %collective-permute-start.75) | collective-permute-done | bytes 524320 | tf_op jit(solution)/shard_map/ppermute | solution.py:88
  853.8 13.3 %collective-permute-done.77.refs_11_ = bf16[256,1024]{1,0:T(8,128)(2,1)} collective-permute-done((bf16[256,1024]{1,0:T(8,128)(2,1)}, bf16[256,1024]{1,0:T(8,128)(2,1)}, u32[]{:S(2)}, u32[]{:S(2)}) %collective-permute-start.77) | collective-permute-done | bytes 524320 | tf_op jit(solution)/shard_map/ppermute | solution.py:92
  870.3 4.6 fusion.6.refs_16_
  887.2 8.7 finish.1
  (434 shorter events, 257.7 us)
Async XLA Ops:
  7.2 139.7 %all-gather.3.cloned.1.call-start = ((), (), s32[]{:S(2)}) async-start(), calls=%async_computation.7 | async-start | bytes 5242880 | tf_op jit(solution)/shard_map/all_gather | solution.py:752
  14.2 73.0 %collective-permute-start.1 = (bf16[256,1024]{1,0:T(8,128)(2,1)}, bf16[256,1024]{1,0:T(8,128)(2,1)}, u32[]{:S(2)}, u32[]{:S(2)}) collective-permute-start(bf16[256,1024]{1,0:T(8,128)(2,1)} %pad_maximum_fusion.refs_0_), channel_id=1, source_target_pairs={{0,2},{1,3},{2,0},{3,1},{4,6},{5,7},{6,4},{7,5},{8,10},{9,11},{10,... | collective-permute-start | bytes 1572872 | tf_op jit(solution)/shard_map/ppermute | solution.py:88
  43.1 45.1 %collective-permute-start.7 = (bf16[256,1024]{1,0:T(8,128)(2,1)}, bf16[256,1024]{1,0:T(8,128)(2,1)S(1)}, u32[]{:S(2)}, u32[]{:S(2)}) collective-permute-start(bf16[256,1024]{1,0:T(8,128)(2,1)} %pad_maximum_fusion.1.refs_2_), channel_id=1, source_target_pairs={{0,2},{1,3},{2,0},{3,1},{4,6},{5,7},{6,4},{7,5},{8,10},{9,11},{10,... | collective-permute-start | bytes 1572872 | tf_op jit(solution)/shard_map/ppermute | solution.py:88
  43.5 41.9 %collective-permute-start.10 = (bf16[256,1024]{1,0:T(8,128)(2,1)}, bf16[256,1024]{1,0:T(8,128)(2,1)}, u32[]{:S(2)}, u32[]{:S(2)}) collective-permute-start(bf16[256,1024]{1,0:T(8,128)(2,1)} %pad_maximum_fusion.1.refs_2_), channel_id=1, source_target_pairs={{0,4},{1,5},{2,6},{3,7},{4,0},{5,1},{6,2},{7,3},{8,12},{9,13},{10,... | collective-permute-start | bytes 1572872 | tf_op jit(solution)/shard_map/ppermute | solution.py:88
  86.8 58.6 %collective-permute-start.32 = (bf16[256,2048]{1,0:T(8,128)(2,1)S(1)}, bf16[256,2048]{1,0:T(8,128)(2,1)S(1)}, u32[]{:S(2)}, u32[]{:S(2)}) collective-permute-start(bf16[256,2048]{1,0:T(8,128)(2,1)S(1)} %bitcast.144), channel_id=1, source_target_pairs={{0,4},{1,5},{2,6},{3,7},{4,0},{5,1},{6,2},{7,3},{8,12},{9,13},{10,... | collective-permute-start | bytes 3145736 | tf_op jit(solution)/shard_map/ppermute | solution.py:88
  88.2 46.0 %collective-permute-start.4 = (bf16[256,1024]{1,0:T(8,128)(2,1)}, bf16[256,1024]{1,0:T(8,128)(2,1)S(1)}, u32[]{:S(2)}, u32[]{:S(2)}) collective-permute-start(bf16[256,1024]{1,0:T(8,128)(2,1)} %collective-permute-done.3.refs_4_), channel_id=1, source_target_pairs={{0,1},{1,0},{2,3},{3,2},{4,5},{5,4},{6,7},{7,6},{8,9},{9,8},{10,11... | collective-permute-start | bytes 1572872 | tf_op jit(solution)/shard_map/ppermute | solution.py:88
  99.7 33.7 %collective-permute-start.2 = (bf16[256,1024]{1,0:T(8,128)(2,1)}, bf16[256,1024]{1,0:T(8,128)(2,1)S(1)}, u32[]{:S(2)}, u32[]{:S(2)}) collective-permute-start(bf16[256,1024]{1,0:T(8,128)(2,1)} %collective-permute-done.1.refs_2_), channel_id=1, source_target_pairs={{0,1},{1,0},{2,3},{3,2},{4,5},{5,4},{6,7},{7,6},{8,9},{9,8},{10,11... | collective-permute-start | bytes 1572872 | tf_op jit(solution)/shard_map/ppermute | solution.py:88
  105.7 38.9 %collective-permute-start.13 = (bf16[256,1024]{1,0:T(8,128)(2,1)S(1)}, bf16[256,1024]{1,0:T(8,128)(2,1)S(1)}, u32[]{:S(2)}, u32[]{:S(2)}) collective-permute-start(bf16[256,1024]{1,0:T(8,128)(2,1)S(1)} %collective-permute-done.12.refs_8_), channel_id=1, source_target_pairs={{0,1},{1,0},{2,3},{3,2},{4,5},{5,4},{6,7},{7,6},{8,9},{9,8},{10,11... | collective-permute-start | bytes 1572872 | tf_op jit(solution)/shard_map/ppermute | solution.py:88
  110.9 47.0 %collective-permute-start.14 = (bf16[256,2048]{1,0:T(8,128)(2,1)S(1)}, bf16[256,2048]{1,0:T(8,128)(2,1)}, u32[]{:S(2)}, u32[]{:S(2)}) collective-permute-start(bf16[256,2048]{1,0:T(8,128)(2,1)S(1)} %bitcast.145), channel_id=1, source_target_pairs={{0,2},{1,3},{2,0},{3,1},{4,6},{5,7},{6,4},{7,5},{8,10},{9,11},{10,... | collective-permute-start | bytes 3145736 | tf_op jit(solution)/shard_map/ppermute | solution.py:88
  144.6 33.8 %collective-permute-start.9 = (bf16[256,1024]{1,0:T(8,128)(2,1)S(1)}, bf16[256,1024]{1,0:T(8,128)(2,1)}, u32[]{:S(2)}, u32[]{:S(2)}) collective-permute-start(bf16[256,1024]{1,0:T(8,128)(2,1)S(1)} %collective-permute-done.7.refs_4_), channel_id=1, source_target_pairs={{0,1},{1,0},{2,3},{3,2},{4,5},{5,4},{6,7},{7,6},{8,9},{9,8},{10,11... | collective-permute-start | bytes 1572872 | tf_op jit(solution)/shard_map/ppermute | solution.py:88
  159.4 74.2 %collective-permute-start.27 = (bf16[256,2048]{1,0:T(8,128)(2,1)}, bf16[256,2048]{1,0:T(8,128)(2,1)}, u32[]{:S(2)}, u32[]{:S(2)}) collective-permute-start(bf16[256,2048]{1,0:T(8,128)(2,1)} %collective-permute-done.14.refs_1_), channel_id=1, source_target_pairs={{0,1},{1,0},{2,3},{3,2},{4,5},{5,4},{6,7},{7,6},{8,9},{9,8},{10,11... | collective-permute-start | bytes 3145736 | tf_op jit(solution)/shard_map/ppermute | solution.py:88
  161.0 62.3 %collective-permute-start.28 = (bf16[256,2048]{1,0:T(8,128)(2,1)S(1)}, bf16[256,2048]{1,0:T(8,128)(2,1)}, u32[]{:S(2)}, u32[]{:S(2)}) collective-permute-start(bf16[256,2048]{1,0:T(8,128)(2,1)S(1)} %bitcast.146), channel_id=1, source_target_pairs={{0,1},{1,0},{2,3},{3,2},{4,5},{5,4},{6,7},{7,6},{8,9},{9,8},{10,11... | collective-permute-start | bytes 3145736 | tf_op jit(solution)/shard_map/ppermute | solution.py:88
  167.2 86.7 %collective-permute-start.35 = (bf16[256,2048]{1,0:T(8,128)(2,1)S(1)}, bf16[256,2048]{1,0:T(8,128)(2,1)}, u32[]{:S(2)}, u32[]{:S(2)}) collective-permute-start(bf16[256,2048]{1,0:T(8,128)(2,1)S(1)} %collective-permute-done.32.refs_1_), channel_id=1, source_target_pairs={{0,1},{1,0},{2,3},{3,2},{4,5},{5,4},{6,7},{7,6},{8,9},{9,8},{10,11... | collective-permute-start | bytes 3145736 | tf_op jit(solution)/shard_map/ppermute | solution.py:88
  168.4 99.9 %collective-permute-start.34 = (bf16[256,2048]{1,0:T(8,128)(2,1)}, bf16[256,2048]{1,0:T(8,128)(2,1)}, u32[]{:S(2)}, u32[]{:S(2)}) collective-permute-start(bf16[256,2048]{1,0:T(8,128)(2,1)} %collective-permute-done.33.refs_1_), channel_id=1, source_target_pairs={{0,1},{1,0},{2,3},{3,2},{4,5},{5,4},{6,7},{7,6},{8,9},{9,8},{10,11... | collective-permute-start | bytes 3145736 | tf_op jit(solution)/shard_map/ppermute | solution.py:88
  188.3 41.5 %collective-permute-start.25 = (bf16[2048,512]{1,0:T(8,128)(2,1)}, bf16[2048,512]{1,0:T(8,128)(2,1)}, u32[]{:S(2)}, u32[]{:S(2)}) collective-permute-start(bf16[2048,512]{1,0:T(8,128)(2,1)} %get-tuple-element.126.refs_4_.refs_2_), channel_id=1, source_target_pairs={{0,16},{8,24},{16,0},{24,8},{1,17},{9,25},{17,1},{25,9},{2,18},{10... | collective-permute-start | bytes 6291464 | tf_op jit(solution)/shard_map/ppermute | solution.py:92
  210.2 479.4 %all-gather.5.cloned.1.call-start = ((), (), s32[]{:S(2)}) async-start(), calls=%async_computation.8 | async-start | bytes 5242880 | tf_op jit(solution)/shard_map/all_gather | solution.py:838
  238.6 636.3 %reduce-scatter.6.cloned.1.call-start = ((), (), s32[]{:S(2)}) async-start(), calls=%async_computation.10 | async-start | bytes 10485760 | tf_op jit(solution)/shard_map/reduce_scatter | solution.py:891
  247.4 49.2 %collective-permute-start.36 = (bf16[256,2048]{1,0:T(8,128)(2,1)}, bf16[256,2048]{1,0:T(8,128)(2,1)}, u32[]{:S(2)}, u32[]{:S(2)}) collective-permute-start(bf16[256,2048]{1,0:T(8,128)(2,1)} %get-tuple-element.130.refs_0_), channel_id=1, source_target_pairs={{0,4},{1,5},{2,6},{3,7},{4,0},{5,1},{6,2},{7,3},{8,12},{9,13},{10,... | collective-permute-start | bytes 3145736 | tf_op jit(solution)/shard_map/ppermute | solution.py:88
  250.0 48.1 %collective-permute-start.29 = (bf16[256,2048]{1,0:T(8,128)(2,1)}, bf16[256,2048]{1,0:T(8,128)(2,1)S(1)}, u32[]{:S(2)}, u32[]{:S(2)}) collective-permute-start(bf16[256,2048]{1,0:T(8,128)(2,1)} %get-tuple-element.130.refs_0_), channel_id=1, source_target_pairs={{0,2},{1,3},{2,0},{3,1},{4,6},{5,7},{6,4},{7,5},{8,10},{9,11},{10,... | collective-permute-start | bytes 3145736 | tf_op jit(solution)/shard_map/ppermute | solution.py:88
  250.2 48.6 %collective-permute-start.31 = (bf16[256,2048]{1,0:T(8,128)(2,1)}, bf16[256,2048]{1,0:T(8,128)(2,1)}, u32[]{:S(2)}, u32[]{:S(2)}) collective-permute-start(bf16[256,2048]{1,0:T(8,128)(2,1)} %get-tuple-element.130.refs_0_), channel_id=1, source_target_pairs={{0,1},{1,0},{2,3},{3,2},{4,5},{5,4},{6,7},{7,6},{8,9},{9,8},{10,11... | collective-permute-start | bytes 3145736 | tf_op jit(solution)/shard_map/ppermute | solution.py:88
  296.7 95.7 %collective-permute-start.37 = (bf16[256,2048]{1,0:T(8,128)(2,1)}, bf16[256,2048]{1,0:T(8,128)(2,1)}, u32[]{:S(2)}, u32[]{:S(2)}) collective-permute-start(bf16[256,2048]{1,0:T(8,128)(2,1)} %collective-permute-done.36.refs_1_), channel_id=1, source_target_pairs={{0,2},{1,3},{2,0},{3,1},{4,6},{5,7},{6,4},{7,5},{8,10},{9,11},{10,... | collective-permute-start | bytes 3145736 | tf_op jit(solution)/shard_map/ppermute | solution.py:88
  296.7 97.4 %collective-permute-start.39 = (bf16[256,2048]{1,0:T(8,128)(2,1)}, bf16[256,2048]{1,0:T(8,128)(2,1)}, u32[]{:S(2)}, u32[]{:S(2)}) collective-permute-start(bf16[256,2048]{1,0:T(8,128)(2,1)} %collective-permute-done.36.refs_1_), channel_id=1, source_target_pairs={{0,1},{1,0},{2,3},{3,2},{4,5},{5,4},{6,7},{7,6},{8,9},{9,8},{10,11... | collective-permute-start | bytes 3145736 | tf_op jit(solution)/shard_map/ppermute | solution.py:88
  298.1 46.0 %collective-permute-start.30 = (bf16[256,2048]{1,0:T(8,128)(2,1)S(1)}, bf16[256,2048]{1,0:T(8,128)(2,1)S(1)}, u32[]{:S(2)}, u32[]{:S(2)}) collective-permute-start(bf16[256,2048]{1,0:T(8,128)(2,1)S(1)} %collective-permute-done.29.refs_0_), channel_id=1, source_target_pairs={{0,1},{1,0},{2,3},{3,2},{4,5},{5,4},{6,7},{7,6},{8,9},{9,8},{10,11... | collective-permute-start | bytes 3145736 | tf_op jit(solution)/shard_map/ppermute | solution.py:88
  430.3 62.8 %collective-permute-start.40 = (bf16[256,2048]{1,0:T(8,128)(2,1)}, bf16[256,2048]{1,0:T(8,128)(2,1)}, u32[]{:S(2)}, u32[]{:S(2)}) collective-permute-start(bf16[256,2048]{1,0:T(8,128)(2,1)} %get-tuple-element.144.refs_7_.refs_5_), channel_id=1, source_target_pairs={{0,1},{1,0},{2,3},{3,2},{4,5},{5,4},{6,7},{7,6},{8,9},{9,8},{10,11... | collective-permute-start | bytes 3145736 | tf_op jit(solution)/shard_map/ppermute | solution.py:88
  432.0 64.8 %collective-permute-start.41 = (bf16[256,2048]{1,0:T(8,128)(2,1)}, bf16[256,2048]{1,0:T(8,128)(2,1)}, u32[]{:S(2)}, u32[]{:S(2)}) collective-permute-start(bf16[256,2048]{1,0:T(8,128)(2,1)} %get-tuple-element.146.refs_9_.refs_7_), channel_id=1, source_target_pairs={{0,1},{1,0},{2,3},{3,2},{4,5},{5,4},{6,7},{7,6},{8,9},{9,8},{10,11... | collective-permute-start | bytes 3145736 | tf_op jit(solution)/shard_map/ppermute | solution.py:88
  510.0 87.9 %collective-permute-start.49 = (bf16[256,2048]{1,0:T(8,128)(2,1)}, bf16[256,2048]{1,0:T(8,128)(2,1)}, u32[]{:S(2)}, u32[]{:S(2)}) collective-permute-start(bf16[256,2048]{1,0:T(8,128)(2,1)} %add_convert_fusion.9.refs_4_.refs_5_), channel_id=1, source_target_pairs={{0,2},{1,3},{2,0},{3,1},{4,6},{5,7},{6,4},{7,5},{8,10},{9,11},{10,... | collective-permute-start | bytes 3145736 | tf_op jit(solution)/shard_map/ppermute | solution.py:88
  511.4 43.0 %collective-permute-start.42 = (bf16[256,2048]{1,0:T(8,128)(2,1)}, bf16[256,2048]{1,0:T(8,128)(2,1)}, u32[]{:S(2)}, u32[]{:S(2)}) collective-permute-start(bf16[256,2048]{1,0:T(8,128)(2,1)} %get-tuple-element.151.refs_9_), channel_id=1, source_target_pairs={{0,1},{1,0},{2,3},{3,2},{4,5},{5,4},{6,7},{7,6},{8,9},{9,8},{10,11... | collective-permute-start | bytes 3145736 | tf_op jit(solution)/shard_map/ppermute | solution.py:88
  517.7 34.6 %all-to-all-start.1 = ((f32[8,2,256]{2,1,0:T(2,128)}), f32[8,2,256]{2,1,0:T(2,128)}, u32[]{:S(2)}, u32[]{:S(2)}) async-start(f32[8,2,256]{2,1,0:T(2,128)} %constant_dynamic-update-slice_fusion.16), calls=%async_computation.1 | async-start | bytes 32768 | tf_op jit(solution)/shard_map/all_to_all | solution.py:894
  521.7 357.3 %reduce-scatter.4.cloned.1.call-start = ((), (), s32[]{:S(2)}) async-start(), calls=%async_computation.9 | async-start | bytes 10485760 | tf_op jit(solution)/shard_map/reduce_scatter | solution.py:891
  559.0 45.2 %collective-permute-start.50 = (bf16[256,2048]{1,0:T(8,128)(2,1)}, bf16[256,2048]{1,0:T(8,128)(2,1)}, u32[]{:S(2)}, u32[]{:S(2)}) collective-permute-start(bf16[256,2048]{1,0:T(8,128)(2,1)} %get-tuple-element.213.refs_3_), channel_id=1, source_target_pairs={{0,4},{1,5},{2,6},{3,7},{4,0},{5,1},{6,2},{7,3},{8,12},{9,13},{10,... | collective-permute-start | bytes 3145736 | tf_op jit(solution)/shard_map/ppermute | solution.py:88
  587.0 36.2 %collective-permute-start.48 = (bf16[256,2048]{1,0:T(8,128)(2,1)}, bf16[256,2048]{1,0:T(8,128)(2,1)}, u32[]{:S(2)}, u32[]{:S(2)}) collective-permute-start(bf16[256,2048]{1,0:T(8,128)(2,1)} %get-tuple-element.168.refs_16_), channel_id=1, source_target_pairs={{0,1},{1,0},{2,3},{3,2},{4,5},{5,4},{6,7},{7,6},{8,9},{9,8},{10,11... | collective-permute-start | bytes 3145736 | tf_op jit(solution)/shard_map/ppermute | solution.py:88
  591.7 44.1 %collective-permute-start.46 = (bf16[256,2048]{1,0:T(8,128)(2,1)}, bf16[256,2048]{1,0:T(8,128)(2,1)}, u32[]{:S(2)}, u32[]{:S(2)}) collective-permute-start(bf16[256,2048]{1,0:T(8,128)(2,1)} %get-tuple-element.162.refs_14_), channel_id=1, source_target_pairs={{0,1},{1,0},{2,3},{3,2},{4,5},{5,4},{6,7},{7,6},{8,9},{9,8},{10,11... | collective-permute-start | bytes 3145736 | tf_op jit(solution)/shard_map/ppermute | solution.py:88
  593.0 65.3 %collective-permute-start.47 = (bf16[256,2048]{1,0:T(8,128)(2,1)}, bf16[256,2048]{1,0:T(8,128)(2,1)}, u32[]{:S(2)}, u32[]{:S(2)}) collective-permute-start(bf16[256,2048]{1,0:T(8,128)(2,1)} %get-tuple-element.164.refs_12_), channel_id=1, source_target_pairs={{0,1},{1,0},{2,3},{3,2},{4,5},{5,4},{6,7},{7,6},{8,9},{9,8},{10,11... | collective-permute-start | bytes 3145736 | tf_op jit(solution)/shard_map/ppermute | solution.py:88
  597.9 144.6 %collective-permute-start.45 = (bf16[256,2048]{1,0:T(8,128)(2,1)}, bf16[256,2048]{1,0:T(8,128)(2,1)}, u32[]{:S(2)}, u32[]{:S(2)}) collective-permute-start(bf16[256,2048]{1,0:T(8,128)(2,1)} %get-tuple-element.159.refs_10_), channel_id=1, source_target_pairs={{0,1},{1,0},{2,3},{3,2},{4,5},{5,4},{6,7},{7,6},{8,9},{9,8},{10,11... | collective-permute-start | bytes 3145736 | tf_op jit(solution)/shard_map/ppermute | solution.py:88
  619.4 41.6 %all-to-all-start.2 = ((bf16[256,4,512]{2,0,1:T(8,128)(2,1)}), bf16[256,4,512]{2,0,1:T(8,128)(2,1)S(1)}, u32[]{:S(2)}, u32[]{:S(2)}) async-start(bf16[256,4,512]{2,0,1:T(8,128)(2,1)} %bitcast.136), calls=%async_computation.2 | async-start | bytes 2097152 | tf_op jit(solution)/shard_map/all_to_all | solution.py:924
  664.5 218.6 %reduce-scatter.8.cloned.1.call-start = ((), (), s32[]{:S(2)}) async-start(), calls=%async_computation.11 | async-start | bytes 10485760 | tf_op jit(solution)/shard_map/reduce_scatter | solution.py:891
  664.5 42.3 %collective-permute-start.52 = (bf16[256,2048]{1,0:T(8,128)(2,1)}, bf16[256,2048]{1,0:T(8,128)(2,1)}, u32[]{:S(2)}, u32[]{:S(2)}) collective-permute-start(bf16[256,2048]{1,0:T(8,128)(2,1)} %add_convert_fusion.2), channel_id=1, source_target_pairs={{0,2},{1,3},{2,0},{3,1},{4,6},{5,7},{6,4},{7,5},{8,10},{9,11},{10,... | collective-permute-start | bytes 3145736 | tf_op jit(solution)/shard_map/ppermute | solution.py:88
  688.2 54.9 %collective-permute-start.51 = (bf16[256,2048]{1,0:T(8,128)(2,1)}, bf16[256,2048]{1,0:T(8,128)(2,1)}, u32[]{:S(2)}, u32[]{:S(2)}) collective-permute-start(bf16[256,2048]{1,0:T(8,128)(2,1)} %add_convert_fusion.3), channel_id=1, source_target_pairs={{0,2},{1,3},{2,0},{3,1},{4,6},{5,7},{6,4},{7,5},{8,10},{9,11},{10,... | collective-permute-start | bytes 3145736 | tf_op jit(solution)/shard_map/ppermute | solution.py:88
  709.4 48.4 %collective-permute-start.53 = (bf16[256,2048]{1,0:T(8,128)(2,1)}, bf16[256,2048]{1,0:T(8,128)(2,1)}, u32[]{:S(2)}, u32[]{:S(2)}) collective-permute-start(bf16[256,2048]{1,0:T(8,128)(2,1)} %add_convert_fusion.1), channel_id=1, source_target_pairs={{0,4},{1,5},{2,6},{3,7},{4,0},{5,1},{6,2},{7,3},{8,12},{9,13},{10,... | collective-permute-start | bytes 3145736 | tf_op jit(solution)/shard_map/ppermute | solution.py:88
  731.4 59.3 %collective-permute-start.72 = (bf16[256,1024]{1,0:T(8,128)(2,1)}, bf16[256,1024]{1,0:T(8,128)(2,1)}, u32[]{:S(2)}, u32[]{:S(2)}) collective-permute-start(bf16[256,1024]{1,0:T(8,128)(2,1)} %get-tuple-element.202), channel_id=1, source_target_pairs={{0,1},{1,0},{2,3},{3,2},{4,5},{5,4},{6,7},{7,6},{8,9},{9,8},{10,11... | collective-permute-start | bytes 1572872 | tf_op jit(solution)/shard_map/ppermute | solution.py:88
  739.4 37.1 %collective-permute-start.70 = (bf16[256,1024]{1,0:T(8,128)(2,1)}, bf16[256,1024]{1,0:T(8,128)(2,1)}, u32[]{:S(2)}, u32[]{:S(2)}) collective-permute-start(bf16[256,1024]{1,0:T(8,128)(2,1)} %get-tuple-element.200), channel_id=1, source_target_pairs={{0,1},{1,0},{2,3},{3,2},{4,5},{5,4},{6,7},{7,6},{8,9},{9,8},{10,11... | collective-permute-start | bytes 1572872 | tf_op jit(solution)/shard_map/ppermute | solution.py:88
  742.5 44.5 %collective-permute-start.62 = (bf16[272,1024]{1,0:T(8,128)(2,1)}, bf16[272,1024]{1,0:T(8,128)(2,1)}, u32[]{:S(2)}, u32[]{:S(2)}) collective-permute-start(bf16[272,1024]{1,0:T(8,128)(2,1)} %get-tuple-element.194), channel_id=1, source_target_pairs={{0,1},{1,0},{2,3},{3,2},{4,5},{5,4},{6,7},{7,6},{8,9},{9,8},{10,11... | collective-permute-start | bytes 1671176 | tf_op jit(solution)/shard_map/ppermute | solution.py:88
  743.2 40.9 %collective-permute-start.60 = (bf16[272,1024]{1,0:T(8,128)(2,1)}, bf16[272,1024]{1,0:T(8,128)(2,1)}, u32[]{:S(2)}, u32[]{:S(2)}) collective-permute-start(bf16[272,1024]{1,0:T(8,128)(2,1)} %get-tuple-element.192), channel_id=1, source_target_pairs={{0,1},{1,0},{2,3},{3,2},{4,5},{5,4},{6,7},{7,6},{8,9},{9,8},{10,11... | collective-permute-start | bytes 1671176 | tf_op jit(solution)/shard_map/ppermute | solution.py:88
  776.5 34.8 %collective-permute-start.57 = (bf16[256,2048]{1,0:T(8,128)(2,1)S(1)}, bf16[256,2048]{1,0:T(8,128)(2,1)S(1)}, u32[]{:S(2)}, u32[]{:S(2)}) collective-permute-start(bf16[256,2048]{1,0:T(8,128)(2,1)S(1)} %get-tuple-element.216), channel_id=1, source_target_pairs={{0,8},{8,0},{16,24},{24,16},{1,9},{9,1},{17,25},{25,17},{2,10},{10... | collective-permute-start | bytes 3145736 | tf_op jit(solution)/shard_map/ppermute | solution.py:92
  787.0 47.5 %collective-permute-start.69 = (bf16[256,1024]{1,0:T(8,128)(2,1)S(1)}, bf16[256,1024]{1,0:T(8,128)(2,1)S(1)}, u32[]{:S(2)}, u32[]{:S(2)}) collective-permute-start(bf16[256,1024]{1,0:T(8,128)(2,1)S(1)} %copy-done.66), channel_id=1, source_target_pairs={{0,1},{1,0},{2,3},{3,2},{4,5},{5,4},{6,7},{7,6},{8,9},{9,8},{10,11... | collective-permute-start | bytes 1572872 | tf_op jit(solution)/shard_map/ppermute | solution.py:88
  811.3 37.0 %collective-permute-start.75 = (bf16[256,1024]{1,0:T(8,128)(2,1)S(1)}, bf16[256,1024]{1,0:T(8,128)(2,1)S(1)}, u32[]{:S(2)}, u32[]{:S(2)}) collective-permute-start(bf16[256,1024]{1,0:T(8,128)(2,1)S(1)} %add_convert_fusion.18), channel_id=1, source_target_pairs={{0,4},{1,5},{2,6},{3,7},{4,0},{5,1},{6,2},{7,3},{8,12},{9,13},{10,... | collective-permute-start | bytes 1572872 | tf_op jit(solution)/shard_map/ppermute | solution.py:88
  818.1 49.6 %collective-permute-start.56 = (bf16[256,2048]{1,0:T(8,128)(2,1)}, bf16[256,2048]{1,0:T(8,128)(2,1)}, u32[]{:S(2)}, u32[]{:S(2)}) collective-permute-start(bf16[256,2048]{1,0:T(8,128)(2,1)} %get-tuple-element.215), channel_id=1, source_target_pairs={{0,8},{8,0},{16,24},{24,16},{1,9},{9,1},{17,25},{25,17},{2,10},{10... | collective-permute-start | bytes 3145736 | tf_op jit(solution)/shard_map/ppermute | solution.py:92
  831.3 36.4 %collective-permute-start.58 = (bf16[256,2048]{1,0:T(8,128)(2,1)}, bf16[256,2048]{1,0:T(8,128)(2,1)}, u32[]{:S(2)}, u32[]{:S(2)}) collective-permute-start(bf16[256,2048]{1,0:T(8,128)(2,1)} %fusion.8), channel_id=1, source_target_pairs={{0,16},{8,24},{16,0},{24,8},{1,17},{9,25},{17,1},{25,9},{2,18},{10... | collective-permute-start | bytes 3145736 | tf_op jit(solution)/shard_map/ppermute | solution.py:92
  (117 other events, 1857.8 us)
Sparse Core Ops, SparseCore 0:
  12.0 37.1 all-gather.2
  238.7 33.8 all-gather.4
  493.1 70.2 reduce-scatter.5
  566.0 81.8 reduce-scatter.3
  731.5 70.4 reduce-scatter.7

commit v4 on v3

--- a/solution.py
+++ b/solution.py
@@ -115,7 +115,12 @@
 
 
 def gather(value, n_ep):
-    return across_x(along_z(value)) if n_ep == 8 else gather_whole(value)
+    if n_ep != 8:
+        return gather_whole(value)
+    blocks = along_z(value)
+    near = across_x(blocks[:2])
+    near[3], blocks[2], blocks[3] = tie(near[3], blocks[2], blocks[3])
+    return near + across_x(blocks[2:])
 
 
 def plus(left, right):
@@ -128,14 +133,14 @@
 
 def scatter_z(own, near, far, farther):
     far = plus(far, swap(farther, 2))
-    return own.astype(F32) + swap(near, 2).astype(F32) + swap(far, 4).astype(F32), far
+    return own.astype(F32) + swap(near, 2).astype(F32) + swap(far, 4).astype(F32)
 
 
 def scatter(pieces, n_ep):
     if n_ep != 8:
         stacked = jnp.stack(pieces)
         return lax.psum_scatter(stacked, "ep", scatter_dimension=0, tiled=False).astype(F32)
-    return scatter_z(*crossed_sums(pieces))[0]
+    return scatter_z(*crossed_sums(pieces))
 
 
 def gather_sp(value):
@@ -154,8 +159,8 @@
     return pl.ds(pl.multiple_of(ids[position] * size, size), size)
 
 
-def qk_kernel(count, ids, h_ref, *refs):
-    pieces, (q_ref, k_ref, squares_ref, w_ref) = refs[:count], refs[count:]
+def qk_kernel(count, ids, x_ref, gain_ref, *refs):
+    pieces, (q_ref, k_ref, squares_ref, w_ref, h_ref) = refs[:count], refs[count:]
     shard = pieces[0].shape[0]
 
     @pl.when(pl.program_id(0) == 0)
@@ -163,6 +168,9 @@
         for k in range(count):
             w_ref[block_at(ids, k, shard), :] = pieces[k][...]
 
+    x_rows = x_ref[...].astype(F32)
+    scale = lax.rsqrt(jnp.mean(x_rows * x_rows, axis=1, keepdims=True) + EPS)
+    h_ref[...] = (x_rows * scale * gain_ref[...]).astype(BF16)
     width = q_ref.shape[1]
     for at, ref in enumerate((q_ref, k_ref)):
         part = product(h_ref[...], w_ref[:, at * width : (at + 1) * width])
@@ -170,22 +178,24 @@
         squares_ref[8 * at : 8 * at + 8, :] = row_sums(part * part)
 
 
-def qk_project(ids, h_all, pieces):
-    total, depth = h_all.shape
+def qk_project(ids, x_all, gain, pieces):
+    total, depth = x_all.shape
     shard, both = pieces[0].shape
     width = both // 2
     rows = min(256, total)
     block = pl.BlockSpec((rows, width), lambda i, ids: (i, 0))
+    wide = pl.BlockSpec((rows, depth), lambda i, ids: (i, 0))
     return call(
         functools.partial(qk_kernel, len(pieces)),
-        [like((total, width), F32)] * 2 + [like((16, total), F32), like((depth, both), BF16)],
-        [h_all, *pieces],
+        [like((total, width), F32)] * 2
+        + [like((16, total), F32), like((depth, both), BF16), like((total, depth), BF16)],
+        [x_all, gain, *pieces],
         2 * total * depth * both,
         "qk_project",
         scalars=(ids,),
         grid=(total // rows,),
-        in_specs=[pl.BlockSpec((rows, depth), lambda i, ids: (i, 0))] + [None] * len(pieces),
-        out_specs=[block, block, pl.BlockSpec((16, rows), lambda i, ids: (0, i)), None],
+        in_specs=[wide] + [None] * (len(pieces) + 1),
+        out_specs=[block, block, pl.BlockSpec((16, rows), lambda i, ids: (0, i)), None, wide],
     )
 
 
@@ -368,12 +378,12 @@
         for at, grad, weight in ((0, gq_ref, wq_ref), (1, gk_ref, wk_ref), (2, gv_ref, wv_ref)):
             part = firsts[j][:shard, at * width : (at + 1) * width] if at < 2 else seconds[j][:, :width]
             value = part.astype(F32)
-            grad[:, cols] = value * gain_ref[...]
+            grad[:, cols] = value
             dots += jnp.sum(value * weight[:, cols].astype(F32), axis=1, keepdims=True)
         go_ref[:, cols] = seconds[j][:, width:].astype(F32)
         tiny += firsts[j][shard:, :].astype(F32)
     tiny_ref[...] = tiny
-    attn_ref[...] = dots
+    attn_ref[...] = dots / gain_ref[...]
 
 
 def finish(ids, n_ep, w_query, w_key, w_value, gain, firsts, seconds, after):
@@ -732,43 +742,47 @@
     def own_columns(value):
         return lax.dynamic_slice_in_dim(value, sp_index * head_width, head_width, 1)
 
-    def by_block(value):
-        order = jnp.bitwise_xor(jnp.arange(n_ep, dtype=jnp.int32), ep_index) if n_ep == 8 else blocks
+    def by_piece(value):
         return jnp.stack(
-            [lax.dynamic_index_in_dim(value, order[i], 0, keepdims=False) for i in range(n_ep)]
+            [lax.dynamic_index_in_dim(value, blocks[i], 0, keepdims=False) for i in range(n_ep)]
         )
-
-    row_gain = attn_gain.astype(F32)[:, None]
-
-    def scaled(value):
-        return (own_columns(value).astype(F32) * row_gain).astype(BF16)
-
-    qk_own = jnp.concatenate([scaled(w_query), scaled(w_key)], axis=1)
-    vo_own = jnp.concatenate([scaled(w_value), own_columns(w_out)], axis=1)
-    cot_own = cotangent[0]
-    x_rows = tokens[0].astype(F32)
-    x_scale = lax.rsqrt(jnp.mean(x_rows * x_rows, axis=-1, keepdims=True) + EPS)
-    x_normed = x_rows * x_scale
-    h_all = lax.all_gather(x_normed.astype(BF16), "sp", axis=0, tiled=True)
 
     expert_ids = jnp.arange(expert_count, dtype=jnp.int32)
     picked = jnp.any(routes[0][:, :, None] == expert_ids[None, None, :], axis=1)
+    picked_low = picked.T.astype(BF16)
     small = jnp.concatenate(
         [
-            jnp.stack([q_gain, k_gain, ffn_gain]),
-            jnp.zeros((13, shard), BF16),
+            jnp.stack([attn_gain, q_gain, k_gain, ffn_gain]),
+            jnp.zeros((12, shard), BF16),
             w_router.T,
         ],
         axis=0,
     )
-    picked_low = picked.T.astype(BF16)
+
+    def to_all(value):
+        value = jnp.broadcast_to(value[None], (n_ep, *value.shape))
+        return lax.all_to_all(value, "ep", split_axis=0, concat_axis=0, tiled=True)
+
+    if shard == tok_dev:
+        both = to_all(jnp.concatenate([small, picked_low], axis=0))
+        small_all, picked_all = both[:, : 16 + expert_count], both[:, 16 + expert_count :]
+    else:
+        small_all, picked_all = to_all(small), to_all(picked_low)
+    small_rows = jnp.swapaxes(small_all, 0, 1).reshape(16 + expert_count, width)
+    gains = small_rows[:4].astype(F32)
+    full_router = small_rows[16:]
+    picked_all = by_piece(picked_all)
+
+    qk_own = jnp.concatenate([own_columns(w_query), own_columns(w_key)], axis=1)
+    vo_own = jnp.concatenate([own_columns(w_value), own_columns(w_out)], axis=1)
+    cot_own = cotangent[0]
     if n_ep == 8:
-        qk_blocks = along_z(qk_own)
-        qk_blocks[2], vo_own, small = tie(qk_blocks[2], vo_own, small)
+        own_x, near, far = swap(qk_own, 1), swap(qk_own, 2), swap(qk_own, 4)
+        own_x, near, far, vo_own = tie(own_x, near, far, vo_own)
         vo_blocks = along_z(vo_own)
+        qk_pieces = [qk_own, own_x] + across_x([near, far, swap(far, 2)])
         vo_blocks[2], cot_own = tie(vo_blocks[2], cot_own)
         cot_blocks = along_z(cot_own)
-        qk_pieces = across_x(qk_blocks)
         qk_pieces[7], vo_blocks[0], vo_blocks[1] = tie(qk_pieces[7], vo_blocks[0], vo_blocks[1])
         vo_pieces = across_x(vo_blocks)
         vo_pieces[7], cot_blocks[0], cot_blocks[1] = tie(vo_pieces[7], cot_blocks[0], cot_blocks[1])
@@ -777,15 +791,7 @@
         qk_pieces, vo_pieces, cot_pieces = (
             gather_whole(value) for value in (qk_own, vo_own, cot_own)
         )
-    if shard == tok_dev:
-        both = jnp.stack(gather(jnp.concatenate([small, picked_low], axis=0), n_ep))
-        small_all, picked_all = both[:, : 16 + expert_count], both[:, 16 + expert_count :]
-    else:
-        small_all = jnp.stack(gather(small, n_ep))
-        picked_all = jnp.stack(gather(picked_low, n_ep))
-    small_rows = jnp.swapaxes(by_block(small_all), 0, 1).reshape(16 + expert_count, width)
-    gains = small_rows[:3].astype(F32)
-    full_router = small_rows[16:]
+    x_all = lax.all_gather(tokens[0], "sp", axis=0, tiled=True)
 
     upper = (
         jnp.arange(tok_dev, dtype=jnp.int32)[:, None] < jnp.arange(tok_dev, dtype=jnp.int32)[None, :]
@@ -809,11 +815,11 @@
     sine = jnp.concatenate([-jnp.sin(angles), jnp.sin(angles)], axis=1)
     starts = starts[:, None].astype(jnp.int32)
 
-    q_raw, k_raw, squares, w_qk = qk_project(ids, h_all, qk_pieces)
+    q_raw, k_raw, squares, w_qk, h_all = qk_project(ids, x_all, gains[0:1], qk_pieces)
     scales = lax.rsqrt(sum_sp(squares) / width + EPS)
     v_low, w_v, w_o = v_project(ids, h_all, vo_pieces, [q_raw])
     w_o_parts = gather_sp(w_o)
-    gain_q, gain_k = own_columns(gains)[0:1], own_columns(gains)[1:2]
+    gain_q, gain_k = own_columns(gains)[1:2], own_columns(gains)[2:3]
     q_rot, k_rot, mixed = attend(
         q_raw, k_raw, v_low, scales, gain_q, gain_k, cosine, sine, starts
     )
@@ -833,7 +839,7 @@
     attn_tok = lax.all_to_all(mixed, "sp", split_axis=0, concat_axis=1, tiled=True)
     near_rows = cot_rows(0, [mixed])
     x_one, h2_low = out_project(
-        ids, n_ep, attn_tok, tokens[0], gains[2:3], w_o_parts, [near_rows]
+        ids, n_ep, attn_tok, tokens[0], gains[3:4], w_o_parts, [near_rows]
     )
     attn_all = lax.all_gather(attn_tok, "sp", axis=0, tiled=True)
 
@@ -878,29 +884,31 @@
     d_up_rows = [made[2] for _, _, made in groups]
     ins = [rows for rows, _, _ in groups]
     outs = [d_rows for _, d_rows, _ in groups]
-    if n_ep == 8:
-        d_h2, inside = scatter_z(*d_sums)
-        inside = [inside]
-    else:
-        d_h2, inside = scatter(d_pieces, n_ep), []
     grad_down = weight_grad(acts, outs, d_pieces)
-    grad_gate = weight_grad(ins, d_gate_rows)
-    grad_up = weight_grad(ins, d_up_rows, [*d_sums, grad_down, grad_gate])
-
-    def over_sp(value):
-        return lax.psum_scatter(value, "sp", scatter_dimension=1, tiled=True).astype(F32)
-
-    d_gates = by_block(jnp.concatenate(d_gates, axis=0).reshape(n_ep, local, tok_dev))
-    d_gates = lax.all_to_all(d_gates, "ep", split_axis=0, concat_axis=0, tiled=True)
-    d_gates = d_gates.reshape(expert_count, tok_dev)
-
+    grad_gate = weight_grad(ins, d_gate_rows, [grad_down])
     mix_pieces = []
     for g, (_, _, made) in enumerate(groups):
         for at in range(group // 2):
             mix_pieces += combine(
                 pair_places(g * group + 2 * at), made[4], 2, local, cap, at, None,
-                [grad_up, *inside],
+                [grad_gate, *d_sums],
             )
+    if n_ep == 8:
+        *d_sums, mix_pieces[1], mix_pieces[3], mix_pieces[5], mix_pieces[7] = tie(
+            *d_sums, mix_pieces[1], mix_pieces[3], mix_pieces[5], mix_pieces[7]
+        )
+        mix_sums = crossed_sums(mix_pieces)
+        d_h2 = scatter_z(*d_sums)
+    else:
+        d_h2 = scatter(d_pieces, n_ep)
+    grad_up = weight_grad(ins, d_up_rows, mix_pieces)
+
+    def over_sp(value):
+        return lax.psum_scatter(value, "sp", scatter_dimension=1, tiled=True).astype(F32)
+
+    d_gates = by_piece(jnp.concatenate(d_gates, axis=0).reshape(n_ep, local, tok_dev))
+    d_gates = lax.all_to_all(d_gates, "ep", split_axis=0, concat_axis=0, tiled=True)
+    d_gates = d_gates.reshape(expert_count, tok_dev)
 
     if n_ep == 8:
         gates_here = home_gates[:expert_count]
@@ -915,7 +923,7 @@
     one_scale = lax.rsqrt(jnp.mean(x_one * x_one, axis=-1, keepdims=True) + EPS)
     one_normed = x_one * one_scale
     grad_ffn = jnp.sum(d_h2 * one_normed, axis=0)
-    d_normed = d_h2 * gains[2][None, :]
+    d_normed = d_h2 * gains[3][None, :]
     d_one = cotangent[0].astype(F32) + one_scale * (
         d_normed - one_normed * jnp.mean(d_normed * one_normed, axis=-1, keepdims=True)
     )
@@ -924,16 +932,16 @@
     d_heads = lax.all_to_all(d_attn, "sp", split_axis=1, concat_axis=0, tiled=True)
     d_z_cols = lax.all_to_all(d_z, "sp", split_axis=1, concat_axis=0, tiled=True)
     if n_ep == 8:
-        mix_sums = crossed_sums(mix_pieces)
-        mix_sums[3], d_heads = tie(mix_sums[3], d_heads)
+        *mix_sums, d_heads = tie(*mix_sums, d_heads)
     grad_down, grad_gate, grad_up = over_sp(grad_down), over_sp(grad_gate), over_sp(grad_up)
 
     d_qn, d_kn, d_v, sums, grad_qg, grad_kg = attend_back(
         q_rot, k_rot, v_low, d_heads, q_raw, k_raw, scales, gain_q, gain_k, cosine, sine, starts
     )
     if n_ep == 8:
-        mix_sums[2], mix_sums[1], d_v = tie(mix_sums[2], mix_sums[1], d_v)
-        mix = scatter_z(*mix_sums)[0]
+        own, near, far, farther = mix_sums
+        far, d_v = tie(plus(far, swap(farther, 2)), d_v)
+        mix = own.astype(F32) + swap(near, 2).astype(F32) + swap(far, 4).astype(F32)
     else:
         mix = scatter(mix_pieces, n_ep)
     output = (x_one + mix).astype(BF16)
@@ -960,12 +968,16 @@
     kept = plus(parts[0], swap_sp(parts[1], 1))
     sent = plus(parts[2], swap_sp(parts[3], 1))
     d_h = kept.astype(F32) + swap_sp(sent, 2).astype(F32)
+    x_rows = tokens[0].astype(F32)
+    x_scale = lax.rsqrt(jnp.mean(x_rows * x_rows, axis=-1, keepdims=True) + EPS)
+    x_normed = x_rows * x_scale
+    d_normed = d_h * gains[0][None, :]
     input_grad = d_one + x_scale * (
-        d_h - x_normed * jnp.mean(d_h * x_normed, axis=-1, keepdims=True)
+        d_normed - x_normed * jnp.mean(d_normed * x_normed, axis=-1, keepdims=True)
     )
 
     g_query, g_key, g_value, g_out, tiny, g_attn = finish(
-        ids, n_ep, w_query, w_key, w_value, row_gain,
+        ids, n_ep, w_query, w_key, w_value, attn_gain.astype(F32)[:, None],
         gather_sp(grad_qk), gather_sp(grad_vo), [grad_down, grad_gate, grad_up, input_grad],
     )
     per_row = 2 * head_width // shard

time: 918 us -> 897 us (0.977)
  waiting for transfers between devices: 340 us -> 321 us
  other arithmetic: 78.7 us -> 68.3 us
    ppermute x63 -> x56, waiting for transfers between devices: 317 us -> 249 us  [swap(): return lax.ppermute(value, 'ep', [(i, i ^ bits) for i in range(8)])]
    ppermute x16, waiting for transfers between devices: 22.4 us -> 47.7 us  [swap_sp(): return lax.ppermute(value, 'sp', [(i, i ^ bits) for i in range(4)])]
    all_to_all x1, waiting for transfers between devices: 0.01 us -> 14 us  [body(): lax.all_to_all(d_gates, 'ep', split_axis=0, concat_axis=0, tiled=True)]
    convert_element_type x15 -> x17, other arithmetic: 32.7 us -> 30.9 us  [plus(): return (left.astype(F32) + right.astype(F32)).astype(left.dtype)]
    ppermute x63 -> x56, starting transfers between devices: 68.4 us -> 69.2 us  [swap(): return lax.ppermute(value, 'ep', [(i, i ^ bits) for i in range(8)])]
  transfers between devices with their start and end apart: 88 -> 82, of which waited for: 39 -> 31; matrix products, arithmetic and copies ran while one was open for 11% -> 10% of each run, Pallas kernels for 35% -> 36%
where the time goes in v4:
time: 897 us; the launch traced here: 887 us
  Pallas kernels  326 us (36%)
  waiting for transfers between devices  321 us (36%)
  starting transfers between devices  99 us (11%)
  other arithmetic  68.3 us (8%)
  between operations  38.7 us (4%)
  local copies, waits for them, and re-layouts  31.3 us (3%)
    pallas_call x31, Pallas kernels, call(): pl.pallas_call(kernel, grid_spec=pltpu.PrefetchScalarGridSpec(num_scalar_...  326 us
    ppermute x56, waiting for transfers between devices, swap(): return lax.ppermute(value, 'ep', [(i, i ^ bits) for i in range(8)])  249 us
    ppermute x56, starting transfers between devices, swap(): return lax.ppermute(value, 'ep', [(i, i ^ bits) for i in range(8)])  69.2 us
    ppermute x16, waiting for transfers between devices, swap_sp(): return lax.ppermute(value, 'sp', [(i, i ^ bits) for i in range(4)])  47.7 us
    convert_element_type x17, other arithmetic, plus(): return (left.astype(F32) + right.astype(F32)).astype(left.dtype)  30.9 us
  transfers between devices with their start and end apart: 82, of which 31 were waited for; matrix products, arithmetic and copies ran while one was open for 10% of the time, Pallas kernels for 36%

profile of v4, /device:TPU:0, one launch (start us, length us, event | category | flops | bytes accessed | tf_op | source)
XLA Modules:
  0.0 887.1 jit_solution(11892034560711221333)
XLA Ops:
  49.0 21.5 %collective-permute-done.5.refs_6_ = bf16[256,1024]{1,0:T(8,128)(2,1)} collective-permute-done((bf16[256,1024]{1,0:T(8,128)(2,1)}, bf16[256,1024]{1,0:T(8,128)(2,1)}, u32[]{:S(2)}, u32[]{:S(2)}) %collective-permute-start.5) | collective-permute-done | bytes 524320 | tf_op jit(solution)/shard_map/ppermute | solution.py:88
  76.0 28.2 %collective-permute-done.7.refs_4_ = bf16[256,1024]{1,0:T(8,128)(2,1)} collective-permute-done((bf16[256,1024]{1,0:T(8,128)(2,1)S(1)}, bf16[256,1024]{1,0:T(8,128)(2,1)}, u32[]{:S(2)}, u32[]{:S(2)}) %collective-permute-start.7) | collective-permute-done | bytes 524320 | tf_op jit(solution)/shard_map/ppermute | solution.py:88
  108.8 10.5 %collective-permute-done.3.refs_3_ = bf16[256,1024]{1,0:T(8,128)(2,1)S(1)} collective-permute-done((bf16[256,1024]{1,0:T(8,128)(2,1)}, bf16[256,1024]{1,0:T(8,128)(2,1)S(1)}, u32[]{:S(2)}, u32[]{:S(2)}) %collective-permute-start.3) | collective-permute-done | bytes 524320 | tf_op jit(solution)/shard_map/ppermute | solution.py:88
  120.9 14.9 %collective-permute-done.12.refs_8_ = bf16[256,1024]{1,0:T(8,128)(2,1)S(1)} collective-permute-done((bf16[256,1024]{1,0:T(8,128)(2,1)}, bf16[256,1024]{1,0:T(8,128)(2,1)S(1)}, u32[]{:S(2)}, u32[]{:S(2)}) %collective-permute-start.12) | collective-permute-done | bytes 524320 | tf_op jit(solution)/shard_map/ppermute | solution.py:88
  139.9 11.8 %qk_project.1 = (f32[1024,512]{1,0:T(8,128)}, f32[1024,512]{1,0:T(8,128)}, f32[16,1024]{1,0:T(8,128)}, bf16[2048,1024]{1,0:T(8,128)(2,1)}, bf16[1024,2048]{1,0:T(8,128)(2,1)}) custom-call(s32[12]{0:T(128)} %pad_add_fusion.ids.refs_0_, bf16[1024,2048]{1,0:T(8,128)(2,1)} %bitcast.169, f32[1,2048]{1,0:T(1,128)} %bitcast.151, bf16[256,1024]{1,0:T(8,128)(2,1)} %copy-done.27, ...), custom_call_target="tpu_custom_call" | custom-call | flops 85899345920 | bytes 21045248 | tf_op jit(solution)/shard_map/qk_project/pallas_call | solution.py:62
  151.7 7.7 collective-permute-done.13.refs_9_
  167.3 8.4 v_project.1
  176.9 17.2 %attend.1 = (bf16[1024,512]{1,0:T(8,128)(2,1)}, bf16[1024,512]{1,0:T(8,128)(2,1)}, bf16[1024,512]{1,0:T(8,128)(2,1)}) custom-call(f32[1024,512]{1,0:T(8,128)} %get-tuple-element.132.refs_10_.qr_ref.refs_4_, f32[1024,512]{1,0:T(8,128)} %get-tuple-element.133.kr_ref.refs_5_, bf16[1024,512]{1,0:T(8,128)(2,1)} %get-tuple-element.140.v_ref, ...), custom_call_target="tpu_custom_call" | custom-call | flops 32212254720 | bytes 9510912 | tf_op jit(solution)/shard_map/attend/pallas_call | solution.py:62
  198.6 26.0 %collective-permute-done.18.refs_6_.refs_4_ = bf16[2048,512]{1,0:T(8,128)(2,1)} collective-permute-done((bf16[2048,512]{1,0:T(8,128)(2,1)}, bf16[2048,512]{1,0:T(8,128)(2,1)}, u32[]{:S(2)}, u32[]{:S(2)}) %collective-permute-start.18) | collective-permute-done | bytes 2097184 | tf_op jit(solution)/shard_map/ppermute | solution.py:92
  234.7 8.8 out_project.1
  258.1 33.5 %collective-permute-done.22.refs_0_ = bf16[256,2048]{1,0:T(8,128)(2,1)S(1)} collective-permute-done((bf16[256,2048]{1,0:T(8,128)(2,1)}, bf16[256,2048]{1,0:T(8,128)(2,1)S(1)}, u32[]{:S(2)}, u32[]{:S(2)}) %collective-permute-start.22) | collective-permute-done | bytes 1048608 | tf_op jit(solution)/shard_map/ppermute | solution.py:88
  296.0 4.5 dispatch.10
  300.5 14.2 %collective-permute-done.23.refs_1_ = bf16[256,2048]{1,0:T(8,128)(2,1)S(1)} collective-permute-done((bf16[256,2048]{1,0:T(8,128)(2,1)S(1)}, bf16[256,2048]{1,0:T(8,128)(2,1)S(1)}, u32[]{:S(2)}, u32[]{:S(2)}) %collective-permute-start.23) | collective-permute-done | bytes 1048608 | tf_op jit(solution)/shard_map/ppermute | solution.py:88
  319.1 4.5 dispatch.11
  323.6 42.5 %experts.2 = (bf16[2,576,1024]{2,1,0:T(8,128)(2,1)}, bf16[2,576,1024]{2,1,0:T(8,128)(2,1)}, bf16[2,576,1024]{2,1,0:T(8,128)(2,1)}, f32[2,576,1]{2,1,0:T(8,128)},...) custom-call(bf16[2,576,2048]{2,1,0:T(8,128)(2,1)} %get-tuple-element.151.refs_0_, ...), custom_call_target="tpu_custom_call" | custom-call | flops 579820584960 | bytes 51127296 | tf_op jit(solution)/shard_map/experts/pallas_call | solution.py:62
  366.1 4.5 dispatch.14
  370.6 4.5 dispatch.15
  385.1 42.5 %experts.3 = (bf16[2,576,1024]{2,1,0:T(8,128)(2,1)}, bf16[2,576,1024]{2,1,0:T(8,128)(2,1)}, bf16[2,576,1024]{2,1,0:T(8,128)(2,1)}, f32[2,576,1]{2,1,0:T(8,128)},...) custom-call(bf16[2,576,2048]{2,1,0:T(8,128)(2,1)} %get-tuple-element.159.refs_3_.refs_0_.refs_1_, ...), custom_call_target="tpu_custom_call" | custom-call | flops 579820584960 | bytes 51127296 | tf_op jit(solution)/shard_map/experts/pallas_call | solution.py:62
  441.0 18.4 %weight_grad.3.refs_4_.refs_8_ = bf16[2,1024,2048]{2,1,0:T(8,128)(2,1)} custom-call(bf16[2,576,1024]{2,1,0:T(8,128)(2,1)} %get-tuple-element.168.refs_0_, bf16[2,576,1024]{2,1,0:T(8,128)(2,1)} %get-tuple-element.169.refs_1_, bf16[2,576,2048]{2,1,0:T(8,128)(2,1)} %dispatch.9.refs_8_.refs_1_.refs_6_.refs_10_.refs_2_, ...), custom_call_target="tpu_custom_call" | custom-call | flops 193273528320 | bytes 22544384 | tf_op jit(solution)/shard_map/weight_grad/pallas_call | solution.py:62
  459.4 18.3 %weight_grad.4.refs_2_.refs_7_ = bf16[2,2048,1024]{2,1,0:T(8,128)(2,1)} custom-call(bf16[2,576,2048]{2,1,0:T(8,128)(2,1)} %get-tuple-element.151.refs_0_, bf16[2,576,2048]{2,1,0:T(8,128)(2,1)} %get-tuple-element.159.refs_3_.refs_0_.refs_1_, bf16[2,576,1024]{2,1,0:T(8,128)(2,1)} %get-tuple-element.160.refs_2_, ...), custom_call_target="tpu_custom_call" | custom-call | flops 193273528320 | bytes 22544384 | tf_op jit(solution)/shard_map/weight_grad/pallas_call | solution.py:62
  484.8 4.6 all-to-all-start.2
  492.0 14.0 %all-to-all-done.2 = f32[8,2,256]{2,1,0:T(2,128)S(1)} async-done(((f32[8,2,256]{2,1,0:T(2,128)}), f32[8,2,256]{2,1,0:T(2,128)S(1)}, u32[]{:S(2)}, u32[]{:S(2)}) %all-to-all-start.2) | async-done | bytes 16416 | tf_op jit(solution)/shard_map/all_to_all | solution.py:910
  510.3 12.3 %collective-permute-done.35 = bf16[256,2048]{1,0:T(8,128)(2,1)S(1)} collective-permute-done((bf16[256,2048]{1,0:T(8,128)(2,1)}, bf16[256,2048]{1,0:T(8,128)(2,1)S(1)}, u32[]{:S(2)}, u32[]{:S(2)}) %collective-permute-start.35) | collective-permute-done | bytes 1048608 | tf_op jit(solution)/shard_map/ppermute | solution.py:88
  535.8 4.0 combine.12
  546.5 19.7 %weight_grad.5.refs_6_ = bf16[2,2048,1024]{2,1,0:T(8,128)(2,1)} custom-call(bf16[2,576,2048]{2,1,0:T(8,128)(2,1)} %get-tuple-element.151.refs_0_, bf16[2,576,2048]{2,1,0:T(8,128)(2,1)} %get-tuple-element.159.refs_3_.refs_0_.refs_1_, bf16[2,576,1024]{2,1,0:T(8,128)(2,1)} %get-tuple-element.198.refs_2_, bf16[2,576,1024]{2,1,0:T(8,128)(2,1)} %get-tuple-element.199.refs_3_, ...), custom_call_target="tpu_custom_call" | custom-call | flops 193273528320 | bytes 22544384 | tf_op jit(solution)/shard_map/weight_grad/pallas_call | solution.py:62
  571.7 19.7 %collective-permute-done.39 = bf16[256,2048]{1,0:T(8,128)(2,1)} collective-permute-done((bf16[256,2048]{1,0:T(8,128)(2,1)}, bf16[256,2048]{1,0:T(8,128)(2,1)}, u32[]{:S(2)}, u32[]{:S(2)}) %collective-permute-start.39) | collective-permute-done | bytes 1048608 | tf_op jit(solution)/shard_map/ppermute | solution.py:88
  593.0 11.2 %collective-permute-done.41 = bf16[256,2048]{1,0:T(8,128)(2,1)S(1)} collective-permute-done((bf16[256,2048]{1,0:T(8,128)(2,1)S(1)}, bf16[256,2048]{1,0:T(8,128)(2,1)S(1)}, u32[]{:S(2)}, u32[]{:S(2)}) %collective-permute-start.41) | collective-permute-done | bytes 1048608 | tf_op jit(solution)/shard_map/ppermute | solution.py:88
  604.2 5.6 collective-permute-done.43
  613.9 7.8 out_back.1
  624.0 4.4 all-to-all-start.3
  635.1 7.8 all-to-all-done.3
  642.9 4.2 all-to-all-start.4
  647.3 23.2 %attend_back.1 = (f32[1024,512]{1,0:T(8,128)}, f32[1024,512]{1,0:T(8,128)}, bf16[1024,512]{1,0:T(8,128)(2,1)}, f32[16,1024]{1,0:T(8,128)}, f32[1,512]{1,0:T(1,128)}, /*index=5*/f32[1,512]{1,0:T(1,128)}) custom-call(bf16[1024,512]{1,0:T(8,128)(2,1)} %get-tuple-element.204.q_ref, bf16[1024,512]{1,0:T(8,128)(2,1)} %get-tuple-element.205.k_ref, ...), custom_call_target="tpu_custom_call" | custom-call | flops 75161927680 | bytes 14823424 | tf_op jit(solution)/shard_map/attend_back/pallas_call | solution.py:62
  680.2 10.1 %vo_grads.1 = (bf16[256,1024]{1,0:T(8,128)(2,1)}, bf16[256,1024]{1,0:T(8,128)(2,1)}, bf16[256,1024]{1,0:T(8,128)(2,1)}, bf16[256,1024]{1,0:T(8,128)(2,1)}, bf16[...) custom-call(s32[12]{0:T(128)} %pad_add_fusion.ids.refs_0_, ...), custom_call_target="tpu_custom_call" | custom-call | flops 85899345920 | bytes 14680064 | tf_op jit(solution)/shard_map/vo_grads/pallas_call | solution.py:62
  691.1 12.5 %qk_back.1 = (bf16[272,1024]{1,0:T(8,128)(2,1)}, bf16[272,1024]{1,0:T(8,128)(2,1)}, bf16[272,1024]{1,0:T(8,128)(2,1)}, bf16[272,1024]{1,0:T(8,128)(2,1)}, bf16[2...) custom-call(s32[12]{0:T(128)} %pad_add_fusion.ids.refs_0_, ...), custom_call_target="tpu_custom_call" | custom-call | flops 85899345920 | bytes 19423232 | tf_op jit(solution)/shard_map/qk_back/pallas_call | solution.py:62
  723.3 15.5 %collective-permute-done.46 = bf16[256,2048]{1,0:T(8,128)(2,1)} collective-permute-done((bf16[256,2048]{1,0:T(8,128)(2,1)S(1)}, bf16[256,2048]{1,0:T(8,128)(2,1)}, u32[]{:S(2)}, u32[]{:S(2)}) %collective-permute-start.46) | collective-permute-done | bytes 1048608 | tf_op jit(solution)/shard_map/ppermute | solution.py:88
  741.9 12.0 %d_h.1 = bf16[1024,2048]{1,0:T(8,128)(2,1)} custom-call(bf16[1024,1024]{1,0:T(8,128)(2,1)} %get-tuple-element.216.refs_0_, bf16[1024,512]{1,0:T(8,128)(2,1)} %get-tuple-element.214.dv_ref.refs_1_, bf16[2048,1024]{1,0:T(8,128)(2,1)} %get-tuple-element.217.refs_2_, bf16[2048,512]{1,0:T(8,128)(2,1)} %get-tuple-element.218.refs_3_, ...), custom_call_target="tpu_custom_call" | custom-call | flops 128849018880 | bytes 13631488 | tf_op jit(solution)/shard_map/d_h/pallas_call | solution.py:62
  769.1 4.0 collective-permute-done.67
  776.3 11.7 %collective-permute-done.52 = bf16[272,1024]{1,0:T(8,128)(2,1)S(1)} collective-permute-done((bf16[272,1024]{1,0:T(8,128)(2,1)S(1)}, bf16[272,1024]{1,0:T(8,128)(2,1)S(1)}, u32[]{:S(2)}, u32[]{:S(2)}) %collective-permute-start.52) | collective-permute-done | bytes 557088 | tf_op jit(solution)/shard_map/ppermute | solution.py:88
  794.7 7.0 collective-permute-done.58
  804.9 11.9 %collective-permute-done.64 = bf16[256,1024]{1,0:T(8,128)(2,1)S(1)} collective-permute-done((bf16[256,1024]{1,0:T(8,128)(2,1)S(1)}, bf16[256,1024]{1,0:T(8,128)(2,1)S(1)}, u32[]{:S(2)}, u32[]{:S(2)}) %collective-permute-start.64) | collective-permute-done | bytes 524320 | tf_op jit(solution)/shard_map/ppermute | solution.py:88
  816.8 5.9 collective-permute-done.68
  828.4 19.1 %collective-permute-done.70.refs_11_ = bf16[256,1024]{1,0:T(8,128)(2,1)} collective-permute-done((bf16[256,1024]{1,0:T(8,128)(2,1)}, bf16[256,1024]{1,0:T(8,128)(2,1)}, u32[]{:S(2)}, u32[]{:S(2)}) %collective-permute-start.70) | collective-permute-done | bytes 524320 | tf_op jit(solution)/shard_map/ppermute | solution.py:92
  851.0 4.6 fusion.5.refs_16_
  855.6 4.1 convert_element_type.397.refs_14_
  859.7 4.1 convert_element_type.396.refs_13_
  863.8 4.1 convert_element_type.398.refs_15_
  867.9 7.9 finish.1
  (402 shorter events, 233.2 us)
Async XLA Ops:
  7.3 132.6 %all-gather.6.cloned.1.call-start = ((), (), s32[]{:S(2)}) async-start(), calls=%async_computation.12 | async-start | bytes 5242880 | tf_op jit(solution)/shard_map/all_gather | solution.py:794
  9.1 34.8 %collective-permute-start = (bf16[256,1024]{1,0:T(8,128)(2,1)S(1)}, bf16[256,1024]{1,0:T(8,128)(2,1)S(1)}, u32[]{:S(2)}, u32[]{:S(2)}) collective-permute-start(bf16[256,1024]{1,0:T(8,128)(2,1)S(1)} %pad_maximum_fusion.refs_0_), channel_id=1, source_target_pairs={{0,1},{1,0},{2,3},{3,2},{4,5},{5,4},{6,7},{7,6},{8,9},{9,8},{10,11... | collective-permute-start | bytes 1572872 | tf_op jit(solution)/shard_map/ppermute | solution.py:88
  48.4 55.8 %collective-permute-start.7 = (bf16[256,1024]{1,0:T(8,128)(2,1)S(1)}, bf16[256,1024]{1,0:T(8,128)(2,1)}, u32[]{:S(2)}, u32[]{:S(2)}) collective-permute-start(bf16[256,1024]{1,0:T(8,128)(2,1)S(1)} %pad_maximum_fusion.1.refs_2_), channel_id=1, source_target_pairs={{0,2},{1,3},{2,0},{3,1},{4,6},{5,7},{6,4},{7,5},{8,10},{9,11},{10,... | collective-permute-start | bytes 1572872 | tf_op jit(solution)/shard_map/ppermute | solution.py:88
  70.5 35.3 %collective-permute-start.6 = (bf16[256,1024]{1,0:T(8,128)(2,1)}, bf16[256,1024]{1,0:T(8,128)(2,1)}, u32[]{:S(2)}, u32[]{:S(2)}) collective-permute-start(bf16[256,1024]{1,0:T(8,128)(2,1)} %collective-permute-done.5.refs_6_), channel_id=1, source_target_pairs={{0,1},{1,0},{2,3},{3,2},{4,5},{5,4},{6,7},{7,6},{8,9},{9,8},{10,11... | collective-permute-start | bytes 1572872 | tf_op jit(solution)/shard_map/ppermute | solution.py:88
  72.2 65.2 %collective-permute-start.14 = (bf16[256,2048]{1,0:T(8,128)(2,1)S(1)}, bf16[256,2048]{1,0:T(8,128)(2,1)S(1)}, u32[]{:S(2)}, u32[]{:S(2)}) collective-permute-start(bf16[256,2048]{1,0:T(8,128)(2,1)S(1)} %bitcast.135), channel_id=1, source_target_pairs={{0,2},{1,3},{2,0},{3,1},{4,6},{5,7},{6,4},{7,5},{8,10},{9,11},{10,... | collective-permute-start | bytes 3145736 | tf_op jit(solution)/shard_map/ppermute | solution.py:88
  73.4 64.4 %collective-permute-start.27 = (bf16[256,2048]{1,0:T(8,128)(2,1)S(1)}, bf16[256,2048]{1,0:T(8,128)(2,1)S(1)}, u32[]{:S(2)}, u32[]{:S(2)}) collective-permute-start(bf16[256,2048]{1,0:T(8,128)(2,1)S(1)} %bitcast.136), channel_id=1, source_target_pairs={{0,4},{1,5},{2,6},{3,7},{4,0},{5,1},{6,2},{7,3},{8,12},{9,13},{10,... | collective-permute-start | bytes 3145736 | tf_op jit(solution)/shard_map/ppermute | solution.py:88
  75.4 33.0 %collective-permute-start.4 = (bf16[256,1024]{1,0:T(8,128)(2,1)}, bf16[256,1024]{1,0:T(8,128)(2,1)S(1)}, u32[]{:S(2)}, u32[]{:S(2)}) collective-permute-start(bf16[256,1024]{1,0:T(8,128)(2,1)} %collective-permute-done.2.refs_4_), channel_id=1, source_target_pairs={{0,1},{1,0},{2,3},{3,2},{4,5},{5,4},{6,7},{7,6},{8,9},{9,8},{10,11... | collective-permute-start | bytes 1572872 | tf_op jit(solution)/shard_map/ppermute | solution.py:88
  108.3 54.9 %collective-permute-start.11 = (bf16[256,1024]{1,0:T(8,128)(2,1)}, bf16[256,1024]{1,0:T(8,128)(2,1)}, u32[]{:S(2)}, u32[]{:S(2)}) collective-permute-start(bf16[256,1024]{1,0:T(8,128)(2,1)} %collective-permute-done.10.refs_6_), channel_id=1, source_target_pairs={{0,1},{1,0},{2,3},{3,2},{4,5},{5,4},{6,7},{7,6},{8,9},{9,8},{10,11... | collective-permute-start | bytes 1572872 | tf_op jit(solution)/shard_map/ppermute | solution.py:88
  119.3 44.5 %collective-permute-start.8 = (bf16[256,1024]{1,0:T(8,128)(2,1)S(1)}, bf16[256,1024]{1,0:T(8,128)(2,1)}, u32[]{:S(2)}, u32[]{:S(2)}) collective-permute-start(bf16[256,1024]{1,0:T(8,128)(2,1)S(1)} %pad_maximum_fusion.1.refs_2_), channel_id=1, source_target_pairs={{0,1},{1,0},{2,3},{3,2},{4,5},{5,4},{6,7},{7,6},{8,9},{9,8},{10,11... | collective-permute-start | bytes 1572872 | tf_op jit(solution)/shard_map/ppermute | solution.py:88
  160.8 37.3 %collective-permute-start.21 = (bf16[256,2048]{1,0:T(8,128)(2,1)S(1)}, bf16[256,2048]{1,0:T(8,128)(2,1)}, u32[]{:S(2)}, u32[]{:S(2)}) collective-permute-start(bf16[256,2048]{1,0:T(8,128)(2,1)S(1)} %bitcast.137), channel_id=1, source_target_pairs={{0,1},{1,0},{2,3},{3,2},{4,5},{5,4},{6,7},{7,6},{8,9},{9,8},{10,11... | collective-permute-start | bytes 3145736 | tf_op jit(solution)/shard_map/ppermute | solution.py:88
  163.2 65.1 %collective-permute-start.20 = (bf16[256,2048]{1,0:T(8,128)(2,1)}, bf16[256,2048]{1,0:T(8,128)(2,1)}, u32[]{:S(2)}, u32[]{:S(2)}) collective-permute-start(bf16[256,2048]{1,0:T(8,128)(2,1)} %copy-done.54), channel_id=1, source_target_pairs={{0,1},{1,0},{2,3},{3,2},{4,5},{5,4},{6,7},{7,6},{8,9},{9,8},{10,11... | collective-permute-start | bytes 3145736 | tf_op jit(solution)/shard_map/ppermute | solution.py:88
  163.8 86.2 %collective-permute-start.30 = (bf16[256,2048]{1,0:T(8,128)(2,1)S(1)}, bf16[256,2048]{1,0:T(8,128)(2,1)}, u32[]{:S(2)}, u32[]{:S(2)}) collective-permute-start(bf16[256,2048]{1,0:T(8,128)(2,1)S(1)} %collective-permute-done.27.refs_1_), channel_id=1, source_target_pairs={{0,1},{1,0},{2,3},{3,2},{4,5},{5,4},{6,7},{7,6},{8,9},{9,8},{10,11... | collective-permute-start | bytes 3145736 | tf_op jit(solution)/shard_map/ppermute | solution.py:88
  165.3 89.0 %collective-permute-start.29 = (bf16[256,2048]{1,0:T(8,128)(2,1)}, bf16[256,2048]{1,0:T(8,128)(2,1)}, u32[]{:S(2)}, u32[]{:S(2)}) collective-permute-start(bf16[256,2048]{1,0:T(8,128)(2,1)} %collective-permute-done.28.refs_1_), channel_id=1, source_target_pairs={{0,1},{1,0},{2,3},{3,2},{4,5},{5,4},{6,7},{7,6},{8,9},{9,8},{10,11... | collective-permute-start | bytes 3145736 | tf_op jit(solution)/shard_map/ppermute | solution.py:88
  175.7 48.9 %collective-permute-start.18 = (bf16[2048,512]{1,0:T(8,128)(2,1)}, bf16[2048,512]{1,0:T(8,128)(2,1)}, u32[]{:S(2)}, u32[]{:S(2)}) collective-permute-start(bf16[2048,512]{1,0:T(8,128)(2,1)} %get-tuple-element.143.refs_4_.refs_2_), channel_id=1, source_target_pairs={{0,16},{8,24},{16,0},{24,8},{1,17},{9,25},{17,1},{25,9},{2,18},{10... | collective-permute-start | bytes 6291464 | tf_op jit(solution)/shard_map/ppermute | solution.py:92
  194.1 39.4 %all-to-all-start.1 = ((bf16[4,256,512]{2,1,0:T(8,128)(2,1)}), bf16[4,256,512]{2,1,0:T(8,128)(2,1)S(1)}, u32[]{:S(2)}, u32[]{:S(2)}) async-start(bf16[4,256,512]{2,1,0:T(8,128)(2,1)} %bitcast.138), calls=%async_computation.1 | async-start | bytes 2097152 | tf_op jit(solution)/shard_map/all_to_all | solution.py:839
  197.6 482.6 %all-gather.4.cloned.1.call-start = ((), (), s32[]{:S(2)}) async-start(), calls=%async_computation.8 | async-start | bytes 5242880 | tf_op jit(solution)/shard_map/all_gather | solution.py:844
  198.1 36.6 %collective-permute-start.17 = (bf16[2048,512]{1,0:T(8,128)(2,1)}, bf16[2048,512]{1,0:T(8,128)(2,1)}, u32[]{:S(2)}, u32[]{:S(2)}) collective-permute-start(bf16[2048,512]{1,0:T(8,128)(2,1)} %get-tuple-element.143.refs_4_.refs_2_), channel_id=1, source_target_pairs={{0,8},{8,0},{16,24},{24,16},{1,9},{9,1},{17,25},{25,17},{2,10},{10... | collective-permute-start | bytes 6291464 | tf_op jit(solution)/shard_map/ppermute | solution.py:92
  234.7 620.9 %reduce-scatter.6.cloned.1.call-start = ((), (), s32[]{:S(2)}) async-start(), calls=%async_computation.10 | async-start | bytes 10485760 | tf_op jit(solution)/shard_map/reduce_scatter | solution.py:907
  243.5 51.5 %collective-permute-start.26 = (bf16[256,2048]{1,0:T(8,128)(2,1)}, bf16[256,2048]{1,0:T(8,128)(2,1)S(1)}, u32[]{:S(2)}, u32[]{:S(2)}) collective-permute-start(bf16[256,2048]{1,0:T(8,128)(2,1)} %get-tuple-element.147.refs_0_), channel_id=1, source_target_pairs={{0,1},{1,0},{2,3},{3,2},{4,5},{5,4},{6,7},{7,6},{8,9},{9,8},{10,11... | collective-permute-start | bytes 3145736 | tf_op jit(solution)/shard_map/ppermute | solution.py:88
  245.1 46.4 %collective-permute-start.22 = (bf16[256,2048]{1,0:T(8,128)(2,1)}, bf16[256,2048]{1,0:T(8,128)(2,1)S(1)}, u32[]{:S(2)}, u32[]{:S(2)}) collective-permute-start(bf16[256,2048]{1,0:T(8,128)(2,1)} %get-tuple-element.147.refs_0_), channel_id=1, source_target_pairs={{0,2},{1,3},{2,0},{3,1},{4,6},{5,7},{6,4},{7,5},{8,10},{9,11},{10,... | collective-permute-start | bytes 3145736 | tf_op jit(solution)/shard_map/ppermute | solution.py:88
  246.4 48.4 %collective-permute-start.24 = (bf16[256,2048]{1,0:T(8,128)(2,1)}, bf16[256,2048]{1,0:T(8,128)(2,1)}, u32[]{:S(2)}, u32[]{:S(2)}) collective-permute-start(bf16[256,2048]{1,0:T(8,128)(2,1)} %get-tuple-element.147.refs_0_), channel_id=1, source_target_pairs={{0,4},{1,5},{2,6},{3,7},{4,0},{5,1},{6,2},{7,3},{8,12},{9,13},{10,... | collective-permute-start | bytes 3145736 | tf_op jit(solution)/shard_map/ppermute | solution.py:88
  317.1 49.0 %collective-permute-start.32 = (bf16[256,2048]{1,0:T(8,128)(2,1)}, bf16[256,2048]{1,0:T(8,128)(2,1)}, u32[]{:S(2)}, u32[]{:S(2)}) collective-permute-start(bf16[256,2048]{1,0:T(8,128)(2,1)} %collective-permute-done.24.refs_1_), channel_id=1, source_target_pairs={{0,1},{1,0},{2,3},{3,2},{4,5},{5,4},{6,7},{7,6},{8,9},{9,8},{10,11... | collective-permute-start | bytes 3145736 | tf_op jit(solution)/shard_map/ppermute | solution.py:88
  317.7 53.0 %collective-permute-start.31 = (bf16[256,2048]{1,0:T(8,128)(2,1)}, bf16[256,2048]{1,0:T(8,128)(2,1)}, u32[]{:S(2)}, u32[]{:S(2)}) collective-permute-start(bf16[256,2048]{1,0:T(8,128)(2,1)} %collective-permute-done.25.refs_1_), channel_id=1, source_target_pairs={{0,1},{1,0},{2,3},{3,2},{4,5},{5,4},{6,7},{7,6},{8,9},{9,8},{10,11... | collective-permute-start | bytes 3145736 | tf_op jit(solution)/shard_map/ppermute | solution.py:88
  383.1 44.6 %collective-permute-start.34 = (bf16[256,2048]{1,0:T(8,128)(2,1)}, bf16[256,2048]{1,0:T(8,128)(2,1)}, u32[]{:S(2)}, u32[]{:S(2)}) collective-permute-start(bf16[256,2048]{1,0:T(8,128)(2,1)} %get-tuple-element.166.refs_9_.refs_7_), channel_id=1, source_target_pairs={{0,1},{1,0},{2,3},{3,2},{4,5},{5,4},{6,7},{7,6},{8,9},{9,8},{10,11... | collective-permute-start | bytes 3145736 | tf_op jit(solution)/shard_map/ppermute | solution.py:88
  383.7 46.7 %collective-permute-start.33 = (bf16[256,2048]{1,0:T(8,128)(2,1)}, bf16[256,2048]{1,0:T(8,128)(2,1)}, u32[]{:S(2)}, u32[]{:S(2)}) collective-permute-start(bf16[256,2048]{1,0:T(8,128)(2,1)} %get-tuple-element.164.refs_7_.refs_5_), channel_id=1, source_target_pairs={{0,1},{1,0},{2,3},{3,2},{4,5},{5,4},{6,7},{7,6},{8,9},{9,8},{10,11... | collective-permute-start | bytes 3145736 | tf_op jit(solution)/shard_map/ppermute | solution.py:88
  489.4 370.3 %reduce-scatter.4.cloned.1.call-start = ((), (), s32[]{:S(2)}) async-start(), calls=%async_computation.9 | async-start | bytes 10485760 | tf_op jit(solution)/shard_map/reduce_scatter | solution.py:907
  490.0 32.6 %collective-permute-start.35 = (bf16[256,2048]{1,0:T(8,128)(2,1)}, bf16[256,2048]{1,0:T(8,128)(2,1)S(1)}, u32[]{:S(2)}, u32[]{:S(2)}) collective-permute-start(bf16[256,2048]{1,0:T(8,128)(2,1)} %get-tuple-element.173.refs_9_), channel_id=1, source_target_pairs={{0,1},{1,0},{2,3},{3,2},{4,5},{5,4},{6,7},{7,6},{8,9},{9,8},{10,11... | collective-permute-start | bytes 3145736 | tf_op jit(solution)/shard_map/ppermute | solution.py:88
  542.9 48.4 %collective-permute-start.39 = (bf16[256,2048]{1,0:T(8,128)(2,1)}, bf16[256,2048]{1,0:T(8,128)(2,1)}, u32[]{:S(2)}, u32[]{:S(2)}) collective-permute-start(bf16[256,2048]{1,0:T(8,128)(2,1)} %get-tuple-element.186.refs_9_.refs_14_), channel_id=1, source_target_pairs={{0,1},{1,0},{2,3},{3,2},{4,5},{5,4},{6,7},{7,6},{8,9},{9,8},{10,11... | collective-permute-start | bytes 3145736 | tf_op jit(solution)/shard_map/ppermute | solution.py:88
  544.5 83.9 %collective-permute-start.38 = (bf16[256,2048]{1,0:T(8,128)(2,1)}, bf16[256,2048]{1,0:T(8,128)(2,1)}, u32[]{:S(2)}, u32[]{:S(2)}) collective-permute-start(bf16[256,2048]{1,0:T(8,128)(2,1)} %get-tuple-element.184.refs_7_.refs_12_), channel_id=1, source_target_pairs={{0,1},{1,0},{2,3},{3,2},{4,5},{5,4},{6,7},{7,6},{8,9},{9,8},{10,11... | collective-permute-start | bytes 3145736 | tf_op jit(solution)/shard_map/ppermute | solution.py:88
  545.0 86.3 %collective-permute-start.37 = (bf16[256,2048]{1,0:T(8,128)(2,1)}, bf16[256,2048]{1,0:T(8,128)(2,1)}, u32[]{:S(2)}, u32[]{:S(2)}) collective-permute-start(bf16[256,2048]{1,0:T(8,128)(2,1)} %get-tuple-element.182.refs_5_.refs_10_), channel_id=1, source_target_pairs={{0,1},{1,0},{2,3},{3,2},{4,5},{5,4},{6,7},{7,6},{8,9},{9,8},{10,11... | collective-permute-start | bytes 3145736 | tf_op jit(solution)/shard_map/ppermute | solution.py:88
  566.2 38.0 %collective-permute-start.41 = (bf16[256,2048]{1,0:T(8,128)(2,1)S(1)}, bf16[256,2048]{1,0:T(8,128)(2,1)S(1)}, u32[]{:S(2)}, u32[]{:S(2)}) collective-permute-start(bf16[256,2048]{1,0:T(8,128)(2,1)S(1)} %copy-done.13), channel_id=1, source_target_pairs={{0,2},{1,3},{2,0},{3,1},{4,6},{5,7},{6,4},{7,5},{8,10},{9,11},{10,... | collective-permute-start | bytes 3145736 | tf_op jit(solution)/shard_map/ppermute | solution.py:88
  568.9 40.9 %collective-permute-start.43 = (bf16[256,2048]{1,0:T(8,128)(2,1)S(1)}, bf16[256,2048]{1,0:T(8,128)(2,1)S(1)}, u32[]{:S(2)}, u32[]{:S(2)}) collective-permute-start(bf16[256,2048]{1,0:T(8,128)(2,1)S(1)} %add_convert_fusion.2), channel_id=1, source_target_pairs={{0,4},{1,5},{2,6},{3,7},{4,0},{5,1},{6,2},{7,3},{8,12},{9,13},{10,... | collective-permute-start | bytes 3145736 | tf_op jit(solution)/shard_map/ppermute | solution.py:88
  642.9 37.3 %all-to-all-start.4 = ((bf16[256,4,512]{2,0,1:T(8,128)(2,1)}), bf16[256,4,512]{2,0,1:T(8,128)(2,1)}, u32[]{:S(2)}, u32[]{:S(2)}) async-start(bf16[256,4,512]{2,0,1:T(8,128)(2,1)} %bitcast.122), calls=%async_computation.4 | async-start | bytes 2097152 | tf_op jit(solution)/shard_map/all_to_all | solution.py:933
  647.2 216.7 %reduce-scatter.8.cloned.1.call-start = ((), (), s32[]{:S(2)}) async-start(), calls=%async_computation.11 | async-start | bytes 10485760 | tf_op jit(solution)/shard_map/reduce_scatter | solution.py:907
  647.2 32.6 %collective-permute-start.45 = (bf16[256,2048]{1,0:T(8,128)(2,1)S(1)}, bf16[256,2048]{1,0:T(8,128)(2,1)S(1)}, u32[]{:S(2)}, u32[]{:S(2)}) collective-permute-start(bf16[256,2048]{1,0:T(8,128)(2,1)S(1)} %add_convert_fusion.3), channel_id=1, source_target_pairs={{0,2},{1,3},{2,0},{3,1},{4,6},{5,7},{6,4},{7,5},{8,10},{9,11},{10,... | collective-permute-start | bytes 3145736 | tf_op jit(solution)/shard_map/ppermute | solution.py:88
  670.9 52.1 %collective-permute-start.44 = (bf16[256,2048]{1,0:T(8,128)(2,1)}, bf16[256,2048]{1,0:T(8,128)(2,1)}, u32[]{:S(2)}, u32[]{:S(2)}) collective-permute-start(bf16[256,2048]{1,0:T(8,128)(2,1)} %add_convert_fusion.5), channel_id=1, source_target_pairs={{0,2},{1,3},{2,0},{3,1},{4,6},{5,7},{6,4},{7,5},{8,10},{9,11},{10,... | collective-permute-start | bytes 3145736 | tf_op jit(solution)/shard_map/ppermute | solution.py:88
  690.9 47.9 %collective-permute-start.46 = (bf16[256,2048]{1,0:T(8,128)(2,1)S(1)}, bf16[256,2048]{1,0:T(8,128)(2,1)}, u32[]{:S(2)}, u32[]{:S(2)}) collective-permute-start(bf16[256,2048]{1,0:T(8,128)(2,1)S(1)} %add_convert_fusion.1), channel_id=1, source_target_pairs={{0,4},{1,5},{2,6},{3,7},{4,0},{5,1},{6,2},{7,3},{8,12},{9,13},{10,... | collective-permute-start | bytes 3145736 | tf_op jit(solution)/shard_map/ppermute | solution.py:88
  711.9 44.8 %collective-permute-start.66 = (bf16[256,1024]{1,0:T(8,128)(2,1)}, bf16[256,1024]{1,0:T(8,128)(2,1)}, u32[]{:S(2)}, u32[]{:S(2)}) collective-permute-start(bf16[256,1024]{1,0:T(8,128)(2,1)} %get-tuple-element.215.refs_9_), channel_id=1, source_target_pairs={{0,1},{1,0},{2,3},{3,2},{4,5},{5,4},{6,7},{7,6},{8,9},{9,8},{10,11... | collective-permute-start | bytes 1572872 | tf_op jit(solution)/shard_map/ppermute | solution.py:88
  712.2 55.2 %collective-permute-start.65 = (bf16[256,1024]{1,0:T(8,128)(2,1)}, bf16[256,1024]{1,0:T(8,128)(2,1)}, u32[]{:S(2)}, u32[]{:S(2)}) collective-permute-start(bf16[256,1024]{1,0:T(8,128)(2,1)} %get-tuple-element.232), channel_id=1, source_target_pairs={{0,1},{1,0},{2,3},{3,2},{4,5},{5,4},{6,7},{7,6},{8,9},{9,8},{10,11... | collective-permute-start | bytes 1572872 | tf_op jit(solution)/shard_map/ppermute | solution.py:88
  719.5 38.7 %collective-permute-start.53 = (bf16[272,1024]{1,0:T(8,128)(2,1)}, bf16[272,1024]{1,0:T(8,128)(2,1)}, u32[]{:S(2)}, u32[]{:S(2)}) collective-permute-start(bf16[272,1024]{1,0:T(8,128)(2,1)} %get-tuple-element.222), channel_id=1, source_target_pairs={{0,1},{1,0},{2,3},{3,2},{4,5},{5,4},{6,7},{7,6},{8,9},{9,8},{10,11... | collective-permute-start | bytes 1671176 | tf_op jit(solution)/shard_map/ppermute | solution.py:88
  723.0 40.9 %collective-permute-start.55 = (bf16[272,1024]{1,0:T(8,128)(2,1)}, bf16[272,1024]{1,0:T(8,128)(2,1)}, u32[]{:S(2)}, u32[]{:S(2)}) collective-permute-start(bf16[272,1024]{1,0:T(8,128)(2,1)} %get-tuple-element.224), channel_id=1, source_target_pairs={{0,1},{1,0},{2,3},{3,2},{4,5},{5,4},{6,7},{7,6},{8,9},{9,8},{10,11... | collective-permute-start | bytes 1671176 | tf_op jit(solution)/shard_map/ppermute | solution.py:88
  756.7 32.8 %collective-permute-start.50 = (bf16[256,2048]{1,0:T(8,128)(2,1)S(1)}, bf16[256,2048]{1,0:T(8,128)(2,1)S(1)}, u32[]{:S(2)}, u32[]{:S(2)}) collective-permute-start(bf16[256,2048]{1,0:T(8,128)(2,1)S(1)} %get-tuple-element.244), channel_id=1, source_target_pairs={{0,8},{8,0},{16,24},{24,16},{1,9},{9,1},{17,25},{25,17},{2,10},{10... | collective-permute-start | bytes 3145736 | tf_op jit(solution)/shard_map/ppermute | solution.py:92
  763.9 40.2 %collective-permute-start.62 = (bf16[256,1024]{1,0:T(8,128)(2,1)S(1)}, bf16[256,1024]{1,0:T(8,128)(2,1)S(1)}, u32[]{:S(2)}, u32[]{:S(2)}) collective-permute-start(bf16[256,1024]{1,0:T(8,128)(2,1)S(1)} %copy-done.61), channel_id=1, source_target_pairs={{0,1},{1,0},{2,3},{3,2},{4,5},{5,4},{6,7},{7,6},{8,9},{9,8},{10,11... | collective-permute-start | bytes 1572872 | tf_op jit(solution)/shard_map/ppermute | solution.py:88
  789.6 33.2 %collective-permute-start.68 = (bf16[256,1024]{1,0:T(8,128)(2,1)S(1)}, bf16[256,1024]{1,0:T(8,128)(2,1)S(1)}, u32[]{:S(2)}, u32[]{:S(2)}) collective-permute-start(bf16[256,1024]{1,0:T(8,128)(2,1)S(1)} %add_convert_fusion.18), channel_id=1, source_target_pairs={{0,4},{1,5},{2,6},{3,7},{4,0},{5,1},{6,2},{7,3},{8,12},{9,13},{10,... | collective-permute-start | bytes 1572872 | tf_op jit(solution)/shard_map/ppermute | solution.py:88
  794.6 52.9 %collective-permute-start.49 = (bf16[256,2048]{1,0:T(8,128)(2,1)}, bf16[256,2048]{1,0:T(8,128)(2,1)}, u32[]{:S(2)}, u32[]{:S(2)}) collective-permute-start(bf16[256,2048]{1,0:T(8,128)(2,1)} %get-tuple-element.243), channel_id=1, source_target_pairs={{0,8},{8,0},{16,24},{24,16},{1,9},{9,1},{17,25},{25,17},{2,10},{10... | collective-permute-start | bytes 3145736 | tf_op jit(solution)/shard_map/ppermute | solution.py:92
  801.7 46.4 %collective-permute-start.51 = (bf16[256,2048]{1,0:T(8,128)(2,1)}, bf16[256,2048]{1,0:T(8,128)(2,1)}, u32[]{:S(2)}, u32[]{:S(2)}) collective-permute-start(bf16[256,2048]{1,0:T(8,128)(2,1)} %fusion.7), channel_id=1, source_target_pairs={{0,16},{8,24},{16,0},{24,8},{1,17},{9,25},{17,1},{25,9},{2,18},{10... | collective-permute-start | bytes 3145736 | tf_op jit(solution)/shard_map/ppermute | solution.py:92
  804.2 43.9 %collective-permute-start.60 = (bf16[272,1024]{1,0:T(8,128)(2,1)}, bf16[272,1024]{1,0:T(8,128)(2,1)}, u32[]{:S(2)}, u32[]{:S(2)}) collective-permute-start(bf16[272,1024]{1,0:T(8,128)(2,1)} %add_convert_fusion.11.refs_5_), channel_id=1, source_target_pairs={{0,16},{8,24},{16,0},{24,8},{1,17},{9,25},{17,1},{25,9},{2,18},{10... | collective-permute-start | bytes 1671176 | tf_op jit(solution)/shard_map/ppermute | solution.py:92
  828.3 39.6 %collective-permute-start.69 = (bf16[256,1024]{1,0:T(8,128)(2,1)}, bf16[256,1024]{1,0:T(8,128)(2,1)}, u32[]{:S(2)}, u32[]{:S(2)}) collective-permute-start(bf16[256,1024]{1,0:T(8,128)(2,1)} %add_convert_fusion.17.refs_9_), channel_id=1, source_target_pairs={{0,8},{8,0},{16,24},{24,16},{1,9},{9,1},{17,25},{25,17},{2,10},{10... | collective-permute-start | bytes 1572872 | tf_op jit(solution)/shard_map/ppermute | solution.py:92
  (104 other events, 1889.6 us)
Sparse Core Ops, SparseCore 0:
  9.6 37.1 all-gather.5
  234.8 35.5 all-gather.3
  477.8 70.0 reduce-scatter.5
  550.5 71.6 reduce-scatter.3
  712.0 71.0 reduce-scatter.7

commit v5 on v4

--- a/solution.py
+++ b/solution.py
@@ -136,6 +136,13 @@
     return own.astype(F32) + swap(near, 2).astype(F32) + swap(far, 4).astype(F32)
 
 
+def scatter_x_last(pieces, n_ep):
+    if n_ep != 8:
+        return scatter(pieces, n_ep)
+    kept, sent = scatter_z(*pieces[0::2]), scatter_z(*pieces[1::2])
+    return kept + swap(sent.astype(BF16), 1).astype(F32)
+
+
 def scatter(pieces, n_ep):
     if n_ep != 8:
         stacked = jnp.stack(pieces)
@@ -149,8 +156,7 @@
 
 
 def sum_sp(value):
-    value = value + swap_sp(value, 1)
-    return value + swap_sp(value, 2)
+    return (value + swap_sp(value, 1)) + (swap_sp(value, 2) + swap_sp(value, 3))
 
 
 def block_at(ids, position, size):
@@ -773,26 +779,34 @@
     full_router = small_rows[16:]
     picked_all = by_piece(picked_all)
 
+    x_all = lax.all_gather(tokens[0], "sp", axis=0, tiled=True)
     qk_own = jnp.concatenate([own_columns(w_query), own_columns(w_key)], axis=1)
     vo_own = jnp.concatenate([own_columns(w_value), own_columns(w_out)], axis=1)
     cot_own = cotangent[0]
     if n_ep == 8:
         own_x, near, far = swap(qk_own, 1), swap(qk_own, 2), swap(qk_own, 4)
-        own_x, near, far, vo_own = tie(own_x, near, far, vo_own)
+        own_x, near, far = tie(own_x, near, far)
+        farther = swap(far, 2)
+        farther, vo_own = tie(farther, vo_own)
+        near_x, far_x, farther_x = swap(near, 1), swap(far, 1), swap(farther, 1)
+        near_x, far_x, farther_x, vo_own_x = tie(near_x, far_x, farther_x, vo_own)
+        qk_pieces = [qk_own, own_x, near, near_x, far, far_x, farther, farther_x]
         vo_blocks = along_z(vo_own)
-        qk_pieces = [qk_own, own_x] + across_x([near, far, swap(far, 2)])
-        vo_blocks[2], cot_own = tie(vo_blocks[2], cot_own)
+        vo_crossed, vo_blocks[2] = tie(swap(vo_own_x, 1), vo_blocks[2])
+        vo_blocks[3] = swap(vo_blocks[2], 2)
+        vo_crossed, vo_blocks[1], vo_blocks[3] = tie(vo_crossed, vo_blocks[1], vo_blocks[3])
+        q_raw, k_raw, squares, w_qk, h_all = qk_project(ids, x_all, gains[0:1], qk_pieces)
+        vo_crossed, squares = tie(vo_crossed, squares)
+        vo_others = along_z(vo_crossed)
+        vo_pieces = [piece for two in zip(vo_blocks, vo_others) for piece in two]
+        vo_pieces[7], cot_own = tie(vo_pieces[7], cot_own)
         cot_blocks = along_z(cot_own)
-        qk_pieces[7], vo_blocks[0], vo_blocks[1] = tie(qk_pieces[7], vo_blocks[0], vo_blocks[1])
-        vo_pieces = across_x(vo_blocks)
-        vo_pieces[7], cot_blocks[0], cot_blocks[1] = tie(vo_pieces[7], cot_blocks[0], cot_blocks[1])
         cot_pieces = across_x(cot_blocks)
     else:
         qk_pieces, vo_pieces, cot_pieces = (
             gather_whole(value) for value in (qk_own, vo_own, cot_own)
         )
-    x_all = lax.all_gather(tokens[0], "sp", axis=0, tiled=True)
-
+        q_raw, k_raw, squares, w_qk, h_all = qk_project(ids, x_all, gains[0:1], qk_pieces)
     upper = (
         jnp.arange(tok_dev, dtype=jnp.int32)[:, None] < jnp.arange(tok_dev, dtype=jnp.int32)[None, :]
     ).astype(BF16)
@@ -815,7 +829,6 @@
     sine = jnp.concatenate([-jnp.sin(angles), jnp.sin(angles)], axis=1)
     starts = starts[:, None].astype(jnp.int32)
 
-    q_raw, k_raw, squares, w_qk, h_all = qk_project(ids, x_all, gains[0:1], qk_pieces)
     scales = lax.rsqrt(sum_sp(squares) / width + EPS)
     v_low, w_v, w_o = v_project(ids, h_all, vo_pieces, [q_raw])
     w_o_parts = gather_sp(w_o)
@@ -885,7 +898,10 @@
     ins = [rows for rows, _, _ in groups]
     outs = [d_rows for _, d_rows, _ in groups]
     grad_down = weight_grad(acts, outs, d_pieces)
-    grad_gate = weight_grad(ins, d_gate_rows, [grad_down])
+    d_gates = by_piece(jnp.concatenate(d_gates, axis=0).reshape(n_ep, local, tok_dev))
+    d_gates = lax.all_to_all(d_gates, "ep", split_axis=0, concat_axis=0, tiled=True)
+    d_gates = d_gates.reshape(expert_count, tok_dev)
+    grad_gate = weight_grad(ins, d_gate_rows, [grad_down, d_gates])
     mix_pieces = []
     for g, (_, _, made) in enumerate(groups):
         for at in range(group // 2):
@@ -897,6 +913,7 @@
         *d_sums, mix_pieces[1], mix_pieces[3], mix_pieces[5], mix_pieces[7] = tie(
             *d_sums, mix_pieces[1], mix_pieces[3], mix_pieces[5], mix_pieces[7]
         )
+        mix_pieces[0], grad_down, grad_gate = tie(mix_pieces[0], grad_down, grad_gate)
         mix_sums = crossed_sums(mix_pieces)
         d_h2 = scatter_z(*d_sums)
     else:
@@ -906,9 +923,6 @@
     def over_sp(value):
         return lax.psum_scatter(value, "sp", scatter_dimension=1, tiled=True).astype(F32)
 
-    d_gates = by_piece(jnp.concatenate(d_gates, axis=0).reshape(n_ep, local, tok_dev))
-    d_gates = lax.all_to_all(d_gates, "ep", split_axis=0, concat_axis=0, tiled=True)
-    d_gates = d_gates.reshape(expert_count, tok_dev)
 
     if n_ep == 8:
         gates_here = home_gates[:expert_count]
@@ -927,7 +941,7 @@
     d_one = cotangent[0].astype(F32) + one_scale * (
         d_normed - one_normed * jnp.mean(d_normed * one_normed, axis=-1, keepdims=True)
     )
-    d_z = d_one.astype(BF16)
+    d_z, grad_up = tie(d_one.astype(BF16), grad_up)
     d_attn = out_back(ids, n_ep, d_z, w_o_parts, [grad_up, grad_gate, grad_down, *mix_pieces])
     d_heads = lax.all_to_all(d_attn, "sp", split_axis=1, concat_axis=0, tiled=True)
     d_z_cols = lax.all_to_all(d_z, "sp", split_axis=1, concat_axis=0, tiled=True)
@@ -946,7 +960,7 @@
         mix = scatter(mix_pieces, n_ep)
     output = (x_one + mix).astype(BF16)
     vo_pieces = vo_grads(ids, n_ep, h_all, d_v, attn_all, d_z_cols)
-    grad_vo = scatter(vo_pieces, n_ep).astype(BF16)
+    grad_vo = scatter_x_last(vo_pieces, n_ep).astype(BF16)
 
     def placed(value):
         return lax.dynamic_update_slice_in_dim(
@@ -961,7 +975,9 @@
     )
     grad_qk = scatter(qk_pieces, n_ep).astype(BF16)
 
-    d_h = d_h_rows(d_qk, d_v, w_qk, w_v, [output]).reshape(n_sp, tok_dev, width)
+    d_h = d_h_rows(d_qk, d_v, w_qk, w_v, [])
+    output, d_h = tie(output, d_h)
+    d_h = d_h.reshape(n_sp, tok_dev, width)
     parts = [
         lax.dynamic_index_in_dim(d_h, partners[j], 0, keepdims=False) for j in range(4)
     ]

time: 897 us -> 951 us (1.060)
  waiting for transfers between devices: 321 us -> 384 us
    ppermute x56, waiting for transfers between devices: 249 us -> 303 us  [swap(): return lax.ppermute(value, 'ep', [(i, i ^ bits) for i in range(8)])]
    all_to_all x1, waiting for transfers between devices: 1.34 us -> 32 us  [body(): lax.all_to_all(mixed, 'sp', split_axis=0, concat_axis=1, tiled=True)]
    ppermute x16 -> x18, waiting for transfers between devices: 47.7 us -> 28.4 us  [swap_sp(): return lax.ppermute(value, 'sp', [(i, i ^ bits) for i in range(4)])]
    all_to_all x1, waiting for transfers between devices: 14 us -> 0.01 us  [body(): lax.all_to_all(d_gates, 'ep', split_axis=0, concat_axis=0, tiled=True)]
    all_to_all x1, waiting for transfers between devices: 7.8 us -> 19.1 us  [body(): lax.all_to_all(d_attn, 'sp', split_axis=1, concat_axis=0, tiled=True)]
    convert_element_type x17 -> x16, other arithmetic: 30.9 us -> 28.7 us  [plus(): return (left.astype(F32) + right.astype(F32)).astype(left.dtype)]
  transfers between devices with their start and end apart: 82 -> 84, of which waited for: 31 -> 34; matrix products, arithmetic and copies ran while one was open for 10% -> 10% of each run, Pallas kernels for 36% -> 33%
where the time goes in v5:
time: 951 us; the launch traced here: 941 us
  waiting for transfers between devices  384 us (40%)
  Pallas kernels  327 us (34%)
  starting transfers between devices  91.6 us (10%)
  other arithmetic  67 us (7%)
  between operations  38.4 us (4%)
  local copies, waits for them, and re-layouts  30.9 us (3%)
    pallas_call x31, Pallas kernels, call(): pl.pallas_call(kernel, grid_spec=pltpu.PrefetchScalarGridSpec(num_scalar_...  327 us
    ppermute x56, waiting for transfers between devices, swap(): return lax.ppermute(value, 'ep', [(i, i ^ bits) for i in range(8)])  303 us
    ppermute x56, starting transfers between devices, swap(): return lax.ppermute(value, 'ep', [(i, i ^ bits) for i in range(8)])  61.2 us
    all_to_all x1, waiting for transfers between devices, body(): lax.all_to_all(mixed, 'sp', split_axis=0, concat_axis=1, tiled=True)  32 us
    convert_element_type x16, other arithmetic, plus(): return (left.astype(F32) + right.astype(F32)).astype(left.dtype)  28.7 us
    ppermute x18, waiting for transfers between devices, swap_sp(): return lax.ppermute(value, 'sp', [(i, i ^ bits) for i in range(4)])  28.4 us
    all_to_all x1, waiting for transfers between devices, body(): lax.all_to_all(d_attn, 'sp', split_axis=1, concat_axis=0, tiled=True)  19.1 us
  transfers between devices with their start and end apart: 84, of which 34 were waited for; matrix products, arithmetic and copies ran while one was open for 10% of the time, Pallas kernels for 33%

profile of v5, /device:TPU:0, one launch (start us, length us, event | category | flops | bytes accessed | tf_op | source)
XLA Modules:
  0.0 941.1 jit_solution(12077288420870809483)
XLA Ops:
  24.3 12.3 %collective-permute-done.1.refs_2_ = bf16[256,1024]{1,0:T(8,128)(2,1)S(1)} collective-permute-done((bf16[256,1024]{1,0:T(8,128)(2,1)S(1)}, bf16[256,1024]{1,0:T(8,128)(2,1)S(1)}, u32[]{:S(2)}, u32[]{:S(2)}) %collective-permute-start.1) | collective-permute-done | bytes 524320 | tf_op jit(solution)/shard_map/ppermute | solution.py:88
  36.7 4.8 collective-permute-done.2.refs_4_
  45.7 6.6 collective-permute-done.5.refs_6_
  80.7 14.0 %collective-permute-done.8.refs_6_ = bf16[256,1024]{1,0:T(8,128)(2,1)S(1)} collective-permute-done((bf16[256,1024]{1,0:T(8,128)(2,1)S(1)}, bf16[256,1024]{1,0:T(8,128)(2,1)S(1)}, u32[]{:S(2)}, u32[]{:S(2)}) %collective-permute-start.8) | collective-permute-done | bytes 524320 | tf_op jit(solution)/shard_map/ppermute | solution.py:88
  98.0 11.0 %collective-permute-done.10.refs_8_ = bf16[256,1024]{1,0:T(8,128)(2,1)} collective-permute-done((bf16[256,1024]{1,0:T(8,128)(2,1)S(1)}, bf16[256,1024]{1,0:T(8,128)(2,1)}, u32[]{:S(2)}, u32[]{:S(2)}) %collective-permute-start.10) | collective-permute-done | bytes 524320 | tf_op jit(solution)/shard_map/ppermute | solution.py:88
  109.0 11.9 %qk_project.1 = (f32[1024,512]{1,0:T(8,128)}, f32[1024,512]{1,0:T(8,128)}, f32[16,1024]{1,0:T(8,128)}, bf16[2048,1024]{1,0:T(8,128)(2,1)}, bf16[1024,2048]{1,0:T(8,128)(2,1)}) custom-call(s32[12]{0:T(128)} %pad_add_fusion.ids.refs_0_, bf16[1024,2048]{1,0:T(8,128)(2,1)} %bitcast.169, f32[1,2048]{1,0:T(1,128)} %bitcast.151, bf16[256,1024]{1,0:T(8,128)(2,1)} %copy-done.31, ...), custom_call_target="tpu_custom_call" | custom-call | flops 85899345920 | bytes 21045248 | tf_op jit(solution)/shard_map/qk_project/pallas_call | solution.py:62
  123.1 22.8 %collective-permute-done.12.refs_7_ = bf16[256,1024]{1,0:T(8,128)(2,1)S(1)} collective-permute-done((bf16[256,1024]{1,0:T(8,128)(2,1)}, bf16[256,1024]{1,0:T(8,128)(2,1)S(1)}, u32[]{:S(2)}, u32[]{:S(2)}) %collective-permute-start.12) | collective-permute-done | bytes 524320 | tf_op jit(solution)/shard_map/ppermute | solution.py:88
  153.5 6.3 collective-permute-done.13.refs_9_
  164.0 8.4 v_project.1
  173.9 17.2 %attend.1 = (bf16[1024,512]{1,0:T(8,128)(2,1)}, bf16[1024,512]{1,0:T(8,128)(2,1)}, bf16[1024,512]{1,0:T(8,128)(2,1)}) custom-call(f32[1024,512]{1,0:T(8,128)} %get-tuple-element.148.refs_10_.qr_ref.refs_4_, f32[1024,512]{1,0:T(8,128)} %get-tuple-element.149.kr_ref.refs_5_, bf16[1024,512]{1,0:T(8,128)(2,1)} %get-tuple-element.160.v_ref, ...), custom_call_target="tpu_custom_call" | custom-call | flops 32212254720 | bytes 9510912 | tf_op jit(solution)/shard_map/attend/pallas_call | solution.py:62
  197.6 32.0 %all-to-all-done.1 = bf16[4,256,512]{2,1,0:T(8,128)(2,1)S(1)} async-done(((bf16[4,256,512]{2,1,0:T(8,128)(2,1)}), bf16[4,256,512]{2,1,0:T(8,128)(2,1)S(1)}, u32[]{:S(2)}, u32[]{:S(2)}) %all-to-all-start.1) | async-done | bytes 1048608 | tf_op jit(solution)/shard_map/all_to_all | solution.py:852
  237.2 17.0 %collective-permute-done.29.refs_1_ = bf16[256,2048]{1,0:T(8,128)(2,1)} collective-permute-done((bf16[256,2048]{1,0:T(8,128)(2,1)S(1)}, bf16[256,2048]{1,0:T(8,128)(2,1)}, u32[]{:S(2)}, u32[]{:S(2)}) %collective-permute-start.29) | collective-permute-done | bytes 1048608 | tf_op jit(solution)/shard_map/ppermute | solution.py:88
  255.1 24.4 %collective-permute-done.21.refs_2_ = bf16[256,2048]{1,0:T(8,128)(2,1)} collective-permute-done((bf16[256,2048]{1,0:T(8,128)(2,1)}, bf16[256,2048]{1,0:T(8,128)(2,1)}, u32[]{:S(2)}, u32[]{:S(2)}) %collective-permute-start.21) | collective-permute-done | bytes 1048608 | tf_op jit(solution)/shard_map/ppermute | solution.py:88
  284.6 8.7 out_project.1
  305.8 28.3 %collective-permute-done.23.refs_0_ = bf16[256,2048]{1,0:T(8,128)(2,1)S(1)} collective-permute-done((bf16[256,2048]{1,0:T(8,128)(2,1)}, bf16[256,2048]{1,0:T(8,128)(2,1)S(1)}, u32[]{:S(2)}, u32[]{:S(2)}) %collective-permute-start.23) | collective-permute-done | bytes 1048608 | tf_op jit(solution)/shard_map/ppermute | solution.py:88
  337.8 4.5 dispatch.10
  342.3 15.1 %collective-permute-done.24.refs_1_ = bf16[256,2048]{1,0:T(8,128)(2,1)S(1)} collective-permute-done((bf16[256,2048]{1,0:T(8,128)(2,1)S(1)}, bf16[256,2048]{1,0:T(8,128)(2,1)S(1)}, u32[]{:S(2)}, u32[]{:S(2)}) %collective-permute-start.24) | collective-permute-done | bytes 1048608 | tf_op jit(solution)/shard_map/ppermute | solution.py:88
  360.9 4.4 dispatch.11
  365.4 42.7 %experts.2 = (bf16[2,576,1024]{2,1,0:T(8,128)(2,1)}, bf16[2,576,1024]{2,1,0:T(8,128)(2,1)}, bf16[2,576,1024]{2,1,0:T(8,128)(2,1)}, f32[2,576,1]{2,1,0:T(8,128)},...) custom-call(bf16[2,576,2048]{2,1,0:T(8,128)(2,1)} %get-tuple-element.170.refs_0_, ...), custom_call_target="tpu_custom_call" | custom-call | flops 579820584960 | bytes 51127296 | tf_op jit(solution)/shard_map/experts/pallas_call | solution.py:62
  408.1 4.5 dispatch.14
  412.6 4.5 dispatch.15
  427.0 42.7 %experts.3 = (bf16[2,576,1024]{2,1,0:T(8,128)(2,1)}, bf16[2,576,1024]{2,1,0:T(8,128)(2,1)}, bf16[2,576,1024]{2,1,0:T(8,128)(2,1)}, f32[2,576,1]{2,1,0:T(8,128)},...) custom-call(bf16[2,576,2048]{2,1,0:T(8,128)(2,1)} %get-tuple-element.178.refs_3_.refs_0_.refs_1_, ...), custom_call_target="tpu_custom_call" | custom-call | flops 579820584960 | bytes 51127296 | tf_op jit(solution)/shard_map/experts/pallas_call | solution.py:62
  494.4 18.4 %weight_grad.3.refs_4_.refs_8_ = bf16[2,1024,2048]{2,1,0:T(8,128)(2,1)} custom-call(bf16[2,576,1024]{2,1,0:T(8,128)(2,1)} %get-tuple-element.187.refs_0_, bf16[2,576,1024]{2,1,0:T(8,128)(2,1)} %get-tuple-element.188.refs_1_, bf16[2,576,2048]{2,1,0:T(8,128)(2,1)} %dispatch.9.refs_8_.refs_1_.refs_6_.refs_10_.refs_2_, ...), custom_call_target="tpu_custom_call" | custom-call | flops 193273528320 | bytes 22544384 | tf_op jit(solution)/shard_map/weight_grad/pallas_call | solution.py:62
  514.2 18.3 %weight_grad.4.refs_2_.refs_7_ = bf16[2,2048,1024]{2,1,0:T(8,128)(2,1)} custom-call(bf16[2,576,2048]{2,1,0:T(8,128)(2,1)} %get-tuple-element.170.refs_0_, bf16[2,576,2048]{2,1,0:T(8,128)(2,1)} %get-tuple-element.178.refs_3_.refs_0_.refs_1_, bf16[2,576,1024]{2,1,0:T(8,128)(2,1)} %get-tuple-element.179.refs_2_, ...), custom_call_target="tpu_custom_call" | custom-call | flops 193273528320 | bytes 22544384 | tf_op jit(solution)/shard_map/weight_grad/pallas_call | solution.py:62
  550.4 4.7 combine.15
  555.0 4.6 combine.14
  569.4 18.6 %weight_grad.5.refs_6_ = bf16[2,2048,1024]{2,1,0:T(8,128)(2,1)} custom-call(bf16[2,576,2048]{2,1,0:T(8,128)(2,1)} %get-tuple-element.170.refs_0_, bf16[2,576,2048]{2,1,0:T(8,128)(2,1)} %get-tuple-element.178.refs_3_.refs_0_.refs_1_, bf16[2,576,1024]{2,1,0:T(8,128)(2,1)} %get-tuple-element.218.refs_2_, bf16[2,576,1024]{2,1,0:T(8,128)(2,1)} %get-tuple-element.219.refs_3_, ...), custom_call_target="tpu_custom_call" | custom-call | flops 193273528320 | bytes 22544384 | tf_op jit(solution)/shard_map/weight_grad/pallas_call | solution.py:62
  595.8 18.3 %collective-permute-done.40 = bf16[256,2048]{1,0:T(8,128)(2,1)} collective-permute-done((bf16[256,2048]{1,0:T(8,128)(2,1)}, bf16[256,2048]{1,0:T(8,128)(2,1)}, u32[]{:S(2)}, u32[]{:S(2)}) %collective-permute-start.40) | collective-permute-done | bytes 1048608 | tf_op jit(solution)/shard_map/ppermute | solution.py:88
  615.9 10.9 %collective-permute-done.42 = bf16[256,2048]{1,0:T(8,128)(2,1)S(1)} collective-permute-done((bf16[256,2048]{1,0:T(8,128)(2,1)S(1)}, bf16[256,2048]{1,0:T(8,128)(2,1)S(1)}, u32[]{:S(2)}, u32[]{:S(2)}) %collective-permute-start.42) | collective-permute-done | bytes 1048608 | tf_op jit(solution)/shard_map/ppermute | solution.py:88
  634.7 7.7 out_back.1
  644.7 4.4 all-to-all-start.3
  656.1 19.1 %all-to-all-done.3 = bf16[256,4,512]{2,0,1:T(8,128)(2,1)} async-done(((bf16[256,4,512]{2,0,1:T(8,128)(2,1)}), bf16[256,4,512]{2,0,1:T(8,128)(2,1)}, u32[]{:S(2)}, u32[]{:S(2)}) %all-to-all-start.3) | async-done | bytes 1048608 | tf_op jit(solution)/shard_map/all_to_all | solution.py:946
  675.2 4.2 all-to-all-start.4
  680.3 23.2 %attend_back.1 = (f32[1024,512]{1,0:T(8,128)}, f32[1024,512]{1,0:T(8,128)}, bf16[1024,512]{1,0:T(8,128)(2,1)}, f32[16,1024]{1,0:T(8,128)}, f32[1,512]{1,0:T(1,128)}, /*index=5*/f32[1,512]{1,0:T(1,128)}) custom-call(bf16[1024,512]{1,0:T(8,128)(2,1)} %get-tuple-element.228.q_ref, bf16[1024,512]{1,0:T(8,128)(2,1)} %get-tuple-element.229.k_ref, ...), custom_call_target="tpu_custom_call" | custom-call | flops 75161927680 | bytes 14823424 | tf_op jit(solution)/shard_map/attend_back/pallas_call | solution.py:62
  715.4 10.0 %vo_grads.1 = (bf16[256,1024]{1,0:T(8,128)(2,1)}, bf16[256,1024]{1,0:T(8,128)(2,1)}, bf16[256,1024]{1,0:T(8,128)(2,1)}, bf16[256,1024]{1,0:T(8,128)(2,1)}, bf16[...) custom-call(s32[12]{0:T(128)} %pad_add_fusion.ids.refs_0_, ...), custom_call_target="tpu_custom_call" | custom-call | flops 85899345920 | bytes 14680064 | tf_op jit(solution)/shard_map/vo_grads/pallas_call | solution.py:62
  727.4 14.0 %qk_back.1 = (bf16[272,1024]{1,0:T(8,128)(2,1)}, bf16[272,1024]{1,0:T(8,128)(2,1)}, bf16[272,1024]{1,0:T(8,128)(2,1)}, bf16[272,1024]{1,0:T(8,128)(2,1)}, bf16[2...) custom-call(s32[12]{0:T(128)} %pad_add_fusion.ids.refs_0_, ...), custom_call_target="tpu_custom_call" | custom-call | flops 85899345920 | bytes 19423232 | tf_op jit(solution)/shard_map/qk_back/pallas_call | solution.py:62
  745.7 11.7 %d_h.1 = bf16[1024,2048]{1,0:T(8,128)(2,1)} custom-call(bf16[1024,1024]{1,0:T(8,128)(2,1)} %get-tuple-element.240.d_ref, bf16[1024,512]{1,0:T(8,128)(2,1)} %get-tuple-element.238.dv_ref, bf16[2048,1024]{1,0:T(8,128)(2,1)} %get-tuple-element.241.qk_ref, bf16[2048,512]{1,0:T(8,128)(2,1)} %get-tuple-element.242.v_ref), custom_call_target="tpu_custom_call" | custom-call | flops 128849018880 | bytes 13631488 | tf_op jit(solution)/shard_map/d_h/pallas_call | solution.py:62
  763.3 28.1 %collective-permute-done.47 = bf16[256,2048]{1,0:T(8,128)(2,1)} collective-permute-done((bf16[256,2048]{1,0:T(8,128)(2,1)S(1)}, bf16[256,2048]{1,0:T(8,128)(2,1)}, u32[]{:S(2)}, u32[]{:S(2)}) %collective-permute-start.47) | collective-permute-done | bytes 1048608 | tf_op jit(solution)/shard_map/ppermute | solution.py:88
  801.2 10.2 %collective-permute-done.59 = bf16[272,1024]{1,0:T(8,128)(2,1)S(1)} collective-permute-done((bf16[272,1024]{1,0:T(8,128)(2,1)S(1)}, bf16[272,1024]{1,0:T(8,128)(2,1)S(1)}, u32[]{:S(2)}, u32[]{:S(2)}) %collective-permute-start.59) | collective-permute-done | bytes 557088 | tf_op jit(solution)/shard_map/ppermute | solution.py:88
  812.3 12.5 %collective-permute-done.69 = bf16[256,1024]{1,0:T(8,128)(2,1)S(1)} collective-permute-done((bf16[256,1024]{1,0:T(8,128)(2,1)S(1)}, bf16[256,1024]{1,0:T(8,128)(2,1)S(1)}, u32[]{:S(2)}, u32[]{:S(2)}) %collective-permute-start.69) | collective-permute-done | bytes 524320 | tf_op jit(solution)/shard_map/ppermute | solution.py:88
  829.9 22.5 %collective-permute-done.56 = bf16[272,1024]{1,0:T(8,128)(2,1)S(1)} collective-permute-done((bf16[272,1024]{1,0:T(8,128)(2,1)S(1)}, bf16[272,1024]{1,0:T(8,128)(2,1)S(1)}, u32[]{:S(2)}, u32[]{:S(2)}) %collective-permute-start.56) | collective-permute-done | bytes 557088 | tf_op jit(solution)/shard_map/ppermute | solution.py:88
  852.4 11.9 %collective-permute-done.60 = bf16[272,1024]{1,0:T(8,128)(2,1)S(1)} collective-permute-done((bf16[272,1024]{1,0:T(8,128)(2,1)S(1)}, bf16[272,1024]{1,0:T(8,128)(2,1)S(1)}, u32[]{:S(2)}, u32[]{:S(2)}) %collective-permute-start.60) | collective-permute-done | bytes 557088 | tf_op jit(solution)/shard_map/ppermute | solution.py:88
  867.6 6.8 collective-permute-done.66
  880.1 21.4 %collective-permute-done.72.refs_11_ = bf16[256,1024]{1,0:T(8,128)(2,1)} collective-permute-done((bf16[256,1024]{1,0:T(8,128)(2,1)}, bf16[256,1024]{1,0:T(8,128)(2,1)}, u32[]{:S(2)}, u32[]{:S(2)}) %collective-permute-start.72) | collective-permute-done | bytes 524320 | tf_op jit(solution)/shard_map/ppermute | solution.py:92
  904.9 4.6 fusion.5.refs_16_
  909.6 4.1 convert_element_type.380.refs_13_
  913.7 4.1 convert_element_type.381.refs_14_
  921.9 7.9 finish.1
  (416 shorter events, 236.2 us)
Async XLA Ops:
  7.3 101.7 %all-gather.6.cloned.1.call-start = ((), (), s32[]{:S(2)}) async-start(), calls=%async_computation.12 | async-start | bytes 5242880 | tf_op jit(solution)/shard_map/all_gather | solution.py:782
  17.9 61.5 %all-to-all-start = ((bf16[8,48,256]{2,1,0:T(8,128)(2,1)}), bf16[8,48,256]{2,1,0:T(8,128)(2,1)S(1)}, u32[]{:S(2)}, u32[]{:S(2)}) async-start(bf16[8,48,256]{2,1,0:T(8,128)(2,1)} %broadcast_in_dim.59), calls=%async_computation | async-start | bytes 393216 | tf_op jit(solution)/shard_map/all_to_all | solution.py:770
  121.1 42.1 %collective-permute-start.11 = (bf16[256,1024]{1,0:T(8,128)(2,1)}, bf16[256,1024]{1,0:T(8,128)(2,1)S(1)}, u32[]{:S(2)}, u32[]{:S(2)}) collective-permute-start(bf16[256,1024]{1,0:T(8,128)(2,1)} %collective-permute-done.7.refs_3_), channel_id=1, source_target_pairs={{0,2},{1,3},{2,0},{3,1},{4,6},{5,7},{6,4},{7,5},{8,10},{9,11},{10,... | collective-permute-start | bytes 1572872 | tf_op jit(solution)/shard_map/ppermute | solution.py:88
  159.8 72.2 %collective-permute-start.22 = (bf16[256,2048]{1,0:T(8,128)(2,1)S(1)}, bf16[256,2048]{1,0:T(8,128)(2,1)}, u32[]{:S(2)}, u32[]{:S(2)}) collective-permute-start(bf16[256,2048]{1,0:T(8,128)(2,1)S(1)} %bitcast.135), channel_id=1, source_target_pairs={{0,1},{1,0},{2,3},{3,2},{4,5},{5,4},{6,7},{7,6},{8,9},{9,8},{10,11... | collective-permute-start | bytes 3145736 | tf_op jit(solution)/shard_map/ppermute | solution.py:88
  160.9 71.7 %collective-permute-start.20 = (bf16[256,2048]{1,0:T(8,128)(2,1)S(1)}, bf16[256,2048]{1,0:T(8,128)(2,1)}, u32[]{:S(2)}, u32[]{:S(2)}) collective-permute-start(bf16[256,2048]{1,0:T(8,128)(2,1)S(1)} %bitcast.136), channel_id=1, source_target_pairs={{0,2},{1,3},{2,0},{3,1},{4,6},{5,7},{6,4},{7,5},{8,10},{9,11},{10,... | collective-permute-start | bytes 3145736 | tf_op jit(solution)/shard_map/ppermute | solution.py:88
  161.2 69.6 %collective-permute-start.28 = (bf16[256,2048]{1,0:T(8,128)(2,1)S(1)}, bf16[256,2048]{1,0:T(8,128)(2,1)S(1)}, u32[]{:S(2)}, u32[]{:S(2)}) collective-permute-start(bf16[256,2048]{1,0:T(8,128)(2,1)S(1)} %bitcast.137), channel_id=1, source_target_pairs={{0,4},{1,5},{2,6},{3,7},{4,0},{5,1},{6,2},{7,3},{8,12},{9,13},{10,... | collective-permute-start | bytes 3145736 | tf_op jit(solution)/shard_map/ppermute | solution.py:88
  172.4 61.1 %collective-permute-start.18 = (bf16[2048,512]{1,0:T(8,128)(2,1)}, bf16[2048,512]{1,0:T(8,128)(2,1)}, u32[]{:S(2)}, u32[]{:S(2)}) collective-permute-start(bf16[2048,512]{1,0:T(8,128)(2,1)} %get-tuple-element.163.refs_4_.refs_2_), channel_id=1, source_target_pairs={{0,16},{8,24},{16,0},{24,8},{1,17},{9,25},{17,1},{25,9},{2,18},{10... | collective-permute-start | bytes 6291464 | tf_op jit(solution)/shard_map/ppermute | solution.py:92
  191.1 38.5 %all-to-all-start.1 = ((bf16[4,256,512]{2,1,0:T(8,128)(2,1)}), bf16[4,256,512]{2,1,0:T(8,128)(2,1)S(1)}, u32[]{:S(2)}, u32[]{:S(2)}) async-start(bf16[4,256,512]{2,1,0:T(8,128)(2,1)} %bitcast.138), calls=%async_computation.1 | async-start | bytes 2097152 | tf_op jit(solution)/shard_map/all_to_all | solution.py:852
  194.6 520.8 %all-gather.4.cloned.1.call-start = ((), (), s32[]{:S(2)}) async-start(), calls=%async_computation.8 | async-start | bytes 5242880 | tf_op jit(solution)/shard_map/all_gather | solution.py:857
  197.2 86.1 %collective-permute-start.17 = (bf16[2048,512]{1,0:T(8,128)(2,1)}, bf16[2048,512]{1,0:T(8,128)(2,1)}, u32[]{:S(2)}, u32[]{:S(2)}) collective-permute-start(bf16[2048,512]{1,0:T(8,128)(2,1)} %get-tuple-element.163.refs_4_.refs_2_), channel_id=1, source_target_pairs={{0,8},{8,0},{16,24},{24,16},{1,9},{9,1},{17,25},{25,17},{2,10},{10... | collective-permute-start | bytes 6291464 | tf_op jit(solution)/shard_map/ppermute | solution.py:92
  230.8 66.2 %collective-permute-start.31 = (bf16[256,2048]{1,0:T(8,128)(2,1)S(1)}, bf16[256,2048]{1,0:T(8,128)(2,1)}, u32[]{:S(2)}, u32[]{:S(2)}) collective-permute-start(bf16[256,2048]{1,0:T(8,128)(2,1)S(1)} %collective-permute-done.28.refs_1_), channel_id=1, source_target_pairs={{0,1},{1,0},{2,3},{3,2},{4,5},{5,4},{6,7},{7,6},{8,9},{9,8},{10,11... | collective-permute-start | bytes 3145736 | tf_op jit(solution)/shard_map/ppermute | solution.py:88
  232.6 46.9 %collective-permute-start.21 = (bf16[256,2048]{1,0:T(8,128)(2,1)}, bf16[256,2048]{1,0:T(8,128)(2,1)}, u32[]{:S(2)}, u32[]{:S(2)}) collective-permute-start(bf16[256,2048]{1,0:T(8,128)(2,1)} %collective-permute-done.20.refs_1_), channel_id=1, source_target_pairs={{0,1},{1,0},{2,3},{3,2},{4,5},{5,4},{6,7},{7,6},{8,9},{9,8},{10,11... | collective-permute-start | bytes 3145736 | tf_op jit(solution)/shard_map/ppermute | solution.py:88
  233.5 49.8 %collective-permute-start.19 = (bf16[2048,512]{1,0:T(8,128)(2,1)}, bf16[2048,512]{1,0:T(8,128)(2,1)S(1)}, u32[]{:S(2)}, u32[]{:S(2)}) collective-permute-start(bf16[2048,512]{1,0:T(8,128)(2,1)} %collective-permute-done.18.refs_6_.refs_4_), channel_id=1, source_target_pairs={{0,8},{8,0},{16,24},{24,16},{1,9},{9,1},{17,25},{25,17},{2,10},{10... | collective-permute-start | bytes 6291464 | tf_op jit(solution)/shard_map/ppermute | solution.py:92
  254.2 47.8 %collective-permute-start.30 = (bf16[256,2048]{1,0:T(8,128)(2,1)}, bf16[256,2048]{1,0:T(8,128)(2,1)}, u32[]{:S(2)}, u32[]{:S(2)}) collective-permute-start(bf16[256,2048]{1,0:T(8,128)(2,1)} %collective-permute-done.29.refs_1_), channel_id=1, source_target_pairs={{0,1},{1,0},{2,3},{3,2},{4,5},{5,4},{6,7},{7,6},{8,9},{9,8},{10,11... | collective-permute-start | bytes 3145736 | tf_op jit(solution)/shard_map/ppermute | solution.py:88
  293.4 43.4 %collective-permute-start.27 = (bf16[256,2048]{1,0:T(8,128)(2,1)}, bf16[256,2048]{1,0:T(8,128)(2,1)S(1)}, u32[]{:S(2)}, u32[]{:S(2)}) collective-permute-start(bf16[256,2048]{1,0:T(8,128)(2,1)} %get-tuple-element.166.refs_0_), channel_id=1, source_target_pairs={{0,1},{1,0},{2,3},{3,2},{4,5},{5,4},{6,7},{7,6},{8,9},{9,8},{10,11... | collective-permute-start | bytes 3145736 | tf_op jit(solution)/shard_map/ppermute | solution.py:88
  294.5 39.6 %collective-permute-start.23 = (bf16[256,2048]{1,0:T(8,128)(2,1)}, bf16[256,2048]{1,0:T(8,128)(2,1)S(1)}, u32[]{:S(2)}, u32[]{:S(2)}) collective-permute-start(bf16[256,2048]{1,0:T(8,128)(2,1)} %get-tuple-element.166.refs_0_), channel_id=1, source_target_pairs={{0,2},{1,3},{2,0},{3,1},{4,6},{5,7},{6,4},{7,5},{8,10},{9,11},{10,... | collective-permute-start | bytes 3145736 | tf_op jit(solution)/shard_map/ppermute | solution.py:88
  295.1 41.7 %collective-permute-start.25 = (bf16[256,2048]{1,0:T(8,128)(2,1)}, bf16[256,2048]{1,0:T(8,128)(2,1)}, u32[]{:S(2)}, u32[]{:S(2)}) collective-permute-start(bf16[256,2048]{1,0:T(8,128)(2,1)} %get-tuple-element.166.refs_0_), channel_id=1, source_target_pairs={{0,4},{1,5},{2,6},{3,7},{4,0},{5,1},{6,2},{7,3},{8,12},{9,13},{10,... | collective-permute-start | bytes 3145736 | tf_op jit(solution)/shard_map/ppermute | solution.py:88
  358.9 49.2 %collective-permute-start.33 = (bf16[256,2048]{1,0:T(8,128)(2,1)}, bf16[256,2048]{1,0:T(8,128)(2,1)}, u32[]{:S(2)}, u32[]{:S(2)}) collective-permute-start(bf16[256,2048]{1,0:T(8,128)(2,1)} %collective-permute-done.25.refs_1_), channel_id=1, source_target_pairs={{0,1},{1,0},{2,3},{3,2},{4,5},{5,4},{6,7},{7,6},{8,9},{9,8},{10,11... | collective-permute-start | bytes 3145736 | tf_op jit(solution)/shard_map/ppermute | solution.py:88
  359.9 52.7 %collective-permute-start.32 = (bf16[256,2048]{1,0:T(8,128)(2,1)}, bf16[256,2048]{1,0:T(8,128)(2,1)}, u32[]{:S(2)}, u32[]{:S(2)}) collective-permute-start(bf16[256,2048]{1,0:T(8,128)(2,1)} %collective-permute-done.26.refs_1_), channel_id=1, source_target_pairs={{0,1},{1,0},{2,3},{3,2},{4,5},{5,4},{6,7},{7,6},{8,9},{9,8},{10,11... | collective-permute-start | bytes 3145736 | tf_op jit(solution)/shard_map/ppermute | solution.py:88
  425.0 44.7 %collective-permute-start.35 = (bf16[256,2048]{1,0:T(8,128)(2,1)}, bf16[256,2048]{1,0:T(8,128)(2,1)}, u32[]{:S(2)}, u32[]{:S(2)}) collective-permute-start(bf16[256,2048]{1,0:T(8,128)(2,1)} %get-tuple-element.185.refs_9_.refs_7_), channel_id=1, source_target_pairs={{0,1},{1,0},{2,3},{3,2},{4,5},{5,4},{6,7},{7,6},{8,9},{9,8},{10,11... | collective-permute-start | bytes 3145736 | tf_op jit(solution)/shard_map/ppermute | solution.py:88
  425.9 46.4 %collective-permute-start.34 = (bf16[256,2048]{1,0:T(8,128)(2,1)}, bf16[256,2048]{1,0:T(8,128)(2,1)}, u32[]{:S(2)}, u32[]{:S(2)}) collective-permute-start(bf16[256,2048]{1,0:T(8,128)(2,1)} %get-tuple-element.183.refs_7_.refs_5_), channel_id=1, source_target_pairs={{0,1},{1,0},{2,3},{3,2},{4,5},{5,4},{6,7},{7,6},{8,9},{9,8},{10,11... | collective-permute-start | bytes 3145736 | tf_op jit(solution)/shard_map/ppermute | solution.py:88
  492.3 417.3 %reduce-scatter.4.cloned.1.call-start = ((), (), s32[]{:S(2)}) async-start(), calls=%async_computation.9 | async-start | bytes 10485760 | tf_op jit(solution)/shard_map/reduce_scatter | solution.py:924
  492.3 40.2 %collective-permute-start.37 = (bf16[256,2048]{1,0:T(8,128)(2,1)}, bf16[256,2048]{1,0:T(8,128)(2,1)}, u32[]{:S(2)}, u32[]{:S(2)}) collective-permute-start(bf16[256,2048]{1,0:T(8,128)(2,1)} %get-tuple-element.194.refs_11_), channel_id=1, source_target_pairs={{0,1},{1,0},{2,3},{3,2},{4,5},{5,4},{6,7},{7,6},{8,9},{9,8},{10,11... | collective-permute-start | bytes 3145736 | tf_op jit(solution)/shard_map/ppermute | solution.py:88
  494.2 41.0 %collective-permute-start.36 = (bf16[256,2048]{1,0:T(8,128)(2,1)}, bf16[256,2048]{1,0:T(8,128)(2,1)}, u32[]{:S(2)}, u32[]{:S(2)}) collective-permute-start(bf16[256,2048]{1,0:T(8,128)(2,1)} %get-tuple-element.192.refs_9_), channel_id=1, source_target_pairs={{0,1},{1,0},{2,3},{3,2},{4,5},{5,4},{6,7},{7,6},{8,9},{9,8},{10,11... | collective-permute-start | bytes 3145736 | tf_op jit(solution)/shard_map/ppermute | solution.py:88
  541.8 371.9 %reduce-scatter.6.cloned.1.call-start = ((), (), s32[]{:S(2)}) async-start(), calls=%async_computation.10 | async-start | bytes 10485760 | tf_op jit(solution)/shard_map/reduce_scatter | solution.py:924
  566.8 47.4 %collective-permute-start.40 = (bf16[256,2048]{1,0:T(8,128)(2,1)}, bf16[256,2048]{1,0:T(8,128)(2,1)}, u32[]{:S(2)}, u32[]{:S(2)}) collective-permute-start(bf16[256,2048]{1,0:T(8,128)(2,1)} %get-tuple-element.210.refs_9_.refs_14_), channel_id=1, source_target_pairs={{0,1},{1,0},{2,3},{3,2},{4,5},{5,4},{6,7},{7,6},{8,9},{9,8},{10,11... | collective-permute-start | bytes 3145736 | tf_op jit(solution)/shard_map/ppermute | solution.py:88
  567.3 81.8 %collective-permute-start.39 = (bf16[256,2048]{1,0:T(8,128)(2,1)}, bf16[256,2048]{1,0:T(8,128)(2,1)}, u32[]{:S(2)}, u32[]{:S(2)}) collective-permute-start(bf16[256,2048]{1,0:T(8,128)(2,1)} %get-tuple-element.208.refs_7_.refs_12_), channel_id=1, source_target_pairs={{0,1},{1,0},{2,3},{3,2},{4,5},{5,4},{6,7},{7,6},{8,9},{9,8},{10,11... | collective-permute-start | bytes 3145736 | tf_op jit(solution)/shard_map/ppermute | solution.py:88
  568.8 83.4 %collective-permute-start.38 = (bf16[256,2048]{1,0:T(8,128)(2,1)}, bf16[256,2048]{1,0:T(8,128)(2,1)}, u32[]{:S(2)}, u32[]{:S(2)}) collective-permute-start(bf16[256,2048]{1,0:T(8,128)(2,1)} %get-tuple-element.206.refs_5_.refs_10_), channel_id=1, source_target_pairs={{0,1},{1,0},{2,3},{3,2},{4,5},{5,4},{6,7},{7,6},{8,9},{9,8},{10,11... | collective-permute-start | bytes 3145736 | tf_op jit(solution)/shard_map/ppermute | solution.py:88
  588.0 38.8 %collective-permute-start.42 = (bf16[256,2048]{1,0:T(8,128)(2,1)S(1)}, bf16[256,2048]{1,0:T(8,128)(2,1)S(1)}, u32[]{:S(2)}, u32[]{:S(2)}) collective-permute-start(bf16[256,2048]{1,0:T(8,128)(2,1)S(1)} %copy-done.14), channel_id=1, source_target_pairs={{0,2},{1,3},{2,0},{3,1},{4,6},{5,7},{6,4},{7,5},{8,10},{9,11},{10,... | collective-permute-start | bytes 3145736 | tf_op jit(solution)/shard_map/ppermute | solution.py:88
  591.7 38.9 %collective-permute-start.44 = (bf16[256,2048]{1,0:T(8,128)(2,1)S(1)}, bf16[256,2048]{1,0:T(8,128)(2,1)S(1)}, u32[]{:S(2)}, u32[]{:S(2)}) collective-permute-start(bf16[256,2048]{1,0:T(8,128)(2,1)S(1)} %add_convert_fusion.2), channel_id=1, source_target_pairs={{0,4},{1,5},{2,6},{3,7},{4,0},{5,1},{6,2},{7,3},{8,12},{9,13},{10,... | collective-permute-start | bytes 3145736 | tf_op jit(solution)/shard_map/ppermute | solution.py:88
  649.1 268.7 %reduce-scatter.8.cloned.1.call-start = ((), (), s32[]{:S(2)}) async-start(), calls=%async_computation.11 | async-start | bytes 10485760 | tf_op jit(solution)/shard_map/reduce_scatter | solution.py:924
  675.2 40.2 %all-to-all-start.4 = ((bf16[256,4,512]{2,0,1:T(8,128)(2,1)}), bf16[256,4,512]{2,0,1:T(8,128)(2,1)}, u32[]{:S(2)}, u32[]{:S(2)}) async-start(bf16[256,4,512]{2,0,1:T(8,128)(2,1)} %bitcast.122), calls=%async_computation.4 | async-start | bytes 2097152 | tf_op jit(solution)/shard_map/all_to_all | solution.py:947
  679.4 34.6 %collective-permute-start.46 = (bf16[256,2048]{1,0:T(8,128)(2,1)S(1)}, bf16[256,2048]{1,0:T(8,128)(2,1)S(1)}, u32[]{:S(2)}, u32[]{:S(2)}) collective-permute-start(bf16[256,2048]{1,0:T(8,128)(2,1)S(1)} %add_convert_fusion.3), channel_id=1, source_target_pairs={{0,2},{1,3},{2,0},{3,1},{4,6},{5,7},{6,4},{7,5},{8,10},{9,11},{10,... | collective-permute-start | bytes 3145736 | tf_op jit(solution)/shard_map/ppermute | solution.py:88
  705.6 56.1 %collective-permute-start.45 = (bf16[256,2048]{1,0:T(8,128)(2,1)}, bf16[256,2048]{1,0:T(8,128)(2,1)}, u32[]{:S(2)}, u32[]{:S(2)}) collective-permute-start(bf16[256,2048]{1,0:T(8,128)(2,1)} %add_convert_fusion.5), channel_id=1, source_target_pairs={{0,2},{1,3},{2,0},{3,1},{4,6},{5,7},{6,4},{7,5},{8,10},{9,11},{10,... | collective-permute-start | bytes 3145736 | tf_op jit(solution)/shard_map/ppermute | solution.py:88
  726.6 69.3 %collective-permute-start.68 = (bf16[256,1024]{1,0:T(8,128)(2,1)}, bf16[256,1024]{1,0:T(8,128)(2,1)}, u32[]{:S(2)}, u32[]{:S(2)}) collective-permute-start(bf16[256,1024]{1,0:T(8,128)(2,1)} %get-tuple-element.239.refs_9_), channel_id=1, source_target_pairs={{0,2},{1,3},{2,0},{3,1},{4,6},{5,7},{6,4},{7,5},{8,10},{9,11},{10,... | collective-permute-start | bytes 1572872 | tf_op jit(solution)/shard_map/ppermute | solution.py:88
  743.0 48.5 %collective-permute-start.47 = (bf16[256,2048]{1,0:T(8,128)(2,1)S(1)}, bf16[256,2048]{1,0:T(8,128)(2,1)}, u32[]{:S(2)}, u32[]{:S(2)}) collective-permute-start(bf16[256,2048]{1,0:T(8,128)(2,1)S(1)} %copy-done.20), channel_id=1, source_target_pairs={{0,4},{1,5},{2,6},{3,7},{4,0},{5,1},{6,2},{7,3},{8,12},{9,13},{10,... | collective-permute-start | bytes 3145736 | tf_op jit(solution)/shard_map/ppermute | solution.py:88
  757.5 54.7 %collective-permute-start.67 = (bf16[256,1024]{1,0:T(8,128)(2,1)}, bf16[256,1024]{1,0:T(8,128)(2,1)S(1)}, u32[]{:S(2)}, u32[]{:S(2)}) collective-permute-start(bf16[256,1024]{1,0:T(8,128)(2,1)} %get-tuple-element.258), channel_id=1, source_target_pairs={{0,2},{1,3},{2,0},{3,1},{4,6},{5,7},{6,4},{7,5},{8,10},{9,11},{10,... | collective-permute-start | bytes 1572872 | tf_op jit(solution)/shard_map/ppermute | solution.py:88
  759.8 37.5 %collective-permute-start.55 = (bf16[272,1024]{1,0:T(8,128)(2,1)}, bf16[272,1024]{1,0:T(8,128)(2,1)S(1)}, u32[]{:S(2)}, u32[]{:S(2)}) collective-permute-start(bf16[272,1024]{1,0:T(8,128)(2,1)} %get-tuple-element.248), channel_id=1, source_target_pairs={{0,1},{1,0},{2,3},{3,2},{4,5},{5,4},{6,7},{7,6},{8,9},{9,8},{10,11... | collective-permute-start | bytes 1671176 | tf_op jit(solution)/shard_map/ppermute | solution.py:88
  761.8 39.3 %collective-permute-start.57 = (bf16[272,1024]{1,0:T(8,128)(2,1)}, bf16[272,1024]{1,0:T(8,128)(2,1)S(1)}, u32[]{:S(2)}, u32[]{:S(2)}) collective-permute-start(bf16[272,1024]{1,0:T(8,128)(2,1)} %get-tuple-element.250), channel_id=1, source_target_pairs={{0,1},{1,0},{2,3},{3,2},{4,5},{5,4},{6,7},{7,6},{8,9},{9,8},{10,11... | collective-permute-start | bytes 1671176 | tf_op jit(solution)/shard_map/ppermute | solution.py:88
  801.1 65.8 %collective-permute-start.64 = (bf16[256,1024]{1,0:T(8,128)(2,1)S(1)}, bf16[256,1024]{1,0:T(8,128)(2,1)S(1)}, u32[]{:S(2)}, u32[]{:S(2)}) collective-permute-start(bf16[256,1024]{1,0:T(8,128)(2,1)S(1)} %copy-done.65), channel_id=1, source_target_pairs={{0,2},{1,3},{2,0},{3,1},{4,6},{5,7},{6,4},{7,5},{8,10},{9,11},{10,... | collective-permute-start | bytes 1572872 | tf_op jit(solution)/shard_map/ppermute | solution.py:88
  812.2 40.2 %collective-permute-start.56 = (bf16[272,1024]{1,0:T(8,128)(2,1)S(1)}, bf16[272,1024]{1,0:T(8,128)(2,1)S(1)}, u32[]{:S(2)}, u32[]{:S(2)}) collective-permute-start(bf16[272,1024]{1,0:T(8,128)(2,1)S(1)} %add_convert_fusion.15), channel_id=1, source_target_pairs={{0,2},{1,3},{2,0},{3,1},{4,6},{5,7},{6,4},{7,5},{8,10},{9,11},{10,... | collective-permute-start | bytes 1671176 | tf_op jit(solution)/shard_map/ppermute | solution.py:88
  824.7 39.6 %collective-permute-start.60 = (bf16[272,1024]{1,0:T(8,128)(2,1)S(1)}, bf16[272,1024]{1,0:T(8,128)(2,1)S(1)}, u32[]{:S(2)}, u32[]{:S(2)}) collective-permute-start(bf16[272,1024]{1,0:T(8,128)(2,1)S(1)} %add_convert_fusion.12), channel_id=1, source_target_pairs={{0,4},{1,5},{2,6},{3,7},{4,0},{5,1},{6,2},{7,3},{8,12},{9,13},{10,... | collective-permute-start | bytes 1671176 | tf_op jit(solution)/shard_map/ppermute | solution.py:88
  825.0 49.3 %collective-permute-start.66 = (bf16[256,1024]{1,0:T(8,128)(2,1)S(1)}, bf16[256,1024]{1,0:T(8,128)(2,1)S(1)}, u32[]{:S(2)}, u32[]{:S(2)}) collective-permute-start(bf16[256,1024]{1,0:T(8,128)(2,1)S(1)} %add_convert_fusion.20), channel_id=1, source_target_pairs={{0,4},{1,5},{2,6},{3,7},{4,0},{5,1},{6,2},{7,3},{8,12},{9,13},{10,... | collective-permute-start | bytes 1572872 | tf_op jit(solution)/shard_map/ppermute | solution.py:88
  828.0 46.3 %collective-permute-start.70 = (bf16[256,1024]{1,0:T(8,128)(2,1)S(1)}, bf16[256,1024]{1,0:T(8,128)(2,1)S(1)}, u32[]{:S(2)}, u32[]{:S(2)}) collective-permute-start(bf16[256,1024]{1,0:T(8,128)(2,1)S(1)} %add_convert_fusion.18), channel_id=1, source_target_pairs={{0,1},{1,0},{2,3},{3,2},{4,5},{5,4},{6,7},{7,6},{8,9},{9,8},{10,11... | collective-permute-start | bytes 1572872 | tf_op jit(solution)/shard_map/ppermute | solution.py:88
  852.4 49.1 %collective-permute-start.51 = (bf16[256,2048]{1,0:T(8,128)(2,1)}, bf16[256,2048]{1,0:T(8,128)(2,1)}, u32[]{:S(2)}, u32[]{:S(2)}) collective-permute-start(bf16[256,2048]{1,0:T(8,128)(2,1)} %get-tuple-element.269), channel_id=1, source_target_pairs={{0,8},{8,0},{16,24},{24,16},{1,9},{9,1},{17,25},{25,17},{2,10},{10... | collective-permute-start | bytes 3145736 | tf_op jit(solution)/shard_map/ppermute | solution.py:92
  864.3 37.7 %collective-permute-start.53 = (bf16[256,2048]{1,0:T(8,128)(2,1)}, bf16[256,2048]{1,0:T(8,128)(2,1)}, u32[]{:S(2)}, u32[]{:S(2)}) collective-permute-start(bf16[256,2048]{1,0:T(8,128)(2,1)} %fusion.7), channel_id=1, source_target_pairs={{0,16},{8,24},{16,0},{24,8},{1,17},{9,25},{17,1},{25,9},{2,18},{10... | collective-permute-start | bytes 3145736 | tf_op jit(solution)/shard_map/ppermute | solution.py:92
  867.0 35.0 %collective-permute-start.62 = (bf16[272,1024]{1,0:T(8,128)(2,1)}, bf16[272,1024]{1,0:T(8,128)(2,1)}, u32[]{:S(2)}, u32[]{:S(2)}) collective-permute-start(bf16[272,1024]{1,0:T(8,128)(2,1)} %add_convert_fusion.11.refs_5_), channel_id=1, source_target_pairs={{0,16},{8,24},{16,0},{24,8},{1,17},{9,25},{17,1},{25,9},{2,18},{10... | collective-permute-start | bytes 1671176 | tf_op jit(solution)/shard_map/ppermute | solution.py:92
  880.0 41.8 %collective-permute-start.71 = (bf16[256,1024]{1,0:T(8,128)(2,1)}, bf16[256,1024]{1,0:T(8,128)(2,1)}, u32[]{:S(2)}, u32[]{:S(2)}) collective-permute-start(bf16[256,1024]{1,0:T(8,128)(2,1)} %add_convert_fusion.17.refs_9_), channel_id=1, source_target_pairs={{0,8},{8,0},{16,24},{24,16},{1,9},{9,1},{17,25},{25,17},{2,10},{10... | collective-permute-start | bytes 1572872 | tf_op jit(solution)/shard_map/ppermute | solution.py:92
  (112 other events, 1964.9 us)
Sparse Core Ops, SparseCore 0:
  9.6 37.1 all-gather.5
  230.9 33.6 all-gather.3
  541.9 72.9 reduce-scatter.3
  617.5 96.9 reduce-scatter.5
  717.0 71.7 reduce-scatter.7

commit v6 on v5

--- a/solution.py
+++ b/solution.py
@@ -73,7 +73,7 @@
         cost_estimate=pl.CostEstimate(flops=int(COVER * flops), bytes_accessed=int(moved), transcendentals=0),
         name=name,
     )(*scalars, *args)
-    return result[0] if single else result
+    return result[0] if single else list(result)
 
 
 def like(shape, dtype):
@@ -136,13 +136,6 @@
     return own.astype(F32) + swap(near, 2).astype(F32) + swap(far, 4).astype(F32)
 
 
-def scatter_x_last(pieces, n_ep):
-    if n_ep != 8:
-        return scatter(pieces, n_ep)
-    kept, sent = scatter_z(*pieces[0::2]), scatter_z(*pieces[1::2])
-    return kept + swap(sent.astype(BF16), 1).astype(F32)
-
-
 def scatter(pieces, n_ep):
     if n_ep != 8:
         stacked = jnp.stack(pieces)
@@ -150,6 +143,30 @@
     return scatter_z(*crossed_sums(pieces))
 
 
+def stack_at(piece, n_ep):
+    if n_ep != 8:
+        return 0, piece
+    return 2 * (piece % 2) + (piece // 2) % 2, piece // 4
+
+
+def stack_shapes(n_ep, shape):
+    return [like((2, *shape), BF16)] * 4 if n_ep == 8 else [like((n_ep, *shape), BF16)]
+
+
+def scatter_stacks(stacks, n_ep):
+    if n_ep != 8:
+        total = lax.psum_scatter(stacks[0], "ep", scatter_dimension=0, tiled=False)
+        return total.astype(F32), None
+    even, odd, even_sent, odd_sent = stacks
+    odd = plus(odd, swap(odd_sent, 1))
+    even = even.astype(F32) + swap(even_sent, 1).astype(F32) + swap(odd, 2).astype(F32)
+    return even[0], even[1].astype(BF16)
+
+
+def last_hop(total, far):
+    return total if far is None else total + swap(far, 4).astype(F32)
+
+
 def gather_sp(value):
     over = swap_sp(value, 2)
     return [value, swap_sp(value, 1), over, swap_sp(over, 1)]
@@ -165,76 +182,49 @@
     return pl.ds(pl.multiple_of(ids[position] * size, size), size)
 
 
-def qk_kernel(count, ids, x_ref, gain_ref, *refs):
-    pieces, (q_ref, k_ref, squares_ref, w_ref, h_ref) = refs[:count], refs[count:]
+def qkv_kernel(count, ids, x_ref, gain_ref, *refs):
+    pieces, refs = refs[:count], refs[count:]
+    q_ref, k_ref, v_ref, squares_ref, w_ref, out_ref, h_ref = refs
     shard = pieces[0].shape[0]
+    width = q_ref.shape[1]
 
     @pl.when(pl.program_id(0) == 0)
     def _():
         for k in range(count):
-            w_ref[block_at(ids, k, shard), :] = pieces[k][...]
+            rows = block_at(ids, k, shard)
+            w_ref[rows, :] = pieces[k][:, : 3 * width]
+            out_ref[rows, :] = pieces[k][:, 3 * width :]
 
     x_rows = x_ref[...].astype(F32)
     scale = lax.rsqrt(jnp.mean(x_rows * x_rows, axis=1, keepdims=True) + EPS)
     h_ref[...] = (x_rows * scale * gain_ref[...]).astype(BF16)
-    width = q_ref.shape[1]
     for at, ref in enumerate((q_ref, k_ref)):
         part = product(h_ref[...], w_ref[:, at * width : (at + 1) * width])
         ref[...] = part
         squares_ref[8 * at : 8 * at + 8, :] = row_sums(part * part)
-
-
-def qk_project(ids, x_all, gain, pieces):
+    v_ref[...] = product(h_ref[...], w_ref[:, 2 * width :]).astype(BF16)
+
+
+def qkv_project(ids, x_all, gain, pieces):
     total, depth = x_all.shape
-    shard, both = pieces[0].shape
-    width = both // 2
+    width = pieces[0].shape[1] // 4
     rows = min(256, total)
     block = pl.BlockSpec((rows, width), lambda i, ids: (i, 0))
     wide = pl.BlockSpec((rows, depth), lambda i, ids: (i, 0))
     return call(
-        functools.partial(qk_kernel, len(pieces)),
+        functools.partial(qkv_kernel, len(pieces)),
         [like((total, width), F32)] * 2
-        + [like((16, total), F32), like((depth, both), BF16), like((total, depth), BF16)],
+        + [like((total, width), BF16), like((16, total), F32), like((depth, 3 * width), BF16)]
+        + [like((depth, width), BF16), like((total, depth), BF16)],
         [x_all, gain, *pieces],
-        2 * total * depth * both,
-        "qk_project",
+        6 * total * depth * width,
+        "qkv_project",
         scalars=(ids,),
         grid=(total // rows,),
         in_specs=[wide] + [None] * (len(pieces) + 1),
-        out_specs=[block, block, pl.BlockSpec((16, rows), lambda i, ids: (0, i)), None, wide],
-    )
-
-
-def v_kernel(count, ids, h_ref, *refs):
-    pieces, (v_ref, w_ref, out_ref) = refs[:count], refs[count:]
-    shard = pieces[0].shape[0]
-    width = v_ref.shape[1]
-
-    @pl.when(pl.program_id(0) == 0)
-    def _():
-        for k in range(count):
-            rows = block_at(ids, k, shard)
-            w_ref[rows, :] = pieces[k][:, :width]
-            out_ref[rows, :] = pieces[k][:, width:]
-
-    v_ref[...] = product(h_ref[...], w_ref[...]).astype(BF16)
-
-
-def v_project(ids, h_all, pieces, after):
-    total, depth = h_all.shape
-    width = pieces[0].shape[1] // 2
-    rows = min(256, total)
-    return call(
-        functools.partial(v_kernel, len(pieces)),
-        [like((total, width), BF16), like((depth, width), BF16), like((depth, width), BF16)],
-        [h_all, *pieces],
-        2 * total * depth * width,
-        "v_project",
-        after=after,
-        scalars=(ids,),
-        grid=(total // rows,),
-        in_specs=[pl.BlockSpec((rows, depth), lambda i, ids: (i, 0))] + [None] * len(pieces),
-        out_specs=[pl.BlockSpec((rows, width), lambda i, ids: (i, 0)), None, None],
+        out_specs=[
+            block, block, block, pl.BlockSpec((16, rows), lambda i, ids: (0, i)), None, None, wide,
+        ],
     )
 
 
@@ -283,21 +273,21 @@
     )
 
 
-def vo_grads_kernel(count, ids, h_ref, dv_ref, attn_ref, dz_ref, *pieces):
-    shard = pieces[0].shape[0]
+def vo_grads_kernel(count, shard, ids, h_ref, dv_ref, attn_ref, dz_ref, *stacks):
     width = dv_ref.shape[1]
     for k in range(count):
         block = block_at(ids, k, shard)
-        pieces[k][:, :width] = product_left(h_ref[:, block], dv_ref[...]).astype(BF16)
-        pieces[k][:, width:] = product_left(attn_ref[:, block], dz_ref[...]).astype(BF16)
+        array, place = stack_at(k, count)
+        stacks[array][place, :, :width] = product_left(h_ref[:, block], dv_ref[...]).astype(BF16)
+        stacks[array][place, :, width:] = product_left(attn_ref[:, block], dz_ref[...]).astype(BF16)
 
 
 def vo_grads(ids, count, h_all, d_v, attn_all, d_z_cols):
     shard = h_all.shape[1] // count
     width = d_v.shape[1]
     return call(
-        functools.partial(vo_grads_kernel, count),
-        [like((shard, 2 * width), BF16)] * count,
+        functools.partial(vo_grads_kernel, count, shard),
+        stack_shapes(count, (shard, 2 * width)),
         [h_all, d_v, attn_all, d_z_cols],
         4 * h_all.size * width,
         "vo_grads",
@@ -306,27 +296,28 @@
 
 
 def qk_back_kernel(
-    count, width_all, ids, h_ref, dqn_ref, dkn_ref, qr_ref, kr_ref, scale_ref, sums_ref,
-    tiny_ref, *refs
+    count, shard, ids, h_ref, dqn_ref, dkn_ref, qr_ref, kr_ref, scale_ref, sums_ref, tiny_ref, *refs
 ):
-    pieces, d_ref = refs[:count], refs[count]
+    stacks, d_ref = refs[:-1], refs[-1]
     width = dqn_ref.shape[1]
     scales = jnp.transpose(scale_ref[...])
-    means = jnp.transpose(sums_ref[...]) * (1.0 / width_all)
+    means = jnp.transpose(sums_ref[...]) * (1.0 / h_ref.shape[1])
     for at, (d_normed, raw) in enumerate(((dqn_ref, qr_ref), (dkn_ref, kr_ref))):
         scale, mean = scales[:, 8 * at : 8 * at + 1], means[:, 8 * at : 8 * at + 1]
         d_ref[:, at * width : (at + 1) * width] = (
             scale * (d_normed[...] - raw[...] * scale * mean)
         ).astype(BF16)
-    shard = h_ref.shape[1] // count
     per_row = 2 * width // shard
+    extra = stacks[0].shape[1] - shard
     for k in range(count):
         block = block_at(ids, k, shard)
-        pieces[k][:shard, :] = product_left(h_ref[:, block], d_ref[...]).astype(BF16)
-        pieces[k][shard:, :] = jnp.zeros_like(pieces[k][shard:, :])
+        array, place = stack_at(k, count)
+        ref = stacks[array]
+        ref[place, :shard, :] = product_left(h_ref[:, block], d_ref[...]).astype(BF16)
+        ref[place, shard:, :] = jnp.zeros((extra, 2 * width), BF16)
         for at in range(tiny_ref.shape[0]):
             row, col = shard + at // per_row, (at % per_row) * shard
-            pieces[k][row : row + 1, col : col + shard] = tiny_ref[at : at + 1, block].astype(BF16)
+            ref[place, row : row + 1, col : col + shard] = tiny_ref[at : at + 1, block].astype(BF16)
 
 
 def qk_back(ids, count, h_all, d_qn, d_kn, q_raw, k_raw, scales, sums, tiny, after):
@@ -336,8 +327,8 @@
     extra = -(-tiny.shape[0] // (2 * width // shard))
     extra = -(-extra // 16) * 16
     return call(
-        functools.partial(qk_back_kernel, count, depth),
-        [like((shard + extra, 2 * width), BF16)] * count + [like((total, 2 * width), BF16)],
+        functools.partial(qk_back_kernel, count, shard),
+        stack_shapes(count, (shard + extra, 2 * width)) + [like((total, 2 * width), BF16)],
         [h_all, d_qn, d_kn, q_raw, k_raw, scales, sums, tiny],
         2 * h_all.size * 2 * width,
         "qk_back",
@@ -346,29 +337,33 @@
     )
 
 
-def d_h_kernel(d_ref, dv_ref, qk_ref, v_ref, out_ref):
-    out_ref[...] = (
-        product_right(d_ref[...], qk_ref[...]) + product_right(dv_ref[...], v_ref[...])
+def d_h_kernel(ids, d_ref, dv_ref, w_ref, out_ref):
+    both = d_ref.shape[1]
+    out_ref[0] = (
+        product_right(d_ref[...], w_ref[:, :both]) + product_right(dv_ref[...], w_ref[:, both:])
     ).astype(BF16)
 
 
-def d_h_rows(d_qk, d_v, w_qk, w_v, after):
+def d_h_rows(ids, n_ep, n_sp, d_qk, d_v, w_qkv):
     total, wide = d_qk.shape
-    depth = w_qk.shape[0]
-    rows = min(256, total)
+    depth = w_qkv.shape[0]
+    rows = total // n_sp
+
+    def partner(j, ids):
+        return ids[n_ep + (j % 2) * 2 + j // 2], 0
+
     return call(
         d_h_kernel,
-        like((total, depth), BF16),
-        [d_qk, d_v, w_qk, w_v],
+        like((n_sp, rows, depth), BF16),
+        [d_qk, d_v, w_qkv],
         3 * d_qk.size * depth,
         "d_h",
-        after=after,
-        grid=(total // rows,),
+        scalars=(ids,),
+        grid=(n_sp,),
         in_specs=[
-            pl.BlockSpec((rows, wide), lambda i: (i, 0)),
-            pl.BlockSpec((rows, d_v.shape[1]), lambda i: (i, 0)), None, None,
+            pl.BlockSpec((rows, wide), partner), pl.BlockSpec((rows, d_v.shape[1]), partner), None,
         ],
-        out_specs=[pl.BlockSpec((rows, depth), lambda i: (i, 0))],
+        out_specs=[pl.BlockSpec((1, rows, depth), lambda j, ids: (j, 0, 0))],
     )
 
 
@@ -694,6 +689,32 @@
     )
 
 
+def combine_stacks_kernel(count, local, cap, group, places_ref, *refs):
+    groups = count // group
+    for k in range(count):
+        rows = refs[k // group]
+        at = (k % group) * cap
+        total = None
+        for e in range(local):
+            chosen = chooser(places_ref, k * local + e, cap).astype(BF16)
+            part = product_left(chosen, rows[e, at : at + cap, :])
+            total = part if total is None else total + part
+        array, place = stack_at(k, count)
+        refs[groups + array][place] = total.astype(BF16)
+
+
+def combine_stacks(places, rows, count, local, cap, group, after):
+    tokens, width = places.shape[1], rows[0].shape[2]
+    return call(
+        functools.partial(combine_stacks_kernel, count, local, cap, group),
+        stack_shapes(count, (tokens, width)),
+        [places, *rows],
+        2 * count * local * cap * tokens * width,
+        "combine_stacks",
+        after=after,
+    )
+
+
 def weight_grad_kernel(groups, *refs):
     lefts, rights = refs[:groups], refs[groups : 2 * groups]
     total = None
@@ -780,33 +801,18 @@
     picked_all = by_piece(picked_all)
 
     x_all = lax.all_gather(tokens[0], "sp", axis=0, tiled=True)
-    qk_own = jnp.concatenate([own_columns(w_query), own_columns(w_key)], axis=1)
-    vo_own = jnp.concatenate([own_columns(w_value), own_columns(w_out)], axis=1)
+    w_own = jnp.concatenate([own_columns(w) for w in (w_query, w_key, w_value, w_out)], axis=1)
     cot_own = cotangent[0]
     if n_ep == 8:
-        own_x, near, far = swap(qk_own, 1), swap(qk_own, 2), swap(qk_own, 4)
-        own_x, near, far = tie(own_x, near, far)
-        farther = swap(far, 2)
-        farther, vo_own = tie(farther, vo_own)
-        near_x, far_x, farther_x = swap(near, 1), swap(far, 1), swap(farther, 1)
-        near_x, far_x, farther_x, vo_own_x = tie(near_x, far_x, farther_x, vo_own)
-        qk_pieces = [qk_own, own_x, near, near_x, far, far_x, farther, farther_x]
-        vo_blocks = along_z(vo_own)
-        vo_crossed, vo_blocks[2] = tie(swap(vo_own_x, 1), vo_blocks[2])
-        vo_blocks[3] = swap(vo_blocks[2], 2)
-        vo_crossed, vo_blocks[1], vo_blocks[3] = tie(vo_crossed, vo_blocks[1], vo_blocks[3])
-        q_raw, k_raw, squares, w_qk, h_all = qk_project(ids, x_all, gains[0:1], qk_pieces)
-        vo_crossed, squares = tie(vo_crossed, squares)
-        vo_others = along_z(vo_crossed)
-        vo_pieces = [piece for two in zip(vo_blocks, vo_others) for piece in two]
-        vo_pieces[7], cot_own = tie(vo_pieces[7], cot_own)
+        blocks_z = along_z(w_own)
+        blocks_z[3], cot_own = tie(blocks_z[3], cot_own)
         cot_blocks = along_z(cot_own)
+        w_pieces = across_x(blocks_z)
+        w_pieces[7], cot_blocks[0], cot_blocks[1] = tie(w_pieces[7], cot_blocks[0], cot_blocks[1])
         cot_pieces = across_x(cot_blocks)
     else:
-        qk_pieces, vo_pieces, cot_pieces = (
-            gather_whole(value) for value in (qk_own, vo_own, cot_own)
-        )
-        q_raw, k_raw, squares, w_qk, h_all = qk_project(ids, x_all, gains[0:1], qk_pieces)
+        w_pieces, cot_pieces = gather_whole(w_own), gather_whole(cot_own)
+
     upper = (
         jnp.arange(tok_dev, dtype=jnp.int32)[:, None] < jnp.arange(tok_dev, dtype=jnp.int32)[None, :]
     ).astype(BF16)
@@ -829,8 +835,8 @@
     sine = jnp.concatenate([-jnp.sin(angles), jnp.sin(angles)], axis=1)
     starts = starts[:, None].astype(jnp.int32)
 
+    q_raw, k_raw, v_low, squares, w_qkv, w_o, h_all = qkv_project(ids, x_all, gains[0:1], w_pieces)
     scales = lax.rsqrt(sum_sp(squares) / width + EPS)
-    v_low, w_v, w_o = v_project(ids, h_all, vo_pieces, [q_raw])
     w_o_parts = gather_sp(w_o)
     gain_q, gain_k = own_columns(gains)[1:2], own_columns(gains)[2:3]
     q_rot, k_rot, mixed = attend(
@@ -850,9 +856,9 @@
         return d_rows
 
     attn_tok = lax.all_to_all(mixed, "sp", split_axis=0, concat_axis=1, tiled=True)
-    near_rows = cot_rows(0, [mixed])
+    near_rows = cot_rows(0, [])
     x_one, h2_low = out_project(
-        ids, n_ep, attn_tok, tokens[0], gains[3:4], w_o_parts, [near_rows]
+        ids, n_ep, attn_tok, tokens[0], gains[3:4], w_o_parts, []
     )
     attn_all = lax.all_gather(attn_tok, "sp", axis=0, tiled=True)
 
@@ -902,23 +908,12 @@
     d_gates = lax.all_to_all(d_gates, "ep", split_axis=0, concat_axis=0, tiled=True)
     d_gates = d_gates.reshape(expert_count, tok_dev)
     grad_gate = weight_grad(ins, d_gate_rows, [grad_down, d_gates])
-    mix_pieces = []
-    for g, (_, _, made) in enumerate(groups):
-        for at in range(group // 2):
-            mix_pieces += combine(
-                pair_places(g * group + 2 * at), made[4], 2, local, cap, at, None,
-                [grad_gate, *d_sums],
-            )
-    if n_ep == 8:
-        *d_sums, mix_pieces[1], mix_pieces[3], mix_pieces[5], mix_pieces[7] = tie(
-            *d_sums, mix_pieces[1], mix_pieces[3], mix_pieces[5], mix_pieces[7]
-        )
-        mix_pieces[0], grad_down, grad_gate = tie(mix_pieces[0], grad_down, grad_gate)
-        mix_sums = crossed_sums(mix_pieces)
-        d_h2 = scatter_z(*d_sums)
-    else:
-        d_h2 = scatter(d_pieces, n_ep)
-    grad_up = weight_grad(ins, d_up_rows, mix_pieces)
+    mix_stacks = combine_stacks(
+        places, [made[4] for _, _, made in groups], n_ep, local, cap, group, [grad_gate, *d_sums]
+    )
+    mix_stacks[0], grad_down, grad_gate = tie(mix_stacks[0], grad_down, grad_gate)
+    d_h2 = scatter_z(*d_sums) if n_ep == 8 else scatter(d_pieces, n_ep)
+    grad_up = weight_grad(ins, d_up_rows, mix_stacks[:1])
 
     def over_sp(value):
         return lax.psum_scatter(value, "sp", scatter_dimension=1, tiled=True).astype(F32)
@@ -942,25 +937,20 @@
         d_normed - one_normed * jnp.mean(d_normed * one_normed, axis=-1, keepdims=True)
     )
     d_z, grad_up = tie(d_one.astype(BF16), grad_up)
-    d_attn = out_back(ids, n_ep, d_z, w_o_parts, [grad_up, grad_gate, grad_down, *mix_pieces])
+    d_attn = out_back(ids, n_ep, d_z, w_o_parts, [])
     d_heads = lax.all_to_all(d_attn, "sp", split_axis=1, concat_axis=0, tiled=True)
     d_z_cols = lax.all_to_all(d_z, "sp", split_axis=1, concat_axis=0, tiled=True)
+    mix, mix_far = scatter_stacks(mix_stacks, n_ep)
     if n_ep == 8:
-        *mix_sums, d_heads = tie(*mix_sums, d_heads)
+        mix, mix_far, d_heads = tie(mix, mix_far, d_heads)
     grad_down, grad_gate, grad_up = over_sp(grad_down), over_sp(grad_gate), over_sp(grad_up)
 
     d_qn, d_kn, d_v, sums, grad_qg, grad_kg = attend_back(
         q_rot, k_rot, v_low, d_heads, q_raw, k_raw, scales, gain_q, gain_k, cosine, sine, starts
     )
-    if n_ep == 8:
-        own, near, far, farther = mix_sums
-        far, d_v = tie(plus(far, swap(farther, 2)), d_v)
-        mix = own.astype(F32) + swap(near, 2).astype(F32) + swap(far, 4).astype(F32)
-    else:
-        mix = scatter(mix_pieces, n_ep)
-    output = (x_one + mix).astype(BF16)
-    vo_pieces = vo_grads(ids, n_ep, h_all, d_v, attn_all, d_z_cols)
-    grad_vo = scatter_x_last(vo_pieces, n_ep).astype(BF16)
+    output = (x_one + last_hop(mix, mix_far)).astype(BF16)
+    vo_stacks = vo_grads(ids, n_ep, h_all, d_v, attn_all, d_z_cols)
+    grad_vo = last_hop(*scatter_stacks(vo_stacks, n_ep)).astype(BF16)
 
     def placed(value):
         return lax.dynamic_update_slice_in_dim(
@@ -970,20 +960,15 @@
     tiny = jnp.concatenate(
         [placed(grad_qg), placed(grad_kg), grad_ffn[None], grad_router], axis=0
     )
-    *qk_pieces, d_qk = qk_back(
-        ids, n_ep, h_all, d_qn, d_kn, q_raw, k_raw, scales, sum_sp(sums), tiny, vo_pieces[-1:]
-    )
-    grad_qk = scatter(qk_pieces, n_ep).astype(BF16)
-
-    d_h = d_h_rows(d_qk, d_v, w_qk, w_v, [])
+    *qk_stacks, d_qk = qk_back(
+        ids, n_ep, h_all, d_qn, d_kn, q_raw, k_raw, scales, sum_sp(sums), tiny, vo_stacks[:1]
+    )
+    grad_qk = last_hop(*scatter_stacks(qk_stacks, n_ep)).astype(BF16)
+
+    d_h = d_h_rows(ids, n_ep, n_sp, d_qk, d_v, w_qkv)
     output, d_h = tie(output, d_h)
-    d_h = d_h.reshape(n_sp, tok_dev, width)
-    parts = [
-        lax.dynamic_index_in_dim(d_h, partners[j], 0, keepdims=False) for j in range(4)
-    ]
-    kept = plus(parts[0], swap_sp(parts[1], 1))
-    sent = plus(parts[2], swap_sp(parts[3], 1))
-    d_h = kept.astype(F32) + swap_sp(sent, 2).astype(F32)
+    halves = plus(d_h[:2], swap_sp(d_h[2:], 1))
+    d_h = halves[0].astype(F32) + swap_sp(halves[1], 2).astype(F32)
     x_rows = tokens[0].astype(F32)
     x_scale = lax.rsqrt(jnp.mean(x_rows * x_rows, axis=-1, keepdims=True) + EPS)
     x_normed = x_rows * x_scale

time: 951 us -> 886 us (0.932)
  waiting for transfers between devices: 384 us -> 357 us
  starting transfers between devices: 91.6 us -> 71 us
    all_to_all x1, waiting for transfers between devices: 32 us -> 8.64 us  [body(): lax.all_to_all(mixed, 'sp', split_axis=0, concat_axis=1, tiled=True)]
    ppermute x56 -> x40, waiting for transfers between devices: 303 us -> 326 us  [swap(): return lax.ppermute(value, 'ep', [(i, i ^ bits) for i in range(8)])]
    ppermute x56 -> x40, starting transfers between devices: 61.2 us -> 41.6 us  [swap(): return lax.ppermute(value, 'ep', [(i, i ^ bits) for i in range(8)])]
    all_to_all x1, waiting for transfers between devices: 19.1 us -> 0.01 us  [body(): lax.all_to_all(d_attn, 'sp', split_axis=1, concat_axis=0, tiled=True)]
    convert_element_type x16 -> x8, other arithmetic: 28.7 us -> 19.1 us  [plus(): return (left.astype(F32) + right.astype(F32)).astype(left.dtype)]
    pallas_call x31 -> x27, Pallas kernels: 327 us -> 319 us  [call(): pl.pallas_call(kernel, grid_spec=pltpu.PrefetchScalarGridSpec(num_scalar_...]
    ppermute x18 -> x17, waiting for transfers between devices: 28.4 us -> 21.4 us  [swap_sp(): return lax.ppermute(value, 'sp', [(i, i ^ bits) for i in range(4)])]
  transfers between devices with their start and end apart: 84 -> 67, of which waited for: 34 -> 24; matrix products, arithmetic and copies ran while one was open for 10% -> 10% of each run, Pallas kernels for 33% -> 36%
where the time goes in v6:
time: 886 us; the launch traced here: 876 us
  waiting for transfers between devices  357 us (40%)
  Pallas kernels  319 us (36%)
  starting transfers between devices  71 us (8%)
  other arithmetic  61.4 us (7%)
  local copies, waits for them, and re-layouts  32.5 us (4%)
  between operations  30.8 us (3%)
    ppermute x40, waiting for transfers between devices, swap(): return lax.ppermute(value, 'ep', [(i, i ^ bits) for i in range(8)])  326 us
    pallas_call x27, Pallas kernels, call(): pl.pallas_call(kernel, grid_spec=pltpu.PrefetchScalarGridSpec(num_scalar_...  319 us
    ppermute x40, starting transfers between devices, swap(): return lax.ppermute(value, 'ep', [(i, i ^ bits) for i in range(8)])  41.6 us
    ppermute x17, waiting for transfers between devices, swap_sp(): return lax.ppermute(value, 'sp', [(i, i ^ bits) for i in range(4)])  21.4 us
    convert_element_type x8, other arithmetic, plus(): return (left.astype(F32) + right.astype(F32)).astype(left.dtype)  19.1 us
  transfers between devices with their start and end apart: 67, of which 24 were waited for; matrix products, arithmetic and copies ran while one was open for 10% of the time, Pallas kernels for 36%

profile of v6, /device:TPU:0, one launch (start us, length us, event | category | flops | bytes accessed | tf_op | source)
XLA Modules:
  0.0 876.2 jit_solution(5931967669914843435)
XLA Ops:
  26.1 40.3 %collective-permute-done.3.refs_4_ = bf16[256,2048]{1,0:T(8,128)(2,1)} collective-permute-done((bf16[256,2048]{1,0:T(8,128)(2,1)}, bf16[256,2048]{1,0:T(8,128)(2,1)}, u32[]{:S(2)}, u32[]{:S(2)}) %collective-permute-start.3) | collective-permute-done | bytes 1048608 | tf_op jit(solution)/shard_map/ppermute | solution.py:88
  90.4 62.4 %collective-permute-done.6.refs_7_ = bf16[256,2048]{1,0:T(8,128)(2,1)S(1)} collective-permute-done((bf16[256,2048]{1,0:T(8,128)(2,1)}, bf16[256,2048]{1,0:T(8,128)(2,1)S(1)}, u32[]{:S(2)}, u32[]{:S(2)}) %collective-permute-start.6) | collective-permute-done | bytes 1048608 | tf_op jit(solution)/shard_map/ppermute | solution.py:88
  154.4 17.0 %qkv_project.1 = (f32[1024,512]{1,0:T(8,128)}, f32[1024,512]{1,0:T(8,128)}, bf16[1024,512]{1,0:T(8,128)(2,1)}, f32[16,1024]{1,0:T(8,128)}, bf16[2048,1536]{1,0:T...) custom-call(s32[12]{0:T(128)} %pad_add_fusion.ids.refs_0_, bf16[1024,2048]{1,0:T(8,128)(2,1)} %bitcast.177, ...), custom_call_target="tpu_custom_call" | custom-call | flops 128849018880 | bytes 30482432 | tf_op jit(solution)/shard_map/qkv_project/pallas_call | solution.py:62
  175.8 17.6 %collective-permute-done.21.refs_1_ = bf16[256,2048]{1,0:T(8,128)(2,1)} collective-permute-done((bf16[256,2048]{1,0:T(8,128)(2,1)S(1)}, bf16[256,2048]{1,0:T(8,128)(2,1)}, u32[]{:S(2)}, u32[]{:S(2)}) %collective-permute-start.21) | collective-permute-done | bytes 1048608 | tf_op jit(solution)/shard_map/ppermute | solution.py:88
  195.9 3.9 dispatch.10.refs_3_
  199.8 19.0 %collective-permute-done.22.refs_1_ = bf16[256,2048]{1,0:T(8,128)(2,1)} collective-permute-done((bf16[256,2048]{1,0:T(8,128)(2,1)}, bf16[256,2048]{1,0:T(8,128)(2,1)}, u32[]{:S(2)}, u32[]{:S(2)}) %collective-permute-start.22) | collective-permute-done | bytes 1048608 | tf_op jit(solution)/shard_map/ppermute | solution.py:88
  222.5 17.2 %attend.1 = (bf16[1024,512]{1,0:T(8,128)(2,1)}, bf16[1024,512]{1,0:T(8,128)(2,1)}, bf16[1024,512]{1,0:T(8,128)(2,1)}) custom-call(f32[1024,512]{1,0:T(8,128)} %get-tuple-element.105.qr_ref.refs_4_, f32[1024,512]{1,0:T(8,128)} %get-tuple-element.106.kr_ref.refs_5_, bf16[1024,512]{1,0:T(8,128)(2,1)} %get-tuple-element.107.v_ref, ...), custom_call_target="tpu_custom_call" | custom-call | flops 32212254720 | bytes 9510912 | tf_op jit(solution)/shard_map/attend/pallas_call | solution.py:62
  245.2 3.8 dispatch.11.refs_1_.refs_6_.refs_10_.refs_2_
  249.0 8.6 all-to-all-done.1
  258.8 9.2 %out_project.1 = (f32[256,2048]{1,0:T(8,128)}, bf16[256,2048]{1,0:T(8,128)(2,1)}) custom-call(s32[12]{0:T(128)} %pad_add_fusion.ids.refs_0_, bf16[256,2048]{1,0:T(8,128)(2,1)} %bitcast.141, bf16[256,2048]{1,0:T(8,128)(2,1)} %bitcast.134, f32[1,2048]{1,0:T(1,128)} %bitcast.154, bf16[2048,512]{1,0:T(8,128)(2,1)} %get-tuple-element.110.refs_0_, ...), custom_call_target="tpu_custom_call" | custom-call | flops 42949672960 | bytes 13639680 | tf_op jit(solution)/shard_map/out_project/pallas_call | solution.py:62
  273.5 16.7 %collective-permute-done.23.refs_2_ = bf16[256,2048]{1,0:T(8,128)(2,1)} collective-permute-done((bf16[256,2048]{1,0:T(8,128)(2,1)}, bf16[256,2048]{1,0:T(8,128)(2,1)}, u32[]{:S(2)}, u32[]{:S(2)}) %collective-permute-start.23) | collective-permute-done | bytes 1048608 | tf_op jit(solution)/shard_map/ppermute | solution.py:88
  290.1 3.8 dispatch.13.refs_7_.refs_1_.refs_11_.refs_3_
  293.9 19.1 %collective-permute-done.14.refs_0_ = bf16[256,2048]{1,0:T(8,128)(2,1)S(1)} collective-permute-done((bf16[256,2048]{1,0:T(8,128)(2,1)}, bf16[256,2048]{1,0:T(8,128)(2,1)S(1)}, u32[]{:S(2)}, u32[]{:S(2)}) %collective-permute-start.14) | collective-permute-done | bytes 1048608 | tf_op jit(solution)/shard_map/ppermute | solution.py:88
  317.3 4.4 dispatch.8
  321.8 15.5 %collective-permute-done.15.refs_1_ = bf16[256,2048]{1,0:T(8,128)(2,1)S(1)} collective-permute-done((bf16[256,2048]{1,0:T(8,128)(2,1)S(1)}, bf16[256,2048]{1,0:T(8,128)(2,1)S(1)}, u32[]{:S(2)}, u32[]{:S(2)}) %collective-permute-start.15) | collective-permute-done | bytes 1048608 | tf_op jit(solution)/shard_map/ppermute | solution.py:88
  342.4 4.5 dispatch.9
  346.9 42.5 %experts.2 = (bf16[2,576,1024]{2,1,0:T(8,128)(2,1)}, bf16[2,576,1024]{2,1,0:T(8,128)(2,1)}, bf16[2,576,1024]{2,1,0:T(8,128)(2,1)}, f32[2,576,1]{2,1,0:T(8,128)},...) custom-call(bf16[2,576,2048]{2,1,0:T(8,128)(2,1)} %get-tuple-element.116.refs_0_, ...), custom_call_target="tpu_custom_call" | custom-call | flops 579820584960 | bytes 51127296 | tf_op jit(solution)/shard_map/experts/pallas_call | solution.py:62
  389.4 4.5 dispatch.14
  393.9 4.5 dispatch.15
  398.4 4.0 combine.4
  402.4 4.0 combine.5
  408.4 42.6 %experts.3 = (bf16[2,576,1024]{2,1,0:T(8,128)(2,1)}, bf16[2,576,1024]{2,1,0:T(8,128)(2,1)}, bf16[2,576,1024]{2,1,0:T(8,128)(2,1)}, f32[2,576,1]{2,1,0:T(8,128)},...) custom-call(bf16[2,576,2048]{2,1,0:T(8,128)(2,1)} %get-tuple-element.126.refs_3_.refs_0_.refs_1_, ...), custom_call_target="tpu_custom_call" | custom-call | flops 579820584960 | bytes 51127296 | tf_op jit(solution)/shard_map/experts/pallas_call | solution.py:62
  456.3 3.9 combine.6
  460.2 4.0 combine.7
  469.5 3.9 all-to-all-start.2
  475.5 18.4 %weight_grad.3.refs_4_ = bf16[2,1024,2048]{2,1,0:T(8,128)(2,1)} custom-call(bf16[2,576,1024]{2,1,0:T(8,128)(2,1)} %get-tuple-element.136.refs_0_, bf16[2,576,1024]{2,1,0:T(8,128)(2,1)} %get-tuple-element.137.refs_1_, bf16[2,576,2048]{2,1,0:T(8,128)(2,1)} %dispatch.11.refs_1_.refs_6_.refs_10_.refs_2_, ...), custom_call_target="tpu_custom_call" | custom-call | flops 193273528320 | bytes 22544384 | tf_op jit(solution)/shard_map/weight_grad/pallas_call | solution.py:62
  495.2 4.7 collective-permute-done.30
  504.3 18.4 %weight_grad.4.refs_3_ = bf16[2,2048,1024]{2,1,0:T(8,128)(2,1)} custom-call(bf16[2,576,2048]{2,1,0:T(8,128)(2,1)} %get-tuple-element.116.refs_0_, bf16[2,576,2048]{2,1,0:T(8,128)(2,1)} %get-tuple-element.126.refs_3_.refs_0_.refs_1_, bf16[2,576,1024]{2,1,0:T(8,128)(2,1)} %get-tuple-element.134.refs_2_, bf16[2,576,1024]{2,1,0:T(8,128)(2,1)} %get-tuple-element.135.refs_3_, ...), custom_call_target="tpu_custom_call" | custom-call | flops 193273528320 | bytes 22544384 | tf_op jit(solution)/shard_map/weight_grad/pallas_call | solution.py:62
  526.3 10.4 %combine_stacks.1 = (bf16[2,256,2048]{2,1,0:T(8,128)(2,1)}, bf16[2,256,2048]{2,1,0:T(8,128)(2,1)}, bf16[2,256,2048]{2,1,0:T(8,128)(2,1)}, bf16[2,256,2048]{2,1,0:T(8,128)(2,1)}) custom-call(s32[16,256]{1,0:T(8,128)} %copy-done.41, bf16[2,576,2048]{2,1,0:T(8,128)(2,1)} %get-tuple-element.120.refs_1_, bf16[2,576,2048]{2,1,0:T(8,128)(2,1)} %get-tuple-element.133.refs_2_, ...), custom_call_target="tpu_custom_call" | custom-call | flops 48318382080 | bytes 17842176 | tf_op jit(solution)/shard_map/combine_stacks/pallas_call | solution.py:62
  545.1 19.7 %weight_grad.5 = bf16[2,2048,1024]{2,1,0:T(8,128)(2,1)} custom-call(bf16[2,576,2048]{2,1,0:T(8,128)(2,1)} %get-tuple-element.116.refs_0_, bf16[2,576,2048]{2,1,0:T(8,128)(2,1)} %get-tuple-element.126.refs_3_.refs_0_.refs_1_, bf16[2,576,1024]{2,1,0:T(8,128)(2,1)} %get-tuple-element.154.refs_2_, bf16[2,576,1024]{2,1,0:T(8,128)(2,1)} %get-tuple-element.155.refs_3_, ...), custom_call_target="tpu_custom_call" | custom-call | flops 193273528320 | bytes 22544384 | tf_op jit(solution)/shard_map/weight_grad/pallas_call | solution.py:62
  564.8 10.7 %collective-permute-done.34 = bf16[256,2048]{1,0:T(8,128)(2,1)} collective-permute-done((bf16[256,2048]{1,0:T(8,128)(2,1)}, bf16[256,2048]{1,0:T(8,128)(2,1)}, u32[]{:S(2)}, u32[]{:S(2)}) %collective-permute-start.34) | collective-permute-done | bytes 1048608 | tf_op jit(solution)/shard_map/ppermute | solution.py:88
  575.5 7.0 collective-permute-done.36
  594.7 7.9 out_back.1
  609.7 15.3 %collective-permute-done.31 = bf16[2,256,2048]{2,1,0:T(8,128)(2,1)} collective-permute-done((bf16[2,256,2048]{2,1,0:T(8,128)(2,1)}, bf16[2,256,2048]{2,1,0:T(8,128)(2,1)}, u32[]{:S(2)}, u32[]{:S(2)}) %collective-permute-start.31) | collective-permute-done | bytes 2097184 | tf_op jit(solution)/shard_map/ppermute | solution.py:88
  638.3 23.2 %attend_back.1 = (f32[1024,512]{1,0:T(8,128)}, f32[1024,512]{1,0:T(8,128)}, bf16[1024,512]{1,0:T(8,128)(2,1)}, f32[16,1024]{1,0:T(8,128)}, f32[1,512]{1,0:T(1,128)}, /*index=5*/f32[1,512]{1,0:T(1,128)}) custom-call(bf16[1024,512]{1,0:T(8,128)(2,1)} %get-tuple-element.160.q_ref, bf16[1024,512]{1,0:T(8,128)(2,1)} %get-tuple-element.161.k_ref, ...), custom_call_target="tpu_custom_call" | custom-call | flops 75161927680 | bytes 14823424 | tf_op jit(solution)/shard_map/attend_back/pallas_call | solution.py:62
  666.3 10.5 %vo_grads.1 = (bf16[2,256,1024]{2,1,0:T(8,128)(2,1)}, bf16[2,256,1024]{2,1,0:T(8,128)(2,1)}, bf16[2,256,1024]{2,1,0:T(8,128)(2,1)}, bf16[2,256,1024]{2,1,0:T(8,128)(2,1)}) custom-call(s32[12]{0:T(128)} %pad_add_fusion.ids.refs_0_, bf16[1024,2048]{1,0:T(8,128)(2,1)} %get-tuple-element.159.h_ref.refs_1_, bf16[1024,512]{1,0:T(8,128)(2,1)} %get-tuple-element.168.dv_ref, ...), custom_call_target="tpu_custom_call" | custom-call | flops 85899345920 | bytes 14680064 | tf_op jit(solution)/shard_map/vo_grads/pallas_call | solution.py:62
  680.3 12.8 %qk_back.1 = (bf16[2,272,1024]{2,1,0:T(8,128)(2,1)}, bf16[2,272,1024]{2,1,0:T(8,128)(2,1)}, bf16[2,272,1024]{2,1,0:T(8,128)(2,1)}, bf16[2,272,1024]{2,1,0:T(8,128)(2,1)}, bf16[1024,1024]{1,0:T(8,128)(2,1)}) custom-call(s32[12]{0:T(128)} %pad_add_fusion.ids.refs_0_, bf16[1024,2048]{1,0:T(8,128)(2,1)} %get-tuple-element.159.h_ref.refs_1_, ...), custom_call_target="tpu_custom_call" | custom-call | flops 85899345920 | bytes 19423232 | tf_op jit(solution)/shard_map/qk_back/pallas_call | solution.py:62
  694.6 12.5 %d_h.1 = bf16[4,256,2048]{2,1,0:T(8,128)(2,1)} custom-call(s32[12]{0:T(128)} %pad_add_fusion.ids.refs_0_, bf16[1024,1024]{1,0:T(8,128)(2,1)} %get-tuple-element.170.d_ref, bf16[1024,512]{1,0:T(8,128)(2,1)} %get-tuple-element.168.dv_ref, bf16[2048,1536]{1,0:T(8,128)(2,1)} %get-tuple-element.171.w_ref), custom_call_target="tpu_custom_call" | custom-call | flops 128849018880 | bytes 13631488 | tf_op jit(solution)/shard_map/d_h/pallas_call | solution.py:62
  719.0 30.4 %collective-permute-done.44 = bf16[2,272,1024]{2,1,0:T(8,128)(2,1)S(1)} collective-permute-done((bf16[2,272,1024]{2,1,0:T(8,128)(2,1)}, bf16[2,272,1024]{2,1,0:T(8,128)(2,1)S(1)}, u32[]{:S(2)}, u32[]{:S(2)}) %collective-permute-start.44) | collective-permute-done | bytes 1114144 | tf_op jit(solution)/shard_map/ppermute | solution.py:88
  754.2 18.1 %collective-permute-done.43 = bf16[2,272,1024]{2,1,0:T(8,128)(2,1)S(1)} collective-permute-done((bf16[2,272,1024]{2,1,0:T(8,128)(2,1)S(1)}, bf16[2,272,1024]{2,1,0:T(8,128)(2,1)S(1)}, u32[]{:S(2)}, u32[]{:S(2)}) %collective-permute-start.43) | collective-permute-done | bytes 1114144 | tf_op jit(solution)/shard_map/ppermute | solution.py:88
  772.3 13.6 %collective-permute-done.45 = bf16[2,272,1024]{2,1,0:T(8,128)(2,1)S(1)} collective-permute-done((bf16[2,272,1024]{2,1,0:T(8,128)(2,1)S(1)}, bf16[2,272,1024]{2,1,0:T(8,128)(2,1)S(1)}, u32[]{:S(2)}, u32[]{:S(2)}) %collective-permute-start.45) | collective-permute-done | bytes 1114144 | tf_op jit(solution)/shard_map/ppermute | solution.py:88
  790.1 20.5 %collective-permute-done.46 = bf16[272,1024]{1,0:T(8,128)(2,1)S(1)} collective-permute-done((bf16[272,1024]{1,0:T(8,128)(2,1)S(1)}, bf16[272,1024]{1,0:T(8,128)(2,1)S(1)}, u32[]{:S(2)}, u32[]{:S(2)}) %collective-permute-start.46) | collective-permute-done | bytes 557088 | tf_op jit(solution)/shard_map/ppermute | solution.py:88
  816.3 21.4 %collective-permute-done.55.refs_11_ = bf16[256,1024]{1,0:T(8,128)(2,1)} collective-permute-done((bf16[256,1024]{1,0:T(8,128)(2,1)}, bf16[256,1024]{1,0:T(8,128)(2,1)}, u32[]{:S(2)}, u32[]{:S(2)}) %collective-permute-start.55) | collective-permute-done | bytes 524320 | tf_op jit(solution)/shard_map/ppermute | solution.py:92
  840.4 4.3 fusion.5.refs_16_
  844.7 4.1 convert_element_type.263.refs_13_
  848.9 4.1 convert_element_type.264.refs_14_
  852.9 4.1 convert_element_type.265.refs_15_
  857.0 7.9 finish.1
  (351 shorter events, 168.8 us)
Async XLA Ops:
  7.2 147.2 %all-gather.6.cloned.1.call-start = ((), (), s32[]{:S(2)}) async-start(), calls=%async_computation.12 | async-start | bytes 5242880 | tf_op jit(solution)/shard_map/all_gather | solution.py:803
  11.3 143.1 %collective-permute-start = (bf16[256,2048]{1,0:T(8,128)(2,1)}, bf16[256,2048]{1,0:T(8,128)(2,1)}, u32[]{:S(2)}, u32[]{:S(2)}) collective-permute-start(bf16[256,2048]{1,0:T(8,128)(2,1)} %pad_maximum_fusion.refs_0_), channel_id=1, source_target_pairs={{0,1},{1,0},{2,3},{3,2},{4,5},{5,4},{6,7},{7,6},{8,9},{9,8},{10,11... | collective-permute-start | bytes 3145736 | tf_op jit(solution)/shard_map/ppermute | solution.py:88
  14.2 71.7 %collective-permute-start.1 = (bf16[256,2048]{1,0:T(8,128)(2,1)}, bf16[256,2048]{1,0:T(8,128)(2,1)}, u32[]{:S(2)}, u32[]{:S(2)}) collective-permute-start(bf16[256,2048]{1,0:T(8,128)(2,1)} %pad_maximum_fusion.refs_0_), channel_id=1, source_target_pairs={{0,2},{1,3},{2,0},{3,1},{4,6},{5,7},{6,4},{7,5},{8,10},{9,11},{10,... | collective-permute-start | bytes 3145736 | tf_op jit(solution)/shard_map/ppermute | solution.py:88
  15.8 50.6 %collective-permute-start.3 = (bf16[256,2048]{1,0:T(8,128)(2,1)}, bf16[256,2048]{1,0:T(8,128)(2,1)}, u32[]{:S(2)}, u32[]{:S(2)}) collective-permute-start(bf16[256,2048]{1,0:T(8,128)(2,1)} %pad_maximum_fusion.refs_0_), channel_id=1, source_target_pairs={{0,4},{1,5},{2,6},{3,7},{4,0},{5,1},{6,2},{7,3},{8,12},{9,13},{10,... | collective-permute-start | bytes 3145736 | tf_op jit(solution)/shard_map/ppermute | solution.py:88
  19.8 65.3 %all-to-all-start = ((bf16[8,48,256]{2,1,0:T(8,128)(2,1)}), bf16[8,48,256]{2,1,0:T(8,128)(2,1)S(1)}, u32[]{:S(2)}, u32[]{:S(2)}) async-start(bf16[8,48,256]{2,1,0:T(8,128)(2,1)} %broadcast_in_dim.59), calls=%async_computation | async-start | bytes 393216 | tf_op jit(solution)/shard_map/all_to_all | solution.py:791
  85.3 69.1 %collective-permute-start.4 = (bf16[256,2048]{1,0:T(8,128)(2,1)}, bf16[256,2048]{1,0:T(8,128)(2,1)}, u32[]{:S(2)}, u32[]{:S(2)}) collective-permute-start(bf16[256,2048]{1,0:T(8,128)(2,1)} %collective-permute-done.3.refs_4_), channel_id=1, source_target_pairs={{0,1},{1,0},{2,3},{3,2},{4,5},{5,4},{6,7},{7,6},{8,9},{9,8},{10,11... | collective-permute-start | bytes 3145736 | tf_op jit(solution)/shard_map/ppermute | solution.py:88
  85.9 68.5 %collective-permute-start.2 = (bf16[256,2048]{1,0:T(8,128)(2,1)}, bf16[256,2048]{1,0:T(8,128)(2,1)}, u32[]{:S(2)}, u32[]{:S(2)}) collective-permute-start(bf16[256,2048]{1,0:T(8,128)(2,1)} %collective-permute-done.1.refs_2_), channel_id=1, source_target_pairs={{0,1},{1,0},{2,3},{3,2},{4,5},{5,4},{6,7},{7,6},{8,9},{9,8},{10,11... | collective-permute-start | bytes 3145736 | tf_op jit(solution)/shard_map/ppermute | solution.py:88
  89.1 63.7 %collective-permute-start.6 = (bf16[256,2048]{1,0:T(8,128)(2,1)}, bf16[256,2048]{1,0:T(8,128)(2,1)S(1)}, u32[]{:S(2)}, u32[]{:S(2)}) collective-permute-start(bf16[256,2048]{1,0:T(8,128)(2,1)} %collective-permute-done.5.refs_6_), channel_id=1, source_target_pairs={{0,1},{1,0},{2,3},{3,2},{4,5},{5,4},{6,7},{7,6},{8,9},{9,8},{10,11... | collective-permute-start | bytes 3145736 | tf_op jit(solution)/shard_map/ppermute | solution.py:88
  89.7 64.1 %collective-permute-start.7 = (bf16[256,2048]{1,0:T(8,128)(2,1)S(1)}, bf16[256,2048]{1,0:T(8,128)(2,1)}, u32[]{:S(2)}, u32[]{:S(2)}) collective-permute-start(bf16[256,2048]{1,0:T(8,128)(2,1)S(1)} %bitcast.137), channel_id=1, source_target_pairs={{0,2},{1,3},{2,0},{3,1},{4,6},{5,7},{6,4},{7,5},{8,10},{9,11},{10,... | collective-permute-start | bytes 3145736 | tf_op jit(solution)/shard_map/ppermute | solution.py:88
  152.9 40.5 %collective-permute-start.21 = (bf16[256,2048]{1,0:T(8,128)(2,1)S(1)}, bf16[256,2048]{1,0:T(8,128)(2,1)}, u32[]{:S(2)}, u32[]{:S(2)}) collective-permute-start(bf16[256,2048]{1,0:T(8,128)(2,1)S(1)} %bitcast.138), channel_id=1, source_target_pairs={{0,4},{1,5},{2,6},{3,7},{4,0},{5,1},{6,2},{7,3},{8,12},{9,13},{10,... | collective-permute-start | bytes 3145736 | tf_op jit(solution)/shard_map/ppermute | solution.py:88
  153.8 41.1 %collective-permute-start.20 = (bf16[256,2048]{1,0:T(8,128)(2,1)S(1)}, bf16[256,2048]{1,0:T(8,128)(2,1)S(1)}, u32[]{:S(2)}, u32[]{:S(2)}) collective-permute-start(bf16[256,2048]{1,0:T(8,128)(2,1)S(1)} %bitcast.139), channel_id=1, source_target_pairs={{0,1},{1,0},{2,3},{3,2},{4,5},{5,4},{6,7},{7,6},{8,9},{9,8},{10,11... | collective-permute-start | bytes 3145736 | tf_op jit(solution)/shard_map/ppermute | solution.py:88
  171.4 50.5 %collective-permute-start.12 = (bf16[2048,512]{1,0:T(8,128)(2,1)}, bf16[2048,512]{1,0:T(8,128)(2,1)}, u32[]{:S(2)}, u32[]{:S(2)}) collective-permute-start(bf16[2048,512]{1,0:T(8,128)(2,1)} %get-tuple-element.110.refs_0_), channel_id=1, source_target_pairs={{0,16},{8,24},{16,0},{24,8},{1,17},{9,25},{17,1},{25,9},{2,18},{10... | collective-permute-start | bytes 6291464 | tf_op jit(solution)/shard_map/ppermute | solution.py:92
  219.3 50.4 %collective-permute-start.24 = (bf16[256,2048]{1,0:T(8,128)(2,1)}, bf16[256,2048]{1,0:T(8,128)(2,1)}, u32[]{:S(2)}, u32[]{:S(2)}) collective-permute-start(bf16[256,2048]{1,0:T(8,128)(2,1)} %collective-permute-done.21.refs_1_), channel_id=1, source_target_pairs={{0,1},{1,0},{2,3},{3,2},{4,5},{5,4},{6,7},{7,6},{8,9},{9,8},{10,11... | collective-permute-start | bytes 3145736 | tf_op jit(solution)/shard_map/ppermute | solution.py:88
  220.8 69.3 %collective-permute-start.23 = (bf16[256,2048]{1,0:T(8,128)(2,1)}, bf16[256,2048]{1,0:T(8,128)(2,1)}, u32[]{:S(2)}, u32[]{:S(2)}) collective-permute-start(bf16[256,2048]{1,0:T(8,128)(2,1)} %collective-permute-done.22.refs_1_), channel_id=1, source_target_pairs={{0,1},{1,0},{2,3},{3,2},{4,5},{5,4},{6,7},{7,6},{8,9},{9,8},{10,11... | collective-permute-start | bytes 3145736 | tf_op jit(solution)/shard_map/ppermute | solution.py:88
  221.3 37.5 %collective-permute-start.11 = (bf16[2048,512]{1,0:T(8,128)(2,1)S(1)}, bf16[2048,512]{1,0:T(8,128)(2,1)}, u32[]{:S(2)}, u32[]{:S(2)}) collective-permute-start(bf16[2048,512]{1,0:T(8,128)(2,1)S(1)} %copy-done.52), channel_id=1, source_target_pairs={{0,8},{8,0},{16,24},{24,16},{1,9},{9,1},{17,25},{25,17},{2,10},{10... | collective-permute-start | bytes 6291464 | tf_op jit(solution)/shard_map/ppermute | solution.py:92
  222.0 36.8 %collective-permute-start.13 = (bf16[2048,512]{1,0:T(8,128)(2,1)}, bf16[2048,512]{1,0:T(8,128)(2,1)}, u32[]{:S(2)}, u32[]{:S(2)}) collective-permute-start(bf16[2048,512]{1,0:T(8,128)(2,1)} %collective-permute-done.12.refs_2_), channel_id=1, source_target_pairs={{0,8},{8,0},{16,24},{24,16},{1,9},{9,1},{17,25},{25,17},{2,10},{10... | collective-permute-start | bytes 6291464 | tf_op jit(solution)/shard_map/ppermute | solution.py:92
  243.2 422.1 %all-gather.4.cloned.1.call-start = ((), (), s32[]{:S(2)}) async-start(), calls=%async_computation.8 | async-start | bytes 5242880 | tf_op jit(solution)/shard_map/all_gather | solution.py:863
  268.0 45.0 %collective-permute-start.14 = (bf16[256,2048]{1,0:T(8,128)(2,1)}, bf16[256,2048]{1,0:T(8,128)(2,1)S(1)}, u32[]{:S(2)}, u32[]{:S(2)}) collective-permute-start(bf16[256,2048]{1,0:T(8,128)(2,1)} %get-tuple-element.112.refs_0_), channel_id=1, source_target_pairs={{0,2},{1,3},{2,0},{3,1},{4,6},{5,7},{6,4},{7,5},{8,10},{9,11},{10,... | collective-permute-start | bytes 3145736 | tf_op jit(solution)/shard_map/ppermute | solution.py:88
  268.0 48.3 %collective-permute-start.16 = (bf16[256,2048]{1,0:T(8,128)(2,1)}, bf16[256,2048]{1,0:T(8,128)(2,1)}, u32[]{:S(2)}, u32[]{:S(2)}) collective-permute-start(bf16[256,2048]{1,0:T(8,128)(2,1)} %get-tuple-element.112.refs_0_), channel_id=1, source_target_pairs={{0,4},{1,5},{2,6},{3,7},{4,0},{5,1},{6,2},{7,3},{8,12},{9,13},{10,... | collective-permute-start | bytes 3145736 | tf_op jit(solution)/shard_map/ppermute | solution.py:88
  268.2 48.2 %collective-permute-start.18 = (bf16[256,2048]{1,0:T(8,128)(2,1)}, bf16[256,2048]{1,0:T(8,128)(2,1)S(1)}, u32[]{:S(2)}, u32[]{:S(2)}) collective-permute-start(bf16[256,2048]{1,0:T(8,128)(2,1)} %get-tuple-element.112.refs_0_), channel_id=1, source_target_pairs={{0,1},{1,0},{2,3},{3,2},{4,5},{5,4},{6,7},{7,6},{8,9},{9,8},{10,11... | collective-permute-start | bytes 3145736 | tf_op jit(solution)/shard_map/ppermute | solution.py:88
  340.4 53.5 %collective-permute-start.25 = (bf16[256,2048]{1,0:T(8,128)(2,1)}, bf16[256,2048]{1,0:T(8,128)(2,1)}, u32[]{:S(2)}, u32[]{:S(2)}) collective-permute-start(bf16[256,2048]{1,0:T(8,128)(2,1)} %collective-permute-done.17.refs_1_), channel_id=1, source_target_pairs={{0,1},{1,0},{2,3},{3,2},{4,5},{5,4},{6,7},{7,6},{8,9},{9,8},{10,11... | collective-permute-start | bytes 3145736 | tf_op jit(solution)/shard_map/ppermute | solution.py:88
  341.9 47.5 %collective-permute-start.26 = (bf16[256,2048]{1,0:T(8,128)(2,1)}, bf16[256,2048]{1,0:T(8,128)(2,1)}, u32[]{:S(2)}, u32[]{:S(2)}) collective-permute-start(bf16[256,2048]{1,0:T(8,128)(2,1)} %collective-permute-done.16.refs_1_), channel_id=1, source_target_pairs={{0,1},{1,0},{2,3},{3,2},{4,5},{5,4},{6,7},{7,6},{8,9},{9,8},{10,11... | collective-permute-start | bytes 3145736 | tf_op jit(solution)/shard_map/ppermute | solution.py:88
  406.3 44.6 %collective-permute-start.27 = (bf16[256,2048]{1,0:T(8,128)(2,1)}, bf16[256,2048]{1,0:T(8,128)(2,1)}, u32[]{:S(2)}, u32[]{:S(2)}) collective-permute-start(bf16[256,2048]{1,0:T(8,128)(2,1)} %get-tuple-element.130.refs_7_.refs_5_), channel_id=1, source_target_pairs={{0,1},{1,0},{2,3},{3,2},{4,5},{5,4},{6,7},{7,6},{8,9},{9,8},{10,11... | collective-permute-start | bytes 3145736 | tf_op jit(solution)/shard_map/ppermute | solution.py:88
  407.9 45.8 %collective-permute-start.28 = (bf16[256,2048]{1,0:T(8,128)(2,1)}, bf16[256,2048]{1,0:T(8,128)(2,1)}, u32[]{:S(2)}, u32[]{:S(2)}) collective-permute-start(bf16[256,2048]{1,0:T(8,128)(2,1)} %get-tuple-element.132.refs_9_.refs_7_), channel_id=1, source_target_pairs={{0,1},{1,0},{2,3},{3,2},{4,5},{5,4},{6,7},{7,6},{8,9},{9,8},{10,11... | collective-permute-start | bytes 3145736 | tf_op jit(solution)/shard_map/ppermute | solution.py:88
  473.3 371.4 %reduce-scatter.4.cloned.1.call-start = ((), (), s32[]{:S(2)}) async-start(), calls=%async_computation.9 | async-start | bytes 10485760 | tf_op jit(solution)/shard_map/reduce_scatter | solution.py:919
  473.4 26.5 %collective-permute-start.30 = (bf16[256,2048]{1,0:T(8,128)(2,1)}, bf16[256,2048]{1,0:T(8,128)(2,1)}, u32[]{:S(2)}, u32[]{:S(2)}) collective-permute-start(bf16[256,2048]{1,0:T(8,128)(2,1)} %get-tuple-element.143.refs_11_), channel_id=1, source_target_pairs={{0,1},{1,0},{2,3},{3,2},{4,5},{5,4},{6,7},{7,6},{8,9},{9,8},{10,11... | collective-permute-start | bytes 3145736 | tf_op jit(solution)/shard_map/ppermute | solution.py:88
  475.2 47.5 %collective-permute-start.29 = (bf16[256,2048]{1,0:T(8,128)(2,1)}, bf16[256,2048]{1,0:T(8,128)(2,1)}, u32[]{:S(2)}, u32[]{:S(2)}) collective-permute-start(bf16[256,2048]{1,0:T(8,128)(2,1)} %get-tuple-element.141.refs_9_), channel_id=1, source_target_pairs={{0,1},{1,0},{2,3},{3,2},{4,5},{5,4},{6,7},{7,6},{8,9},{9,8},{10,11... | collective-permute-start | bytes 3145736 | tf_op jit(solution)/shard_map/ppermute | solution.py:88
  536.8 312.1 %reduce-scatter.6.cloned.1.call-start = ((), (), s32[]{:S(2)}) async-start(), calls=%async_computation.10 | async-start | bytes 10485760 | tf_op jit(solution)/shard_map/reduce_scatter | solution.py:919
  539.1 36.3 %collective-permute-start.34 = (bf16[256,2048]{1,0:T(8,128)(2,1)}, bf16[256,2048]{1,0:T(8,128)(2,1)}, u32[]{:S(2)}, u32[]{:S(2)}) collective-permute-start(bf16[256,2048]{1,0:T(8,128)(2,1)} %add_convert_fusion.8.refs_4_.refs_5_), channel_id=1, source_target_pairs={{0,2},{1,3},{2,0},{3,1},{4,6},{5,7},{6,4},{7,5},{8,10},{9,11},{10,... | collective-permute-start | bytes 3145736 | tf_op jit(solution)/shard_map/ppermute | solution.py:88
  540.3 48.9 %collective-permute-start.32 = (bf16[2,256,2048]{2,1,0:T(8,128)(2,1)}, bf16[2,256,2048]{2,1,0:T(8,128)(2,1)}, u32[]{:S(2)}, u32[]{:S(2)}) collective-permute-start(bf16[2,256,2048]{2,1,0:T(8,128)(2,1)} %get-tuple-element.152), channel_id=1, source_target_pairs={{0,1},{1,0},{2,3},{3,2},{4,5},{5,4},{6,7},{7,6},{8,9},{9,8},{10,11... | collective-permute-start | bytes 6291464 | tf_op jit(solution)/shard_map/ppermute | solution.py:88
  542.1 82.8 %collective-permute-start.31 = (bf16[2,256,2048]{2,1,0:T(8,128)(2,1)}, bf16[2,256,2048]{2,1,0:T(8,128)(2,1)}, u32[]{:S(2)}, u32[]{:S(2)}) collective-permute-start(bf16[2,256,2048]{2,1,0:T(8,128)(2,1)} %get-tuple-element.150), channel_id=1, source_target_pairs={{0,1},{1,0},{2,3},{3,2},{4,5},{5,4},{6,7},{7,6},{8,9},{9,8},{10,11... | collective-permute-start | bytes 6291464 | tf_op jit(solution)/shard_map/ppermute | solution.py:88
  542.4 40.1 %collective-permute-start.36 = (bf16[256,2048]{1,0:T(8,128)(2,1)}, bf16[256,2048]{1,0:T(8,128)(2,1)}, u32[]{:S(2)}, u32[]{:S(2)}) collective-permute-start(bf16[256,2048]{1,0:T(8,128)(2,1)} %get-tuple-element.193), channel_id=1, source_target_pairs={{0,4},{1,5},{2,6},{3,7},{4,0},{5,1},{6,2},{7,3},{8,12},{9,13},{10,... | collective-permute-start | bytes 3145736 | tf_op jit(solution)/shard_map/ppermute | solution.py:88
  592.9 35.8 %collective-permute-start.33 = (bf16[2,256,2048]{2,1,0:T(8,128)(2,1)}, bf16[2,256,2048]{2,1,0:T(8,128)(2,1)}, u32[]{:S(2)}, u32[]{:S(2)}) collective-permute-start(bf16[2,256,2048]{2,1,0:T(8,128)(2,1)} %add_convert_fusion.1), channel_id=1, source_target_pairs={{0,2},{1,3},{2,0},{3,1},{4,6},{5,7},{6,4},{7,5},{8,10},{9,11},{10,... | collective-permute-start | bytes 6291464 | tf_op jit(solution)/shard_map/ppermute | solution.py:88
  605.0 29.8 %all-to-all-start.3 = ((bf16[256,4,512]{2,0,1:T(8,128)(2,1)}), bf16[256,4,512]{2,0,1:T(8,128)(2,1)S(1)}, u32[]{:S(2)}, u32[]{:S(2)}) async-start(bf16[256,4,512]{2,0,1:T(8,128)(2,1)} %bitcast.133), calls=%async_computation.3 | async-start | bytes 2097152 | tf_op jit(solution)/shard_map/all_to_all | solution.py:941
  608.5 244.4 %reduce-scatter.8.cloned.1.call-start = ((), (), s32[]{:S(2)}) async-start(), calls=%async_computation.11 | async-start | bytes 10485760 | tf_op jit(solution)/shard_map/reduce_scatter | solution.py:919
  634.8 30.5 %all-to-all-start.4 = ((bf16[256,4,512]{2,0,1:T(8,128)(2,1)}), bf16[256,4,512]{2,0,1:T(8,128)(2,1)S(1)}, u32[]{:S(2)}, u32[]{:S(2)}) async-start(bf16[256,4,512]{2,0,1:T(8,128)(2,1)} %bitcast.132), calls=%async_computation.4 | async-start | bytes 2097152 | tf_op jit(solution)/shard_map/all_to_all | solution.py:942
  663.7 49.2 %collective-permute-start.37 = (bf16[256,2048]{1,0:T(8,128)(2,1)}, bf16[256,2048]{1,0:T(8,128)(2,1)}, u32[]{:S(2)}, u32[]{:S(2)}) collective-permute-start(bf16[256,2048]{1,0:T(8,128)(2,1)} %fusion.10), channel_id=1, source_target_pairs={{0,4},{1,5},{2,6},{3,7},{4,0},{5,1},{6,2},{7,3},{8,12},{9,13},{10,... | collective-permute-start | bytes 3145736 | tf_op jit(solution)/shard_map/ppermute | solution.py:88
  676.8 30.3 %collective-permute-start.51 = (bf16[2,256,1024]{2,1,0:T(8,128)(2,1)}, bf16[2,256,1024]{2,1,0:T(8,128)(2,1)}, u32[]{:S(2)}, u32[]{:S(2)}) collective-permute-start(bf16[2,256,1024]{2,1,0:T(8,128)(2,1)} %get-tuple-element.180), channel_id=1, source_target_pairs={{0,1},{1,0},{2,3},{3,2},{4,5},{5,4},{6,7},{7,6},{8,9},{9,8},{10,11... | collective-permute-start | bytes 3145736 | tf_op jit(solution)/shard_map/ppermute | solution.py:88
  679.1 72.5 %collective-permute-start.50 = (bf16[2,256,1024]{2,1,0:T(8,128)(2,1)}, bf16[2,256,1024]{2,1,0:T(8,128)(2,1)}, u32[]{:S(2)}, u32[]{:S(2)}) collective-permute-start(bf16[2,256,1024]{2,1,0:T(8,128)(2,1)} %get-tuple-element.178), channel_id=1, source_target_pairs={{0,1},{1,0},{2,3},{3,2},{4,5},{5,4},{6,7},{7,6},{8,9},{9,8},{10,11... | collective-permute-start | bytes 3145736 | tf_op jit(solution)/shard_map/ppermute | solution.py:88
  693.1 56.3 %collective-permute-start.44 = (bf16[2,272,1024]{2,1,0:T(8,128)(2,1)}, bf16[2,272,1024]{2,1,0:T(8,128)(2,1)S(1)}, u32[]{:S(2)}, u32[]{:S(2)}) collective-permute-start(bf16[2,272,1024]{2,1,0:T(8,128)(2,1)} %get-tuple-element.177), channel_id=1, source_target_pairs={{0,1},{1,0},{2,3},{3,2},{4,5},{5,4},{6,7},{7,6},{8,9},{9,8},{10,11... | collective-permute-start | bytes 3342344 | tf_op jit(solution)/shard_map/ppermute | solution.py:88
  709.7 41.9 %collective-permute-start.52 = (bf16[2,256,1024]{2,1,0:T(8,128)(2,1)S(1)}, bf16[2,256,1024]{2,1,0:T(8,128)(2,1)S(1)}, u32[]{:S(2)}, u32[]{:S(2)}) collective-permute-start(bf16[2,256,1024]{2,1,0:T(8,128)(2,1)S(1)} %add_convert_fusion.3), channel_id=1, source_target_pairs={{0,2},{1,3},{2,0},{3,1},{4,6},{5,7},{6,4},{7,5},{8,10},{9,11},{10,... | collective-permute-start | bytes 3145736 | tf_op jit(solution)/shard_map/ppermute | solution.py:88
  716.7 70.1 %collective-permute-start.41 = (bf16[2,256,2048]{2,1,0:T(8,128)(2,1)S(1)}, bf16[2,256,2048]{2,1,0:T(8,128)(2,1)S(1)}, u32[]{:S(2)}, u32[]{:S(2)}) collective-permute-start(bf16[2,256,2048]{2,1,0:T(8,128)(2,1)S(1)} %slice.240), channel_id=1, source_target_pairs={{0,8},{8,0},{16,24},{24,16},{1,9},{9,1},{17,25},{25,17},{2,10},{10... | collective-permute-start | bytes 6291464 | tf_op jit(solution)/shard_map/ppermute | solution.py:92
  717.6 54.7 %collective-permute-start.43 = (bf16[2,272,1024]{2,1,0:T(8,128)(2,1)S(1)}, bf16[2,272,1024]{2,1,0:T(8,128)(2,1)S(1)}, u32[]{:S(2)}, u32[]{:S(2)}) collective-permute-start(bf16[2,272,1024]{2,1,0:T(8,128)(2,1)S(1)} %copy-done.53), channel_id=1, source_target_pairs={{0,1},{1,0},{2,3},{3,2},{4,5},{5,4},{6,7},{7,6},{8,9},{9,8},{10,11... | collective-permute-start | bytes 3342344 | tf_op jit(solution)/shard_map/ppermute | solution.py:88
  749.8 36.1 %collective-permute-start.45 = (bf16[2,272,1024]{2,1,0:T(8,128)(2,1)S(1)}, bf16[2,272,1024]{2,1,0:T(8,128)(2,1)S(1)}, u32[]{:S(2)}, u32[]{:S(2)}) collective-permute-start(bf16[2,272,1024]{2,1,0:T(8,128)(2,1)S(1)} %add_convert_fusion.2), channel_id=1, source_target_pairs={{0,2},{1,3},{2,0},{3,1},{4,6},{5,7},{6,4},{7,5},{8,10},{9,11},{10,... | collective-permute-start | bytes 3342344 | tf_op jit(solution)/shard_map/ppermute | solution.py:88
  753.5 59.4 %collective-permute-start.53 = (bf16[256,1024]{1,0:T(8,128)(2,1)S(1)}, bf16[256,1024]{1,0:T(8,128)(2,1)S(1)}, u32[]{:S(2)}, u32[]{:S(2)}) collective-permute-start(bf16[256,1024]{1,0:T(8,128)(2,1)S(1)} %fusion.14), channel_id=1, source_target_pairs={{0,4},{1,5},{2,6},{3,7},{4,0},{5,1},{6,2},{7,3},{8,12},{9,13},{10,... | collective-permute-start | bytes 1572872 | tf_op jit(solution)/shard_map/ppermute | solution.py:88
  788.8 49.4 %collective-permute-start.42 = (bf16[256,2048]{1,0:T(8,128)(2,1)}, bf16[256,2048]{1,0:T(8,128)(2,1)}, u32[]{:S(2)}, u32[]{:S(2)}) collective-permute-start(bf16[256,2048]{1,0:T(8,128)(2,1)} %slice_bitcast_fusion.3), channel_id=1, source_target_pairs={{0,16},{8,24},{16,0},{24,8},{1,17},{9,25},{17,1},{25,9},{2,18},{10... | collective-permute-start | bytes 3145736 | tf_op jit(solution)/shard_map/ppermute | solution.py:92
  815.7 41.3 %collective-permute-start.54 = (bf16[256,1024]{1,0:T(8,128)(2,1)}, bf16[256,1024]{1,0:T(8,128)(2,1)}, u32[]{:S(2)}, u32[]{:S(2)}) collective-permute-start(bf16[256,1024]{1,0:T(8,128)(2,1)} %fusion.12.refs_9_), channel_id=1, source_target_pairs={{0,8},{8,0},{16,24},{24,16},{1,9},{9,1},{17,25},{25,17},{2,10},{10... | collective-permute-start | bytes 1572872 | tf_op jit(solution)/shard_map/ppermute | solution.py:92
  815.8 41.2 %collective-permute-start.47 = (bf16[272,1024]{1,0:T(8,128)(2,1)}, bf16[272,1024]{1,0:T(8,128)(2,1)}, u32[]{:S(2)}, u32[]{:S(2)}) collective-permute-start(bf16[272,1024]{1,0:T(8,128)(2,1)} %fusion.9.refs_5_), channel_id=1, source_target_pairs={{0,8},{8,0},{16,24},{24,16},{1,9},{9,1},{17,25},{25,17},{2,10},{10... | collective-permute-start | bytes 1671176 | tf_op jit(solution)/shard_map/ppermute | solution.py:92
  (83 other events, 1445.3 us)
Sparse Core Ops, SparseCore 0:
  9.6 37.1 all-gather.5
  258.9 31.7 all-gather.3
  536.9 70.8 reduce-scatter.3
  610.4 85.7 reduce-scatter.5
  698.6 71.7 reduce-scatter.7

commit v7 on v6

--- a/solution.py
+++ b/solution.py
@@ -97,16 +97,16 @@
     return jnp.bitwise_xor(ids, ep_index) if n_ep == 8 else ids
 
 
-def along_z(value):
-    far = swap(value, 4)
-    return [value, swap(value, 2), far, swap(far, 2)]
-
-
-def across_x(blocks):
-    pieces = []
-    for own in blocks:
-        pieces += [own, swap(own, 1)]
-    return pieces
+def gather_steps(value, after=None):
+    near, far = swap(value, 2), swap(value, 4)
+    crossed = value
+    if after is not None:
+        after, crossed, near = tie(after, value, near)
+    near_x = swap(near, 1)
+    near_x, far = tie(near_x, far)
+    farther = swap(far, 2)
+    pieces = [value, swap(crossed, 1), near, near_x, far, swap(far, 1), farther, swap(farther, 1)]
+    return pieces, after
 
 
 def gather_whole(value):
@@ -115,12 +115,7 @@
 
 
 def gather(value, n_ep):
-    if n_ep != 8:
-        return gather_whole(value)
-    blocks = along_z(value)
-    near = across_x(blocks[:2])
-    near[3], blocks[2], blocks[3] = tie(near[3], blocks[2], blocks[3])
-    return near + across_x(blocks[2:])
+    return gather_steps(value)[0] if n_ep == 8 else gather_whole(value)
 
 
 def plus(left, right):
@@ -804,12 +799,9 @@
     w_own = jnp.concatenate([own_columns(w) for w in (w_query, w_key, w_value, w_out)], axis=1)
     cot_own = cotangent[0]
     if n_ep == 8:
-        blocks_z = along_z(w_own)
-        blocks_z[3], cot_own = tie(blocks_z[3], cot_own)
-        cot_blocks = along_z(cot_own)
-        w_pieces = across_x(blocks_z)
-        w_pieces[7], cot_blocks[0], cot_blocks[1] = tie(w_pieces[7], cot_blocks[0], cot_blocks[1])
-        cot_pieces = across_x(cot_blocks)
+        w_pieces = gather_steps(w_own)[0]
+        w_pieces[6], cot_own = tie(w_pieces[6], cot_own)
+        cot_pieces, w_pieces[7] = gather_steps(cot_own, w_pieces[7])
     else:
         w_pieces, cot_pieces = gather_whole(w_own), gather_whole(cot_own)
 
@@ -881,7 +873,7 @@
     rows, gates, home_gates = rows_of(0, [])
     for g in range(0, n_ep, group):
         d_rows = cots[g // group]
-        made = experts(rows, d_rows, gates, w_gate, w_up, w_down, d_pieces[-group:] + cots)
+        made = experts(rows, d_rows, gates, w_gate, w_up, w_down, d_pieces[-group:] + cots + h2_pieces[6:7])
         groups.append((rows, d_rows, made))
         following = []
         if g + group < n_ep:
@@ -903,17 +895,20 @@
     d_up_rows = [made[2] for _, _, made in groups]
     ins = [rows for rows, _, _ in groups]
     outs = [d_rows for _, d_rows, _ in groups]
-    grad_down = weight_grad(acts, outs, d_pieces)
+    mix_stacks = combine_stacks(
+        places, [made[4] for _, _, made in groups], n_ep, local, cap, group, d_pieces
+    )
+    grad_down = weight_grad(acts, outs, mix_stacks[:1])
     d_gates = by_piece(jnp.concatenate(d_gates, axis=0).reshape(n_ep, local, tok_dev))
     d_gates = lax.all_to_all(d_gates, "ep", split_axis=0, concat_axis=0, tiled=True)
     d_gates = d_gates.reshape(expert_count, tok_dev)
-    grad_gate = weight_grad(ins, d_gate_rows, [grad_down, d_gates])
-    mix_stacks = combine_stacks(
-        places, [made[4] for _, _, made in groups], n_ep, local, cap, group, [grad_gate, *d_sums]
-    )
-    mix_stacks[0], grad_down, grad_gate = tie(mix_stacks[0], grad_down, grad_gate)
+    grad_gate = weight_grad(ins, d_gate_rows, [grad_down, d_gates, *d_sums[3:]])
+    if n_ep == 8:
+        d_sums[2], mix_stacks[2], mix_stacks[3], grad_down, grad_gate = tie(
+            d_sums[2], mix_stacks[2], mix_stacks[3], grad_down, grad_gate
+        )
     d_h2 = scatter_z(*d_sums) if n_ep == 8 else scatter(d_pieces, n_ep)
-    grad_up = weight_grad(ins, d_up_rows, mix_stacks[:1])
+    grad_up = weight_grad(ins, d_up_rows, [*d_sums, grad_gate])
 
     def over_sp(value):
         return lax.psum_scatter(value, "sp", scatter_dimension=1, tiled=True).astype(F32)
@@ -963,7 +958,11 @@
     *qk_stacks, d_qk = qk_back(
         ids, n_ep, h_all, d_qn, d_kn, q_raw, k_raw, scales, sum_sp(sums), tiny, vo_stacks[:1]
     )
-    grad_qk = last_hop(*scatter_stacks(qk_stacks, n_ep)).astype(BF16)
+    grad_qk, qk_far = scatter_stacks(qk_stacks, n_ep)
+    if n_ep == 8:
+        qk_far, grad_vo = tie(qk_far, grad_vo)
+    grad_qk = last_hop(grad_qk, qk_far).astype(BF16)
+    grad_qk, grad_down, grad_gate, grad_up = tie(grad_qk, grad_down, grad_gate, grad_up)
 
     d_h = d_h_rows(ids, n_ep, n_sp, d_qk, d_v, w_qkv)
     output, d_h = tie(output, d_h)

time: 886 us -> 910 us (1.027)
  starting transfers between devices: 71 us -> 81.4 us
    convert_element_type x8 -> x9, other arithmetic: 19.1 us -> 20.6 us  [plus(): return (left.astype(F32) + right.astype(F32)).astype(left.dtype)]
  transfers between devices with their start and end apart: 67 -> 67, of which waited for: 24 -> 23; matrix products, arithmetic and copies ran while one was open for 10% -> 10% of each run, Pallas kernels for 36% -> 35%
where the time goes in v7:
time: 910 us; the launch traced here: 900 us
  waiting for transfers between devices  366 us (40%)
  Pallas kernels  321 us (35%)
  starting transfers between devices  81.4 us (9%)
  other arithmetic  63.2 us (7%)
  local copies, waits for them, and re-layouts  33.8 us (4%)
  between operations  30.8 us (3%)
    ppermute x40, waiting for transfers between devices, swap(): return lax.ppermute(value, 'ep', [(i, i ^ bits) for i in range(8)])  327 us
    pallas_call x27, Pallas kernels, call(): pl.pallas_call(kernel, grid_spec=pltpu.PrefetchScalarGridSpec(num_scalar_...  321 us
    ppermute x40, starting transfers between devices, swap(): return lax.ppermute(value, 'ep', [(i, i ^ bits) for i in range(8)])  48.3 us
    ppermute x17, waiting for transfers between devices, swap_sp(): return lax.ppermute(value, 'sp', [(i, i ^ bits) for i in range(4)])  21.3 us
    convert_element_type x9, other arithmetic, plus(): return (left.astype(F32) + right.astype(F32)).astype(left.dtype)  20.6 us
  transfers between devices with their start and end apart: 67, of which 23 were waited for; matrix products, arithmetic and copies ran while one was open for 10% of the time, Pallas kernels for 35%

profile of v7, /device:TPU:0, one launch (start us, length us, event | category | flops | bytes accessed | tf_op | source)
XLA Modules:
  0.0 900.5 jit_solution(16115684213633044904)
XLA Ops:
  18.4 41.7 %collective-permute-done.1.refs_2_ = bf16[256,2048]{1,0:T(8,128)(2,1)} collective-permute-done((bf16[256,2048]{1,0:T(8,128)(2,1)}, bf16[256,2048]{1,0:T(8,128)(2,1)}, u32[]{:S(2)}, u32[]{:S(2)}) %collective-permute-start.1) | collective-permute-done | bytes 1048608 | tf_op jit(solution)/shard_map/ppermute | solution.py:88
  69.3 17.3 %collective-permute-done.2.refs_3_ = bf16[256,2048]{1,0:T(8,128)(2,1)} collective-permute-done((bf16[256,2048]{1,0:T(8,128)(2,1)}, bf16[256,2048]{1,0:T(8,128)(2,1)}, u32[]{:S(2)}, u32[]{:S(2)}) %collective-permute-start.2) | collective-permute-done | bytes 1048608 | tf_op jit(solution)/shard_map/ppermute | solution.py:88
  115.2 37.9 %collective-permute-done.7.refs_0_ = bf16[256,2048]{1,0:T(8,128)(2,1)S(1)} collective-permute-done((bf16[256,2048]{1,0:T(8,128)(2,1)S(1)}, bf16[256,2048]{1,0:T(8,128)(2,1)S(1)}, u32[]{:S(2)}, u32[]{:S(2)}) %collective-permute-start.7) | collective-permute-done | bytes 1048608 | tf_op jit(solution)/shard_map/ppermute | solution.py:88
  155.3 17.0 %qkv_project.1 = (f32[1024,512]{1,0:T(8,128)}, f32[1024,512]{1,0:T(8,128)}, bf16[1024,512]{1,0:T(8,128)(2,1)}, f32[16,1024]{1,0:T(8,128)}, bf16[2048,1536]{1,0:T...) custom-call(s32[12]{0:T(128)} %pad_add_fusion.ids.refs_0_, bf16[1024,2048]{1,0:T(8,128)(2,1)} %bitcast.177, ...), custom_call_target="tpu_custom_call" | custom-call | flops 128849018880 | bytes 30482432 | tf_op jit(solution)/shard_map/qkv_project/pallas_call | solution.py:62
  182.9 19.0 %collective-permute-done.20.refs_1_ = bf16[256,2048]{1,0:T(8,128)(2,1)} collective-permute-done((bf16[256,2048]{1,0:T(8,128)(2,1)S(1)}, bf16[256,2048]{1,0:T(8,128)(2,1)}, u32[]{:S(2)}, u32[]{:S(2)}) %collective-permute-start.20) | collective-permute-done | bytes 1048608 | tf_op jit(solution)/shard_map/ppermute | solution.py:88
  203.4 3.9 dispatch.10.refs_3_
  207.2 12.3 %collective-permute-done.10 = f32[16,1024]{1,0:T(8,128)S(1)} collective-permute-done((f32[16,1024]{1,0:T(8,128)}, f32[16,1024]{1,0:T(8,128)S(1)}, u32[]{:S(2)}, u32[]{:S(2)}) %collective-permute-start.10) | collective-permute-done | bytes 65568 | tf_op jit(solution)/shard_map/ppermute | solution.py:92
  221.5 17.2 %attend.1 = (bf16[1024,512]{1,0:T(8,128)(2,1)}, bf16[1024,512]{1,0:T(8,128)(2,1)}, bf16[1024,512]{1,0:T(8,128)(2,1)}) custom-call(f32[1024,512]{1,0:T(8,128)} %get-tuple-element.118.qr_ref.refs_4_, f32[1024,512]{1,0:T(8,128)} %get-tuple-element.119.kr_ref.refs_5_, bf16[1024,512]{1,0:T(8,128)(2,1)} %get-tuple-element.120.v_ref, ...), custom_call_target="tpu_custom_call" | custom-call | flops 32212254720 | bytes 9510912 | tf_op jit(solution)/shard_map/attend/pallas_call | solution.py:62
  248.2 8.6 all-to-all-done.1
  257.9 8.9 out_project.1
  277.9 36.5 %collective-permute-done.14.refs_0_ = bf16[256,2048]{1,0:T(8,128)(2,1)S(1)} collective-permute-done((bf16[256,2048]{1,0:T(8,128)(2,1)}, bf16[256,2048]{1,0:T(8,128)(2,1)S(1)}, u32[]{:S(2)}, u32[]{:S(2)}) %collective-permute-start.14) | collective-permute-done | bytes 1048608 | tf_op jit(solution)/shard_map/ppermute | solution.py:88
  315.7 4.6 dispatch.8
  320.3 17.8 %collective-permute-done.15.refs_1_ = bf16[256,2048]{1,0:T(8,128)(2,1)S(1)} collective-permute-done((bf16[256,2048]{1,0:T(8,128)(2,1)S(1)}, bf16[256,2048]{1,0:T(8,128)(2,1)S(1)}, u32[]{:S(2)}, u32[]{:S(2)}) %collective-permute-start.15) | collective-permute-done | bytes 1048608 | tf_op jit(solution)/shard_map/ppermute | solution.py:88
  339.1 4.5 dispatch.9
  343.6 17.6 %collective-permute-done.24.refs_8_.refs_1_.refs_12_ = bf16[256,2048]{1,0:T(8,128)(2,1)} collective-permute-done((bf16[256,2048]{1,0:T(8,128)(2,1)}, bf16[256,2048]{1,0:T(8,128)(2,1)}, u32[]{:S(2)}, u32[]{:S(2)}) %collective-permute-start.24) | collective-permute-done | bytes 1048608 | tf_op jit(solution)/shard_map/ppermute | solution.py:88
  361.4 42.5 %experts.2 = (bf16[2,576,1024]{2,1,0:T(8,128)(2,1)}, bf16[2,576,1024]{2,1,0:T(8,128)(2,1)}, bf16[2,576,1024]{2,1,0:T(8,128)(2,1)}, f32[2,576,1]{2,1,0:T(8,128)},...) custom-call(bf16[2,576,2048]{2,1,0:T(8,128)(2,1)} %get-tuple-element.129.refs_0_, ...), custom_call_target="tpu_custom_call" | custom-call | flops 579820584960 | bytes 51127296 | tf_op jit(solution)/shard_map/experts/pallas_call | solution.py:62
  403.9 4.4 dispatch.14
  408.4 4.5 dispatch.15
  412.8 3.9 combine.5
  416.8 4.0 combine.4
  422.8 42.8 %experts.3 = (bf16[2,576,1024]{2,1,0:T(8,128)(2,1)}, bf16[2,576,1024]{2,1,0:T(8,128)(2,1)}, bf16[2,576,1024]{2,1,0:T(8,128)(2,1)}, f32[2,576,1]{2,1,0:T(8,128)},...) custom-call(bf16[2,576,2048]{2,1,0:T(8,128)(2,1)} %get-tuple-element.140.refs_3_.refs_0_.refs_1_, ...), custom_call_target="tpu_custom_call" | custom-call | flops 579820584960 | bytes 51127296 | tf_op jit(solution)/shard_map/experts/pallas_call | solution.py:62
  470.9 4.0 combine.7
  474.9 4.0 combine.6
  485.9 3.9 all-to-all-start.2
  492.2 10.6 %combine_stacks.1 = (bf16[2,256,2048]{2,1,0:T(8,128)(2,1)}, bf16[2,256,2048]{2,1,0:T(8,128)(2,1)}, bf16[2,256,2048]{2,1,0:T(8,128)(2,1)}, bf16[2,256,2048]{2,1,0:T(8,128)(2,1)}) custom-call(s32[16,256]{1,0:T(8,128)} %copy-done.45, bf16[2,576,2048]{2,1,0:T(8,128)(2,1)} %get-tuple-element.136.refs_1_, bf16[2,576,2048]{2,1,0:T(8,128)(2,1)} %get-tuple-element.147.refs_2_, ...), custom_call_target="tpu_custom_call" | custom-call | flops 48318382080 | bytes 17842176 | tf_op jit(solution)/shard_map/combine_stacks/pallas_call | solution.py:62
  502.8 18.1 %weight_grad.3.refs_4_ = bf16[2,1024,2048]{2,1,0:T(8,128)(2,1)} custom-call(bf16[2,576,1024]{2,1,0:T(8,128)(2,1)} %get-tuple-element.157.refs_0_, bf16[2,576,1024]{2,1,0:T(8,128)(2,1)} %get-tuple-element.158.refs_1_, bf16[2,576,2048]{2,1,0:T(8,128)(2,1)} %dispatch.11.refs_1_.refs_6_.refs_10_.refs_2_, ...), custom_call_target="tpu_custom_call" | custom-call | flops 193273528320 | bytes 22544384 | tf_op jit(solution)/shard_map/weight_grad/pallas_call | solution.py:62
  524.8 18.3 %weight_grad.4.refs_8_ = bf16[2,2048,1024]{2,1,0:T(8,128)(2,1)} custom-call(bf16[2,576,2048]{2,1,0:T(8,128)(2,1)} %get-tuple-element.129.refs_0_, bf16[2,576,2048]{2,1,0:T(8,128)(2,1)} %get-tuple-element.140.refs_3_.refs_0_.refs_1_, bf16[2,576,1024]{2,1,0:T(8,128)(2,1)} %get-tuple-element.159.refs_2_, bf16[2,576,1024]{2,1,0:T(8,128)(2,1)} %get-tuple-element.160.refs_3_, ...), custom_call_target="tpu_custom_call" | custom-call | flops 193273528320 | bytes 22544384 | tf_op jit(solution)/shard_map/weight_grad/pallas_call | solution.py:62
  552.1 30.8 %collective-permute-done.35 = bf16[256,2048]{1,0:T(8,128)(2,1)} collective-permute-done((bf16[256,2048]{1,0:T(8,128)(2,1)}, bf16[256,2048]{1,0:T(8,128)(2,1)}, u32[]{:S(2)}, u32[]{:S(2)}) %collective-permute-start.35) | collective-permute-done | bytes 1048608 | tf_op jit(solution)/shard_map/ppermute | solution.py:88
  586.8 18.5 %weight_grad.5 = bf16[2,2048,1024]{2,1,0:T(8,128)(2,1)} custom-call(bf16[2,576,2048]{2,1,0:T(8,128)(2,1)} %get-tuple-element.129.refs_0_, bf16[2,576,2048]{2,1,0:T(8,128)(2,1)} %get-tuple-element.140.refs_3_.refs_0_.refs_1_, bf16[2,576,1024]{2,1,0:T(8,128)(2,1)} %get-tuple-element.170.refs_2_, bf16[2,576,1024]{2,1,0:T(8,128)(2,1)} %get-tuple-element.171.refs_3_, ...), custom_call_target="tpu_custom_call" | custom-call | flops 193273528320 | bytes 22544384 | tf_op jit(solution)/shard_map/weight_grad/pallas_call | solution.py:62
  611.8 9.1 %collective-permute-done.36 = bf16[256,2048]{1,0:T(8,128)(2,1)} collective-permute-done((bf16[256,2048]{1,0:T(8,128)(2,1)}, bf16[256,2048]{1,0:T(8,128)(2,1)}, u32[]{:S(2)}, u32[]{:S(2)}) %collective-permute-start.36) | collective-permute-done | bytes 1048608 | tf_op jit(solution)/shard_map/ppermute | solution.py:88
  627.3 9.9 %out_back.1 = bf16[256,2048]{1,0:T(8,128)(2,1)} custom-call(s32[12]{0:T(128)} %pad_add_fusion.ids.refs_0_, bf16[256,2048]{1,0:T(8,128)(2,1)} %fusion.17.d_ref, bf16[2048,512]{1,0:T(8,128)(2,1)} %get-tuple-element.123.refs_0_, bf16[2048,512]{1,0:T(8,128)(2,1)} %collective-permute-done.11.refs_1_, bf16[2048,512]{1,0:T(8,128)(2,1)} %collective-permute-done.12.refs_2_, ...), custom_call_target="tpu_custom_call" | custom-call | flops 42949672960 | bytes 10485760 | tf_op jit(solution)/shard_map/out_back/pallas_call | solution.py:62
  644.2 11.3 %collective-permute-done.33 = bf16[2,256,2048]{2,1,0:T(8,128)(2,1)} collective-permute-done((bf16[2,256,2048]{2,1,0:T(8,128)(2,1)}, bf16[2,256,2048]{2,1,0:T(8,128)(2,1)}, u32[]{:S(2)}, u32[]{:S(2)}) %collective-permute-start.33) | collective-permute-done | bytes 2097184 | tf_op jit(solution)/shard_map/ppermute | solution.py:88
  661.6 7.4 all-to-all-done.3
  672.6 23.4 %attend_back.1 = (f32[1024,512]{1,0:T(8,128)}, f32[1024,512]{1,0:T(8,128)}, bf16[1024,512]{1,0:T(8,128)(2,1)}, f32[16,1024]{1,0:T(8,128)}, f32[1,512]{1,0:T(1,128)}, /*index=5*/f32[1,512]{1,0:T(1,128)}) custom-call(bf16[1024,512]{1,0:T(8,128)(2,1)} %get-tuple-element.177.q_ref, bf16[1024,512]{1,0:T(8,128)(2,1)} %get-tuple-element.178.k_ref, ...), custom_call_target="tpu_custom_call" | custom-call | flops 75161927680 | bytes 14823424 | tf_op jit(solution)/shard_map/attend_back/pallas_call | solution.py:62
  699.5 10.6 %vo_grads.1 = (bf16[2,256,1024]{2,1,0:T(8,128)(2,1)}, bf16[2,256,1024]{2,1,0:T(8,128)(2,1)}, bf16[2,256,1024]{2,1,0:T(8,128)(2,1)}, bf16[2,256,1024]{2,1,0:T(8,128)(2,1)}) custom-call(s32[12]{0:T(128)} %pad_add_fusion.ids.refs_0_, bf16[1024,2048]{1,0:T(8,128)(2,1)} %get-tuple-element.176.h_ref.refs_1_, bf16[1024,512]{1,0:T(8,128)(2,1)} %get-tuple-element.185.dv_ref, ...), custom_call_target="tpu_custom_call" | custom-call | flops 85899345920 | bytes 14680064 | tf_op jit(solution)/shard_map/vo_grads/pallas_call | solution.py:62
  713.6 12.8 %qk_back.1 = (bf16[2,272,1024]{2,1,0:T(8,128)(2,1)}, bf16[2,272,1024]{2,1,0:T(8,128)(2,1)}, bf16[2,272,1024]{2,1,0:T(8,128)(2,1)}, bf16[2,272,1024]{2,1,0:T(8,128)(2,1)}, bf16[1024,1024]{1,0:T(8,128)(2,1)}) custom-call(s32[12]{0:T(128)} %pad_add_fusion.ids.refs_0_, bf16[1024,2048]{1,0:T(8,128)(2,1)} %get-tuple-element.176.h_ref.refs_1_, ...), custom_call_target="tpu_custom_call" | custom-call | flops 85899345920 | bytes 19423232 | tf_op jit(solution)/shard_map/qk_back/pallas_call | solution.py:62
  728.5 13.8 %d_h.1 = bf16[4,256,2048]{2,1,0:T(8,128)(2,1)} custom-call(s32[12]{0:T(128)} %pad_add_fusion.ids.refs_0_, bf16[1024,1024]{1,0:T(8,128)(2,1)} %get-tuple-element.187.d_ref, bf16[1024,512]{1,0:T(8,128)(2,1)} %get-tuple-element.185.dv_ref, bf16[2048,1536]{1,0:T(8,128)(2,1)} %get-tuple-element.188.w_ref), custom_call_target="tpu_custom_call" | custom-call | flops 128849018880 | bytes 13631488 | tf_op jit(solution)/shard_map/d_h/pallas_call | solution.py:62
  747.1 13.6 %collective-permute-done.37 = bf16[256,2048]{1,0:T(8,128)(2,1)} collective-permute-done((bf16[256,2048]{1,0:T(8,128)(2,1)}, bf16[256,2048]{1,0:T(8,128)(2,1)}, u32[]{:S(2)}, u32[]{:S(2)}) %collective-permute-start.37) | collective-permute-done | bytes 1048608 | tf_op jit(solution)/shard_map/ppermute | solution.py:88
  764.5 18.3 %collective-permute-done.44 = bf16[2,272,1024]{2,1,0:T(8,128)(2,1)} collective-permute-done((bf16[2,272,1024]{2,1,0:T(8,128)(2,1)}, bf16[2,272,1024]{2,1,0:T(8,128)(2,1)}, u32[]{:S(2)}, u32[]{:S(2)}) %collective-permute-start.44) | collective-permute-done | bytes 1114144 | tf_op jit(solution)/shard_map/ppermute | solution.py:88
  789.1 16.6 %collective-permute-done.43 = bf16[2,272,1024]{2,1,0:T(8,128)(2,1)S(1)} collective-permute-done((bf16[2,272,1024]{2,1,0:T(8,128)(2,1)}, bf16[2,272,1024]{2,1,0:T(8,128)(2,1)S(1)}, u32[]{:S(2)}, u32[]{:S(2)}) %collective-permute-start.43) | collective-permute-done | bytes 1114144 | tf_op jit(solution)/shard_map/ppermute | solution.py:88
  805.7 15.0 %collective-permute-done.45 = bf16[2,272,1024]{2,1,0:T(8,128)(2,1)S(1)} collective-permute-done((bf16[2,272,1024]{2,1,0:T(8,128)(2,1)S(1)}, bf16[2,272,1024]{2,1,0:T(8,128)(2,1)S(1)}, u32[]{:S(2)}, u32[]{:S(2)}) %collective-permute-start.45) | collective-permute-done | bytes 1114144 | tf_op jit(solution)/shard_map/ppermute | solution.py:88
  828.4 18.4 %collective-permute-done.50 = bf16[272,1024]{1,0:T(8,128)(2,1)S(1)} collective-permute-done((bf16[272,1024]{1,0:T(8,128)(2,1)S(1)}, bf16[272,1024]{1,0:T(8,128)(2,1)S(1)}, u32[]{:S(2)}, u32[]{:S(2)}) %collective-permute-start.50) | collective-permute-done | bytes 557088 | tf_op jit(solution)/shard_map/ppermute | solution.py:88
  847.8 4.1 convert_element_type.263.refs_13_
  851.9 4.1 convert_element_type.264.refs_14_
  856.0 4.1 convert_element_type.265.refs_15_
  866.4 8.6 collective-permute-done.52.refs_7_
  875.0 4.3 fusion.5.refs_16_
  881.1 7.9 finish.1
  (360 shorter events, 181.4 us)
Async XLA Ops:
  7.2 148.1 %all-gather.6.cloned.1.call-start = ((), (), s32[]{:S(2)}) async-start(), calls=%async_computation.12 | async-start | bytes 5242880 | tf_op jit(solution)/shard_map/all_gather | solution.py:798
  11.3 48.8 %collective-permute-start.1 = (bf16[256,2048]{1,0:T(8,128)(2,1)}, bf16[256,2048]{1,0:T(8,128)(2,1)}, u32[]{:S(2)}, u32[]{:S(2)}) collective-permute-start(bf16[256,2048]{1,0:T(8,128)(2,1)} %pad_maximum_fusion.refs_0_), channel_id=1, source_target_pairs={{0,2},{1,3},{2,0},{3,1},{4,6},{5,7},{6,4},{7,5},{8,10},{9,11},{10,... | collective-permute-start | bytes 3145736 | tf_op jit(solution)/shard_map/ppermute | solution.py:88
  14.3 55.0 %collective-permute-start.3 = (bf16[256,2048]{1,0:T(8,128)(2,1)}, bf16[256,2048]{1,0:T(8,128)(2,1)}, u32[]{:S(2)}, u32[]{:S(2)}) collective-permute-start(bf16[256,2048]{1,0:T(8,128)(2,1)} %pad_maximum_fusion.refs_0_), channel_id=1, source_target_pairs={{0,4},{1,5},{2,6},{3,7},{4,0},{5,1},{6,2},{7,3},{8,12},{9,13},{10,... | collective-permute-start | bytes 3145736 | tf_op jit(solution)/shard_map/ppermute | solution.py:88
  16.9 138.3 %collective-permute-start = (bf16[256,2048]{1,0:T(8,128)(2,1)}, bf16[256,2048]{1,0:T(8,128)(2,1)}, u32[]{:S(2)}, u32[]{:S(2)}) collective-permute-start(bf16[256,2048]{1,0:T(8,128)(2,1)} %pad_maximum_fusion.refs_0_), channel_id=1, source_target_pairs={{0,1},{1,0},{2,3},{3,2},{4,5},{5,4},{6,7},{7,6},{8,9},{9,8},{10,11... | collective-permute-start | bytes 3145736 | tf_op jit(solution)/shard_map/ppermute | solution.py:88
  62.7 42.5 %all-to-all-start = ((bf16[8,48,256]{2,1,0:T(8,128)(2,1)}), bf16[8,48,256]{2,1,0:T(8,128)(2,1)S(1)}, u32[]{:S(2)}, u32[]{:S(2)}) async-start(bf16[8,48,256]{2,1,0:T(8,128)(2,1)} %broadcast_in_dim.59), calls=%async_computation | async-start | bytes 393216 | tf_op jit(solution)/shard_map/all_to_all | solution.py:786
  105.3 49.9 %collective-permute-start.4 = (bf16[256,2048]{1,0:T(8,128)(2,1)}, bf16[256,2048]{1,0:T(8,128)(2,1)}, u32[]{:S(2)}, u32[]{:S(2)}) collective-permute-start(bf16[256,2048]{1,0:T(8,128)(2,1)} %collective-permute-done.3.refs_4_), channel_id=1, source_target_pairs={{0,1},{1,0},{2,3},{3,2},{4,5},{5,4},{6,7},{7,6},{8,9},{9,8},{10,11... | collective-permute-start | bytes 3145736 | tf_op jit(solution)/shard_map/ppermute | solution.py:88
  110.1 43.0 %collective-permute-start.7 = (bf16[256,2048]{1,0:T(8,128)(2,1)S(1)}, bf16[256,2048]{1,0:T(8,128)(2,1)S(1)}, u32[]{:S(2)}, u32[]{:S(2)}) collective-permute-start(bf16[256,2048]{1,0:T(8,128)(2,1)S(1)} %bitcast.137), channel_id=1, source_target_pairs={{0,2},{1,3},{2,0},{3,1},{4,6},{5,7},{6,4},{7,5},{8,10},{9,11},{10,... | collective-permute-start | bytes 3145736 | tf_op jit(solution)/shard_map/ppermute | solution.py:88
  110.4 42.8 %collective-permute-start.6 = (bf16[256,2048]{1,0:T(8,128)(2,1)}, bf16[256,2048]{1,0:T(8,128)(2,1)S(1)}, u32[]{:S(2)}, u32[]{:S(2)}) collective-permute-start(bf16[256,2048]{1,0:T(8,128)(2,1)} %collective-permute-done.5.refs_6_), channel_id=1, source_target_pairs={{0,1},{1,0},{2,3},{3,2},{4,5},{5,4},{6,7},{7,6},{8,9},{9,8},{10,11... | collective-permute-start | bytes 3145736 | tf_op jit(solution)/shard_map/ppermute | solution.py:88
  112.2 64.5 %collective-permute-start.19 = (bf16[256,2048]{1,0:T(8,128)(2,1)S(1)}, bf16[256,2048]{1,0:T(8,128)(2,1)}, u32[]{:S(2)}, u32[]{:S(2)}) collective-permute-start(bf16[256,2048]{1,0:T(8,128)(2,1)S(1)} %bitcast.138), channel_id=1, source_target_pairs={{0,4},{1,5},{2,6},{3,7},{4,0},{5,1},{6,2},{7,3},{8,12},{9,13},{10,... | collective-permute-start | bytes 3145736 | tf_op jit(solution)/shard_map/ppermute | solution.py:88
  154.4 47.5 %collective-permute-start.20 = (bf16[256,2048]{1,0:T(8,128)(2,1)S(1)}, bf16[256,2048]{1,0:T(8,128)(2,1)}, u32[]{:S(2)}, u32[]{:S(2)}) collective-permute-start(bf16[256,2048]{1,0:T(8,128)(2,1)S(1)} %bitcast.139), channel_id=1, source_target_pairs={{0,1},{1,0},{2,3},{3,2},{4,5},{5,4},{6,7},{7,6},{8,9},{9,8},{10,11... | collective-permute-start | bytes 3145736 | tf_op jit(solution)/shard_map/ppermute | solution.py:88
  172.3 49.2 %collective-permute-start.12 = (bf16[2048,512]{1,0:T(8,128)(2,1)}, bf16[2048,512]{1,0:T(8,128)(2,1)}, u32[]{:S(2)}, u32[]{:S(2)}) collective-permute-start(bf16[2048,512]{1,0:T(8,128)(2,1)} %get-tuple-element.123.refs_0_), channel_id=1, source_target_pairs={{0,16},{8,24},{16,0},{24,8},{1,17},{9,25},{17,1},{25,9},{2,18},{10... | collective-permute-start | bytes 6291464 | tf_op jit(solution)/shard_map/ppermute | solution.py:92
  179.3 91.1 %collective-permute-start.23 = (bf16[256,2048]{1,0:T(8,128)(2,1)}, bf16[256,2048]{1,0:T(8,128)(2,1)}, u32[]{:S(2)}, u32[]{:S(2)}) collective-permute-start(bf16[256,2048]{1,0:T(8,128)(2,1)} %collective-permute-done.19.refs_1_), channel_id=1, source_target_pairs={{0,1},{1,0},{2,3},{3,2},{4,5},{5,4},{6,7},{7,6},{8,9},{9,8},{10,11... | collective-permute-start | bytes 3145736 | tf_op jit(solution)/shard_map/ppermute | solution.py:88
  180.5 39.1 %collective-permute-start.10 = (f32[16,1024]{1,0:T(8,128)}, f32[16,1024]{1,0:T(8,128)S(1)}, u32[]{:S(2)}, u32[]{:S(2)}) collective-permute-start(f32[16,1024]{1,0:T(8,128)} %get-tuple-element.121), channel_id=1, source_target_pairs={{0,24},{8,16},{16,8},{24,0},{1,25},{9,17},{17,9},{25,1},{2,26},{10... | collective-permute-start | bytes 196616 | tf_op jit(solution)/shard_map/ppermute | solution.py:92
  180.5 39.1 %collective-permute-start.8 = (f32[16,1024]{1,0:T(8,128)}, f32[16,1024]{1,0:T(8,128)S(1)}, u32[]{:S(2)}, u32[]{:S(2)}) collective-permute-start(f32[16,1024]{1,0:T(8,128)} %get-tuple-element.121), channel_id=1, source_target_pairs={{0,8},{8,0},{16,24},{24,16},{1,9},{9,1},{17,25},{25,17},{2,10},{10... | collective-permute-start | bytes 196616 | tf_op jit(solution)/shard_map/ppermute | solution.py:92
  219.6 38.4 %collective-permute-start.11 = (bf16[2048,512]{1,0:T(8,128)(2,1)S(1)}, bf16[2048,512]{1,0:T(8,128)(2,1)}, u32[]{:S(2)}, u32[]{:S(2)}) collective-permute-start(bf16[2048,512]{1,0:T(8,128)(2,1)S(1)} %copy-done.56), channel_id=1, source_target_pairs={{0,8},{8,0},{16,24},{24,16},{1,9},{9,1},{17,25},{25,17},{2,10},{10... | collective-permute-start | bytes 6291464 | tf_op jit(solution)/shard_map/ppermute | solution.py:92
  221.5 36.4 %collective-permute-start.13 = (bf16[2048,512]{1,0:T(8,128)(2,1)}, bf16[2048,512]{1,0:T(8,128)(2,1)}, u32[]{:S(2)}, u32[]{:S(2)}) collective-permute-start(bf16[2048,512]{1,0:T(8,128)(2,1)} %collective-permute-done.12.refs_2_), channel_id=1, source_target_pairs={{0,8},{8,0},{16,24},{24,16},{1,9},{9,1},{17,25},{25,17},{2,10},{10... | collective-permute-start | bytes 6291464 | tf_op jit(solution)/shard_map/ppermute | solution.py:92
  242.3 455.8 %all-gather.4.cloned.1.call-start = ((), (), s32[]{:S(2)}) async-start(), calls=%async_computation.8 | async-start | bytes 5242880 | tf_op jit(solution)/shard_map/all_gather | solution.py:855
  266.8 47.9 %collective-permute-start.17 = (bf16[256,2048]{1,0:T(8,128)(2,1)}, bf16[256,2048]{1,0:T(8,128)(2,1)S(1)}, u32[]{:S(2)}, u32[]{:S(2)}) collective-permute-start(bf16[256,2048]{1,0:T(8,128)(2,1)} %get-tuple-element.125.refs_0_), channel_id=1, source_target_pairs={{0,1},{1,0},{2,3},{3,2},{4,5},{5,4},{6,7},{7,6},{8,9},{9,8},{10,11... | collective-permute-start | bytes 3145736 | tf_op jit(solution)/shard_map/ppermute | solution.py:88
  268.4 46.0 %collective-permute-start.14 = (bf16[256,2048]{1,0:T(8,128)(2,1)}, bf16[256,2048]{1,0:T(8,128)(2,1)S(1)}, u32[]{:S(2)}, u32[]{:S(2)}) collective-permute-start(bf16[256,2048]{1,0:T(8,128)(2,1)} %get-tuple-element.125.refs_0_), channel_id=1, source_target_pairs={{0,2},{1,3},{2,0},{3,1},{4,6},{5,7},{6,4},{7,5},{8,10},{9,11},{10,... | collective-permute-start | bytes 3145736 | tf_op jit(solution)/shard_map/ppermute | solution.py:88
  269.7 50.6 %collective-permute-start.16 = (bf16[256,2048]{1,0:T(8,128)(2,1)}, bf16[256,2048]{1,0:T(8,128)(2,1)}, u32[]{:S(2)}, u32[]{:S(2)}) collective-permute-start(bf16[256,2048]{1,0:T(8,128)(2,1)} %get-tuple-element.125.refs_0_), channel_id=1, source_target_pairs={{0,4},{1,5},{2,6},{3,7},{4,0},{5,1},{6,2},{7,3},{8,12},{9,13},{10,... | collective-permute-start | bytes 3145736 | tf_op jit(solution)/shard_map/ppermute | solution.py:88
  338.1 65.8 %collective-permute-start.26 = (bf16[256,2048]{1,0:T(8,128)(2,1)}, bf16[256,2048]{1,0:T(8,128)(2,1)}, u32[]{:S(2)}, u32[]{:S(2)}) collective-permute-start(bf16[256,2048]{1,0:T(8,128)(2,1)} %collective-permute-done.16.refs_1_), channel_id=1, source_target_pairs={{0,1},{1,0},{2,3},{3,2},{4,5},{5,4},{6,7},{7,6},{8,9},{9,8},{10,11... | collective-permute-start | bytes 3145736 | tf_op jit(solution)/shard_map/ppermute | solution.py:88
  361.2 47.1 %collective-permute-start.25 = (bf16[256,2048]{1,0:T(8,128)(2,1)}, bf16[256,2048]{1,0:T(8,128)(2,1)}, u32[]{:S(2)}, u32[]{:S(2)}) collective-permute-start(bf16[256,2048]{1,0:T(8,128)(2,1)} %collective-permute-done.24.refs_8_.refs_1_.refs_12_), channel_id=1, source_target_pairs={{0,1},{1,0},{2,3},{3,2},{4,5},{5,4},{6,7},{7,6},{8,9},{9,8},{10,11... | collective-permute-start | bytes 3145736 | tf_op jit(solution)/shard_map/ppermute | solution.py:88
  420.7 44.8 %collective-permute-start.28 = (bf16[256,2048]{1,0:T(8,128)(2,1)}, bf16[256,2048]{1,0:T(8,128)(2,1)}, u32[]{:S(2)}, u32[]{:S(2)}) collective-permute-start(bf16[256,2048]{1,0:T(8,128)(2,1)} %get-tuple-element.146.refs_9_.refs_6_), channel_id=1, source_target_pairs={{0,1},{1,0},{2,3},{3,2},{4,5},{5,4},{6,7},{7,6},{8,9},{9,8},{10,11... | collective-permute-start | bytes 3145736 | tf_op jit(solution)/shard_map/ppermute | solution.py:88
  422.5 45.7 %collective-permute-start.27 = (bf16[256,2048]{1,0:T(8,128)(2,1)}, bf16[256,2048]{1,0:T(8,128)(2,1)}, u32[]{:S(2)}, u32[]{:S(2)}) collective-permute-start(bf16[256,2048]{1,0:T(8,128)(2,1)} %get-tuple-element.144.refs_7_.refs_4_), channel_id=1, source_target_pairs={{0,1},{1,0},{2,3},{3,2},{4,5},{5,4},{6,7},{7,6},{8,9},{9,8},{10,11... | collective-permute-start | bytes 3145736 | tf_op jit(solution)/shard_map/ppermute | solution.py:88
  478.8 43.4 %collective-permute-start.30 = (bf16[256,2048]{1,0:T(8,128)(2,1)}, bf16[256,2048]{1,0:T(8,128)(2,1)}, u32[]{:S(2)}, u32[]{:S(2)}) collective-permute-start(bf16[256,2048]{1,0:T(8,128)(2,1)} %get-tuple-element.153.refs_10_), channel_id=1, source_target_pairs={{0,1},{1,0},{2,3},{3,2},{4,5},{5,4},{6,7},{7,6},{8,9},{9,8},{10,11... | collective-permute-start | bytes 3145736 | tf_op jit(solution)/shard_map/ppermute | solution.py:88
  485.9 35.0 %all-to-all-start.2 = ((f32[8,2,256]{2,1,0:T(2,128)}), f32[8,2,256]{2,1,0:T(2,128)}, u32[]{:S(2)}, u32[]{:S(2)}) async-start(f32[8,2,256]{2,1,0:T(2,128)} %constant_dynamic-update-slice_fusion.8), calls=%async_computation.2 | async-start | bytes 32768 | tf_op jit(solution)/shard_map/all_to_all | solution.py:903
  489.8 358.0 %reduce-scatter.4.cloned.1.call-start = ((), (), s32[]{:S(2)}) async-start(), calls=%async_computation.9 | async-start | bytes 10485760 | tf_op jit(solution)/shard_map/reduce_scatter | solution.py:914
  490.3 52.9 %collective-permute-start.29 = (bf16[256,2048]{1,0:T(8,128)(2,1)}, bf16[256,2048]{1,0:T(8,128)(2,1)}, u32[]{:S(2)}, u32[]{:S(2)}) collective-permute-start(bf16[256,2048]{1,0:T(8,128)(2,1)} %get-tuple-element.151.refs_8_), channel_id=1, source_target_pairs={{0,1},{1,0},{2,3},{3,2},{4,5},{5,4},{6,7},{7,6},{8,9},{9,8},{10,11... | collective-permute-start | bytes 3145736 | tf_op jit(solution)/shard_map/ppermute | solution.py:88
  544.9 307.1 %reduce-scatter.6.cloned.1.call-start = ((), (), s32[]{:S(2)}) async-start(), calls=%async_computation.10 | async-start | bytes 10485760 | tf_op jit(solution)/shard_map/reduce_scatter | solution.py:914
  545.1 37.7 %collective-permute-start.35 = (bf16[256,2048]{1,0:T(8,128)(2,1)}, bf16[256,2048]{1,0:T(8,128)(2,1)}, u32[]{:S(2)}, u32[]{:S(2)}) collective-permute-start(bf16[256,2048]{1,0:T(8,128)(2,1)} %add_convert_fusion.6.refs_6_.refs_7_), channel_id=1, source_target_pairs={{0,2},{1,3},{2,0},{3,1},{4,6},{5,7},{6,4},{7,5},{8,10},{9,11},{10,... | collective-permute-start | bytes 3145736 | tf_op jit(solution)/shard_map/ppermute | solution.py:88
  547.6 64.3 %collective-permute-start.34 = (bf16[256,2048]{1,0:T(8,128)(2,1)}, bf16[256,2048]{1,0:T(8,128)(2,1)}, u32[]{:S(2)}, u32[]{:S(2)}) collective-permute-start(bf16[256,2048]{1,0:T(8,128)(2,1)} %add_convert_fusion.8.refs_4_.refs_5_), channel_id=1, source_target_pairs={{0,2},{1,3},{2,0},{3,1},{4,6},{5,7},{6,4},{7,5},{8,10},{9,11},{10,... | collective-permute-start | bytes 3145736 | tf_op jit(solution)/shard_map/ppermute | solution.py:88
  550.0 55.3 %collective-permute-start.32 = (bf16[2,256,2048]{2,1,0:T(8,128)(2,1)}, bf16[2,256,2048]{2,1,0:T(8,128)(2,1)}, u32[]{:S(2)}, u32[]{:S(2)}) collective-permute-start(bf16[2,256,2048]{2,1,0:T(8,128)(2,1)} %get-tuple-element.167), channel_id=1, source_target_pairs={{0,1},{1,0},{2,3},{3,2},{4,5},{5,4},{6,7},{7,6},{8,9},{9,8},{10,11... | collective-permute-start | bytes 6291464 | tf_op jit(solution)/shard_map/ppermute | solution.py:88
  550.6 93.7 %collective-permute-start.31 = (bf16[2,256,2048]{2,1,0:T(8,128)(2,1)}, bf16[2,256,2048]{2,1,0:T(8,128)(2,1)}, u32[]{:S(2)}, u32[]{:S(2)}) collective-permute-start(bf16[2,256,2048]{2,1,0:T(8,128)(2,1)} %get-tuple-element.165), channel_id=1, source_target_pairs={{0,1},{1,0},{2,3},{3,2},{4,5},{5,4},{6,7},{7,6},{8,9},{9,8},{10,11... | collective-permute-start | bytes 6291464 | tf_op jit(solution)/shard_map/ppermute | solution.py:88
  585.4 35.5 %collective-permute-start.36 = (bf16[256,2048]{1,0:T(8,128)(2,1)}, bf16[256,2048]{1,0:T(8,128)(2,1)}, u32[]{:S(2)}, u32[]{:S(2)}) collective-permute-start(bf16[256,2048]{1,0:T(8,128)(2,1)} %add_convert_fusion.5), channel_id=1, source_target_pairs={{0,4},{1,5},{2,6},{3,7},{4,0},{5,1},{6,2},{7,3},{8,12},{9,13},{10,... | collective-permute-start | bytes 3145736 | tf_op jit(solution)/shard_map/ppermute | solution.py:88
  609.2 46.3 %collective-permute-start.33 = (bf16[2,256,2048]{2,1,0:T(8,128)(2,1)}, bf16[2,256,2048]{2,1,0:T(8,128)(2,1)}, u32[]{:S(2)}, u32[]{:S(2)}) collective-permute-start(bf16[2,256,2048]{2,1,0:T(8,128)(2,1)} %add_convert_fusion.1), channel_id=1, source_target_pairs={{0,2},{1,3},{2,0},{3,1},{4,6},{5,7},{6,4},{7,5},{8,10},{9,11},{10,... | collective-permute-start | bytes 6291464 | tf_op jit(solution)/shard_map/ppermute | solution.py:88
  639.5 29.5 %all-to-all-start.3 = ((bf16[256,4,512]{2,0,1:T(8,128)(2,1)}), bf16[256,4,512]{2,0,1:T(8,128)(2,1)S(1)}, u32[]{:S(2)}, u32[]{:S(2)}) async-start(bf16[256,4,512]{2,0,1:T(8,128)(2,1)} %bitcast.133), calls=%async_computation.3 | async-start | bytes 2097152 | tf_op jit(solution)/shard_map/all_to_all | solution.py:936
  643.1 212.9 %reduce-scatter.8.cloned.1.call-start = ((), (), s32[]{:S(2)}) async-start(), calls=%async_computation.11 | async-start | bytes 10485760 | tf_op jit(solution)/shard_map/reduce_scatter | solution.py:914
  710.1 32.2 %collective-permute-start.47 = (bf16[2,256,1024]{2,1,0:T(8,128)(2,1)}, bf16[2,256,1024]{2,1,0:T(8,128)(2,1)}, u32[]{:S(2)}, u32[]{:S(2)}) collective-permute-start(bf16[2,256,1024]{2,1,0:T(8,128)(2,1)} %get-tuple-element.197), channel_id=1, source_target_pairs={{0,1},{1,0},{2,3},{3,2},{4,5},{5,4},{6,7},{7,6},{8,9},{9,8},{10,11... | collective-permute-start | bytes 3145736 | tf_op jit(solution)/shard_map/ppermute | solution.py:88
  710.1 74.4 %collective-permute-start.46 = (bf16[2,256,1024]{2,1,0:T(8,128)(2,1)}, bf16[2,256,1024]{2,1,0:T(8,128)(2,1)}, u32[]{:S(2)}, u32[]{:S(2)}) collective-permute-start(bf16[2,256,1024]{2,1,0:T(8,128)(2,1)} %get-tuple-element.195), channel_id=1, source_target_pairs={{0,1},{1,0},{2,3},{3,2},{4,5},{5,4},{6,7},{7,6},{8,9},{9,8},{10,11... | collective-permute-start | bytes 3145736 | tf_op jit(solution)/shard_map/ppermute | solution.py:88
  713.0 47.7 %collective-permute-start.37 = (bf16[256,2048]{1,0:T(8,128)(2,1)}, bf16[256,2048]{1,0:T(8,128)(2,1)}, u32[]{:S(2)}, u32[]{:S(2)}) collective-permute-start(bf16[256,2048]{1,0:T(8,128)(2,1)} %fusion.10), channel_id=1, source_target_pairs={{0,4},{1,5},{2,6},{3,7},{4,0},{5,1},{6,2},{7,3},{8,12},{9,13},{10,... | collective-permute-start | bytes 3145736 | tf_op jit(solution)/shard_map/ppermute | solution.py:88
  726.5 56.3 %collective-permute-start.44 = (bf16[2,272,1024]{2,1,0:T(8,128)(2,1)}, bf16[2,272,1024]{2,1,0:T(8,128)(2,1)}, u32[]{:S(2)}, u32[]{:S(2)}) collective-permute-start(bf16[2,272,1024]{2,1,0:T(8,128)(2,1)} %get-tuple-element.194), channel_id=1, source_target_pairs={{0,1},{1,0},{2,3},{3,2},{4,5},{5,4},{6,7},{7,6},{8,9},{9,8},{10,11... | collective-permute-start | bytes 3342344 | tf_op jit(solution)/shard_map/ppermute | solution.py:88
  726.6 79.2 %collective-permute-start.43 = (bf16[2,272,1024]{2,1,0:T(8,128)(2,1)}, bf16[2,272,1024]{2,1,0:T(8,128)(2,1)S(1)}, u32[]{:S(2)}, u32[]{:S(2)}) collective-permute-start(bf16[2,272,1024]{2,1,0:T(8,128)(2,1)} %get-tuple-element.192), channel_id=1, source_target_pairs={{0,1},{1,0},{2,3},{3,2},{4,5},{5,4},{6,7},{7,6},{8,9},{9,8},{10,11... | collective-permute-start | bytes 3342344 | tf_op jit(solution)/shard_map/ppermute | solution.py:88
  744.4 40.1 %collective-permute-start.48 = (bf16[2,256,1024]{2,1,0:T(8,128)(2,1)S(1)}, bf16[2,256,1024]{2,1,0:T(8,128)(2,1)S(1)}, u32[]{:S(2)}, u32[]{:S(2)}) collective-permute-start(bf16[2,256,1024]{2,1,0:T(8,128)(2,1)S(1)} %add_convert_fusion.3), channel_id=1, source_target_pairs={{0,2},{1,3},{2,0},{3,1},{4,6},{5,7},{6,4},{7,5},{8,10},{9,11},{10,... | collective-permute-start | bytes 3145736 | tf_op jit(solution)/shard_map/ppermute | solution.py:88
  764.3 58.5 %collective-permute-start.41 = (bf16[2,256,2048]{2,1,0:T(8,128)(2,1)S(1)}, bf16[2,256,2048]{2,1,0:T(8,128)(2,1)S(1)}, u32[]{:S(2)}, u32[]{:S(2)}) collective-permute-start(bf16[2,256,2048]{2,1,0:T(8,128)(2,1)S(1)} %slice.240), channel_id=1, source_target_pairs={{0,8},{8,0},{16,24},{24,16},{1,9},{9,1},{17,25},{25,17},{2,10},{10... | collective-permute-start | bytes 6291464 | tf_op jit(solution)/shard_map/ppermute | solution.py:92
  784.5 36.2 %collective-permute-start.45 = (bf16[2,272,1024]{2,1,0:T(8,128)(2,1)S(1)}, bf16[2,272,1024]{2,1,0:T(8,128)(2,1)S(1)}, u32[]{:S(2)}, u32[]{:S(2)}) collective-permute-start(bf16[2,272,1024]{2,1,0:T(8,128)(2,1)S(1)} %add_convert_fusion.2), channel_id=1, source_target_pairs={{0,2},{1,3},{2,0},{3,1},{4,6},{5,7},{6,4},{7,5},{8,10},{9,11},{10,... | collective-permute-start | bytes 3342344 | tf_op jit(solution)/shard_map/ppermute | solution.py:88
  786.5 34.9 %collective-permute-start.49 = (bf16[256,1024]{1,0:T(8,128)(2,1)S(1)}, bf16[256,1024]{1,0:T(8,128)(2,1)S(1)}, u32[]{:S(2)}, u32[]{:S(2)}) collective-permute-start(bf16[256,1024]{1,0:T(8,128)(2,1)S(1)} %fusion.14), channel_id=1, source_target_pairs={{0,4},{1,5},{2,6},{3,7},{4,0},{5,1},{6,2},{7,3},{8,12},{9,13},{10,... | collective-permute-start | bytes 1572872 | tf_op jit(solution)/shard_map/ppermute | solution.py:88
  826.1 37.7 %collective-permute-start.42 = (bf16[256,2048]{1,0:T(8,128)(2,1)}, bf16[256,2048]{1,0:T(8,128)(2,1)}, u32[]{:S(2)}, u32[]{:S(2)}) collective-permute-start(bf16[256,2048]{1,0:T(8,128)(2,1)} %slice_bitcast_fusion.3), channel_id=1, source_target_pairs={{0,16},{8,24},{16,0},{24,8},{1,17},{9,25},{17,1},{25,9},{2,18},{10... | collective-permute-start | bytes 3145736 | tf_op jit(solution)/shard_map/ppermute | solution.py:92
  828.0 35.3 %collective-permute-start.55 = (bf16[256,1024]{1,0:T(8,128)(2,1)}, bf16[256,1024]{1,0:T(8,128)(2,1)}, u32[]{:S(2)}, u32[]{:S(2)}) collective-permute-start(bf16[256,1024]{1,0:T(8,128)(2,1)} %fusion.12.refs_9_), channel_id=1, source_target_pairs={{0,16},{8,24},{16,0},{24,8},{1,17},{9,25},{17,1},{25,9},{2,18},{10... | collective-permute-start | bytes 1572872 | tf_op jit(solution)/shard_map/ppermute | solution.py:92
  (87 other events, 1490.3 us)
Sparse Core Ops, SparseCore 0:
  9.6 37.1 all-gather.5
  258.0 32.7 all-gather.3
  545.0 71.4 reduce-scatter.3
  619.1 96.9 reduce-scatter.5
  718.5 71.5 reduce-scatter.7

commit v8 on v7

--- a/solution.py
+++ b/solution.py
@@ -97,16 +97,28 @@
     return jnp.bitwise_xor(ids, ep_index) if n_ep == 8 else ids
 
 
-def gather_steps(value, after=None):
+MIDDLE = [(2, 4), (3, 5), (4, 2), (5, 3)]
+OUTWARD = [(2, 0), (3, 1), (4, 6), (5, 7)]
+
+
+def gather_line(value):
+    crossed = swap(value, 1)
+    near = swap(value, 2)
+    inner = lax.ppermute(value, "ep", MIDDLE)
+    near_x, outer = swap(near, 1), lax.ppermute(near, "ep", MIDDLE)
+    near_x, crossed, outer = tie(near_x, crossed, outer)
+    far = outer + lax.ppermute(inner, "ep", OUTWARD)
+    farther = inner + lax.ppermute(outer, "ep", OUTWARD)
+    return [value, crossed, near, near_x, far, swap(far, 1), farther, swap(farther, 1)]
+
+
+def gather_double(value, after):
     near, far = swap(value, 2), swap(value, 4)
-    crossed = value
-    if after is not None:
-        after, crossed, near = tie(after, value, near)
-    near_x = swap(near, 1)
-    near_x, far = tie(near_x, far)
     farther = swap(far, 2)
-    pieces = [value, swap(crossed, 1), near, near_x, far, swap(far, 1), farther, swap(farther, 1)]
-    return pieces, after
+    after, crossed, near = tie(after, value, near)
+    return [
+        value, swap(crossed, 1), near, swap(near, 1), far, swap(far, 1), farther, swap(farther, 1)
+    ], after
 
 
 def gather_whole(value):
@@ -115,7 +127,7 @@
 
 
 def gather(value, n_ep):
-    return gather_steps(value)[0] if n_ep == 8 else gather_whole(value)
+    return gather_line(value) if n_ep == 8 else gather_whole(value)
 
 
 def plus(left, right):
@@ -128,20 +140,40 @@
 
 def scatter_z(own, near, far, farther):
     far = plus(far, swap(farther, 2))
-    return own.astype(F32) + swap(near, 2).astype(F32) + swap(far, 4).astype(F32)
+    far, near = tie(far, near)
+    return own.astype(F32) + swap(near, 2).astype(F32) + swap(far, 4).astype(F32), far
 
 
 def scatter(pieces, n_ep):
     if n_ep != 8:
         stacked = jnp.stack(pieces)
         return lax.psum_scatter(stacked, "ep", scatter_dimension=0, tiled=False).astype(F32)
-    return scatter_z(*crossed_sums(pieces))
+    return scatter_z(*crossed_sums(pieces))[0]
 
 
 def stack_at(piece, n_ep):
     if n_ep != 8:
         return 0, piece
     return 2 * (piece % 2) + (piece // 2) % 2, piece // 4
+
+
+def stack_at_z(piece, n_ep):
+    if n_ep != 8:
+        return 0, piece
+    return (piece // 2) % 2, 2 * (piece % 2) + piece // 4
+
+
+def stack_shapes_z(n_ep, shape):
+    return [like((4, *shape), BF16)] * 2 if n_ep == 8 else [like((n_ep, *shape), BF16)]
+
+
+def scatter_stacks_z(stacks, n_ep):
+    if n_ep != 8:
+        return scatter_stacks(stacks, n_ep)[0]
+    even = stacks[0].astype(F32) + swap(stacks[1], 2).astype(F32)
+    far = jnp.concatenate([even[1:2], even[3:4]]).astype(BF16)
+    far = swap(far, 4).astype(F32)
+    return even[0] + far[0] + swap((even[2] + far[1]).astype(BF16), 1).astype(F32)
 
 
 def stack_shapes(n_ep, shape):
@@ -272,7 +304,7 @@
     width = dv_ref.shape[1]
     for k in range(count):
         block = block_at(ids, k, shard)
-        array, place = stack_at(k, count)
+        array, place = stack_at_z(k, count)
         stacks[array][place, :, :width] = product_left(h_ref[:, block], dv_ref[...]).astype(BF16)
         stacks[array][place, :, width:] = product_left(attn_ref[:, block], dz_ref[...]).astype(BF16)
 
@@ -282,7 +314,7 @@
     width = d_v.shape[1]
     return call(
         functools.partial(vo_grads_kernel, count, shard),
-        stack_shapes(count, (shard, 2 * width)),
+        stack_shapes_z(count, (shard, 2 * width)),
         [h_all, d_v, attn_all, d_z_cols],
         4 * h_all.size * width,
         "vo_grads",
@@ -799,9 +831,9 @@
     w_own = jnp.concatenate([own_columns(w) for w in (w_query, w_key, w_value, w_out)], axis=1)
     cot_own = cotangent[0]
     if n_ep == 8:
-        w_pieces = gather_steps(w_own)[0]
+        w_pieces = gather_line(w_own)
         w_pieces[6], cot_own = tie(w_pieces[6], cot_own)
-        cot_pieces, w_pieces[7] = gather_steps(cot_own, w_pieces[7])
+        cot_pieces, w_pieces[7] = gather_double(cot_own, w_pieces[7])
     else:
         w_pieces, cot_pieces = gather_whole(w_own), gather_whole(cot_own)
 
@@ -873,7 +905,7 @@
     rows, gates, home_gates = rows_of(0, [])
     for g in range(0, n_ep, group):
         d_rows = cots[g // group]
-        made = experts(rows, d_rows, gates, w_gate, w_up, w_down, d_pieces[-group:] + cots + h2_pieces[6:7])
+        made = experts(rows, d_rows, gates, w_gate, w_up, w_down, d_pieces[-group:] + cots + h2_pieces[4:7:2])
         groups.append((rows, d_rows, made))
         following = []
         if g + group < n_ep:
@@ -902,13 +934,16 @@
     d_gates = by_piece(jnp.concatenate(d_gates, axis=0).reshape(n_ep, local, tok_dev))
     d_gates = lax.all_to_all(d_gates, "ep", split_axis=0, concat_axis=0, tiled=True)
     d_gates = d_gates.reshape(expert_count, tok_dev)
-    grad_gate = weight_grad(ins, d_gate_rows, [grad_down, d_gates, *d_sums[3:]])
     if n_ep == 8:
-        d_sums[2], mix_stacks[2], mix_stacks[3], grad_down, grad_gate = tie(
-            d_sums[2], mix_stacks[2], mix_stacks[3], grad_down, grad_gate
+        d_sums[2], mix_stacks[2], mix_stacks[3], grad_down = tie(
+            d_sums[2], mix_stacks[2], mix_stacks[3], grad_down
         )
-    d_h2 = scatter_z(*d_sums) if n_ep == 8 else scatter(d_pieces, n_ep)
-    grad_up = weight_grad(ins, d_up_rows, [*d_sums, grad_gate])
+        d_h2, d_far = scatter_z(*d_sums)
+        d_last = [d_far]
+    else:
+        d_h2, d_last = scatter(d_pieces, n_ep), []
+    grad_gate = weight_grad(ins, d_gate_rows, [grad_down, d_gates, *d_last])
+    grad_up = weight_grad(ins, d_up_rows, [grad_gate])
 
     def over_sp(value):
         return lax.psum_scatter(value, "sp", scatter_dimension=1, tiled=True).astype(F32)
@@ -945,7 +980,7 @@
     )
     output = (x_one + last_hop(mix, mix_far)).astype(BF16)
     vo_stacks = vo_grads(ids, n_ep, h_all, d_v, attn_all, d_z_cols)
-    grad_vo = last_hop(*scatter_stacks(vo_stacks, n_ep)).astype(BF16)
+    grad_vo = scatter_stacks_z(vo_stacks, n_ep).astype(BF16)
 
     def placed(value):
         return lax.dynamic_update_slice_in_dim(
@@ -959,10 +994,7 @@
         ids, n_ep, h_all, d_qn, d_kn, q_raw, k_raw, scales, sum_sp(sums), tiny, vo_stacks[:1]
     )
     grad_qk, qk_far = scatter_stacks(qk_stacks, n_ep)
-    if n_ep == 8:
-        qk_far, grad_vo = tie(qk_far, grad_vo)
     grad_qk = last_hop(grad_qk, qk_far).astype(BF16)
-    grad_qk, grad_down, grad_gate, grad_up = tie(grad_qk, grad_down, grad_gate, grad_up)
 
     d_h = d_h_rows(ids, n_ep, n_sp, d_qk, d_v, w_qkv)
     output, d_h = tie(output, d_h)

time: 910 us -> 895 us (0.984)
  waiting for transfers between devices: 366 us -> 353 us
  other arithmetic: 63.2 us -> 72.5 us
    ppermute x40 -> x35, waiting for transfers between devices: 327 us -> 263 us  [swap(): return lax.ppermute(value, 'ep', [(i, i ^ bits) for i in range(8)])]
    ppermute x17, waiting for transfers between devices: 21.3 us -> 50.9 us  [swap_sp(): return lax.ppermute(value, 'sp', [(i, i ^ bits) for i in range(4)])]
    ppermute x0 -> x8, waiting for transfers between devices: none -> 22.9 us  [the longest x2 21.3 us: gather_line(): farther = inner + lax.ppermute(outer, 'ep', OUTWARD)]
    add x0 -> x5, other arithmetic: none -> 10.1 us  [the longest x2 4.53 us: gather_line(): far = outer + lax.ppermute(inner, 'ep', OUTWARD)]
    ppermute x0 -> x8, starting transfers between devices: none -> 9.62 us  [the longest x2 2.78 us: gather_line(): farther = inner + lax.ppermute(outer, 'ep', OUTWARD)]
    ppermute x40 -> x35, starting transfers between devices: 48.3 us -> 41.3 us  [swap(): return lax.ppermute(value, 'ep', [(i, i ^ bits) for i in range(8)])]
    convert_element_type x9 -> x8, other arithmetic: 20.6 us -> 16.5 us  [plus(): return (left.astype(F32) + right.astype(F32)).astype(left.dtype)]
  transfers between devices with their start and end apart: 67 -> 70, of which waited for: 23 -> 23; matrix products, arithmetic and copies ran while one was open for 10% -> 11% of each run, Pallas kernels for 35% -> 35%
where the time goes in v8:
time: 895 us; the launch traced here: 889 us
  waiting for transfers between devices  353 us (39%)
  Pallas kernels  319 us (36%)
  starting transfers between devices  81.3 us (9%)
  other arithmetic  72.5 us (8%)
  between operations  31 us (3%)
  local copies, waits for them, and re-layouts  29.7 us (3%)
    pallas_call x27, Pallas kernels, call(): pl.pallas_call(kernel, grid_spec=pltpu.PrefetchScalarGridSpec(num_scalar_...  319 us
    ppermute x35, waiting for transfers between devices, swap(): return lax.ppermute(value, 'ep', [(i, i ^ bits) for i in range(8)])  263 us
    ppermute x17, waiting for transfers between devices, swap_sp(): return lax.ppermute(value, 'sp', [(i, i ^ bits) for i in range(4)])  50.9 us
    ppermute x35, starting transfers between devices, swap(): return lax.ppermute(value, 'ep', [(i, i ^ bits) for i in range(8)])  41.3 us
    ppermute x2, waiting for transfers between devices, gather_line(): farther = inner + lax.ppermute(outer, 'ep', OUTWARD)  21.3 us
  transfers between devices with their start and end apart: 70, of which 23 were waited for; matrix products, arithmetic and copies ran while one was open for 11% of the time, Pallas kernels for 35%

profile of v8, /device:TPU:0, one launch (start us, length us, event | category | flops | bytes accessed | tf_op | source)
XLA Modules:
  0.0 889.5 jit_solution(11031590824472462506)
XLA Ops:
  16.6 21.2 %collective-permute-done.refs_2_ = bf16[256,2048]{1,0:T(8,128)(2,1)} collective-permute-done((bf16[256,2048]{1,0:T(8,128)(2,1)}, bf16[256,2048]{1,0:T(8,128)(2,1)}, u32[]{:S(2)}, u32[]{:S(2)}) %collective-permute-start) | collective-permute-done | bytes 1048608 | tf_op jit(solution)/shard_map/ppermute | solution.py:88
  42.0 4.9 all-to-all-start
  51.0 12.7 %collective-permute-done.1.refs_3_ = bf16[256,2048]{1,0:T(8,128)(2,1)} collective-permute-done((bf16[256,2048]{1,0:T(8,128)(2,1)}, bf16[256,2048]{1,0:T(8,128)(2,1)}, u32[]{:S(2)}, u32[]{:S(2)}) %collective-permute-start.1) | collective-permute-done | bytes 1048608 | tf_op jit(solution)/shard_map/ppermute | solution.py:88
  87.3 12.0 %collective-permute-done.7 = bf16[256,2048]{1,0:T(8,128)(2,1)} collective-permute-done((bf16[256,2048]{1,0:T(8,128)(2,1)}, bf16[256,2048]{1,0:T(8,128)(2,1)}, u32[]{:S(2)}, u32[]{:S(2)}) %collective-permute-start.7) | collective-permute-done | bytes 1048608 | tf_op jit(solution)/shard_map/ppermute | solution.py:111
  106.7 40.1 %collective-permute-done.9.refs_0_ = bf16[256,2048]{1,0:T(8,128)(2,1)} collective-permute-done((bf16[256,2048]{1,0:T(8,128)(2,1)S(1)}, bf16[256,2048]{1,0:T(8,128)(2,1)}, u32[]{:S(2)}, u32[]{:S(2)}) %collective-permute-start.9) | collective-permute-done | bytes 1048608 | tf_op jit(solution)/shard_map/ppermute | solution.py:88
  147.3 17.0 %qkv_project.1 = (f32[1024,512]{1,0:T(8,128)}, f32[1024,512]{1,0:T(8,128)}, bf16[1024,512]{1,0:T(8,128)(2,1)}, f32[16,1024]{1,0:T(8,128)}, bf16[2048,1536]{1,0:T...) custom-call(s32[12]{0:T(128)} %pad_add_fusion.ids.refs_0_, bf16[1024,2048]{1,0:T(8,128)(2,1)} %bitcast.177, ...), custom_call_target="tpu_custom_call" | custom-call | flops 128849018880 | bytes 30482432 | tf_op jit(solution)/shard_map/qkv_project/pallas_call | solution.py:62
  175.0 16.8 %collective-permute-done.23.refs_1_ = bf16[256,2048]{1,0:T(8,128)(2,1)} collective-permute-done((bf16[256,2048]{1,0:T(8,128)(2,1)}, bf16[256,2048]{1,0:T(8,128)(2,1)}, u32[]{:S(2)}, u32[]{:S(2)}) %collective-permute-start.23) | collective-permute-done | bytes 1048608 | tf_op jit(solution)/shard_map/ppermute | solution.py:88
  193.9 18.5 %collective-permute-done.11 = f32[16,1024]{1,0:T(8,128)S(1)} collective-permute-done((f32[16,1024]{1,0:T(8,128)}, f32[16,1024]{1,0:T(8,128)S(1)}, u32[]{:S(2)}, u32[]{:S(2)}) %collective-permute-start.11) | collective-permute-done | bytes 65568 | tf_op jit(solution)/shard_map/ppermute | solution.py:92
  215.0 17.2 %attend.1 = (bf16[1024,512]{1,0:T(8,128)(2,1)}, bf16[1024,512]{1,0:T(8,128)(2,1)}, bf16[1024,512]{1,0:T(8,128)(2,1)}) custom-call(f32[1024,512]{1,0:T(8,128)} %get-tuple-element.112.qr_ref.refs_4_, f32[1024,512]{1,0:T(8,128)} %get-tuple-element.113.kr_ref.refs_5_, bf16[1024,512]{1,0:T(8,128)(2,1)} %get-tuple-element.114.v_ref, ...), custom_call_target="tpu_custom_call" | custom-call | flops 32212254720 | bytes 9510912 | tf_op jit(solution)/shard_map/attend/pallas_call | solution.py:62
  239.5 10.6 %all-to-all-done.1 = bf16[4,256,512]{2,1,0:T(8,128)(2,1)S(1)} async-done(((bf16[4,256,512]{2,1,0:T(8,128)(2,1)}), bf16[4,256,512]{2,1,0:T(8,128)(2,1)S(1)}, u32[]{:S(2)}, u32[]{:S(2)}) %all-to-all-start.1) | async-done | bytes 1048608 | tf_op jit(solution)/shard_map/all_to_all | solution.py:882
  251.3 9.2 %out_project.1 = (f32[256,2048]{1,0:T(8,128)}, bf16[256,2048]{1,0:T(8,128)(2,1)}) custom-call(s32[12]{0:T(128)} %pad_add_fusion.ids.refs_0_, bf16[256,2048]{1,0:T(8,128)(2,1)} %bitcast.141, bf16[256,2048]{1,0:T(8,128)(2,1)} %bitcast.134, f32[1,2048]{1,0:T(1,128)} %bitcast.154, bf16[2048,512]{1,0:T(8,128)(2,1)} %get-tuple-element.117.refs_0_, ...), custom_call_target="tpu_custom_call" | custom-call | flops 42949672960 | bytes 13639680 | tf_op jit(solution)/shard_map/out_project/pallas_call | solution.py:62
  267.9 17.4 %collective-permute-done.16.refs_0_ = bf16[256,2048]{1,0:T(8,128)(2,1)S(1)} collective-permute-done((bf16[256,2048]{1,0:T(8,128)(2,1)}, bf16[256,2048]{1,0:T(8,128)(2,1)S(1)}, u32[]{:S(2)}, u32[]{:S(2)}) %collective-permute-start.16) | collective-permute-done | bytes 1048608 | tf_op jit(solution)/shard_map/ppermute | solution.py:88
  291.6 17.7 %collective-permute-done.17.refs_1_ = bf16[256,2048]{1,0:T(8,128)(2,1)} collective-permute-done((bf16[256,2048]{1,0:T(8,128)(2,1)S(1)}, bf16[256,2048]{1,0:T(8,128)(2,1)}, u32[]{:S(2)}, u32[]{:S(2)}) %collective-permute-start.17) | collective-permute-done | bytes 1048608 | tf_op jit(solution)/shard_map/ppermute | solution.py:88
  316.3 4.5 dispatch.8
  320.8 4.5 dispatch.9
  325.3 9.3 %collective-permute-done.28 = bf16[256,2048]{1,0:T(8,128)(2,1)S(1)} collective-permute-done((bf16[256,2048]{1,0:T(8,128)(2,1)S(1)}, bf16[256,2048]{1,0:T(8,128)(2,1)S(1)}, u32[]{:S(2)}, u32[]{:S(2)}) %collective-permute-start.28) | collective-permute-done | bytes 1048608 | tf_op jit(solution)/shard_map/ppermute | solution.py:111
  337.4 42.5 %experts.2 = (bf16[2,576,1024]{2,1,0:T(8,128)(2,1)}, bf16[2,576,1024]{2,1,0:T(8,128)(2,1)}, bf16[2,576,1024]{2,1,0:T(8,128)(2,1)}, f32[2,576,1]{2,1,0:T(8,128)},...) custom-call(bf16[2,576,2048]{2,1,0:T(8,128)(2,1)} %get-tuple-element.124.refs_0_, ...), custom_call_target="tpu_custom_call" | custom-call | flops 579820584960 | bytes 51127296 | tf_op jit(solution)/shard_map/experts/pallas_call | solution.py:62
  379.8 4.5 dispatch.14
  384.3 4.5 dispatch.15
  388.8 4.0 combine.5
  392.8 4.0 combine.4
  398.8 42.2 %experts.3 = (bf16[2,576,1024]{2,1,0:T(8,128)(2,1)}, bf16[2,576,1024]{2,1,0:T(8,128)(2,1)}, bf16[2,576,1024]{2,1,0:T(8,128)(2,1)}, f32[2,576,1]{2,1,0:T(8,128)},...) custom-call(bf16[2,576,2048]{2,1,0:T(8,128)(2,1)} %get-tuple-element.133.refs_3_.refs_0_.refs_1_, ...), custom_call_target="tpu_custom_call" | custom-call | flops 579820584960 | bytes 51127296 | tf_op jit(solution)/shard_map/experts/pallas_call | solution.py:62
  450.4 4.0 combine.6
  466.2 10.5 %combine_stacks.1 = (bf16[2,256,2048]{2,1,0:T(8,128)(2,1)}, bf16[2,256,2048]{2,1,0:T(8,128)(2,1)}, bf16[2,256,2048]{2,1,0:T(8,128)(2,1)}, bf16[2,256,2048]{2,1,0:T(8,128)(2,1)}) custom-call(s32[16,256]{1,0:T(8,128)} %copy-done.39, bf16[2,576,2048]{2,1,0:T(8,128)(2,1)} %get-tuple-element.129.refs_1_, bf16[2,576,2048]{2,1,0:T(8,128)(2,1)} %get-tuple-element.140.refs_2_, ...), custom_call_target="tpu_custom_call" | custom-call | flops 48318382080 | bytes 17842176 | tf_op jit(solution)/shard_map/combine_stacks/pallas_call | solution.py:62
  476.6 18.1 %weight_grad.3.refs_4_ = bf16[2,1024,2048]{2,1,0:T(8,128)(2,1)} custom-call(bf16[2,576,1024]{2,1,0:T(8,128)(2,1)} %get-tuple-element.150.refs_0_, bf16[2,576,1024]{2,1,0:T(8,128)(2,1)} %get-tuple-element.151.refs_1_, bf16[2,576,2048]{2,1,0:T(8,128)(2,1)} %dispatch.11.refs_1_.refs_6_.refs_10_.refs_2_, ...), custom_call_target="tpu_custom_call" | custom-call | flops 193273528320 | bytes 22544384 | tf_op jit(solution)/shard_map/weight_grad/pallas_call | solution.py:62
  494.7 4.4 all-to-all-done.2
  508.5 14.9 %collective-permute-done.38 = bf16[256,2048]{1,0:T(8,128)(2,1)S(1)} collective-permute-done((bf16[256,2048]{1,0:T(8,128)(2,1)S(1)}, bf16[256,2048]{1,0:T(8,128)(2,1)S(1)}, u32[]{:S(2)}, u32[]{:S(2)}) %collective-permute-start.38) | collective-permute-done | bytes 1048608 | tf_op jit(solution)/shard_map/ppermute | solution.py:88
  527.9 18.3 %weight_grad.4.refs_4_ = bf16[2,2048,1024]{2,1,0:T(8,128)(2,1)} custom-call(bf16[2,576,2048]{2,1,0:T(8,128)(2,1)} %get-tuple-element.124.refs_0_, bf16[2,576,2048]{2,1,0:T(8,128)(2,1)} %get-tuple-element.133.refs_3_.refs_0_.refs_1_, bf16[2,576,1024]{2,1,0:T(8,128)(2,1)} %get-tuple-element.165.refs_2_, bf16[2,576,1024]{2,1,0:T(8,128)(2,1)} %get-tuple-element.166.refs_3_, ...), custom_call_target="tpu_custom_call" | custom-call | flops 193273528320 | bytes 22544384 | tf_op jit(solution)/shard_map/weight_grad/pallas_call | solution.py:62
  546.3 18.4 %weight_grad.5 = bf16[2,2048,1024]{2,1,0:T(8,128)(2,1)} custom-call(bf16[2,576,2048]{2,1,0:T(8,128)(2,1)} %get-tuple-element.124.refs_0_, bf16[2,576,2048]{2,1,0:T(8,128)(2,1)} %get-tuple-element.133.refs_3_.refs_0_.refs_1_, bf16[2,576,1024]{2,1,0:T(8,128)(2,1)} %get-tuple-element.163.refs_2_, bf16[2,576,1024]{2,1,0:T(8,128)(2,1)} %get-tuple-element.164.refs_3_, ...), custom_call_target="tpu_custom_call" | custom-call | flops 193273528320 | bytes 22544384 | tf_op jit(solution)/shard_map/weight_grad/pallas_call | solution.py:62
  575.1 7.8 out_back.1
  590.0 4.7 collective-permute-done.34
  594.8 17.8 %collective-permute-done.36 = bf16[2,256,2048]{2,1,0:T(8,128)(2,1)} collective-permute-done((bf16[2,256,2048]{2,1,0:T(8,128)(2,1)}, bf16[2,256,2048]{2,1,0:T(8,128)(2,1)}, u32[]{:S(2)}, u32[]{:S(2)}) %collective-permute-start.36) | collective-permute-done | bytes 2097184 | tf_op jit(solution)/shard_map/ppermute | solution.py:88
  622.3 23.2 %attend_back.1 = (f32[1024,512]{1,0:T(8,128)}, f32[1024,512]{1,0:T(8,128)}, bf16[1024,512]{1,0:T(8,128)(2,1)}, f32[16,1024]{1,0:T(8,128)}, f32[1,512]{1,0:T(1,128)}, /*index=5*/f32[1,512]{1,0:T(1,128)}) custom-call(bf16[1024,512]{1,0:T(8,128)(2,1)} %get-tuple-element.172.q_ref, bf16[1024,512]{1,0:T(8,128)(2,1)} %get-tuple-element.173.k_ref, ...), custom_call_target="tpu_custom_call" | custom-call | flops 75161927680 | bytes 14823424 | tf_op jit(solution)/shard_map/attend_back/pallas_call | solution.py:62
  649.2 10.7 %vo_grads.1 = (bf16[4,256,1024]{2,1,0:T(8,128)(2,1)}, bf16[4,256,1024]{2,1,0:T(8,128)(2,1)}) custom-call(s32[12]{0:T(128)} %pad_add_fusion.ids.refs_0_, bf16[1024,2048]{1,0:T(8,128)(2,1)} %get-tuple-element.171.h_ref.refs_1_, bf16[1024,512]{1,0:T(8,128)(2,1)} %get-tuple-element.180.dv_ref, bf16[1024,2048]{1,0:T(8,128)(2,1)} %all-gather.4.cloned.1.call-done.attn_ref, ...), custom_call_target="tpu_custom_call" | custom-call | flops 85899345920 | bytes 14680064 | tf_op jit(solution)/shard_map/vo_grads/pallas_call | solution.py:62
  665.0 12.8 %qk_back.1 = (bf16[2,272,1024]{2,1,0:T(8,128)(2,1)}, bf16[2,272,1024]{2,1,0:T(8,128)(2,1)}, bf16[2,272,1024]{2,1,0:T(8,128)(2,1)}, bf16[2,272,1024]{2,1,0:T(8,128)(2,1)}, bf16[1024,1024]{1,0:T(8,128)(2,1)}) custom-call(s32[12]{0:T(128)} %pad_add_fusion.ids.refs_0_, bf16[1024,2048]{1,0:T(8,128)(2,1)} %get-tuple-element.171.h_ref.refs_1_, ...), custom_call_target="tpu_custom_call" | custom-call | flops 85899345920 | bytes 19423232 | tf_op jit(solution)/shard_map/qk_back/pallas_call | solution.py:62
  679.9 14.2 %d_h.1 = bf16[4,256,2048]{2,1,0:T(8,128)(2,1)} custom-call(s32[12]{0:T(128)} %pad_add_fusion.ids.refs_0_, bf16[1024,1024]{1,0:T(8,128)(2,1)} %get-tuple-element.182.d_ref, bf16[1024,512]{1,0:T(8,128)(2,1)} %get-tuple-element.180.dv_ref, bf16[2048,1536]{1,0:T(8,128)(2,1)} %get-tuple-element.183.w_ref), custom_call_target="tpu_custom_call" | custom-call | flops 128849018880 | bytes 13631488 | tf_op jit(solution)/shard_map/d_h/pallas_call | solution.py:62
  694.1 33.9 %collective-permute-done.41 = bf16[256,2048]{1,0:T(8,128)(2,1)} collective-permute-done((bf16[256,2048]{1,0:T(8,128)(2,1)}, bf16[256,2048]{1,0:T(8,128)(2,1)}, u32[]{:S(2)}, u32[]{:S(2)}) %collective-permute-start.41) | collective-permute-done | bytes 1048608 | tf_op jit(solution)/shard_map/ppermute | solution.py:88
  734.2 4.1 collective-permute-start.49
  741.3 40.5 %collective-permute-done.49 = bf16[2,272,1024]{2,1,0:T(8,128)(2,1)S(1)} collective-permute-done((bf16[2,272,1024]{2,1,0:T(8,128)(2,1)S(1)}, bf16[2,272,1024]{2,1,0:T(8,128)(2,1)S(1)}, u32[]{:S(2)}, u32[]{:S(2)}) %collective-permute-start.49) | collective-permute-done | bytes 1114144 | tf_op jit(solution)/shard_map/ppermute | solution.py:88
  783.6 19.0 %collective-permute-done.55 = bf16[2,256,1024]{2,1,0:T(8,128)(2,1)S(1)} collective-permute-done((bf16[2,256,1024]{2,1,0:T(8,128)(2,1)S(1)}, bf16[2,256,1024]{2,1,0:T(8,128)(2,1)S(1)}, u32[]{:S(2)}, u32[]{:S(2)}) %collective-permute-start.55) | collective-permute-done | bytes 1048608 | tf_op jit(solution)/shard_map/ppermute | solution.py:88
  807.4 5.5 collective-permute-done.50
  818.5 25.6 %collective-permute-done.52.refs_7_ = bf16[272,1024]{1,0:T(8,128)(2,1)} collective-permute-done((bf16[272,1024]{1,0:T(8,128)(2,1)}, bf16[272,1024]{1,0:T(8,128)(2,1)}, u32[]{:S(2)}, u32[]{:S(2)}) %collective-permute-start.52) | collective-permute-done | bytes 557088 | tf_op jit(solution)/shard_map/ppermute | solution.py:92
  844.7 6.7 collective-permute-done.58.refs_11_
  853.7 4.3 fusion.5.refs_16_
  858.0 4.1 convert_element_type.255.refs_13_
  862.1 4.1 convert_element_type.256.refs_14_
  866.2 4.1 convert_element_type.257.refs_15_
  870.2 7.9 finish.1
  (357 shorter events, 183.5 us)
Async XLA Ops:
  7.2 140.1 %all-gather.6.cloned.1.call-start = ((), (), s32[]{:S(2)}) async-start(), calls=%async_computation.12 | async-start | bytes 5242880 | tf_op jit(solution)/shard_map/all_gather | solution.py:830
  14.3 36.7 %collective-permute-start.2 = (bf16[256,2048]{1,0:T(8,128)(2,1)}, bf16[256,2048]{1,0:T(8,128)(2,1)}, u32[]{:S(2)}, u32[]{:S(2)}) collective-permute-start(bf16[256,2048]{1,0:T(8,128)(2,1)} %pad_maximum_fusion.refs_0_), channel_id=1, source_target_pairs={{0,1},{1,0},{2,3},{3,2},{4,5},{5,4},{6,7},{7,6},{8,9},{9,8},{10,11... | collective-permute-start | bytes 3145736 | tf_op jit(solution)/shard_map/ppermute | solution.py:88
  15.8 33.9 %collective-permute-start.4 = (bf16[256,2048]{1,0:T(8,128)(2,1)}, bf16[256,2048]{1,0:T(8,128)(2,1)S(1)}, u32[]{:S(2)}, u32[]{:S(2)}) collective-permute-start(bf16[256,2048]{1,0:T(8,128)(2,1)} %pad_maximum_fusion.refs_0_), channel_id=1, source_target_pairs={{2,4},{3,5},{4,2},{5,3},{10,12},{11,13},{12,10},{13,11},{18,20},{1... | collective-permute-start | bytes 3145736 | tf_op jit(solution)/shard_map/ppermute | solution.py:107
  42.0 41.7 %all-to-all-start = ((bf16[8,48,256]{2,1,0:T(8,128)(2,1)}), bf16[8,48,256]{2,1,0:T(8,128)(2,1)S(1)}, u32[]{:S(2)}, u32[]{:S(2)}) async-start(bf16[8,48,256]{2,1,0:T(8,128)(2,1)} %broadcast_in_dim.59), calls=%async_computation | async-start | bytes 393216 | tf_op jit(solution)/shard_map/all_to_all | solution.py:818
  49.7 34.2 %collective-permute-start.5 = (bf16[256,2048]{1,0:T(8,128)(2,1)S(1)}, bf16[256,2048]{1,0:T(8,128)(2,1)}, u32[]{:S(2)}, u32[]{:S(2)}) collective-permute-start(bf16[256,2048]{1,0:T(8,128)(2,1)S(1)} %collective-permute-done.4), channel_id=1, source_target_pairs={{2,0},{3,1},{4,6},{5,7},{10,8},{11,9},{12,14},{13,15},{18,16},{19,... | collective-permute-start | bytes 3145736 | tf_op jit(solution)/shard_map/ppermute | solution.py:110
  63.7 35.5 %collective-permute-start.7 = (bf16[256,2048]{1,0:T(8,128)(2,1)}, bf16[256,2048]{1,0:T(8,128)(2,1)}, u32[]{:S(2)}, u32[]{:S(2)}) collective-permute-start(bf16[256,2048]{1,0:T(8,128)(2,1)} %collective-permute-done.3), channel_id=1, source_target_pairs={{2,0},{3,1},{4,6},{5,7},{10,8},{11,9},{12,14},{13,15},{18,16},{19,... | collective-permute-start | bytes 3145736 | tf_op jit(solution)/shard_map/ppermute | solution.py:111
  85.9 61.4 %collective-permute-start.6 = (bf16[256,2048]{1,0:T(8,128)(2,1)S(1)}, bf16[256,2048]{1,0:T(8,128)(2,1)}, u32[]{:S(2)}, u32[]{:S(2)}) collective-permute-start(bf16[256,2048]{1,0:T(8,128)(2,1)S(1)} %add.185.refs_4_), channel_id=1, source_target_pairs={{0,1},{1,0},{2,3},{3,2},{4,5},{5,4},{6,7},{7,6},{8,9},{9,8},{10,11... | collective-permute-start | bytes 3145736 | tf_op jit(solution)/shard_map/ppermute | solution.py:88
  100.9 45.8 %collective-permute-start.8 = (bf16[256,2048]{1,0:T(8,128)(2,1)S(1)}, bf16[256,2048]{1,0:T(8,128)(2,1)}, u32[]{:S(2)}, u32[]{:S(2)}) collective-permute-start(bf16[256,2048]{1,0:T(8,128)(2,1)S(1)} %add.186.refs_6_), channel_id=1, source_target_pairs={{0,1},{1,0},{2,3},{3,2},{4,5},{5,4},{6,7},{7,6},{8,9},{9,8},{10,11... | collective-permute-start | bytes 3145736 | tf_op jit(solution)/shard_map/ppermute | solution.py:88
  102.7 44.0 %collective-permute-start.9 = (bf16[256,2048]{1,0:T(8,128)(2,1)S(1)}, bf16[256,2048]{1,0:T(8,128)(2,1)}, u32[]{:S(2)}, u32[]{:S(2)}) collective-permute-start(bf16[256,2048]{1,0:T(8,128)(2,1)S(1)} %bitcast.137), channel_id=1, source_target_pairs={{0,2},{1,3},{2,0},{3,1},{4,6},{5,7},{6,4},{7,5},{8,10},{9,11},{10,... | collective-permute-start | bytes 3145736 | tf_op jit(solution)/shard_map/ppermute | solution.py:88
  103.4 65.3 %collective-permute-start.22 = (bf16[256,2048]{1,0:T(8,128)(2,1)S(1)}, bf16[256,2048]{1,0:T(8,128)(2,1)}, u32[]{:S(2)}, u32[]{:S(2)}) collective-permute-start(bf16[256,2048]{1,0:T(8,128)(2,1)S(1)} %bitcast.138), channel_id=1, source_target_pairs={{0,4},{1,5},{2,6},{3,7},{4,0},{5,1},{6,2},{7,3},{8,12},{9,13},{10,... | collective-permute-start | bytes 3145736 | tf_op jit(solution)/shard_map/ppermute | solution.py:88
  164.4 50.1 %collective-permute-start.14 = (bf16[2048,512]{1,0:T(8,128)(2,1)}, bf16[2048,512]{1,0:T(8,128)(2,1)}, u32[]{:S(2)}, u32[]{:S(2)}) collective-permute-start(bf16[2048,512]{1,0:T(8,128)(2,1)} %get-tuple-element.117.refs_0_), channel_id=1, source_target_pairs={{0,16},{8,24},{16,0},{24,8},{1,17},{9,25},{17,1},{25,9},{2,18},{10... | collective-permute-start | bytes 6291464 | tf_op jit(solution)/shard_map/ppermute | solution.py:92
  168.7 43.6 %collective-permute-start.11 = (f32[16,1024]{1,0:T(8,128)}, f32[16,1024]{1,0:T(8,128)S(1)}, u32[]{:S(2)}, u32[]{:S(2)}) collective-permute-start(f32[16,1024]{1,0:T(8,128)} %get-tuple-element.115), channel_id=1, source_target_pairs={{0,16},{8,24},{16,0},{24,8},{1,17},{9,25},{17,1},{25,9},{2,18},{10... | collective-permute-start | bytes 196616 | tf_op jit(solution)/shard_map/ppermute | solution.py:92
  170.1 43.7 %collective-permute-start.12 = (f32[16,1024]{1,0:T(8,128)}, f32[16,1024]{1,0:T(8,128)S(1)}, u32[]{:S(2)}, u32[]{:S(2)}) collective-permute-start(f32[16,1024]{1,0:T(8,128)} %get-tuple-element.115), channel_id=1, source_target_pairs={{0,24},{8,16},{16,8},{24,0},{1,25},{9,17},{17,9},{25,1},{2,26},{10... | collective-permute-start | bytes 196616 | tf_op jit(solution)/shard_map/ppermute | solution.py:92
  191.8 43.9 %collective-permute-start.20 = (bf16[256,2048]{1,0:T(8,128)(2,1)}, bf16[256,2048]{1,0:T(8,128)(2,1)}, u32[]{:S(2)}, u32[]{:S(2)}) collective-permute-start(bf16[256,2048]{1,0:T(8,128)(2,1)} %collective-permute-done.9.refs_0_), channel_id=1, source_target_pairs={{0,1},{1,0},{2,3},{3,2},{4,5},{5,4},{6,7},{7,6},{8,9},{9,8},{10,11... | collective-permute-start | bytes 3145736 | tf_op jit(solution)/shard_map/ppermute | solution.py:88
  193.3 70.9 %collective-permute-start.25 = (bf16[256,2048]{1,0:T(8,128)(2,1)}, bf16[256,2048]{1,0:T(8,128)(2,1)}, u32[]{:S(2)}, u32[]{:S(2)}) collective-permute-start(bf16[256,2048]{1,0:T(8,128)(2,1)} %collective-permute-done.22.refs_1_), channel_id=1, source_target_pairs={{0,1},{1,0},{2,3},{3,2},{4,5},{5,4},{6,7},{7,6},{8,9},{9,8},{10,11... | collective-permute-start | bytes 3145736 | tf_op jit(solution)/shard_map/ppermute | solution.py:88
  212.4 75.3 %collective-permute-start.24 = (bf16[256,2048]{1,0:T(8,128)(2,1)}, bf16[256,2048]{1,0:T(8,128)(2,1)}, u32[]{:S(2)}, u32[]{:S(2)}) collective-permute-start(bf16[256,2048]{1,0:T(8,128)(2,1)} %collective-permute-done.23.refs_1_), channel_id=1, source_target_pairs={{0,1},{1,0},{2,3},{3,2},{4,5},{5,4},{6,7},{7,6},{8,9},{9,8},{10,11... | collective-permute-start | bytes 3145736 | tf_op jit(solution)/shard_map/ppermute | solution.py:88
  213.8 37.4 %collective-permute-start.13 = (bf16[2048,512]{1,0:T(8,128)(2,1)S(1)}, bf16[2048,512]{1,0:T(8,128)(2,1)}, u32[]{:S(2)}, u32[]{:S(2)}) collective-permute-start(bf16[2048,512]{1,0:T(8,128)(2,1)S(1)} %copy-done.52), channel_id=1, source_target_pairs={{0,8},{8,0},{16,24},{24,16},{1,9},{9,1},{17,25},{25,17},{2,10},{10... | collective-permute-start | bytes 6291464 | tf_op jit(solution)/shard_map/ppermute | solution.py:92
  214.5 36.8 %collective-permute-start.15 = (bf16[2048,512]{1,0:T(8,128)(2,1)}, bf16[2048,512]{1,0:T(8,128)(2,1)}, u32[]{:S(2)}, u32[]{:S(2)}) collective-permute-start(bf16[2048,512]{1,0:T(8,128)(2,1)} %collective-permute-done.14.refs_2_), channel_id=1, source_target_pairs={{0,8},{8,0},{16,24},{24,16},{1,9},{9,1},{17,25},{25,17},{2,10},{10... | collective-permute-start | bytes 6291464 | tf_op jit(solution)/shard_map/ppermute | solution.py:92
  235.7 412.2 %all-gather.4.cloned.1.call-start = ((), (), s32[]{:S(2)}) async-start(), calls=%async_computation.8 | async-start | bytes 5242880 | tf_op jit(solution)/shard_map/all_gather | solution.py:887
  260.5 31.1 %collective-permute-start.18 = (bf16[256,2048]{1,0:T(8,128)(2,1)}, bf16[256,2048]{1,0:T(8,128)(2,1)}, u32[]{:S(2)}, u32[]{:S(2)}) collective-permute-start(bf16[256,2048]{1,0:T(8,128)(2,1)} %get-tuple-element.119.refs_0_), channel_id=1, source_target_pairs={{0,1},{1,0},{2,3},{3,2},{4,5},{5,4},{6,7},{7,6},{8,9},{9,8},{10,11... | collective-permute-start | bytes 3145736 | tf_op jit(solution)/shard_map/ppermute | solution.py:88
  314.7 65.1 %collective-permute-start.30 = (bf16[256,2048]{1,0:T(8,128)(2,1)}, bf16[256,2048]{1,0:T(8,128)(2,1)}, u32[]{:S(2)}, u32[]{:S(2)}) collective-permute-start(bf16[256,2048]{1,0:T(8,128)(2,1)} %add.201.refs_8_.refs_1_.refs_12_), channel_id=1, source_target_pairs={{0,1},{1,0},{2,3},{3,2},{4,5},{5,4},{6,7},{7,6},{8,9},{9,8},{10,11... | collective-permute-start | bytes 3145736 | tf_op jit(solution)/shard_map/ppermute | solution.py:88
  335.9 48.4 %collective-permute-start.29 = (bf16[256,2048]{1,0:T(8,128)(2,1)}, bf16[256,2048]{1,0:T(8,128)(2,1)}, u32[]{:S(2)}, u32[]{:S(2)}) collective-permute-start(bf16[256,2048]{1,0:T(8,128)(2,1)} %add.202.refs_9_.refs_1_.refs_13_), channel_id=1, source_target_pairs={{0,1},{1,0},{2,3},{3,2},{4,5},{5,4},{6,7},{7,6},{8,9},{9,8},{10,11... | collective-permute-start | bytes 3145736 | tf_op jit(solution)/shard_map/ppermute | solution.py:88
  396.8 44.3 %collective-permute-start.32 = (bf16[256,2048]{1,0:T(8,128)(2,1)}, bf16[256,2048]{1,0:T(8,128)(2,1)}, u32[]{:S(2)}, u32[]{:S(2)}) collective-permute-start(bf16[256,2048]{1,0:T(8,128)(2,1)} %get-tuple-element.139.refs_9_.refs_6_), channel_id=1, source_target_pairs={{0,1},{1,0},{2,3},{3,2},{4,5},{5,4},{6,7},{7,6},{8,9},{9,8},{10,11... | collective-permute-start | bytes 3145736 | tf_op jit(solution)/shard_map/ppermute | solution.py:88
  397.4 46.5 %collective-permute-start.31 = (bf16[256,2048]{1,0:T(8,128)(2,1)}, bf16[256,2048]{1,0:T(8,128)(2,1)}, u32[]{:S(2)}, u32[]{:S(2)}) collective-permute-start(bf16[256,2048]{1,0:T(8,128)(2,1)} %get-tuple-element.137.refs_7_.refs_4_), channel_id=1, source_target_pairs={{0,1},{1,0},{2,3},{3,2},{4,5},{5,4},{6,7},{7,6},{8,9},{9,8},{10,11... | collective-permute-start | bytes 3145736 | tf_op jit(solution)/shard_map/ppermute | solution.py:88
  454.4 45.5 %collective-permute-start.37 = (bf16[256,2048]{1,0:T(8,128)(2,1)}, bf16[256,2048]{1,0:T(8,128)(2,1)}, u32[]{:S(2)}, u32[]{:S(2)}) collective-permute-start(bf16[256,2048]{1,0:T(8,128)(2,1)} %get-tuple-element.146.refs_10_), channel_id=1, source_target_pairs={{0,1},{1,0},{2,3},{3,2},{4,5},{5,4},{6,7},{7,6},{8,9},{9,8},{10,11... | collective-permute-start | bytes 3145736 | tf_op jit(solution)/shard_map/ppermute | solution.py:88
  455.0 49.4 %collective-permute-start.33 = (bf16[256,2048]{1,0:T(8,128)(2,1)}, bf16[256,2048]{1,0:T(8,128)(2,1)}, u32[]{:S(2)}, u32[]{:S(2)}) collective-permute-start(bf16[256,2048]{1,0:T(8,128)(2,1)} %get-tuple-element.144.refs_8_), channel_id=1, source_target_pairs={{0,1},{1,0},{2,3},{3,2},{4,5},{5,4},{6,7},{7,6},{8,9},{9,8},{10,11... | collective-permute-start | bytes 3145736 | tf_op jit(solution)/shard_map/ppermute | solution.py:88
  461.8 37.4 %all-to-all-start.2 = ((f32[8,2,256]{2,1,0:T(2,128)}), f32[8,2,256]{2,1,0:T(2,128)}, u32[]{:S(2)}, u32[]{:S(2)}) async-start(f32[8,2,256]{2,1,0:T(2,128)} %constant_dynamic-update-slice_fusion.8), calls=%async_computation.2 | async-start | bytes 32768 | tf_op jit(solution)/shard_map/all_to_all | solution.py:935
  465.7 392.2 %reduce-scatter.4.cloned.1.call-start = ((), (), s32[]{:S(2)}) async-start(), calls=%async_computation.9 | async-start | bytes 10485760 | tf_op jit(solution)/shard_map/reduce_scatter | solution.py:949
  506.1 58.5 %collective-permute-start.35 = (bf16[2,256,2048]{2,1,0:T(8,128)(2,1)}, bf16[2,256,2048]{2,1,0:T(8,128)(2,1)}, u32[]{:S(2)}, u32[]{:S(2)}) collective-permute-start(bf16[2,256,2048]{2,1,0:T(8,128)(2,1)} %get-tuple-element.154), channel_id=1, source_target_pairs={{0,1},{1,0},{2,3},{3,2},{4,5},{5,4},{6,7},{7,6},{8,9},{9,8},{10,11... | collective-permute-start | bytes 6291464 | tf_op jit(solution)/shard_map/ppermute | solution.py:88
  506.8 87.9 %collective-permute-start.34 = (bf16[2,256,2048]{2,1,0:T(8,128)(2,1)}, bf16[2,256,2048]{2,1,0:T(8,128)(2,1)}, u32[]{:S(2)}, u32[]{:S(2)}) collective-permute-start(bf16[2,256,2048]{2,1,0:T(8,128)(2,1)} %get-tuple-element.152), channel_id=1, source_target_pairs={{0,1},{1,0},{2,3},{3,2},{4,5},{5,4},{6,7},{7,6},{8,9},{9,8},{10,11... | collective-permute-start | bytes 6291464 | tf_op jit(solution)/shard_map/ppermute | solution.py:88
  508.2 353.8 %reduce-scatter.6.cloned.1.call-start = ((), (), s32[]{:S(2)}) async-start(), calls=%async_computation.10 | async-start | bytes 10485760 | tf_op jit(solution)/shard_map/reduce_scatter | solution.py:949
  524.8 44.0 %collective-permute-start.39 = (bf16[256,2048]{1,0:T(8,128)(2,1)}, bf16[256,2048]{1,0:T(8,128)(2,1)}, u32[]{:S(2)}, u32[]{:S(2)}) collective-permute-start(bf16[256,2048]{1,0:T(8,128)(2,1)} %add_convert_fusion.7.refs_4_), channel_id=1, source_target_pairs={{0,2},{1,3},{2,0},{3,1},{4,6},{5,7},{6,4},{7,5},{8,10},{9,11},{10,... | collective-permute-start | bytes 3145736 | tf_op jit(solution)/shard_map/ppermute | solution.py:88
  524.8 44.0 %collective-permute-start.40 = (bf16[256,2048]{1,0:T(8,128)(2,1)}, bf16[256,2048]{1,0:T(8,128)(2,1)}, u32[]{:S(2)}, u32[]{:S(2)}) collective-permute-start(bf16[256,2048]{1,0:T(8,128)(2,1)} %add_convert_fusion.4.refs_6_), channel_id=1, source_target_pairs={{0,4},{1,5},{2,6},{3,7},{4,0},{5,1},{6,2},{7,3},{8,12},{9,13},{10,... | collective-permute-start | bytes 3145736 | tf_op jit(solution)/shard_map/ppermute | solution.py:88
  568.6 44.0 %collective-permute-start.36 = (bf16[2,256,2048]{2,1,0:T(8,128)(2,1)}, bf16[2,256,2048]{2,1,0:T(8,128)(2,1)}, u32[]{:S(2)}, u32[]{:S(2)}) collective-permute-start(bf16[2,256,2048]{2,1,0:T(8,128)(2,1)} %add_convert_fusion.1), channel_id=1, source_target_pairs={{0,2},{1,3},{2,0},{3,1},{4,6},{5,7},{6,4},{7,5},{8,10},{9,11},{10,... | collective-permute-start | bytes 6291464 | tf_op jit(solution)/shard_map/ppermute | solution.py:88
  585.3 33.4 %all-to-all-start.3 = ((bf16[256,4,512]{2,0,1:T(8,128)(2,1)}), bf16[256,4,512]{2,0,1:T(8,128)(2,1)S(1)}, u32[]{:S(2)}, u32[]{:S(2)}) async-start(bf16[256,4,512]{2,0,1:T(8,128)(2,1)} %bitcast.133), calls=%async_computation.3 | async-start | bytes 2097152 | tf_op jit(solution)/shard_map/all_to_all | solution.py:971
  588.9 277.3 %reduce-scatter.8.cloned.1.call-start = ((), (), s32[]{:S(2)}) async-start(), calls=%async_computation.11 | async-start | bytes 10485760 | tf_op jit(solution)/shard_map/reduce_scatter | solution.py:949
  660.0 78.4 %collective-permute-start.54 = (bf16[4,256,1024]{2,1,0:T(8,128)(2,1)}, bf16[4,256,1024]{2,1,0:T(8,128)(2,1)}, u32[]{:S(2)}, u32[]{:S(2)}) collective-permute-start(bf16[4,256,1024]{2,1,0:T(8,128)(2,1)} %get-tuple-element.190), channel_id=1, source_target_pairs={{0,2},{1,3},{2,0},{3,1},{4,6},{5,7},{6,4},{7,5},{8,10},{9,11},{10,... | collective-permute-start | bytes 6291464 | tf_op jit(solution)/shard_map/ppermute | solution.py:88
  660.3 67.7 %collective-permute-start.41 = (bf16[256,2048]{1,0:T(8,128)(2,1)}, bf16[256,2048]{1,0:T(8,128)(2,1)}, u32[]{:S(2)}, u32[]{:S(2)}) collective-permute-start(bf16[256,2048]{1,0:T(8,128)(2,1)} %fusion.10), channel_id=1, source_target_pairs={{0,4},{1,5},{2,6},{3,7},{4,0},{5,1},{6,2},{7,3},{8,12},{9,13},{10,... | collective-permute-start | bytes 3145736 | tf_op jit(solution)/shard_map/ppermute | solution.py:88
  677.8 53.8 %collective-permute-start.48 = (bf16[2,272,1024]{2,1,0:T(8,128)(2,1)}, bf16[2,272,1024]{2,1,0:T(8,128)(2,1)}, u32[]{:S(2)}, u32[]{:S(2)}) collective-permute-start(bf16[2,272,1024]{2,1,0:T(8,128)(2,1)} %get-tuple-element.189), channel_id=1, source_target_pairs={{0,1},{1,0},{2,3},{3,2},{4,5},{5,4},{6,7},{7,6},{8,9},{9,8},{10,11... | collective-permute-start | bytes 3342344 | tf_op jit(solution)/shard_map/ppermute | solution.py:88
  678.3 63.0 %collective-permute-start.47 = (bf16[2,272,1024]{2,1,0:T(8,128)(2,1)}, bf16[2,272,1024]{2,1,0:T(8,128)(2,1)S(1)}, u32[]{:S(2)}, u32[]{:S(2)}) collective-permute-start(bf16[2,272,1024]{2,1,0:T(8,128)(2,1)} %get-tuple-element.187), channel_id=1, source_target_pairs={{0,1},{1,0},{2,3},{3,2},{4,5},{5,4},{6,7},{7,6},{8,9},{9,8},{10,11... | collective-permute-start | bytes 3342344 | tf_op jit(solution)/shard_map/ppermute | solution.py:88
  731.5 72.1 %collective-permute-start.45 = (bf16[2,256,2048]{2,1,0:T(8,128)(2,1)S(1)}, bf16[2,256,2048]{2,1,0:T(8,128)(2,1)S(1)}, u32[]{:S(2)}, u32[]{:S(2)}) collective-permute-start(bf16[2,256,2048]{2,1,0:T(8,128)(2,1)S(1)} %slice.253), channel_id=1, source_target_pairs={{0,8},{8,0},{16,24},{24,16},{1,9},{9,1},{17,25},{25,17},{2,10},{10... | collective-permute-start | bytes 6291464 | tf_op jit(solution)/shard_map/ppermute | solution.py:92
  734.2 47.6 %collective-permute-start.49 = (bf16[2,272,1024]{2,1,0:T(8,128)(2,1)S(1)}, bf16[2,272,1024]{2,1,0:T(8,128)(2,1)S(1)}, u32[]{:S(2)}, u32[]{:S(2)}) collective-permute-start(bf16[2,272,1024]{2,1,0:T(8,128)(2,1)S(1)} %add_convert_fusion.2), channel_id=1, source_target_pairs={{0,2},{1,3},{2,0},{3,1},{4,6},{5,7},{6,4},{7,5},{8,10},{9,11},{10,... | collective-permute-start | bytes 3342344 | tf_op jit(solution)/shard_map/ppermute | solution.py:88
  741.2 61.5 %collective-permute-start.55 = (bf16[2,256,1024]{2,1,0:T(8,128)(2,1)S(1)}, bf16[2,256,1024]{2,1,0:T(8,128)(2,1)S(1)}, u32[]{:S(2)}, u32[]{:S(2)}) collective-permute-start(bf16[2,256,1024]{2,1,0:T(8,128)(2,1)S(1)} %pad_maximum_fusion.1), channel_id=1, source_target_pairs={{0,4},{1,5},{2,6},{3,7},{4,0},{5,1},{6,2},{7,3},{8,12},{9,13},{10,... | collective-permute-start | bytes 3145736 | tf_op jit(solution)/shard_map/ppermute | solution.py:88
  782.5 30.4 %collective-permute-start.50 = (bf16[272,1024]{1,0:T(8,128)(2,1)S(1)}, bf16[272,1024]{1,0:T(8,128)(2,1)S(1)}, u32[]{:S(2)}, u32[]{:S(2)}) collective-permute-start(bf16[272,1024]{1,0:T(8,128)(2,1)S(1)} %fusion.15), channel_id=1, source_target_pairs={{0,4},{1,5},{2,6},{3,7},{4,0},{5,1},{6,2},{7,3},{8,12},{9,13},{10,... | collective-permute-start | bytes 1671176 | tf_op jit(solution)/shard_map/ppermute | solution.py:88
  805.8 45.6 %collective-permute-start.46 = (bf16[256,2048]{1,0:T(8,128)(2,1)}, bf16[256,2048]{1,0:T(8,128)(2,1)}, u32[]{:S(2)}, u32[]{:S(2)}) collective-permute-start(bf16[256,2048]{1,0:T(8,128)(2,1)} %slice_bitcast_fusion.2), channel_id=1, source_target_pairs={{0,16},{8,24},{16,0},{24,8},{1,17},{9,25},{17,1},{25,9},{2,18},{10... | collective-permute-start | bytes 3145736 | tf_op jit(solution)/shard_map/ppermute | solution.py:92
  813.9 30.2 %collective-permute-start.52 = (bf16[272,1024]{1,0:T(8,128)(2,1)}, bf16[272,1024]{1,0:T(8,128)(2,1)}, u32[]{:S(2)}, u32[]{:S(2)}) collective-permute-start(bf16[272,1024]{1,0:T(8,128)(2,1)} %fusion.9.refs_5_), channel_id=1, source_target_pairs={{0,16},{8,24},{16,0},{24,8},{1,17},{9,25},{17,1},{25,9},{2,18},{10... | collective-permute-start | bytes 1671176 | tf_op jit(solution)/shard_map/ppermute | solution.py:92
  817.3 34.2 %collective-permute-start.58 = (bf16[256,1024]{1,0:T(8,128)(2,1)}, bf16[256,1024]{1,0:T(8,128)(2,1)}, u32[]{:S(2)}, u32[]{:S(2)}) collective-permute-start(bf16[256,1024]{1,0:T(8,128)(2,1)} %fusion.14.refs_9_), channel_id=1, source_target_pairs={{0,16},{8,24},{16,0},{24,8},{1,17},{9,25},{17,1},{25,9},{2,18},{10... | collective-permute-start | bytes 1572872 | tf_op jit(solution)/shard_map/ppermute | solution.py:92
  818.5 51.8 %collective-permute-start.51 = (bf16[272,1024]{1,0:T(8,128)(2,1)}, bf16[272,1024]{1,0:T(8,128)(2,1)}, u32[]{:S(2)}, u32[]{:S(2)}) collective-permute-start(bf16[272,1024]{1,0:T(8,128)(2,1)} %fusion.9.refs_5_), channel_id=1, source_target_pairs={{0,8},{8,0},{16,24},{24,16},{1,9},{9,1},{17,25},{25,17},{2,10},{10... | collective-permute-start | bytes 1671176 | tf_op jit(solution)/shard_map/ppermute | solution.py:92
  (82 other events, 1627.6 us)
Sparse Core Ops, SparseCore 0:
  9.6 37.1 all-gather.5
  251.4 31.8 all-gather.3
  508.4 70.8 reduce-scatter.3
  581.9 85.7 reduce-scatter.5
  670.1 71.6 reduce-scatter.7

commit v9 on v8

--- a/solution.py
+++ b/solution.py
@@ -113,11 +113,12 @@
 
 
 def gather_double(value, after):
+    after, held = tie(after, value)
+    crossed = swap(held, 1)
     near, far = swap(value, 2), swap(value, 4)
     farther = swap(far, 2)
-    after, crossed, near = tie(after, value, near)
     return [
-        value, swap(crossed, 1), near, swap(near, 1), far, swap(far, 1), farther, swap(farther, 1)
+        value, crossed, near, swap(near, 1), far, swap(far, 1), farther, swap(farther, 1)
     ], after
 
 
@@ -155,25 +156,6 @@
     if n_ep != 8:
         return 0, piece
     return 2 * (piece % 2) + (piece // 2) % 2, piece // 4
-
-
-def stack_at_z(piece, n_ep):
-    if n_ep != 8:
-        return 0, piece
-    return (piece // 2) % 2, 2 * (piece % 2) + piece // 4
-
-
-def stack_shapes_z(n_ep, shape):
-    return [like((4, *shape), BF16)] * 2 if n_ep == 8 else [like((n_ep, *shape), BF16)]
-
-
-def scatter_stacks_z(stacks, n_ep):
-    if n_ep != 8:
-        return scatter_stacks(stacks, n_ep)[0]
-    even = stacks[0].astype(F32) + swap(stacks[1], 2).astype(F32)
-    far = jnp.concatenate([even[1:2], even[3:4]]).astype(BF16)
-    far = swap(far, 4).astype(F32)
-    return even[0] + far[0] + swap((even[2] + far[1]).astype(BF16), 1).astype(F32)
 
 
 def stack_shapes(n_ep, shape):
@@ -200,6 +182,12 @@
 
 
 def sum_sp(value):
+    n_sp = lax.axis_size("sp")
+    value = jnp.broadcast_to(value[None], (n_sp, *value.shape))
+    return jnp.sum(lax.all_to_all(value, "sp", split_axis=0, concat_axis=0, tiled=True), axis=0)
+
+
+def sum_sp_swaps(value):
     return (value + swap_sp(value, 1)) + (swap_sp(value, 2) + swap_sp(value, 3))
 
 
@@ -304,7 +292,7 @@
     width = dv_ref.shape[1]
     for k in range(count):
         block = block_at(ids, k, shard)
-        array, place = stack_at_z(k, count)
+        array, place = stack_at(k, count)
         stacks[array][place, :, :width] = product_left(h_ref[:, block], dv_ref[...]).astype(BF16)
         stacks[array][place, :, width:] = product_left(attn_ref[:, block], dz_ref[...]).astype(BF16)
 
@@ -314,7 +302,7 @@
     width = d_v.shape[1]
     return call(
         functools.partial(vo_grads_kernel, count, shard),
-        stack_shapes_z(count, (shard, 2 * width)),
+        stack_shapes(count, (shard, 2 * width)),
         [h_all, d_v, attn_all, d_z_cols],
         4 * h_all.size * width,
         "vo_grads",
@@ -371,7 +359,7 @@
     ).astype(BF16)
 
 
-def d_h_rows(ids, n_ep, n_sp, d_qk, d_v, w_qkv):
+def d_h_rows(ids, n_ep, n_sp, d_qk, d_v, w_qkv, after):
     total, wide = d_qk.shape
     depth = w_qkv.shape[0]
     rows = total // n_sp
@@ -385,6 +373,7 @@
         [d_qk, d_v, w_qkv],
         3 * d_qk.size * depth,
         "d_h",
+        after=after,
         scalars=(ids,),
         grid=(n_sp,),
         in_specs=[
@@ -860,8 +849,9 @@
     starts = starts[:, None].astype(jnp.int32)
 
     q_raw, k_raw, v_low, squares, w_qkv, w_o, h_all = qkv_project(ids, x_all, gains[0:1], w_pieces)
-    scales = lax.rsqrt(sum_sp(squares) / width + EPS)
-    w_o_parts = gather_sp(w_o)
+    squares, w_o = tie(sum_sp(squares), w_o)
+    scales = lax.rsqrt(squares / width + EPS)
+    w_o_over = swap_sp(w_o, 2)
     gain_q, gain_k = own_columns(gains)[1:2], own_columns(gains)[2:3]
     q_rot, k_rot, mixed = attend(
         q_raw, k_raw, v_low, scales, gain_q, gain_k, cosine, sine, starts
@@ -880,14 +870,15 @@
         return d_rows
 
     attn_tok = lax.all_to_all(mixed, "sp", split_axis=0, concat_axis=1, tiled=True)
-    near_rows = cot_rows(0, [])
+    w_o_over, attn_tok = tie(w_o_over, attn_tok)
+    w_o_parts = [w_o, swap_sp(w_o, 1), w_o_over, swap_sp(w_o_over, 1)]
     x_one, h2_low = out_project(
         ids, n_ep, attn_tok, tokens[0], gains[3:4], w_o_parts, []
     )
     attn_all = lax.all_gather(attn_tok, "sp", axis=0, tiled=True)
 
     h2_pieces = gather(h2_low, n_ep)
-    cots = [near_rows] + [cot_rows(g, [x_one]) for g in range(group, n_ep, group)]
+    cots = [cot_rows(g, [x_one]) for g in range(0, n_ep, group)]
     groups, d_pieces, d_gates, d_sums = [], [], [], []
     home_gates = None
 
@@ -930,7 +921,7 @@
     mix_stacks = combine_stacks(
         places, [made[4] for _, _, made in groups], n_ep, local, cap, group, d_pieces
     )
-    grad_down = weight_grad(acts, outs, mix_stacks[:1])
+    grad_down = weight_grad(acts, outs, [mix_stacks[0], *d_sums[3:]])
     d_gates = by_piece(jnp.concatenate(d_gates, axis=0).reshape(n_ep, local, tok_dev))
     d_gates = lax.all_to_all(d_gates, "ep", split_axis=0, concat_axis=0, tiled=True)
     d_gates = d_gates.reshape(expert_count, tok_dev)
@@ -980,7 +971,7 @@
     )
     output = (x_one + last_hop(mix, mix_far)).astype(BF16)
     vo_stacks = vo_grads(ids, n_ep, h_all, d_v, attn_all, d_z_cols)
-    grad_vo = scatter_stacks_z(vo_stacks, n_ep).astype(BF16)
+    grad_vo = last_hop(*scatter_stacks(vo_stacks, n_ep)).astype(BF16)
 
     def placed(value):
         return lax.dynamic_update_slice_in_dim(
@@ -991,13 +982,12 @@
         [placed(grad_qg), placed(grad_kg), grad_ffn[None], grad_router], axis=0
     )
     *qk_stacks, d_qk = qk_back(
-        ids, n_ep, h_all, d_qn, d_kn, q_raw, k_raw, scales, sum_sp(sums), tiny, vo_stacks[:1]
+        ids, n_ep, h_all, d_qn, d_kn, q_raw, k_raw, scales, sum_sp_swaps(sums), tiny, vo_stacks[:1]
     )
     grad_qk, qk_far = scatter_stacks(qk_stacks, n_ep)
     grad_qk = last_hop(grad_qk, qk_far).astype(BF16)
 
-    d_h = d_h_rows(ids, n_ep, n_sp, d_qk, d_v, w_qkv)
-    output, d_h = tie(output, d_h)
+    d_h = d_h_rows(ids, n_ep, n_sp, d_qk, d_v, w_qkv, [output, grad_down, grad_gate])
     halves = plus(d_h[:2], swap_sp(d_h[2:], 1))
     d_h = halves[0].astype(F32) + swap_sp(halves[1], 2).astype(F32)
     x_rows = tokens[0].astype(F32)

time: 895 us -> 938 us (1.048)
  waiting for transfers between devices: 353 us -> 378 us
  starting transfers between devices: 81.3 us -> 93.2 us
    ppermute x17 -> x14, waiting for transfers between devices: 50.9 us -> 21.6 us  [swap_sp(): return lax.ppermute(value, 'sp', [(i, i ^ bits) for i in range(4)])]
    all_to_all x1, waiting for transfers between devices: 10.6 us -> 34.5 us  [body(): lax.all_to_all(mixed, 'sp', split_axis=0, concat_axis=1, tiled=True)]
    all_to_all x1, waiting for transfers between devices: 4.41 us -> 22.1 us  [body(): lax.all_to_all(d_gates, 'ep', split_axis=0, concat_axis=0, tiled=True)]
    ppermute x35 -> x36, starting transfers between devices: 41.3 us -> 49.7 us  [swap(): return lax.ppermute(value, 'ep', [(i, i ^ bits) for i in range(8)])]
    ppermute x35 -> x36, waiting for transfers between devices: 263 us -> 267 us  [swap(): return lax.ppermute(value, 'ep', [(i, i ^ bits) for i in range(8)])]
    convert_element_type x8 -> x9, other arithmetic: 16.5 us -> 19 us  [plus(): return (left.astype(F32) + right.astype(F32)).astype(left.dtype)]
  transfers between devices with their start and end apart: 70 -> 69, of which waited for: 23 -> 23; matrix products, arithmetic and copies ran while one was open for 11% -> 11% of each run, Pallas kernels for 35% -> 32%
where the time goes in v9:
time: 938 us; the launch traced here: 929 us
  waiting for transfers between devices  378 us (40%)
  Pallas kernels  318 us (34%)
  starting transfers between devices  93.2 us (10%)
  other arithmetic  72 us (8%)
  local copies, waits for them, and re-layouts  33.7 us (4%)
  between operations  31 us (3%)
    pallas_call x27, Pallas kernels, call(): pl.pallas_call(kernel, grid_spec=pltpu.PrefetchScalarGridSpec(num_scalar_...  318 us
    ppermute x36, waiting for transfers between devices, swap(): return lax.ppermute(value, 'ep', [(i, i ^ bits) for i in range(8)])  267 us
    ppermute x36, starting transfers between devices, swap(): return lax.ppermute(value, 'ep', [(i, i ^ bits) for i in range(8)])  49.7 us
    all_to_all x1, waiting for transfers between devices, body(): lax.all_to_all(mixed, 'sp', split_axis=0, concat_axis=1, tiled=True)  34.5 us
    ppermute x2, waiting for transfers between devices, gather_line(): farther = inner + lax.ppermute(outer, 'ep', OUTWARD)  26.7 us
    all_to_all x1, waiting for transfers between devices, body(): lax.all_to_all(d_gates, 'ep', split_axis=0, concat_axis=0, tiled=True)  22.1 us
    ppermute x14, waiting for transfers between devices, swap_sp(): return lax.ppermute(value, 'sp', [(i, i ^ bits) for i in range(4)])  21.6 us
    convert_element_type x9, other arithmetic, plus(): return (left.astype(F32) + right.astype(F32)).astype(left.dtype)  19 us
  transfers between devices with their start and end apart: 69, of which 23 were waited for; matrix products, arithmetic and copies ran while one was open for 11% of the time, Pallas kernels for 32%

profile of v9, /device:TPU:0, one launch (start us, length us, event | category | flops | bytes accessed | tf_op | source)
XLA Modules:
  0.0 928.5 jit_solution(8699187081411730394)
XLA Ops:
  15.7 20.9 %collective-permute-done.refs_2_ = bf16[256,2048]{1,0:T(8,128)(2,1)S(1)} collective-permute-done((bf16[256,2048]{1,0:T(8,128)(2,1)S(1)}, bf16[256,2048]{1,0:T(8,128)(2,1)S(1)}, u32[]{:S(2)}, u32[]{:S(2)}) %collective-permute-start) | collective-permute-done | bytes 1048608 | tf_op jit(solution)/shard_map/ppermute | solution.py:88
  40.3 21.0 %collective-permute-done.1.refs_3_ = bf16[256,2048]{1,0:T(8,128)(2,1)S(1)} collective-permute-done((bf16[256,2048]{1,0:T(8,128)(2,1)S(1)}, bf16[256,2048]{1,0:T(8,128)(2,1)S(1)}, u32[]{:S(2)}, u32[]{:S(2)}) %collective-permute-start.1) | collective-permute-done | bytes 1048608 | tf_op jit(solution)/shard_map/ppermute | solution.py:88
  65.1 7.5 all-to-all-start
  77.4 14.6 %collective-permute-done.7 = bf16[256,2048]{1,0:T(8,128)(2,1)} collective-permute-done((bf16[256,2048]{1,0:T(8,128)(2,1)S(1)}, bf16[256,2048]{1,0:T(8,128)(2,1)}, u32[]{:S(2)}, u32[]{:S(2)}) %collective-permute-start.7) | collective-permute-done | bytes 1048608 | tf_op jit(solution)/shard_map/ppermute | solution.py:111
  98.4 24.2 %collective-permute-done.8.refs_7_ = bf16[256,2048]{1,0:T(8,128)(2,1)} collective-permute-done((bf16[256,2048]{1,0:T(8,128)(2,1)S(1)}, bf16[256,2048]{1,0:T(8,128)(2,1)}, u32[]{:S(2)}, u32[]{:S(2)}) %collective-permute-start.8) | collective-permute-done | bytes 1048608 | tf_op jit(solution)/shard_map/ppermute | solution.py:88
  122.6 17.1 %qkv_project.1 = (f32[1024,512]{1,0:T(8,128)}, f32[1024,512]{1,0:T(8,128)}, bf16[1024,512]{1,0:T(8,128)(2,1)}, f32[16,1024]{1,0:T(8,128)}, bf16[2048,1536]{1,0:T...) custom-call(s32[12]{0:T(128)} %pad_add_fusion.ids.refs_0_, bf16[1024,2048]{1,0:T(8,128)(2,1)} %bitcast.177, ...), custom_call_target="tpu_custom_call" | custom-call | flops 128849018880 | bytes 30482432 | tf_op jit(solution)/shard_map/qkv_project/pallas_call | solution.py:62
  146.6 4.1 all-to-all-done.1
  151.7 17.2 %attend.1 = (bf16[1024,512]{1,0:T(8,128)(2,1)}, bf16[1024,512]{1,0:T(8,128)(2,1)}, bf16[1024,512]{1,0:T(8,128)(2,1)}) custom-call(f32[1024,512]{1,0:T(8,128)} %get-tuple-element.118.qr_ref.refs_4_, f32[1024,512]{1,0:T(8,128)} %get-tuple-element.119.kr_ref.refs_5_, bf16[1024,512]{1,0:T(8,128)(2,1)} %get-tuple-element.120.v_ref, ...), custom_call_target="tpu_custom_call" | custom-call | flops 32212254720 | bytes 9510912 | tf_op jit(solution)/shard_map/attend/pallas_call | solution.py:62
  175.4 34.5 %all-to-all-done.2 = bf16[4,256,512]{2,1,0:T(8,128)(2,1)S(1)} async-done(((bf16[4,256,512]{2,1,0:T(8,128)(2,1)}), bf16[4,256,512]{2,1,0:T(8,128)(2,1)S(1)}, u32[]{:S(2)}, u32[]{:S(2)}) %all-to-all-start.2) | async-done | bytes 1048608 | tf_op jit(solution)/shard_map/all_to_all | solution.py:872
  233.8 20.7 %collective-permute-done.16.refs_1_ = bf16[256,2048]{1,0:T(8,128)(2,1)} collective-permute-done((bf16[256,2048]{1,0:T(8,128)(2,1)S(1)}, bf16[256,2048]{1,0:T(8,128)(2,1)}, u32[]{:S(2)}, u32[]{:S(2)}) %collective-permute-start.16) | collective-permute-done | bytes 1048608 | tf_op jit(solution)/shard_map/ppermute | solution.py:88
  255.7 20.9 %collective-permute-done.20.refs_1_ = bf16[256,2048]{1,0:T(8,128)(2,1)} collective-permute-done((bf16[256,2048]{1,0:T(8,128)(2,1)}, bf16[256,2048]{1,0:T(8,128)(2,1)}, u32[]{:S(2)}, u32[]{:S(2)}) %collective-permute-start.20) | collective-permute-done | bytes 1048608 | tf_op jit(solution)/shard_map/ppermute | solution.py:88
  278.6 8.8 out_project.1
  300.3 25.7 %collective-permute-done.21.refs_2_ = bf16[256,2048]{1,0:T(8,128)(2,1)} collective-permute-done((bf16[256,2048]{1,0:T(8,128)(2,1)}, bf16[256,2048]{1,0:T(8,128)(2,1)}, u32[]{:S(2)}, u32[]{:S(2)}) %collective-permute-start.21) | collective-permute-done | bytes 1048608 | tf_op jit(solution)/shard_map/ppermute | solution.py:88
  336.9 11.6 %collective-permute-done.14.refs_1_ = bf16[256,2048]{1,0:T(8,128)(2,1)} collective-permute-done((bf16[256,2048]{1,0:T(8,128)(2,1)S(1)}, bf16[256,2048]{1,0:T(8,128)(2,1)}, u32[]{:S(2)}, u32[]{:S(2)}) %collective-permute-start.14) | collective-permute-done | bytes 1048608 | tf_op jit(solution)/shard_map/ppermute | solution.py:88
  348.5 21.6 %collective-permute-done.13.refs_1_ = bf16[256,2048]{1,0:T(8,128)(2,1)} collective-permute-done((bf16[256,2048]{1,0:T(8,128)(2,1)}, bf16[256,2048]{1,0:T(8,128)(2,1)}, u32[]{:S(2)}, u32[]{:S(2)}) %collective-permute-start.13) | collective-permute-done | bytes 1048608 | tf_op jit(solution)/shard_map/ppermute | solution.py:88
  375.2 4.5 dispatch.8
  379.6 4.5 dispatch.9
  384.1 12.1 %collective-permute-done.25 = bf16[256,2048]{1,0:T(8,128)(2,1)S(1)} collective-permute-done((bf16[256,2048]{1,0:T(8,128)(2,1)S(1)}, bf16[256,2048]{1,0:T(8,128)(2,1)S(1)}, u32[]{:S(2)}, u32[]{:S(2)}) %collective-permute-start.25) | collective-permute-done | bytes 1048608 | tf_op jit(solution)/shard_map/ppermute | solution.py:111
  398.8 42.5 %experts.2 = (bf16[2,576,1024]{2,1,0:T(8,128)(2,1)}, bf16[2,576,1024]{2,1,0:T(8,128)(2,1)}, bf16[2,576,1024]{2,1,0:T(8,128)(2,1)}, f32[2,576,1]{2,1,0:T(8,128)},...) custom-call(bf16[2,576,2048]{2,1,0:T(8,128)(2,1)} %get-tuple-element.131.refs_0_, ...), custom_call_target="tpu_custom_call" | custom-call | flops 579820584960 | bytes 51127296 | tf_op jit(solution)/shard_map/experts/pallas_call | solution.py:62
  441.3 4.5 dispatch.14
  445.8 4.5 dispatch.15
  454.2 4.0 combine.4
  460.2 42.6 %experts.3 = (bf16[2,576,1024]{2,1,0:T(8,128)(2,1)}, bf16[2,576,1024]{2,1,0:T(8,128)(2,1)}, bf16[2,576,1024]{2,1,0:T(8,128)(2,1)}, f32[2,576,1]{2,1,0:T(8,128)},...) custom-call(bf16[2,576,2048]{2,1,0:T(8,128)(2,1)} %get-tuple-element.139.refs_3_.refs_0_.refs_1_, ...), custom_call_target="tpu_custom_call" | custom-call | flops 579820584960 | bytes 51127296 | tf_op jit(solution)/shard_map/experts/pallas_call | solution.py:62
  512.0 4.0 combine.6
  523.5 4.8 all-to-all-start.3
  528.8 10.7 %combine_stacks.1 = (bf16[2,256,2048]{2,1,0:T(8,128)(2,1)}, bf16[2,256,2048]{2,1,0:T(8,128)(2,1)}, bf16[2,256,2048]{2,1,0:T(8,128)(2,1)}, bf16[2,256,2048]{2,1,0:T(8,128)(2,1)}) custom-call(s32[16,256]{1,0:T(8,128)} %copy-done.45, bf16[2,576,2048]{2,1,0:T(8,128)(2,1)} %get-tuple-element.135.refs_1_, bf16[2,576,2048]{2,1,0:T(8,128)(2,1)} %get-tuple-element.146.refs_2_, ...), custom_call_target="tpu_custom_call" | custom-call | flops 48318382080 | bytes 17842176 | tf_op jit(solution)/shard_map/combine_stacks/pallas_call | solution.py:62
  539.5 22.1 %all-to-all-done.3 = f32[8,2,256]{2,1,0:T(2,128)S(1)} async-done(((f32[8,2,256]{2,1,0:T(2,128)}), f32[8,2,256]{2,1,0:T(2,128)S(1)}, u32[]{:S(2)}, u32[]{:S(2)}) %all-to-all-start.3) | async-done | bytes 16416 | tf_op jit(solution)/shard_map/all_to_all | solution.py:926
  565.8 18.1 %weight_grad.3.refs_4_ = bf16[2,1024,2048]{2,1,0:T(8,128)(2,1)} custom-call(bf16[2,576,1024]{2,1,0:T(8,128)(2,1)} %get-tuple-element.156.refs_0_, bf16[2,576,1024]{2,1,0:T(8,128)(2,1)} %get-tuple-element.157.refs_1_, bf16[2,576,2048]{2,1,0:T(8,128)(2,1)} %dispatch.11.refs_1_.refs_6_.refs_10_.refs_2_, ...), custom_call_target="tpu_custom_call" | custom-call | flops 193273528320 | bytes 22544384 | tf_op jit(solution)/shard_map/weight_grad/pallas_call | solution.py:62
  594.2 19.0 %weight_grad.4.refs_4_ = bf16[2,2048,1024]{2,1,0:T(8,128)(2,1)} custom-call(bf16[2,576,2048]{2,1,0:T(8,128)(2,1)} %get-tuple-element.131.refs_0_, bf16[2,576,2048]{2,1,0:T(8,128)(2,1)} %get-tuple-element.139.refs_3_.refs_0_.refs_1_, bf16[2,576,1024]{2,1,0:T(8,128)(2,1)} %get-tuple-element.171.refs_2_, bf16[2,576,1024]{2,1,0:T(8,128)(2,1)} %get-tuple-element.172.refs_3_, ...), custom_call_target="tpu_custom_call" | custom-call | flops 193273528320 | bytes 22544384 | tf_op jit(solution)/shard_map/weight_grad/pallas_call | solution.py:62
  613.2 18.4 %weight_grad.5 = bf16[2,2048,1024]{2,1,0:T(8,128)(2,1)} custom-call(bf16[2,576,2048]{2,1,0:T(8,128)(2,1)} %get-tuple-element.131.refs_0_, bf16[2,576,2048]{2,1,0:T(8,128)(2,1)} %get-tuple-element.139.refs_3_.refs_0_.refs_1_, bf16[2,576,1024]{2,1,0:T(8,128)(2,1)} %get-tuple-element.169.refs_2_, bf16[2,576,1024]{2,1,0:T(8,128)(2,1)} %get-tuple-element.170.refs_3_, ...), custom_call_target="tpu_custom_call" | custom-call | flops 193273528320 | bytes 22544384 | tf_op jit(solution)/shard_map/weight_grad/pallas_call | solution.py:62
  646.8 7.8 out_back.1
  661.7 13.4 %collective-permute-done.32 = bf16[2,256,2048]{2,1,0:T(8,128)(2,1)} collective-permute-done((bf16[2,256,2048]{2,1,0:T(8,128)(2,1)}, bf16[2,256,2048]{2,1,0:T(8,128)(2,1)}, u32[]{:S(2)}, u32[]{:S(2)}) %collective-permute-start.32) | collective-permute-done | bytes 2097184 | tf_op jit(solution)/shard_map/ppermute | solution.py:88
  675.1 4.4 collective-permute-done.34
  689.0 23.2 %attend_back.1 = (f32[1024,512]{1,0:T(8,128)}, f32[1024,512]{1,0:T(8,128)}, bf16[1024,512]{1,0:T(8,128)(2,1)}, f32[16,1024]{1,0:T(8,128)}, f32[1,512]{1,0:T(1,128)}, /*index=5*/f32[1,512]{1,0:T(1,128)}) custom-call(bf16[1024,512]{1,0:T(8,128)(2,1)} %get-tuple-element.178.q_ref, bf16[1024,512]{1,0:T(8,128)(2,1)} %get-tuple-element.179.k_ref, ...), custom_call_target="tpu_custom_call" | custom-call | flops 75161927680 | bytes 14823424 | tf_op jit(solution)/shard_map/attend_back/pallas_call | solution.py:62
  716.0 10.7 %vo_grads.1 = (bf16[2,256,1024]{2,1,0:T(8,128)(2,1)}, bf16[2,256,1024]{2,1,0:T(8,128)(2,1)}, bf16[2,256,1024]{2,1,0:T(8,128)(2,1)}, bf16[2,256,1024]{2,1,0:T(8,128)(2,1)}) custom-call(s32[12]{0:T(128)} %pad_add_fusion.ids.refs_0_, bf16[1024,2048]{1,0:T(8,128)(2,1)} %get-tuple-element.177.h_ref.refs_1_, bf16[1024,512]{1,0:T(8,128)(2,1)} %get-tuple-element.186.dv_ref.refs_2_, ...), custom_call_target="tpu_custom_call" | custom-call | flops 85899345920 | bytes 14680064 | tf_op jit(solution)/shard_map/vo_grads/pallas_call | solution.py:62
  733.4 12.8 %qk_back.1 = (bf16[2,272,1024]{2,1,0:T(8,128)(2,1)}, bf16[2,272,1024]{2,1,0:T(8,128)(2,1)}, bf16[2,272,1024]{2,1,0:T(8,128)(2,1)}, bf16[2,272,1024]{2,1,0:T(8,128)(2,1)}, bf16[1024,1024]{1,0:T(8,128)(2,1)}) custom-call(s32[12]{0:T(128)} %pad_add_fusion.ids.refs_0_, bf16[1024,2048]{1,0:T(8,128)(2,1)} %get-tuple-element.177.h_ref.refs_1_, ...), custom_call_target="tpu_custom_call" | custom-call | flops 85899345920 | bytes 19423232 | tf_op jit(solution)/shard_map/qk_back/pallas_call | solution.py:62
  747.2 5.9 collective-permute-done.52
  757.6 20.7 %collective-permute-done.38 = bf16[256,2048]{1,0:T(8,128)(2,1)} collective-permute-done((bf16[256,2048]{1,0:T(8,128)(2,1)}, bf16[256,2048]{1,0:T(8,128)(2,1)}, u32[]{:S(2)}, u32[]{:S(2)}) %collective-permute-start.38) | collective-permute-done | bytes 1048608 | tf_op jit(solution)/shard_map/ppermute | solution.py:88
  781.6 4.2 convert_element_type.239.refs_5_.refs_13_
  785.8 4.1 convert_element_type.240.refs_6_.refs_14_
  789.9 12.4 %d_h.1 = bf16[4,256,2048]{2,1,0:T(8,128)(2,1)} custom-call(s32[12]{0:T(128)} %pad_add_fusion.ids.refs_0_, bf16[1024,1024]{1,0:T(8,128)(2,1)} %get-tuple-element.188.refs_1_, bf16[1024,512]{1,0:T(8,128)(2,1)} %get-tuple-element.186.dv_ref.refs_2_, bf16[2048,1536]{1,0:T(8,128)(2,1)} %get-tuple-element.189.refs_3_, ...), custom_call_target="tpu_custom_call" | custom-call | flops 128849018880 | bytes 13631488 | tf_op jit(solution)/shard_map/d_h/pallas_call | solution.py:62
  811.6 19.7 %collective-permute-done.44 = bf16[2,272,1024]{2,1,0:T(8,128)(2,1)S(1)} collective-permute-done((bf16[2,272,1024]{2,1,0:T(8,128)(2,1)S(1)}, bf16[2,272,1024]{2,1,0:T(8,128)(2,1)S(1)}, u32[]{:S(2)}, u32[]{:S(2)}) %collective-permute-start.44) | collective-permute-done | bytes 1114144 | tf_op jit(solution)/shard_map/ppermute | solution.py:88
  831.2 12.4 %collective-permute-done.46 = bf16[2,272,1024]{2,1,0:T(8,128)(2,1)S(1)} collective-permute-done((bf16[2,272,1024]{2,1,0:T(8,128)(2,1)S(1)}, bf16[2,272,1024]{2,1,0:T(8,128)(2,1)S(1)}, u32[]{:S(2)}, u32[]{:S(2)}) %collective-permute-start.46) | collective-permute-done | bytes 1114144 | tf_op jit(solution)/shard_map/ppermute | solution.py:88
  849.8 21.3 %collective-permute-done.47 = bf16[272,1024]{1,0:T(8,128)(2,1)S(1)} collective-permute-done((bf16[272,1024]{1,0:T(8,128)(2,1)S(1)}, bf16[272,1024]{1,0:T(8,128)(2,1)S(1)}, u32[]{:S(2)}, u32[]{:S(2)}) %collective-permute-start.47) | collective-permute-done | bytes 557088 | tf_op jit(solution)/shard_map/ppermute | solution.py:88
  876.8 21.6 %collective-permute-done.56.refs_11_ = bf16[256,1024]{1,0:T(8,128)(2,1)} collective-permute-done((bf16[256,1024]{1,0:T(8,128)(2,1)}, bf16[256,1024]{1,0:T(8,128)(2,1)}, u32[]{:S(2)}, u32[]{:S(2)}) %collective-permute-start.56) | collective-permute-done | bytes 524320 | tf_op jit(solution)/shard_map/ppermute | solution.py:92
  898.9 4.2 convert_element_type.265.refs_15_
  905.3 4.0 fusion.5.refs_16_
  909.3 7.9 finish.1
  (369 shorter events, 200.4 us)
Async XLA Ops:
  7.2 115.4 %all-gather.6.cloned.1.call-start = ((), (), s32[]{:S(2)}) async-start(), calls=%async_computation.13 | async-start | bytes 5242880 | tf_op jit(solution)/shard_map/all_gather | solution.py:819
  39.0 35.0 %collective-permute-start.5 = (bf16[256,2048]{1,0:T(8,128)(2,1)S(1)}, bf16[256,2048]{1,0:T(8,128)(2,1)S(1)}, u32[]{:S(2)}, u32[]{:S(2)}) collective-permute-start(bf16[256,2048]{1,0:T(8,128)(2,1)S(1)} %collective-permute-done.4), channel_id=1, source_target_pairs={{2,0},{3,1},{4,6},{5,7},{10,8},{11,9},{12,14},{13,15},{18,16},{19,... | collective-permute-start | bytes 3145736 | tf_op jit(solution)/shard_map/ppermute | solution.py:110
  62.3 29.7 %collective-permute-start.7 = (bf16[256,2048]{1,0:T(8,128)(2,1)S(1)}, bf16[256,2048]{1,0:T(8,128)(2,1)}, u32[]{:S(2)}, u32[]{:S(2)}) collective-permute-start(bf16[256,2048]{1,0:T(8,128)(2,1)S(1)} %collective-permute-done.3), channel_id=1, source_target_pairs={{2,0},{3,1},{4,6},{5,7},{10,8},{11,9},{12,14},{13,15},{18,16},{19,... | collective-permute-start | bytes 3145736 | tf_op jit(solution)/shard_map/ppermute | solution.py:111
  65.1 32.6 %all-to-all-start = ((bf16[8,48,256]{2,1,0:T(8,128)(2,1)}), bf16[8,48,256]{2,1,0:T(8,128)(2,1)S(1)}, u32[]{:S(2)}, u32[]{:S(2)}) async-start(bf16[8,48,256]{2,1,0:T(8,128)(2,1)} %broadcast_in_dim.65), calls=%async_computation | async-start | bytes 393216 | tf_op jit(solution)/shard_map/all_to_all | solution.py:807
  75.4 47.2 %collective-permute-start.6 = (bf16[256,2048]{1,0:T(8,128)(2,1)}, bf16[256,2048]{1,0:T(8,128)(2,1)}, u32[]{:S(2)}, u32[]{:S(2)}) collective-permute-start(bf16[256,2048]{1,0:T(8,128)(2,1)} %add.172.refs_4_), channel_id=1, source_target_pairs={{0,1},{1,0},{2,3},{3,2},{4,5},{5,4},{6,7},{7,6},{8,9},{9,8},{10,11... | collective-permute-start | bytes 3145736 | tf_op jit(solution)/shard_map/ppermute | solution.py:88
  151.3 59.8 %collective-permute-start.9 = (bf16[2048,512]{1,0:T(8,128)(2,1)}, bf16[2048,512]{1,0:T(8,128)(2,1)}, u32[]{:S(2)}, u32[]{:S(2)}) collective-permute-start(bf16[2048,512]{1,0:T(8,128)(2,1)} %get-tuple-element.117.refs_0_), channel_id=1, source_target_pairs={{0,16},{8,24},{16,0},{24,8},{1,17},{9,25},{17,1},{25,9},{2,18},{10... | collective-permute-start | bytes 6291464 | tf_op jit(solution)/shard_map/ppermute | solution.py:92
  168.9 41.1 %all-to-all-start.2 = ((bf16[4,256,512]{2,1,0:T(8,128)(2,1)}), bf16[4,256,512]{2,1,0:T(8,128)(2,1)S(1)}, u32[]{:S(2)}, u32[]{:S(2)}) async-start(bf16[4,256,512]{2,1,0:T(8,128)(2,1)} %bitcast.146), calls=%async_computation.2 | async-start | bytes 2097152 | tf_op jit(solution)/shard_map/all_to_all | solution.py:872
  172.6 541.9 %all-gather.4.cloned.1.call-start = ((), (), s32[]{:S(2)}) async-start(), calls=%async_computation.9 | async-start | bytes 5242880 | tf_op jit(solution)/shard_map/all_gather | solution.py:878
  173.1 56.5 %collective-permute-start.19 = (bf16[256,2048]{1,0:T(8,128)(2,1)S(1)}, bf16[256,2048]{1,0:T(8,128)(2,1)}, u32[]{:S(2)}, u32[]{:S(2)}) collective-permute-start(bf16[256,2048]{1,0:T(8,128)(2,1)S(1)} %bitcast.137), channel_id=1, source_target_pairs={{0,4},{1,5},{2,6},{3,7},{4,0},{5,1},{6,2},{7,3},{8,12},{9,13},{10,... | collective-permute-start | bytes 3145736 | tf_op jit(solution)/shard_map/ppermute | solution.py:88
  175.3 102.5 %collective-permute-start.10 = (bf16[2048,512]{1,0:T(8,128)(2,1)}, bf16[2048,512]{1,0:T(8,128)(2,1)}, u32[]{:S(2)}, u32[]{:S(2)}) collective-permute-start(bf16[2048,512]{1,0:T(8,128)(2,1)} %get-tuple-element.117.refs_0_), channel_id=1, source_target_pairs={{0,8},{8,0},{16,24},{24,16},{1,9},{9,1},{17,25},{25,17},{2,10},{10... | collective-permute-start | bytes 6291464 | tf_op jit(solution)/shard_map/ppermute | solution.py:92
  211.1 67.5 %collective-permute-start.11 = (bf16[2048,512]{1,0:T(8,128)(2,1)}, bf16[2048,512]{1,0:T(8,128)(2,1)}, u32[]{:S(2)}, u32[]{:S(2)}) collective-permute-start(bf16[2048,512]{1,0:T(8,128)(2,1)} %collective-permute-done.9.refs_2_), channel_id=1, source_target_pairs={{0,8},{8,0},{16,24},{24,16},{1,9},{9,1},{17,25},{25,17},{2,10},{10... | collective-permute-start | bytes 6291464 | tf_op jit(solution)/shard_map/ppermute | solution.py:92
  229.6 46.9 %collective-permute-start.20 = (bf16[256,2048]{1,0:T(8,128)(2,1)}, bf16[256,2048]{1,0:T(8,128)(2,1)}, u32[]{:S(2)}, u32[]{:S(2)}) collective-permute-start(bf16[256,2048]{1,0:T(8,128)(2,1)} %collective-permute-done.19.refs_1_), channel_id=1, source_target_pairs={{0,2},{1,3},{2,0},{3,1},{4,6},{5,7},{6,4},{7,5},{8,10},{9,11},{10,... | collective-permute-start | bytes 3145736 | tf_op jit(solution)/shard_map/ppermute | solution.py:88
  232.6 63.2 %collective-permute-start.18 = (bf16[256,2048]{1,0:T(8,128)(2,1)S(1)}, bf16[256,2048]{1,0:T(8,128)(2,1)}, u32[]{:S(2)}, u32[]{:S(2)}) collective-permute-start(bf16[256,2048]{1,0:T(8,128)(2,1)S(1)} %bitcast.139), channel_id=1, source_target_pairs={{0,1},{1,0},{2,3},{3,2},{4,5},{5,4},{6,7},{7,6},{8,9},{9,8},{10,11... | collective-permute-start | bytes 3145736 | tf_op jit(solution)/shard_map/ppermute | solution.py:88
  254.5 36.5 %collective-permute-start.22 = (bf16[256,2048]{1,0:T(8,128)(2,1)}, bf16[256,2048]{1,0:T(8,128)(2,1)}, u32[]{:S(2)}, u32[]{:S(2)}) collective-permute-start(bf16[256,2048]{1,0:T(8,128)(2,1)} %collective-permute-done.19.refs_1_), channel_id=1, source_target_pairs={{0,1},{1,0},{2,3},{3,2},{4,5},{5,4},{6,7},{7,6},{8,9},{9,8},{10,11... | collective-permute-start | bytes 3145736 | tf_op jit(solution)/shard_map/ppermute | solution.py:88
  276.6 56.4 %collective-permute-start.17 = (bf16[256,2048]{1,0:T(8,128)(2,1)}, bf16[256,2048]{1,0:T(8,128)(2,1)}, u32[]{:S(2)}, u32[]{:S(2)}) collective-permute-start(bf16[256,2048]{1,0:T(8,128)(2,1)} %collective-permute-done.16.refs_1_), channel_id=1, source_target_pairs={{0,1},{1,0},{2,3},{3,2},{4,5},{5,4},{6,7},{7,6},{8,9},{9,8},{10,11... | collective-permute-start | bytes 3145736 | tf_op jit(solution)/shard_map/ppermute | solution.py:88
  277.8 48.2 %collective-permute-start.21 = (bf16[256,2048]{1,0:T(8,128)(2,1)}, bf16[256,2048]{1,0:T(8,128)(2,1)}, u32[]{:S(2)}, u32[]{:S(2)}) collective-permute-start(bf16[256,2048]{1,0:T(8,128)(2,1)} %collective-permute-done.20.refs_1_), channel_id=1, source_target_pairs={{0,1},{1,0},{2,3},{3,2},{4,5},{5,4},{6,7},{7,6},{8,9},{9,8},{10,11... | collective-permute-start | bytes 3145736 | tf_op jit(solution)/shard_map/ppermute | solution.py:88
  287.4 42.3 %collective-permute-start.12 = (bf16[256,2048]{1,0:T(8,128)(2,1)}, bf16[256,2048]{1,0:T(8,128)(2,1)}, u32[]{:S(2)}, u32[]{:S(2)}) collective-permute-start(bf16[256,2048]{1,0:T(8,128)(2,1)} %get-tuple-element.126.refs_0_), channel_id=1, source_target_pairs={{0,2},{1,3},{2,0},{3,1},{4,6},{5,7},{6,4},{7,5},{8,10},{9,11},{10,... | collective-permute-start | bytes 3145736 | tf_op jit(solution)/shard_map/ppermute | solution.py:88
  291.0 57.5 %collective-permute-start.14 = (bf16[256,2048]{1,0:T(8,128)(2,1)S(1)}, bf16[256,2048]{1,0:T(8,128)(2,1)}, u32[]{:S(2)}, u32[]{:S(2)}) collective-permute-start(bf16[256,2048]{1,0:T(8,128)(2,1)S(1)} %copy-done.24), channel_id=1, source_target_pairs={{0,1},{1,0},{2,3},{3,2},{4,5},{5,4},{6,7},{7,6},{8,9},{9,8},{10,11... | collective-permute-start | bytes 3145736 | tf_op jit(solution)/shard_map/ppermute | solution.py:88
  295.7 35.9 %collective-permute-start.23 = (bf16[256,2048]{1,0:T(8,128)(2,1)S(1)}, bf16[256,2048]{1,0:T(8,128)(2,1)S(1)}, u32[]{:S(2)}, u32[]{:S(2)}) collective-permute-start(bf16[256,2048]{1,0:T(8,128)(2,1)S(1)} %copy-done.24), channel_id=1, source_target_pairs={{2,4},{3,5},{4,2},{5,3},{10,12},{11,13},{12,10},{13,11},{18,20},{1... | collective-permute-start | bytes 3145736 | tf_op jit(solution)/shard_map/ppermute | solution.py:107
  329.7 40.3 %collective-permute-start.13 = (bf16[256,2048]{1,0:T(8,128)(2,1)}, bf16[256,2048]{1,0:T(8,128)(2,1)}, u32[]{:S(2)}, u32[]{:S(2)}) collective-permute-start(bf16[256,2048]{1,0:T(8,128)(2,1)} %collective-permute-done.12.refs_0_), channel_id=1, source_target_pairs={{0,1},{1,0},{2,3},{3,2},{4,5},{5,4},{6,7},{7,6},{8,9},{9,8},{10,11... | collective-permute-start | bytes 3145736 | tf_op jit(solution)/shard_map/ppermute | solution.py:88
  331.0 39.1 %collective-permute-start.15 = (bf16[256,2048]{1,0:T(8,128)(2,1)}, bf16[256,2048]{1,0:T(8,128)(2,1)S(1)}, u32[]{:S(2)}, u32[]{:S(2)}) collective-permute-start(bf16[256,2048]{1,0:T(8,128)(2,1)} %collective-permute-done.12.refs_0_), channel_id=1, source_target_pairs={{2,4},{3,5},{4,2},{5,3},{10,12},{11,13},{12,10},{13,11},{18,20},{1... | collective-permute-start | bytes 3145736 | tf_op jit(solution)/shard_map/ppermute | solution.py:108
  331.7 39.7 %collective-permute-start.24 = (bf16[256,2048]{1,0:T(8,128)(2,1)S(1)}, bf16[256,2048]{1,0:T(8,128)(2,1)}, u32[]{:S(2)}, u32[]{:S(2)}) collective-permute-start(bf16[256,2048]{1,0:T(8,128)(2,1)S(1)} %collective-permute-done.23), channel_id=1, source_target_pairs={{2,0},{3,1},{4,6},{5,7},{10,8},{11,9},{12,14},{13,15},{18,16},{19,... | collective-permute-start | bytes 3145736 | tf_op jit(solution)/shard_map/ppermute | solution.py:110
  374.0 67.4 %collective-permute-start.27 = (bf16[256,2048]{1,0:T(8,128)(2,1)}, bf16[256,2048]{1,0:T(8,128)(2,1)}, u32[]{:S(2)}, u32[]{:S(2)}) collective-permute-start(bf16[256,2048]{1,0:T(8,128)(2,1)} %add.185.refs_8_.refs_1_.refs_12_), channel_id=1, source_target_pairs={{0,1},{1,0},{2,3},{3,2},{4,5},{5,4},{6,7},{7,6},{8,9},{9,8},{10,11... | collective-permute-start | bytes 3145736 | tf_op jit(solution)/shard_map/ppermute | solution.py:88
  397.6 48.2 %collective-permute-start.26 = (bf16[256,2048]{1,0:T(8,128)(2,1)}, bf16[256,2048]{1,0:T(8,128)(2,1)}, u32[]{:S(2)}, u32[]{:S(2)}) collective-permute-start(bf16[256,2048]{1,0:T(8,128)(2,1)} %add.186.refs_9_.refs_1_.refs_13_), channel_id=1, source_target_pairs={{0,1},{1,0},{2,3},{3,2},{4,5},{5,4},{6,7},{7,6},{8,9},{9,8},{10,11... | collective-permute-start | bytes 3145736 | tf_op jit(solution)/shard_map/ppermute | solution.py:88
  458.2 44.6 %collective-permute-start.29 = (bf16[256,2048]{1,0:T(8,128)(2,1)}, bf16[256,2048]{1,0:T(8,128)(2,1)}, u32[]{:S(2)}, u32[]{:S(2)}) collective-permute-start(bf16[256,2048]{1,0:T(8,128)(2,1)} %get-tuple-element.145.refs_9_.refs_6_), channel_id=1, source_target_pairs={{0,1},{1,0},{2,3},{3,2},{4,5},{5,4},{6,7},{7,6},{8,9},{9,8},{10,11... | collective-permute-start | bytes 3145736 | tf_op jit(solution)/shard_map/ppermute | solution.py:88
  459.0 46.5 %collective-permute-start.28 = (bf16[256,2048]{1,0:T(8,128)(2,1)}, bf16[256,2048]{1,0:T(8,128)(2,1)}, u32[]{:S(2)}, u32[]{:S(2)}) collective-permute-start(bf16[256,2048]{1,0:T(8,128)(2,1)} %get-tuple-element.143.refs_7_.refs_4_), channel_id=1, source_target_pairs={{0,1},{1,0},{2,3},{3,2},{4,5},{5,4},{6,7},{7,6},{8,9},{9,8},{10,11... | collective-permute-start | bytes 3145736 | tf_op jit(solution)/shard_map/ppermute | solution.py:88
  516.0 48.4 %collective-permute-start.31 = (bf16[256,2048]{1,0:T(8,128)(2,1)}, bf16[256,2048]{1,0:T(8,128)(2,1)S(1)}, u32[]{:S(2)}, u32[]{:S(2)}) collective-permute-start(bf16[256,2048]{1,0:T(8,128)(2,1)} %get-tuple-element.152.refs_10_), channel_id=1, source_target_pairs={{0,1},{1,0},{2,3},{3,2},{4,5},{5,4},{6,7},{7,6},{8,9},{9,8},{10,11... | collective-permute-start | bytes 3145736 | tf_op jit(solution)/shard_map/ppermute | solution.py:88
  516.8 67.1 %collective-permute-start.30 = (bf16[256,2048]{1,0:T(8,128)(2,1)}, bf16[256,2048]{1,0:T(8,128)(2,1)}, u32[]{:S(2)}, u32[]{:S(2)}) collective-permute-start(bf16[256,2048]{1,0:T(8,128)(2,1)} %get-tuple-element.150.refs_8_), channel_id=1, source_target_pairs={{0,1},{1,0},{2,3},{3,2},{4,5},{5,4},{6,7},{7,6},{8,9},{9,8},{10,11... | collective-permute-start | bytes 3145736 | tf_op jit(solution)/shard_map/ppermute | solution.py:88
  523.5 38.1 %all-to-all-start.3 = ((f32[8,2,256]{2,1,0:T(2,128)}), f32[8,2,256]{2,1,0:T(2,128)S(1)}, u32[]{:S(2)}, u32[]{:S(2)}) async-start(f32[8,2,256]{2,1,0:T(2,128)} %constant_dynamic-update-slice_fusion.8), calls=%async_computation.3 | async-start | bytes 32768 | tf_op jit(solution)/shard_map/all_to_all | solution.py:926
  528.3 253.3 %reduce-scatter.4.cloned.1.call-start = ((), (), s32[]{:S(2)}) async-start(), calls=%async_computation.10 | async-start | bytes 10485760 | tf_op jit(solution)/shard_map/reduce_scatter | solution.py:940
  585.6 49.0 %collective-permute-start.33 = (bf16[2,256,2048]{2,1,0:T(8,128)(2,1)}, bf16[2,256,2048]{2,1,0:T(8,128)(2,1)}, u32[]{:S(2)}, u32[]{:S(2)}) collective-permute-start(bf16[2,256,2048]{2,1,0:T(8,128)(2,1)} %get-tuple-element.160), channel_id=1, source_target_pairs={{0,1},{1,0},{2,3},{3,2},{4,5},{5,4},{6,7},{7,6},{8,9},{9,8},{10,11... | collective-permute-start | bytes 6291464 | tf_op jit(solution)/shard_map/ppermute | solution.py:88
  586.4 88.6 %collective-permute-start.32 = (bf16[2,256,2048]{2,1,0:T(8,128)(2,1)}, bf16[2,256,2048]{2,1,0:T(8,128)(2,1)}, u32[]{:S(2)}, u32[]{:S(2)}) collective-permute-start(bf16[2,256,2048]{2,1,0:T(8,128)(2,1)} %get-tuple-element.158), channel_id=1, source_target_pairs={{0,1},{1,0},{2,3},{3,2},{4,5},{5,4},{6,7},{7,6},{8,9},{9,8},{10,11... | collective-permute-start | bytes 6291464 | tf_op jit(solution)/shard_map/ppermute | solution.py:88
  587.7 198.1 %reduce-scatter.6.cloned.1.call-start = ((), (), s32[]{:S(2)}) async-start(), calls=%async_computation.11 | async-start | bytes 10485760 | tf_op jit(solution)/shard_map/reduce_scatter | solution.py:940
  590.5 49.9 %collective-permute-start.36 = (bf16[256,2048]{1,0:T(8,128)(2,1)}, bf16[256,2048]{1,0:T(8,128)(2,1)}, u32[]{:S(2)}, u32[]{:S(2)}) collective-permute-start(bf16[256,2048]{1,0:T(8,128)(2,1)} %add_convert_fusion.8.refs_4_), channel_id=1, source_target_pairs={{0,2},{1,3},{2,0},{3,1},{4,6},{5,7},{6,4},{7,5},{8,10},{9,11},{10,... | collective-permute-start | bytes 3145736 | tf_op jit(solution)/shard_map/ppermute | solution.py:88
  592.5 47.9 %collective-permute-start.37 = (bf16[256,2048]{1,0:T(8,128)(2,1)}, bf16[256,2048]{1,0:T(8,128)(2,1)}, u32[]{:S(2)}, u32[]{:S(2)}) collective-permute-start(bf16[256,2048]{1,0:T(8,128)(2,1)} %add_convert_fusion.5.refs_6_), channel_id=1, source_target_pairs={{0,4},{1,5},{2,6},{3,7},{4,0},{5,1},{6,2},{7,3},{8,12},{9,13},{10,... | collective-permute-start | bytes 3145736 | tf_op jit(solution)/shard_map/ppermute | solution.py:88
  638.4 41.1 %collective-permute-start.34 = (bf16[2,256,2048]{2,1,0:T(8,128)(2,1)}, bf16[2,256,2048]{2,1,0:T(8,128)(2,1)}, u32[]{:S(2)}, u32[]{:S(2)}) collective-permute-start(bf16[2,256,2048]{2,1,0:T(8,128)(2,1)} %add_convert_fusion.1), channel_id=1, source_target_pairs={{0,2},{1,3},{2,0},{3,1},{4,6},{5,7},{6,4},{7,5},{8,10},{9,11},{10,... | collective-permute-start | bytes 6291464 | tf_op jit(solution)/shard_map/ppermute | solution.py:88
  660.5 238.4 %reduce-scatter.8.cloned.1.call-start = ((), (), s32[]{:S(2)}) async-start(), calls=%async_computation.12 | async-start | bytes 10485760 | tf_op jit(solution)/shard_map/reduce_scatter | solution.py:940
  685.5 29.5 %all-to-all-start.5 = ((bf16[256,4,512]{2,0,1:T(8,128)(2,1)}), bf16[256,4,512]{2,0,1:T(8,128)(2,1)S(1)}, u32[]{:S(2)}, u32[]{:S(2)}) async-start(bf16[256,4,512]{2,0,1:T(8,128)(2,1)} %bitcast.132), calls=%async_computation.5 | async-start | bytes 2097152 | tf_op jit(solution)/shard_map/all_to_all | solution.py:963
  727.8 78.1 %collective-permute-start.51 = (bf16[2,256,1024]{2,1,0:T(8,128)(2,1)}, bf16[2,256,1024]{2,1,0:T(8,128)(2,1)}, u32[]{:S(2)}, u32[]{:S(2)}) collective-permute-start(bf16[2,256,1024]{2,1,0:T(8,128)(2,1)} %get-tuple-element.194), channel_id=1, source_target_pairs={{0,1},{1,0},{2,3},{3,2},{4,5},{5,4},{6,7},{7,6},{8,9},{9,8},{10,11... | collective-permute-start | bytes 3145736 | tf_op jit(solution)/shard_map/ppermute | solution.py:88
  729.5 48.8 %collective-permute-start.38 = (bf16[256,2048]{1,0:T(8,128)(2,1)}, bf16[256,2048]{1,0:T(8,128)(2,1)}, u32[]{:S(2)}, u32[]{:S(2)}) collective-permute-start(bf16[256,2048]{1,0:T(8,128)(2,1)} %fusion.10), channel_id=1, source_target_pairs={{0,4},{1,5},{2,6},{3,7},{4,0},{5,1},{6,2},{7,3},{8,12},{9,13},{10,... | collective-permute-start | bytes 3145736 | tf_op jit(solution)/shard_map/ppermute | solution.py:88
  746.2 59.1 %collective-permute-start.45 = (bf16[2,272,1024]{2,1,0:T(8,128)(2,1)}, bf16[2,272,1024]{2,1,0:T(8,128)(2,1)S(1)}, u32[]{:S(2)}, u32[]{:S(2)}) collective-permute-start(bf16[2,272,1024]{2,1,0:T(8,128)(2,1)} %get-tuple-element.193), channel_id=1, source_target_pairs={{0,1},{1,0},{2,3},{3,2},{4,5},{5,4},{6,7},{7,6},{8,9},{9,8},{10,11... | collective-permute-start | bytes 3342344 | tf_op jit(solution)/shard_map/ppermute | solution.py:88
  756.0 49.9 %collective-permute-start.53 = (bf16[2,256,1024]{2,1,0:T(8,128)(2,1)}, bf16[2,256,1024]{2,1,0:T(8,128)(2,1)}, u32[]{:S(2)}, u32[]{:S(2)}) collective-permute-start(bf16[2,256,1024]{2,1,0:T(8,128)(2,1)} %add_convert_fusion.3), channel_id=1, source_target_pairs={{0,2},{1,3},{2,0},{3,1},{4,6},{5,7},{6,4},{7,5},{8,10},{9,11},{10,... | collective-permute-start | bytes 3145736 | tf_op jit(solution)/shard_map/ppermute | solution.py:88
  804.2 41.3 %collective-permute-start.42 = (bf16[2,256,2048]{2,1,0:T(8,128)(2,1)S(1)}, bf16[2,256,2048]{2,1,0:T(8,128)(2,1)S(1)}, u32[]{:S(2)}, u32[]{:S(2)}) collective-permute-start(bf16[2,256,2048]{2,1,0:T(8,128)(2,1)S(1)} %slice.283), channel_id=1, source_target_pairs={{0,8},{8,0},{16,24},{24,16},{1,9},{9,1},{17,25},{25,17},{2,10},{10... | collective-permute-start | bytes 6291464 | tf_op jit(solution)/shard_map/ppermute | solution.py:92
  805.7 37.9 %collective-permute-start.46 = (bf16[2,272,1024]{2,1,0:T(8,128)(2,1)S(1)}, bf16[2,272,1024]{2,1,0:T(8,128)(2,1)S(1)}, u32[]{:S(2)}, u32[]{:S(2)}) collective-permute-start(bf16[2,272,1024]{2,1,0:T(8,128)(2,1)S(1)} %add_convert_fusion.2), channel_id=1, source_target_pairs={{0,2},{1,3},{2,0},{3,1},{4,6},{5,7},{6,4},{7,5},{8,10},{9,11},{10,... | collective-permute-start | bytes 3342344 | tf_op jit(solution)/shard_map/ppermute | solution.py:88
  808.2 65.9 %collective-permute-start.54 = (bf16[256,1024]{1,0:T(8,128)(2,1)S(1)}, bf16[256,1024]{1,0:T(8,128)(2,1)S(1)}, u32[]{:S(2)}, u32[]{:S(2)}) collective-permute-start(bf16[256,1024]{1,0:T(8,128)(2,1)S(1)} %fusion.14), channel_id=1, source_target_pairs={{0,4},{1,5},{2,6},{3,7},{4,0},{5,1},{6,2},{7,3},{8,12},{9,13},{10,... | collective-permute-start | bytes 1572872 | tf_op jit(solution)/shard_map/ppermute | solution.py:88
  847.9 55.2 %collective-permute-start.43 = (bf16[256,2048]{1,0:T(8,128)(2,1)}, bf16[256,2048]{1,0:T(8,128)(2,1)}, u32[]{:S(2)}, u32[]{:S(2)}) collective-permute-start(bf16[256,2048]{1,0:T(8,128)(2,1)} %slice_bitcast_fusion.3), channel_id=1, source_target_pairs={{0,16},{8,24},{16,0},{24,8},{1,17},{9,25},{17,1},{25,9},{2,18},{10... | collective-permute-start | bytes 3145736 | tf_op jit(solution)/shard_map/ppermute | solution.py:92
  876.2 33.1 %collective-permute-start.55 = (bf16[256,1024]{1,0:T(8,128)(2,1)}, bf16[256,1024]{1,0:T(8,128)(2,1)}, u32[]{:S(2)}, u32[]{:S(2)}) collective-permute-start(bf16[256,1024]{1,0:T(8,128)(2,1)} %fusion.12.refs_9_), channel_id=1, source_target_pairs={{0,8},{8,0},{16,24},{24,16},{1,9},{9,1},{17,25},{25,17},{2,10},{10... | collective-permute-start | bytes 1572872 | tf_op jit(solution)/shard_map/ppermute | solution.py:92
  876.3 33.0 %collective-permute-start.48 = (bf16[272,1024]{1,0:T(8,128)(2,1)}, bf16[272,1024]{1,0:T(8,128)(2,1)}, u32[]{:S(2)}, u32[]{:S(2)}) collective-permute-start(bf16[272,1024]{1,0:T(8,128)(2,1)} %fusion.9.refs_5_), channel_id=1, source_target_pairs={{0,8},{8,0},{16,24},{24,16},{1,9},{9,1},{17,25},{25,17},{2,10},{10... | collective-permute-start | bytes 1671176 | tf_op jit(solution)/shard_map/ppermute | solution.py:92
  (88 other events, 1819.0 us)
Sparse Core Ops, SparseCore 0:
  9.6 37.1 all-gather.5
  233.9 33.8 all-gather.3
  587.8 71.6 reduce-scatter.3
  662.1 85.7 reduce-scatter.5
  750.3 71.7 reduce-scatter.7

commit v10 on v9

--- a/solution.py
+++ b/solution.py
@@ -162,14 +162,20 @@
     return [like((2, *shape), BF16)] * 4 if n_ep == 8 else [like((n_ep, *shape), BF16)]
 
 
+def odd_sums(stacks):
+    return plus(stacks[1], swap(stacks[3], 1))
+
+
+def even_sums(stacks, odd):
+    even = stacks[0].astype(F32) + swap(stacks[2], 1).astype(F32) + swap(odd, 2).astype(F32)
+    return even[0], even[1].astype(BF16)
+
+
 def scatter_stacks(stacks, n_ep):
     if n_ep != 8:
         total = lax.psum_scatter(stacks[0], "ep", scatter_dimension=0, tiled=False)
         return total.astype(F32), None
-    even, odd, even_sent, odd_sent = stacks
-    odd = plus(odd, swap(odd_sent, 1))
-    even = even.astype(F32) + swap(even_sent, 1).astype(F32) + swap(odd, 2).astype(F32)
-    return even[0], even[1].astype(BF16)
+    return even_sums(stacks, odd_sums(stacks))
 
 
 def last_hop(total, far):
@@ -453,7 +459,7 @@
     return pl.BlockSpec((rows, HEAD_DIM), lambda h: (0, h))
 
 
-def attend(q_raw, k_raw, v_low, scales, q_gain, k_gain, cosine, sine, starts):
+def attend(q_raw, k_raw, v_low, scales, q_gain, k_gain, cosine, sine, starts, after):
     total, width = v_low.shape
     heads = width // HEAD_DIM
     head, gain = head_spec(total), head_spec(1)
@@ -463,6 +469,7 @@
         [q_raw, k_raw, v_low, scales, q_gain, k_gain, cosine, sine, starts],
         3 * heads * total * total * HEAD_DIM,
         "attend",
+        after=after,
         grid=(heads,),
         in_specs=[head, head, head, None, gain, gain, None, None, None],
         out_specs=[head, head, head],
@@ -854,7 +861,8 @@
     w_o_over = swap_sp(w_o, 2)
     gain_q, gain_k = own_columns(gains)[1:2], own_columns(gains)[2:3]
     q_rot, k_rot, mixed = attend(
-        q_raw, k_raw, v_low, scales, gain_q, gain_k, cosine, sine, starts
+        q_raw, k_raw, v_low, scales, gain_q, gain_k, cosine, sine, starts,
+        [cot_pieces[k] for k in ((1, 2, 4) if n_ep == 8 else ())],
     )
 
     def pair_places(p):
@@ -869,6 +877,8 @@
             )
         return d_rows
 
+    if n_ep == 8:
+        cot_pieces[3], cot_pieces[6], mixed = tie(cot_pieces[3], cot_pieces[6], mixed)
     attn_tok = lax.all_to_all(mixed, "sp", split_axis=0, concat_axis=1, tiled=True)
     w_o_over, attn_tok = tie(w_o_over, attn_tok)
     w_o_parts = [w_o, swap_sp(w_o, 1), w_o_over, swap_sp(w_o_over, 1)]
@@ -922,9 +932,6 @@
         places, [made[4] for _, _, made in groups], n_ep, local, cap, group, d_pieces
     )
     grad_down = weight_grad(acts, outs, [mix_stacks[0], *d_sums[3:]])
-    d_gates = by_piece(jnp.concatenate(d_gates, axis=0).reshape(n_ep, local, tok_dev))
-    d_gates = lax.all_to_all(d_gates, "ep", split_axis=0, concat_axis=0, tiled=True)
-    d_gates = d_gates.reshape(expert_count, tok_dev)
     if n_ep == 8:
         d_sums[2], mix_stacks[2], mix_stacks[3], grad_down = tie(
             d_sums[2], mix_stacks[2], mix_stacks[3], grad_down
@@ -933,8 +940,13 @@
         d_last = [d_far]
     else:
         d_h2, d_last = scatter(d_pieces, n_ep), []
-    grad_gate = weight_grad(ins, d_gate_rows, [grad_down, d_gates, *d_last])
-    grad_up = weight_grad(ins, d_up_rows, [grad_gate])
+    d_gates = by_piece(jnp.concatenate(d_gates, axis=0).reshape(n_ep, local, tok_dev))
+    if d_last:
+        d_gates, d_last[0] = tie(d_gates, d_last[0])
+    d_gates = lax.all_to_all(d_gates, "ep", split_axis=0, concat_axis=0, tiled=True)
+    d_gates = d_gates.reshape(expert_count, tok_dev)
+    grad_gate = weight_grad(ins, d_gate_rows, [grad_down, *d_last])
+    grad_up = weight_grad(ins, d_up_rows, [grad_gate, d_gates])
 
     def over_sp(value):
         return lax.psum_scatter(value, "sp", scatter_dimension=1, tiled=True).astype(F32)
@@ -971,6 +983,7 @@
     )
     output = (x_one + last_hop(mix, mix_far)).astype(BF16)
     vo_stacks = vo_grads(ids, n_ep, h_all, d_v, attn_all, d_z_cols)
+
     grad_vo = last_hop(*scatter_stacks(vo_stacks, n_ep)).astype(BF16)
 
     def placed(value):
@@ -984,10 +997,10 @@
     *qk_stacks, d_qk = qk_back(
         ids, n_ep, h_all, d_qn, d_kn, q_raw, k_raw, scales, sum_sp_swaps(sums), tiny, vo_stacks[:1]
     )
-    grad_qk, qk_far = scatter_stacks(qk_stacks, n_ep)
-    grad_qk = last_hop(grad_qk, qk_far).astype(BF16)
-
-    d_h = d_h_rows(ids, n_ep, n_sp, d_qk, d_v, w_qkv, [output, grad_down, grad_gate])
+    grad_qk = last_hop(*scatter_stacks(qk_stacks, n_ep)).astype(BF16)
+
+    d_h = d_h_rows(ids, n_ep, n_sp, d_qk, d_v, w_qkv, [])
+    output, d_h = tie(output, d_h)
     halves = plus(d_h[:2], swap_sp(d_h[2:], 1))
     d_h = halves[0].astype(F32) + swap_sp(halves[1], 2).astype(F32)
     x_rows = tokens[0].astype(F32)
@@ -1000,7 +1013,7 @@
 
     g_query, g_key, g_value, g_out, tiny, g_attn = finish(
         ids, n_ep, w_query, w_key, w_value, attn_gain.astype(F32)[:, None],
-        gather_sp(grad_qk), gather_sp(grad_vo), [grad_down, grad_gate, grad_up, input_grad],
+        gather_sp(grad_qk), gather_sp(grad_vo), [grad_down, grad_gate, grad_up],
     )
     per_row = 2 * head_width // shard
 

time: 938 us -> 939 us (level)
    all_to_all x1, waiting for transfers between devices: 22.1 us -> 56.5 us  [body(): lax.all_to_all(d_gates, 'ep', split_axis=0, concat_axis=0, tiled=True)]
    ppermute x36, waiting for transfers between devices: 267 us -> 242 us  [swap(): return lax.ppermute(value, 'ep', [(i, i ^ bits) for i in range(8)])]
  transfers between devices with their start and end apart: 69 -> 69, of which waited for: 23 -> 25; matrix products, arithmetic and copies ran while one was open for 11% -> 11% of each run, Pallas kernels for 32% -> 34%
where the time goes in v10:
time: 939 us; the launch traced here: 929 us
  waiting for transfers between devices  383 us (41%)
  Pallas kernels  320 us (34%)
  starting transfers between devices  87.6 us (9%)
  other arithmetic  71.6 us (8%)
  local copies, waits for them, and re-layouts  34 us (4%)
  between operations  31.1 us (3%)
    pallas_call x27, Pallas kernels, call(): pl.pallas_call(kernel, grid_spec=pltpu.PrefetchScalarGridSpec(num_scalar_...  320 us
    ppermute x36, waiting for transfers between devices, swap(): return lax.ppermute(value, 'ep', [(i, i ^ bits) for i in range(8)])  242 us
    all_to_all x1, waiting for transfers between devices, body(): lax.all_to_all(d_gates, 'ep', split_axis=0, concat_axis=0, tiled=True)  56.5 us
    ppermute x36, starting transfers between devices, swap(): return lax.ppermute(value, 'ep', [(i, i ^ bits) for i in range(8)])  45.1 us
    all_to_all x1, waiting for transfers between devices, body(): lax.all_to_all(mixed, 'sp', split_axis=0, concat_axis=1, tiled=True)  32 us
    ppermute x2, waiting for transfers between devices, gather_line(): farther = inner + lax.ppermute(outer, 'ep', OUTWARD)  27.7 us
    ppermute x14, waiting for transfers between devices, swap_sp(): return lax.ppermute(value, 'sp', [(i, i ^ bits) for i in range(4)])  21.4 us
  transfers between devices with their start and end apart: 69, of which 25 were waited for; matrix products, arithmetic and copies ran while one was open for 11% of the time, Pallas kernels for 34%

profile of v10, /device:TPU:0, one launch (start us, length us, event | category | flops | bytes accessed | tf_op | source)
XLA Modules:
  0.0 928.6 jit_solution(280420021299910156)
XLA Ops:
  15.7 20.9 %collective-permute-done.refs_2_ = bf16[256,2048]{1,0:T(8,128)(2,1)S(1)} collective-permute-done((bf16[256,2048]{1,0:T(8,128)(2,1)S(1)}, bf16[256,2048]{1,0:T(8,128)(2,1)S(1)}, u32[]{:S(2)}, u32[]{:S(2)}) %collective-permute-start) | collective-permute-done | bytes 1048608 | tf_op jit(solution)/shard_map/ppermute | solution.py:88
  40.3 21.0 %collective-permute-done.1.refs_3_ = bf16[256,2048]{1,0:T(8,128)(2,1)S(1)} collective-permute-done((bf16[256,2048]{1,0:T(8,128)(2,1)S(1)}, bf16[256,2048]{1,0:T(8,128)(2,1)S(1)}, u32[]{:S(2)}, u32[]{:S(2)}) %collective-permute-start.1) | collective-permute-done | bytes 1048608 | tf_op jit(solution)/shard_map/ppermute | solution.py:88
  65.1 7.6 all-to-all-start
  77.5 14.5 %collective-permute-done.7 = bf16[256,2048]{1,0:T(8,128)(2,1)} collective-permute-done((bf16[256,2048]{1,0:T(8,128)(2,1)S(1)}, bf16[256,2048]{1,0:T(8,128)(2,1)}, u32[]{:S(2)}, u32[]{:S(2)}) %collective-permute-start.7) | collective-permute-done | bytes 1048608 | tf_op jit(solution)/shard_map/ppermute | solution.py:111
  101.4 21.3 %collective-permute-done.8.refs_7_ = bf16[256,2048]{1,0:T(8,128)(2,1)} collective-permute-done((bf16[256,2048]{1,0:T(8,128)(2,1)}, bf16[256,2048]{1,0:T(8,128)(2,1)}, u32[]{:S(2)}, u32[]{:S(2)}) %collective-permute-start.8) | collective-permute-done | bytes 1048608 | tf_op jit(solution)/shard_map/ppermute | solution.py:88
  124.0 17.0 %qkv_project.1 = (f32[1024,512]{1,0:T(8,128)}, f32[1024,512]{1,0:T(8,128)}, bf16[1024,512]{1,0:T(8,128)(2,1)}, f32[16,1024]{1,0:T(8,128)}, bf16[2048,1536]{1,0:T...) custom-call(s32[12]{0:T(128)} %pad_add_fusion.ids.refs_0_, bf16[1024,2048]{1,0:T(8,128)(2,1)} %bitcast.177, ...), custom_call_target="tpu_custom_call" | custom-call | flops 128849018880 | bytes 30482432 | tf_op jit(solution)/shard_map/qkv_project/pallas_call | solution.py:62
  153.1 17.2 %attend.1 = (bf16[1024,512]{1,0:T(8,128)(2,1)}, bf16[1024,512]{1,0:T(8,128)(2,1)}, bf16[1024,512]{1,0:T(8,128)(2,1)}) custom-call(f32[1024,512]{1,0:T(8,128)} %get-tuple-element.125.refs_0_.qr_ref.refs_4_, f32[1024,512]{1,0:T(8,128)} %get-tuple-element.126.refs_1_.kr_ref.refs_5_, bf16[1024,512]{1,0:T(8,128)(2,1)} %get-tuple-element.127.refs_2_.v_ref, ...), custom_call_target="tpu_custom_call" | custom-call | flops 32212254720 | bytes 9510912 | tf_op jit(solution)/shard_map/attend/pallas_call | solution.py:62
  178.7 32.0 %all-to-all-done.2 = bf16[4,256,512]{2,1,0:T(8,128)(2,1)S(1)} async-done(((bf16[4,256,512]{2,1,0:T(8,128)(2,1)}), bf16[4,256,512]{2,1,0:T(8,128)(2,1)S(1)}, u32[]{:S(2)}, u32[]{:S(2)}) %all-to-all-start.2) | async-done | bytes 1048608 | tf_op jit(solution)/shard_map/all_to_all | solution.py:882
  233.9 8.8 out_project.1
  251.4 6.2 collective-permute-done.22.refs_2_
  270.6 9.4 %collective-permute-done.21.refs_2_ = bf16[256,2048]{1,0:T(8,128)(2,1)} collective-permute-done((bf16[256,2048]{1,0:T(8,128)(2,1)}, bf16[256,2048]{1,0:T(8,128)(2,1)}, u32[]{:S(2)}, u32[]{:S(2)}) %collective-permute-start.21) | collective-permute-done | bytes 1048608 | tf_op jit(solution)/shard_map/ppermute | solution.py:88
  283.8 18.7 %collective-permute-done.19.refs_1_ = bf16[256,2048]{1,0:T(8,128)(2,1)} collective-permute-done((bf16[256,2048]{1,0:T(8,128)(2,1)}, bf16[256,2048]{1,0:T(8,128)(2,1)}, u32[]{:S(2)}, u32[]{:S(2)}) %collective-permute-start.19) | collective-permute-done | bytes 1048608 | tf_op jit(solution)/shard_map/ppermute | solution.py:88
  302.5 22.1 %collective-permute-done.18.refs_1_ = bf16[256,2048]{1,0:T(8,128)(2,1)} collective-permute-done((bf16[256,2048]{1,0:T(8,128)(2,1)S(1)}, bf16[256,2048]{1,0:T(8,128)(2,1)}, u32[]{:S(2)}, u32[]{:S(2)}) %collective-permute-start.18) | collective-permute-done | bytes 1048608 | tf_op jit(solution)/shard_map/ppermute | solution.py:88
  329.2 4.4 dispatch.8
  333.7 4.4 dispatch.9
  338.1 13.2 %collective-permute-done.25 = bf16[256,2048]{1,0:T(8,128)(2,1)S(1)} collective-permute-done((bf16[256,2048]{1,0:T(8,128)(2,1)S(1)}, bf16[256,2048]{1,0:T(8,128)(2,1)S(1)}, u32[]{:S(2)}, u32[]{:S(2)}) %collective-permute-start.25) | collective-permute-done | bytes 1048608 | tf_op jit(solution)/shard_map/ppermute | solution.py:111
  353.3 42.5 %experts.2 = (bf16[2,576,1024]{2,1,0:T(8,128)(2,1)}, bf16[2,576,1024]{2,1,0:T(8,128)(2,1)}, bf16[2,576,1024]{2,1,0:T(8,128)(2,1)}, f32[2,576,1]{2,1,0:T(8,128)},...) custom-call(bf16[2,576,2048]{2,1,0:T(8,128)(2,1)} %get-tuple-element.140.refs_0_, ...), custom_call_target="tpu_custom_call" | custom-call | flops 579820584960 | bytes 51127296 | tf_op jit(solution)/shard_map/experts/pallas_call | solution.py:62
  395.8 4.5 dispatch.14
  400.3 4.5 dispatch.15
  404.8 4.0 combine.5
  408.7 4.0 combine.4
  414.7 42.9 %experts.3 = (bf16[2,576,1024]{2,1,0:T(8,128)(2,1)}, bf16[2,576,1024]{2,1,0:T(8,128)(2,1)}, bf16[2,576,1024]{2,1,0:T(8,128)(2,1)}, f32[2,576,1]{2,1,0:T(8,128)},...) custom-call(bf16[2,576,2048]{2,1,0:T(8,128)(2,1)} %get-tuple-element.149.refs_3_.refs_0_.refs_1_, ...), custom_call_target="tpu_custom_call" | custom-call | flops 579820584960 | bytes 51127296 | tf_op jit(solution)/shard_map/experts/pallas_call | solution.py:62
  463.0 4.0 combine.7
  466.9 4.1 combine.6
  473.1 10.5 %combine_stacks.1 = (bf16[2,256,2048]{2,1,0:T(8,128)(2,1)}, bf16[2,256,2048]{2,1,0:T(8,128)(2,1)}, bf16[2,256,2048]{2,1,0:T(8,128)(2,1)}, bf16[2,256,2048]{2,1,0:T(8,128)(2,1)}) custom-call(s32[16,256]{1,0:T(8,128)} %copy-done.41, bf16[2,576,2048]{2,1,0:T(8,128)(2,1)} %get-tuple-element.145.refs_1_, bf16[2,576,2048]{2,1,0:T(8,128)(2,1)} %get-tuple-element.156.refs_2_, ...), custom_call_target="tpu_custom_call" | custom-call | flops 48318382080 | bytes 17842176 | tf_op jit(solution)/shard_map/combine_stacks/pallas_call | solution.py:62
  488.3 8.8 collective-permute-done.31
  498.6 18.1 %weight_grad.3.refs_4_ = bf16[2,1024,2048]{2,1,0:T(8,128)(2,1)} custom-call(bf16[2,576,1024]{2,1,0:T(8,128)(2,1)} %get-tuple-element.166.refs_0_, bf16[2,576,1024]{2,1,0:T(8,128)(2,1)} %get-tuple-element.167.refs_1_, bf16[2,576,2048]{2,1,0:T(8,128)(2,1)} %dispatch.11.refs_1_.refs_6_.refs_10_.refs_2_, ...), custom_call_target="tpu_custom_call" | custom-call | flops 193273528320 | bytes 22544384 | tf_op jit(solution)/shard_map/weight_grad/pallas_call | solution.py:62
  527.0 3.9 all-to-all-start.3
  532.8 19.3 %weight_grad.4.refs_4_ = bf16[2,2048,1024]{2,1,0:T(8,128)(2,1)} custom-call(bf16[2,576,2048]{2,1,0:T(8,128)(2,1)} %get-tuple-element.140.refs_0_, bf16[2,576,2048]{2,1,0:T(8,128)(2,1)} %get-tuple-element.149.refs_3_.refs_0_.refs_1_, bf16[2,576,1024]{2,1,0:T(8,128)(2,1)} %get-tuple-element.182.refs_2_, bf16[2,576,1024]{2,1,0:T(8,128)(2,1)} %get-tuple-element.183.refs_3_, ...), custom_call_target="tpu_custom_call" | custom-call | flops 193273528320 | bytes 22544384 | tf_op jit(solution)/shard_map/weight_grad/pallas_call | solution.py:62
  552.1 56.5 %all-to-all-done.3 = f32[8,2,256]{2,1,0:T(2,128)} async-done(((f32[8,2,256]{2,1,0:T(2,128)}), f32[8,2,256]{2,1,0:T(2,128)}, u32[]{:S(2)}, u32[]{:S(2)}) %all-to-all-start.3) | async-done | bytes 16416 | tf_op jit(solution)/shard_map/all_to_all | solution.py:946
  610.0 19.0 %weight_grad.5 = bf16[2,2048,1024]{2,1,0:T(8,128)(2,1)} custom-call(bf16[2,576,2048]{2,1,0:T(8,128)(2,1)} %get-tuple-element.140.refs_0_, bf16[2,576,2048]{2,1,0:T(8,128)(2,1)} %get-tuple-element.149.refs_3_.refs_0_.refs_1_, bf16[2,576,1024]{2,1,0:T(8,128)(2,1)} %get-tuple-element.180.refs_2_, bf16[2,576,1024]{2,1,0:T(8,128)(2,1)} %get-tuple-element.181.refs_3_, ...), custom_call_target="tpu_custom_call" | custom-call | flops 193273528320 | bytes 22544384 | tf_op jit(solution)/shard_map/weight_grad/pallas_call | solution.py:62
  640.8 7.9 out_back.1
  655.8 23.2 %collective-permute-done.34 = bf16[2,256,2048]{2,1,0:T(8,128)(2,1)} collective-permute-done((bf16[2,256,2048]{2,1,0:T(8,128)(2,1)}, bf16[2,256,2048]{2,1,0:T(8,128)(2,1)}, u32[]{:S(2)}, u32[]{:S(2)}) %collective-permute-start.34) | collective-permute-done | bytes 2097184 | tf_op jit(solution)/shard_map/ppermute | solution.py:88
  688.7 24.3 %attend_back.1 = (f32[1024,512]{1,0:T(8,128)}, f32[1024,512]{1,0:T(8,128)}, bf16[1024,512]{1,0:T(8,128)(2,1)}, f32[16,1024]{1,0:T(8,128)}, f32[1,512]{1,0:T(1,128)}, /*index=5*/f32[1,512]{1,0:T(1,128)}) custom-call(bf16[1024,512]{1,0:T(8,128)(2,1)} %get-tuple-element.190.q_ref, bf16[1024,512]{1,0:T(8,128)(2,1)} %get-tuple-element.191.k_ref, ...), custom_call_target="tpu_custom_call" | custom-call | flops 75161927680 | bytes 14823424 | tf_op jit(solution)/shard_map/attend_back/pallas_call | solution.py:62
  716.1 10.6 %vo_grads.1 = (bf16[2,256,1024]{2,1,0:T(8,128)(2,1)}, bf16[2,256,1024]{2,1,0:T(8,128)(2,1)}, bf16[2,256,1024]{2,1,0:T(8,128)(2,1)}, bf16[2,256,1024]{2,1,0:T(8,128)(2,1)}) custom-call(s32[12]{0:T(128)} %pad_add_fusion.ids.refs_0_, bf16[1024,2048]{1,0:T(8,128)(2,1)} %get-tuple-element.189.h_ref.refs_1_, bf16[1024,512]{1,0:T(8,128)(2,1)} %get-tuple-element.198.dv_ref, ...), custom_call_target="tpu_custom_call" | custom-call | flops 85899345920 | bytes 14680064 | tf_op jit(solution)/shard_map/vo_grads/pallas_call | solution.py:62
  732.2 12.8 %qk_back.1 = (bf16[2,272,1024]{2,1,0:T(8,128)(2,1)}, bf16[2,272,1024]{2,1,0:T(8,128)(2,1)}, bf16[2,272,1024]{2,1,0:T(8,128)(2,1)}, bf16[2,272,1024]{2,1,0:T(8,128)(2,1)}, bf16[1024,1024]{1,0:T(8,128)(2,1)}) custom-call(s32[12]{0:T(128)} %pad_add_fusion.ids.refs_0_, bf16[1024,2048]{1,0:T(8,128)(2,1)} %get-tuple-element.189.h_ref.refs_1_, ...), custom_call_target="tpu_custom_call" | custom-call | flops 85899345920 | bytes 19423232 | tf_op jit(solution)/shard_map/qk_back/pallas_call | solution.py:62
  746.4 12.4 %d_h.1 = bf16[4,256,2048]{2,1,0:T(8,128)(2,1)} custom-call(s32[12]{0:T(128)} %pad_add_fusion.ids.refs_0_, bf16[1024,1024]{1,0:T(8,128)(2,1)} %get-tuple-element.200.d_ref, bf16[1024,512]{1,0:T(8,128)(2,1)} %get-tuple-element.198.dv_ref, bf16[2048,1536]{1,0:T(8,128)(2,1)} %get-tuple-element.201.w_ref), custom_call_target="tpu_custom_call" | custom-call | flops 128849018880 | bytes 13631488 | tf_op jit(solution)/shard_map/d_h/pallas_call | solution.py:62
  762.7 15.7 %collective-permute-done.38 = bf16[256,2048]{1,0:T(8,128)(2,1)} collective-permute-done((bf16[256,2048]{1,0:T(8,128)(2,1)}, bf16[256,2048]{1,0:T(8,128)(2,1)}, u32[]{:S(2)}, u32[]{:S(2)}) %collective-permute-start.38) | collective-permute-done | bytes 1048608 | tf_op jit(solution)/shard_map/ppermute | solution.py:88
  783.9 15.4 %collective-permute-done.45 = bf16[2,272,1024]{2,1,0:T(8,128)(2,1)S(1)} collective-permute-done((bf16[2,272,1024]{2,1,0:T(8,128)(2,1)}, bf16[2,272,1024]{2,1,0:T(8,128)(2,1)S(1)}, u32[]{:S(2)}, u32[]{:S(2)}) %collective-permute-start.45) | collective-permute-done | bytes 1114144 | tf_op jit(solution)/shard_map/ppermute | solution.py:88
  805.3 17.4 %collective-permute-done.44 = bf16[2,272,1024]{2,1,0:T(8,128)(2,1)S(1)} collective-permute-done((bf16[2,272,1024]{2,1,0:T(8,128)(2,1)S(1)}, bf16[2,272,1024]{2,1,0:T(8,128)(2,1)S(1)}, u32[]{:S(2)}, u32[]{:S(2)}) %collective-permute-start.44) | collective-permute-done | bytes 1114144 | tf_op jit(solution)/shard_map/ppermute | solution.py:88
  822.7 14.0 %collective-permute-done.46 = bf16[2,272,1024]{2,1,0:T(8,128)(2,1)S(1)} collective-permute-done((bf16[2,272,1024]{2,1,0:T(8,128)(2,1)S(1)}, bf16[2,272,1024]{2,1,0:T(8,128)(2,1)S(1)}, u32[]{:S(2)}, u32[]{:S(2)}) %collective-permute-start.46) | collective-permute-done | bytes 1114144 | tf_op jit(solution)/shard_map/ppermute | solution.py:88
  842.3 20.6 %collective-permute-done.47 = bf16[272,1024]{1,0:T(8,128)(2,1)S(1)} collective-permute-done((bf16[272,1024]{1,0:T(8,128)(2,1)S(1)}, bf16[272,1024]{1,0:T(8,128)(2,1)S(1)}, u32[]{:S(2)}, u32[]{:S(2)}) %collective-permute-start.47) | collective-permute-done | bytes 557088 | tf_op jit(solution)/shard_map/ppermute | solution.py:88
  868.6 21.4 %collective-permute-done.56.refs_11_ = bf16[256,1024]{1,0:T(8,128)(2,1)} collective-permute-done((bf16[256,1024]{1,0:T(8,128)(2,1)}, bf16[256,1024]{1,0:T(8,128)(2,1)}, u32[]{:S(2)}, u32[]{:S(2)}) %collective-permute-start.56) | collective-permute-done | bytes 524320 | tf_op jit(solution)/shard_map/ppermute | solution.py:92
  892.8 4.3 fusion.6
  897.1 4.1 convert_element_type.263.refs_13_
  901.2 4.1 convert_element_type.264.refs_14_
  905.3 4.1 convert_element_type.265.refs_15_
  909.4 7.9 finish.1
  (369 shorter events, 192.1 us)
Async XLA Ops:
  7.2 116.8 %all-gather.6.cloned.1.call-start = ((), (), s32[]{:S(2)}) async-start(), calls=%async_computation.13 | async-start | bytes 5242880 | tf_op jit(solution)/shard_map/all_gather | solution.py:826
  39.0 35.1 %collective-permute-start.5 = (bf16[256,2048]{1,0:T(8,128)(2,1)S(1)}, bf16[256,2048]{1,0:T(8,128)(2,1)S(1)}, u32[]{:S(2)}, u32[]{:S(2)}) collective-permute-start(bf16[256,2048]{1,0:T(8,128)(2,1)S(1)} %collective-permute-done.4), channel_id=1, source_target_pairs={{2,0},{3,1},{4,6},{5,7},{10,8},{11,9},{12,14},{13,15},{18,16},{19,... | collective-permute-start | bytes 3145736 | tf_op jit(solution)/shard_map/ppermute | solution.py:110
  62.3 29.7 %collective-permute-start.7 = (bf16[256,2048]{1,0:T(8,128)(2,1)S(1)}, bf16[256,2048]{1,0:T(8,128)(2,1)}, u32[]{:S(2)}, u32[]{:S(2)}) collective-permute-start(bf16[256,2048]{1,0:T(8,128)(2,1)S(1)} %collective-permute-done.3), channel_id=1, source_target_pairs={{2,0},{3,1},{4,6},{5,7},{10,8},{11,9},{12,14},{13,15},{18,16},{19,... | collective-permute-start | bytes 3145736 | tf_op jit(solution)/shard_map/ppermute | solution.py:111
  65.1 33.5 %all-to-all-start = ((bf16[8,48,256]{2,1,0:T(8,128)(2,1)}), bf16[8,48,256]{2,1,0:T(8,128)(2,1)S(1)}, u32[]{:S(2)}, u32[]{:S(2)}) async-start(bf16[8,48,256]{2,1,0:T(8,128)(2,1)} %broadcast_in_dim.65), calls=%async_computation | async-start | bytes 393216 | tf_op jit(solution)/shard_map/all_to_all | solution.py:814
  75.4 48.5 %collective-permute-start.6 = (bf16[256,2048]{1,0:T(8,128)(2,1)}, bf16[256,2048]{1,0:T(8,128)(2,1)}, u32[]{:S(2)}, u32[]{:S(2)}) collective-permute-start(bf16[256,2048]{1,0:T(8,128)(2,1)} %add.172.refs_4_), channel_id=1, source_target_pairs={{0,1},{1,0},{2,3},{3,2},{4,5},{5,4},{6,7},{7,6},{8,9},{9,8},{10,11... | collective-permute-start | bytes 3145736 | tf_op jit(solution)/shard_map/ppermute | solution.py:88
  94.6 28.0 %collective-permute-start.8 = (bf16[256,2048]{1,0:T(8,128)(2,1)}, bf16[256,2048]{1,0:T(8,128)(2,1)}, u32[]{:S(2)}, u32[]{:S(2)}) collective-permute-start(bf16[256,2048]{1,0:T(8,128)(2,1)} %add.173.refs_6_), channel_id=1, source_target_pairs={{0,1},{1,0},{2,3},{3,2},{4,5},{5,4},{6,7},{7,6},{8,9},{9,8},{10,11... | collective-permute-start | bytes 3145736 | tf_op jit(solution)/shard_map/ppermute | solution.py:88
  99.3 48.7 %collective-permute-start.12 = (bf16[256,2048]{1,0:T(8,128)(2,1)S(1)}, bf16[256,2048]{1,0:T(8,128)(2,1)}, u32[]{:S(2)}, u32[]{:S(2)}) collective-permute-start(bf16[256,2048]{1,0:T(8,128)(2,1)S(1)} %bitcast.137), channel_id=1, source_target_pairs={{0,4},{1,5},{2,6},{3,7},{4,0},{5,1},{6,2},{7,3},{8,12},{9,13},{10,... | collective-permute-start | bytes 3145736 | tf_op jit(solution)/shard_map/ppermute | solution.py:88
  99.3 49.7 %collective-permute-start.10 = (bf16[256,2048]{1,0:T(8,128)(2,1)S(1)}, bf16[256,2048]{1,0:T(8,128)(2,1)}, u32[]{:S(2)}, u32[]{:S(2)}) collective-permute-start(bf16[256,2048]{1,0:T(8,128)(2,1)S(1)} %bitcast.138), channel_id=1, source_target_pairs={{0,2},{1,3},{2,0},{3,1},{4,6},{5,7},{6,4},{7,5},{8,10},{9,11},{10,... | collective-permute-start | bytes 3145736 | tf_op jit(solution)/shard_map/ppermute | solution.py:88
  122.7 30.4 %collective-permute-start.14 = (bf16[256,2048]{1,0:T(8,128)(2,1)S(1)}, bf16[256,2048]{1,0:T(8,128)(2,1)}, u32[]{:S(2)}, u32[]{:S(2)}) collective-permute-start(bf16[256,2048]{1,0:T(8,128)(2,1)S(1)} %bitcast.139), channel_id=1, source_target_pairs={{0,1},{1,0},{2,3},{3,2},{4,5},{5,4},{6,7},{7,6},{8,9},{9,8},{10,11... | collective-permute-start | bytes 3145736 | tf_op jit(solution)/shard_map/ppermute | solution.py:88
  152.1 59.9 %collective-permute-start.9 = (bf16[2048,512]{1,0:T(8,128)(2,1)}, bf16[2048,512]{1,0:T(8,128)(2,1)}, u32[]{:S(2)}, u32[]{:S(2)}) collective-permute-start(bf16[2048,512]{1,0:T(8,128)(2,1)} %get-tuple-element.124.refs_0_), channel_id=1, source_target_pairs={{0,16},{8,24},{16,0},{24,8},{1,17},{9,25},{17,1},{25,9},{2,18},{10... | collective-permute-start | bytes 6291464 | tf_op jit(solution)/shard_map/ppermute | solution.py:92
  174.6 36.1 %all-to-all-start.2 = ((bf16[4,256,512]{2,1,0:T(8,128)(2,1)}), bf16[4,256,512]{2,1,0:T(8,128)(2,1)S(1)}, u32[]{:S(2)}, u32[]{:S(2)}) async-start(bf16[4,256,512]{2,1,0:T(8,128)(2,1)} %bitcast.146), calls=%async_computation.2 | async-start | bytes 2097152 | tf_op jit(solution)/shard_map/all_to_all | solution.py:882
  178.3 536.9 %all-gather.4.cloned.1.call-start = ((), (), s32[]{:S(2)}) async-start(), calls=%async_computation.9 | async-start | bytes 5242880 | tf_op jit(solution)/shard_map/all_gather | solution.py:888
  178.3 55.6 %collective-permute-start.15 = (bf16[2048,512]{1,0:T(8,128)(2,1)S(1)}, bf16[2048,512]{1,0:T(8,128)(2,1)}, u32[]{:S(2)}, u32[]{:S(2)}) collective-permute-start(bf16[2048,512]{1,0:T(8,128)(2,1)S(1)} %copy-done.55), channel_id=1, source_target_pairs={{0,8},{8,0},{16,24},{24,16},{1,9},{9,1},{17,25},{25,17},{2,10},{10... | collective-permute-start | bytes 6291464 | tf_op jit(solution)/shard_map/ppermute | solution.py:92
  231.3 26.3 %collective-permute-start.22 = (bf16[256,2048]{1,0:T(8,128)(2,1)}, bf16[256,2048]{1,0:T(8,128)(2,1)}, u32[]{:S(2)}, u32[]{:S(2)}) collective-permute-start(bf16[256,2048]{1,0:T(8,128)(2,1)} %collective-permute-done.12.refs_11_.refs_1_), channel_id=1, source_target_pairs={{0,1},{1,0},{2,3},{3,2},{4,5},{5,4},{6,7},{7,6},{8,9},{9,8},{10,11... | collective-permute-start | bytes 3145736 | tf_op jit(solution)/shard_map/ppermute | solution.py:88
  232.0 48.0 %collective-permute-start.21 = (bf16[256,2048]{1,0:T(8,128)(2,1)}, bf16[256,2048]{1,0:T(8,128)(2,1)}, u32[]{:S(2)}, u32[]{:S(2)}) collective-permute-start(bf16[256,2048]{1,0:T(8,128)(2,1)} %collective-permute-done.13.refs_1_), channel_id=1, source_target_pairs={{0,1},{1,0},{2,3},{3,2},{4,5},{5,4},{6,7},{7,6},{8,9},{9,8},{10,11... | collective-permute-start | bytes 3145736 | tf_op jit(solution)/shard_map/ppermute | solution.py:88
  233.3 663.7 %reduce-scatter.4.cloned.1.call-start = ((), (), s32[]{:S(2)}) async-start(), calls=%async_computation.10 | async-start | bytes 10485760 | tf_op jit(solution)/shard_map/reduce_scatter | solution.py:952
  243.6 58.9 %collective-permute-start.19 = (bf16[256,2048]{1,0:T(8,128)(2,1)}, bf16[256,2048]{1,0:T(8,128)(2,1)}, u32[]{:S(2)}, u32[]{:S(2)}) collective-permute-start(bf16[256,2048]{1,0:T(8,128)(2,1)} %get-tuple-element.135.refs_0_), channel_id=1, source_target_pairs={{0,1},{1,0},{2,3},{3,2},{4,5},{5,4},{6,7},{7,6},{8,9},{9,8},{10,11... | collective-permute-start | bytes 3145736 | tf_op jit(solution)/shard_map/ppermute | solution.py:88
  267.9 56.7 %collective-permute-start.18 = (bf16[256,2048]{1,0:T(8,128)(2,1)S(1)}, bf16[256,2048]{1,0:T(8,128)(2,1)}, u32[]{:S(2)}, u32[]{:S(2)}) collective-permute-start(bf16[256,2048]{1,0:T(8,128)(2,1)S(1)} %collective-permute-done.17.refs_0_), channel_id=1, source_target_pairs={{0,1},{1,0},{2,3},{3,2},{4,5},{5,4},{6,7},{7,6},{8,9},{9,8},{10,11... | collective-permute-start | bytes 3145736 | tf_op jit(solution)/shard_map/ppermute | solution.py:88
  268.6 56.0 %collective-permute-start.20 = (bf16[256,2048]{1,0:T(8,128)(2,1)S(1)}, bf16[256,2048]{1,0:T(8,128)(2,1)S(1)}, u32[]{:S(2)}, u32[]{:S(2)}) collective-permute-start(bf16[256,2048]{1,0:T(8,128)(2,1)S(1)} %collective-permute-done.17.refs_0_), channel_id=1, source_target_pairs={{2,4},{3,5},{4,2},{5,3},{10,12},{11,13},{12,10},{13,11},{18,20},{1... | collective-permute-start | bytes 3145736 | tf_op jit(solution)/shard_map/ppermute | solution.py:108
  269.3 56.6 %collective-permute-start.24 = (bf16[256,2048]{1,0:T(8,128)(2,1)S(1)}, bf16[256,2048]{1,0:T(8,128)(2,1)}, u32[]{:S(2)}, u32[]{:S(2)}) collective-permute-start(bf16[256,2048]{1,0:T(8,128)(2,1)S(1)} %collective-permute-done.23), channel_id=1, source_target_pairs={{2,0},{3,1},{4,6},{5,7},{10,8},{11,9},{12,14},{13,15},{18,16},{19,... | collective-permute-start | bytes 3145736 | tf_op jit(solution)/shard_map/ppermute | solution.py:110
  324.6 26.7 %collective-permute-start.25 = (bf16[256,2048]{1,0:T(8,128)(2,1)S(1)}, bf16[256,2048]{1,0:T(8,128)(2,1)S(1)}, u32[]{:S(2)}, u32[]{:S(2)}) collective-permute-start(bf16[256,2048]{1,0:T(8,128)(2,1)S(1)} %collective-permute-done.20), channel_id=1, source_target_pairs={{2,0},{3,1},{4,6},{5,7},{10,8},{11,9},{12,14},{13,15},{18,16},{19,... | collective-permute-start | bytes 3145736 | tf_op jit(solution)/shard_map/ppermute | solution.py:111
  328.5 67.3 %collective-permute-start.27 = (bf16[256,2048]{1,0:T(8,128)(2,1)}, bf16[256,2048]{1,0:T(8,128)(2,1)}, u32[]{:S(2)}, u32[]{:S(2)}) collective-permute-start(bf16[256,2048]{1,0:T(8,128)(2,1)} %add.185.refs_8_.refs_1_.refs_12_), channel_id=1, source_target_pairs={{0,1},{1,0},{2,3},{3,2},{4,5},{5,4},{6,7},{7,6},{8,9},{9,8},{10,11... | collective-permute-start | bytes 3145736 | tf_op jit(solution)/shard_map/ppermute | solution.py:88
  352.6 47.7 %collective-permute-start.26 = (bf16[256,2048]{1,0:T(8,128)(2,1)}, bf16[256,2048]{1,0:T(8,128)(2,1)}, u32[]{:S(2)}, u32[]{:S(2)}) collective-permute-start(bf16[256,2048]{1,0:T(8,128)(2,1)} %add.186.refs_9_.refs_1_.refs_13_), channel_id=1, source_target_pairs={{0,1},{1,0},{2,3},{3,2},{4,5},{5,4},{6,7},{7,6},{8,9},{9,8},{10,11... | collective-permute-start | bytes 3145736 | tf_op jit(solution)/shard_map/ppermute | solution.py:88
  412.7 44.9 %collective-permute-start.29 = (bf16[256,2048]{1,0:T(8,128)(2,1)}, bf16[256,2048]{1,0:T(8,128)(2,1)}, u32[]{:S(2)}, u32[]{:S(2)}) collective-permute-start(bf16[256,2048]{1,0:T(8,128)(2,1)} %get-tuple-element.155.refs_9_.refs_6_), channel_id=1, source_target_pairs={{0,1},{1,0},{2,3},{3,2},{4,5},{5,4},{6,7},{7,6},{8,9},{9,8},{10,11... | collective-permute-start | bytes 3145736 | tf_op jit(solution)/shard_map/ppermute | solution.py:88
  414.0 46.4 %collective-permute-start.28 = (bf16[256,2048]{1,0:T(8,128)(2,1)}, bf16[256,2048]{1,0:T(8,128)(2,1)}, u32[]{:S(2)}, u32[]{:S(2)}) collective-permute-start(bf16[256,2048]{1,0:T(8,128)(2,1)} %get-tuple-element.153.refs_7_.refs_4_), channel_id=1, source_target_pairs={{0,1},{1,0},{2,3},{3,2},{4,5},{5,4},{6,7},{7,6},{8,9},{9,8},{10,11... | collective-permute-start | bytes 3145736 | tf_op jit(solution)/shard_map/ppermute | solution.py:88
  472.4 44.4 %collective-permute-start.30 = (bf16[256,2048]{1,0:T(8,128)(2,1)}, bf16[256,2048]{1,0:T(8,128)(2,1)}, u32[]{:S(2)}, u32[]{:S(2)}) collective-permute-start(bf16[256,2048]{1,0:T(8,128)(2,1)} %get-tuple-element.160.refs_8_), channel_id=1, source_target_pairs={{0,1},{1,0},{2,3},{3,2},{4,5},{5,4},{6,7},{7,6},{8,9},{9,8},{10,11... | collective-permute-start | bytes 3145736 | tf_op jit(solution)/shard_map/ppermute | solution.py:88
  518.4 112.0 %collective-permute-start.33 = (bf16[2,256,2048]{2,1,0:T(8,128)(2,1)}, bf16[2,256,2048]{2,1,0:T(8,128)(2,1)}, u32[]{:S(2)}, u32[]{:S(2)}) collective-permute-start(bf16[2,256,2048]{2,1,0:T(8,128)(2,1)} %get-tuple-element.170), channel_id=1, source_target_pairs={{0,1},{1,0},{2,3},{3,2},{4,5},{5,4},{6,7},{7,6},{8,9},{9,8},{10,11... | collective-permute-start | bytes 6291464 | tf_op jit(solution)/shard_map/ppermute | solution.py:88
  519.8 136.0 %collective-permute-start.32 = (bf16[2,256,2048]{2,1,0:T(8,128)(2,1)}, bf16[2,256,2048]{2,1,0:T(8,128)(2,1)}, u32[]{:S(2)}, u32[]{:S(2)}) collective-permute-start(bf16[2,256,2048]{2,1,0:T(8,128)(2,1)} %get-tuple-element.168), channel_id=1, source_target_pairs={{0,1},{1,0},{2,3},{3,2},{4,5},{5,4},{6,7},{7,6},{8,9},{9,8},{10,11... | collective-permute-start | bytes 6291464 | tf_op jit(solution)/shard_map/ppermute | solution.py:88
  523.2 111.3 %collective-permute-start.37 = (bf16[256,2048]{1,0:T(8,128)(2,1)}, bf16[256,2048]{1,0:T(8,128)(2,1)}, u32[]{:S(2)}, u32[]{:S(2)}) collective-permute-start(bf16[256,2048]{1,0:T(8,128)(2,1)} %add_convert_fusion.5.refs_5_), channel_id=1, source_target_pairs={{0,4},{1,5},{2,6},{3,7},{4,0},{5,1},{6,2},{7,3},{8,12},{9,13},{10,... | collective-permute-start | bytes 3145736 | tf_op jit(solution)/shard_map/ppermute | solution.py:88
  527.0 81.7 %all-to-all-start.3 = ((f32[8,2,256]{2,1,0:T(2,128)}), f32[8,2,256]{2,1,0:T(2,128)}, u32[]{:S(2)}, u32[]{:S(2)}) async-start(f32[8,2,256]{2,1,0:T(2,128)} %constant_dynamic-update-slice_fusion.8), calls=%async_computation.3 | async-start | bytes 32768 | tf_op jit(solution)/shard_map/all_to_all | solution.py:946
  530.9 370.3 %reduce-scatter.6.cloned.1.call-start = ((), (), s32[]{:S(2)}) async-start(), calls=%async_computation.11 | async-start | bytes 10485760 | tf_op jit(solution)/shard_map/reduce_scatter | solution.py:952
  530.9 103.6 %collective-permute-start.36 = (bf16[256,2048]{1,0:T(8,128)(2,1)}, bf16[256,2048]{1,0:T(8,128)(2,1)}, u32[]{:S(2)}, u32[]{:S(2)}) collective-permute-start(bf16[256,2048]{1,0:T(8,128)(2,1)} %add_convert_fusion.8.refs_4_), channel_id=1, source_target_pairs={{0,2},{1,3},{2,0},{3,1},{4,6},{5,7},{6,4},{7,5},{8,10},{9,11},{10,... | collective-permute-start | bytes 3145736 | tf_op jit(solution)/shard_map/ppermute | solution.py:88
  634.5 44.5 %collective-permute-start.34 = (bf16[2,256,2048]{2,1,0:T(8,128)(2,1)}, bf16[2,256,2048]{2,1,0:T(8,128)(2,1)}, u32[]{:S(2)}, u32[]{:S(2)}) collective-permute-start(bf16[2,256,2048]{2,1,0:T(8,128)(2,1)} %add_convert_fusion.1), channel_id=1, source_target_pairs={{0,2},{1,3},{2,0},{3,1},{4,6},{5,7},{6,4},{7,5},{8,10},{9,11},{10,... | collective-permute-start | bytes 6291464 | tf_op jit(solution)/shard_map/ppermute | solution.py:88
  651.1 34.0 %all-to-all-start.4 = ((bf16[256,4,512]{2,0,1:T(8,128)(2,1)}), bf16[256,4,512]{2,0,1:T(8,128)(2,1)S(1)}, u32[]{:S(2)}, u32[]{:S(2)}) async-start(bf16[256,4,512]{2,0,1:T(8,128)(2,1)} %bitcast.134), calls=%async_computation.4 | async-start | bytes 2097152 | tf_op jit(solution)/shard_map/all_to_all | solution.py:974
  654.6 250.7 %reduce-scatter.8.cloned.1.call-start = ((), (), s32[]{:S(2)}) async-start(), calls=%async_computation.12 | async-start | bytes 10485760 | tf_op jit(solution)/shard_map/reduce_scatter | solution.py:952
  685.1 30.1 %all-to-all-start.5 = ((bf16[256,4,512]{2,0,1:T(8,128)(2,1)}), bf16[256,4,512]{2,0,1:T(8,128)(2,1)S(1)}, u32[]{:S(2)}, u32[]{:S(2)}) async-start(bf16[256,4,512]{2,0,1:T(8,128)(2,1)} %bitcast.133), calls=%async_computation.5 | async-start | bytes 2097152 | tf_op jit(solution)/shard_map/all_to_all | solution.py:975
  726.7 32.1 %collective-permute-start.52 = (bf16[2,256,1024]{2,1,0:T(8,128)(2,1)}, bf16[2,256,1024]{2,1,0:T(8,128)(2,1)}, u32[]{:S(2)}, u32[]{:S(2)}) collective-permute-start(bf16[2,256,1024]{2,1,0:T(8,128)(2,1)} %get-tuple-element.210), channel_id=1, source_target_pairs={{0,1},{1,0},{2,3},{3,2},{4,5},{5,4},{6,7},{7,6},{8,9},{9,8},{10,11... | collective-permute-start | bytes 3145736 | tf_op jit(solution)/shard_map/ppermute | solution.py:88
  727.9 72.3 %collective-permute-start.51 = (bf16[2,256,1024]{2,1,0:T(8,128)(2,1)}, bf16[2,256,1024]{2,1,0:T(8,128)(2,1)}, u32[]{:S(2)}, u32[]{:S(2)}) collective-permute-start(bf16[2,256,1024]{2,1,0:T(8,128)(2,1)} %get-tuple-element.208), channel_id=1, source_target_pairs={{0,1},{1,0},{2,3},{3,2},{4,5},{5,4},{6,7},{7,6},{8,9},{9,8},{10,11... | collective-permute-start | bytes 3145736 | tf_op jit(solution)/shard_map/ppermute | solution.py:88
  729.6 48.8 %collective-permute-start.38 = (bf16[256,2048]{1,0:T(8,128)(2,1)}, bf16[256,2048]{1,0:T(8,128)(2,1)}, u32[]{:S(2)}, u32[]{:S(2)}) collective-permute-start(bf16[256,2048]{1,0:T(8,128)(2,1)} %fusion.11), channel_id=1, source_target_pairs={{0,4},{1,5},{2,6},{3,7},{4,0},{5,1},{6,2},{7,3},{8,12},{9,13},{10,... | collective-permute-start | bytes 3145736 | tf_op jit(solution)/shard_map/ppermute | solution.py:88
  745.0 54.2 %collective-permute-start.45 = (bf16[2,272,1024]{2,1,0:T(8,128)(2,1)}, bf16[2,272,1024]{2,1,0:T(8,128)(2,1)S(1)}, u32[]{:S(2)}, u32[]{:S(2)}) collective-permute-start(bf16[2,272,1024]{2,1,0:T(8,128)(2,1)} %get-tuple-element.207), channel_id=1, source_target_pairs={{0,1},{1,0},{2,3},{3,2},{4,5},{5,4},{6,7},{7,6},{8,9},{9,8},{10,11... | collective-permute-start | bytes 3342344 | tf_op jit(solution)/shard_map/ppermute | solution.py:88
  761.0 39.6 %collective-permute-start.53 = (bf16[2,256,1024]{2,1,0:T(8,128)(2,1)S(1)}, bf16[2,256,1024]{2,1,0:T(8,128)(2,1)S(1)}, u32[]{:S(2)}, u32[]{:S(2)}) collective-permute-start(bf16[2,256,1024]{2,1,0:T(8,128)(2,1)S(1)} %add_convert_fusion.3), channel_id=1, source_target_pairs={{0,2},{1,3},{2,0},{3,1},{4,6},{5,7},{6,4},{7,5},{8,10},{9,11},{10,... | collective-permute-start | bytes 3145736 | tf_op jit(solution)/shard_map/ppermute | solution.py:88
  781.9 56.4 %collective-permute-start.42 = (bf16[2,256,2048]{2,1,0:T(8,128)(2,1)S(1)}, bf16[2,256,2048]{2,1,0:T(8,128)(2,1)S(1)}, u32[]{:S(2)}, u32[]{:S(2)}) collective-permute-start(bf16[2,256,2048]{2,1,0:T(8,128)(2,1)S(1)} %slice.240), channel_id=1, source_target_pairs={{0,8},{8,0},{16,24},{24,16},{1,9},{9,1},{17,25},{25,17},{2,10},{10... | collective-permute-start | bytes 6291464 | tf_op jit(solution)/shard_map/ppermute | solution.py:92
  782.9 39.8 %collective-permute-start.44 = (bf16[2,272,1024]{2,1,0:T(8,128)(2,1)S(1)}, bf16[2,272,1024]{2,1,0:T(8,128)(2,1)S(1)}, u32[]{:S(2)}, u32[]{:S(2)}) collective-permute-start(bf16[2,272,1024]{2,1,0:T(8,128)(2,1)S(1)} %copy-done.56), channel_id=1, source_target_pairs={{0,1},{1,0},{2,3},{3,2},{4,5},{5,4},{6,7},{7,6},{8,9},{9,8},{10,11... | collective-permute-start | bytes 3342344 | tf_op jit(solution)/shard_map/ppermute | solution.py:88
  799.7 37.1 %collective-permute-start.46 = (bf16[2,272,1024]{2,1,0:T(8,128)(2,1)S(1)}, bf16[2,272,1024]{2,1,0:T(8,128)(2,1)S(1)}, u32[]{:S(2)}, u32[]{:S(2)}) collective-permute-start(bf16[2,272,1024]{2,1,0:T(8,128)(2,1)S(1)} %add_convert_fusion.2), channel_id=1, source_target_pairs={{0,2},{1,3},{2,0},{3,1},{4,6},{5,7},{6,4},{7,5},{8,10},{9,11},{10,... | collective-permute-start | bytes 3342344 | tf_op jit(solution)/shard_map/ppermute | solution.py:88
  802.5 63.3 %collective-permute-start.54 = (bf16[256,1024]{1,0:T(8,128)(2,1)S(1)}, bf16[256,1024]{1,0:T(8,128)(2,1)S(1)}, u32[]{:S(2)}, u32[]{:S(2)}) collective-permute-start(bf16[256,1024]{1,0:T(8,128)(2,1)S(1)} %fusion.15), channel_id=1, source_target_pairs={{0,4},{1,5},{2,6},{3,7},{4,0},{5,1},{6,2},{7,3},{8,12},{9,13},{10,... | collective-permute-start | bytes 1572872 | tf_op jit(solution)/shard_map/ppermute | solution.py:88
  840.4 50.2 %collective-permute-start.43 = (bf16[256,2048]{1,0:T(8,128)(2,1)}, bf16[256,2048]{1,0:T(8,128)(2,1)}, u32[]{:S(2)}, u32[]{:S(2)}) collective-permute-start(bf16[256,2048]{1,0:T(8,128)(2,1)} %slice_bitcast_fusion.3), channel_id=1, source_target_pairs={{0,16},{8,24},{16,0},{24,8},{1,17},{9,25},{17,1},{25,9},{2,18},{10... | collective-permute-start | bytes 3145736 | tf_op jit(solution)/shard_map/ppermute | solution.py:92
  868.1 41.3 %collective-permute-start.55 = (bf16[256,1024]{1,0:T(8,128)(2,1)}, bf16[256,1024]{1,0:T(8,128)(2,1)}, u32[]{:S(2)}, u32[]{:S(2)}) collective-permute-start(bf16[256,1024]{1,0:T(8,128)(2,1)} %fusion.13.refs_9_), channel_id=1, source_target_pairs={{0,8},{8,0},{16,24},{24,16},{1,9},{9,1},{17,25},{25,17},{2,10},{10... | collective-permute-start | bytes 1572872 | tf_op jit(solution)/shard_map/ppermute | solution.py:92
  868.1 41.2 %collective-permute-start.48 = (bf16[272,1024]{1,0:T(8,128)(2,1)}, bf16[272,1024]{1,0:T(8,128)(2,1)}, u32[]{:S(2)}, u32[]{:S(2)}) collective-permute-start(bf16[272,1024]{1,0:T(8,128)(2,1)} %fusion.10.refs_5_), channel_id=1, source_target_pairs={{0,8},{8,0},{16,24},{24,16},{1,9},{9,1},{17,25},{25,17},{2,10},{10... | collective-permute-start | bytes 1671176 | tf_op jit(solution)/shard_map/ppermute | solution.py:92
  (88 other events, 1917.6 us)
Sparse Core Ops, SparseCore 0:
  9.6 37.1 all-gather.5
  233.5 33.7 all-gather.3
  520.7 72.0 reduce-scatter.3
  595.3 79.7 reduce-scatter.5
  677.5 74.7 reduce-scatter.7

commit v11 on v10

--- a/solution.py
+++ b/solution.py
@@ -205,7 +205,7 @@
 
 def qkv_kernel(count, ids, x_ref, gain_ref, *refs):
     pieces, refs = refs[:count], refs[count:]
-    q_ref, k_ref, v_ref, squares_ref, w_ref, out_ref, h_ref = refs
+    q_ref, k_ref, v_ref, squares_ref, w_ref, h_ref = refs
     shard = pieces[0].shape[0]
     width = q_ref.shape[1]
 
@@ -214,7 +214,6 @@
         for k in range(count):
             rows = block_at(ids, k, shard)
             w_ref[rows, :] = pieces[k][:, : 3 * width]
-            out_ref[rows, :] = pieces[k][:, 3 * width :]
 
     x_rows = x_ref[...].astype(F32)
     scale = lax.rsqrt(jnp.mean(x_rows * x_rows, axis=1, keepdims=True) + EPS)
@@ -226,7 +225,7 @@
     v_ref[...] = product(h_ref[...], w_ref[:, 2 * width :]).astype(BF16)
 
 
-def qkv_project(ids, x_all, gain, pieces):
+def qkv_project(ids, x_all, gain, pieces, after):
     total, depth = x_all.shape
     width = pieces[0].shape[1] // 4
     rows = min(256, total)
@@ -236,60 +235,74 @@
         functools.partial(qkv_kernel, len(pieces)),
         [like((total, width), F32)] * 2
         + [like((total, width), BF16), like((16, total), F32), like((depth, 3 * width), BF16)]
-        + [like((depth, width), BF16), like((total, depth), BF16)],
+        + [like((total, depth), BF16)],
         [x_all, gain, *pieces],
         6 * total * depth * width,
         "qkv_project",
+        after=after,
         scalars=(ids,),
         grid=(total // rows,),
         in_specs=[wide] + [None] * (len(pieces) + 1),
         out_specs=[
-            block, block, block, pl.BlockSpec((16, rows), lambda i, ids: (0, i)), None, None, wide,
+            block, block, block, pl.BlockSpec((16, rows), lambda i, ids: (0, i)), None, wide,
         ],
     )
 
 
-def out_kernel(n_ep, ids, attn_ref, x_ref, gain_ref, *refs):
-    weights, (one_ref, low_ref) = refs[:-2], refs[-2:]
-    width = weights[0].shape[1]
-    for j, weight in enumerate(weights):
+def out_kernel(n_ep, n_sp, ids, attn_ref, x_ref, gain_ref, *refs):
+    weights, (one_ref, low_ref, turned_ref) = refs[: 2 * n_sp], refs[2 * n_sp :]
+    rows, width = weights[0].shape
+    shard = 2 * rows // n_ep
+    for k in range(n_ep):
+        turned_ref[:, k * shard : (k + 1) * shard] = attn_ref[:, block_at(ids, k, shard)]
+    for j in range(n_sp):
         cols = block_at(ids, n_ep + j, width)
-        one_ref[:, cols] = x_ref[:, cols].astype(F32) + product(attn_ref[...], weight[...])
+        one_ref[:, cols] = (
+            x_ref[:, cols].astype(F32)
+            + product(turned_ref[:, :rows], weights[2 * j][...])
+            + product(turned_ref[:, rows:], weights[2 * j + 1][...])
+        )
     one = one_ref[...]
     scale = lax.rsqrt(jnp.mean(one * one, axis=1, keepdims=True) + EPS)
     low_ref[...] = (one * scale * gain_ref[...]).astype(BF16)
 
 
-def out_project(ids, n_ep, attn_tok, tokens, gain, weights, after):
-    return call(
-        functools.partial(out_kernel, n_ep),
+def out_project(ids, n_ep, attn_tok, tokens, gain, weights):
+    return call(
+        functools.partial(out_kernel, n_ep, len(weights) // 2),
         [like(tokens.shape, F32), like(tokens.shape, BF16)],
         [attn_tok, tokens, gain, *weights],
         2 * tokens.size * attn_tok.shape[1],
         "out_project",
-        after=after,
+        scratch=[pltpu.VMEM(attn_tok.shape, BF16)],
         scalars=(ids,),
     )
 
 
-def out_back_kernel(n_ep, ids, d_ref, *refs):
+def out_back_kernel(n_ep, n_sp, ids, d_ref, *refs):
     weights, d_attn_ref = refs[:-1], refs[-1]
-    width = weights[0].shape[1]
-    total = None
-    for j, weight in enumerate(weights):
-        part = product_right(d_ref[:, block_at(ids, n_ep + j, width)], weight[...])
-        total = part if total is None else total + part
-    d_attn_ref[...] = total.astype(BF16)
-
-
-def out_back(ids, n_ep, d_z, weights, after):
-    return call(
-        functools.partial(out_back_kernel, n_ep),
-        like((d_z.shape[0], weights[0].shape[0]), BF16),
+    rows, width = weights[0].shape
+    shard = 2 * rows // n_ep
+    for half in range(2):
+        total = None
+        for j in range(n_sp):
+            part = product_right(
+                d_ref[:, block_at(ids, n_ep + j, width)], weights[2 * j + half][...]
+            )
+            total = part if total is None else total + part
+        total = total.astype(BF16)
+        for k in range(n_ep // 2):
+            block = block_at(ids, half * (n_ep // 2) + k, shard)
+            d_attn_ref[:, block] = total[:, k * shard : (k + 1) * shard]
+
+
+def out_back(ids, n_ep, d_z, weights):
+    return call(
+        functools.partial(out_back_kernel, n_ep, len(weights) // 2),
+        like((d_z.shape[0], 2 * weights[0].shape[0]), BF16),
         [d_z, *weights],
-        2 * d_z.size * weights[0].shape[0],
+        2 * d_z.size * weights[0].shape[0] * 2,
         "out_back",
-        after=after,
         scalars=(ids,),
     )
 
@@ -855,14 +868,19 @@
     sine = jnp.concatenate([-jnp.sin(angles), jnp.sin(angles)], axis=1)
     starts = starts[:, None].astype(jnp.int32)
 
-    q_raw, k_raw, v_low, squares, w_qkv, w_o, h_all = qkv_project(ids, x_all, gains[0:1], w_pieces)
-    squares, w_o = tie(sum_sp(squares), w_o)
-    scales = lax.rsqrt(squares / width + EPS)
-    w_o_over = swap_sp(w_o, 2)
+    w_o = [
+        jnp.concatenate([piece[:, 3 * head_width :] for piece in half])
+        for half in (w_pieces[: n_ep // 2], w_pieces[n_ep // 2 :])
+    ]
+    w_o_over = [swap_sp(half, 2) for half in w_o]
+    q_raw, k_raw, v_low, squares, w_qkv, h_all = qkv_project(
+        ids, x_all, gains[0:1], w_pieces, [places, picked_flat]
+    )
+    scales = lax.rsqrt(sum_sp(squares) / width + EPS)
     gain_q, gain_k = own_columns(gains)[1:2], own_columns(gains)[2:3]
     q_rot, k_rot, mixed = attend(
         q_raw, k_raw, v_low, scales, gain_q, gain_k, cosine, sine, starts,
-        [cot_pieces[k] for k in ((1, 2, 4) if n_ep == 8 else ())],
+        [w_o_over[0]] + [cot_pieces[k] for k in ((1, 2, 4) if n_ep == 8 else ())],
     )
 
     def pair_places(p):
@@ -878,12 +896,17 @@
         return d_rows
 
     if n_ep == 8:
-        cot_pieces[3], cot_pieces[6], mixed = tie(cot_pieces[3], cot_pieces[6], mixed)
+        cot_pieces[3], cot_pieces[6], w_o_over[1], mixed = tie(
+            cot_pieces[3], cot_pieces[6], w_o_over[1], mixed
+        )
     attn_tok = lax.all_to_all(mixed, "sp", split_axis=0, concat_axis=1, tiled=True)
-    w_o_over, attn_tok = tie(w_o_over, attn_tok)
-    w_o_parts = [w_o, swap_sp(w_o, 1), w_o_over, swap_sp(w_o_over, 1)]
+    w_o_parts = (
+        w_o + [swap_sp(half, 1) for half in w_o] + w_o_over + [swap_sp(half, 1) for half in w_o_over]
+    )
+    if n_ep == 8:
+        cot_pieces[5], attn_tok = tie(cot_pieces[5], attn_tok)
     x_one, h2_low = out_project(
-        ids, n_ep, attn_tok, tokens[0], gains[3:4], w_o_parts, []
+        ids, n_ep, attn_tok, tokens[0], gains[3:4], w_o_parts
     )
     attn_all = lax.all_gather(attn_tok, "sp", axis=0, tiled=True)
 
@@ -928,10 +951,13 @@
     d_up_rows = [made[2] for _, _, made in groups]
     ins = [rows for rows, _, _ in groups]
     outs = [d_rows for _, d_rows, _ in groups]
+    d_gates = by_piece(jnp.concatenate(d_gates, axis=0).reshape(n_ep, local, tok_dev))
+    d_gates = lax.all_to_all(d_gates, "ep", split_axis=0, concat_axis=0, tiled=True)
+    d_gates = d_gates.reshape(expert_count, tok_dev)
     mix_stacks = combine_stacks(
         places, [made[4] for _, _, made in groups], n_ep, local, cap, group, d_pieces
     )
-    grad_down = weight_grad(acts, outs, [mix_stacks[0], *d_sums[3:]])
+    grad_down = weight_grad(acts, outs, mix_stacks[:1])
     if n_ep == 8:
         d_sums[2], mix_stacks[2], mix_stacks[3], grad_down = tie(
             d_sums[2], mix_stacks[2], mix_stacks[3], grad_down
@@ -940,13 +966,8 @@
         d_last = [d_far]
     else:
         d_h2, d_last = scatter(d_pieces, n_ep), []
-    d_gates = by_piece(jnp.concatenate(d_gates, axis=0).reshape(n_ep, local, tok_dev))
-    if d_last:
-        d_gates, d_last[0] = tie(d_gates, d_last[0])
-    d_gates = lax.all_to_all(d_gates, "ep", split_axis=0, concat_axis=0, tiled=True)
-    d_gates = d_gates.reshape(expert_count, tok_dev)
-    grad_gate = weight_grad(ins, d_gate_rows, [grad_down, *d_last])
-    grad_up = weight_grad(ins, d_up_rows, [grad_gate, d_gates])
+    grad_gate = weight_grad(ins, d_gate_rows, [grad_down, d_gates, *d_last])
+    grad_up = weight_grad(ins, d_up_rows, [grad_gate])
 
     def over_sp(value):
         return lax.psum_scatter(value, "sp", scatter_dimension=1, tiled=True).astype(F32)
@@ -970,7 +991,7 @@
         d_normed - one_normed * jnp.mean(d_normed * one_normed, axis=-1, keepdims=True)
     )
     d_z, grad_up = tie(d_one.astype(BF16), grad_up)
-    d_attn = out_back(ids, n_ep, d_z, w_o_parts, [])
+    d_attn = out_back(ids, n_ep, d_z, w_o_parts)
     d_heads = lax.all_to_all(d_attn, "sp", split_axis=1, concat_axis=0, tiled=True)
     d_z_cols = lax.all_to_all(d_z, "sp", split_axis=1, concat_axis=0, tiled=True)
     mix, mix_far = scatter_stacks(mix_stacks, n_ep)

time: 939 us -> 870 us (0.927)
  waiting for transfers between devices: 383 us -> 301 us
    all_to_all x1, waiting for transfers between devices: 56.5 us -> 4.72 us  [body(): lax.all_to_all(d_gates, 'ep', split_axis=0, concat_axis=0, tiled=True)]
    all_to_all x1, waiting for transfers between devices: 32 us -> 12 us  [body(): lax.all_to_all(mixed, 'sp', split_axis=0, concat_axis=1, tiled=True)]
    ppermute x2, waiting for transfers between devices: 27.7 us -> 17.9 us  [gather_line(): farther = inner + lax.ppermute(outer, 'ep', OUTWARD)]
    ppermute x14 -> x17, waiting for transfers between devices: 21.4 us -> 21.7 us  [swap_sp(): return lax.ppermute(value, 'sp', [(i, i ^ bits) for i in range(4)])]
  transfers between devices with their start and end apart: 69 -> 72, of which waited for: 25 -> 24; matrix products, arithmetic and copies ran while one was open for 11% -> 13% of each run, Pallas kernels for 34% -> 36%
where the time goes in v11:
time: 870 us; the launch traced here: 859 us
  Pallas kernels  318 us (37%)
  waiting for transfers between devices  301 us (35%)
  starting transfers between devices  91.6 us (11%)
  other arithmetic  74.2 us (9%)
  local copies, waits for them, and re-layouts  40.2 us (5%)
  between operations  31.1 us (4%)
    pallas_call x27, Pallas kernels, call(): pl.pallas_call(kernel, grid_spec=pltpu.PrefetchScalarGridSpec(num_scalar_...  318 us
    ppermute x36, waiting for transfers between devices, swap(): return lax.ppermute(value, 'ep', [(i, i ^ bits) for i in range(8)])  242 us
    ppermute x36, starting transfers between devices, swap(): return lax.ppermute(value, 'ep', [(i, i ^ bits) for i in range(8)])  45.3 us
    ppermute x17, waiting for transfers between devices, swap_sp(): return lax.ppermute(value, 'sp', [(i, i ^ bits) for i in range(4)])  21.7 us
    ppermute x2, waiting for transfers between devices, gather_line(): farther = inner + lax.ppermute(outer, 'ep', OUTWARD)  17.9 us
    convert_element_type x9, other arithmetic, plus(): return (left.astype(F32) + right.astype(F32)).astype(left.dtype)  17.5 us
  transfers between devices with their start and end apart: 72, of which 24 were waited for; matrix products, arithmetic and copies ran while one was open for 13% of the time, Pallas kernels for 36%

profile of v11, /device:TPU:0, one launch (start us, length us, event | category | flops | bytes accessed | tf_op | source)
XLA Modules:
  0.0 859.4 jit_solution(4781260551756299836)
XLA Ops:
  18.1 5.6 all-to-all-start
  23.9 14.4 %collective-permute-done.1.refs_5_ = bf16[256,2048]{1,0:T(8,128)(2,1)} collective-permute-done((bf16[256,2048]{1,0:T(8,128)(2,1)}, bf16[256,2048]{1,0:T(8,128)(2,1)}, u32[]{:S(2)}, u32[]{:S(2)}) %collective-permute-start.1) | collective-permute-done | bytes 1048608 | tf_op jit(solution)/shard_map/ppermute | solution.py:88
  45.6 18.3 %collective-permute-done.2.refs_6_ = bf16[256,2048]{1,0:T(8,128)(2,1)} collective-permute-done((bf16[256,2048]{1,0:T(8,128)(2,1)}, bf16[256,2048]{1,0:T(8,128)(2,1)}, u32[]{:S(2)}, u32[]{:S(2)}) %collective-permute-start.2) | collective-permute-done | bytes 1048608 | tf_op jit(solution)/shard_map/ppermute | solution.py:88
  87.5 6.5 collective-permute-done.5
  107.7 24.2 %collective-permute-done.13.refs_10_ = bf16[256,2048]{1,0:T(8,128)(2,1)} collective-permute-done((bf16[256,2048]{1,0:T(8,128)(2,1)S(1)}, bf16[256,2048]{1,0:T(8,128)(2,1)}, u32[]{:S(2)}, u32[]{:S(2)}) %collective-permute-start.13) | collective-permute-done | bytes 1048608 | tf_op jit(solution)/shard_map/ppermute | solution.py:88
  133.6 16.2 %qkv_project.1 = (f32[1024,512]{1,0:T(8,128)}, f32[1024,512]{1,0:T(8,128)}, bf16[1024,512]{1,0:T(8,128)(2,1)}, f32[16,1024]{1,0:T(8,128)}, bf16[2048,1536]{1,0:T(8,128)(2,1)}, /*index=5*/bf16[1024,2048]{1,0:T(8,128)(2,1)}) custom-call(s32[12]{0:T(128)} %pad_add_fusion.refs_0_.ids, bf16[1024,2048]{1,0:T(8,128)(2,1)} %bitcast.179, f32[1,2048]{1,0:T(1,128)} %bitcast.161, ...), custom_call_target="tpu_custom_call" | custom-call | flops 128849018880 | bytes 28385280 | tf_op jit(solution)/shard_map/qkv_project/pallas_call | solution.py:62
  162.5 6.7 collective-permute-start.10
  171.3 17.2 %attend.1 = (bf16[1024,512]{1,0:T(8,128)(2,1)}, bf16[1024,512]{1,0:T(8,128)(2,1)}, bf16[1024,512]{1,0:T(8,128)(2,1)}) custom-call(f32[1024,512]{1,0:T(8,128)} %get-tuple-element.118.refs_0_.qr_ref.refs_4_, f32[1024,512]{1,0:T(8,128)} %get-tuple-element.119.refs_1_.kr_ref.refs_5_, bf16[1024,512]{1,0:T(8,128)(2,1)} %get-tuple-element.120.refs_2_.v_ref, ...), custom_call_target="tpu_custom_call" | custom-call | flops 32212254720 | bytes 9510912 | tf_op jit(solution)/shard_map/attend/pallas_call | solution.py:62
  188.6 4.3 collective-permute-done.10.refs_1_
  193.0 23.9 %collective-permute-done.9.refs_2_ = bf16[256,2048]{1,0:T(8,128)(2,1)} collective-permute-done((bf16[256,2048]{1,0:T(8,128)(2,1)}, bf16[256,2048]{1,0:T(8,128)(2,1)}, u32[]{:S(2)}, u32[]{:S(2)}) %collective-permute-start.9) | collective-permute-done | bytes 1048608 | tf_op jit(solution)/shard_map/ppermute | solution.py:88
  222.9 12.0 %all-to-all-done.2 = bf16[4,256,512]{2,1,0:T(8,128)(2,1)S(1)} async-done(((bf16[4,256,512]{2,1,0:T(8,128)(2,1)}), bf16[4,256,512]{2,1,0:T(8,128)(2,1)S(1)}, u32[]{:S(2)}, u32[]{:S(2)}) %all-to-all-start.2) | async-done | bytes 1048608 | tf_op jit(solution)/shard_map/all_to_all | solution.py:902
  238.6 9.2 %out_project.1 = (f32[256,2048]{1,0:T(8,128)}, bf16[256,2048]{1,0:T(8,128)(2,1)}) custom-call(s32[12]{0:T(128)} %pad_add_fusion.refs_0_.ids, bf16[256,2048]{1,0:T(8,128)(2,1)} %bitcast.142, bf16[256,2048]{1,0:T(8,128)(2,1)} %bitcast.136, f32[1,2048]{1,0:T(1,128)} %bitcast.156, bf16[1024,512]{1,0:T(8,128)(2,1)} %pad_maximum_fusion.2.refs_0_, ...), custom_call_target="tpu_custom_call" | custom-call | flops 42949672960 | bytes 13639680 | tf_op jit(solution)/shard_map/out_project/pallas_call | solution.py:62
  262.6 9.5 %collective-permute-done.21.refs_0_ = bf16[256,2048]{1,0:T(8,128)(2,1)S(1)} collective-permute-done((bf16[256,2048]{1,0:T(8,128)(2,1)}, bf16[256,2048]{1,0:T(8,128)(2,1)S(1)}, u32[]{:S(2)}, u32[]{:S(2)}) %collective-permute-start.21) | collective-permute-done | bytes 1048608 | tf_op jit(solution)/shard_map/ppermute | solution.py:88
  278.2 6.6 collective-permute-done.23.refs_1_
  284.9 21.1 %collective-permute-done.22.refs_1_ = bf16[256,2048]{1,0:T(8,128)(2,1)} collective-permute-done((bf16[256,2048]{1,0:T(8,128)(2,1)S(1)}, bf16[256,2048]{1,0:T(8,128)(2,1)}, u32[]{:S(2)}, u32[]{:S(2)}) %collective-permute-start.22) | collective-permute-done | bytes 1048608 | tf_op jit(solution)/shard_map/ppermute | solution.py:88
  311.3 4.4 dispatch.8
  315.8 4.4 dispatch.9
  320.2 11.4 %collective-permute-done.28 = bf16[256,2048]{1,0:T(8,128)(2,1)S(1)} collective-permute-done((bf16[256,2048]{1,0:T(8,128)(2,1)S(1)}, bf16[256,2048]{1,0:T(8,128)(2,1)S(1)}, u32[]{:S(2)}, u32[]{:S(2)}) %collective-permute-start.28) | collective-permute-done | bytes 1048608 | tf_op jit(solution)/shard_map/ppermute | solution.py:111
  334.5 42.5 %experts.2 = (bf16[2,576,1024]{2,1,0:T(8,128)(2,1)}, bf16[2,576,1024]{2,1,0:T(8,128)(2,1)}, bf16[2,576,1024]{2,1,0:T(8,128)(2,1)}, f32[2,576,1]{2,1,0:T(8,128)},...) custom-call(bf16[2,576,2048]{2,1,0:T(8,128)(2,1)} %get-tuple-element.133.refs_0_, ...), custom_call_target="tpu_custom_call" | custom-call | flops 579820584960 | bytes 51127296 | tf_op jit(solution)/shard_map/experts/pallas_call | solution.py:62
  377.0 4.5 dispatch.14
  381.5 4.4 dispatch.15
  389.9 4.0 combine.4
  395.9 42.6 %experts.3 = (bf16[2,576,1024]{2,1,0:T(8,128)(2,1)}, bf16[2,576,1024]{2,1,0:T(8,128)(2,1)}, bf16[2,576,1024]{2,1,0:T(8,128)(2,1)}, f32[2,576,1]{2,1,0:T(8,128)},...) custom-call(bf16[2,576,2048]{2,1,0:T(8,128)(2,1)} %get-tuple-element.143.refs_3_.refs_0_.refs_1_, ...), custom_call_target="tpu_custom_call" | custom-call | flops 579820584960 | bytes 51127296 | tf_op jit(solution)/shard_map/experts/pallas_call | solution.py:62
  447.8 4.0 combine.6
  463.6 10.5 %combine_stacks.1 = (bf16[2,256,2048]{2,1,0:T(8,128)(2,1)}, bf16[2,256,2048]{2,1,0:T(8,128)(2,1)}, bf16[2,256,2048]{2,1,0:T(8,128)(2,1)}, bf16[2,256,2048]{2,1,0:T(8,128)(2,1)}) custom-call(s32[16,256]{1,0:T(8,128)} %and_select_fusion.refs_11_.refs_0_, bf16[2,576,2048]{2,1,0:T(8,128)(2,1)} %get-tuple-element.139.refs_1_, ...), custom_call_target="tpu_custom_call" | custom-call | flops 48318382080 | bytes 17842176 | tf_op jit(solution)/shard_map/combine_stacks/pallas_call | solution.py:62
  474.2 18.1 %weight_grad.3.refs_4_ = bf16[2,1024,2048]{2,1,0:T(8,128)(2,1)} custom-call(bf16[2,576,1024]{2,1,0:T(8,128)(2,1)} %get-tuple-element.160.refs_0_, bf16[2,576,1024]{2,1,0:T(8,128)(2,1)} %get-tuple-element.161.refs_1_, bf16[2,576,2048]{2,1,0:T(8,128)(2,1)} %dispatch.11.refs_1_.refs_6_.refs_10_.refs_2_, ...), custom_call_target="tpu_custom_call" | custom-call | flops 193273528320 | bytes 22544384 | tf_op jit(solution)/shard_map/weight_grad/pallas_call | solution.py:62
  492.2 4.7 all-to-all-done.3
  506.2 15.0 %collective-permute-done.38 = bf16[256,2048]{1,0:T(8,128)(2,1)S(1)} collective-permute-done((bf16[256,2048]{1,0:T(8,128)(2,1)S(1)}, bf16[256,2048]{1,0:T(8,128)(2,1)S(1)}, u32[]{:S(2)}, u32[]{:S(2)}) %collective-permute-start.38) | collective-permute-done | bytes 1048608 | tf_op jit(solution)/shard_map/ppermute | solution.py:88
  525.5 18.3 %weight_grad.4.refs_4_ = bf16[2,2048,1024]{2,1,0:T(8,128)(2,1)} custom-call(bf16[2,576,2048]{2,1,0:T(8,128)(2,1)} %get-tuple-element.133.refs_0_, bf16[2,576,2048]{2,1,0:T(8,128)(2,1)} %get-tuple-element.143.refs_3_.refs_0_.refs_1_, bf16[2,576,1024]{2,1,0:T(8,128)(2,1)} %get-tuple-element.175.refs_2_, bf16[2,576,1024]{2,1,0:T(8,128)(2,1)} %get-tuple-element.176.refs_3_, ...), custom_call_target="tpu_custom_call" | custom-call | flops 193273528320 | bytes 22544384 | tf_op jit(solution)/shard_map/weight_grad/pallas_call | solution.py:62
  543.8 18.5 %weight_grad.5 = bf16[2,2048,1024]{2,1,0:T(8,128)(2,1)} custom-call(bf16[2,576,2048]{2,1,0:T(8,128)(2,1)} %get-tuple-element.133.refs_0_, bf16[2,576,2048]{2,1,0:T(8,128)(2,1)} %get-tuple-element.143.refs_3_.refs_0_.refs_1_, bf16[2,576,1024]{2,1,0:T(8,128)(2,1)} %get-tuple-element.173.refs_2_, bf16[2,576,1024]{2,1,0:T(8,128)(2,1)} %get-tuple-element.174.refs_3_, ...), custom_call_target="tpu_custom_call" | custom-call | flops 193273528320 | bytes 22544384 | tf_op jit(solution)/shard_map/weight_grad/pallas_call | solution.py:62
  573.1 7.8 out_back.1
  588.0 4.9 collective-permute-done.34
  592.9 17.9 %collective-permute-done.36 = bf16[2,256,2048]{2,1,0:T(8,128)(2,1)} collective-permute-done((bf16[2,256,2048]{2,1,0:T(8,128)(2,1)}, bf16[2,256,2048]{2,1,0:T(8,128)(2,1)}, u32[]{:S(2)}, u32[]{:S(2)}) %collective-permute-start.36) | collective-permute-done | bytes 2097184 | tf_op jit(solution)/shard_map/ppermute | solution.py:88
  620.5 23.2 %attend_back.1 = (f32[1024,512]{1,0:T(8,128)}, f32[1024,512]{1,0:T(8,128)}, bf16[1024,512]{1,0:T(8,128)(2,1)}, f32[16,1024]{1,0:T(8,128)}, f32[1,512]{1,0:T(1,128)}, /*index=5*/f32[1,512]{1,0:T(1,128)}) custom-call(bf16[1024,512]{1,0:T(8,128)(2,1)} %get-tuple-element.182.q_ref, bf16[1024,512]{1,0:T(8,128)(2,1)} %get-tuple-element.183.k_ref, ...), custom_call_target="tpu_custom_call" | custom-call | flops 75161927680 | bytes 14823424 | tf_op jit(solution)/shard_map/attend_back/pallas_call | solution.py:62
  647.5 10.5 %vo_grads.1 = (bf16[2,256,1024]{2,1,0:T(8,128)(2,1)}, bf16[2,256,1024]{2,1,0:T(8,128)(2,1)}, bf16[2,256,1024]{2,1,0:T(8,128)(2,1)}, bf16[2,256,1024]{2,1,0:T(8,128)(2,1)}) custom-call(s32[12]{0:T(128)} %pad_add_fusion.refs_0_.ids, bf16[1024,2048]{1,0:T(8,128)(2,1)} %get-tuple-element.181.h_ref.refs_1_, bf16[1024,512]{1,0:T(8,128)(2,1)} %get-tuple-element.190.dv_ref, ...), custom_call_target="tpu_custom_call" | custom-call | flops 85899345920 | bytes 14680064 | tf_op jit(solution)/shard_map/vo_grads/pallas_call | solution.py:62
  662.6 12.8 %qk_back.1 = (bf16[2,272,1024]{2,1,0:T(8,128)(2,1)}, bf16[2,272,1024]{2,1,0:T(8,128)(2,1)}, bf16[2,272,1024]{2,1,0:T(8,128)(2,1)}, bf16[2,272,1024]{2,1,0:T(8,128)(2,1)}, bf16[1024,1024]{1,0:T(8,128)(2,1)}) custom-call(s32[12]{0:T(128)} %pad_add_fusion.refs_0_.ids, bf16[1024,2048]{1,0:T(8,128)(2,1)} %get-tuple-element.181.h_ref.refs_1_, ...), custom_call_target="tpu_custom_call" | custom-call | flops 85899345920 | bytes 19423232 | tf_op jit(solution)/shard_map/qk_back/pallas_call | solution.py:62
  676.0 13.9 %d_h.1 = bf16[4,256,2048]{2,1,0:T(8,128)(2,1)} custom-call(s32[12]{0:T(128)} %pad_add_fusion.refs_0_.ids, bf16[1024,1024]{1,0:T(8,128)(2,1)} %get-tuple-element.192.d_ref, bf16[1024,512]{1,0:T(8,128)(2,1)} %get-tuple-element.190.dv_ref, bf16[2048,1536]{1,0:T(8,128)(2,1)} %get-tuple-element.193.w_ref), custom_call_target="tpu_custom_call" | custom-call | flops 128849018880 | bytes 13631488 | tf_op jit(solution)/shard_map/d_h/pallas_call | solution.py:62
  693.9 14.8 %collective-permute-done.41 = bf16[256,2048]{1,0:T(8,128)(2,1)} collective-permute-done((bf16[256,2048]{1,0:T(8,128)(2,1)}, bf16[256,2048]{1,0:T(8,128)(2,1)}, u32[]{:S(2)}, u32[]{:S(2)}) %collective-permute-start.41) | collective-permute-done | bytes 1048608 | tf_op jit(solution)/shard_map/ppermute | solution.py:88
  713.8 16.7 %collective-permute-done.48 = bf16[2,272,1024]{2,1,0:T(8,128)(2,1)S(1)} collective-permute-done((bf16[2,272,1024]{2,1,0:T(8,128)(2,1)}, bf16[2,272,1024]{2,1,0:T(8,128)(2,1)S(1)}, u32[]{:S(2)}, u32[]{:S(2)}) %collective-permute-start.48) | collective-permute-done | bytes 1114144 | tf_op jit(solution)/shard_map/ppermute | solution.py:88
  735.8 17.6 %collective-permute-done.47 = bf16[2,272,1024]{2,1,0:T(8,128)(2,1)S(1)} collective-permute-done((bf16[2,272,1024]{2,1,0:T(8,128)(2,1)S(1)}, bf16[2,272,1024]{2,1,0:T(8,128)(2,1)S(1)}, u32[]{:S(2)}, u32[]{:S(2)}) %collective-permute-start.47) | collective-permute-done | bytes 1114144 | tf_op jit(solution)/shard_map/ppermute | solution.py:88
  753.4 13.5 %collective-permute-done.49 = bf16[2,272,1024]{2,1,0:T(8,128)(2,1)S(1)} collective-permute-done((bf16[2,272,1024]{2,1,0:T(8,128)(2,1)S(1)}, bf16[2,272,1024]{2,1,0:T(8,128)(2,1)S(1)}, u32[]{:S(2)}, u32[]{:S(2)}) %collective-permute-start.49) | collective-permute-done | bytes 1114144 | tf_op jit(solution)/shard_map/ppermute | solution.py:88
  772.4 19.4 %collective-permute-done.50 = bf16[272,1024]{1,0:T(8,128)(2,1)S(1)} collective-permute-done((bf16[272,1024]{1,0:T(8,128)(2,1)S(1)}, bf16[272,1024]{1,0:T(8,128)(2,1)S(1)}, u32[]{:S(2)}, u32[]{:S(2)}) %collective-permute-start.50) | collective-permute-done | bytes 557088 | tf_op jit(solution)/shard_map/ppermute | solution.py:88
  799.0 21.7 %collective-permute-done.59.refs_11_ = bf16[256,1024]{1,0:T(8,128)(2,1)} collective-permute-done((bf16[256,1024]{1,0:T(8,128)(2,1)}, bf16[256,1024]{1,0:T(8,128)(2,1)}, u32[]{:S(2)}, u32[]{:S(2)}) %collective-permute-start.59) | collective-permute-done | bytes 524320 | tf_op jit(solution)/shard_map/ppermute | solution.py:92
  823.5 4.3 fusion.6
  827.8 4.1 convert_element_type.265.refs_13_
  831.9 4.1 convert_element_type.266.refs_14_
  836.0 4.1 convert_element_type.267.refs_15_
  840.0 7.9 finish.1
  (385 shorter events, 205.9 us)
Async XLA Ops:
  7.2 126.5 %all-gather.6.cloned.1.call-start = ((), (), s32[]{:S(2)}) async-start(), calls=%async_computation.13 | async-start | bytes 5242880 | tf_op jit(solution)/shard_map/all_gather | solution.py:839
  18.1 65.6 %all-to-all-start = ((bf16[8,48,256]{2,1,0:T(8,128)(2,1)}), bf16[8,48,256]{2,1,0:T(8,128)(2,1)S(1)}, u32[]{:S(2)}, u32[]{:S(2)}) async-start(bf16[8,48,256]{2,1,0:T(8,128)(2,1)} %broadcast_in_dim.65), calls=%async_computation | async-start | bytes 393216 | tf_op jit(solution)/shard_map/all_to_all | solution.py:827
  44.3 39.6 %collective-permute-start.11 = (bf16[256,2048]{1,0:T(8,128)(2,1)S(1)}, bf16[256,2048]{1,0:T(8,128)(2,1)}, u32[]{:S(2)}, u32[]{:S(2)}) collective-permute-start(bf16[256,2048]{1,0:T(8,128)(2,1)S(1)} %collective-permute-done), channel_id=1, source_target_pairs={{2,0},{3,1},{4,6},{5,7},{10,8},{11,9},{12,14},{13,15},{18,16},{19,... | collective-permute-start | bytes 3145736 | tf_op jit(solution)/shard_map/ppermute | solution.py:110
  85.9 47.7 %collective-permute-start.12 = (bf16[256,2048]{1,0:T(8,128)(2,1)S(1)}, bf16[256,2048]{1,0:T(8,128)(2,1)}, u32[]{:S(2)}, u32[]{:S(2)}) collective-permute-start(bf16[256,2048]{1,0:T(8,128)(2,1)S(1)} %add.173.refs_7_), channel_id=1, source_target_pairs={{0,1},{1,0},{2,3},{3,2},{4,5},{5,4},{6,7},{7,6},{8,9},{9,8},{10,11... | collective-permute-start | bytes 3145736 | tf_op jit(solution)/shard_map/ppermute | solution.py:88
  95.6 36.3 %collective-permute-start.13 = (bf16[256,2048]{1,0:T(8,128)(2,1)S(1)}, bf16[256,2048]{1,0:T(8,128)(2,1)}, u32[]{:S(2)}, u32[]{:S(2)}) collective-permute-start(bf16[256,2048]{1,0:T(8,128)(2,1)S(1)} %add.172.refs_9_), channel_id=1, source_target_pairs={{0,1},{1,0},{2,3},{3,2},{4,5},{5,4},{6,7},{7,6},{8,9},{9,8},{10,11... | collective-permute-start | bytes 3145736 | tf_op jit(solution)/shard_map/ppermute | solution.py:88
  103.3 58.2 %collective-permute-start.15 = (bf16[1024,512]{1,0:T(8,128)(2,1)}, bf16[1024,512]{1,0:T(8,128)(2,1)}, u32[]{:S(2)}, u32[]{:S(2)}) collective-permute-start(bf16[1024,512]{1,0:T(8,128)(2,1)} %pad_maximum_fusion.2.refs_0_), channel_id=1, source_target_pairs={{0,16},{8,24},{16,0},{24,8},{1,17},{9,25},{17,1},{25,9},{2,18},{10... | collective-permute-start | bytes 3145736 | tf_op jit(solution)/shard_map/ppermute | solution.py:92
  104.8 57.7 %collective-permute-start.6 = (bf16[256,2048]{1,0:T(8,128)(2,1)S(1)}, bf16[256,2048]{1,0:T(8,128)(2,1)}, u32[]{:S(2)}, u32[]{:S(2)}) collective-permute-start(bf16[256,2048]{1,0:T(8,128)(2,1)S(1)} %bitcast.138), channel_id=1, source_target_pairs={{0,4},{1,5},{2,6},{3,7},{4,0},{5,1},{6,2},{7,3},{8,12},{9,13},{10,... | collective-permute-start | bytes 3145736 | tf_op jit(solution)/shard_map/ppermute | solution.py:88
  107.1 62.2 %collective-permute-start.8 = (bf16[256,2048]{1,0:T(8,128)(2,1)S(1)}, bf16[256,2048]{1,0:T(8,128)(2,1)}, u32[]{:S(2)}, u32[]{:S(2)}) collective-permute-start(bf16[256,2048]{1,0:T(8,128)(2,1)S(1)} %bitcast.139), channel_id=1, source_target_pairs={{0,2},{1,3},{2,0},{3,1},{4,6},{5,7},{6,4},{7,5},{8,10},{9,11},{10,... | collective-permute-start | bytes 3145736 | tf_op jit(solution)/shard_map/ppermute | solution.py:88
  131.9 38.9 %collective-permute-start.16 = (bf16[256,2048]{1,0:T(8,128)(2,1)S(1)}, bf16[256,2048]{1,0:T(8,128)(2,1)}, u32[]{:S(2)}, u32[]{:S(2)}) collective-permute-start(bf16[256,2048]{1,0:T(8,128)(2,1)S(1)} %bitcast.140), channel_id=1, source_target_pairs={{0,1},{1,0},{2,3},{3,2},{4,5},{5,4},{6,7},{7,6},{8,9},{9,8},{10,11... | collective-permute-start | bytes 3145736 | tf_op jit(solution)/shard_map/ppermute | solution.py:88
  156.5 81.0 %collective-permute-start.17 = (bf16[1024,512]{1,0:T(8,128)(2,1)}, bf16[1024,512]{1,0:T(8,128)(2,1)S(1)}, u32[]{:S(2)}, u32[]{:S(2)}) collective-permute-start(bf16[1024,512]{1,0:T(8,128)(2,1)} %pad_maximum_fusion.2.refs_0_), channel_id=1, source_target_pairs={{0,8},{8,0},{16,24},{24,16},{1,9},{9,1},{17,25},{25,17},{2,10},{10... | collective-permute-start | bytes 3145736 | tf_op jit(solution)/shard_map/ppermute | solution.py:92
  169.3 66.7 %collective-permute-start.7 = (bf16[256,2048]{1,0:T(8,128)(2,1)}, bf16[256,2048]{1,0:T(8,128)(2,1)}, u32[]{:S(2)}, u32[]{:S(2)}) collective-permute-start(bf16[256,2048]{1,0:T(8,128)(2,1)} %collective-permute-done.6.refs_12_.refs_1_), channel_id=1, source_target_pairs={{0,1},{1,0},{2,3},{3,2},{4,5},{5,4},{6,7},{7,6},{8,9},{9,8},{10,11... | collective-permute-start | bytes 3145736 | tf_op jit(solution)/shard_map/ppermute | solution.py:88
  170.8 46.2 %collective-permute-start.9 = (bf16[256,2048]{1,0:T(8,128)(2,1)}, bf16[256,2048]{1,0:T(8,128)(2,1)}, u32[]{:S(2)}, u32[]{:S(2)}) collective-permute-start(bf16[256,2048]{1,0:T(8,128)(2,1)} %collective-permute-done.8.refs_11_.refs_1_), channel_id=1, source_target_pairs={{0,1},{1,0},{2,3},{3,2},{4,5},{5,4},{6,7},{7,6},{8,9},{9,8},{10,11... | collective-permute-start | bytes 3145736 | tf_op jit(solution)/shard_map/ppermute | solution.py:88
  188.6 49.0 %collective-permute-start.19 = (bf16[1024,512]{1,0:T(8,128)(2,1)}, bf16[1024,512]{1,0:T(8,128)(2,1)}, u32[]{:S(2)}, u32[]{:S(2)}) collective-permute-start(bf16[1024,512]{1,0:T(8,128)(2,1)} %collective-permute-done.15.refs_9_.refs_4_), channel_id=1, source_target_pairs={{0,8},{8,0},{16,24},{24,16},{1,9},{9,1},{17,25},{25,17},{2,10},{10... | collective-permute-start | bytes 3145736 | tf_op jit(solution)/shard_map/ppermute | solution.py:92
  193.0 44.6 %collective-permute-start.18 = (bf16[1024,512]{1,0:T(8,128)(2,1)S(1)}, bf16[1024,512]{1,0:T(8,128)(2,1)}, u32[]{:S(2)}, u32[]{:S(2)}) collective-permute-start(bf16[1024,512]{1,0:T(8,128)(2,1)S(1)} %pad_maximum_fusion.1.refs_1_), channel_id=1, source_target_pairs={{0,8},{8,0},{16,24},{24,16},{1,9},{9,1},{17,25},{25,17},{2,10},{10... | collective-permute-start | bytes 3145736 | tf_op jit(solution)/shard_map/ppermute | solution.py:92
  220.4 425.7 %all-gather.4.cloned.1.call-start = ((), (), s32[]{:S(2)}) async-start(), calls=%async_computation.9 | async-start | bytes 5242880 | tf_op jit(solution)/shard_map/all_gather | solution.py:911
  236.0 38.5 %collective-permute-start.25 = (bf16[256,2048]{1,0:T(8,128)(2,1)}, bf16[256,2048]{1,0:T(8,128)(2,1)}, u32[]{:S(2)}, u32[]{:S(2)}) collective-permute-start(bf16[256,2048]{1,0:T(8,128)(2,1)} %collective-permute-done.10.refs_1_), channel_id=1, source_target_pairs={{0,1},{1,0},{2,3},{3,2},{4,5},{5,4},{6,7},{7,6},{8,9},{9,8},{10,11... | collective-permute-start | bytes 3145736 | tf_op jit(solution)/shard_map/ppermute | solution.py:88
  247.8 37.1 %collective-permute-start.23 = (bf16[256,2048]{1,0:T(8,128)(2,1)}, bf16[256,2048]{1,0:T(8,128)(2,1)}, u32[]{:S(2)}, u32[]{:S(2)}) collective-permute-start(bf16[256,2048]{1,0:T(8,128)(2,1)} %get-tuple-element.128.refs_0_), channel_id=1, source_target_pairs={{0,1},{1,0},{2,3},{3,2},{4,5},{5,4},{6,7},{7,6},{8,9},{9,8},{10,11... | collective-permute-start | bytes 3145736 | tf_op jit(solution)/shard_map/ppermute | solution.py:88
  272.1 33.9 %collective-permute-start.22 = (bf16[256,2048]{1,0:T(8,128)(2,1)S(1)}, bf16[256,2048]{1,0:T(8,128)(2,1)}, u32[]{:S(2)}, u32[]{:S(2)}) collective-permute-start(bf16[256,2048]{1,0:T(8,128)(2,1)S(1)} %collective-permute-done.21.refs_0_), channel_id=1, source_target_pairs={{0,1},{1,0},{2,3},{3,2},{4,5},{5,4},{6,7},{7,6},{8,9},{9,8},{10,11... | collective-permute-start | bytes 3145736 | tf_op jit(solution)/shard_map/ppermute | solution.py:88
  272.5 33.5 %collective-permute-start.24 = (bf16[256,2048]{1,0:T(8,128)(2,1)S(1)}, bf16[256,2048]{1,0:T(8,128)(2,1)S(1)}, u32[]{:S(2)}, u32[]{:S(2)}) collective-permute-start(bf16[256,2048]{1,0:T(8,128)(2,1)S(1)} %collective-permute-done.21.refs_0_), channel_id=1, source_target_pairs={{2,4},{3,5},{4,2},{5,3},{10,12},{11,13},{12,10},{13,11},{18,20},{1... | collective-permute-start | bytes 3145736 | tf_op jit(solution)/shard_map/ppermute | solution.py:108
  273.2 34.0 %collective-permute-start.27 = (bf16[256,2048]{1,0:T(8,128)(2,1)S(1)}, bf16[256,2048]{1,0:T(8,128)(2,1)}, u32[]{:S(2)}, u32[]{:S(2)}) collective-permute-start(bf16[256,2048]{1,0:T(8,128)(2,1)S(1)} %collective-permute-done.26), channel_id=1, source_target_pairs={{2,0},{3,1},{4,6},{5,7},{10,8},{11,9},{12,14},{13,15},{18,16},{19,... | collective-permute-start | bytes 3145736 | tf_op jit(solution)/shard_map/ppermute | solution.py:110
  309.9 67.2 %collective-permute-start.30 = (bf16[256,2048]{1,0:T(8,128)(2,1)}, bf16[256,2048]{1,0:T(8,128)(2,1)}, u32[]{:S(2)}, u32[]{:S(2)}) collective-permute-start(bf16[256,2048]{1,0:T(8,128)(2,1)} %add.185.refs_8_.refs_1_.refs_12_), channel_id=1, source_target_pairs={{0,1},{1,0},{2,3},{3,2},{4,5},{5,4},{6,7},{7,6},{8,9},{9,8},{10,11... | collective-permute-start | bytes 3145736 | tf_op jit(solution)/shard_map/ppermute | solution.py:88
  333.0 48.5 %collective-permute-start.29 = (bf16[256,2048]{1,0:T(8,128)(2,1)}, bf16[256,2048]{1,0:T(8,128)(2,1)}, u32[]{:S(2)}, u32[]{:S(2)}) collective-permute-start(bf16[256,2048]{1,0:T(8,128)(2,1)} %add.186.refs_9_.refs_1_.refs_13_), channel_id=1, source_target_pairs={{0,1},{1,0},{2,3},{3,2},{4,5},{5,4},{6,7},{7,6},{8,9},{9,8},{10,11... | collective-permute-start | bytes 3145736 | tf_op jit(solution)/shard_map/ppermute | solution.py:88
  393.9 44.6 %collective-permute-start.32 = (bf16[256,2048]{1,0:T(8,128)(2,1)}, bf16[256,2048]{1,0:T(8,128)(2,1)}, u32[]{:S(2)}, u32[]{:S(2)}) collective-permute-start(bf16[256,2048]{1,0:T(8,128)(2,1)} %get-tuple-element.149.refs_9_.refs_6_), channel_id=1, source_target_pairs={{0,1},{1,0},{2,3},{3,2},{4,5},{5,4},{6,7},{7,6},{8,9},{9,8},{10,11... | collective-permute-start | bytes 3145736 | tf_op jit(solution)/shard_map/ppermute | solution.py:88
  394.4 46.8 %collective-permute-start.31 = (bf16[256,2048]{1,0:T(8,128)(2,1)}, bf16[256,2048]{1,0:T(8,128)(2,1)}, u32[]{:S(2)}, u32[]{:S(2)}) collective-permute-start(bf16[256,2048]{1,0:T(8,128)(2,1)} %get-tuple-element.147.refs_7_.refs_4_), channel_id=1, source_target_pairs={{0,1},{1,0},{2,3},{3,2},{4,5},{5,4},{6,7},{7,6},{8,9},{9,8},{10,11... | collective-permute-start | bytes 3145736 | tf_op jit(solution)/shard_map/ppermute | solution.py:88
  451.8 45.9 %collective-permute-start.37 = (bf16[256,2048]{1,0:T(8,128)(2,1)}, bf16[256,2048]{1,0:T(8,128)(2,1)}, u32[]{:S(2)}, u32[]{:S(2)}) collective-permute-start(bf16[256,2048]{1,0:T(8,128)(2,1)} %get-tuple-element.156.refs_10_), channel_id=1, source_target_pairs={{0,1},{1,0},{2,3},{3,2},{4,5},{5,4},{6,7},{7,6},{8,9},{9,8},{10,11... | collective-permute-start | bytes 3145736 | tf_op jit(solution)/shard_map/ppermute | solution.py:88
  452.4 49.9 %collective-permute-start.33 = (bf16[256,2048]{1,0:T(8,128)(2,1)}, bf16[256,2048]{1,0:T(8,128)(2,1)}, u32[]{:S(2)}, u32[]{:S(2)}) collective-permute-start(bf16[256,2048]{1,0:T(8,128)(2,1)} %get-tuple-element.154.refs_8_), channel_id=1, source_target_pairs={{0,1},{1,0},{2,3},{3,2},{4,5},{5,4},{6,7},{7,6},{8,9},{9,8},{10,11... | collective-permute-start | bytes 3145736 | tf_op jit(solution)/shard_map/ppermute | solution.py:88
  459.2 37.7 %all-to-all-start.3 = ((f32[8,2,256]{2,1,0:T(2,128)}), f32[8,2,256]{2,1,0:T(2,128)}, u32[]{:S(2)}, u32[]{:S(2)}) async-start(f32[8,2,256]{2,1,0:T(2,128)} %constant_dynamic-update-slice_fusion.8), calls=%async_computation.3 | async-start | bytes 32768 | tf_op jit(solution)/shard_map/all_to_all | solution.py:955
  463.2 364.6 %reduce-scatter.4.cloned.1.call-start = ((), (), s32[]{:S(2)}) async-start(), calls=%async_computation.10 | async-start | bytes 10485760 | tf_op jit(solution)/shard_map/reduce_scatter | solution.py:973
  503.9 58.4 %collective-permute-start.35 = (bf16[2,256,2048]{2,1,0:T(8,128)(2,1)}, bf16[2,256,2048]{2,1,0:T(8,128)(2,1)}, u32[]{:S(2)}, u32[]{:S(2)}) collective-permute-start(bf16[2,256,2048]{2,1,0:T(8,128)(2,1)} %get-tuple-element.164), channel_id=1, source_target_pairs={{0,1},{1,0},{2,3},{3,2},{4,5},{5,4},{6,7},{7,6},{8,9},{9,8},{10,11... | collective-permute-start | bytes 6291464 | tf_op jit(solution)/shard_map/ppermute | solution.py:88
  504.5 88.4 %collective-permute-start.34 = (bf16[2,256,2048]{2,1,0:T(8,128)(2,1)}, bf16[2,256,2048]{2,1,0:T(8,128)(2,1)}, u32[]{:S(2)}, u32[]{:S(2)}) collective-permute-start(bf16[2,256,2048]{2,1,0:T(8,128)(2,1)} %get-tuple-element.162), channel_id=1, source_target_pairs={{0,1},{1,0},{2,3},{3,2},{4,5},{5,4},{6,7},{7,6},{8,9},{9,8},{10,11... | collective-permute-start | bytes 6291464 | tf_op jit(solution)/shard_map/ppermute | solution.py:88
  506.0 325.9 %reduce-scatter.6.cloned.1.call-start = ((), (), s32[]{:S(2)}) async-start(), calls=%async_computation.11 | async-start | bytes 10485760 | tf_op jit(solution)/shard_map/reduce_scatter | solution.py:973
  522.6 44.2 %collective-permute-start.39 = (bf16[256,2048]{1,0:T(8,128)(2,1)}, bf16[256,2048]{1,0:T(8,128)(2,1)}, u32[]{:S(2)}, u32[]{:S(2)}) collective-permute-start(bf16[256,2048]{1,0:T(8,128)(2,1)} %add_convert_fusion.8.refs_4_), channel_id=1, source_target_pairs={{0,2},{1,3},{2,0},{3,1},{4,6},{5,7},{6,4},{7,5},{8,10},{9,11},{10,... | collective-permute-start | bytes 3145736 | tf_op jit(solution)/shard_map/ppermute | solution.py:88
  522.6 44.2 %collective-permute-start.40 = (bf16[256,2048]{1,0:T(8,128)(2,1)}, bf16[256,2048]{1,0:T(8,128)(2,1)}, u32[]{:S(2)}, u32[]{:S(2)}) collective-permute-start(bf16[256,2048]{1,0:T(8,128)(2,1)} %add_convert_fusion.5.refs_6_), channel_id=1, source_target_pairs={{0,4},{1,5},{2,6},{3,7},{4,0},{5,1},{6,2},{7,3},{8,12},{9,13},{10,... | collective-permute-start | bytes 3145736 | tf_op jit(solution)/shard_map/ppermute | solution.py:88
  566.2 44.6 %collective-permute-start.36 = (bf16[2,256,2048]{2,1,0:T(8,128)(2,1)}, bf16[2,256,2048]{2,1,0:T(8,128)(2,1)}, u32[]{:S(2)}, u32[]{:S(2)}) collective-permute-start(bf16[2,256,2048]{2,1,0:T(8,128)(2,1)} %add_convert_fusion.1), channel_id=1, source_target_pairs={{0,2},{1,3},{2,0},{3,1},{4,6},{5,7},{6,4},{7,5},{8,10},{9,11},{10,... | collective-permute-start | bytes 6291464 | tf_op jit(solution)/shard_map/ppermute | solution.py:88
  583.3 33.7 %all-to-all-start.4 = ((bf16[256,4,512]{2,0,1:T(8,128)(2,1)}), bf16[256,4,512]{2,0,1:T(8,128)(2,1)S(1)}, u32[]{:S(2)}, u32[]{:S(2)}) async-start(bf16[256,4,512]{2,0,1:T(8,128)(2,1)} %bitcast.135), calls=%async_computation.4 | async-start | bytes 2097152 | tf_op jit(solution)/shard_map/all_to_all | solution.py:995
  586.8 249.1 %reduce-scatter.8.cloned.1.call-start = ((), (), s32[]{:S(2)}) async-start(), calls=%async_computation.12 | async-start | bytes 10485760 | tf_op jit(solution)/shard_map/reduce_scatter | solution.py:973
  658.0 32.0 %collective-permute-start.55 = (bf16[2,256,1024]{2,1,0:T(8,128)(2,1)}, bf16[2,256,1024]{2,1,0:T(8,128)(2,1)}, u32[]{:S(2)}, u32[]{:S(2)}) collective-permute-start(bf16[2,256,1024]{2,1,0:T(8,128)(2,1)} %get-tuple-element.202), channel_id=1, source_target_pairs={{0,1},{1,0},{2,3},{3,2},{4,5},{5,4},{6,7},{7,6},{8,9},{9,8},{10,11... | collective-permute-start | bytes 3145736 | tf_op jit(solution)/shard_map/ppermute | solution.py:88
  658.4 72.9 %collective-permute-start.54 = (bf16[2,256,1024]{2,1,0:T(8,128)(2,1)}, bf16[2,256,1024]{2,1,0:T(8,128)(2,1)}, u32[]{:S(2)}, u32[]{:S(2)}) collective-permute-start(bf16[2,256,1024]{2,1,0:T(8,128)(2,1)} %get-tuple-element.200), channel_id=1, source_target_pairs={{0,1},{1,0},{2,3},{3,2},{4,5},{5,4},{6,7},{7,6},{8,9},{9,8},{10,11... | collective-permute-start | bytes 3145736 | tf_op jit(solution)/shard_map/ppermute | solution.py:88
  660.8 47.8 %collective-permute-start.41 = (bf16[256,2048]{1,0:T(8,128)(2,1)}, bf16[256,2048]{1,0:T(8,128)(2,1)}, u32[]{:S(2)}, u32[]{:S(2)}) collective-permute-start(bf16[256,2048]{1,0:T(8,128)(2,1)} %fusion.11), channel_id=1, source_target_pairs={{0,4},{1,5},{2,6},{3,7},{4,0},{5,1},{6,2},{7,3},{8,12},{9,13},{10,... | collective-permute-start | bytes 3145736 | tf_op jit(solution)/shard_map/ppermute | solution.py:88
  675.4 55.2 %collective-permute-start.48 = (bf16[2,272,1024]{2,1,0:T(8,128)(2,1)}, bf16[2,272,1024]{2,1,0:T(8,128)(2,1)S(1)}, u32[]{:S(2)}, u32[]{:S(2)}) collective-permute-start(bf16[2,272,1024]{2,1,0:T(8,128)(2,1)} %get-tuple-element.199), channel_id=1, source_target_pairs={{0,1},{1,0},{2,3},{3,2},{4,5},{5,4},{6,7},{7,6},{8,9},{9,8},{10,11... | collective-permute-start | bytes 3342344 | tf_op jit(solution)/shard_map/ppermute | solution.py:88
  692.3 39.0 %collective-permute-start.56 = (bf16[2,256,1024]{2,1,0:T(8,128)(2,1)S(1)}, bf16[2,256,1024]{2,1,0:T(8,128)(2,1)S(1)}, u32[]{:S(2)}, u32[]{:S(2)}) collective-permute-start(bf16[2,256,1024]{2,1,0:T(8,128)(2,1)S(1)} %add_convert_fusion.3), channel_id=1, source_target_pairs={{0,2},{1,3},{2,0},{3,1},{4,6},{5,7},{6,4},{7,5},{8,10},{9,11},{10,... | collective-permute-start | bytes 3145736 | tf_op jit(solution)/shard_map/ppermute | solution.py:88
  712.2 55.8 %collective-permute-start.45 = (bf16[2,256,2048]{2,1,0:T(8,128)(2,1)S(1)}, bf16[2,256,2048]{2,1,0:T(8,128)(2,1)S(1)}, u32[]{:S(2)}, u32[]{:S(2)}) collective-permute-start(bf16[2,256,2048]{2,1,0:T(8,128)(2,1)S(1)} %slice.268), channel_id=1, source_target_pairs={{0,8},{8,0},{16,24},{24,16},{1,9},{9,1},{17,25},{25,17},{2,10},{10... | collective-permute-start | bytes 6291464 | tf_op jit(solution)/shard_map/ppermute | solution.py:92
  713.2 40.2 %collective-permute-start.47 = (bf16[2,272,1024]{2,1,0:T(8,128)(2,1)S(1)}, bf16[2,272,1024]{2,1,0:T(8,128)(2,1)S(1)}, u32[]{:S(2)}, u32[]{:S(2)}) collective-permute-start(bf16[2,272,1024]{2,1,0:T(8,128)(2,1)S(1)} %copy-done.59), channel_id=1, source_target_pairs={{0,1},{1,0},{2,3},{3,2},{4,5},{5,4},{6,7},{7,6},{8,9},{9,8},{10,11... | collective-permute-start | bytes 3342344 | tf_op jit(solution)/shard_map/ppermute | solution.py:88
  731.0 35.8 %collective-permute-start.49 = (bf16[2,272,1024]{2,1,0:T(8,128)(2,1)S(1)}, bf16[2,272,1024]{2,1,0:T(8,128)(2,1)S(1)}, u32[]{:S(2)}, u32[]{:S(2)}) collective-permute-start(bf16[2,272,1024]{2,1,0:T(8,128)(2,1)S(1)} %add_convert_fusion.2), channel_id=1, source_target_pairs={{0,2},{1,3},{2,0},{3,1},{4,6},{5,7},{6,4},{7,5},{8,10},{9,11},{10,... | collective-permute-start | bytes 3342344 | tf_op jit(solution)/shard_map/ppermute | solution.py:88
  733.2 63.1 %collective-permute-start.57 = (bf16[256,1024]{1,0:T(8,128)(2,1)S(1)}, bf16[256,1024]{1,0:T(8,128)(2,1)S(1)}, u32[]{:S(2)}, u32[]{:S(2)}) collective-permute-start(bf16[256,1024]{1,0:T(8,128)(2,1)S(1)} %fusion.15), channel_id=1, source_target_pairs={{0,4},{1,5},{2,6},{3,7},{4,0},{5,1},{6,2},{7,3},{8,12},{9,13},{10,... | collective-permute-start | bytes 1572872 | tf_op jit(solution)/shard_map/ppermute | solution.py:88
  770.0 51.2 %collective-permute-start.46 = (bf16[256,2048]{1,0:T(8,128)(2,1)}, bf16[256,2048]{1,0:T(8,128)(2,1)}, u32[]{:S(2)}, u32[]{:S(2)}) collective-permute-start(bf16[256,2048]{1,0:T(8,128)(2,1)} %slice_bitcast_fusion.3), channel_id=1, source_target_pairs={{0,16},{8,24},{16,0},{24,8},{1,17},{9,25},{17,1},{25,9},{2,18},{10... | collective-permute-start | bytes 3145736 | tf_op jit(solution)/shard_map/ppermute | solution.py:92
  798.5 41.6 %collective-permute-start.58 = (bf16[256,1024]{1,0:T(8,128)(2,1)}, bf16[256,1024]{1,0:T(8,128)(2,1)}, u32[]{:S(2)}, u32[]{:S(2)}) collective-permute-start(bf16[256,1024]{1,0:T(8,128)(2,1)} %fusion.13.refs_9_), channel_id=1, source_target_pairs={{0,8},{8,0},{16,24},{24,16},{1,9},{9,1},{17,25},{25,17},{2,10},{10... | collective-permute-start | bytes 1572872 | tf_op jit(solution)/shard_map/ppermute | solution.py:92
  798.5 41.5 %collective-permute-start.51 = (bf16[272,1024]{1,0:T(8,128)(2,1)}, bf16[272,1024]{1,0:T(8,128)(2,1)}, u32[]{:S(2)}, u32[]{:S(2)}) collective-permute-start(bf16[272,1024]{1,0:T(8,128)(2,1)} %fusion.10.refs_5_), channel_id=1, source_target_pairs={{0,8},{8,0},{16,24},{24,16},{1,9},{9,1},{17,25},{25,17},{2,10},{10... | collective-permute-start | bytes 1671176 | tf_op jit(solution)/shard_map/ppermute | solution.py:92
  (91 other events, 1505.9 us)
Sparse Core Ops, SparseCore 0:
  9.6 37.1 all-gather.5
  237.6 32.5 all-gather.3
  506.1 71.0 reduce-scatter.3
  579.9 85.7 reduce-scatter.5
  668.1 71.6 reduce-scatter.7

commit v12 on v11

--- a/solution.py
+++ b/solution.py
@@ -117,8 +117,9 @@
     crossed = swap(held, 1)
     near, far = swap(value, 2), swap(value, 4)
     farther = swap(far, 2)
+    near_x, held = tie(swap(near, 1), far)
     return [
-        value, crossed, near, swap(near, 1), far, swap(far, 1), farther, swap(farther, 1)
+        value, crossed, near, near_x, far, swap(held, 1), farther, swap(farther, 1)
     ], after
 
 
@@ -839,6 +840,19 @@
     x_all = lax.all_gather(tokens[0], "sp", axis=0, tiled=True)
     w_own = jnp.concatenate([own_columns(w) for w in (w_query, w_key, w_value, w_out)], axis=1)
     cot_own = cotangent[0]
+    positions = jnp.arange(total, dtype=jnp.int32)
+    lengths = doc_lengths[0]
+    doc_ends = jnp.cumsum(lengths)
+    starts = jnp.sum(
+        jnp.where(doc_ends[None, :] <= positions[:, None], lengths[None, :], 0), axis=1
+    )
+    half = HEAD_DIM // 2
+    frequency = THETA ** (-(2.0 * jnp.arange(half, dtype=F32)) / HEAD_DIM)
+    angles = (positions - starts).astype(F32)[:, None] * frequency[None, :]
+    cosine = jnp.concatenate([jnp.cos(angles), jnp.cos(angles)], axis=1)
+    sine = jnp.concatenate([-jnp.sin(angles), jnp.sin(angles)], axis=1)
+    starts = starts[:, None].astype(jnp.int32)
+    w_own, cosine, sine, starts, ids = tie(w_own, cosine, sine, starts, ids)
     if n_ep == 8:
         w_pieces = gather_line(w_own)
         w_pieces[6], cot_own = tie(w_pieces[6], cot_own)
@@ -855,18 +869,6 @@
     places = jnp.where((picked_mine > 0) & (earlier < capacity), earlier, -1)
     picked_flat = picked_all.reshape(n_ep * expert_count, tok_dev).astype(F32)
 
-    positions = jnp.arange(total, dtype=jnp.int32)
-    lengths = doc_lengths[0]
-    doc_ends = jnp.cumsum(lengths)
-    starts = jnp.sum(
-        jnp.where(doc_ends[None, :] <= positions[:, None], lengths[None, :], 0), axis=1
-    )
-    half = HEAD_DIM // 2
-    frequency = THETA ** (-(2.0 * jnp.arange(half, dtype=F32)) / HEAD_DIM)
-    angles = (positions - starts).astype(F32)[:, None] * frequency[None, :]
-    cosine = jnp.concatenate([jnp.cos(angles), jnp.cos(angles)], axis=1)
-    sine = jnp.concatenate([-jnp.sin(angles), jnp.sin(angles)], axis=1)
-    starts = starts[:, None].astype(jnp.int32)
 
     w_o = [
         jnp.concatenate([piece[:, 3 * head_width :] for piece in half])
@@ -896,15 +898,13 @@
         return d_rows
 
     if n_ep == 8:
-        cot_pieces[3], cot_pieces[6], w_o_over[1], mixed = tie(
-            cot_pieces[3], cot_pieces[6], w_o_over[1], mixed
-        )
+        cot_pieces[6], w_o_over[1], mixed = tie(cot_pieces[6], w_o_over[1], mixed)
     attn_tok = lax.all_to_all(mixed, "sp", split_axis=0, concat_axis=1, tiled=True)
     w_o_parts = (
         w_o + [swap_sp(half, 1) for half in w_o] + w_o_over + [swap_sp(half, 1) for half in w_o_over]
     )
     if n_ep == 8:
-        cot_pieces[5], attn_tok = tie(cot_pieces[5], attn_tok)
+        cot_pieces[3], attn_tok = tie(cot_pieces[3], attn_tok)
     x_one, h2_low = out_project(
         ids, n_ep, attn_tok, tokens[0], gains[3:4], w_o_parts
     )
@@ -1020,7 +1020,7 @@
     )
     grad_qk = last_hop(*scatter_stacks(qk_stacks, n_ep)).astype(BF16)
 
-    d_h = d_h_rows(ids, n_ep, n_sp, d_qk, d_v, w_qkv, [])
+    d_h = d_h_rows(ids, n_ep, n_sp, d_qk, d_v, w_qkv, [grad_down, grad_gate])
     output, d_h = tie(output, d_h)
     halves = plus(d_h[:2], swap_sp(d_h[2:], 1))
     d_h = halves[0].astype(F32) + swap_sp(halves[1], 2).astype(F32)

time: 870 us -> 843 us (0.969)
  waiting for transfers between devices: 301 us -> 266 us
    ppermute x36, waiting for transfers between devices: 242 us -> 212 us  [swap(): return lax.ppermute(value, 'ep', [(i, i ^ bits) for i in range(8)])]
    ppermute x17, waiting for transfers between devices: 21.7 us -> 12.4 us  [swap_sp(): return lax.ppermute(value, 'sp', [(i, i ^ bits) for i in range(4)])]
  transfers between devices with their start and end apart: 72 -> 72, of which waited for: 24 -> 25; matrix products, arithmetic and copies ran while one was open for 13% -> 13% of each run, Pallas kernels for 36% -> 38%
where the time goes in v12:
time: 843 us; the launch traced here: 833 us
  Pallas kernels  317 us (38%)
  waiting for transfers between devices  266 us (32%)
  starting transfers between devices  95.6 us (11%)
  other arithmetic  76.4 us (9%)
  local copies, waits for them, and re-layouts  42.8 us (5%)
  between operations  31.1 us (4%)
    pallas_call x27, Pallas kernels, call(): pl.pallas_call(kernel, grid_spec=pltpu.PrefetchScalarGridSpec(num_scalar_...  317 us
    ppermute x36, waiting for transfers between devices, swap(): return lax.ppermute(value, 'ep', [(i, i ^ bits) for i in range(8)])  212 us
    ppermute x36, starting transfers between devices, swap(): return lax.ppermute(value, 'ep', [(i, i ^ bits) for i in range(8)])  52 us
    ppermute x2, waiting for transfers between devices, gather_line(): farther = inner + lax.ppermute(outer, 'ep', OUTWARD)  23.8 us
    convert_element_type x9, other arithmetic, plus(): return (left.astype(F32) + right.astype(F32)).astype(left.dtype)  20.8 us
  transfers between devices with their start and end apart: 72, of which 25 were waited for; matrix products, arithmetic and copies ran while one was open for 13% of the time, Pallas kernels for 38%

profile of v12, /device:TPU:0, one launch (start us, length us, event | category | flops | bytes accessed | tf_op | source)
XLA Modules:
  0.0 832.5 jit_solution(17288984916949729403)
XLA Ops:
  21.1 21.0 %collective-permute-done.1.refs_5_ = bf16[256,2048]{1,0:T(8,128)(2,1)} collective-permute-done((bf16[256,2048]{1,0:T(8,128)(2,1)S(1)}, bf16[256,2048]{1,0:T(8,128)(2,1)}, u32[]{:S(2)}, u32[]{:S(2)}) %collective-permute-start.1) | collective-permute-done | bytes 1048608 | tf_op jit(solution)/shard_map/ppermute | solution.py:88
  46.0 5.6 all-to-all-start
  52.9 15.2 %collective-permute-done.2.refs_6_ = bf16[256,2048]{1,0:T(8,128)(2,1)} collective-permute-done((bf16[256,2048]{1,0:T(8,128)(2,1)}, bf16[256,2048]{1,0:T(8,128)(2,1)}, u32[]{:S(2)}, u32[]{:S(2)}) %collective-permute-start.2) | collective-permute-done | bytes 1048608 | tf_op jit(solution)/shard_map/ppermute | solution.py:88
  90.9 11.4 %collective-permute-done.5 = bf16[256,2048]{1,0:T(8,128)(2,1)} collective-permute-done((bf16[256,2048]{1,0:T(8,128)(2,1)S(1)}, bf16[256,2048]{1,0:T(8,128)(2,1)}, u32[]{:S(2)}, u32[]{:S(2)}) %collective-permute-start.5) | collective-permute-done | bytes 1048608 | tf_op jit(solution)/shard_map/ppermute | solution.py:111
  117.2 18.0 %collective-permute-done.12.refs_10_ = bf16[256,2048]{1,0:T(8,128)(2,1)} collective-permute-done((bf16[256,2048]{1,0:T(8,128)(2,1)S(1)}, bf16[256,2048]{1,0:T(8,128)(2,1)}, u32[]{:S(2)}, u32[]{:S(2)}) %collective-permute-start.12) | collective-permute-done | bytes 1048608 | tf_op jit(solution)/shard_map/ppermute | solution.py:88
  136.7 16.3 %qkv_project.1 = (f32[1024,512]{1,0:T(8,128)}, f32[1024,512]{1,0:T(8,128)}, bf16[1024,512]{1,0:T(8,128)(2,1)}, f32[16,1024]{1,0:T(8,128)}, bf16[2048,1536]{1,0:T(8,128)(2,1)}, /*index=5*/bf16[1024,2048]{1,0:T(8,128)(2,1)}) custom-call(s32[12]{0:T(128)} %pad_add_fusion.refs_0_.ids, bf16[1024,2048]{1,0:T(8,128)(2,1)} %bitcast.178, f32[1,2048]{1,0:T(1,128)} %bitcast.160, ...), custom_call_target="tpu_custom_call" | custom-call | flops 128849018880 | bytes 28385280 | tf_op jit(solution)/shard_map/qkv_project/pallas_call | solution.py:62
  166.0 6.2 collective-permute-start.9
  173.7 17.2 %attend.1 = (bf16[1024,512]{1,0:T(8,128)(2,1)}, bf16[1024,512]{1,0:T(8,128)(2,1)}, bf16[1024,512]{1,0:T(8,128)(2,1)}) custom-call(f32[1024,512]{1,0:T(8,128)} %get-tuple-element.127.refs_0_.qr_ref.refs_4_, f32[1024,512]{1,0:T(8,128)} %get-tuple-element.128.refs_1_.kr_ref.refs_5_, bf16[1024,512]{1,0:T(8,128)(2,1)} %get-tuple-element.129.refs_2_.v_ref, ...), custom_call_target="tpu_custom_call" | custom-call | flops 32212254720 | bytes 9510912 | tf_op jit(solution)/shard_map/attend/pallas_call | solution.py:62
  191.0 4.7 collective-permute-done.9.refs_1_
  203.2 10.5 %all-to-all-done.2 = bf16[4,256,512]{2,1,0:T(8,128)(2,1)S(1)} async-done(((bf16[4,256,512]{2,1,0:T(8,128)(2,1)}), bf16[4,256,512]{2,1,0:T(8,128)(2,1)S(1)}, u32[]{:S(2)}, u32[]{:S(2)}) %all-to-all-start.2) | async-done | bytes 1048608 | tf_op jit(solution)/shard_map/all_to_all | solution.py:902
  216.4 9.0 %out_project.1 = (f32[256,2048]{1,0:T(8,128)}, bf16[256,2048]{1,0:T(8,128)(2,1)}) custom-call(s32[12]{0:T(128)} %pad_add_fusion.refs_0_.ids, bf16[256,2048]{1,0:T(8,128)(2,1)} %bitcast.142, bf16[256,2048]{1,0:T(8,128)(2,1)} %bitcast.136, f32[1,2048]{1,0:T(1,128)} %bitcast.155, bf16[1024,512]{1,0:T(8,128)(2,1)} %pad_maximum_fusion.2.refs_0_, ...), custom_call_target="tpu_custom_call" | custom-call | flops 42949672960 | bytes 13639680 | tf_op jit(solution)/shard_map/out_project/pallas_call | solution.py:62
  242.4 7.5 collective-permute-done.20.refs_0_
  256.9 16.0 %collective-permute-done.22.refs_1_ = bf16[256,2048]{1,0:T(8,128)(2,1)} collective-permute-done((bf16[256,2048]{1,0:T(8,128)(2,1)}, bf16[256,2048]{1,0:T(8,128)(2,1)}, u32[]{:S(2)}, u32[]{:S(2)}) %collective-permute-start.22) | collective-permute-done | bytes 1048608 | tf_op jit(solution)/shard_map/ppermute | solution.py:88
  272.9 22.1 %collective-permute-done.21.refs_1_ = bf16[256,2048]{1,0:T(8,128)(2,1)} collective-permute-done((bf16[256,2048]{1,0:T(8,128)(2,1)S(1)}, bf16[256,2048]{1,0:T(8,128)(2,1)}, u32[]{:S(2)}, u32[]{:S(2)}) %collective-permute-start.21) | collective-permute-done | bytes 1048608 | tf_op jit(solution)/shard_map/ppermute | solution.py:88
  300.4 4.5 dispatch.8
  304.8 4.5 dispatch.9
  309.3 12.3 %collective-permute-done.28 = bf16[256,2048]{1,0:T(8,128)(2,1)S(1)} collective-permute-done((bf16[256,2048]{1,0:T(8,128)(2,1)S(1)}, bf16[256,2048]{1,0:T(8,128)(2,1)S(1)}, u32[]{:S(2)}, u32[]{:S(2)}) %collective-permute-start.28) | collective-permute-done | bytes 1048608 | tf_op jit(solution)/shard_map/ppermute | solution.py:111
  324.5 42.5 %experts.2 = (bf16[2,576,1024]{2,1,0:T(8,128)(2,1)}, bf16[2,576,1024]{2,1,0:T(8,128)(2,1)}, bf16[2,576,1024]{2,1,0:T(8,128)(2,1)}, f32[2,576,1]{2,1,0:T(8,128)},...) custom-call(bf16[2,576,2048]{2,1,0:T(8,128)(2,1)} %get-tuple-element.145.refs_0_, ...), custom_call_target="tpu_custom_call" | custom-call | flops 579820584960 | bytes 51127296 | tf_op jit(solution)/shard_map/experts/pallas_call | solution.py:62
  367.0 4.5 dispatch.14
  371.5 4.5 dispatch.15
  379.9 4.0 combine.4
  386.0 42.5 %experts.3 = (bf16[2,576,1024]{2,1,0:T(8,128)(2,1)}, bf16[2,576,1024]{2,1,0:T(8,128)(2,1)}, bf16[2,576,1024]{2,1,0:T(8,128)(2,1)}, f32[2,576,1]{2,1,0:T(8,128)},...) custom-call(bf16[2,576,2048]{2,1,0:T(8,128)(2,1)} %get-tuple-element.155.refs_3_.refs_0_.refs_1_, ...), custom_call_target="tpu_custom_call" | custom-call | flops 579820584960 | bytes 51127296 | tf_op jit(solution)/shard_map/experts/pallas_call | solution.py:62
  433.8 3.9 combine.7
  437.7 4.0 combine.6
  453.5 10.5 %combine_stacks.1 = (bf16[2,256,2048]{2,1,0:T(8,128)(2,1)}, bf16[2,256,2048]{2,1,0:T(8,128)(2,1)}, bf16[2,256,2048]{2,1,0:T(8,128)(2,1)}, bf16[2,256,2048]{2,1,0:T(8,128)(2,1)}) custom-call(s32[16,256]{1,0:T(8,128)} %and_select_fusion.refs_11_.refs_0_, bf16[2,576,2048]{2,1,0:T(8,128)(2,1)} %get-tuple-element.151.refs_1_, ...), custom_call_target="tpu_custom_call" | custom-call | flops 48318382080 | bytes 17842176 | tf_op jit(solution)/shard_map/combine_stacks/pallas_call | solution.py:62
  464.0 18.1 %weight_grad.3.refs_4_ = bf16[2,1024,2048]{2,1,0:T(8,128)(2,1)} custom-call(bf16[2,576,1024]{2,1,0:T(8,128)(2,1)} %get-tuple-element.172.refs_0_, bf16[2,576,1024]{2,1,0:T(8,128)(2,1)} %get-tuple-element.173.refs_1_, bf16[2,576,2048]{2,1,0:T(8,128)(2,1)} %dispatch.11.refs_1_.refs_6_.refs_10_.refs_2_, ...), custom_call_target="tpu_custom_call" | custom-call | flops 193273528320 | bytes 22544384 | tf_op jit(solution)/shard_map/weight_grad/pallas_call | solution.py:62
  482.1 5.7 all-to-all-done.3
  497.2 15.5 %collective-permute-done.38 = bf16[256,2048]{1,0:T(8,128)(2,1)S(1)} collective-permute-done((bf16[256,2048]{1,0:T(8,128)(2,1)S(1)}, bf16[256,2048]{1,0:T(8,128)(2,1)S(1)}, u32[]{:S(2)}, u32[]{:S(2)}) %collective-permute-start.38) | collective-permute-done | bytes 1048608 | tf_op jit(solution)/shard_map/ppermute | solution.py:88
  517.2 18.3 %weight_grad.4.refs_4_ = bf16[2,2048,1024]{2,1,0:T(8,128)(2,1)} custom-call(bf16[2,576,2048]{2,1,0:T(8,128)(2,1)} %get-tuple-element.145.refs_0_, bf16[2,576,2048]{2,1,0:T(8,128)(2,1)} %get-tuple-element.155.refs_3_.refs_0_.refs_1_, bf16[2,576,1024]{2,1,0:T(8,128)(2,1)} %get-tuple-element.187.refs_2_, bf16[2,576,1024]{2,1,0:T(8,128)(2,1)} %get-tuple-element.188.refs_3_, ...), custom_call_target="tpu_custom_call" | custom-call | flops 193273528320 | bytes 22544384 | tf_op jit(solution)/shard_map/weight_grad/pallas_call | solution.py:62
  535.5 18.4 %weight_grad.5 = bf16[2,2048,1024]{2,1,0:T(8,128)(2,1)} custom-call(bf16[2,576,2048]{2,1,0:T(8,128)(2,1)} %get-tuple-element.145.refs_0_, bf16[2,576,2048]{2,1,0:T(8,128)(2,1)} %get-tuple-element.155.refs_3_.refs_0_.refs_1_, bf16[2,576,1024]{2,1,0:T(8,128)(2,1)} %get-tuple-element.185.refs_2_, bf16[2,576,1024]{2,1,0:T(8,128)(2,1)} %get-tuple-element.186.refs_3_, ...), custom_call_target="tpu_custom_call" | custom-call | flops 193273528320 | bytes 22544384 | tf_op jit(solution)/shard_map/weight_grad/pallas_call | solution.py:62
  565.9 7.8 out_back.1
  576.2 4.5 all-to-all-start.4
  584.8 18.4 %collective-permute-done.36 = bf16[2,256,2048]{2,1,0:T(8,128)(2,1)} collective-permute-done((bf16[2,256,2048]{2,1,0:T(8,128)(2,1)}, bf16[2,256,2048]{2,1,0:T(8,128)(2,1)}, u32[]{:S(2)}, u32[]{:S(2)}) %collective-permute-start.36) | collective-permute-done | bytes 2097184 | tf_op jit(solution)/shard_map/ppermute | solution.py:88
  612.9 23.5 %attend_back.1 = (f32[1024,512]{1,0:T(8,128)}, f32[1024,512]{1,0:T(8,128)}, bf16[1024,512]{1,0:T(8,128)(2,1)}, f32[16,1024]{1,0:T(8,128)}, f32[1,512]{1,0:T(1,128)}, /*index=5*/f32[1,512]{1,0:T(1,128)}) custom-call(bf16[1024,512]{1,0:T(8,128)(2,1)} %get-tuple-element.194.q_ref, bf16[1024,512]{1,0:T(8,128)(2,1)} %get-tuple-element.195.k_ref, ...), custom_call_target="tpu_custom_call" | custom-call | flops 75161927680 | bytes 14823424 | tf_op jit(solution)/shard_map/attend_back/pallas_call | solution.py:62
  639.8 10.6 %vo_grads.1 = (bf16[2,256,1024]{2,1,0:T(8,128)(2,1)}, bf16[2,256,1024]{2,1,0:T(8,128)(2,1)}, bf16[2,256,1024]{2,1,0:T(8,128)(2,1)}, bf16[2,256,1024]{2,1,0:T(8,128)(2,1)}) custom-call(s32[12]{0:T(128)} %pad_add_fusion.refs_0_.ids, bf16[1024,2048]{1,0:T(8,128)(2,1)} %get-tuple-element.193.h_ref.refs_1_, bf16[1024,512]{1,0:T(8,128)(2,1)} %get-tuple-element.202.dv_ref.refs_2_, ...), custom_call_target="tpu_custom_call" | custom-call | flops 85899345920 | bytes 14680064 | tf_op jit(solution)/shard_map/vo_grads/pallas_call | solution.py:62
  654.2 12.8 %qk_back.1 = (bf16[2,272,1024]{2,1,0:T(8,128)(2,1)}, bf16[2,272,1024]{2,1,0:T(8,128)(2,1)}, bf16[2,272,1024]{2,1,0:T(8,128)(2,1)}, bf16[2,272,1024]{2,1,0:T(8,128)(2,1)}, bf16[1024,1024]{1,0:T(8,128)(2,1)}) custom-call(s32[12]{0:T(128)} %pad_add_fusion.refs_0_.ids, bf16[1024,2048]{1,0:T(8,128)(2,1)} %get-tuple-element.193.h_ref.refs_1_, ...), custom_call_target="tpu_custom_call" | custom-call | flops 85899345920 | bytes 19423232 | tf_op jit(solution)/shard_map/qk_back/pallas_call | solution.py:62
  670.6 6.1 collective-permute-done.55
  680.7 18.9 %collective-permute-done.41 = bf16[256,2048]{1,0:T(8,128)(2,1)} collective-permute-done((bf16[256,2048]{1,0:T(8,128)(2,1)}, bf16[256,2048]{1,0:T(8,128)(2,1)}, u32[]{:S(2)}, u32[]{:S(2)}) %collective-permute-start.41) | collective-permute-done | bytes 1048608 | tf_op jit(solution)/shard_map/ppermute | solution.py:88
  705.1 4.2 convert_element_type.240.refs_4_.refs_13_
  709.2 4.2 convert_element_type.241.refs_5_.refs_14_
  713.4 12.7 %d_h.1 = bf16[4,256,2048]{2,1,0:T(8,128)(2,1)} custom-call(s32[12]{0:T(128)} %pad_add_fusion.refs_0_.ids, bf16[1024,1024]{1,0:T(8,128)(2,1)} %get-tuple-element.204.refs_1_, bf16[1024,512]{1,0:T(8,128)(2,1)} %get-tuple-element.202.dv_ref.refs_2_, bf16[2048,1536]{1,0:T(8,128)(2,1)} %get-tuple-element.205.refs_3_, ...), custom_call_target="tpu_custom_call" | custom-call | flops 128849018880 | bytes 13631488 | tf_op jit(solution)/shard_map/d_h/pallas_call | solution.py:62
  733.6 12.4 %collective-permute-done.47 = bf16[2,272,1024]{2,1,0:T(8,128)(2,1)S(1)} collective-permute-done((bf16[2,272,1024]{2,1,0:T(8,128)(2,1)}, bf16[2,272,1024]{2,1,0:T(8,128)(2,1)S(1)}, u32[]{:S(2)}, u32[]{:S(2)}) %collective-permute-start.47) | collective-permute-done | bytes 1114144 | tf_op jit(solution)/shard_map/ppermute | solution.py:88
  749.0 20.6 %collective-permute-done.57 = bf16[256,1024]{1,0:T(8,128)(2,1)S(1)} collective-permute-done((bf16[256,1024]{1,0:T(8,128)(2,1)S(1)}, bf16[256,1024]{1,0:T(8,128)(2,1)S(1)}, u32[]{:S(2)}, u32[]{:S(2)}) %collective-permute-start.57) | collective-permute-done | bytes 524320 | tf_op jit(solution)/shard_map/ppermute | solution.py:88
  771.3 10.0 %collective-permute-done.50 = bf16[272,1024]{1,0:T(8,128)(2,1)S(1)} collective-permute-done((bf16[272,1024]{1,0:T(8,128)(2,1)S(1)}, bf16[272,1024]{1,0:T(8,128)(2,1)S(1)}, u32[]{:S(2)}, u32[]{:S(2)}) %collective-permute-start.50) | collective-permute-done | bytes 557088 | tf_op jit(solution)/shard_map/ppermute | solution.py:88
  786.9 10.1 %collective-permute-done.52.refs_7_ = bf16[272,1024]{1,0:T(8,128)(2,1)S(1)} collective-permute-done((bf16[272,1024]{1,0:T(8,128)(2,1)S(1)}, bf16[272,1024]{1,0:T(8,128)(2,1)S(1)}, u32[]{:S(2)}, u32[]{:S(2)}) %collective-permute-start.52) | collective-permute-done | bytes 557088 | tf_op jit(solution)/shard_map/ppermute | solution.py:92
  798.7 4.1 convert_element_type.267.refs_15_
  803.7 7.9 finish.1
  820.7 4.9 fusion.6
  (390 shorter events, 213.4 us)
Async XLA Ops:
  7.2 129.5 %all-gather.6.cloned.1.call-start = ((), (), s32[]{:S(2)}) async-start(), calls=%async_computation.13 | async-start | bytes 5242880 | tf_op jit(solution)/shard_map/all_gather | solution.py:840
  18.8 32.8 %collective-permute-start = (bf16[256,2048]{1,0:T(8,128)(2,1)S(1)}, bf16[256,2048]{1,0:T(8,128)(2,1)S(1)}, u32[]{:S(2)}, u32[]{:S(2)}) collective-permute-start(bf16[256,2048]{1,0:T(8,128)(2,1)S(1)} %pad_maximum_fusion.refs_3_), channel_id=1, source_target_pairs={{2,4},{3,5},{4,2},{5,3},{10,12},{11,13},{12,10},{13,11},{18,20},{1... | collective-permute-start | bytes 3145736 | tf_op jit(solution)/shard_map/ppermute | solution.py:107
  19.5 33.4 %collective-permute-start.3 = (bf16[256,2048]{1,0:T(8,128)(2,1)S(1)}, bf16[256,2048]{1,0:T(8,128)(2,1)}, u32[]{:S(2)}, u32[]{:S(2)}) collective-permute-start(bf16[256,2048]{1,0:T(8,128)(2,1)S(1)} %pad_maximum_fusion.refs_3_), channel_id=1, source_target_pairs={{0,1},{1,0},{2,3},{3,2},{4,5},{5,4},{6,7},{7,6},{8,9},{9,8},{10,11... | collective-permute-start | bytes 3145736 | tf_op jit(solution)/shard_map/ppermute | solution.py:88
  46.0 40.6 %all-to-all-start = ((bf16[8,48,256]{2,1,0:T(8,128)(2,1)}), bf16[8,48,256]{2,1,0:T(8,128)(2,1)}, u32[]{:S(2)}, u32[]{:S(2)}) async-start(bf16[8,48,256]{2,1,0:T(8,128)(2,1)} %broadcast_in_dim.68), calls=%async_computation | async-start | bytes 393216 | tf_op jit(solution)/shard_map/all_to_all | solution.py:828
  51.6 36.0 %collective-permute-start.10 = (bf16[256,2048]{1,0:T(8,128)(2,1)S(1)}, bf16[256,2048]{1,0:T(8,128)(2,1)}, u32[]{:S(2)}, u32[]{:S(2)}) collective-permute-start(bf16[256,2048]{1,0:T(8,128)(2,1)S(1)} %collective-permute-done), channel_id=1, source_target_pairs={{2,0},{3,1},{4,6},{5,7},{10,8},{11,9},{12,14},{13,15},{18,16},{19,... | collective-permute-start | bytes 3145736 | tf_op jit(solution)/shard_map/ppermute | solution.py:110
  68.1 34.3 %collective-permute-start.5 = (bf16[256,2048]{1,0:T(8,128)(2,1)S(1)}, bf16[256,2048]{1,0:T(8,128)(2,1)}, u32[]{:S(2)}, u32[]{:S(2)}) collective-permute-start(bf16[256,2048]{1,0:T(8,128)(2,1)S(1)} %collective-permute-done.4), channel_id=1, source_target_pairs={{2,0},{3,1},{4,6},{5,7},{10,8},{11,9},{12,14},{13,15},{18,16},{19,... | collective-permute-start | bytes 3145736 | tf_op jit(solution)/shard_map/ppermute | solution.py:111
  89.3 47.4 %collective-permute-start.11 = (bf16[256,2048]{1,0:T(8,128)(2,1)S(1)}, bf16[256,2048]{1,0:T(8,128)(2,1)}, u32[]{:S(2)}, u32[]{:S(2)}) collective-permute-start(bf16[256,2048]{1,0:T(8,128)(2,1)S(1)} %add.173.refs_7_), channel_id=1, source_target_pairs={{0,1},{1,0},{2,3},{3,2},{4,5},{5,4},{6,7},{7,6},{8,9},{9,8},{10,11... | collective-permute-start | bytes 3145736 | tf_op jit(solution)/shard_map/ppermute | solution.py:88
  104.0 31.2 %collective-permute-start.12 = (bf16[256,2048]{1,0:T(8,128)(2,1)S(1)}, bf16[256,2048]{1,0:T(8,128)(2,1)}, u32[]{:S(2)}, u32[]{:S(2)}) collective-permute-start(bf16[256,2048]{1,0:T(8,128)(2,1)S(1)} %add.172.refs_9_), channel_id=1, source_target_pairs={{0,1},{1,0},{2,3},{3,2},{4,5},{5,4},{6,7},{7,6},{8,9},{9,8},{10,11... | collective-permute-start | bytes 3145736 | tf_op jit(solution)/shard_map/ppermute | solution.py:88
  112.4 49.7 %collective-permute-start.14 = (bf16[1024,512]{1,0:T(8,128)(2,1)}, bf16[1024,512]{1,0:T(8,128)(2,1)}, u32[]{:S(2)}, u32[]{:S(2)}) collective-permute-start(bf16[1024,512]{1,0:T(8,128)(2,1)} %pad_maximum_fusion.2.refs_0_), channel_id=1, source_target_pairs={{0,16},{8,24},{16,0},{24,8},{1,17},{9,25},{17,1},{25,9},{2,18},{10... | collective-permute-start | bytes 3145736 | tf_op jit(solution)/shard_map/ppermute | solution.py:92
  113.9 50.7 %collective-permute-start.8 = (bf16[256,2048]{1,0:T(8,128)(2,1)S(1)}, bf16[256,2048]{1,0:T(8,128)(2,1)}, u32[]{:S(2)}, u32[]{:S(2)}) collective-permute-start(bf16[256,2048]{1,0:T(8,128)(2,1)S(1)} %bitcast.138), channel_id=1, source_target_pairs={{0,4},{1,5},{2,6},{3,7},{4,0},{5,1},{6,2},{7,3},{8,12},{9,13},{10,... | collective-permute-start | bytes 3145736 | tf_op jit(solution)/shard_map/ppermute | solution.py:88
  114.6 51.4 %collective-permute-start.6 = (bf16[256,2048]{1,0:T(8,128)(2,1)S(1)}, bf16[256,2048]{1,0:T(8,128)(2,1)}, u32[]{:S(2)}, u32[]{:S(2)}) collective-permute-start(bf16[256,2048]{1,0:T(8,128)(2,1)S(1)} %bitcast.139), channel_id=1, source_target_pairs={{0,2},{1,3},{2,0},{3,1},{4,6},{5,7},{6,4},{7,5},{8,10},{9,11},{10,... | collective-permute-start | bytes 3145736 | tf_op jit(solution)/shard_map/ppermute | solution.py:88
  135.2 37.0 %collective-permute-start.15 = (bf16[256,2048]{1,0:T(8,128)(2,1)S(1)}, bf16[256,2048]{1,0:T(8,128)(2,1)}, u32[]{:S(2)}, u32[]{:S(2)}) collective-permute-start(bf16[256,2048]{1,0:T(8,128)(2,1)S(1)} %bitcast.140), channel_id=1, source_target_pairs={{0,1},{1,0},{2,3},{3,2},{4,5},{5,4},{6,7},{7,6},{8,9},{9,8},{10,11... | collective-permute-start | bytes 3145736 | tf_op jit(solution)/shard_map/ppermute | solution.py:88
  159.6 55.2 %collective-permute-start.16 = (bf16[1024,512]{1,0:T(8,128)(2,1)}, bf16[1024,512]{1,0:T(8,128)(2,1)S(1)}, u32[]{:S(2)}, u32[]{:S(2)}) collective-permute-start(bf16[1024,512]{1,0:T(8,128)(2,1)} %pad_maximum_fusion.2.refs_0_), channel_id=1, source_target_pairs={{0,8},{8,0},{16,24},{24,16},{1,9},{9,1},{17,25},{25,17},{2,10},{10... | collective-permute-start | bytes 3145736 | tf_op jit(solution)/shard_map/ppermute | solution.py:92
  162.1 54.3 %collective-permute-start.18 = (bf16[1024,512]{1,0:T(8,128)(2,1)}, bf16[1024,512]{1,0:T(8,128)(2,1)}, u32[]{:S(2)}, u32[]{:S(2)}) collective-permute-start(bf16[1024,512]{1,0:T(8,128)(2,1)} %collective-permute-done.14.refs_9_.refs_4_), channel_id=1, source_target_pairs={{0,8},{8,0},{16,24},{24,16},{1,9},{9,1},{17,25},{25,17},{2,10},{10... | collective-permute-start | bytes 3145736 | tf_op jit(solution)/shard_map/ppermute | solution.py:92
  166.0 29.7 %collective-permute-start.9 = (bf16[256,2048]{1,0:T(8,128)(2,1)}, bf16[256,2048]{1,0:T(8,128)(2,1)}, u32[]{:S(2)}, u32[]{:S(2)}) collective-permute-start(bf16[256,2048]{1,0:T(8,128)(2,1)} %collective-permute-done.8.refs_12_.refs_1_), channel_id=1, source_target_pairs={{0,2},{1,3},{2,0},{3,1},{4,6},{5,7},{6,4},{7,5},{8,10},{9,11},{10,... | collective-permute-start | bytes 3145736 | tf_op jit(solution)/shard_map/ppermute | solution.py:88
  199.2 439.1 %all-gather.4.cloned.1.call-start = ((), (), s32[]{:S(2)}) async-start(), calls=%async_computation.9 | async-start | bytes 5242880 | tf_op jit(solution)/shard_map/all_gather | solution.py:911
  201.7 33.1 %collective-permute-start.25 = (bf16[256,2048]{1,0:T(8,128)(2,1)}, bf16[256,2048]{1,0:T(8,128)(2,1)}, u32[]{:S(2)}, u32[]{:S(2)}) collective-permute-start(bf16[256,2048]{1,0:T(8,128)(2,1)} %collective-permute-done.8.refs_12_.refs_1_), channel_id=1, source_target_pairs={{0,1},{1,0},{2,3},{3,2},{4,5},{5,4},{6,7},{7,6},{8,9},{9,8},{10,11... | collective-permute-start | bytes 3145736 | tf_op jit(solution)/shard_map/ppermute | solution.py:88
  214.8 38.3 %collective-permute-start.24 = (bf16[256,2048]{1,0:T(8,128)(2,1)}, bf16[256,2048]{1,0:T(8,128)(2,1)}, u32[]{:S(2)}, u32[]{:S(2)}) collective-permute-start(bf16[256,2048]{1,0:T(8,128)(2,1)} %collective-permute-done.9.refs_1_), channel_id=1, source_target_pairs={{0,1},{1,0},{2,3},{3,2},{4,5},{5,4},{6,7},{7,6},{8,9},{9,8},{10,11... | collective-permute-start | bytes 3145736 | tf_op jit(solution)/shard_map/ppermute | solution.py:88
  227.1 45.8 %collective-permute-start.22 = (bf16[256,2048]{1,0:T(8,128)(2,1)}, bf16[256,2048]{1,0:T(8,128)(2,1)}, u32[]{:S(2)}, u32[]{:S(2)}) collective-permute-start(bf16[256,2048]{1,0:T(8,128)(2,1)} %get-tuple-element.140.refs_0_), channel_id=1, source_target_pairs={{0,1},{1,0},{2,3},{3,2},{4,5},{5,4},{6,7},{7,6},{8,9},{9,8},{10,11... | collective-permute-start | bytes 3145736 | tf_op jit(solution)/shard_map/ppermute | solution.py:88
  249.9 45.1 %collective-permute-start.21 = (bf16[256,2048]{1,0:T(8,128)(2,1)S(1)}, bf16[256,2048]{1,0:T(8,128)(2,1)}, u32[]{:S(2)}, u32[]{:S(2)}) collective-permute-start(bf16[256,2048]{1,0:T(8,128)(2,1)S(1)} %collective-permute-done.20.refs_0_), channel_id=1, source_target_pairs={{0,1},{1,0},{2,3},{3,2},{4,5},{5,4},{6,7},{7,6},{8,9},{9,8},{10,11... | collective-permute-start | bytes 3145736 | tf_op jit(solution)/shard_map/ppermute | solution.py:88
  251.1 43.8 %collective-permute-start.23 = (bf16[256,2048]{1,0:T(8,128)(2,1)S(1)}, bf16[256,2048]{1,0:T(8,128)(2,1)S(1)}, u32[]{:S(2)}, u32[]{:S(2)}) collective-permute-start(bf16[256,2048]{1,0:T(8,128)(2,1)S(1)} %collective-permute-done.20.refs_0_), channel_id=1, source_target_pairs={{2,4},{3,5},{4,2},{5,3},{10,12},{11,13},{12,10},{13,11},{18,20},{1... | collective-permute-start | bytes 3145736 | tf_op jit(solution)/shard_map/ppermute | solution.py:108
  251.9 44.4 %collective-permute-start.27 = (bf16[256,2048]{1,0:T(8,128)(2,1)S(1)}, bf16[256,2048]{1,0:T(8,128)(2,1)}, u32[]{:S(2)}, u32[]{:S(2)}) collective-permute-start(bf16[256,2048]{1,0:T(8,128)(2,1)S(1)} %collective-permute-done.26), channel_id=1, source_target_pairs={{2,0},{3,1},{4,6},{5,7},{10,8},{11,9},{12,14},{13,15},{18,16},{19,... | collective-permute-start | bytes 3145736 | tf_op jit(solution)/shard_map/ppermute | solution.py:110
  298.9 68.1 %collective-permute-start.30 = (bf16[256,2048]{1,0:T(8,128)(2,1)}, bf16[256,2048]{1,0:T(8,128)(2,1)}, u32[]{:S(2)}, u32[]{:S(2)}) collective-permute-start(bf16[256,2048]{1,0:T(8,128)(2,1)} %add.185.refs_8_.refs_1_.refs_12_), channel_id=1, source_target_pairs={{0,1},{1,0},{2,3},{3,2},{4,5},{5,4},{6,7},{7,6},{8,9},{9,8},{10,11... | collective-permute-start | bytes 3145736 | tf_op jit(solution)/shard_map/ppermute | solution.py:88
  323.0 48.5 %collective-permute-start.29 = (bf16[256,2048]{1,0:T(8,128)(2,1)}, bf16[256,2048]{1,0:T(8,128)(2,1)}, u32[]{:S(2)}, u32[]{:S(2)}) collective-permute-start(bf16[256,2048]{1,0:T(8,128)(2,1)} %add.186.refs_9_.refs_1_.refs_13_), channel_id=1, source_target_pairs={{0,1},{1,0},{2,3},{3,2},{4,5},{5,4},{6,7},{7,6},{8,9},{9,8},{10,11... | collective-permute-start | bytes 3145736 | tf_op jit(solution)/shard_map/ppermute | solution.py:88
  383.9 44.6 %collective-permute-start.32 = (bf16[256,2048]{1,0:T(8,128)(2,1)}, bf16[256,2048]{1,0:T(8,128)(2,1)}, u32[]{:S(2)}, u32[]{:S(2)}) collective-permute-start(bf16[256,2048]{1,0:T(8,128)(2,1)} %get-tuple-element.161.refs_9_.refs_6_), channel_id=1, source_target_pairs={{0,1},{1,0},{2,3},{3,2},{4,5},{5,4},{6,7},{7,6},{8,9},{9,8},{10,11... | collective-permute-start | bytes 3145736 | tf_op jit(solution)/shard_map/ppermute | solution.py:88
  384.5 46.7 %collective-permute-start.31 = (bf16[256,2048]{1,0:T(8,128)(2,1)}, bf16[256,2048]{1,0:T(8,128)(2,1)}, u32[]{:S(2)}, u32[]{:S(2)}) collective-permute-start(bf16[256,2048]{1,0:T(8,128)(2,1)} %get-tuple-element.159.refs_7_.refs_4_), channel_id=1, source_target_pairs={{0,1},{1,0},{2,3},{3,2},{4,5},{5,4},{6,7},{7,6},{8,9},{9,8},{10,11... | collective-permute-start | bytes 3145736 | tf_op jit(solution)/shard_map/ppermute | solution.py:88
  441.8 46.9 %collective-permute-start.37 = (bf16[256,2048]{1,0:T(8,128)(2,1)}, bf16[256,2048]{1,0:T(8,128)(2,1)}, u32[]{:S(2)}, u32[]{:S(2)}) collective-permute-start(bf16[256,2048]{1,0:T(8,128)(2,1)} %get-tuple-element.168.refs_10_), channel_id=1, source_target_pairs={{0,1},{1,0},{2,3},{3,2},{4,5},{5,4},{6,7},{7,6},{8,9},{9,8},{10,11... | collective-permute-start | bytes 3145736 | tf_op jit(solution)/shard_map/ppermute | solution.py:88
  442.3 50.9 %collective-permute-start.33 = (bf16[256,2048]{1,0:T(8,128)(2,1)}, bf16[256,2048]{1,0:T(8,128)(2,1)}, u32[]{:S(2)}, u32[]{:S(2)}) collective-permute-start(bf16[256,2048]{1,0:T(8,128)(2,1)} %get-tuple-element.166.refs_8_), channel_id=1, source_target_pairs={{0,1},{1,0},{2,3},{3,2},{4,5},{5,4},{6,7},{7,6},{8,9},{9,8},{10,11... | collective-permute-start | bytes 3145736 | tf_op jit(solution)/shard_map/ppermute | solution.py:88
  449.2 38.7 %all-to-all-start.3 = ((f32[8,2,256]{2,1,0:T(2,128)}), f32[8,2,256]{2,1,0:T(2,128)}, u32[]{:S(2)}, u32[]{:S(2)}) async-start(f32[8,2,256]{2,1,0:T(2,128)} %constant_dynamic-update-slice_fusion.8), calls=%async_computation.3 | async-start | bytes 32768 | tf_op jit(solution)/shard_map/all_to_all | solution.py:955
  453.1 252.0 %reduce-scatter.4.cloned.1.call-start = ((), (), s32[]{:S(2)}) async-start(), calls=%async_computation.10 | async-start | bytes 10485760 | tf_op jit(solution)/shard_map/reduce_scatter | solution.py:973
  494.8 59.1 %collective-permute-start.35 = (bf16[2,256,2048]{2,1,0:T(8,128)(2,1)}, bf16[2,256,2048]{2,1,0:T(8,128)(2,1)}, u32[]{:S(2)}, u32[]{:S(2)}) collective-permute-start(bf16[2,256,2048]{2,1,0:T(8,128)(2,1)} %get-tuple-element.176), channel_id=1, source_target_pairs={{0,1},{1,0},{2,3},{3,2},{4,5},{5,4},{6,7},{7,6},{8,9},{9,8},{10,11... | collective-permute-start | bytes 6291464 | tf_op jit(solution)/shard_map/ppermute | solution.py:88
  495.4 89.4 %collective-permute-start.34 = (bf16[2,256,2048]{2,1,0:T(8,128)(2,1)}, bf16[2,256,2048]{2,1,0:T(8,128)(2,1)}, u32[]{:S(2)}, u32[]{:S(2)}) collective-permute-start(bf16[2,256,2048]{2,1,0:T(8,128)(2,1)} %get-tuple-element.174), channel_id=1, source_target_pairs={{0,1},{1,0},{2,3},{3,2},{4,5},{5,4},{6,7},{7,6},{8,9},{9,8},{10,11... | collective-permute-start | bytes 6291464 | tf_op jit(solution)/shard_map/ppermute | solution.py:88
  496.9 212.3 %reduce-scatter.6.cloned.1.call-start = ((), (), s32[]{:S(2)}) async-start(), calls=%async_computation.11 | async-start | bytes 10485760 | tf_op jit(solution)/shard_map/reduce_scatter | solution.py:973
  514.1 45.5 %collective-permute-start.39 = (bf16[256,2048]{1,0:T(8,128)(2,1)}, bf16[256,2048]{1,0:T(8,128)(2,1)}, u32[]{:S(2)}, u32[]{:S(2)}) collective-permute-start(bf16[256,2048]{1,0:T(8,128)(2,1)} %add_convert_fusion.8.refs_4_), channel_id=1, source_target_pairs={{0,2},{1,3},{2,0},{3,1},{4,6},{5,7},{6,4},{7,5},{8,10},{9,11},{10,... | collective-permute-start | bytes 3145736 | tf_op jit(solution)/shard_map/ppermute | solution.py:88
  514.4 45.3 %collective-permute-start.40 = (bf16[256,2048]{1,0:T(8,128)(2,1)}, bf16[256,2048]{1,0:T(8,128)(2,1)}, u32[]{:S(2)}, u32[]{:S(2)}) collective-permute-start(bf16[256,2048]{1,0:T(8,128)(2,1)} %add_convert_fusion.5.refs_6_), channel_id=1, source_target_pairs={{0,4},{1,5},{2,6},{3,7},{4,0},{5,1},{6,2},{7,3},{8,12},{9,13},{10,... | collective-permute-start | bytes 3145736 | tf_op jit(solution)/shard_map/ppermute | solution.py:88
  557.8 45.4 %collective-permute-start.36 = (bf16[2,256,2048]{2,1,0:T(8,128)(2,1)}, bf16[2,256,2048]{2,1,0:T(8,128)(2,1)}, u32[]{:S(2)}, u32[]{:S(2)}) collective-permute-start(bf16[2,256,2048]{2,1,0:T(8,128)(2,1)} %add_convert_fusion.1), channel_id=1, source_target_pairs={{0,2},{1,3},{2,0},{3,1},{4,6},{5,7},{6,4},{7,5},{8,10},{9,11},{10,... | collective-permute-start | bytes 6291464 | tf_op jit(solution)/shard_map/ppermute | solution.py:88
  576.2 33.1 %all-to-all-start.4 = ((bf16[256,4,512]{2,0,1:T(8,128)(2,1)}), bf16[256,4,512]{2,0,1:T(8,128)(2,1)}, u32[]{:S(2)}, u32[]{:S(2)}) async-start(bf16[256,4,512]{2,0,1:T(8,128)(2,1)} %bitcast.135), calls=%async_computation.4 | async-start | bytes 2097152 | tf_op jit(solution)/shard_map/all_to_all | solution.py:995
  612.8 185.9 %reduce-scatter.8.cloned.1.call-start = ((), (), s32[]{:S(2)}) async-start(), calls=%async_computation.12 | async-start | bytes 10485760 | tf_op jit(solution)/shard_map/reduce_scatter | solution.py:973
  651.1 48.6 %collective-permute-start.41 = (bf16[256,2048]{1,0:T(8,128)(2,1)}, bf16[256,2048]{1,0:T(8,128)(2,1)}, u32[]{:S(2)}, u32[]{:S(2)}) collective-permute-start(bf16[256,2048]{1,0:T(8,128)(2,1)} %fusion.11), channel_id=1, source_target_pairs={{0,4},{1,5},{2,6},{3,7},{4,0},{5,1},{6,2},{7,3},{8,12},{9,13},{10,... | collective-permute-start | bytes 3145736 | tf_op jit(solution)/shard_map/ppermute | solution.py:88
  667.0 35.4 %collective-permute-start.48 = (bf16[2,272,1024]{2,1,0:T(8,128)(2,1)}, bf16[2,272,1024]{2,1,0:T(8,128)(2,1)}, u32[]{:S(2)}, u32[]{:S(2)}) collective-permute-start(bf16[2,272,1024]{2,1,0:T(8,128)(2,1)} %get-tuple-element.211), channel_id=1, source_target_pairs={{0,1},{1,0},{2,3},{3,2},{4,5},{5,4},{6,7},{7,6},{8,9},{9,8},{10,11... | collective-permute-start | bytes 3342344 | tf_op jit(solution)/shard_map/ppermute | solution.py:88
  668.5 59.6 %collective-permute-start.54 = (bf16[2,256,1024]{2,1,0:T(8,128)(2,1)}, bf16[2,256,1024]{2,1,0:T(8,128)(2,1)}, u32[]{:S(2)}, u32[]{:S(2)}) collective-permute-start(bf16[2,256,1024]{2,1,0:T(8,128)(2,1)} %get-tuple-element.212), channel_id=1, source_target_pairs={{0,1},{1,0},{2,3},{3,2},{4,5},{5,4},{6,7},{7,6},{8,9},{9,8},{10,11... | collective-permute-start | bytes 3145736 | tf_op jit(solution)/shard_map/ppermute | solution.py:88
  669.1 76.9 %collective-permute-start.47 = (bf16[2,272,1024]{2,1,0:T(8,128)(2,1)}, bf16[2,272,1024]{2,1,0:T(8,128)(2,1)S(1)}, u32[]{:S(2)}, u32[]{:S(2)}) collective-permute-start(bf16[2,272,1024]{2,1,0:T(8,128)(2,1)} %get-tuple-element.209), channel_id=1, source_target_pairs={{0,1},{1,0},{2,3},{3,2},{4,5},{5,4},{6,7},{7,6},{8,9},{9,8},{10,11... | collective-permute-start | bytes 3342344 | tf_op jit(solution)/shard_map/ppermute | solution.py:88
  680.1 48.0 %collective-permute-start.56 = (bf16[2,256,1024]{2,1,0:T(8,128)(2,1)}, bf16[2,256,1024]{2,1,0:T(8,128)(2,1)}, u32[]{:S(2)}, u32[]{:S(2)}) collective-permute-start(bf16[2,256,1024]{2,1,0:T(8,128)(2,1)} %add_convert_fusion.3), channel_id=1, source_target_pairs={{0,2},{1,3},{2,0},{3,1},{4,6},{5,7},{6,4},{7,5},{8,10},{9,11},{10,... | collective-permute-start | bytes 3145736 | tf_op jit(solution)/shard_map/ppermute | solution.py:88
  705.1 41.8 %collective-permute-start.49 = (bf16[2,272,1024]{2,1,0:T(8,128)(2,1)}, bf16[2,272,1024]{2,1,0:T(8,128)(2,1)S(1)}, u32[]{:S(2)}, u32[]{:S(2)}) collective-permute-start(bf16[2,272,1024]{2,1,0:T(8,128)(2,1)} %add_convert_fusion.2), channel_id=1, source_target_pairs={{0,2},{1,3},{2,0},{3,1},{4,6},{5,7},{6,4},{7,5},{8,10},{9,11},{10,... | collective-permute-start | bytes 3342344 | tf_op jit(solution)/shard_map/ppermute | solution.py:88
  728.0 55.0 %collective-permute-start.45 = (bf16[2,256,2048]{2,1,0:T(8,128)(2,1)S(1)}, bf16[2,256,2048]{2,1,0:T(8,128)(2,1)S(1)}, u32[]{:S(2)}, u32[]{:S(2)}) collective-permute-start(bf16[2,256,2048]{2,1,0:T(8,128)(2,1)S(1)} %slice.272), channel_id=1, source_target_pairs={{0,8},{8,0},{16,24},{24,16},{1,9},{9,1},{17,25},{25,17},{2,10},{10... | collective-permute-start | bytes 6291464 | tf_op jit(solution)/shard_map/ppermute | solution.py:92
  730.4 39.2 %collective-permute-start.57 = (bf16[256,1024]{1,0:T(8,128)(2,1)S(1)}, bf16[256,1024]{1,0:T(8,128)(2,1)S(1)}, u32[]{:S(2)}, u32[]{:S(2)}) collective-permute-start(bf16[256,1024]{1,0:T(8,128)(2,1)S(1)} %fusion.15), channel_id=1, source_target_pairs={{0,4},{1,5},{2,6},{3,7},{4,0},{5,1},{6,2},{7,3},{8,12},{9,13},{10,... | collective-permute-start | bytes 1572872 | tf_op jit(solution)/shard_map/ppermute | solution.py:88
  747.6 33.6 %collective-permute-start.50 = (bf16[272,1024]{1,0:T(8,128)(2,1)S(1)}, bf16[272,1024]{1,0:T(8,128)(2,1)S(1)}, u32[]{:S(2)}, u32[]{:S(2)}) collective-permute-start(bf16[272,1024]{1,0:T(8,128)(2,1)S(1)} %fusion.14), channel_id=1, source_target_pairs={{0,4},{1,5},{2,6},{3,7},{4,0},{5,1},{6,2},{7,3},{8,12},{9,13},{10,... | collective-permute-start | bytes 1671176 | tf_op jit(solution)/shard_map/ppermute | solution.py:88
  786.3 32.2 %collective-permute-start.46 = (bf16[256,2048]{1,0:T(8,128)(2,1)}, bf16[256,2048]{1,0:T(8,128)(2,1)}, u32[]{:S(2)}, u32[]{:S(2)}) collective-permute-start(bf16[256,2048]{1,0:T(8,128)(2,1)} %slice_bitcast_fusion.3), channel_id=1, source_target_pairs={{0,16},{8,24},{16,0},{24,8},{1,17},{9,25},{17,1},{25,9},{2,18},{10... | collective-permute-start | bytes 3145736 | tf_op jit(solution)/shard_map/ppermute | solution.py:92
  (93 other events, 1479.0 us)
Sparse Core Ops, SparseCore 0:
  9.6 37.1 all-gather.5
  214.9 33.9 all-gather.3
  497.1 70.7 reduce-scatter.3
  570.4 85.8 reduce-scatter.5
  668.6 69.7 reduce-scatter.7

commit v13 on v12

--- a/solution.py
+++ b/solution.py
@@ -119,7 +119,7 @@
     farther = swap(far, 2)
     near_x, held = tie(swap(near, 1), far)
     return [
-        value, crossed, near, near_x, far, swap(held, 1), farther, swap(farther, 1)
+        value, crossed, near, near_x, far, swap(held, 1), farther
     ], after
 
 
@@ -911,6 +911,9 @@
     attn_all = lax.all_gather(attn_tok, "sp", axis=0, tiled=True)
 
     h2_pieces = gather(h2_low, n_ep)
+    if n_ep == 8:
+        h2_pieces[3], held = tie(h2_pieces[3], cot_pieces[6])
+        cot_pieces.append(swap(held, 1))
     cots = [cot_rows(g, [x_one]) for g in range(0, n_ep, group)]
     groups, d_pieces, d_gates, d_sums = [], [], [], []
     home_gates = None
@@ -929,7 +932,7 @@
     rows, gates, home_gates = rows_of(0, [])
     for g in range(0, n_ep, group):
         d_rows = cots[g // group]
-        made = experts(rows, d_rows, gates, w_gate, w_up, w_down, d_pieces[-group:] + cots + h2_pieces[4:7:2])
+        made = experts(rows, d_rows, gates, w_gate, w_up, w_down, d_pieces[-group:] + h2_pieces[4:7:2])
         groups.append((rows, d_rows, made))
         following = []
         if g + group < n_ep:
@@ -1020,9 +1023,9 @@
     )
     grad_qk = last_hop(*scatter_stacks(qk_stacks, n_ep)).astype(BF16)
 
-    d_h = d_h_rows(ids, n_ep, n_sp, d_qk, d_v, w_qkv, [grad_down, grad_gate])
-    output, d_h = tie(output, d_h)
+    d_h = d_h_rows(ids, n_ep, n_sp, d_qk, d_v, w_qkv, [])
     halves = plus(d_h[:2], swap_sp(d_h[2:], 1))
+    halves, output, grad_down, grad_gate = tie(halves, output, grad_down, grad_gate)
     d_h = halves[0].astype(F32) + swap_sp(halves[1], 2).astype(F32)
     x_rows = tokens[0].astype(F32)
     x_scale = lax.rsqrt(jnp.mean(x_rows * x_rows, axis=-1, keepdims=True) + EPS)

time: 843 us -> 849 us (level)
    ppermute x17, waiting for transfers between devices: 12.4 us -> 25.8 us  [swap_sp(): return lax.ppermute(value, 'sp', [(i, i ^ bits) for i in range(4)])]
  transfers between devices with their start and end apart: 72 -> 72, of which waited for: 25 -> 22; matrix products, arithmetic and copies ran while one was open for 13% -> 13% of each run, Pallas kernels for 38% -> 37%
where the time goes in v13:
time: 849 us; the launch traced here: 838 us
  Pallas kernels  317 us (37%)
  waiting for transfers between devices  267 us (31%)
  starting transfers between devices  97.5 us (11%)
  other arithmetic  77.3 us (9%)
  local copies, waits for them, and re-layouts  44.9 us (5%)
  between operations  31 us (4%)
    pallas_call x27, Pallas kernels, call(): pl.pallas_call(kernel, grid_spec=pltpu.PrefetchScalarGridSpec(num_scalar_...  317 us
    ppermute x36, waiting for transfers between devices, swap(): return lax.ppermute(value, 'ep', [(i, i ^ bits) for i in range(8)])  206 us
    ppermute x36, starting transfers between devices, swap(): return lax.ppermute(value, 'ep', [(i, i ^ bits) for i in range(8)])  53.6 us
    ppermute x17, waiting for transfers between devices, swap_sp(): return lax.ppermute(value, 'sp', [(i, i ^ bits) for i in range(4)])  25.8 us
    ppermute x2, waiting for transfers between devices, gather_line(): farther = inner + lax.ppermute(outer, 'ep', OUTWARD)  20.1 us
    convert_element_type x9, other arithmetic, plus(): return (left.astype(F32) + right.astype(F32)).astype(left.dtype)  17.8 us
  transfers between devices with their start and end apart: 72, of which 22 were waited for; matrix products, arithmetic and copies ran while one was open for 13% of the time, Pallas kernels for 37%

profile of v13, /device:TPU:0, one launch (start us, length us, event | category | flops | bytes accessed | tf_op | source)
XLA Modules:
  0.0 838.2 jit_solution(414285770322106757)
XLA Ops:
  21.2 21.0 %collective-permute-done.refs_5_ = bf16[256,2048]{1,0:T(8,128)(2,1)} collective-permute-done((bf16[256,2048]{1,0:T(8,128)(2,1)S(1)}, bf16[256,2048]{1,0:T(8,128)(2,1)}, u32[]{:S(2)}, u32[]{:S(2)}) %collective-permute-start) | collective-permute-done | bytes 1048608 | tf_op jit(solution)/shard_map/ppermute | solution.py:88
  46.1 5.6 all-to-all-start
  53.0 15.2 %collective-permute-done.1.refs_6_ = bf16[256,2048]{1,0:T(8,128)(2,1)} collective-permute-done((bf16[256,2048]{1,0:T(8,128)(2,1)}, bf16[256,2048]{1,0:T(8,128)(2,1)}, u32[]{:S(2)}, u32[]{:S(2)}) %collective-permute-start.1) | collective-permute-done | bytes 1048608 | tf_op jit(solution)/shard_map/ppermute | solution.py:88
  91.0 11.5 %collective-permute-done.7 = bf16[256,2048]{1,0:T(8,128)(2,1)} collective-permute-done((bf16[256,2048]{1,0:T(8,128)(2,1)S(1)}, bf16[256,2048]{1,0:T(8,128)(2,1)}, u32[]{:S(2)}, u32[]{:S(2)}) %collective-permute-start.7) | collective-permute-done | bytes 1048608 | tf_op jit(solution)/shard_map/ppermute | solution.py:111
  117.3 18.0 %collective-permute-done.8.refs_10_ = bf16[256,2048]{1,0:T(8,128)(2,1)} collective-permute-done((bf16[256,2048]{1,0:T(8,128)(2,1)S(1)}, bf16[256,2048]{1,0:T(8,128)(2,1)}, u32[]{:S(2)}, u32[]{:S(2)}) %collective-permute-start.8) | collective-permute-done | bytes 1048608 | tf_op jit(solution)/shard_map/ppermute | solution.py:88
  136.8 16.3 %qkv_project.1 = (f32[1024,512]{1,0:T(8,128)}, f32[1024,512]{1,0:T(8,128)}, bf16[1024,512]{1,0:T(8,128)(2,1)}, f32[16,1024]{1,0:T(8,128)}, bf16[2048,1536]{1,0:T(8,128)(2,1)}, /*index=5*/bf16[1024,2048]{1,0:T(8,128)(2,1)}) custom-call(s32[12]{0:T(128)} %pad_add_fusion.refs_0_.ids, bf16[1024,2048]{1,0:T(8,128)(2,1)} %bitcast.176, f32[1,2048]{1,0:T(1,128)} %bitcast.158, ...), custom_call_target="tpu_custom_call" | custom-call | flops 128849018880 | bytes 28385280 | tf_op jit(solution)/shard_map/qkv_project/pallas_call | solution.py:62
  166.6 7.1 collective-permute-start.14
  173.8 17.2 %attend.1 = (bf16[1024,512]{1,0:T(8,128)(2,1)}, bf16[1024,512]{1,0:T(8,128)(2,1)}, bf16[1024,512]{1,0:T(8,128)(2,1)}) custom-call(f32[1024,512]{1,0:T(8,128)} %get-tuple-element.131.refs_0_.qr_ref.refs_4_, f32[1024,512]{1,0:T(8,128)} %get-tuple-element.132.refs_1_.kr_ref.refs_5_, bf16[1024,512]{1,0:T(8,128)(2,1)} %get-tuple-element.133.refs_2_.v_ref, ...), custom_call_target="tpu_custom_call" | custom-call | flops 32212254720 | bytes 9510912 | tf_op jit(solution)/shard_map/attend/pallas_call | solution.py:62
  191.0 6.0 collective-permute-done.14.refs_1_
  204.0 11.5 %all-to-all-done.2 = bf16[4,256,512]{2,1,0:T(8,128)(2,1)S(1)} async-done(((bf16[4,256,512]{2,1,0:T(8,128)(2,1)}), bf16[4,256,512]{2,1,0:T(8,128)(2,1)S(1)}, u32[]{:S(2)}, u32[]{:S(2)}) %all-to-all-start.2) | async-done | bytes 1048608 | tf_op jit(solution)/shard_map/all_to_all | solution.py:902
  217.7 9.1 %out_project.1 = (f32[256,2048]{1,0:T(8,128)}, bf16[256,2048]{1,0:T(8,128)(2,1)}) custom-call(s32[12]{0:T(128)} %pad_add_fusion.refs_0_.ids, bf16[256,2048]{1,0:T(8,128)(2,1)} %bitcast.139, bf16[256,2048]{1,0:T(8,128)(2,1)} %bitcast.133, f32[1,2048]{1,0:T(1,128)} %bitcast.153, bf16[1024,512]{1,0:T(8,128)(2,1)} %pad_maximum_fusion.1.refs_0_, ...), custom_call_target="tpu_custom_call" | custom-call | flops 42949672960 | bytes 13639680 | tf_op jit(solution)/shard_map/out_project/pallas_call | solution.py:62
  227.5 4.6 collective-permute-start.20
  242.3 12.7 %collective-permute-done.20.refs_0_ = bf16[256,2048]{1,0:T(8,128)(2,1)S(1)} collective-permute-done((bf16[256,2048]{1,0:T(8,128)(2,1)}, bf16[256,2048]{1,0:T(8,128)(2,1)S(1)}, u32[]{:S(2)}, u32[]{:S(2)}) %collective-permute-start.20) | collective-permute-done | bytes 1048608 | tf_op jit(solution)/shard_map/ppermute | solution.py:88
  261.0 18.0 %collective-permute-done.21.refs_1_ = bf16[256,2048]{1,0:T(8,128)(2,1)} collective-permute-done((bf16[256,2048]{1,0:T(8,128)(2,1)S(1)}, bf16[256,2048]{1,0:T(8,128)(2,1)}, u32[]{:S(2)}, u32[]{:S(2)}) %collective-permute-start.21) | collective-permute-done | bytes 1048608 | tf_op jit(solution)/shard_map/ppermute | solution.py:88
  286.8 4.5 dispatch.8
  291.3 4.5 dispatch.9
  295.8 8.7 %collective-permute-done.26 = bf16[256,2048]{1,0:T(8,128)(2,1)S(1)} collective-permute-done((bf16[256,2048]{1,0:T(8,128)(2,1)S(1)}, bf16[256,2048]{1,0:T(8,128)(2,1)S(1)}, u32[]{:S(2)}, u32[]{:S(2)}) %collective-permute-start.26) | collective-permute-done | bytes 1048608 | tf_op jit(solution)/shard_map/ppermute | solution.py:111
  307.4 42.5 %experts.2 = (bf16[2,576,1024]{2,1,0:T(8,128)(2,1)}, bf16[2,576,1024]{2,1,0:T(8,128)(2,1)}, bf16[2,576,1024]{2,1,0:T(8,128)(2,1)}, f32[2,576,1]{2,1,0:T(8,128)},...) custom-call(bf16[2,576,2048]{2,1,0:T(8,128)(2,1)} %get-tuple-element.153.refs_0_, ...), custom_call_target="tpu_custom_call" | custom-call | flops 579820584960 | bytes 51127296 | tf_op jit(solution)/shard_map/experts/pallas_call | solution.py:62
  349.9 4.5 dispatch.12
  358.1 4.4 dispatch.13
  362.6 3.9 combine.4
  366.5 3.9 combine.5
  372.5 42.6 %experts.3 = (bf16[2,576,1024]{2,1,0:T(8,128)(2,1)}, bf16[2,576,1024]{2,1,0:T(8,128)(2,1)}, bf16[2,576,1024]{2,1,0:T(8,128)(2,1)}, f32[2,576,1]{2,1,0:T(8,128)},...) custom-call(bf16[2,576,2048]{2,1,0:T(8,128)(2,1)} %get-tuple-element.162.refs_3_.refs_0_.refs_1_, ...), custom_call_target="tpu_custom_call" | custom-call | flops 579820584960 | bytes 51127296 | tf_op jit(solution)/shard_map/experts/pallas_call | solution.py:62
  424.4 4.0 combine.7
  434.2 4.8 all-to-all-start.3
  441.5 10.5 %combine_stacks.1 = (bf16[2,256,2048]{2,1,0:T(8,128)(2,1)}, bf16[2,256,2048]{2,1,0:T(8,128)(2,1)}, bf16[2,256,2048]{2,1,0:T(8,128)(2,1)}, bf16[2,256,2048]{2,1,0:T(8,128)(2,1)}) custom-call(s32[16,256]{1,0:T(8,128)} %and_select_fusion.refs_11_.refs_0_, bf16[2,576,2048]{2,1,0:T(8,128)(2,1)} %get-tuple-element.158.refs_1_, ...), custom_call_target="tpu_custom_call" | custom-call | flops 48318382080 | bytes 17842176 | tf_op jit(solution)/shard_map/combine_stacks/pallas_call | solution.py:62
  452.0 18.0 %weight_grad.3.refs_4_ = bf16[2,1024,2048]{2,1,0:T(8,128)(2,1)} custom-call(bf16[2,576,1024]{2,1,0:T(8,128)(2,1)} %get-tuple-element.181.refs_0_, bf16[2,576,1024]{2,1,0:T(8,128)(2,1)} %get-tuple-element.182.refs_1_, bf16[2,576,2048]{2,1,0:T(8,128)(2,1)} %dispatch.11.refs_1_.refs_2_, bf16[2,576,2048]{2,1,0:T(8,128)(2,1)} %dispatch.15.refs_1_.refs_3_, ...), custom_call_target="tpu_custom_call" | custom-call | flops 193273528320 | bytes 22544384 | tf_op jit(solution)/shard_map/weight_grad/pallas_call | solution.py:62
  481.0 13.7 %collective-permute-done.38 = bf16[256,2048]{1,0:T(8,128)(2,1)S(1)} collective-permute-done((bf16[256,2048]{1,0:T(8,128)(2,1)S(1)}, bf16[256,2048]{1,0:T(8,128)(2,1)S(1)}, u32[]{:S(2)}, u32[]{:S(2)}) %collective-permute-start.38) | collective-permute-done | bytes 1048608 | tf_op jit(solution)/shard_map/ppermute | solution.py:88
  501.6 18.3 %weight_grad.4.refs_4_ = bf16[2,2048,1024]{2,1,0:T(8,128)(2,1)} custom-call(bf16[2,576,2048]{2,1,0:T(8,128)(2,1)} %get-tuple-element.153.refs_0_, bf16[2,576,2048]{2,1,0:T(8,128)(2,1)} %get-tuple-element.162.refs_3_.refs_0_.refs_1_, bf16[2,576,1024]{2,1,0:T(8,128)(2,1)} %get-tuple-element.196.refs_2_, bf16[2,576,1024]{2,1,0:T(8,128)(2,1)} %get-tuple-element.197.refs_3_, ...), custom_call_target="tpu_custom_call" | custom-call | flops 193273528320 | bytes 22544384 | tf_op jit(solution)/shard_map/weight_grad/pallas_call | solution.py:62
  519.9 18.5 %weight_grad.5 = bf16[2,2048,1024]{2,1,0:T(8,128)(2,1)} custom-call(bf16[2,576,2048]{2,1,0:T(8,128)(2,1)} %get-tuple-element.153.refs_0_, bf16[2,576,2048]{2,1,0:T(8,128)(2,1)} %get-tuple-element.162.refs_3_.refs_0_.refs_1_, bf16[2,576,1024]{2,1,0:T(8,128)(2,1)} %get-tuple-element.194.refs_2_, bf16[2,576,1024]{2,1,0:T(8,128)(2,1)} %get-tuple-element.195.refs_3_, ...), custom_call_target="tpu_custom_call" | custom-call | flops 193273528320 | bytes 22544384 | tf_op jit(solution)/shard_map/weight_grad/pallas_call | solution.py:62
  549.1 7.8 out_back.1
  567.3 19.7 %collective-permute-done.36 = bf16[2,256,2048]{2,1,0:T(8,128)(2,1)} collective-permute-done((bf16[2,256,2048]{2,1,0:T(8,128)(2,1)}, bf16[2,256,2048]{2,1,0:T(8,128)(2,1)}, u32[]{:S(2)}, u32[]{:S(2)}) %collective-permute-start.36) | collective-permute-done | bytes 2097184 | tf_op jit(solution)/shard_map/ppermute | solution.py:88
  597.0 23.3 %attend_back.1 = (f32[1024,512]{1,0:T(8,128)}, f32[1024,512]{1,0:T(8,128)}, bf16[1024,512]{1,0:T(8,128)(2,1)}, f32[16,1024]{1,0:T(8,128)}, f32[1,512]{1,0:T(1,128)}, /*index=5*/f32[1,512]{1,0:T(1,128)}) custom-call(bf16[1024,512]{1,0:T(8,128)(2,1)} %get-tuple-element.139.q_ref, bf16[1024,512]{1,0:T(8,128)(2,1)} %get-tuple-element.140.k_ref, ...), custom_call_target="tpu_custom_call" | custom-call | flops 75161927680 | bytes 14823424 | tf_op jit(solution)/shard_map/attend_back/pallas_call | solution.py:62
  624.6 10.5 %vo_grads.1 = (bf16[2,256,1024]{2,1,0:T(8,128)(2,1)}, bf16[2,256,1024]{2,1,0:T(8,128)(2,1)}, bf16[2,256,1024]{2,1,0:T(8,128)(2,1)}, bf16[2,256,1024]{2,1,0:T(8,128)(2,1)}) custom-call(s32[12]{0:T(128)} %pad_add_fusion.refs_0_.ids, bf16[1024,2048]{1,0:T(8,128)(2,1)} %get-tuple-element.130.h_ref.refs_1_, bf16[1024,512]{1,0:T(8,128)(2,1)} %get-tuple-element.206.dv_ref, ...), custom_call_target="tpu_custom_call" | custom-call | flops 85899345920 | bytes 14680064 | tf_op jit(solution)/shard_map/vo_grads/pallas_call | solution.py:62
  638.6 13.0 %qk_back.1 = (bf16[2,272,1024]{2,1,0:T(8,128)(2,1)}, bf16[2,272,1024]{2,1,0:T(8,128)(2,1)}, bf16[2,272,1024]{2,1,0:T(8,128)(2,1)}, bf16[2,272,1024]{2,1,0:T(8,128)(2,1)}, bf16[1024,1024]{1,0:T(8,128)(2,1)}) custom-call(s32[12]{0:T(128)} %pad_add_fusion.refs_0_.ids, bf16[1024,2048]{1,0:T(8,128)(2,1)} %get-tuple-element.130.h_ref.refs_1_, ...), custom_call_target="tpu_custom_call" | custom-call | flops 85899345920 | bytes 19423232 | tf_op jit(solution)/shard_map/qk_back/pallas_call | solution.py:62
  651.9 9.4 %collective-permute-done.55 = bf16[2,256,1024]{2,1,0:T(8,128)(2,1)S(1)} collective-permute-done((bf16[2,256,1024]{2,1,0:T(8,128)(2,1)}, bf16[2,256,1024]{2,1,0:T(8,128)(2,1)S(1)}, u32[]{:S(2)}, u32[]{:S(2)}) %collective-permute-start.55) | collective-permute-done | bytes 1048608 | tf_op jit(solution)/shard_map/ppermute | solution.py:88
  665.6 12.9 %d_h.1 = bf16[4,256,2048]{2,1,0:T(8,128)(2,1)} custom-call(s32[12]{0:T(128)} %pad_add_fusion.refs_0_.ids, bf16[1024,1024]{1,0:T(8,128)(2,1)} %get-tuple-element.208.d_ref, bf16[1024,512]{1,0:T(8,128)(2,1)} %get-tuple-element.206.dv_ref, bf16[2048,1536]{1,0:T(8,128)(2,1)} %get-tuple-element.209.w_ref), custom_call_target="tpu_custom_call" | custom-call | flops 128849018880 | bytes 13631488 | tf_op jit(solution)/shard_map/d_h/pallas_call | solution.py:62
  680.6 26.3 %collective-permute-done.48 = bf16[2,272,1024]{2,1,0:T(8,128)(2,1)S(1)} collective-permute-done((bf16[2,272,1024]{2,1,0:T(8,128)(2,1)}, bf16[2,272,1024]{2,1,0:T(8,128)(2,1)S(1)}, u32[]{:S(2)}, u32[]{:S(2)}) %collective-permute-start.48) | collective-permute-done | bytes 1114144 | tf_op jit(solution)/shard_map/ppermute | solution.py:88
  716.9 16.0 %collective-permute-done.47 = bf16[2,272,1024]{2,1,0:T(8,128)(2,1)S(1)} collective-permute-done((bf16[2,272,1024]{2,1,0:T(8,128)(2,1)}, bf16[2,272,1024]{2,1,0:T(8,128)(2,1)S(1)}, u32[]{:S(2)}, u32[]{:S(2)}) %collective-permute-start.47) | collective-permute-done | bytes 1114144 | tf_op jit(solution)/shard_map/ppermute | solution.py:88
  733.0 12.8 %collective-permute-done.49 = bf16[2,272,1024]{2,1,0:T(8,128)(2,1)S(1)} collective-permute-done((bf16[2,272,1024]{2,1,0:T(8,128)(2,1)S(1)}, bf16[2,272,1024]{2,1,0:T(8,128)(2,1)S(1)}, u32[]{:S(2)}, u32[]{:S(2)}) %collective-permute-start.49) | collective-permute-done | bytes 1114144 | tf_op jit(solution)/shard_map/ppermute | solution.py:88
  751.0 4.1 convert_element_type.243.refs_13_
  755.1 4.2 convert_element_type.244.refs_14_
  761.6 12.4 %collective-permute-done.50 = bf16[272,1024]{1,0:T(8,128)(2,1)} collective-permute-done((bf16[272,1024]{1,0:T(8,128)(2,1)}, bf16[272,1024]{1,0:T(8,128)(2,1)}, u32[]{:S(2)}, u32[]{:S(2)}) %collective-permute-start.50) | collective-permute-done | bytes 557088 | tf_op jit(solution)/shard_map/ppermute | solution.py:88
  780.5 18.2 %collective-permute-done.52.refs_7_ = bf16[272,1024]{1,0:T(8,128)(2,1)} collective-permute-done((bf16[272,1024]{1,0:T(8,128)(2,1)}, bf16[272,1024]{1,0:T(8,128)(2,1)}, u32[]{:S(2)}, u32[]{:S(2)}) %collective-permute-start.52) | collective-permute-done | bytes 557088 | tf_op jit(solution)/shard_map/ppermute | solution.py:92
  800.0 7.6 collective-permute-done.59.refs_11_
  807.6 4.2 convert_element_type.267.refs_15_
  813.8 7.9 finish.1
  826.2 5.1 fusion.6
  (392 shorter events, 210.7 us)
Async XLA Ops:
  7.2 129.6 %all-gather.6.cloned.1.call-start = ((), (), s32[]{:S(2)}) async-start(), calls=%async_computation.13 | async-start | bytes 5242880 | tf_op jit(solution)/shard_map/all_gather | solution.py:840
  18.9 32.8 %collective-permute-start.4 = (bf16[256,2048]{1,0:T(8,128)(2,1)S(1)}, bf16[256,2048]{1,0:T(8,128)(2,1)S(1)}, u32[]{:S(2)}, u32[]{:S(2)}) collective-permute-start(bf16[256,2048]{1,0:T(8,128)(2,1)S(1)} %pad_maximum_fusion.refs_3_), channel_id=1, source_target_pairs={{2,4},{3,5},{4,2},{5,3},{10,12},{11,13},{12,10},{13,11},{18,20},{1... | collective-permute-start | bytes 3145736 | tf_op jit(solution)/shard_map/ppermute | solution.py:107
  19.6 33.4 %collective-permute-start.2 = (bf16[256,2048]{1,0:T(8,128)(2,1)S(1)}, bf16[256,2048]{1,0:T(8,128)(2,1)}, u32[]{:S(2)}, u32[]{:S(2)}) collective-permute-start(bf16[256,2048]{1,0:T(8,128)(2,1)S(1)} %pad_maximum_fusion.refs_3_), channel_id=1, source_target_pairs={{0,1},{1,0},{2,3},{3,2},{4,5},{5,4},{6,7},{7,6},{8,9},{9,8},{10,11... | collective-permute-start | bytes 3145736 | tf_op jit(solution)/shard_map/ppermute | solution.py:88
  46.1 40.6 %all-to-all-start = ((bf16[8,48,256]{2,1,0:T(8,128)(2,1)}), bf16[8,48,256]{2,1,0:T(8,128)(2,1)}, u32[]{:S(2)}, u32[]{:S(2)}) async-start(bf16[8,48,256]{2,1,0:T(8,128)(2,1)} %broadcast_in_dim.68), calls=%async_computation | async-start | bytes 393216 | tf_op jit(solution)/shard_map/all_to_all | solution.py:828
  51.7 36.0 %collective-permute-start.5 = (bf16[256,2048]{1,0:T(8,128)(2,1)S(1)}, bf16[256,2048]{1,0:T(8,128)(2,1)}, u32[]{:S(2)}, u32[]{:S(2)}) collective-permute-start(bf16[256,2048]{1,0:T(8,128)(2,1)S(1)} %collective-permute-done.4), channel_id=1, source_target_pairs={{2,0},{3,1},{4,6},{5,7},{10,8},{11,9},{12,14},{13,15},{18,16},{19,... | collective-permute-start | bytes 3145736 | tf_op jit(solution)/shard_map/ppermute | solution.py:110
  68.2 34.3 %collective-permute-start.7 = (bf16[256,2048]{1,0:T(8,128)(2,1)S(1)}, bf16[256,2048]{1,0:T(8,128)(2,1)}, u32[]{:S(2)}, u32[]{:S(2)}) collective-permute-start(bf16[256,2048]{1,0:T(8,128)(2,1)S(1)} %collective-permute-done.3), channel_id=1, source_target_pairs={{2,0},{3,1},{4,6},{5,7},{10,8},{11,9},{12,14},{13,15},{18,16},{19,... | collective-permute-start | bytes 3145736 | tf_op jit(solution)/shard_map/ppermute | solution.py:111
  89.4 47.4 %collective-permute-start.6 = (bf16[256,2048]{1,0:T(8,128)(2,1)S(1)}, bf16[256,2048]{1,0:T(8,128)(2,1)}, u32[]{:S(2)}, u32[]{:S(2)}) collective-permute-start(bf16[256,2048]{1,0:T(8,128)(2,1)S(1)} %add.172.refs_7_), channel_id=1, source_target_pairs={{0,1},{1,0},{2,3},{3,2},{4,5},{5,4},{6,7},{7,6},{8,9},{9,8},{10,11... | collective-permute-start | bytes 3145736 | tf_op jit(solution)/shard_map/ppermute | solution.py:88
  104.1 31.2 %collective-permute-start.8 = (bf16[256,2048]{1,0:T(8,128)(2,1)S(1)}, bf16[256,2048]{1,0:T(8,128)(2,1)}, u32[]{:S(2)}, u32[]{:S(2)}) collective-permute-start(bf16[256,2048]{1,0:T(8,128)(2,1)S(1)} %add.173.refs_9_), channel_id=1, source_target_pairs={{0,1},{1,0},{2,3},{3,2},{4,5},{5,4},{6,7},{7,6},{8,9},{9,8},{10,11... | collective-permute-start | bytes 3145736 | tf_op jit(solution)/shard_map/ppermute | solution.py:88
  112.5 49.7 %collective-permute-start.9 = (bf16[1024,512]{1,0:T(8,128)(2,1)}, bf16[1024,512]{1,0:T(8,128)(2,1)}, u32[]{:S(2)}, u32[]{:S(2)}) collective-permute-start(bf16[1024,512]{1,0:T(8,128)(2,1)} %pad_maximum_fusion.1.refs_0_), channel_id=1, source_target_pairs={{0,16},{8,24},{16,0},{24,8},{1,17},{9,25},{17,1},{25,9},{2,18},{10... | collective-permute-start | bytes 3145736 | tf_op jit(solution)/shard_map/ppermute | solution.py:92
  114.0 50.7 %collective-permute-start.11 = (bf16[256,2048]{1,0:T(8,128)(2,1)S(1)}, bf16[256,2048]{1,0:T(8,128)(2,1)}, u32[]{:S(2)}, u32[]{:S(2)}) collective-permute-start(bf16[256,2048]{1,0:T(8,128)(2,1)S(1)} %bitcast.135), channel_id=1, source_target_pairs={{0,2},{1,3},{2,0},{3,1},{4,6},{5,7},{6,4},{7,5},{8,10},{9,11},{10,... | collective-permute-start | bytes 3145736 | tf_op jit(solution)/shard_map/ppermute | solution.py:88
  114.0 52.1 %collective-permute-start.12 = (bf16[256,2048]{1,0:T(8,128)(2,1)S(1)}, bf16[256,2048]{1,0:T(8,128)(2,1)}, u32[]{:S(2)}, u32[]{:S(2)}) collective-permute-start(bf16[256,2048]{1,0:T(8,128)(2,1)S(1)} %bitcast.136), channel_id=1, source_target_pairs={{0,4},{1,5},{2,6},{3,7},{4,0},{5,1},{6,2},{7,3},{8,12},{9,13},{10,... | collective-permute-start | bytes 3145736 | tf_op jit(solution)/shard_map/ppermute | solution.py:88
  135.3 31.3 %collective-permute-start.10 = (bf16[256,2048]{1,0:T(8,128)(2,1)S(1)}, bf16[256,2048]{1,0:T(8,128)(2,1)}, u32[]{:S(2)}, u32[]{:S(2)}) collective-permute-start(bf16[256,2048]{1,0:T(8,128)(2,1)S(1)} %bitcast.137), channel_id=1, source_target_pairs={{0,1},{1,0},{2,3},{3,2},{4,5},{5,4},{6,7},{7,6},{8,9},{9,8},{10,11... | collective-permute-start | bytes 3145736 | tf_op jit(solution)/shard_map/ppermute | solution.py:88
  159.7 56.9 %collective-permute-start.16 = (bf16[1024,512]{1,0:T(8,128)(2,1)}, bf16[1024,512]{1,0:T(8,128)(2,1)S(1)}, u32[]{:S(2)}, u32[]{:S(2)}) collective-permute-start(bf16[1024,512]{1,0:T(8,128)(2,1)} %pad_maximum_fusion.1.refs_0_), channel_id=1, source_target_pairs={{0,8},{8,0},{16,24},{24,16},{1,9},{9,1},{17,25},{25,17},{2,10},{10... | collective-permute-start | bytes 3145736 | tf_op jit(solution)/shard_map/ppermute | solution.py:92
  162.2 54.5 %collective-permute-start.18 = (bf16[1024,512]{1,0:T(8,128)(2,1)}, bf16[1024,512]{1,0:T(8,128)(2,1)}, u32[]{:S(2)}, u32[]{:S(2)}) collective-permute-start(bf16[1024,512]{1,0:T(8,128)(2,1)} %collective-permute-done.9.refs_9_.refs_4_), channel_id=1, source_target_pairs={{0,8},{8,0},{16,24},{24,16},{1,9},{9,1},{17,25},{25,17},{2,10},{10... | collective-permute-start | bytes 3145736 | tf_op jit(solution)/shard_map/ppermute | solution.py:92
  164.7 32.3 %collective-permute-start.15 = (bf16[1024,512]{1,0:T(8,128)(2,1)S(1)}, bf16[1024,512]{1,0:T(8,128)(2,1)}, u32[]{:S(2)}, u32[]{:S(2)}) collective-permute-start(bf16[1024,512]{1,0:T(8,128)(2,1)S(1)} %pad_maximum_fusion.2.refs_1_), channel_id=1, source_target_pairs={{0,16},{8,24},{16,0},{24,8},{1,17},{9,25},{17,1},{25,9},{2,18},{10... | collective-permute-start | bytes 3145736 | tf_op jit(solution)/shard_map/ppermute | solution.py:92
  166.1 37.4 %collective-permute-start.13 = (bf16[256,2048]{1,0:T(8,128)(2,1)}, bf16[256,2048]{1,0:T(8,128)(2,1)}, u32[]{:S(2)}, u32[]{:S(2)}) collective-permute-start(bf16[256,2048]{1,0:T(8,128)(2,1)} %collective-permute-done.11.refs_11_.refs_1_), channel_id=1, source_target_pairs={{0,1},{1,0},{2,3},{3,2},{4,5},{5,4},{6,7},{7,6},{8,9},{9,8},{10,11... | collective-permute-start | bytes 3145736 | tf_op jit(solution)/shard_map/ppermute | solution.py:88
  166.6 30.4 %collective-permute-start.14 = (bf16[256,2048]{1,0:T(8,128)(2,1)}, bf16[256,2048]{1,0:T(8,128)(2,1)}, u32[]{:S(2)}, u32[]{:S(2)}) collective-permute-start(bf16[256,2048]{1,0:T(8,128)(2,1)} %collective-permute-done.12.refs_12_.refs_1_), channel_id=1, source_target_pairs={{0,2},{1,3},{2,0},{3,1},{4,6},{5,7},{6,4},{7,5},{8,10},{9,11},{10,... | collective-permute-start | bytes 3145736 | tf_op jit(solution)/shard_map/ppermute | solution.py:88
  201.1 422.6 %all-gather.4.cloned.1.call-start = ((), (), s32[]{:S(2)}) async-start(), calls=%async_computation.9 | async-start | bytes 5242880 | tf_op jit(solution)/shard_map/all_gather | solution.py:911
  203.5 35.0 %collective-permute-start.30 = (bf16[256,2048]{1,0:T(8,128)(2,1)}, bf16[256,2048]{1,0:T(8,128)(2,1)}, u32[]{:S(2)}, u32[]{:S(2)}) collective-permute-start(bf16[256,2048]{1,0:T(8,128)(2,1)} %collective-permute-done.12.refs_12_.refs_1_), channel_id=1, source_target_pairs={{0,1},{1,0},{2,3},{3,2},{4,5},{5,4},{6,7},{7,6},{8,9},{9,8},{10,11... | collective-permute-start | bytes 3145736 | tf_op jit(solution)/shard_map/ppermute | solution.py:88
  226.8 29.1 %collective-permute-start.24 = (bf16[256,2048]{1,0:T(8,128)(2,1)}, bf16[256,2048]{1,0:T(8,128)(2,1)S(1)}, u32[]{:S(2)}, u32[]{:S(2)}) collective-permute-start(bf16[256,2048]{1,0:T(8,128)(2,1)} %get-tuple-element.146.refs_0_), channel_id=1, source_target_pairs={{2,4},{3,5},{4,2},{5,3},{10,12},{11,13},{12,10},{13,11},{18,20},{1... | collective-permute-start | bytes 3145736 | tf_op jit(solution)/shard_map/ppermute | solution.py:107
  232.1 28.9 %collective-permute-start.22 = (bf16[256,2048]{1,0:T(8,128)(2,1)}, bf16[256,2048]{1,0:T(8,128)(2,1)}, u32[]{:S(2)}, u32[]{:S(2)}) collective-permute-start(bf16[256,2048]{1,0:T(8,128)(2,1)} %get-tuple-element.146.refs_0_), channel_id=1, source_target_pairs={{0,1},{1,0},{2,3},{3,2},{4,5},{5,4},{6,7},{7,6},{8,9},{9,8},{10,11... | collective-permute-start | bytes 3145736 | tf_op jit(solution)/shard_map/ppermute | solution.py:88
  284.8 65.1 %collective-permute-start.28 = (bf16[256,2048]{1,0:T(8,128)(2,1)}, bf16[256,2048]{1,0:T(8,128)(2,1)}, u32[]{:S(2)}, u32[]{:S(2)}) collective-permute-start(bf16[256,2048]{1,0:T(8,128)(2,1)} %add.185.refs_6_.refs_1_.refs_10_), channel_id=1, source_target_pairs={{0,1},{1,0},{2,3},{3,2},{4,5},{5,4},{6,7},{7,6},{8,9},{9,8},{10,11... | collective-permute-start | bytes 3145736 | tf_op jit(solution)/shard_map/ppermute | solution.py:88
  286.5 67.9 %collective-permute-start.29 = (bf16[256,2048]{1,0:T(8,128)(2,1)}, bf16[256,2048]{1,0:T(8,128)(2,1)}, u32[]{:S(2)}, u32[]{:S(2)}) collective-permute-start(bf16[256,2048]{1,0:T(8,128)(2,1)} %collective-permute-done.14.refs_1_), channel_id=1, source_target_pairs={{0,1},{1,0},{2,3},{3,2},{4,5},{5,4},{6,7},{7,6},{8,9},{9,8},{10,11... | collective-permute-start | bytes 3145736 | tf_op jit(solution)/shard_map/ppermute | solution.py:88
  305.8 52.3 %collective-permute-start.27 = (bf16[256,2048]{1,0:T(8,128)(2,1)}, bf16[256,2048]{1,0:T(8,128)(2,1)}, u32[]{:S(2)}, u32[]{:S(2)}) collective-permute-start(bf16[256,2048]{1,0:T(8,128)(2,1)} %add.186.refs_7_.refs_1_.refs_11_), channel_id=1, source_target_pairs={{0,1},{1,0},{2,3},{3,2},{4,5},{5,4},{6,7},{7,6},{8,9},{9,8},{10,11... | collective-permute-start | bytes 3145736 | tf_op jit(solution)/shard_map/ppermute | solution.py:88
  370.5 44.7 %collective-permute-start.31 = (bf16[256,2048]{1,0:T(8,128)(2,1)}, bf16[256,2048]{1,0:T(8,128)(2,1)}, u32[]{:S(2)}, u32[]{:S(2)}) collective-permute-start(bf16[256,2048]{1,0:T(8,128)(2,1)} %get-tuple-element.168.refs_7_.refs_4_), channel_id=1, source_target_pairs={{0,1},{1,0},{2,3},{3,2},{4,5},{5,4},{6,7},{7,6},{8,9},{9,8},{10,11... | collective-permute-start | bytes 3145736 | tf_op jit(solution)/shard_map/ppermute | solution.py:88
  370.9 47.0 %collective-permute-start.32 = (bf16[256,2048]{1,0:T(8,128)(2,1)}, bf16[256,2048]{1,0:T(8,128)(2,1)}, u32[]{:S(2)}, u32[]{:S(2)}) collective-permute-start(bf16[256,2048]{1,0:T(8,128)(2,1)} %get-tuple-element.170.refs_9_.refs_6_), channel_id=1, source_target_pairs={{0,1},{1,0},{2,3},{3,2},{4,5},{5,4},{6,7},{7,6},{8,9},{9,8},{10,11... | collective-permute-start | bytes 3145736 | tf_op jit(solution)/shard_map/ppermute | solution.py:88
  428.4 48.6 %collective-permute-start.33 = (bf16[256,2048]{1,0:T(8,128)(2,1)}, bf16[256,2048]{1,0:T(8,128)(2,1)}, u32[]{:S(2)}, u32[]{:S(2)}) collective-permute-start(bf16[256,2048]{1,0:T(8,128)(2,1)} %get-tuple-element.175.refs_8_), channel_id=1, source_target_pairs={{0,1},{1,0},{2,3},{3,2},{4,5},{5,4},{6,7},{7,6},{8,9},{9,8},{10,11... | collective-permute-start | bytes 3145736 | tf_op jit(solution)/shard_map/ppermute | solution.py:88
  434.2 35.9 %all-to-all-start.3 = ((f32[8,2,256]{2,1,0:T(2,128)}), f32[8,2,256]{2,1,0:T(2,128)}, u32[]{:S(2)}, u32[]{:S(2)}) async-start(f32[8,2,256]{2,1,0:T(2,128)} %constant_dynamic-update-slice_fusion.8), calls=%async_computation.3 | async-start | bytes 32768 | tf_op jit(solution)/shard_map/all_to_all | solution.py:958
  439.0 311.9 %reduce-scatter.4.cloned.1.call-start = ((), (), s32[]{:S(2)}) async-start(), calls=%async_computation.10 | async-start | bytes 10485760 | tf_op jit(solution)/shard_map/reduce_scatter | solution.py:976
  439.5 33.2 %collective-permute-start.37 = (bf16[256,2048]{1,0:T(8,128)(2,1)}, bf16[256,2048]{1,0:T(8,128)(2,1)}, u32[]{:S(2)}, u32[]{:S(2)}) collective-permute-start(bf16[256,2048]{1,0:T(8,128)(2,1)} %get-tuple-element.177.refs_10_), channel_id=1, source_target_pairs={{0,1},{1,0},{2,3},{3,2},{4,5},{5,4},{6,7},{7,6},{8,9},{9,8},{10,11... | collective-permute-start | bytes 3145736 | tf_op jit(solution)/shard_map/ppermute | solution.py:88
  478.7 59.7 %collective-permute-start.35 = (bf16[2,256,2048]{2,1,0:T(8,128)(2,1)}, bf16[2,256,2048]{2,1,0:T(8,128)(2,1)}, u32[]{:S(2)}, u32[]{:S(2)}) collective-permute-start(bf16[2,256,2048]{2,1,0:T(8,128)(2,1)} %get-tuple-element.185), channel_id=1, source_target_pairs={{0,1},{1,0},{2,3},{3,2},{4,5},{5,4},{6,7},{7,6},{8,9},{9,8},{10,11... | collective-permute-start | bytes 6291464 | tf_op jit(solution)/shard_map/ppermute | solution.py:88
  479.2 88.1 %collective-permute-start.34 = (bf16[2,256,2048]{2,1,0:T(8,128)(2,1)}, bf16[2,256,2048]{2,1,0:T(8,128)(2,1)}, u32[]{:S(2)}, u32[]{:S(2)}) collective-permute-start(bf16[2,256,2048]{2,1,0:T(8,128)(2,1)} %get-tuple-element.183), channel_id=1, source_target_pairs={{0,1},{1,0},{2,3},{3,2},{4,5},{5,4},{6,7},{7,6},{8,9},{9,8},{10,11... | collective-permute-start | bytes 6291464 | tf_op jit(solution)/shard_map/ppermute | solution.py:88
  480.8 274.3 %reduce-scatter.6.cloned.1.call-start = ((), (), s32[]{:S(2)}) async-start(), calls=%async_computation.11 | async-start | bytes 10485760 | tf_op jit(solution)/shard_map/reduce_scatter | solution.py:976
  496.1 46.7 %collective-permute-start.40 = (bf16[256,2048]{1,0:T(8,128)(2,1)}, bf16[256,2048]{1,0:T(8,128)(2,1)}, u32[]{:S(2)}, u32[]{:S(2)}) collective-permute-start(bf16[256,2048]{1,0:T(8,128)(2,1)} %add_convert_fusion.5.refs_6_), channel_id=1, source_target_pairs={{0,4},{1,5},{2,6},{3,7},{4,0},{5,1},{6,2},{7,3},{8,12},{9,13},{10,... | collective-permute-start | bytes 3145736 | tf_op jit(solution)/shard_map/ppermute | solution.py:88
  499.8 42.9 %collective-permute-start.39 = (bf16[256,2048]{1,0:T(8,128)(2,1)}, bf16[256,2048]{1,0:T(8,128)(2,1)}, u32[]{:S(2)}, u32[]{:S(2)}) collective-permute-start(bf16[256,2048]{1,0:T(8,128)(2,1)} %add_convert_fusion.8.refs_4_), channel_id=1, source_target_pairs={{0,2},{1,3},{2,0},{3,1},{4,6},{5,7},{6,4},{7,5},{8,10},{9,11},{10,... | collective-permute-start | bytes 3145736 | tf_op jit(solution)/shard_map/ppermute | solution.py:88
  542.3 44.8 %collective-permute-start.36 = (bf16[2,256,2048]{2,1,0:T(8,128)(2,1)}, bf16[2,256,2048]{2,1,0:T(8,128)(2,1)}, u32[]{:S(2)}, u32[]{:S(2)}) collective-permute-start(bf16[2,256,2048]{2,1,0:T(8,128)(2,1)} %add_convert_fusion.1), channel_id=1, source_target_pairs={{0,2},{1,3},{2,0},{3,1},{4,6},{5,7},{6,4},{7,5},{8,10},{9,11},{10,... | collective-permute-start | bytes 6291464 | tf_op jit(solution)/shard_map/ppermute | solution.py:88
  559.3 34.1 %all-to-all-start.4 = ((bf16[256,4,512]{2,0,1:T(8,128)(2,1)}), bf16[256,4,512]{2,0,1:T(8,128)(2,1)S(1)}, u32[]{:S(2)}, u32[]{:S(2)}) async-start(bf16[256,4,512]{2,0,1:T(8,128)(2,1)} %bitcast.132), calls=%async_computation.4 | async-start | bytes 2097152 | tf_op jit(solution)/shard_map/all_to_all | solution.py:998
  562.9 244.7 %reduce-scatter.8.cloned.1.call-start = ((), (), s32[]{:S(2)}) async-start(), calls=%async_computation.12 | async-start | bytes 10485760 | tf_op jit(solution)/shard_map/reduce_scatter | solution.py:976
  593.4 30.2 %all-to-all-start.5 = ((bf16[256,4,512]{2,0,1:T(8,128)(2,1)}), bf16[256,4,512]{2,0,1:T(8,128)(2,1)S(1)}, u32[]{:S(2)}, u32[]{:S(2)}) async-start(bf16[256,4,512]{2,0,1:T(8,128)(2,1)} %bitcast.131), calls=%async_computation.5 | async-start | bytes 2097152 | tf_op jit(solution)/shard_map/all_to_all | solution.py:999
  622.6 85.0 %collective-permute-start.45 = (bf16[256,2048]{1,0:T(8,128)(2,1)}, bf16[256,2048]{1,0:T(8,128)(2,1)}, u32[]{:S(2)}, u32[]{:S(2)}) collective-permute-start(bf16[256,2048]{1,0:T(8,128)(2,1)} %fusion.11), channel_id=1, source_target_pairs={{0,4},{1,5},{2,6},{3,7},{4,0},{5,1},{6,2},{7,3},{8,12},{9,13},{10,... | collective-permute-start | bytes 3145736 | tf_op jit(solution)/shard_map/ppermute | solution.py:88
  636.1 77.1 %collective-permute-start.54 = (bf16[2,256,1024]{2,1,0:T(8,128)(2,1)}, bf16[2,256,1024]{2,1,0:T(8,128)(2,1)}, u32[]{:S(2)}, u32[]{:S(2)}) collective-permute-start(bf16[2,256,1024]{2,1,0:T(8,128)(2,1)} %get-tuple-element.218), channel_id=1, source_target_pairs={{0,1},{1,0},{2,3},{3,2},{4,5},{5,4},{6,7},{7,6},{8,9},{9,8},{10,11... | collective-permute-start | bytes 3145736 | tf_op jit(solution)/shard_map/ppermute | solution.py:88
  651.5 55.3 %collective-permute-start.48 = (bf16[2,272,1024]{2,1,0:T(8,128)(2,1)}, bf16[2,272,1024]{2,1,0:T(8,128)(2,1)S(1)}, u32[]{:S(2)}, u32[]{:S(2)}) collective-permute-start(bf16[2,272,1024]{2,1,0:T(8,128)(2,1)} %get-tuple-element.217), channel_id=1, source_target_pairs={{0,1},{1,0},{2,3},{3,2},{4,5},{5,4},{6,7},{7,6},{8,9},{9,8},{10,11... | collective-permute-start | bytes 3342344 | tf_op jit(solution)/shard_map/ppermute | solution.py:88
  662.7 50.5 %collective-permute-start.56 = (bf16[2,256,1024]{2,1,0:T(8,128)(2,1)}, bf16[2,256,1024]{2,1,0:T(8,128)(2,1)}, u32[]{:S(2)}, u32[]{:S(2)}) collective-permute-start(bf16[2,256,1024]{2,1,0:T(8,128)(2,1)} %add_convert_fusion.3), channel_id=1, source_target_pairs={{0,2},{1,3},{2,0},{3,1},{4,6},{5,7},{6,4},{7,5},{8,10},{9,11},{10,... | collective-permute-start | bytes 3145736 | tf_op jit(solution)/shard_map/ppermute | solution.py:88
  680.5 68.1 %collective-permute-start.44 = (bf16[2,256,2048]{2,1,0:T(8,128)(2,1)S(1)}, bf16[2,256,2048]{2,1,0:T(8,128)(2,1)S(1)}, u32[]{:S(2)}, u32[]{:S(2)}) collective-permute-start(bf16[2,256,2048]{2,1,0:T(8,128)(2,1)S(1)} %slice.318), channel_id=1, source_target_pairs={{0,8},{8,0},{16,24},{24,16},{1,9},{9,1},{17,25},{25,17},{2,10},{10... | collective-permute-start | bytes 6291464 | tf_op jit(solution)/shard_map/ppermute | solution.py:92
  707.6 38.1 %collective-permute-start.49 = (bf16[2,272,1024]{2,1,0:T(8,128)(2,1)S(1)}, bf16[2,272,1024]{2,1,0:T(8,128)(2,1)S(1)}, u32[]{:S(2)}, u32[]{:S(2)}) collective-permute-start(bf16[2,272,1024]{2,1,0:T(8,128)(2,1)S(1)} %add_convert_fusion.2), channel_id=1, source_target_pairs={{0,2},{1,3},{2,0},{3,1},{4,6},{5,7},{6,4},{7,5},{8,10},{9,11},{10,... | collective-permute-start | bytes 3342344 | tf_op jit(solution)/shard_map/ppermute | solution.py:88
  716.4 60.5 %collective-permute-start.57 = (bf16[256,1024]{1,0:T(8,128)(2,1)}, bf16[256,1024]{1,0:T(8,128)(2,1)}, u32[]{:S(2)}, u32[]{:S(2)}) collective-permute-start(bf16[256,1024]{1,0:T(8,128)(2,1)} %fusion.15), channel_id=1, source_target_pairs={{0,4},{1,5},{2,6},{3,7},{4,0},{5,1},{6,2},{7,3},{8,12},{9,13},{10,... | collective-permute-start | bytes 1572872 | tf_op jit(solution)/shard_map/ppermute | solution.py:88
  760.4 51.5 %collective-permute-start.46 = (bf16[256,2048]{1,0:T(8,128)(2,1)}, bf16[256,2048]{1,0:T(8,128)(2,1)}, u32[]{:S(2)}, u32[]{:S(2)}) collective-permute-start(bf16[256,2048]{1,0:T(8,128)(2,1)} %slice_bitcast_fusion.3), channel_id=1, source_target_pairs={{0,16},{8,24},{16,0},{24,8},{1,17},{9,25},{17,1},{25,9},{2,18},{10... | collective-permute-start | bytes 3145736 | tf_op jit(solution)/shard_map/ppermute | solution.py:92
  780.4 33.4 %collective-permute-start.51 = (bf16[272,1024]{1,0:T(8,128)(2,1)}, bf16[272,1024]{1,0:T(8,128)(2,1)}, u32[]{:S(2)}, u32[]{:S(2)}) collective-permute-start(bf16[272,1024]{1,0:T(8,128)(2,1)} %fusion.10.refs_5_), channel_id=1, source_target_pairs={{0,8},{8,0},{16,24},{24,16},{1,9},{9,1},{17,25},{25,17},{2,10},{10... | collective-permute-start | bytes 1671176 | tf_op jit(solution)/shard_map/ppermute | solution.py:92
  (94 other events, 1533.7 us)
Sparse Core Ops, SparseCore 0:
  9.6 37.1 all-gather.5
  216.8 32.9 all-gather.3
  480.9 71.9 reduce-scatter.3
  555.5 85.7 reduce-scatter.5
  643.7 71.7 reduce-scatter.7

commit v14 on v13

--- a/solution.py
+++ b/solution.py
@@ -1023,9 +1023,9 @@
     )
     grad_qk = last_hop(*scatter_stacks(qk_stacks, n_ep)).astype(BF16)
 
-    d_h = d_h_rows(ids, n_ep, n_sp, d_qk, d_v, w_qkv, [])
+    d_h = d_h_rows(ids, n_ep, n_sp, d_qk, d_v, w_qkv, [grad_down, grad_gate])
+    output, d_h = tie(output, d_h)
     halves = plus(d_h[:2], swap_sp(d_h[2:], 1))
-    halves, output, grad_down, grad_gate = tie(halves, output, grad_down, grad_gate)
     d_h = halves[0].astype(F32) + swap_sp(halves[1], 2).astype(F32)
     x_rows = tokens[0].astype(F32)
     x_scale = lax.rsqrt(jnp.mean(x_rows * x_rows, axis=-1, keepdims=True) + EPS)

time: 849 us -> 825 us (0.972)
  waiting for transfers between devices: 267 us -> 253 us
  starting transfers between devices: 97.5 us -> 87.8 us
    ppermute x17, waiting for transfers between devices: 25.8 us -> 12.5 us  [swap_sp(): return lax.ppermute(value, 'sp', [(i, i ^ bits) for i in range(4)])]
    ppermute x36, starting transfers between devices: 53.6 us -> 43.6 us  [swap(): return lax.ppermute(value, 'ep', [(i, i ^ bits) for i in range(8)])]
  transfers between devices with their start and end apart: 72 -> 72, of which waited for: 22 -> 25; matrix products, arithmetic and copies ran while one was open for 13% -> 14% of each run, Pallas kernels for 37% -> 39%
where the time goes in v14:
time: 825 us; the launch traced here: 813 us
  Pallas kernels  317 us (38%)
  waiting for transfers between devices  253 us (31%)
  starting transfers between devices  87.8 us (11%)
  other arithmetic  76.7 us (9%)
  local copies, waits for them, and re-layouts  43.6 us (5%)
  between operations  31.1 us (4%)
    pallas_call x27, Pallas kernels, call(): pl.pallas_call(kernel, grid_spec=pltpu.PrefetchScalarGridSpec(num_scalar_...  317 us
    ppermute x36, waiting for transfers between devices, swap(): return lax.ppermute(value, 'ep', [(i, i ^ bits) for i in range(8)])  199 us
    ppermute x36, starting transfers between devices, swap(): return lax.ppermute(value, 'ep', [(i, i ^ bits) for i in range(8)])  43.6 us
    convert_element_type x9, other arithmetic, plus(): return (left.astype(F32) + right.astype(F32)).astype(left.dtype)  20.9 us
    ppermute x2, waiting for transfers between devices, gather_line(): farther = inner + lax.ppermute(outer, 'ep', OUTWARD)  19.3 us
  transfers between devices with their start and end apart: 72, of which 25 were waited for; matrix products, arithmetic and copies ran while one was open for 14% of the time, Pallas kernels for 39%

profile of v14, /device:TPU:0, one launch (start us, length us, event | category | flops | bytes accessed | tf_op | source)
XLA Modules:
  0.0 813.2 jit_solution(10349930740602416552)
XLA Ops:
  21.2 21.0 %collective-permute-done.1.refs_5_ = bf16[256,2048]{1,0:T(8,128)(2,1)} collective-permute-done((bf16[256,2048]{1,0:T(8,128)(2,1)S(1)}, bf16[256,2048]{1,0:T(8,128)(2,1)}, u32[]{:S(2)}, u32[]{:S(2)}) %collective-permute-start.1) | collective-permute-done | bytes 1048608 | tf_op jit(solution)/shard_map/ppermute | solution.py:88
  46.1 5.6 all-to-all-start
  53.0 15.2 %collective-permute-done.2.refs_6_ = bf16[256,2048]{1,0:T(8,128)(2,1)} collective-permute-done((bf16[256,2048]{1,0:T(8,128)(2,1)}, bf16[256,2048]{1,0:T(8,128)(2,1)}, u32[]{:S(2)}, u32[]{:S(2)}) %collective-permute-start.2) | collective-permute-done | bytes 1048608 | tf_op jit(solution)/shard_map/ppermute | solution.py:88
  91.0 11.5 %collective-permute-done.5 = bf16[256,2048]{1,0:T(8,128)(2,1)} collective-permute-done((bf16[256,2048]{1,0:T(8,128)(2,1)S(1)}, bf16[256,2048]{1,0:T(8,128)(2,1)}, u32[]{:S(2)}, u32[]{:S(2)}) %collective-permute-start.5) | collective-permute-done | bytes 1048608 | tf_op jit(solution)/shard_map/ppermute | solution.py:111
  117.3 18.0 %collective-permute-done.12.refs_10_ = bf16[256,2048]{1,0:T(8,128)(2,1)} collective-permute-done((bf16[256,2048]{1,0:T(8,128)(2,1)S(1)}, bf16[256,2048]{1,0:T(8,128)(2,1)}, u32[]{:S(2)}, u32[]{:S(2)}) %collective-permute-start.12) | collective-permute-done | bytes 1048608 | tf_op jit(solution)/shard_map/ppermute | solution.py:88
  136.8 16.3 %qkv_project.1 = (f32[1024,512]{1,0:T(8,128)}, f32[1024,512]{1,0:T(8,128)}, bf16[1024,512]{1,0:T(8,128)(2,1)}, f32[16,1024]{1,0:T(8,128)}, bf16[2048,1536]{1,0:T(8,128)(2,1)}, /*index=5*/bf16[1024,2048]{1,0:T(8,128)(2,1)}) custom-call(s32[12]{0:T(128)} %pad_add_fusion.refs_0_.ids, bf16[1024,2048]{1,0:T(8,128)(2,1)} %bitcast.178, f32[1,2048]{1,0:T(1,128)} %bitcast.160, ...), custom_call_target="tpu_custom_call" | custom-call | flops 128849018880 | bytes 28385280 | tf_op jit(solution)/shard_map/qkv_project/pallas_call | solution.py:62
  166.1 6.2 collective-permute-start.9
  173.8 17.2 %attend.1 = (bf16[1024,512]{1,0:T(8,128)(2,1)}, bf16[1024,512]{1,0:T(8,128)(2,1)}, bf16[1024,512]{1,0:T(8,128)(2,1)}) custom-call(f32[1024,512]{1,0:T(8,128)} %get-tuple-element.129.refs_0_.qr_ref.refs_4_, f32[1024,512]{1,0:T(8,128)} %get-tuple-element.130.refs_1_.kr_ref.refs_5_, bf16[1024,512]{1,0:T(8,128)(2,1)} %get-tuple-element.131.refs_2_.v_ref, ...), custom_call_target="tpu_custom_call" | custom-call | flops 32212254720 | bytes 9510912 | tf_op jit(solution)/shard_map/attend/pallas_call | solution.py:62
  191.1 4.7 collective-permute-done.9.refs_1_
  203.2 10.5 %all-to-all-done.2 = bf16[4,256,512]{2,1,0:T(8,128)(2,1)S(1)} async-done(((bf16[4,256,512]{2,1,0:T(8,128)(2,1)}), bf16[4,256,512]{2,1,0:T(8,128)(2,1)S(1)}, u32[]{:S(2)}, u32[]{:S(2)}) %all-to-all-start.2) | async-done | bytes 1048608 | tf_op jit(solution)/shard_map/all_to_all | solution.py:902
  215.9 8.8 %out_project.1 = (f32[256,2048]{1,0:T(8,128)}, bf16[256,2048]{1,0:T(8,128)(2,1)}) custom-call(s32[12]{0:T(128)} %pad_add_fusion.refs_0_.ids, bf16[256,2048]{1,0:T(8,128)(2,1)} %bitcast.142, bf16[256,2048]{1,0:T(8,128)(2,1)} %bitcast.136, f32[1,2048]{1,0:T(1,128)} %bitcast.155, bf16[1024,512]{1,0:T(8,128)(2,1)} %pad_maximum_fusion.2.refs_0_, ...), custom_call_target="tpu_custom_call" | custom-call | flops 42949672960 | bytes 13639680 | tf_op jit(solution)/shard_map/out_project/pallas_call | solution.py:62
  238.7 10.9 %collective-permute-done.20.refs_0_ = bf16[256,2048]{1,0:T(8,128)(2,1)S(1)} collective-permute-done((bf16[256,2048]{1,0:T(8,128)(2,1)}, bf16[256,2048]{1,0:T(8,128)(2,1)S(1)}, u32[]{:S(2)}, u32[]{:S(2)}) %collective-permute-start.20) | collective-permute-done | bytes 1048608 | tf_op jit(solution)/shard_map/ppermute | solution.py:88
  257.1 16.6 %collective-permute-done.21.refs_1_ = bf16[256,2048]{1,0:T(8,128)(2,1)} collective-permute-done((bf16[256,2048]{1,0:T(8,128)(2,1)S(1)}, bf16[256,2048]{1,0:T(8,128)(2,1)}, u32[]{:S(2)}, u32[]{:S(2)}) %collective-permute-start.21) | collective-permute-done | bytes 1048608 | tf_op jit(solution)/shard_map/ppermute | solution.py:88
  275.0 5.3 collective-permute-done.25
  284.9 4.5 dispatch.8
  289.5 4.4 dispatch.9
  293.9 7.8 collective-permute-done.26
  303.6 42.5 %experts.2 = (bf16[2,576,1024]{2,1,0:T(8,128)(2,1)}, bf16[2,576,1024]{2,1,0:T(8,128)(2,1)}, bf16[2,576,1024]{2,1,0:T(8,128)(2,1)}, f32[2,576,1]{2,1,0:T(8,128)},...) custom-call(bf16[2,576,2048]{2,1,0:T(8,128)(2,1)} %get-tuple-element.149.refs_0_, ...), custom_call_target="tpu_custom_call" | custom-call | flops 579820584960 | bytes 51127296 | tf_op jit(solution)/shard_map/experts/pallas_call | solution.py:62
  346.1 4.5 dispatch.12
  354.3 4.5 dispatch.13
  368.7 42.6 %experts.3 = (bf16[2,576,1024]{2,1,0:T(8,128)(2,1)}, bf16[2,576,1024]{2,1,0:T(8,128)(2,1)}, bf16[2,576,1024]{2,1,0:T(8,128)(2,1)}, f32[2,576,1]{2,1,0:T(8,128)},...) custom-call(bf16[2,576,2048]{2,1,0:T(8,128)(2,1)} %get-tuple-element.157.refs_3_.refs_0_.refs_1_, ...), custom_call_target="tpu_custom_call" | custom-call | flops 579820584960 | bytes 51127296 | tf_op jit(solution)/shard_map/experts/pallas_call | solution.py:62
  416.7 4.0 combine.7
  420.7 4.0 combine.6
  436.5 10.5 %combine_stacks.1 = (bf16[2,256,2048]{2,1,0:T(8,128)(2,1)}, bf16[2,256,2048]{2,1,0:T(8,128)(2,1)}, bf16[2,256,2048]{2,1,0:T(8,128)(2,1)}, bf16[2,256,2048]{2,1,0:T(8,128)(2,1)}) custom-call(s32[16,256]{1,0:T(8,128)} %and_select_fusion.refs_11_.refs_0_, bf16[2,576,2048]{2,1,0:T(8,128)(2,1)} %get-tuple-element.153.refs_1_, ...), custom_call_target="tpu_custom_call" | custom-call | flops 48318382080 | bytes 17842176 | tf_op jit(solution)/shard_map/combine_stacks/pallas_call | solution.py:62
  447.1 18.0 %weight_grad.3.refs_4_ = bf16[2,1024,2048]{2,1,0:T(8,128)(2,1)} custom-call(bf16[2,576,1024]{2,1,0:T(8,128)(2,1)} %get-tuple-element.176.refs_0_, bf16[2,576,1024]{2,1,0:T(8,128)(2,1)} %get-tuple-element.177.refs_1_, bf16[2,576,2048]{2,1,0:T(8,128)(2,1)} %dispatch.11.refs_1_.refs_2_, bf16[2,576,2048]{2,1,0:T(8,128)(2,1)} %dispatch.15.refs_1_.refs_3_, ...), custom_call_target="tpu_custom_call" | custom-call | flops 193273528320 | bytes 22544384 | tf_op jit(solution)/shard_map/weight_grad/pallas_call | solution.py:62
  465.1 5.0 all-to-all-done.3
  479.4 14.9 %collective-permute-done.38 = bf16[256,2048]{1,0:T(8,128)(2,1)S(1)} collective-permute-done((bf16[256,2048]{1,0:T(8,128)(2,1)S(1)}, bf16[256,2048]{1,0:T(8,128)(2,1)S(1)}, u32[]{:S(2)}, u32[]{:S(2)}) %collective-permute-start.38) | collective-permute-done | bytes 1048608 | tf_op jit(solution)/shard_map/ppermute | solution.py:88
  496.8 18.3 %weight_grad.4.refs_4_ = bf16[2,2048,1024]{2,1,0:T(8,128)(2,1)} custom-call(bf16[2,576,2048]{2,1,0:T(8,128)(2,1)} %get-tuple-element.149.refs_0_, bf16[2,576,2048]{2,1,0:T(8,128)(2,1)} %get-tuple-element.157.refs_3_.refs_0_.refs_1_, bf16[2,576,1024]{2,1,0:T(8,128)(2,1)} %get-tuple-element.191.refs_2_, bf16[2,576,1024]{2,1,0:T(8,128)(2,1)} %get-tuple-element.192.refs_3_, ...), custom_call_target="tpu_custom_call" | custom-call | flops 193273528320 | bytes 22544384 | tf_op jit(solution)/shard_map/weight_grad/pallas_call | solution.py:62
  515.1 18.7 %weight_grad.5 = bf16[2,2048,1024]{2,1,0:T(8,128)(2,1)} custom-call(bf16[2,576,2048]{2,1,0:T(8,128)(2,1)} %get-tuple-element.149.refs_0_, bf16[2,576,2048]{2,1,0:T(8,128)(2,1)} %get-tuple-element.157.refs_3_.refs_0_.refs_1_, bf16[2,576,1024]{2,1,0:T(8,128)(2,1)} %get-tuple-element.189.refs_2_, bf16[2,576,1024]{2,1,0:T(8,128)(2,1)} %get-tuple-element.190.refs_3_, ...), custom_call_target="tpu_custom_call" | custom-call | flops 193273528320 | bytes 22544384 | tf_op jit(solution)/shard_map/weight_grad/pallas_call | solution.py:62
  546.6 7.9 out_back.1
  556.9 4.5 all-to-all-start.4
  566.3 17.8 %collective-permute-done.36 = bf16[2,256,2048]{2,1,0:T(8,128)(2,1)} collective-permute-done((bf16[2,256,2048]{2,1,0:T(8,128)(2,1)}, bf16[2,256,2048]{2,1,0:T(8,128)(2,1)}, u32[]{:S(2)}, u32[]{:S(2)}) %collective-permute-start.36) | collective-permute-done | bytes 2097184 | tf_op jit(solution)/shard_map/ppermute | solution.py:88
  594.1 23.2 %attend_back.1 = (f32[1024,512]{1,0:T(8,128)}, f32[1024,512]{1,0:T(8,128)}, bf16[1024,512]{1,0:T(8,128)(2,1)}, f32[16,1024]{1,0:T(8,128)}, f32[1,512]{1,0:T(1,128)}, /*index=5*/f32[1,512]{1,0:T(1,128)}) custom-call(bf16[1024,512]{1,0:T(8,128)(2,1)} %get-tuple-element.198.q_ref, bf16[1024,512]{1,0:T(8,128)(2,1)} %get-tuple-element.199.k_ref, ...), custom_call_target="tpu_custom_call" | custom-call | flops 75161927680 | bytes 14823424 | tf_op jit(solution)/shard_map/attend_back/pallas_call | solution.py:62
  621.0 10.6 %vo_grads.1 = (bf16[2,256,1024]{2,1,0:T(8,128)(2,1)}, bf16[2,256,1024]{2,1,0:T(8,128)(2,1)}, bf16[2,256,1024]{2,1,0:T(8,128)(2,1)}, bf16[2,256,1024]{2,1,0:T(8,128)(2,1)}) custom-call(s32[12]{0:T(128)} %pad_add_fusion.refs_0_.ids, bf16[1024,2048]{1,0:T(8,128)(2,1)} %get-tuple-element.197.h_ref.refs_1_, bf16[1024,512]{1,0:T(8,128)(2,1)} %get-tuple-element.206.dv_ref.refs_2_, ...), custom_call_target="tpu_custom_call" | custom-call | flops 85899345920 | bytes 14680064 | tf_op jit(solution)/shard_map/vo_grads/pallas_call | solution.py:62
  634.5 12.8 %qk_back.1 = (bf16[2,272,1024]{2,1,0:T(8,128)(2,1)}, bf16[2,272,1024]{2,1,0:T(8,128)(2,1)}, bf16[2,272,1024]{2,1,0:T(8,128)(2,1)}, bf16[2,272,1024]{2,1,0:T(8,128)(2,1)}, bf16[1024,1024]{1,0:T(8,128)(2,1)}) custom-call(s32[12]{0:T(128)} %pad_add_fusion.refs_0_.ids, bf16[1024,2048]{1,0:T(8,128)(2,1)} %get-tuple-element.197.h_ref.refs_1_, ...), custom_call_target="tpu_custom_call" | custom-call | flops 85899345920 | bytes 19423232 | tf_op jit(solution)/shard_map/qk_back/pallas_call | solution.py:62
  650.0 7.9 collective-permute-done.55
  661.6 19.5 %collective-permute-done.41 = bf16[256,2048]{1,0:T(8,128)(2,1)} collective-permute-done((bf16[256,2048]{1,0:T(8,128)(2,1)}, bf16[256,2048]{1,0:T(8,128)(2,1)}, u32[]{:S(2)}, u32[]{:S(2)}) %collective-permute-start.41) | collective-permute-done | bytes 1048608 | tf_op jit(solution)/shard_map/ppermute | solution.py:88
  686.5 4.2 convert_element_type.240.refs_4_.refs_13_
  690.7 4.1 convert_element_type.241.refs_5_.refs_14_
  694.8 12.6 %d_h.1 = bf16[4,256,2048]{2,1,0:T(8,128)(2,1)} custom-call(s32[12]{0:T(128)} %pad_add_fusion.refs_0_.ids, bf16[1024,1024]{1,0:T(8,128)(2,1)} %get-tuple-element.208.refs_1_, bf16[1024,512]{1,0:T(8,128)(2,1)} %get-tuple-element.206.dv_ref.refs_2_, bf16[2048,1536]{1,0:T(8,128)(2,1)} %get-tuple-element.209.refs_3_, ...), custom_call_target="tpu_custom_call" | custom-call | flops 128849018880 | bytes 13631488 | tf_op jit(solution)/shard_map/d_h/pallas_call | solution.py:62
  712.3 14.9 %collective-permute-done.47 = bf16[2,272,1024]{2,1,0:T(8,128)(2,1)S(1)} collective-permute-done((bf16[2,272,1024]{2,1,0:T(8,128)(2,1)}, bf16[2,272,1024]{2,1,0:T(8,128)(2,1)S(1)}, u32[]{:S(2)}, u32[]{:S(2)}) %collective-permute-start.47) | collective-permute-done | bytes 1114144 | tf_op jit(solution)/shard_map/ppermute | solution.py:88
  727.2 5.4 collective-permute-done.49
  733.4 17.2 %collective-permute-done.57 = bf16[256,1024]{1,0:T(8,128)(2,1)S(1)} collective-permute-done((bf16[256,1024]{1,0:T(8,128)(2,1)S(1)}, bf16[256,1024]{1,0:T(8,128)(2,1)S(1)}, u32[]{:S(2)}, u32[]{:S(2)}) %collective-permute-start.57) | collective-permute-done | bytes 524320 | tf_op jit(solution)/shard_map/ppermute | solution.py:88
  752.6 9.4 %collective-permute-done.50 = bf16[272,1024]{1,0:T(8,128)(2,1)S(1)} collective-permute-done((bf16[272,1024]{1,0:T(8,128)(2,1)S(1)}, bf16[272,1024]{1,0:T(8,128)(2,1)S(1)}, u32[]{:S(2)}, u32[]{:S(2)}) %collective-permute-start.50) | collective-permute-done | bytes 557088 | tf_op jit(solution)/shard_map/ppermute | solution.py:88
  767.6 10.2 %collective-permute-done.52.refs_7_ = bf16[272,1024]{1,0:T(8,128)(2,1)S(1)} collective-permute-done((bf16[272,1024]{1,0:T(8,128)(2,1)S(1)}, bf16[272,1024]{1,0:T(8,128)(2,1)S(1)}, u32[]{:S(2)}, u32[]{:S(2)}) %collective-permute-start.52) | collective-permute-done | bytes 557088 | tf_op jit(solution)/shard_map/ppermute | solution.py:92
  779.6 4.1 convert_element_type.267.refs_15_
  784.5 7.9 finish.1
  801.3 4.9 fusion.6
  (390 shorter events, 211.0 us)
Async XLA Ops:
  7.2 129.6 %all-gather.6.cloned.1.call-start = ((), (), s32[]{:S(2)}) async-start(), calls=%async_computation.13 | async-start | bytes 5242880 | tf_op jit(solution)/shard_map/all_gather | solution.py:840
  18.9 32.8 %collective-permute-start = (bf16[256,2048]{1,0:T(8,128)(2,1)S(1)}, bf16[256,2048]{1,0:T(8,128)(2,1)S(1)}, u32[]{:S(2)}, u32[]{:S(2)}) collective-permute-start(bf16[256,2048]{1,0:T(8,128)(2,1)S(1)} %pad_maximum_fusion.refs_3_), channel_id=1, source_target_pairs={{2,4},{3,5},{4,2},{5,3},{10,12},{11,13},{12,10},{13,11},{18,20},{1... | collective-permute-start | bytes 3145736 | tf_op jit(solution)/shard_map/ppermute | solution.py:107
  19.6 33.4 %collective-permute-start.3 = (bf16[256,2048]{1,0:T(8,128)(2,1)S(1)}, bf16[256,2048]{1,0:T(8,128)(2,1)}, u32[]{:S(2)}, u32[]{:S(2)}) collective-permute-start(bf16[256,2048]{1,0:T(8,128)(2,1)S(1)} %pad_maximum_fusion.refs_3_), channel_id=1, source_target_pairs={{0,1},{1,0},{2,3},{3,2},{4,5},{5,4},{6,7},{7,6},{8,9},{9,8},{10,11... | collective-permute-start | bytes 3145736 | tf_op jit(solution)/shard_map/ppermute | solution.py:88
  46.1 40.6 %all-to-all-start = ((bf16[8,48,256]{2,1,0:T(8,128)(2,1)}), bf16[8,48,256]{2,1,0:T(8,128)(2,1)}, u32[]{:S(2)}, u32[]{:S(2)}) async-start(bf16[8,48,256]{2,1,0:T(8,128)(2,1)} %broadcast_in_dim.68), calls=%async_computation | async-start | bytes 393216 | tf_op jit(solution)/shard_map/all_to_all | solution.py:828
  51.7 36.0 %collective-permute-start.10 = (bf16[256,2048]{1,0:T(8,128)(2,1)S(1)}, bf16[256,2048]{1,0:T(8,128)(2,1)}, u32[]{:S(2)}, u32[]{:S(2)}) collective-permute-start(bf16[256,2048]{1,0:T(8,128)(2,1)S(1)} %collective-permute-done), channel_id=1, source_target_pairs={{2,0},{3,1},{4,6},{5,7},{10,8},{11,9},{12,14},{13,15},{18,16},{19,... | collective-permute-start | bytes 3145736 | tf_op jit(solution)/shard_map/ppermute | solution.py:110
  68.2 34.3 %collective-permute-start.5 = (bf16[256,2048]{1,0:T(8,128)(2,1)S(1)}, bf16[256,2048]{1,0:T(8,128)(2,1)}, u32[]{:S(2)}, u32[]{:S(2)}) collective-permute-start(bf16[256,2048]{1,0:T(8,128)(2,1)S(1)} %collective-permute-done.4), channel_id=1, source_target_pairs={{2,0},{3,1},{4,6},{5,7},{10,8},{11,9},{12,14},{13,15},{18,16},{19,... | collective-permute-start | bytes 3145736 | tf_op jit(solution)/shard_map/ppermute | solution.py:111
  89.4 47.4 %collective-permute-start.11 = (bf16[256,2048]{1,0:T(8,128)(2,1)S(1)}, bf16[256,2048]{1,0:T(8,128)(2,1)}, u32[]{:S(2)}, u32[]{:S(2)}) collective-permute-start(bf16[256,2048]{1,0:T(8,128)(2,1)S(1)} %add.173.refs_7_), channel_id=1, source_target_pairs={{0,1},{1,0},{2,3},{3,2},{4,5},{5,4},{6,7},{7,6},{8,9},{9,8},{10,11... | collective-permute-start | bytes 3145736 | tf_op jit(solution)/shard_map/ppermute | solution.py:88
  104.1 31.2 %collective-permute-start.12 = (bf16[256,2048]{1,0:T(8,128)(2,1)S(1)}, bf16[256,2048]{1,0:T(8,128)(2,1)}, u32[]{:S(2)}, u32[]{:S(2)}) collective-permute-start(bf16[256,2048]{1,0:T(8,128)(2,1)S(1)} %add.172.refs_9_), channel_id=1, source_target_pairs={{0,1},{1,0},{2,3},{3,2},{4,5},{5,4},{6,7},{7,6},{8,9},{9,8},{10,11... | collective-permute-start | bytes 3145736 | tf_op jit(solution)/shard_map/ppermute | solution.py:88
  112.5 49.6 %collective-permute-start.14 = (bf16[1024,512]{1,0:T(8,128)(2,1)}, bf16[1024,512]{1,0:T(8,128)(2,1)}, u32[]{:S(2)}, u32[]{:S(2)}) collective-permute-start(bf16[1024,512]{1,0:T(8,128)(2,1)} %pad_maximum_fusion.2.refs_0_), channel_id=1, source_target_pairs={{0,16},{8,24},{16,0},{24,8},{1,17},{9,25},{17,1},{25,9},{2,18},{10... | collective-permute-start | bytes 3145736 | tf_op jit(solution)/shard_map/ppermute | solution.py:92
  114.0 50.6 %collective-permute-start.8 = (bf16[256,2048]{1,0:T(8,128)(2,1)S(1)}, bf16[256,2048]{1,0:T(8,128)(2,1)}, u32[]{:S(2)}, u32[]{:S(2)}) collective-permute-start(bf16[256,2048]{1,0:T(8,128)(2,1)S(1)} %bitcast.138), channel_id=1, source_target_pairs={{0,4},{1,5},{2,6},{3,7},{4,0},{5,1},{6,2},{7,3},{8,12},{9,13},{10,... | collective-permute-start | bytes 3145736 | tf_op jit(solution)/shard_map/ppermute | solution.py:88
  114.7 51.3 %collective-permute-start.6 = (bf16[256,2048]{1,0:T(8,128)(2,1)S(1)}, bf16[256,2048]{1,0:T(8,128)(2,1)}, u32[]{:S(2)}, u32[]{:S(2)}) collective-permute-start(bf16[256,2048]{1,0:T(8,128)(2,1)S(1)} %bitcast.139), channel_id=1, source_target_pairs={{0,2},{1,3},{2,0},{3,1},{4,6},{5,7},{6,4},{7,5},{8,10},{9,11},{10,... | collective-permute-start | bytes 3145736 | tf_op jit(solution)/shard_map/ppermute | solution.py:88
  135.3 37.0 %collective-permute-start.15 = (bf16[256,2048]{1,0:T(8,128)(2,1)S(1)}, bf16[256,2048]{1,0:T(8,128)(2,1)}, u32[]{:S(2)}, u32[]{:S(2)}) collective-permute-start(bf16[256,2048]{1,0:T(8,128)(2,1)S(1)} %bitcast.140), channel_id=1, source_target_pairs={{0,1},{1,0},{2,3},{3,2},{4,5},{5,4},{6,7},{7,6},{8,9},{9,8},{10,11... | collective-permute-start | bytes 3145736 | tf_op jit(solution)/shard_map/ppermute | solution.py:88
  159.7 55.2 %collective-permute-start.16 = (bf16[1024,512]{1,0:T(8,128)(2,1)}, bf16[1024,512]{1,0:T(8,128)(2,1)S(1)}, u32[]{:S(2)}, u32[]{:S(2)}) collective-permute-start(bf16[1024,512]{1,0:T(8,128)(2,1)} %pad_maximum_fusion.2.refs_0_), channel_id=1, source_target_pairs={{0,8},{8,0},{16,24},{24,16},{1,9},{9,1},{17,25},{25,17},{2,10},{10... | collective-permute-start | bytes 3145736 | tf_op jit(solution)/shard_map/ppermute | solution.py:92
  162.2 52.7 %collective-permute-start.18 = (bf16[1024,512]{1,0:T(8,128)(2,1)}, bf16[1024,512]{1,0:T(8,128)(2,1)}, u32[]{:S(2)}, u32[]{:S(2)}) collective-permute-start(bf16[1024,512]{1,0:T(8,128)(2,1)} %collective-permute-done.14.refs_9_.refs_4_), channel_id=1, source_target_pairs={{0,8},{8,0},{16,24},{24,16},{1,9},{9,1},{17,25},{25,17},{2,10},{10... | collective-permute-start | bytes 3145736 | tf_op jit(solution)/shard_map/ppermute | solution.py:92
  166.1 29.7 %collective-permute-start.9 = (bf16[256,2048]{1,0:T(8,128)(2,1)}, bf16[256,2048]{1,0:T(8,128)(2,1)}, u32[]{:S(2)}, u32[]{:S(2)}) collective-permute-start(bf16[256,2048]{1,0:T(8,128)(2,1)} %collective-permute-done.8.refs_12_.refs_1_), channel_id=1, source_target_pairs={{0,2},{1,3},{2,0},{3,1},{4,6},{5,7},{6,4},{7,5},{8,10},{9,11},{10,... | collective-permute-start | bytes 3145736 | tf_op jit(solution)/shard_map/ppermute | solution.py:88
  172.3 29.5 %collective-permute-start.7 = (bf16[256,2048]{1,0:T(8,128)(2,1)}, bf16[256,2048]{1,0:T(8,128)(2,1)}, u32[]{:S(2)}, u32[]{:S(2)}) collective-permute-start(bf16[256,2048]{1,0:T(8,128)(2,1)} %collective-permute-done.6.refs_11_.refs_1_), channel_id=1, source_target_pairs={{0,1},{1,0},{2,3},{3,2},{4,5},{5,4},{6,7},{7,6},{8,9},{9,8},{10,11... | collective-permute-start | bytes 3145736 | tf_op jit(solution)/shard_map/ppermute | solution.py:88
  199.3 420.3 %all-gather.4.cloned.1.call-start = ((), (), s32[]{:S(2)}) async-start(), calls=%async_computation.9 | async-start | bytes 5242880 | tf_op jit(solution)/shard_map/all_gather | solution.py:911
  201.7 33.2 %collective-permute-start.30 = (bf16[256,2048]{1,0:T(8,128)(2,1)}, bf16[256,2048]{1,0:T(8,128)(2,1)}, u32[]{:S(2)}, u32[]{:S(2)}) collective-permute-start(bf16[256,2048]{1,0:T(8,128)(2,1)} %collective-permute-done.8.refs_12_.refs_1_), channel_id=1, source_target_pairs={{0,1},{1,0},{2,3},{3,2},{4,5},{5,4},{6,7},{7,6},{8,9},{9,8},{10,11... | collective-permute-start | bytes 3145736 | tf_op jit(solution)/shard_map/ppermute | solution.py:88
  226.5 30.6 %collective-permute-start.22 = (bf16[256,2048]{1,0:T(8,128)(2,1)}, bf16[256,2048]{1,0:T(8,128)(2,1)}, u32[]{:S(2)}, u32[]{:S(2)}) collective-permute-start(bf16[256,2048]{1,0:T(8,128)(2,1)} %get-tuple-element.142.refs_0_), channel_id=1, source_target_pairs={{0,1},{1,0},{2,3},{3,2},{4,5},{5,4},{6,7},{7,6},{8,9},{9,8},{10,11... | collective-permute-start | bytes 3145736 | tf_op jit(solution)/shard_map/ppermute | solution.py:88
  251.9 28.4 %collective-permute-start.25 = (bf16[256,2048]{1,0:T(8,128)(2,1)S(1)}, bf16[256,2048]{1,0:T(8,128)(2,1)}, u32[]{:S(2)}, u32[]{:S(2)}) collective-permute-start(bf16[256,2048]{1,0:T(8,128)(2,1)S(1)} %collective-permute-done.24), channel_id=1, source_target_pairs={{2,0},{3,1},{4,6},{5,7},{10,8},{11,9},{12,14},{13,15},{18,16},{19,... | collective-permute-start | bytes 3145736 | tf_op jit(solution)/shard_map/ppermute | solution.py:110
  282.9 63.2 %collective-permute-start.28 = (bf16[256,2048]{1,0:T(8,128)(2,1)}, bf16[256,2048]{1,0:T(8,128)(2,1)}, u32[]{:S(2)}, u32[]{:S(2)}) collective-permute-start(bf16[256,2048]{1,0:T(8,128)(2,1)} %add.185.refs_6_.refs_1_.refs_10_), channel_id=1, source_target_pairs={{0,1},{1,0},{2,3},{3,2},{4,5},{5,4},{6,7},{7,6},{8,9},{9,8},{10,11... | collective-permute-start | bytes 3145736 | tf_op jit(solution)/shard_map/ppermute | solution.py:88
  283.3 67.3 %collective-permute-start.29 = (bf16[256,2048]{1,0:T(8,128)(2,1)}, bf16[256,2048]{1,0:T(8,128)(2,1)}, u32[]{:S(2)}, u32[]{:S(2)}) collective-permute-start(bf16[256,2048]{1,0:T(8,128)(2,1)} %collective-permute-done.9.refs_1_), channel_id=1, source_target_pairs={{0,1},{1,0},{2,3},{3,2},{4,5},{5,4},{6,7},{7,6},{8,9},{9,8},{10,11... | collective-permute-start | bytes 3145736 | tf_op jit(solution)/shard_map/ppermute | solution.py:88
  303.1 51.2 %collective-permute-start.27 = (bf16[256,2048]{1,0:T(8,128)(2,1)}, bf16[256,2048]{1,0:T(8,128)(2,1)}, u32[]{:S(2)}, u32[]{:S(2)}) collective-permute-start(bf16[256,2048]{1,0:T(8,128)(2,1)} %add.186.refs_7_.refs_1_.refs_11_), channel_id=1, source_target_pairs={{0,1},{1,0},{2,3},{3,2},{4,5},{5,4},{6,7},{7,6},{8,9},{9,8},{10,11... | collective-permute-start | bytes 3145736 | tf_op jit(solution)/shard_map/ppermute | solution.py:88
  366.7 44.7 %collective-permute-start.32 = (bf16[256,2048]{1,0:T(8,128)(2,1)}, bf16[256,2048]{1,0:T(8,128)(2,1)}, u32[]{:S(2)}, u32[]{:S(2)}) collective-permute-start(bf16[256,2048]{1,0:T(8,128)(2,1)} %get-tuple-element.165.refs_9_.refs_6_), channel_id=1, source_target_pairs={{0,1},{1,0},{2,3},{3,2},{4,5},{5,4},{6,7},{7,6},{8,9},{9,8},{10,11... | collective-permute-start | bytes 3145736 | tf_op jit(solution)/shard_map/ppermute | solution.py:88
  368.2 45.9 %collective-permute-start.31 = (bf16[256,2048]{1,0:T(8,128)(2,1)}, bf16[256,2048]{1,0:T(8,128)(2,1)}, u32[]{:S(2)}, u32[]{:S(2)}) collective-permute-start(bf16[256,2048]{1,0:T(8,128)(2,1)} %get-tuple-element.163.refs_7_.refs_4_), channel_id=1, source_target_pairs={{0,1},{1,0},{2,3},{3,2},{4,5},{5,4},{6,7},{7,6},{8,9},{9,8},{10,11... | collective-permute-start | bytes 3145736 | tf_op jit(solution)/shard_map/ppermute | solution.py:88
  424.7 46.2 %collective-permute-start.37 = (bf16[256,2048]{1,0:T(8,128)(2,1)}, bf16[256,2048]{1,0:T(8,128)(2,1)}, u32[]{:S(2)}, u32[]{:S(2)}) collective-permute-start(bf16[256,2048]{1,0:T(8,128)(2,1)} %get-tuple-element.172.refs_10_), channel_id=1, source_target_pairs={{0,1},{1,0},{2,3},{3,2},{4,5},{5,4},{6,7},{7,6},{8,9},{9,8},{10,11... | collective-permute-start | bytes 3145736 | tf_op jit(solution)/shard_map/ppermute | solution.py:88
  426.2 49.2 %collective-permute-start.33 = (bf16[256,2048]{1,0:T(8,128)(2,1)}, bf16[256,2048]{1,0:T(8,128)(2,1)}, u32[]{:S(2)}, u32[]{:S(2)}) collective-permute-start(bf16[256,2048]{1,0:T(8,128)(2,1)} %get-tuple-element.170.refs_8_), channel_id=1, source_target_pairs={{0,1},{1,0},{2,3},{3,2},{4,5},{5,4},{6,7},{7,6},{8,9},{9,8},{10,11... | collective-permute-start | bytes 3145736 | tf_op jit(solution)/shard_map/ppermute | solution.py:88
  432.2 37.9 %all-to-all-start.3 = ((f32[8,2,256]{2,1,0:T(2,128)}), f32[8,2,256]{2,1,0:T(2,128)}, u32[]{:S(2)}, u32[]{:S(2)}) async-start(f32[8,2,256]{2,1,0:T(2,128)} %constant_dynamic-update-slice_fusion.8), calls=%async_computation.3 | async-start | bytes 32768 | tf_op jit(solution)/shard_map/all_to_all | solution.py:958
  436.1 250.4 %reduce-scatter.4.cloned.1.call-start = ((), (), s32[]{:S(2)}) async-start(), calls=%async_computation.10 | async-start | bytes 10485760 | tf_op jit(solution)/shard_map/reduce_scatter | solution.py:976
  477.0 56.7 %collective-permute-start.35 = (bf16[2,256,2048]{2,1,0:T(8,128)(2,1)}, bf16[2,256,2048]{2,1,0:T(8,128)(2,1)}, u32[]{:S(2)}, u32[]{:S(2)}) collective-permute-start(bf16[2,256,2048]{2,1,0:T(8,128)(2,1)} %get-tuple-element.180), channel_id=1, source_target_pairs={{0,1},{1,0},{2,3},{3,2},{4,5},{5,4},{6,7},{7,6},{8,9},{9,8},{10,11... | collective-permute-start | bytes 6291464 | tf_op jit(solution)/shard_map/ppermute | solution.py:88
  478.6 87.7 %collective-permute-start.34 = (bf16[2,256,2048]{2,1,0:T(8,128)(2,1)}, bf16[2,256,2048]{2,1,0:T(8,128)(2,1)}, u32[]{:S(2)}, u32[]{:S(2)}) collective-permute-start(bf16[2,256,2048]{2,1,0:T(8,128)(2,1)} %get-tuple-element.178), channel_id=1, source_target_pairs={{0,1},{1,0},{2,3},{3,2},{4,5},{5,4},{6,7},{7,6},{8,9},{9,8},{10,11... | collective-permute-start | bytes 6291464 | tf_op jit(solution)/shard_map/ppermute | solution.py:88
  479.2 211.6 %reduce-scatter.6.cloned.1.call-start = ((), (), s32[]{:S(2)}) async-start(), calls=%async_computation.11 | async-start | bytes 10485760 | tf_op jit(solution)/shard_map/reduce_scatter | solution.py:976
  495.7 42.8 %collective-permute-start.39 = (bf16[256,2048]{1,0:T(8,128)(2,1)}, bf16[256,2048]{1,0:T(8,128)(2,1)}, u32[]{:S(2)}, u32[]{:S(2)}) collective-permute-start(bf16[256,2048]{1,0:T(8,128)(2,1)} %add_convert_fusion.8.refs_4_), channel_id=1, source_target_pairs={{0,2},{1,3},{2,0},{3,1},{4,6},{5,7},{6,4},{7,5},{8,10},{9,11},{10,... | collective-permute-start | bytes 3145736 | tf_op jit(solution)/shard_map/ppermute | solution.py:88
  495.8 44.5 %collective-permute-start.40 = (bf16[256,2048]{1,0:T(8,128)(2,1)}, bf16[256,2048]{1,0:T(8,128)(2,1)}, u32[]{:S(2)}, u32[]{:S(2)}) collective-permute-start(bf16[256,2048]{1,0:T(8,128)(2,1)} %add_convert_fusion.5.refs_6_), channel_id=1, source_target_pairs={{0,4},{1,5},{2,6},{3,7},{4,0},{5,1},{6,2},{7,3},{8,12},{9,13},{10,... | collective-permute-start | bytes 3145736 | tf_op jit(solution)/shard_map/ppermute | solution.py:88
  537.7 46.5 %collective-permute-start.36 = (bf16[2,256,2048]{2,1,0:T(8,128)(2,1)}, bf16[2,256,2048]{2,1,0:T(8,128)(2,1)}, u32[]{:S(2)}, u32[]{:S(2)}) collective-permute-start(bf16[2,256,2048]{2,1,0:T(8,128)(2,1)} %add_convert_fusion.1), channel_id=1, source_target_pairs={{0,2},{1,3},{2,0},{3,1},{4,6},{5,7},{6,4},{7,5},{8,10},{9,11},{10,... | collective-permute-start | bytes 6291464 | tf_op jit(solution)/shard_map/ppermute | solution.py:88
  556.9 33.6 %all-to-all-start.4 = ((bf16[256,4,512]{2,0,1:T(8,128)(2,1)}), bf16[256,4,512]{2,0,1:T(8,128)(2,1)}, u32[]{:S(2)}, u32[]{:S(2)}) async-start(bf16[256,4,512]{2,0,1:T(8,128)(2,1)} %bitcast.135), calls=%async_computation.4 | async-start | bytes 2097152 | tf_op jit(solution)/shard_map/all_to_all | solution.py:998
  590.5 29.5 %all-to-all-start.5 = ((bf16[256,4,512]{2,0,1:T(8,128)(2,1)}), bf16[256,4,512]{2,0,1:T(8,128)(2,1)S(1)}, u32[]{:S(2)}, u32[]{:S(2)}) async-start(bf16[256,4,512]{2,0,1:T(8,128)(2,1)} %bitcast.134), calls=%async_computation.5 | async-start | bytes 2097152 | tf_op jit(solution)/shard_map/all_to_all | solution.py:999
  594.0 185.5 %reduce-scatter.8.cloned.1.call-start = ((), (), s32[]{:S(2)}) async-start(), calls=%async_computation.12 | async-start | bytes 10485760 | tf_op jit(solution)/shard_map/reduce_scatter | solution.py:976
  633.1 48.0 %collective-permute-start.41 = (bf16[256,2048]{1,0:T(8,128)(2,1)}, bf16[256,2048]{1,0:T(8,128)(2,1)}, u32[]{:S(2)}, u32[]{:S(2)}) collective-permute-start(bf16[256,2048]{1,0:T(8,128)(2,1)} %fusion.11), channel_id=1, source_target_pairs={{0,4},{1,5},{2,6},{3,7},{4,0},{5,1},{6,2},{7,3},{8,12},{9,13},{10,... | collective-permute-start | bytes 3145736 | tf_op jit(solution)/shard_map/ppermute | solution.py:88
  647.4 36.4 %collective-permute-start.48 = (bf16[2,272,1024]{2,1,0:T(8,128)(2,1)}, bf16[2,272,1024]{2,1,0:T(8,128)(2,1)}, u32[]{:S(2)}, u32[]{:S(2)}) collective-permute-start(bf16[2,272,1024]{2,1,0:T(8,128)(2,1)} %get-tuple-element.215), channel_id=1, source_target_pairs={{0,1},{1,0},{2,3},{3,2},{4,5},{5,4},{6,7},{7,6},{8,9},{9,8},{10,11... | collective-permute-start | bytes 3342344 | tf_op jit(solution)/shard_map/ppermute | solution.py:88
  647.9 61.4 %collective-permute-start.54 = (bf16[2,256,1024]{2,1,0:T(8,128)(2,1)}, bf16[2,256,1024]{2,1,0:T(8,128)(2,1)}, u32[]{:S(2)}, u32[]{:S(2)}) collective-permute-start(bf16[2,256,1024]{2,1,0:T(8,128)(2,1)} %get-tuple-element.216), channel_id=1, source_target_pairs={{0,1},{1,0},{2,3},{3,2},{4,5},{5,4},{6,7},{7,6},{8,9},{9,8},{10,11... | collective-permute-start | bytes 3145736 | tf_op jit(solution)/shard_map/ppermute | solution.py:88
  649.5 77.8 %collective-permute-start.47 = (bf16[2,272,1024]{2,1,0:T(8,128)(2,1)}, bf16[2,272,1024]{2,1,0:T(8,128)(2,1)S(1)}, u32[]{:S(2)}, u32[]{:S(2)}) collective-permute-start(bf16[2,272,1024]{2,1,0:T(8,128)(2,1)} %get-tuple-element.213), channel_id=1, source_target_pairs={{0,1},{1,0},{2,3},{3,2},{4,5},{5,4},{6,7},{7,6},{8,9},{9,8},{10,11... | collective-permute-start | bytes 3342344 | tf_op jit(solution)/shard_map/ppermute | solution.py:88
  661.4 48.0 %collective-permute-start.56 = (bf16[2,256,1024]{2,1,0:T(8,128)(2,1)}, bf16[2,256,1024]{2,1,0:T(8,128)(2,1)}, u32[]{:S(2)}, u32[]{:S(2)}) collective-permute-start(bf16[2,256,1024]{2,1,0:T(8,128)(2,1)} %add_convert_fusion.3), channel_id=1, source_target_pairs={{0,2},{1,3},{2,0},{3,1},{4,6},{5,7},{6,4},{7,5},{8,10},{9,11},{10,... | collective-permute-start | bytes 3145736 | tf_op jit(solution)/shard_map/ppermute | solution.py:88
  686.5 46.1 %collective-permute-start.49 = (bf16[2,272,1024]{2,1,0:T(8,128)(2,1)}, bf16[2,272,1024]{2,1,0:T(8,128)(2,1)S(1)}, u32[]{:S(2)}, u32[]{:S(2)}) collective-permute-start(bf16[2,272,1024]{2,1,0:T(8,128)(2,1)} %add_convert_fusion.2), channel_id=1, source_target_pairs={{0,2},{1,3},{2,0},{3,1},{4,6},{5,7},{6,4},{7,5},{8,10},{9,11},{10,... | collective-permute-start | bytes 3342344 | tf_op jit(solution)/shard_map/ppermute | solution.py:88
  709.2 54.8 %collective-permute-start.45 = (bf16[2,256,2048]{2,1,0:T(8,128)(2,1)S(1)}, bf16[2,256,2048]{2,1,0:T(8,128)(2,1)S(1)}, u32[]{:S(2)}, u32[]{:S(2)}) collective-permute-start(bf16[2,256,2048]{2,1,0:T(8,128)(2,1)S(1)} %slice.272), channel_id=1, source_target_pairs={{0,8},{8,0},{16,24},{24,16},{1,9},{9,1},{17,25},{25,17},{2,10},{10... | collective-permute-start | bytes 6291464 | tf_op jit(solution)/shard_map/ppermute | solution.py:92
  711.6 39.0 %collective-permute-start.57 = (bf16[256,1024]{1,0:T(8,128)(2,1)S(1)}, bf16[256,1024]{1,0:T(8,128)(2,1)S(1)}, u32[]{:S(2)}, u32[]{:S(2)}) collective-permute-start(bf16[256,1024]{1,0:T(8,128)(2,1)S(1)} %fusion.15), channel_id=1, source_target_pairs={{0,4},{1,5},{2,6},{3,7},{4,0},{5,1},{6,2},{7,3},{8,12},{9,13},{10,... | collective-permute-start | bytes 1572872 | tf_op jit(solution)/shard_map/ppermute | solution.py:88
  733.3 28.7 %collective-permute-start.50 = (bf16[272,1024]{1,0:T(8,128)(2,1)S(1)}, bf16[272,1024]{1,0:T(8,128)(2,1)S(1)}, u32[]{:S(2)}, u32[]{:S(2)}) collective-permute-start(bf16[272,1024]{1,0:T(8,128)(2,1)S(1)} %fusion.14), channel_id=1, source_target_pairs={{0,4},{1,5},{2,6},{3,7},{4,0},{5,1},{6,2},{7,3},{8,12},{9,13},{10,... | collective-permute-start | bytes 1671176 | tf_op jit(solution)/shard_map/ppermute | solution.py:88
  767.4 31.7 %collective-permute-start.46 = (bf16[256,2048]{1,0:T(8,128)(2,1)}, bf16[256,2048]{1,0:T(8,128)(2,1)}, u32[]{:S(2)}, u32[]{:S(2)}) collective-permute-start(bf16[256,2048]{1,0:T(8,128)(2,1)} %slice_bitcast_fusion.3), channel_id=1, source_target_pairs={{0,16},{8,24},{16,0},{24,8},{1,17},{9,25},{17,1},{25,9},{2,18},{10... | collective-permute-start | bytes 3145736 | tf_op jit(solution)/shard_map/ppermute | solution.py:92
  (93 other events, 1463.0 us)
Sparse Core Ops, SparseCore 0:
  9.6 37.1 all-gather.5
  215.0 33.8 all-gather.3
  479.3 70.8 reduce-scatter.3
  552.8 85.7 reduce-scatter.5
  648.0 72.2 reduce-scatter.7
